TPU v7x, 32 devices: a whole 2x2x4 slice. The times are simulated.
32 devices in a mesh: dp: 8 (over z, y), mp: 4 (over x, core).
Axes of the slice: x: 2, y: 2, z: 4, core: 2. Of those that a mesh axis runs over, the one named last changes fastest.
Arguments:
- tokens: bfloat16 [19200, 768], P(('dp', 'mp')), may hold values from -48 to 48
- token_mask: int32 [96, 200], P('dp'), may hold values from 0 to 1, as said below
- gain_one: bfloat16 [768], P('dp'), may hold values from 0.25 to 1.75
- w_qkv: bfloat16 [768, 3, 768], P('dp', None, 'mp'), may hold values from -0.21875 to 0.21875
- w_out: bfloat16 [768, 768], P('mp', 'dp'), may hold values from -1.75 to 1.75
- gain_two: bfloat16 [768], P('dp'), may hold values from 0.25 to 1.75
- router: bfloat16 [768, 8], P('dp'), may hold values from -0.109375 to 0.109375
- w_in: bfloat16 [8, 768, 3072], P('dp', None, 'mp'), may hold values from -2.5 to 2.5
- w_back: bfloat16 [8, 3072, 768], P('dp', 'mp'), may hold values from -1 to 1
- cotangent: bfloat16 [19200, 768], P(('dp', 'mp')), may hold values from -6 to 6
Outputs:
- out: bfloat16 [19200, 768], P(('dp', 'mp'))
- grad_tokens: float32 [19200, 768], P(('dp', 'mp'))
- grad_gain_one: float32 [768], P('dp')
- grad_w_qkv: float32 [768, 3, 768], P('dp', None, 'mp')
- grad_w_out: float32 [768, 768], P('mp', 'dp')
- grad_gain_two: float32 [768], P('dp')
- grad_router: float32 [768, 8], P('dp')
- grad_w_in: float32 [8, 768, 3072], P('dp', None, 'mp')
- grad_w_back: float32 [8, 3072, 768], P('dp', 'mp')
- root_squares: float32 [3, 96], P(None, 'dp')
Inputs may be any that keep to these rules, and one draw needn't show every extreme that they name: `token_mask`: for each image the positions with 1 form a prefix of 98 to 197 positions; some image has 197; positions 197 and beyond are 0.
All inputs are finite; a program needn't handle non-finite values.
Results may differ from a plain program's by a relative error of at most 0.02.
Values may be sent and summed in bfloat16 or wider, within the bound.
No kernel may reach another device: no remote copies, remote signals or barrier semaphores. Data moves between devices by JAX's collectives and lax.ppermute only.
A program may use at most 192 MiB of HBM per device.

v0:
```python
import jax
import jax.numpy as jnp
from jax import lax
from jax.sharding import PartitionSpec as P

HEAD_DIM = 64


epsilon = 1e-06


def softmax_over(array_in, axis_index):
    shifted = array_in - jnp.max(array_in, axis=axis_index, keepdims=True)
    exp_terms = jnp.exp(shifted)
    return exp_terms / jnp.sum(exp_terms, axis=axis_index, keepdims=True)


def gelu_tanh(array_in):
    tanh_arg = 0.7978845608028654 * (array_in + 0.044715 * array_in * array_in * array_in)
    return 0.5 * array_in * (1.0 + jnp.tanh(tanh_arg))


def normalize(array_in, gain_vec):
    mean_row = jnp.mean(array_in, axis=-1, keepdims=True)
    centered = array_in - mean_row
    variance = jnp.mean(centered * centered, axis=-1, keepdims=True)
    inverse = lax.rsqrt(variance + epsilon)
    unit_rows = centered * inverse
    return (unit_rows * gain_vec, unit_rows, inverse)


def norm_back(grad_rows, unit_rows, inverse, gain_vec):
    scaled = grad_rows * gain_vec
    mean_grad = jnp.mean(scaled, axis=-1, keepdims=True)
    mean_proj = jnp.mean(scaled * unit_rows, axis=-1, keepdims=True)
    return (
        inverse * (scaled - mean_grad - unit_rows * mean_proj),
        jnp.sum(grad_rows * unit_rows, axis=0),
    )


def root_mean(array_in, token_mask):
    images, seq_len = token_mask.shape
    weight_rows = token_mask.astype(jnp.float32)
    shaped = array_in.reshape(images, seq_len, -1)
    squares = jnp.sum(shaped * shaped, axis=-1)
    counted = jnp.sum(weight_rows, axis=1) * shaped.shape[2]
    return jnp.sqrt(jnp.sum(squares * weight_rows, axis=1) / counted)


def return_slots(partial_sum):
    whole_sum = lax.psum(partial_sum, "mp").astype(jnp.bfloat16)
    return lax.all_to_all(whole_sum, "dp", split_axis=0, concat_axis=1, tiled=True)


def per_device(
    tokens, token_mask, gain_one, w_qkv, w_out, gain_two, router, w_in, w_back, cotangent
):
    rows_own = tokens.shape[0]
    model_width = tokens.shape[1]
    images, seq_len = token_mask.shape
    score_scale = HEAD_DIM ** (-0.5)
    offset = lax.axis_index("mp") * rows_own
    tokens_all, cot_all = (
        lax.all_gather(tokens, "mp", axis=0, tiled=True),
        lax.all_gather(cotangent, "mp", axis=0, tiled=True),
    )
    gain_a, qkv_w, gain_b, route_w, out_w = (
        lax.all_gather(gain_one, "dp", axis=0, tiled=True),
        lax.all_gather(w_qkv, "dp", axis=0, tiled=True),
        lax.all_gather(gain_two, "dp", axis=0, tiled=True),
        lax.all_gather(router, "dp", axis=0, tiled=True),
        lax.all_gather(w_out, "dp", axis=1, tiled=True),
    )
    gain_a_f = gain_a.astype(jnp.float32)
    gain_b_f = gain_b.astype(jnp.float32)
    rows_all = tokens_all.shape[0]
    local_heads = qkv_w.shape[2] // HEAD_DIM
    present = token_mask > 0
    key_keep = present[:, None, None, :]
    tokens_f = tokens_all.astype(jnp.float32)
    h_one_f, unit_one, inv_one = normalize(tokens_f, gain_a_f)
    h_one = h_one_f.astype(jnp.bfloat16)
    joined_qkv = jnp.einsum("td,dcf->tcf", h_one, qkv_w, preferred_element_type=jnp.float32).astype(
        jnp.bfloat16
    )
    joined_qkv = joined_qkv.reshape(images, seq_len, 3, local_heads, HEAD_DIM)
    queries = joined_qkv[:, :, 0]
    key_rows = joined_qkv[:, :, 1]
    values = joined_qkv[:, :, 2]

    def score_rows():
        raw_scores = (
            jnp.einsum("bqhe,bkhe->bhqk", queries, key_rows, preferred_element_type=jnp.float32)
            * score_scale
        )
        return jnp.where(key_keep, raw_scores, -1e30)

    scores = score_rows()
    row_peak = jnp.max(scores, axis=-1, keepdims=True)
    exp_terms = jnp.exp(scores - row_peak)
    row_total = jnp.sum(exp_terms, axis=-1, keepdims=True)
    log_total = row_peak + jnp.log(row_total)
    attention = (exp_terms / row_total).astype(jnp.bfloat16)
    heads_out = jnp.einsum("bhqk,bkhe->bqhe", attention, values, preferred_element_type=jnp.float32)
    heads_out = heads_out.reshape(rows_all, local_heads * HEAD_DIM).astype(jnp.bfloat16)
    row_block = heads_out
    branch = lax.psum_scatter(
        jnp.dot(row_block, out_w, preferred_element_type=jnp.float32),
        "mp",
        scatter_dimension=0,
        tiled=True,
    )
    branch_all = lax.all_gather(branch, "mp", axis=0, tiled=True)
    resid_all = tokens_f + branch_all
    h_two_f, unit_two, inv_two = normalize(resid_all, gain_b_f)
    h_two = h_two_f.astype(jnp.bfloat16)
    logits = jnp.einsum("td,de->te", h_two, route_w, preferred_element_type=jnp.float32)
    logits = logits.reshape(images, seq_len, -1)
    dispatch_f = softmax_over(jnp.where(present[:, :, None], logits, -1e30), 1)
    combine_f = softmax_over(logits, 2)
    dispatch = dispatch_f.astype(jnp.bfloat16)
    combine = combine_f.astype(jnp.bfloat16)
    h_two_img = h_two.reshape(images, seq_len, model_width)
    slot_rows = jnp.einsum(
        "bse,bsd->bed", dispatch, h_two_img, preferred_element_type=jnp.float32
    ).astype(jnp.bfloat16)
    slot_in = lax.all_to_all(slot_rows, "dp", split_axis=1, concat_axis=0, tiled=True)
    pre_gelu = jnp.einsum("ned,edf->nef", slot_in, w_in, preferred_element_type=jnp.float32)
    hidden = gelu_tanh(pre_gelu).astype(jnp.bfloat16)
    partial_out = jnp.einsum("nef,efd->ned", hidden, w_back, preferred_element_type=jnp.float32)
    returned = return_slots(partial_out)
    mixed_rows = jnp.einsum(
        "bse,bed->bsd", combine, returned, preferred_element_type=jnp.float32
    ).reshape(rows_all, model_width)
    stream = resid_all + mixed_rows
    out_rows = lax.dynamic_slice_in_dim(stream, offset, rows_own, 0).astype(jnp.bfloat16)
    root_squares = jnp.stack(
        [
            root_mean(stream, token_mask),
            root_mean(branch_all, token_mask),
            root_mean(mixed_rows, token_mask),
        ]
    )
    cot_img = cot_all.reshape(images, seq_len, model_width)
    grad_slot_out = jnp.einsum(
        "bse,bsd->bed", combine, cot_img, preferred_element_type=jnp.float32
    ).astype(jnp.bfloat16)
    grad_combine = jnp.einsum("bsd,bed->bse", cot_img, returned, preferred_element_type=jnp.float32)
    grad_logit_c = combine_f * (
        grad_combine - jnp.sum(grad_combine * combine_f, axis=2, keepdims=True)
    )
    grad_expert = lax.all_to_all(grad_slot_out, "dp", split_axis=1, concat_axis=0, tiled=True)
    grad_hidden = jnp.einsum(
        "ned,efd->nef", grad_expert, w_back, preferred_element_type=jnp.float32
    )
    grad_w_back = jnp.einsum(
        "nef,ned->efd", hidden, grad_expert, preferred_element_type=jnp.float32
    )
    gelu_pull = jax.vjp(gelu_tanh, pre_gelu)[1]
    grad_pre = gelu_pull(grad_hidden)[0].astype(jnp.bfloat16)
    grad_w_in = jnp.einsum("ned,nef->edf", slot_in, grad_pre, preferred_element_type=jnp.float32)
    grad_slot_part = jnp.einsum("nef,edf->ned", grad_pre, w_in, preferred_element_type=jnp.float32)
    grad_slots = return_slots(grad_slot_part)
    grad_dispatch = jnp.einsum(
        "bsd,bed->bse", h_two_img, grad_slots, preferred_element_type=jnp.float32
    )
    grad_logit_d = dispatch_f * (
        grad_dispatch - jnp.sum(grad_dispatch * dispatch_f, axis=1, keepdims=True)
    )
    grad_logits = (grad_logit_d + grad_logit_c).reshape(rows_all, -1).astype(jnp.bfloat16)
    grad_h_two = jnp.einsum(
        "bse,bed->bsd", dispatch, grad_slots, preferred_element_type=jnp.float32
    ).reshape(rows_all, model_width)
    grad_h_two = grad_h_two + jnp.einsum(
        "te,de->td", grad_logits, route_w, preferred_element_type=jnp.float32
    )
    grad_router = jnp.einsum("td,te->de", h_two, grad_logits, preferred_element_type=jnp.float32)
    grad_norm_two, grad_gain_two = norm_back(grad_h_two, unit_two, inv_two, gain_b_f)
    grad_resid = cot_all.astype(jnp.float32) + grad_norm_two
    grad_branch = grad_resid.astype(jnp.bfloat16)
    grad_w_out = jnp.einsum("tf,td->fd", heads_out, grad_branch, preferred_element_type=jnp.float32)
    grad_heads = jnp.einsum(
        "td,fd->tf", grad_branch, out_w, preferred_element_type=jnp.float32
    ).astype(jnp.bfloat16)
    grad_heads = grad_heads.reshape(images, seq_len, local_heads, HEAD_DIM)
    soft_probs = jnp.exp(score_rows() - log_total)
    soft_low = soft_probs.astype(jnp.bfloat16)
    grad_values = jnp.einsum(
        "bhqk,bqhe->bkhe", soft_low, grad_heads, preferred_element_type=jnp.float32
    )
    grad_soft = jnp.einsum(
        "bqhe,bkhe->bhqk", grad_heads, values, preferred_element_type=jnp.float32
    )
    grad_scores = (
        soft_probs * (grad_soft - jnp.sum(grad_soft * soft_probs, axis=-1, keepdims=True))
    ).astype(jnp.bfloat16)
    grad_queries = (
        jnp.einsum("bhqk,bkhe->bqhe", grad_scores, key_rows, preferred_element_type=jnp.float32)
        * score_scale
    )
    grad_keys = (
        jnp.einsum("bhqk,bqhe->bkhe", grad_scores, queries, preferred_element_type=jnp.float32)
        * score_scale
    )
    grad_joined = jnp.stack([grad_queries, grad_keys, grad_values], axis=2)
    grad_joined = grad_joined.reshape(rows_all, 3, local_heads * HEAD_DIM).astype(jnp.bfloat16)
    grad_w_qkv = jnp.einsum("td,tcf->dcf", h_one, grad_joined, preferred_element_type=jnp.float32)
    resid_own = lax.dynamic_slice_in_dim(grad_resid, offset, rows_own, 0)
    row_block = grad_joined
    grad_h_one = lax.psum_scatter(
        jnp.einsum("tcf,dcf->td", row_block, qkv_w, preferred_element_type=jnp.float32).astype(
            jnp.bfloat16
        ),
        "mp",
        scatter_dimension=0,
        tiled=True,
    ).astype(jnp.float32)
    unit_own = lax.dynamic_slice_in_dim(unit_one, offset, rows_own, 0)
    inv_own = lax.dynamic_slice_in_dim(inv_one, offset, rows_own, 0)
    grad_norm_one, grad_gain_one = norm_back(grad_h_one, unit_own, inv_own, gain_a_f)
    grad_tokens = resid_own + grad_norm_one
    summed = (
        lax.psum_scatter(grad_gain_one, "dp", scatter_dimension=0, tiled=True),
        lax.psum_scatter(grad_w_qkv, "dp", scatter_dimension=0, tiled=True),
        lax.psum_scatter(grad_w_out, "dp", scatter_dimension=1, tiled=True),
        lax.psum_scatter(grad_gain_two, "dp", scatter_dimension=0, tiled=True),
        lax.psum_scatter(grad_router, "dp", scatter_dimension=0, tiled=True),
    )
    gain_one_grad = summed[0]
    gain_one_grad = lax.psum(gain_one_grad, "mp")
    return (
        out_rows,
        grad_tokens,
        gain_one_grad,
        summed[1],
        summed[2],
        summed[3],
        summed[4],
        grad_w_in,
        grad_w_back,
        root_squares,
    )


def solution(mesh):
    in_specs = (
        P(("dp", "mp"), None),
        P("dp", None),
        P("dp"),
        P("dp", None, "mp"),
        P("mp", "dp"),
        P("dp"),
        P("dp", None),
        P("dp", None, "mp"),
        P("dp", "mp", None),
        P(("dp", "mp"), None),
    )
    out_specs = (
        P(("dp", "mp"), None),
        P(("dp", "mp"), None),
        P("dp"),
        P("dp", None, "mp"),
        P("mp", "dp"),
        P("dp"),
        P("dp", None),
        P("dp", None, "mp"),
        P("dp", "mp", None),
        P(None, "dp"),
    )
    return jax.shard_map(
        per_device, mesh=mesh, in_specs=in_specs, out_specs=out_specs, check_vma=False
    )
```

profile of v0, /device:TPU:0, one launch (start us, length us, event | category | flops | bytes accessed | tf_op | source)
XLA Modules:
  0.0 693.7 jit_solution(9787443473421323283)
XLA Ops:
  11.7 23.1 %all-reduce.6 = (bf16[768]{0:T(1024)(128)(2,1)S(1)}, bf16[768]{0:T(1024)(128)(2,1)S(1)}) all-reduce(bf16[768]{0:T(1024)(128)(2,1)S(1)} %dynamic-update-slice, bf16[768]{0:T(1024)(128)(2,1)S(1)} %dynamic-update-slice.1), channel_id=1, replica_groups=mesh['dp'=8,'mp'=4] {'dp'}, use_global_device_ids=true, to_apply=%add | all-reduce | flops 1536 | bytes 6144
  35.9 35.2 %all_gather.26 = bf16[768,3,192]{2,1,0:T(4,128)(2,1)S(1)} all-gather(bf16[96,3,192]{2,1,0:T(4,128)(2,1)S(1)} %copy.58), channel_id=1, replica_groups=mesh['dp'=8,'mp'=4] {'dp'}, dimensions={0}, use_global_device_ids=true | all-gather | bytes 995328 | tf_op jit(solution)/shard_map/all_gather | solution.py:70
  73.2 31.0 %all_gather.27 = bf16[192,768]{0,1:T(8,128)(2,1)S(1)} all-gather(bf16[192,96]{0,1:T(8,128)(2,1)S(1)} %copy.65), channel_id=1, replica_groups=mesh['dp'=8,'mp'=4] {'dp'}, dimensions={1}, use_global_device_ids=true | all-gather | bytes 331776 | tf_op jit(solution)/shard_map/all_gather | solution.py:73
  113.3 13.1 %reshape.228 = bf16[12,200,3,3,64]{1,0,4,3,2:T(8,128)(2,1)} reshape(bf16[2400,3,192]{0,2,1:T(8,128)(2,1)} %convert_element_type.93) | data formatting | bytes 5529600 | tf_op jit(solution)/shard_map/reshape | solution.py:87
  142.2 4.2 fusion.122
  146.4 65.7 %reduce-scatter.10.cloned.1.call-done = f32[600,768]{1,0:T(8,128)} async-done(((f32[2400,768]{1,0:T(8,128)}), f32[600,768]{1,0:T(8,128)}) %reduce-scatter.10.cloned.1.call-update) | async-done | bytes 1843216 | tf_op jit(solution)/shard_map/reduce_scatter | solution.py:108
  212.8 26.2 %all-gather = bf16[8,96,8]{1,2,0:T(8,128)(2,1)S(1)} all-gather(bf16[1,96,8]{1,2,0:T(8,128)(2,1)S(1)} %bitcast.198), channel_id=1, replica_groups=mesh['dp'=8,'mp'=4] {'dp'}, dimensions={0}, use_global_device_ids=true | all-gather | bytes 13824 | tf_op jit(solution)/shard_map/all_gather | solution.py:72
  239.1 27.2 %all-gather.7.cloned.1.call-done = f32[2400,768]{1,0:T(8,128)} async-done(((f32[600,768]{1,0:T(8,128)}), f32[2400,768]{1,0:T(8,128)}) %all-gather.7.cloned.1.call-update) | async-done | bytes 7372816 | tf_op jit(solution)/shard_map/all_gather | solution.py:114
  266.3 9.4 %fusion.117 = (f32[2400]{0:T(1024)S(1)}, f32[2400,768]{1,0:T(8,128)S(1)}, f32[2400]{0:T(1024)}, f32[2400,768]{1,0:T(8,128)}) fusion(f32[2400,768]{1,0:T(8,128)} %all-gather.7.cloned.1.call-done, bf16[2400,768]{1,0:T(8,128)(2,1)} %all-gather.5.cloned.1.call-done, f32[2400]{0:T(1024)S(1)} %add_rsqrt_fusion.1, f32[2400]{0:T(1024)S(1)} %broadcast_multiply_fusion.3), kind=kLoop, calls=%fused_computation.163 | loop fusion | flops 12897600 | bytes 25843200 | tf_op jit(solution)/shard_map/reduce_sum | solution.py:24
  287.0 12.3 %all-gather.9.cloned.1.call-done = bf16[2400,768]{1,0:T(8,128)(2,1)} async-done(((bf16[600,768]{1,0:T(8,128)(2,1)}), bf16[2400,768]{1,0:T(8,128)(2,1)}) %all-gather.9.cloned.1.call-update) | async-done | bytes 3686416 | tf_op jit(solution)/shard_map/all_gather | solution.py:66
  302.7 5.5 all-to-all-start.2
  311.6 5.0 all-to-all-done.2
  320.1 7.7 %all-to-all-done = bf16[12,8,768]{2,0,1:T(8,128)(2,1)S(1)} async-done(((bf16[12,8,768]{2,0,1:T(8,128)(2,1)}), bf16[12,8,768]{2,0,1:T(8,128)(2,1)S(1)}, u32[]{:S(2)}, u32[]{:S(2)}) %all-to-all-start) | async-done | bytes 147488 | tf_op jit(solution)/shard_map/all_to_all | solution.py:128
  330.3 16.4 %all-reduce.8 = (bf16[96,1,768]{2,0,1:T(8,128)(2,1)S(1)}, bf16[96,1,768]{2,0,1:T(8,128)(2,1)S(1)}) all-reduce(f32[96,1,768]{2,0,1:T(8,128)S(1)} %fusion.54, f32[96,1,768]{2,0,1:T(8,128)S(1)} %fusion.51), channel_id=1, replica_groups=mesh['dp'=8,'mp'=4] {'mp'}, use_global_device_ids=true, to_apply=%region_11.12 | all-reduce | flops 147456 | bytes 884736 | tf_op jit(solution)/shard_map/psum | solution.py:52
  354.3 5.1 all-to-all-done.1
  363.9 4.7 multiply_reduce_fusion
  374.5 4.5 fusion.90
  383.6 4.4 bitcast_add_fusion
  392.1 6.3 multiply_add_fusion
  398.3 5.3 convolution_convert_fusion
  403.7 5.5 reshape.240
  409.2 7.0 %fusion.33 = bf16[12,200,3,64]{1,3,2,0:T(8,128)(2,1)} fusion(f32[12,3,200]{2,1,0:T(4,128)S(1)} %log_add_fusion, f32[12,3,200,200]{2,3,1,0:T(8,128)} %copy-done.3, pred[12,200]{1,0:T(8,128)(4,1)S(1)} %broadcast_compare_fusion, bf16[12,200,3,64]{1,0,3,2:T(8,128)(2,1)} %reshape.240), kind=kOutput, calls=%fused_computation.61 | convolution fusion | flops 190540800 | bytes 7634400 | tf_op jit(solution)/shard_map/bhqk,bqhe->bkhe/dot_general | solution.py:189
  416.2 4.1 multiply_reduce_fusion.4
  426.6 5.6 fusion.37
  452.1 7.0 %bitcast_convert_fusion = bf16[2400,768]{1,0:T(8,128)(2,1)} fusion(bf16[2400,3,192]{0,2,1:T(8,128)(2,1)} %constant_dynamic-update-slice_fusion, bf16[768,3,192]{0,2,1:T(8,128)(2,1)} %copy.59), kind=kOutput, calls=%fused_computation.9 | convolution fusion | flops 2125209600 | bytes 7335936 | tf_op jit(solution)/shard_map/tcf,dcf->td/dot_general | solution.py:212
  459.8 8.4 %fusion.10 = f32[768,3,192]{2,0,1:T(8,128)} fusion(bf16[2400,3,192]{0,2,1:T(8,128)(2,1)} %constant_dynamic-update-slice_fusion, f32[768]{0:T(1024)S(1)} %copy-done.51, bf16[2400,768]{1,0:T(8,128)(2,1)} %all-gather.5.cloned.1.call-done, f32[2400]{0:T(1024)S(1)} %copy-done.44, f32[2400]{0:T(1024)S(1)} %copy-done.38), kind=kOutput, calls=%fused_computation.33 | convolution fusion | flops 2132582400 | bytes 8242944 | tf_op jit(solution)/shard_map/td,tcf->dcf/dot_general | solution.py:208
  480.1 24.1 %reduce-scatter.18.cloned.1.call-done = f32[96,8]{1,0:T(8,128)} async-done(((f32[768,8]{1,0:T(8,128)}), f32[96,8]{1,0:T(8,128)}) %reduce-scatter.18.cloned.1.call-update) | async-done | bytes 3088
  505.6 64.0 %reduce-scatter.16.cloned.1.call-done = f32[96,192]{1,0:T(8,128)} async-done(((f32[768,192]{1,0:T(8,128)}), f32[96,192]{1,0:T(8,128)}) %reduce-scatter.16.cloned.1.call-update) | async-done | bytes 73744
  571.3 41.2 %reduce-scatter.12.cloned.1.call-done = bf16[600,768]{1,0:T(8,128)(2,1)} async-done(((bf16[2400,768]{1,0:T(8,128)(2,1)}), bf16[600,768]{1,0:T(8,128)(2,1)}) %reduce-scatter.12.cloned.1.call-update) | async-done | bytes 921616 | tf_op jit(solution)/shard_map/reduce_scatter | solution.py:211
  615.1 21.8 %all-reduce.4 = (f32[768]{0:T(1024)S(1)}, f32[768]{0:T(1024)S(1)}) all-reduce(f32[768]{0:T(1024)S(1)} %get-tuple-element.12, f32[768]{0:T(1024)S(1)} %copy-done.52), channel_id=4, replica_groups=mesh['dp'=8,'mp'=4] {'dp'}, use_global_device_ids=true, to_apply=%region_22.23.clone | all-reduce | flops 1536 | bytes 12288
  637.6 6.5 psum.23
  648.2 38.2 %reduce-scatter.14.cloned.1.call-done = f32[96,3,192]{2,0,1:T(8,128)} async-done(((f32[768,3,192]{2,0,1:T(8,128)}), f32[96,3,192]{2,0,1:T(8,128)}) %reduce-scatter.14.cloned.1.call-update) | async-done | bytes 221200 | tf_op jit(solution)/shard_map/reduce_scatter | solution.py:225
  (240 shorter events, 130.9 us)
Async XLA Ops:
  7.2 321.0 %copy-start = (bf16[1,768,768]{2,1,0:T(8,128)(2,1)S(1)}, bf16[1,768,768]{2,1,0:T(8,128)(2,1)}, u32[]{:S(2)}) copy-start(bf16[1,768,768]{2,1,0:T(8,128)(2,1)} %param.18) | copy-start | bytes 3538948
  7.2 65.9 %copy-start.49 = (bf16[192,96]{1,0:T(8,128)(2,1)S(1)}, bf16[192,96]{1,0:T(8,128)(2,1)}, u32[]{:S(2)}) copy-start(bf16[192,96]{1,0:T(8,128)(2,1)} %param.14) | copy-start | bytes 110596
  7.2 97.0 %copy-start.46 = (s32[12,200]{1,0:T(8,128)S(1)}, s32[12,200]{1,0:T(8,128)}, u32[]{:S(2)}) copy-start(s32[12,200]{1,0:T(8,128)} %param.11) | copy-start | bytes 28804
  7.2 97.0 %all-gather.5.cloned.1.call-start = ((), (), s32[]{:S(2)}) async-start(), calls=%async_computation.9 | async-start | bytes 4608000 | tf_op jit(solution)/shard_map/all_gather | solution.py:65
  7.9 204.2 %reduce-scatter.10.cloned.1.call-start = ((), (), s32[]{:S(2)}) async-start(), calls=%async_computation.10 | async-start | bytes 9216000 | tf_op jit(solution)/shard_map/reduce_scatter | solution.py:108
  34.8 73.9 %copy-start.50 = (f32[768]{0:T(1024)}, f32[768]{0:T(1024)S(1)}, u32[]{:S(2)}) copy-start(f32[768]{0:T(1024)S(1)} %convert_element_type.91) | copy-start | bytes 9220
  104.2 37.9 %copy-start.17 = (bf16[192,768]{0,1:T(8,128)(2,1)}, bf16[192,768]{0,1:T(8,128)(2,1)S(1)}, u32[]{:S(2)}) copy-start(bf16[192,768]{0,1:T(8,128)(2,1)S(1)} %all_gather.27) | copy-start | bytes 884740
  107.5 158.8 %copy-start.37 = (f32[2400]{0:T(1024)}, f32[2400]{0:T(1024)S(1)}, u32[]{:S(2)}) copy-start(f32[2400]{0:T(1024)S(1)} %broadcast_multiply_fusion.3) | copy-start | bytes 28804
  108.8 157.5 %copy-start.43 = (f32[2400]{0:T(1024)}, f32[2400]{0:T(1024)S(1)}, u32[]{:S(2)}) copy-start(f32[2400]{0:T(1024)S(1)} %add_rsqrt_fusion.1) | copy-start | bytes 28804
  146.4 66.4 %copy-start.53 = (bf16[96,8]{0,1:T(8,128)(2,1)S(1)}, bf16[96,8]{0,1:T(8,128)(2,1)}, u32[]{:S(2)}) copy-start(bf16[96,8]{0,1:T(8,128)(2,1)} %param.16) | copy-start | bytes 4612
  146.4 119.9 %all-gather.7.cloned.1.call-start = ((), (), s32[]{:S(2)}) async-start(), calls=%async_computation.11 | async-start | bytes 9216000 | tf_op jit(solution)/shard_map/all_gather | solution.py:114
  212.2 87.1 %all-gather.9.cloned.1.call-start = ((), (), s32[]{:S(2)}) async-start(), calls=%async_computation.12 | async-start | bytes 4608000 | tf_op jit(solution)/shard_map/all_gather | solution.py:66
  239.1 42.3 %copy-start.39 = (bf16[768,8]{0,1:T(8,128)(2,1)}, bf16[768,8]{0,1:T(8,128)(2,1)S(1)}, u32[]{:S(2)}) copy-start(bf16[768,8]{0,1:T(8,128)(2,1)S(1)} %reshape.248) | copy-start | bytes 36868
  284.7 79.2 %copy-start.19 = (f32[12,200,8]{1,0,2:T(8,128)}, f32[12,200,8]{1,0,2:T(8,128)S(1)}, u32[]{:S(2)}) copy-start(f32[12,200,8]{1,0,2:T(8,128)S(1)} %reshape.229) | copy-start | bytes 230404
  284.8 18.0 %copy-start.31 = (f32[12,200]{1,0:T(8,128)}, f32[12,200]{1,0:T(8,128)S(1)}, u32[]{:S(2)}) copy-start(f32[12,200]{1,0:T(8,128)S(1)} %sub.110) | copy-start | bytes 28804
  284.9 17.8 %copy-start.34 = (f32[12,200]{1,0:T(8,128)}, f32[12,200]{1,0:T(8,128)S(1)}, u32[]{:S(2)}) copy-start(f32[12,200]{1,0:T(8,128)S(1)} %div.89) | copy-start | bytes 28804
  287.0 23.9 %copy-start.41 = (f32[12,8]{1,0:T(8,128)}, f32[12,8]{1,0:T(8,128)S(1)}, u32[]{:S(2)}) copy-start(f32[12,8]{1,0:T(8,128)S(1)} %get-tuple-element.42) | copy-start | bytes 1156
  302.0 25.8 %copy-start.16 = (bf16[1,768,768]{2,1,0:T(8,128)(2,1)S(1)}, bf16[1,768,768]{2,1,0:T(8,128)(2,1)}, u32[]{:S(2)}) copy-start(bf16[1,768,768]{2,1,0:T(8,128)(2,1)} %param.17) | copy-start | bytes 3538948
  302.7 13.9 %all-to-all-start.2 = ((bf16[12,8,768]{2,0,1:T(8,128)(2,1)}), bf16[12,8,768]{2,0,1:T(8,128)(2,1)S(1)}, u32[]{:S(2)}, u32[]{:S(2)}) async-start(bf16[12,8,768]{2,0,1:T(8,128)(2,1)} %copy.72), calls=%async_computation.3 | async-start | bytes 393216 | tf_op jit(solution)/shard_map/all_to_all | solution.py:153
  316.6 11.1 %all-to-all-start = ((bf16[12,8,768]{2,0,1:T(8,128)(2,1)}), bf16[12,8,768]{2,0,1:T(8,128)(2,1)S(1)}, u32[]{:S(2)}, u32[]{:S(2)}) async-start(bf16[12,8,768]{2,0,1:T(8,128)(2,1)} %copy.69), calls=%async_computation.1 | async-start | bytes 393216 | tf_op jit(solution)/shard_map/all_to_all | solution.py:128
  320.1 10.2 %copy-start.24 = (bf16[96,768]{1,0:T(8,128)(2,1)}, bf16[96,768]{1,0:T(8,128)(2,1)S(1)}, u32[]{:S(2)}) copy-start(bf16[96,768]{1,0:T(8,128)(2,1)S(1)} %reshape.237) | copy-start | bytes 442372
  329.7 34.1 %copy-start.32 = (f32[12,200]{1,0:T(8,128)S(1)}, f32[12,200]{1,0:T(8,128)}, u32[]{:S(2)}) copy-start(f32[12,200]{1,0:T(8,128)} %copy-done.31) | copy-start | bytes 28804
  329.7 34.2 %copy-start.35 = (f32[12,200]{1,0:T(8,128)S(1)}, f32[12,200]{1,0:T(8,128)}, u32[]{:S(2)}) copy-start(f32[12,200]{1,0:T(8,128)} %copy-done.34) | copy-start | bytes 28804
  348.6 10.8 %all-to-all-start.1 = ((bf16[8,2,4608]{2,1,0:T(2,128)(2,1)}), bf16[8,2,4608]{2,1,0:T(2,128)(2,1)S(1)}, u32[]{:S(2)}, u32[]{:S(2)}) async-start(bf16[8,2,4608]{2,1,0:T(2,128)(2,1)} %reshape.265), calls=%async_computation.2 | async-start | bytes 294912 | tf_op jit(solution)/shard_map/all_to_all | solution.py:53
  359.4 10.9 %all-to-all-start.3 = ((bf16[8,2,4608]{2,1,0:T(2,128)(2,1)}), bf16[8,2,4608]{2,1,0:T(2,128)(2,1)S(1)}, u32[]{:S(2)}, u32[]{:S(2)}) async-start(bf16[8,2,4608]{2,1,0:T(2,128)(2,1)} %reshape.267), calls=%async_computation.4 | async-start | bytes 294912 | tf_op jit(solution)/shard_map/all_to_all | solution.py:53
  362.8 141.4 %reduce-scatter.18.cloned.1.call-start = ((), (), s32[]{:S(2)}) async-start(), calls=%async_computation.16 | async-start | bytes 442368
  403.7 12.5 %slice-start.2 = ((s8[7372800]{0:T(1024)(128)(4,1)}), s8[3178496]{0:T(1024)(128)(4,1)S(1)}, s32[]{:S(2)}) async-start(s8[7372800]{0:T(1024)(128)(4,1)} %bitcast.187), calls=%async_computation.19 | async-start | bytes 6356992
  440.8 128.8 %reduce-scatter.16.cloned.1.call-start = ((), (), s32[]{:S(2)}) async-start(), calls=%async_computation.15 | async-start | bytes 884736
  445.8 166.8 %reduce-scatter.12.cloned.1.call-start = ((), (), s32[]{:S(2)}) async-start(), calls=%async_computation.13 | async-start | bytes 4608000 | tf_op jit(solution)/shard_map/reduce_scatter | solution.py:211
  459.2 227.2 %reduce-scatter.14.cloned.1.call-start = ((), (), s32[]{:S(2)}) async-start(), calls=%async_computation.14 | async-start | bytes 2654208 | tf_op jit(solution)/shard_map/reduce_scatter | solution.py:225
  476.7 138.4 %copy-start.52 = (f32[768]{0:T(1024)S(1)}, f32[768]{0:T(1024)}, u32[]{:S(2)}) copy-start(f32[768]{0:T(1024)} %get-tuple-element.10) | copy-start | bytes 9220
  612.6 73.9 %copy-start.1 = (bf16[1,768,768]{2,1,0:T(8,128)(2,1)S(1)}, bf16[1,768,768]{2,1,0:T(8,128)(2,1)}, u32[]{:S(2)}) copy-start(bf16[1,768,768]{2,1,0:T(8,128)(2,1)} %param.18) | copy-start | bytes 3538948
  (40 other events, 185.7 us)
Sparse Core Ops, SparseCore 0:
  9.6 34.2 all-gather.4
  146.5 65.6 reduce-scatter.9
  213.7 52.5 all-gather.6
  267.7 31.5 all-gather.8
  441.0 63.1 reduce-scatter.17
  507.3 62.2 reduce-scatter.15
  572.2 40.2 reduce-scatter.11
  616.6 69.7 reduce-scatter.13
where the time goes:
time: 700 us; the launch traced here: 694 us
  waiting for transfers between devices  292 us (42%)
  blocking collectives  160 us (23%)
  matrix products  90 us (13%)
  local copies, waits for them, and re-layouts  65.6 us (9%)
  other arithmetic  53.1 us (8%)
  between operations  16.9 us (2%)
  starting transfers between devices  16 us (2%)
    unnamed x10, waiting for transfers between devices  89.4 us
    reduce_scatter x1, waiting for transfers between devices, per_device(): lax.psum_scatter(jnp.dot(row_block, out_w, preferred_element_type=jnp.flo...  65.7 us
    unnamed x2, blocking collectives  45 us
    reduce_scatter x1, waiting for transfers between devices, per_device(): lax.psum_scatter(jnp.einsum('tcf,dcf->td', row_block, qkv_w, preferred_el...  41.2 us
    reduce_scatter x1, waiting for transfers between devices, per_device(): lax.psum_scatter(grad_w_qkv, 'dp', scatter_dimension=0, tiled=True)  38.2 us
    all_gather x1, blocking collectives, per_device(): lax.all_gather(w_qkv, 'dp', axis=0, tiled=True)  35.2 us
    all_gather x1, blocking collectives, per_device(): lax.all_gather(w_out, 'dp', axis=1, tiled=True)  31 us
    all_gather x1, waiting for transfers between devices, per_device(): branch_all = lax.all_gather(branch, 'mp', axis=0, tiled=True)  27.2 us
  transfers between devices with their start and end apart: 12, of which 10 were waited for; matrix products, arithmetic and copies ran while one was open for 12% of the time, Pallas kernels for 0%

commit v1 on v0

v1 whole, which is shorter than its diff:
```python
import jax
import jax.numpy as jnp
from jax import lax
from jax.sharding import PartitionSpec as P

HEAD_DIM = 64


epsilon = 1e-06
bf16 = jnp.bfloat16
f32 = jnp.float32


def softmax_over(array_in, axis_index):
    shifted = array_in - jnp.max(array_in, axis=axis_index, keepdims=True)
    exp_terms = jnp.exp(shifted)
    return exp_terms / jnp.sum(exp_terms, axis=axis_index, keepdims=True)


def gelu_tanh(array_in):
    tanh_arg = 0.7978845608028654 * (array_in + 0.044715 * array_in * array_in * array_in)
    return 0.5 * array_in * (1.0 + jnp.tanh(tanh_arg))


def normalize(array_in, gain_vec):
    mean_row = jnp.mean(array_in, axis=-1, keepdims=True)
    centered = array_in - mean_row
    variance = jnp.mean(centered * centered, axis=-1, keepdims=True)
    inverse = lax.rsqrt(variance + epsilon)
    unit_rows = centered * inverse
    return (unit_rows * gain_vec, unit_rows, inverse)


def norm_back(grad_rows, unit_rows, inverse, gain_vec):
    scaled = grad_rows * gain_vec
    mean_grad = jnp.mean(scaled, axis=-1, keepdims=True)
    mean_proj = jnp.mean(scaled * unit_rows, axis=-1, keepdims=True)
    return (
        inverse * (scaled - mean_grad - unit_rows * mean_proj),
        jnp.sum(grad_rows * unit_rows, axis=0),
    )


def root_mean(array_in, token_mask):
    images, seq_len = token_mask.shape
    weight_rows = token_mask.astype(jnp.float32)
    shaped = array_in.reshape(images, seq_len, -1)
    squares = jnp.sum(shaped * shaped, axis=-1)
    counted = jnp.sum(weight_rows, axis=1) * shaped.shape[2]
    return jnp.sqrt(jnp.sum(squares * weight_rows, axis=1) / counted)


def swap(array_in, axis_name, size, bit):
    return lax.ppermute(array_in, axis_name, [(i, i ^ bit) for i in range(size)])


def bits_of(size):
    return [1 << k for k in range(size.bit_length() - 1)]


def gather_dp(block, dp):
    index = lax.axis_index("dp")
    held = block[None]
    for bit in bits_of(dp):
        other = swap(held, "dp", dp, bit)
        upper = (index & bit) > 0
        held = jnp.where(
            upper, jnp.concatenate([other, held], 0), jnp.concatenate([held, other], 0)
        )
    return held


def gather_mp(block, mp):
    held = block[None]
    for bit in reversed(bits_of(mp)):
        other = swap(held, "mp", mp, bit)
        held = jnp.stack([held, other], 1).reshape((-1,) + block.shape)
    return held


def scatter_mp(held, mp):
    for bit in bits_of(mp):
        pairs = held.reshape((-1, 2) + held.shape[1:])
        other = swap(pairs[:, 1], "mp", mp, bit)
        held = (pairs[:, 0].astype(f32) + other.astype(f32)).astype(bf16)
    return held[0]


def scatter_dp(held, dp):
    index = lax.axis_index("dp")
    for bit in reversed(bits_of(dp)):
        half = held.shape[0] // 2
        upper = (index & bit) > 0
        low, high = held[:half], held[half:]
        other = swap(jnp.where(upper, low, high), "dp", dp, bit)
        held = (jnp.where(upper, high, low).astype(f32) + other.astype(f32)).astype(bf16)
    return held[0]


def make(mesh):
    dp, mp = mesh.shape["dp"], mesh.shape["mp"]

    def per_device(
        tokens, token_mask, gain_one, w_qkv, w_out, gain_two, router, w_in, w_back, cotangent
    ):
        rows = tokens.shape[0]
        width = tokens.shape[1]
        seq_len = token_mask.shape[1]
        images = rows // seq_len
        experts = router.shape[1]
        part = w_qkv.shape[2]
        heads = part // HEAD_DIM
        d_rows = w_qkv.shape[0]
        score_scale = HEAD_DIM ** (-0.5)
        mask = lax.dynamic_slice_in_dim(token_mask, lax.axis_index("mp") * images, images, 0)
        present = mask > 0
        key_keep = present[:, None, None, :]
        packed = jnp.concatenate([w_qkv.reshape(d_rows, 3 * part), w_out.T], axis=1)
        extra = jnp.concatenate([gain_one[:, None], gain_two[:, None], router], axis=1)
        extra = gather_dp(extra, dp).reshape(width, experts + 2)
        gain_a_f = extra[:, 0].astype(f32)
        gain_b_f = extra[:, 1].astype(f32)
        route_w = extra[:, 2:]
        weights = gather_mp(gather_dp(packed, dp).reshape(width, 4 * part), mp)
        qkv_w = weights[:, :, : 3 * part]
        out_w = weights[:, :, 3 * part :]

        tokens_f = tokens.astype(f32)
        h_one_f, unit_one, inv_one = normalize(tokens_f, gain_a_f)
        h_one = h_one_f.astype(bf16)
        joined = jnp.einsum("td,jdf->jtf", h_one, qkv_w, preferred_element_type=f32).astype(bf16)
        joined = joined.reshape(mp, images, seq_len, 3, heads, HEAD_DIM)
        queries, key_rows, values = joined[:, :, :, 0], joined[:, :, :, 1], joined[:, :, :, 2]
        raw = jnp.einsum("jbqhe,jbkhe->jbhqk", queries, key_rows, preferred_element_type=f32)
        scores = jnp.where(key_keep, raw * score_scale, -1e30)
        soft = softmax_over(scores, 4)
        attention = soft.astype(bf16)
        heads_out = jnp.einsum("jbhqk,jbkhe->jbqhe", attention, values, preferred_element_type=f32)
        heads_out = heads_out.astype(bf16).reshape(mp, rows, part)
        branch = jnp.einsum("jtf,jdf->td", heads_out, out_w, preferred_element_type=f32)
        resid = tokens_f + branch
        h_two_f, unit_two, inv_two = normalize(resid, gain_b_f)
        h_two = h_two_f.astype(bf16)
        logits = jnp.dot(h_two, route_w, preferred_element_type=f32)
        logits = logits.reshape(images, seq_len, experts)
        dispatch_f = softmax_over(jnp.where(present[:, :, None], logits, -1e30), 1)
        combine_f = softmax_over(logits, 2)
        dispatch = dispatch_f.astype(bf16)
        combine = combine_f.astype(bf16)
        h_two_img = h_two.reshape(images, seq_len, width)
        cot_img = cotangent.reshape(images, seq_len, width)
        slot_rows = jnp.einsum("bse,bsd->ebd", dispatch, h_two_img, preferred_element_type=f32)
        grad_slot = jnp.einsum("bse,bsd->ebd", combine, cot_img, preferred_element_type=f32)
        sent = jnp.stack([slot_rows, grad_slot], 1).astype(bf16)
        got = lax.all_to_all(sent, "dp", split_axis=0, concat_axis=0, tiled=True)
        got = gather_mp(got, mp)
        slot_in = got[:, :, 0].reshape(-1, width)
        grad_expert = got[:, :, 1].reshape(-1, width)
        first_w, second_w = w_in[0], w_back[0]
        pre_gelu = jnp.dot(slot_in, first_w, preferred_element_type=f32)
        hidden_f, gelu_pull = jax.vjp(gelu_tanh, pre_gelu)
        hidden = hidden_f.astype(bf16)
        partial_out = jnp.dot(hidden, second_w, preferred_element_type=f32)
        grad_hidden = jnp.einsum("nd,fd->nf", grad_expert, second_w, preferred_element_type=f32)
        grad_w_back = jnp.einsum("nf,nd->fd", hidden, grad_expert, preferred_element_type=f32)
        grad_pre = gelu_pull(grad_hidden)[0].astype(bf16)
        grad_w_in = jnp.einsum("nd,nf->df", slot_in, grad_pre, preferred_element_type=f32)
        grad_part = jnp.einsum("nf,df->nd", grad_pre, first_w, preferred_element_type=f32)
        shape = got[:, :, 0].shape
        back = jnp.stack([partial_out.reshape(shape), grad_part.reshape(shape)], 2).astype(bf16)
        back = scatter_mp(back, mp)
        back = lax.all_to_all(back, "dp", split_axis=0, concat_axis=0, tiled=True)
        returned, grad_slots = back[:, 0], back[:, 1]

        mixed = jnp.einsum("bse,ebd->bsd", combine, returned, preferred_element_type=f32)
        mixed = mixed.reshape(rows, width)
        stream = resid + mixed
        out_rows = stream.astype(bf16)
        squares = jnp.stack(
            [root_mean(stream, mask), root_mean(branch, mask), root_mean(mixed, mask)]
        )
        root_squares = lax.all_gather(squares, "mp", axis=1, tiled=True)
        grad_combine = jnp.einsum("bsd,ebd->bse", cot_img, returned, preferred_element_type=f32)
        grad_logit_c = combine_f * (
            grad_combine - jnp.sum(grad_combine * combine_f, axis=2, keepdims=True)
        )
        grad_dispatch = jnp.einsum("bsd,ebd->bse", h_two_img, grad_slots, preferred_element_type=f32)
        grad_logit_d = dispatch_f * (
            grad_dispatch - jnp.sum(grad_dispatch * dispatch_f, axis=1, keepdims=True)
        )
        grad_logits = (grad_logit_d + grad_logit_c).reshape(rows, experts).astype(bf16)
        grad_h_two = jnp.einsum(
            "bse,ebd->bsd", dispatch, grad_slots, preferred_element_type=f32
        ).reshape(rows, width)
        grad_h_two = grad_h_two + jnp.einsum(
            "te,de->td", grad_logits, route_w, preferred_element_type=f32
        )
        grad_router = jnp.einsum("td,te->de", h_two, grad_logits, preferred_element_type=f32)
        grad_norm_two, grad_gain_two = norm_back(grad_h_two, unit_two, inv_two, gain_b_f)
        grad_resid = cotangent.astype(f32) + grad_norm_two
        grad_branch = grad_resid.astype(bf16)
        grad_w_out = jnp.einsum("td,jtf->jdf", grad_branch, heads_out, preferred_element_type=f32)
        grad_heads = jnp.einsum("td,jdf->jtf", grad_branch, out_w, preferred_element_type=f32)
        grad_heads = grad_heads.astype(bf16).reshape(mp, images, seq_len, heads, HEAD_DIM)
        grad_values = jnp.einsum(
            "jbhqk,jbqhe->jbkhe", attention, grad_heads, preferred_element_type=f32
        )
        grad_soft = jnp.einsum(
            "jbqhe,jbkhe->jbhqk", grad_heads, values, preferred_element_type=f32
        )
        grad_scores = (
            soft * (grad_soft - jnp.sum(grad_soft * soft, axis=-1, keepdims=True))
        ).astype(bf16)
        grad_queries = score_scale * jnp.einsum(
            "jbhqk,jbkhe->jbqhe", grad_scores, key_rows, preferred_element_type=f32
        )
        grad_keys = score_scale * jnp.einsum(
            "jbhqk,jbqhe->jbkhe", grad_scores, queries, preferred_element_type=f32
        )
        grad_joined = jnp.stack([grad_queries, grad_keys, grad_values], axis=3).astype(bf16)
        grad_joined = grad_joined.reshape(mp, rows, 3 * part)
        grad_w_qkv = jnp.einsum("td,jtf->jdf", h_one, grad_joined, preferred_element_type=f32)
        grad_h_one = jnp.einsum("jtf,jdf->td", grad_joined, qkv_w, preferred_element_type=f32)
        grad_norm_one, grad_gain_one = norm_back(grad_h_one, unit_one, inv_one, gain_a_f)
        grad_tokens = grad_resid + grad_norm_one

        grads = jnp.concatenate([grad_w_qkv, grad_w_out], axis=2).astype(bf16)
        summed = scatter_mp(grads, mp).reshape(dp, d_rows, 4 * part)
        summed = scatter_dp(summed, dp).astype(f32)
        small = jnp.concatenate(
            [grad_gain_one[:, None], grad_gain_two[:, None], grad_router], axis=1
        )
        small = lax.psum(small, ("dp", "mp"))
        small = lax.dynamic_slice_in_dim(small, lax.axis_index("dp") * d_rows, d_rows, 0)
        return (
            out_rows,
            grad_tokens,
            small[:, 0],
            summed[:, : 3 * part].reshape(d_rows, 3, part),
            summed[:, 3 * part :].T,
            small[:, 1],
            small[:, 2:],
            grad_w_in[None],
            grad_w_back[None],
            root_squares,
        )

    return per_device


def solution(mesh):
    in_specs = (
        P(("dp", "mp"), None),
        P("dp", None),
        P("dp"),
        P("dp", None, "mp"),
        P("mp", "dp"),
        P("dp"),
        P("dp", None),
        P("dp", None, "mp"),
        P("dp", "mp", None),
        P(("dp", "mp"), None),
    )
    out_specs = (
        P(("dp", "mp"), None),
        P(("dp", "mp"), None),
        P("dp"),
        P("dp", None, "mp"),
        P("mp", "dp"),
        P("dp"),
        P("dp", None),
        P("dp", None, "mp"),
        P("dp", "mp", None),
        P(None, "dp"),
    )
    return jax.shard_map(
        make(mesh), mesh=mesh, in_specs=in_specs, out_specs=out_specs, check_vma=False
    )
```

time: 700 us -> 395 us (0.56)
  waiting for transfers between devices: 292 us -> 129 us
  blocking collectives: 160 us -> 66.9 us
  matrix products: 90 us -> 63.4 us
  other arithmetic: 53.1 us -> 37.7 us
  between operations: 16.9 us -> 1.65 us
  local copies, waits for them, and re-layouts: 65.6 us -> 72.6 us
    reduce_scatter x3 -> x0, waiting for transfers between devices: 145 us -> none  [the longest x1 65.7 us: per_device(): lax.psum_scatter(jnp.dot(row_block, out_w, preferred_element_type=jnp.flo...]
    ppermute x0 -> x17, waiting for transfers between devices: none -> 129 us  [swap(): lax.ppermute(array_in, axis_name, [(i, i ^ bit) for i in range(size)])]
    unnamed x10 -> x0, waiting for transfers between devices: 89.4 us -> none
    all_gather x3 -> x1, blocking collectives: 92.4 us -> 5.18 us  [per_device(): root_squares = lax.all_gather(squares, 'mp', axis=1, tiled=True)]
    unnamed x2 -> x0, blocking collectives: 45 us -> none
    all_gather x3 -> x0, waiting for transfers between devices: 39.5 us -> none  [the longest x1 27.2 us: per_device(): branch_all = lax.all_gather(branch, 'mp', axis=0, tiled=True)]
    all_to_all x0 -> x2, blocking collectives: none -> 22.4 us  [the longest x1 13 us: per_device(): got = lax.all_to_all(sent, 'dp', split_axis=0, concat_axis=0, tiled=True)]
    ppermute x0 -> x17, starting transfers between devices: none -> 19.2 us  [swap(): lax.ppermute(array_in, axis_name, [(i, i ^ bit) for i in range(size)])]
  transfers between devices with their start and end apart: 12 -> 17, of which waited for: 10 -> 15; matrix products, arithmetic and copies ran while one was open for 12% -> 5% of each run, Pallas kernels for 0% -> 0%
where the time goes in v1:
time: 395 us; the launch traced here: 391 us
  waiting for transfers between devices  129 us (33%)
  local copies, waits for them, and re-layouts  72.6 us (18%)
  blocking collectives  66.9 us (17%)
  matrix products  63.4 us (16%)
  other arithmetic  37.7 us (10%)
  starting transfers between devices  19.2 us (5%)
    ppermute x17, waiting for transfers between devices, swap(): lax.ppermute(array_in, axis_name, [(i, i ^ bit) for i in range(size)])  129 us
    psum x1, blocking collectives, per_device(): small = lax.psum(small, ('dp', 'mp'))  39.3 us
    ppermute x17, starting transfers between devices, swap(): lax.ppermute(array_in, axis_name, [(i, i ^ bit) for i in range(size)])  19.2 us
    all_to_all x1, blocking collectives, per_device(): got = lax.all_to_all(sent, 'dp', split_axis=0, concat_axis=0, tiled=True)  13 us
    unnamed x111, local copies, waits for them, and re-layouts  12.8 us
    reshape x1, local copies, waits for them, and re-layouts, per_device(): joined = joined.reshape(mp, images, seq_len, 3, heads, HEAD_DIM)  11.4 us
    convert_element_type x1, local copies, waits for them, and re-layouts, per_device(): jnp.stack([grad_queries, grad_keys, grad_values], axis=3).astype(bf16)  9.94 us
    all_to_all x1, blocking collectives, per_device(): back = lax.all_to_all(back, 'dp', split_axis=0, concat_axis=0, tiled=True)  9.34 us
  transfers between devices with their start and end apart: 17, of which 15 were waited for; matrix products, arithmetic and copies ran while one was open for 5% of the time, Pallas kernels for 0%

profile of v1, /device:TPU:0, one launch (start us, length us, event | category | flops | bytes accessed | tf_op | source)
XLA Modules:
  0.0 390.6 jit_solution(15745313901306707806)
XLA Ops:
  2.8 3.1 collective-permute-start
  5.9 3.8 collective-permute-done
  11.6 6.4 %collective-permute-done.1 = bf16[2,96,768]{2,1,0:T(8,128)(2,1)S(1)} collective-permute-done((bf16[2,96,768]{2,1,0:T(8,128)(2,1)S(1)}, bf16[2,96,768]{2,1,0:T(8,128)(2,1)S(1)}, u32[]{:S(2)}, u32[]{:S(2)}) %collective-permute-start.1) | collective-permute-done | bytes 294944 | tf_op jit(solution)/shard_map/ppermute | solution.py:54
  20.7 24.6 %collective-permute-done.2 = bf16[4,96,768]{2,1,0:T(8,128)(2,1)S(1)} collective-permute-done((bf16[4,96,768]{2,1,0:T(8,128)(2,1)S(1)}, bf16[4,96,768]{2,1,0:T(8,128)(2,1)S(1)}, u32[]{:S(2)}, u32[]{:S(2)}) %collective-permute-start.2) | collective-permute-done | bytes 589856 | tf_op jit(solution)/shard_map/ppermute | solution.py:54
  46.7 26.1 %collective-permute-done.3 = bf16[1,768,768]{2,1,0:T(8,128)(2,1)S(1)} collective-permute-done((bf16[1,768,768]{2,1,0:T(8,128)(2,1)S(1)}, bf16[1,768,768]{2,1,0:T(8,128)(2,1)S(1)}, u32[]{:S(2)}, u32[]{:S(2)}) %collective-permute-start.3) | collective-permute-done | bytes 1179680 | tf_op jit(solution)/shard_map/ppermute | solution.py:54
  90.5 4.2 %pad_maximum_fusion = bf16[2,2,768,768]{3,2,0,1:T(8,128)(2,1)} fusion(bf16[2,1,768,768]{3,2,0,1:T(8,128)(2,1)} %bitcast.8, bf16[2,1,768,768]{3,2,0,1:T(8,128)(2,1)S(1)} %get-tuple-element.59), kind=kLoop, calls=%fused_computation.9 | loop fusion | flops 2359296 | bytes 9437184 | tf_op jit(solution)/shard_map/stack | solution.py:77
  94.7 7.0 %copy.111 = bf16[2,2,768,768]{2,3,1,0:T(8,128)(2,1)} copy(bf16[2,2,768,768]{3,2,0,1:T(8,128)(2,1)} %pad_maximum_fusion) | data formatting | bytes 9437184 | tf_op jit(solution)/shard_map/stack | solution.py:77
  101.7 6.7 %convert_bitcast_fusion = bf16[4,600,576]{1,2,0:T(8,128)(2,1)} fusion(bf16[4,768,768]{1,2,0:T(8,128)(2,1)} %bitcast.266, bf16[600,768]{1,0:T(8,128)(2,1)S(1)} %copy-done.9, f32[768]{0:T(1024)S(1)} %get-tuple-element.47, f32[600]{0:T(1024)S(1)} %copy-done.46, f32[600]{0:T(1024)S(1)} %broadcast_multiply_fusion.5), kind=kOutput, calls=%fused_computation.23 | convolution fusion | flops 2127052800 | bytes 7233216 | tf_op jit(solution)/shard_map/td,jdf->jtf/dot_general | solution.py:131
  108.4 11.4 %reshape.322 = bf16[4,3,200,3,3,64]{2,1,5,4,3,0:T(4,128)(2,1)} reshape(bf16[4,600,576]{1,2,0:T(8,128)(2,1)} %convert_bitcast_fusion) | data formatting | bytes 5529600 | tf_op jit(solution)/shard_map/reshape | solution.py:132
  119.8 3.5 fusion.147
  126.2 3.2 fusion.150
  135.5 3.5 fusion.146
  145.5 13.0 %all_to_all.10 = bf16[8,2,3,768]{3,1,2,0:T(2,128)(2,1)S(1)} all-to-all(bf16[8,2,3,768]{3,1,2,0:T(2,128)(2,1)S(1)} %copy.120), channel_id=1, replica_groups=mesh['dp'=8,'mp'=4] {'dp'}, dimensions={0} | all-to-all | bytes 147456 | tf_op jit(solution)/shard_map/all_to_all | solution.py:155
  175.8 2.9 collective-permute-done.11
  178.7 9.3 %all_to_all.11 = bf16[8,2,3,768]{3,1,2,0:T(2,128)(2,1)S(1)} all-to-all(bf16[8,2,3,768]{3,1,2,0:T(2,128)(2,1)S(1)} %copy.130), channel_id=1, replica_groups=mesh['dp'=8,'mp'=4] {'dp'}, dimensions={0} | all-to-all | bytes 147456 | tf_op jit(solution)/shard_map/all_to_all | solution.py:172
  200.2 3.4 fusion.55
  203.5 4.7 %reshape.334 = bf16[4,3,200,3,64]{2,1,4,3,0:T(4,128)(2,1)} reshape(bf16[4,600,192]{1,2,0:T(8,128)(2,1)} %fusion.55) | data formatting | bytes 1843200 | tf_op jit(solution)/shard_map/reshape | solution.py:204
  208.3 8.0 %multiply_reduce_fusion = (f32[4,3,3,200]{3,2,1,0:T(4,128)S(1)}, f32[4,3,3,200,200]{3,4,2,1,0:T(8,128)}) fusion(f32[4,3,3,200,200]{3,4,2,1,0:T(8,128)} %copy-done.19, f32[4,3,3,200]{3,2,1,0:T(4,128)S(1)} %copy-done.35, bf16[4,3,200,1,3,64]{2,1,5,4,3,0:T(4,128)(2,1)S(1)} %copy-done.22, bf16[4,3,200,3,64]{2,1,4,3,0:T(4,128)(2,1)} %reshape.334), kind=kOutput, calls=%fused_computation.5 | convolution fusion | flops 188632800 | bytes 13420800 | tf_op jit(solution)/shard_map/jbqhe,jbkhe->jbhqk/dot_general | solution.py:208
  216.3 6.8 %multiply_convert_fusion = bf16[4,3,3,200,200]{3,4,2,1,0:T(8,128)(2,1)S(1)} fusion(f32[4,3,3,200,200]{3,4,2,1,0:T(8,128)} %get-tuple-element.87, f32[4,3,3,200]{3,2,1,0:T(4,128)S(1)} %get-tuple-element.86, f32[4,3,3,200,200]{3,4,2,1,0:T(8,128)} %copy-done.19, f32[4,3,3,200]{3,2,1,0:T(4,128)S(1)} %copy-done.35), kind=kLoop, calls=%fused_computation.4 | loop fusion | flops 5760000 | bytes 14457600 | tf_op jit(solution)/shard_map/convert_element_type | solution.py:213
  225.9 4.5 %fusion.49 = bf16[4,3,200,1,3,64]{2,5,4,1,0,3:T(8,128)(2,1)S(1)} fusion(bf16[4,3,200,3,64]{2,1,4,3,0:T(4,128)(2,1)S(1)} %copy-done.23, f32[4,3,3,200,200]{3,4,2,1,0:T(8,128)} %copy-done.19, f32[4,3,3,200]{3,2,1,0:T(4,128)S(1)} %copy-done.35), kind=kOutput, calls=%fused_computation.80 | convolution fusion | flops 187660800 | bytes 7632000 | tf_op jit(solution)/shard_map/jbhqk,jbqhe->jbkhe/dot_general | solution.py:205
  233.9 5.5 %copy.139 = bf16[4,3,200,3,3,64]{2,1,5,4,3,0:T(4,128)(2,1)} copy(bf16[4,3,200,3,3,64]{2,5,4,1,0,3:T(8,128)(2,1)S(1)} %pad_maximum_fusion.1) | data formatting | bytes 5529600 | tf_op jit(solution)/shard_map/stack | solution.py:220
  239.4 9.9 %convert_element_type.227 = bf16[4,600,576]{1,2,0:T(8,128)(2,1)} reshape(bf16[4,3,200,3,3,64]{2,1,5,4,3,0:T(4,128)(2,1)} %copy.139) | data formatting | bytes 5529600 | tf_op jit(solution)/shard_map/convert_element_type | solution.py:220
  249.4 6.8 %convolution_convert_fusion = bf16[4,576,768]{2,1,0:T(8,128)(2,1)} fusion(bf16[4,600,576]{1,2,0:T(8,128)(2,1)} %convert_element_type.227, bf16[600,768]{1,0:T(8,128)(2,1)S(1)} %copy-done.10, f32[768]{0:T(1024)S(1)} %copy-done.45, f32[600]{0:T(1024)S(1)} %copy-done.47, f32[600]{0:T(1024)S(1)} %copy-done.37), kind=kOutput, calls=%fused_computation.27 | convolution fusion | flops 2127439872 | bytes 7233216 | tf_op jit(solution)/shard_map/td,jtf->jdf/dot_general | solution.py:222
  256.2 6.0 %copy.140 = bf16[2,2,768,576]{3,2,0,1:T(8,128)(2,1)} copy(bf16[2,2,768,576]{2,3,1,0:T(8,128)(2,1)} %bitcast.270) | data formatting | bytes 7077888 | tf_op jit(solution)/shard_map/concatenate | solution.py:227
  264.0 3.4 fusion.16
  272.3 3.3 fusion.13
  277.3 4.8 %fusion.31 = (f32[768]{0:T(1024)S(1)}, f32[600]{0:T(1024)S(1)}, f32[600]{0:T(1024)S(1)}, f32[600,768,1]{1,0,2:T(8,128)S(1)}) fusion(bf16[600,768]{1,0:T(8,128)(2,1)S(1)} %copy-done.11, f32[600]{0:T(1024)S(1)} %copy-done.47, f32[600]{0:T(1024)S(1)} %copy-done.37, f32[768]{0:T(1024)S(1)} %copy-done.45, bf16[4,600,576]{1,2,0:T(8,128)(2,1)S(1)} %copy-done.20, ...), kind=kOutput, calls=%fused_computation.49 | convolution fusion | flops 2127511552 | bytes 9084288 | tf_op jit(solution)/shard_map/jtf,jdf->td/dot_general | solution.py:223
  282.4 21.4 %collective-permute-done.13 = bf16[1,768,768]{2,1,0:T(8,128)(2,1)S(1)} collective-permute-done((bf16[1,768,768]{2,1,0:T(8,128)(2,1)S(1)}, bf16[1,768,768]{2,1,0:T(8,128)(2,1)S(1)}, u32[]{:S(2)}, u32[]{:S(2)}) %collective-permute-start.13) | collective-permute-done | bytes 1179680 | tf_op jit(solution)/shard_map/ppermute | solution.py:54
  307.5 24.4 %collective-permute-done.14 = bf16[4,96,768]{2,1,0:T(8,128)(2,1)S(1)} collective-permute-done((bf16[4,96,768]{2,1,0:T(8,128)(2,1)S(1)}, bf16[4,96,768]{2,1,0:T(8,128)(2,1)S(1)}, u32[]{:S(2)}, u32[]{:S(2)}) %collective-permute-start.14) | collective-permute-done | bytes 589856 | tf_op jit(solution)/shard_map/ppermute | solution.py:54
  333.1 8.0 %collective-permute-done.15 = bf16[2,96,768]{2,1,0:T(8,128)(2,1)S(1)} collective-permute-done((bf16[2,96,768]{2,1,0:T(8,128)(2,1)S(1)}, bf16[2,96,768]{2,1,0:T(8,128)(2,1)S(1)}, u32[]{:S(2)}, u32[]{:S(2)}) %collective-permute-start.15) | collective-permute-done | bytes 294944 | tf_op jit(solution)/shard_map/ppermute | solution.py:54
  341.9 5.2 %all-gather = f32[4,3,3]{2,1,0:T(4,128)S(1)} all-gather(f32[1,3,3]{2,1,0:T(4,128)S(1)} %bitcast.285), channel_id=1, replica_groups=mesh['dp'=8,'mp'=4] {'mp'}, dimensions={0}, use_global_device_ids=true | all-gather | bytes 180 | tf_op jit(solution)/shard_map/all_gather | solution.py:182
  347.8 39.3 %psum.7 = f32[768,10]{0,1:T(8,128)S(1)} all-reduce(f32[768,10]{0,1:T(8,128)S(1)} %pad_maximum_fusion.9), channel_id=1, replica_groups=mesh['dp'=8,'mp'=4] {'dp','mp'}, use_global_device_ids=true, to_apply=%region_19.20 | all-reduce | flops 7680 | bytes 61440 | tf_op jit(solution)/shard_map/psum | solution.py:233
  (238 shorter events, 94.5 us)
Async XLA Ops:
  0.6 164.2 %copy-start = (bf16[1,768,768]{2,1,0:T(8,128)(2,1)S(1)}, bf16[1,768,768]{2,1,0:T(8,128)(2,1)}, u32[]{:S(2)}) copy-start(bf16[1,768,768]{2,1,0:T(8,128)(2,1)} %param.17) | copy-start | bytes 3538948
  2.8 6.9 %collective-permute-start = (bf16[1,96,768]{2,1,0:T(8,128)(2,1)S(1)}, bf16[1,96,768]{2,1,0:T(8,128)(2,1)S(1)}, u32[]{:S(2)}, u32[]{:S(2)}) collective-permute-start(bf16[1,96,768]{2,1,0:T(8,128)(2,1)S(1)} %bitcast.278), channel_id=1, source_target_pairs={{0,4},{4,0},{8,12},{12,8},{16,20},{20,16},{24,28},{28,24},{1,5},{5... | collective-permute-start | bytes 442376 | tf_op jit(solution)/shard_map/ppermute | solution.py:54
  9.8 8.2 %collective-permute-start.1 = (bf16[2,96,768]{2,1,0:T(8,128)(2,1)S(1)}, bf16[2,96,768]{2,1,0:T(8,128)(2,1)S(1)}, u32[]{:S(2)}, u32[]{:S(2)}) collective-permute-start(bf16[2,96,768]{2,1,0:T(8,128)(2,1)S(1)} %maximum_select_fusion.2), channel_id=1, source_target_pairs={{0,8},{4,12},{8,0},{12,4},{16,24},{20,28},{24,16},{28,20},{1,9},{5... | collective-permute-start | bytes 884744 | tf_op jit(solution)/shard_map/ppermute | solution.py:54
  18.1 27.2 %collective-permute-start.2 = (bf16[4,96,768]{2,1,0:T(8,128)(2,1)S(1)}, bf16[4,96,768]{2,1,0:T(8,128)(2,1)S(1)}, u32[]{:S(2)}, u32[]{:S(2)}) collective-permute-start(bf16[4,96,768]{2,1,0:T(8,128)(2,1)S(1)} %maximum_select_fusion.1), channel_id=1, source_target_pairs={{0,16},{4,20},{8,24},{12,28},{16,0},{20,4},{24,8},{28,12},{1,17},{... | collective-permute-start | bytes 1769480 | tf_op jit(solution)/shard_map/ppermute | solution.py:54
  45.5 27.3 %collective-permute-start.3 = (bf16[1,768,768]{2,1,0:T(8,128)(2,1)S(1)}, bf16[1,768,768]{2,1,0:T(8,128)(2,1)S(1)}, u32[]{:S(2)}, u32[]{:S(2)}) collective-permute-start(bf16[1,768,768]{2,1,0:T(8,128)(2,1)S(1)} %bitcast.264), channel_id=1, source_target_pairs={{0,2},{1,3},{2,0},{3,1},{4,6},{5,7},{6,4},{7,5},{8,10},{9,11},{10,... | collective-permute-start | bytes 3538952 | tf_op jit(solution)/shard_map/ppermute | solution.py:54
  74.5 15.9 %collective-permute-start.4 = (bf16[2,768,768]{2,1,0:T(8,128)(2,1)}, bf16[2,768,768]{2,1,0:T(8,128)(2,1)}, u32[]{:S(2)}, u32[]{:S(2)}) collective-permute-start(bf16[2,768,768]{2,1,0:T(8,128)(2,1)} %get-tuple-element.60), channel_id=1, source_target_pairs={{0,1},{1,0},{2,3},{3,2},{4,5},{5,4},{6,7},{7,6},{8,9},{9,8},{10,11... | collective-permute-start | bytes 7077896 | tf_op jit(solution)/shard_map/ppermute | solution.py:54
  74.6 3.7 collective-permute-start.5
  75.7 26.0 %copy-start.36 = (f32[600]{0:T(1024)}, f32[600]{0:T(1024)S(1)}, u32[]{:S(2)}) copy-start(f32[600]{0:T(1024)S(1)} %broadcast_multiply_fusion.5) | copy-start | bytes 7204
  78.2 3.8 collective-permute-start.6
  82.9 4.7 %collective-permute-start.7 = (bf16[4,96,10]{1,2,0:T(8,128)(2,1)S(1)}, bf16[4,96,10]{1,2,0:T(8,128)(2,1)S(1)}, u32[]{:S(2)}, u32[]{:S(2)}) collective-permute-start(bf16[4,96,10]{1,2,0:T(8,128)(2,1)S(1)} %maximum_select_fusion.4), channel_id=1, source_target_pairs={{0,16},{4,20},{8,24},{12,28},{16,0},{20,4},{24,8},{28,12},{1,17},{... | collective-permute-start | bytes 23048 | tf_op jit(solution)/shard_map/ppermute | solution.py:54
  90.4 11.2 %copy-start.44 = (f32[768]{0:T(1024)}, f32[768]{0:T(1024)S(1)}, u32[]{:S(2)}) copy-start(f32[768]{0:T(1024)S(1)} %get-tuple-element.47) | copy-start | bytes 9220
  94.7 7.0 %copy-start.9 = (bf16[600,768]{1,0:T(8,128)(2,1)S(1)}, bf16[600,768]{1,0:T(8,128)(2,1)}, u32[]{:S(2)}) copy-start(bf16[600,768]{1,0:T(8,128)(2,1)} %param.10) | copy-start | bytes 2764804
  94.7 7.0 %copy-start.46 = (f32[600]{0:T(1024)S(1)}, f32[600]{0:T(1024)}, u32[]{:S(2)}) copy-start(f32[600]{0:T(1024)} %add_rsqrt_fusion.1) | copy-start | bytes 7204
  158.5 4.4 %collective-permute-start.8 = (bf16[1,8,2,3,768]{4,1,3,2,0:T(8,128)(2,1)S(1)}, bf16[1,8,2,3,768]{4,1,3,2,0:T(8,128)(2,1)S(1)}, u32[]{:S(2)}, u32[]{:S(2)}) collective-permute-start(bf16[1,8,2,3,768]{4,1,3,2,0:T(8,128)(2,1)S(1)} %bitcast.280), channel_id=1, source_target_pairs={{0,2},{1,3},{2,0},{3,1},{4,6},{5,7},{6,4},{7,5},{8,10},{9,11},{10,... | collective-permute-start | bytes 221192 | tf_op jit(solution)/shard_map/ppermute | solution.py:54
  162.9 1.4 collective-permute-start.9
  171.0 17.2 %copy-start.3 = (bf16[600,768]{1,0:T(8,128)(2,1)S(1)}, bf16[600,768]{1,0:T(8,128)(2,1)}, u32[]{:S(2)}) copy-start(bf16[600,768]{1,0:T(8,128)(2,1)} %copy-done.2) | copy-start | bytes 2764804
  172.7 15.9 %copy-start.29 = (f32[3,200,8]{1,2,0:T(8,128)S(1)}, f32[3,200,8]{1,2,0:T(8,128)}, u32[]{:S(2)}) copy-start(f32[3,200,8]{1,2,0:T(8,128)} %copy-done.28) | copy-start | bytes 57604
  172.7 15.9 %copy-start.43 = (f32[3,8]{1,0:T(4,128)S(1)}, f32[3,8]{1,0:T(4,128)}, u32[]{:S(2)}) copy-start(f32[3,8]{1,0:T(4,128)} %copy-done.42) | copy-start | bytes 292
  172.7 1.4 collective-permute-start.10
  174.2 16.2 %copy-start.12 = (bf16[600,768]{1,0:T(8,128)(2,1)S(1)}, bf16[600,768]{1,0:T(8,128)(2,1)}, u32[]{:S(2)}) copy-start(bf16[600,768]{1,0:T(8,128)(2,1)} %param.19) | copy-start | bytes 2764804
  174.2 4.4 %collective-permute-start.11 = (bf16[1,8,2,3,768]{4,1,3,2,0:T(8,128)(2,1)S(1)}, bf16[1,8,2,3,768]{4,1,3,2,0:T(8,128)(2,1)S(1)}, u32[]{:S(2)}, u32[]{:S(2)}) collective-permute-start(bf16[1,8,2,3,768]{4,1,3,2,0:T(8,128)(2,1)S(1)} %slice_bitcast_fusion.3), channel_id=1, source_target_pairs={{0,2},{1,3},{2,0},{3,1},{4,6},{5,7},{6,4},{7,5},{8,10},{9,11},{10,... | collective-permute-start | bytes 221192 | tf_op jit(solution)/shard_map/ppermute | solution.py:54
  216.3 6.8 %copy-start.7 = (bf16[4,3,200,1,3,64]{2,1,5,4,3,0:T(4,128)(2,1)S(1)}, bf16[4,3,200,1,3,64]{2,1,5,4,3,0:T(4,128)(2,1)}, u32[]{:S(2)}) copy-start(bf16[4,3,200,1,3,64]{2,1,5,4,3,0:T(4,128)(2,1)} %copy-done.6) | copy-start | bytes 2764804
  239.4 10.0 %copy-start.10 = (bf16[600,768]{1,0:T(8,128)(2,1)S(1)}, bf16[600,768]{1,0:T(8,128)(2,1)}, u32[]{:S(2)}) copy-start(bf16[600,768]{1,0:T(8,128)(2,1)} %param.10) | copy-start | bytes 2764804
  239.4 10.0 %copy-start.37 = (f32[600]{0:T(1024)S(1)}, f32[600]{0:T(1024)}, u32[]{:S(2)}) copy-start(f32[600]{0:T(1024)} %copy-done.36) | copy-start | bytes 7204
  239.4 10.0 %copy-start.45 = (f32[768]{0:T(1024)S(1)}, f32[768]{0:T(1024)}, u32[]{:S(2)}) copy-start(f32[768]{0:T(1024)} %copy-done.44) | copy-start | bytes 9220
  239.4 10.0 %copy-start.47 = (f32[600]{0:T(1024)S(1)}, f32[600]{0:T(1024)}, u32[]{:S(2)}) copy-start(f32[600]{0:T(1024)} %add_rsqrt_fusion.1) | copy-start | bytes 7204
  267.4 4.9 %collective-permute-start.12 = (bf16[2,768,768]{2,1,0:T(8,128)(2,1)}, bf16[2,768,768]{2,1,0:T(8,128)(2,1)}, u32[]{:S(2)}, u32[]{:S(2)}) collective-permute-start(bf16[2,768,768]{2,1,0:T(8,128)(2,1)} %fusion.16), channel_id=1, source_target_pairs={{0,1},{1,0},{2,3},{3,2},{4,5},{5,4},{6,7},{7,6},{8,9},{9,8},{10,11... | collective-permute-start | bytes 7077896 | tf_op jit(solution)/shard_map/ppermute | solution.py:54
  275.7 28.1 %collective-permute-start.13 = (bf16[1,768,768]{2,1,0:T(8,128)(2,1)S(1)}, bf16[1,768,768]{2,1,0:T(8,128)(2,1)S(1)}, u32[]{:S(2)}, u32[]{:S(2)}) collective-permute-start(bf16[1,768,768]{2,1,0:T(8,128)(2,1)S(1)} %slice_bitcast_fusion), channel_id=1, source_target_pairs={{0,2},{1,3},{2,0},{3,1},{4,6},{5,7},{6,4},{7,5},{8,10},{9,11},{10,... | collective-permute-start | bytes 3538952 | tf_op jit(solution)/shard_map/ppermute | solution.py:54
  304.2 27.7 %collective-permute-start.14 = (bf16[4,96,768]{2,1,0:T(8,128)(2,1)S(1)}, bf16[4,96,768]{2,1,0:T(8,128)(2,1)S(1)}, u32[]{:S(2)}, u32[]{:S(2)}) collective-permute-start(bf16[4,96,768]{2,1,0:T(8,128)(2,1)S(1)} %bitcast.276), channel_id=1, source_target_pairs={{0,16},{4,20},{8,24},{12,28},{16,0},{20,4},{24,8},{28,12},{1,17},{... | collective-permute-start | bytes 1769480 | tf_op jit(solution)/shard_map/ppermute | solution.py:54
  332.1 9.0 %collective-permute-start.15 = (bf16[2,96,768]{2,1,0:T(8,128)(2,1)S(1)}, bf16[2,96,768]{2,1,0:T(8,128)(2,1)S(1)}, u32[]{:S(2)}, u32[]{:S(2)}) collective-permute-start(bf16[2,96,768]{2,1,0:T(8,128)(2,1)S(1)} %broadcast_select_fusion.2), channel_id=1, source_target_pairs={{0,8},{4,12},{8,0},{12,4},{16,24},{20,28},{24,16},{28,20},{1,9},{5... | collective-permute-start | bytes 884744 | tf_op jit(solution)/shard_map/ppermute | solution.py:54
  341.1 49.3 %copy-start.1 = (bf16[1,768,768]{2,1,0:T(8,128)(2,1)S(1)}, bf16[1,768,768]{2,1,0:T(8,128)(2,1)}, u32[]{:S(2)}) copy-start(bf16[1,768,768]{2,1,0:T(8,128)(2,1)} %param.17) | copy-start | bytes 3538948
  341.3 47.2 %collective-permute-start.16 = (bf16[1,96,768]{2,1,0:T(8,128)(2,1)S(1)}, bf16[1,96,768]{2,1,0:T(8,128)(2,1)S(1)}, u32[]{:S(2)}, u32[]{:S(2)}) collective-permute-start(bf16[1,96,768]{2,1,0:T(8,128)(2,1)S(1)} %broadcast_select_fusion.3), channel_id=1, source_target_pairs={{0,4},{4,0},{8,12},{12,8},{16,20},{20,16},{24,28},{28,24},{1,5},{5... | collective-permute-start | bytes 442376 | tf_op jit(solution)/shard_map/ppermute | solution.py:54
  (38 other events, 91.0 us)

commit v2 on v1

v2 whole, which is shorter than its diff:
```python
import functools
import math

import jax
import jax.numpy as jnp
from jax import lax
from jax.experimental import pallas as pl
from jax.experimental.pallas import tpu as pltpu
from jax.sharding import PartitionSpec as P

HEAD_DIM = 64


epsilon = 1e-06
bf16 = jnp.bfloat16
f32 = jnp.float32


def swap(array_in, axis_name, size, bit):
    return lax.ppermute(array_in, axis_name, [(i, i ^ bit) for i in range(size)])


def bits_of(size):
    return [1 << k for k in reversed(range(size.bit_length() - 1))]


def gather_pair(block, dp, mp, late):
    held = block
    depth = 0
    bits = bits_of(dp)
    for bit in bits[:-1] if late else bits:
        held = jnp.stack([held, swap(held, "dp", dp, bit)], depth)
        depth += 1
    held = jnp.stack([held, swap(held, "mp", mp, 2)], 0)
    if late:
        held = jnp.stack([held, swap(held, "dp", dp, bits[-1])], depth + 1)
    held = held.reshape((mp // 2, dp) + block.shape)
    return held, swap(held, "mp", mp, 1)


def gather_mp(block, mp):
    held = block[None]
    for bit in bits_of(mp):
        other = swap(held, "mp", mp, bit)
        held = jnp.stack([held, other], 1).reshape((-1,) + block.shape)
    return held


def scatter(held, axis_name, size, bits):
    left = sorted(bits)
    for bit in bits:
        inner = 1 << left.index(bit)
        left.remove(bit)
        pairs = held.reshape((held.shape[0] // (2 * inner), 2, inner) + held.shape[1:])
        other = swap(pairs[:, 1], axis_name, size, bit)
        held = pairs[:, 0].astype(f32) + other.astype(f32)
        held = held.astype(bf16).reshape((-1,) + held.shape[2:])
    return held[0]


def mm(a, b):
    return lax.dot_general(a, b, (((1,), (0,)), ((), ())), preferred_element_type=f32)


def mm_nt(a, b):
    return lax.dot_general(a, b, (((1,), (1,)), ((), ())), preferred_element_type=f32)


def mm_tn(a, b):
    return lax.dot_general(a, b, (((0,), (0,)), ((), ())), preferred_element_type=f32)


def unit_of(rows_f):
    mean_row = jnp.mean(rows_f, axis=-1, keepdims=True)
    centered = rows_f - mean_row
    variance = jnp.mean(centered * centered, axis=-1, keepdims=True)
    inverse = lax.rsqrt(variance + epsilon)
    return centered * inverse, inverse


def padded(value, pad):
    return jnp.concatenate([value, jnp.zeros((pad, value.shape[1]), value.dtype)], 0)


def low_lanes(rows):
    return lax.broadcasted_iota(jnp.int32, (rows, 128), 1) < HEAD_DIM


JOINED = 640


def front_kernel(
    x_ref, bias_ref, gain_ref, w_ref, h_ref, qkv_ref, p_ref, ho_ref, br_ref, *, images, seq, tall
):
    groups = w_ref.shape[0]
    scale = HEAD_DIM ** (-0.5)
    for b in range(images):
        unit, _ = unit_of(x_ref[b].astype(f32))
        h_ref[pl.ds(b * tall, tall), :] = padded((unit * gain_ref[...]).astype(bf16), tall - seq)
    br_ref[...] = jnp.zeros_like(br_ref)
    low = low_lanes(tall)

    def group(j, carry):
        qkv_ref[j] = mm(h_ref[...], w_ref[j, :, :JOINED]).astype(bf16)

        def image(b, inner):
            at = pl.ds(pl.multiple_of(b * tall, 16), tall)
            joined = qkv_ref[j, at, :]
            q_pair, k_pair, v_pair = joined[:, :128], joined[:, 128:256], joined[:, 256:384]
            qk_last, v_last = joined[:, 384:512], joined[:, 512:640]
            k_last = pltpu.roll(qk_last.astype(f32), HEAD_DIM, 1).astype(bf16)
            none = jnp.zeros_like(q_pair)
            bias = bias_ref[b]
            outs = []
            for head, (q, k, v) in enumerate(
                (
                    (jnp.where(low, q_pair, none), k_pair, v_pair),
                    (jnp.where(low, none, q_pair), k_pair, v_pair),
                    (jnp.where(low, qk_last, none), k_last, v_last),
                )
            ):
                scores = mm_nt(q, k) * scale + bias
                terms = jnp.exp(scores - jnp.max(scores, axis=-1, keepdims=True))
                probs = (terms * (1.0 / jnp.sum(terms, axis=-1, keepdims=True))).astype(bf16)
                p_ref[j, b, head] = probs
                outs.append(mm(probs, v))
            last = jnp.where(low, 0.0, pltpu.roll(outs[2], HEAD_DIM, 1))
            pair = jnp.where(low, outs[0], outs[1])
            ho_ref[j, at, :] = jnp.concatenate([last, pair], 1).astype(bf16)
            return inner

        lax.fori_loop(0, images, image, 0, unroll=True)
        br_ref[...] += mm_nt(ho_ref[j], w_ref[j, :, 512:])
        return carry

    lax.fori_loop(0, groups, group, 0)


def route_kernel(
    x_ref, br_ref, cot_ref, mask_ref, column_ref, gain_ref, router_ref,
    res_ref, h_ref, soft_ref, sent_ref, sq_ref, *, images, seq, tall
):
    for b in range(images):
        at = pl.ds(b * tall, tall)
        branch = br_ref[at, :]
        resid = padded(x_ref[b].astype(f32), tall - seq) + branch
        res_ref[at, :] = resid
        unit, _ = unit_of(resid)
        h_two = (unit * gain_ref[...]).astype(bf16)
        h_ref[at, :] = h_two
        logits = mm_nt(router_ref[...], h_two)
        seen = mask_ref[b] > 0
        held = jnp.where(seen, logits, -1e30)
        terms = jnp.exp(held - jnp.max(held, axis=1, keepdims=True))
        dispatch = terms / jnp.sum(terms, axis=1, keepdims=True)
        terms = jnp.exp(logits - jnp.max(logits, axis=0, keepdims=True))
        combine = terms / jnp.sum(terms, axis=0, keepdims=True)
        soft_ref[0, b] = dispatch
        soft_ref[1, b] = combine
        cot = padded(cot_ref[b], tall - seq)
        sent_ref[0, b] = mm(dispatch.astype(bf16), h_two).astype(bf16)
        sent_ref[1, b] = mm(combine.astype(bf16), cot).astype(bf16)
        squares = jnp.sum(branch * branch, axis=1, keepdims=True)
        sq_ref[b] = jnp.broadcast_to(
            jnp.sum(squares * column_ref[b], axis=0, keepdims=True), (1, 128)
        )


def expert_kernel(slot_ref, grad_ref, first_ref, second_ref, hid_ref, pre_ref, back_ref):
    slots, grads = slot_ref[...], grad_ref[...]
    u = mm(slots, first_ref[...])
    cubic = 0.7978845608028654 * (u + 0.044715 * u * u * u)
    t = jnp.tanh(cubic)
    hidden = (0.5 * u * (1.0 + t)).astype(bf16)
    hid_ref[...] = hidden
    back_ref[0] = mm(hidden, second_ref[...]).astype(bf16)
    slope = 0.5 * (1.0 + t) + 0.5 * u * (1.0 - t * t) * 0.7978845608028654 * (
        1.0 + 3.0 * 0.044715 * u * u
    )
    grad_pre = (mm_nt(grads, second_ref[...]) * slope).astype(bf16)
    pre_ref[...] = grad_pre
    back_ref[1] = mm_nt(grad_pre, first_ref[...]).astype(bf16)


def mix_kernel(
    res_ref, h_ref, soft_ref, cot_ref, column_ref, gain_ref, router_ref, back_ref,
    out_ref, gres_ref, grouter_ref, ggain_ref, sq_ref, *, images, seq, tall
):
    grouter_ref[...] = jnp.zeros_like(grouter_ref)
    ggain_ref[...] = jnp.zeros_like(ggain_ref)
    for b in range(images):
        at = pl.ds(b * tall, tall)
        resid, h_two = res_ref[at, :], h_ref[at, :]
        dispatch, combine = soft_ref[0, b], soft_ref[1, b]
        dispatch_low, combine_low = dispatch.astype(bf16), combine.astype(bf16)
        returned, grad_slots = back_ref[0, b], back_ref[1, b]
        cot = padded(cot_ref[b], tall - seq)
        mixed = mm_tn(combine_low, returned)
        stream = resid + mixed
        out_ref[b] = stream[:seq].astype(bf16)
        column = column_ref[b]
        for k, value in enumerate((stream, mixed)):
            squares = jnp.sum(value * value, axis=1, keepdims=True)
            sq_ref[k, b] = jnp.broadcast_to(
                jnp.sum(squares * column, axis=0, keepdims=True), (1, 128)
            )
        grad_c = mm_nt(returned, cot)
        grad_c = combine * (grad_c - jnp.sum(grad_c * combine, axis=0, keepdims=True))
        grad_d = mm_nt(grad_slots, h_two)
        grad_d = dispatch * (grad_d - jnp.sum(grad_d * dispatch, axis=1, keepdims=True))
        grad_logits = (grad_d + grad_c).astype(bf16)
        grad_h = mm_tn(dispatch_low, grad_slots) + mm_tn(grad_logits, router_ref[...])
        grouter_ref[...] += mm(grad_logits, h_two)
        unit, inverse = unit_of(resid)
        ggain_ref[...] += jnp.sum(grad_h * unit, axis=0, keepdims=True)
        scaled = grad_h * gain_ref[...]
        mean_grad = jnp.mean(scaled, axis=-1, keepdims=True)
        mean_proj = jnp.mean(scaled * unit, axis=-1, keepdims=True)
        gres_ref[at, :] = cot.astype(f32) + inverse * (scaled - mean_grad - unit * mean_proj)


def back_kernel(
    gres_ref, h_ref, qkv_ref, p_ref, ho_ref, w_ref,
    gw_ref, gh_ref, gb_ref, gj_ref, dho_ref, gbt_ref, ht_ref, *, images, seq, tall
):
    groups = w_ref.shape[0]
    scale = HEAD_DIM ** (-0.5)
    gb_ref[...] = gres_ref[...].astype(bf16)
    gbt_ref[...] = gres_ref[...].T.astype(bf16)
    ht_ref[...] = h_ref[...].T
    gh_ref[...] = jnp.zeros_like(gh_ref)
    low = low_lanes(tall)

    def group(j, carry):
        dho_ref[...] = mm(gb_ref[...], w_ref[j, :, 512:])

        def image(b, inner):
            at = pl.ds(pl.multiple_of(b * tall, 16), tall)
            joined = qkv_ref[j, at, :]
            q_pair, k_pair, v_pair = joined[:, :128], joined[:, 128:256], joined[:, 256:384]
            qk_last, v_last = joined[:, 384:512], joined[:, 512:640]
            heads = ho_ref[j, at, :].astype(f32)
            grad = dho_ref[at, :].astype(bf16).astype(f32)
            product = grad * heads
            pair = product[:, 128:]
            dots = (
                jnp.sum(jnp.where(low, pair, 0.0), axis=1, keepdims=True),
                jnp.sum(jnp.where(low, 0.0, pair), axis=1, keepdims=True),
                jnp.sum(product[:, :128], axis=1, keepdims=True),
            )
            grad_pair = grad[:, 128:]
            grad_last = jnp.where(low, pltpu.roll(grad[:, :128], HEAD_DIM, 1), 0.0).astype(bf16)
            gq, gk, gv = [], [], []
            for head, (g, v, q, k) in enumerate(
                (
                    (jnp.where(low, grad_pair, 0.0).astype(bf16), v_pair, q_pair, k_pair),
                    (jnp.where(low, 0.0, grad_pair).astype(bf16), v_pair, q_pair, k_pair),
                    (grad_last, v_last, qk_last, qk_last),
                )
            ):
                probs = p_ref[j, b, head]
                grad_p = mm_nt(g, v)
                grad_s = (probs.astype(f32) * (grad_p - dots[head])).astype(bf16)
                gq.append(mm(grad_s, k))
                gk.append(mm_tn(grad_s, q))
                gv.append(mm_tn(probs, g))
            last = pltpu.roll(jnp.where(low, gk[2], gq[2]), HEAD_DIM, 1)
            gj_ref[at, :] = jnp.concatenate(
                [
                    jnp.where(low, gq[0], gq[1]) * scale,
                    jnp.where(low, gk[0], gk[1]) * scale,
                    gv[0] + gv[1],
                    last * scale,
                    gv[2],
                ],
                1,
            ).astype(bf16)
            return inner

        lax.fori_loop(0, images, image, 0, unroll=True)
        grad_out = mm(gbt_ref[...], ho_ref[j])
        grad_in = mm(ht_ref[...], gj_ref[...])
        gw_ref[j, :, :512] = grad_in[:, :512].astype(bf16)
        gw_ref[j, :, 512:640] = (grad_in[:, 512:] + grad_out[:, :128]).astype(bf16)
        gw_ref[j, :, 640:] = grad_out[:, 128:].astype(bf16)
        gh_ref[...] += mm_nt(gj_ref[...], w_ref[j, :, :JOINED])
        return carry

    lax.fori_loop(0, groups, group, 0)


def last_kernel(x_ref, gres_ref, gh_ref, gain_ref, gt_ref, ggain_ref, *, images, seq, tall):
    total = jnp.zeros(ggain_ref.shape, f32)
    for b in range(images):
        at = pl.ds(b * tall, seq)
        unit, inverse = unit_of(x_ref[b].astype(f32))
        grad_h = gh_ref[at, :]
        total += jnp.sum(grad_h * unit, axis=0, keepdims=True)
        scaled = grad_h * gain_ref[...]
        mean_grad = jnp.mean(scaled, axis=-1, keepdims=True)
        mean_proj = jnp.mean(scaled * unit, axis=-1, keepdims=True)
        gt_ref[b] = gres_ref[at, :] + inverse * (scaled - mean_grad - unit * mean_proj)
    ggain_ref[...] = total


def call(kernel, outs, args, scratch=(), flops=0, name=None, **static):
    spec = pl.BlockSpec(memory_space=pltpu.VMEM)
    moved = sum(math.prod(a.shape) * a.dtype.itemsize for a in args)
    return pl.pallas_call(
        functools.partial(kernel, **static),
        out_shape=[jax.ShapeDtypeStruct(s, d) for s, d in outs],
        in_specs=[spec] * len(args),
        out_specs=[spec] * len(outs),
        scratch_shapes=list(scratch),
        compiler_params=pltpu.CompilerParams(vmem_limit_bytes=60 << 20),
        cost_estimate=pl.CostEstimate(flops=flops, bytes_accessed=moved, transcendentals=0),
        name=name,
    )(*args)


def assemble_kernel(me_ref, a_ref, a_other_ref, b_ref, b_other_ref, w_ref):
    me = me_ref[0]
    half_groups, dp, half = a_ref.shape[0], a_ref.shape[1], a_ref.shape[2]
    for d in range(dp):
        r = jnp.bitwise_xor(me, d)
        for g in range(half_groups):
            for core, (first, second) in enumerate(((a_ref, b_ref), (a_other_ref, b_other_ref))):
                for part, ref in enumerate((first, second)):
                    at = (2 * d + part) * half
                    w_ref[2 * g + core, at : at + half, :] = ref[g, r]


def spread_kernel(me_ref, gw_ref, out_ref):
    me = me_ref[0]
    groups, dp, rows = out_ref.shape[0], out_ref.shape[1], out_ref.shape[2]
    for d in range(dp):
        r = jnp.bitwise_xor(me, d)
        for j in range(groups):
            out_ref[j, r] = gw_ref[j, d * rows : (d + 1) * rows, :]


def make(mesh):
    dp, mp = mesh.shape["dp"], mesh.shape["mp"]

    def per_device(
        tokens, token_mask, gain_one, w_qkv, w_out, gain_two, router, w_in, w_back, cotangent
    ):
        rows, width = tokens.shape
        seq = token_mask.shape[1]
        tall = -(-seq // 16) * 16
        images = rows // seq
        experts = router.shape[1]
        d_rows, _, part = w_qkv.shape
        half = d_rows // 2
        count = images * tall
        static = {"images": images, "seq": seq, "tall": tall}
        me = lax.axis_index("dp")
        at_mp = lax.axis_index("mp")
        me_word = me.astype(jnp.int32).reshape(1)

        low_dim, mid = 2 * HEAD_DIM, part
        wo = w_out.T
        packed = jnp.concatenate(
            [w_qkv[:, c, :low_dim] for c in range(3)]
            + [w_qkv[:, c, low_dim:mid] for c in range(3)]
            + [wo[:, low_dim:mid], wo[:, :low_dim]],
            axis=1,
        )
        extra = jnp.concatenate([gain_one[None], gain_two[None], router.T], axis=0)
        held = extra
        for depth, bit in enumerate(bits_of(dp)):
            other = swap(held, "dp", dp, bit)
            held = jnp.stack([held, other], depth)
        extra = held.reshape((dp,) + extra.shape)
        for bit in bits_of(dp):
            pairs = extra.reshape((dp // (2 * bit), 2, bit) + extra.shape[1:])
            extra = jnp.where((me & bit) > 0, pairs[:, ::-1], pairs).reshape(extra.shape)
        extra = extra.transpose(1, 0, 2).reshape(experts + 2, width)
        gain_a, gain_b = extra[:1].astype(f32), extra[1:2].astype(f32)
        route_w = extra[2:]

        first, first_other = gather_pair(packed[:half], dp, mp, False)
        second, second_other = gather_pair(packed[half:], dp, mp, True)
        spec = pl.BlockSpec(memory_space=pltpu.VMEM)
        weights = pl.pallas_call(
            assemble_kernel,
            out_shape=jax.ShapeDtypeStruct((mp, width, 4 * part), bf16),
            in_specs=[pl.BlockSpec(memory_space=pltpu.SMEM)] + [spec] * 4,
            out_specs=spec,
            name="assemble",
        )(me_word, first, first_other, second, second_other)

        mask = lax.dynamic_slice_in_dim(token_mask, at_mp * images, images, 0)
        mask = jnp.pad(mask, ((0, 0), (0, tall - seq))).astype(f32)
        bias = jnp.where(mask > 0, 0.0, -1e30)[:, None, :]
        column = mask[:, :, None]
        mask_row = mask[:, None, :]
        valid = jnp.sum(mask, axis=1) * width
        x3 = tokens.reshape(images, seq, width)
        cot3 = cotangent.reshape(images, seq, width)

        h_one, joined, probs, heads_out, branch = call(
            front_kernel,
            [
                ((count, width), bf16),
                ((mp, count, JOINED), bf16),
                ((mp, images, part // HEAD_DIM, tall, tall), bf16),
                ((mp, count, 256), bf16),
                ((count, width), f32),
            ],
            (x3, bias, gain_a, weights),
            flops=4_000_000_000,
            name="front",
            **static,
        )
        resid, h_two, soft, sent, sq_branch = call(
            route_kernel,
            [
                ((count, width), f32),
                ((count, width), bf16),
                ((2, images, experts, tall), f32),
                ((2, images, experts, width), bf16),
                ((images, 1, 128), f32),
            ],
            (x3, branch, cot3, mask_row, column, gain_b, route_w),
            flops=100_000_000,
            name="route",
            **static,
        )
        got = sent.transpose(2, 0, 1, 3)
        got = lax.all_to_all(got, "dp", split_axis=0, concat_axis=0, tiled=True)
        got = gather_mp(got, mp).transpose(2, 0, 1, 3, 4).reshape(2, -1, width)
        slot_in, grad_expert = got[0], got[1]
        hidden, grad_pre, back = call(
            expert_kernel,
            [
                (slot_in.shape[:1] + w_in.shape[2:], bf16),
                (slot_in.shape[:1] + w_in.shape[2:], bf16),
                ((2,) + slot_in.shape, bf16),
            ],
            (slot_in, grad_expert, w_in[0], w_back[0]),
            flops=500_000_000,
            name="expert",
        )
        back = back.reshape(2, mp, dp, images, width).transpose(1, 2, 0, 3, 4)
        back = scatter(back, "mp", mp, [1, 2])
        back = lax.all_to_all(back, "dp", split_axis=0, concat_axis=0, tiled=True)
        back = back.transpose(1, 2, 0, 3)
        grad_w_back = mm_tn(hidden, grad_expert)
        grad_w_in = mm_tn(slot_in, grad_pre)

        out_rows, grad_resid, grad_router, grad_gain_two, sq_rest = call(
            mix_kernel,
            [
                ((images, seq, width), bf16),
                ((count, width), f32),
                ((experts, width), f32),
                ((1, width), f32),
                ((2, images, 1, 128), f32),
            ],
            (resid, h_two, soft, cot3, column, gain_b, route_w, back),
            flops=100_000_000,
            name="mix",
            **static,
        )
        grads, grad_h = call(
            back_kernel,
            [((mp, width, 4 * part), bf16), ((count, width), f32)],
            (grad_resid, h_one, joined, probs, heads_out, weights),
            [
                pltpu.VMEM((count, width), bf16),
                pltpu.VMEM((count, JOINED), bf16),
                pltpu.VMEM((count, 256), f32),
                pltpu.VMEM((width, count), bf16),
                pltpu.VMEM((width, count), bf16),
            ],
            flops=8_000_000_000,
            name="back",
            **static,
        )
        grad_tokens, grad_gain_one = call(
            last_kernel,
            [((images, seq, width), f32), ((1, width), f32)],
            (x3, grad_resid, grad_h, gain_a),
            flops=10_000_000,
            name="last",
            **static,
        )
        grads = pl.pallas_call(
            spread_kernel,
            out_shape=jax.ShapeDtypeStruct((mp, dp, d_rows, 4 * part), bf16),
            in_specs=[pl.BlockSpec(memory_space=pltpu.SMEM), spec],
            out_specs=spec,
            name="spread",
        )(me_word, grads)
        summed = scatter(grads, "mp", mp, [1, 2])
        summed = scatter(summed, "dp", dp, bits_of(dp)[-1:] + bits_of(dp)[:-1]).astype(f32)

        squares = jnp.concatenate([sq_rest[:1, :, 0, 0], sq_branch[None, :, 0, 0], sq_rest[1:, :, 0, 0]])
        squares = jnp.sqrt(squares / valid[None])
        own = lax.broadcasted_iota(jnp.int32, (1, mp, 1), 1) == at_mp
        squares = jnp.where(own, squares[:, None, :], 0.0).reshape(1, -1)
        squares = jnp.pad(squares, ((0, 0), (0, width - squares.shape[1])))
        small = jnp.concatenate([grad_gain_one, grad_gain_two, grad_router, squares], axis=0)
        for bit in bits_of(mp)[::-1]:
            small = small + swap(small, "mp", mp, bit)
        root_squares = small[-1, : 3 * mp * images].reshape(3, mp * images)
        for bit in bits_of(dp)[::-1]:
            small = small + swap(small, "dp", dp, bit)
        small = lax.dynamic_slice_in_dim(small, me * d_rows, d_rows, 1)
        grad_qkv = jnp.stack(
            [
                jnp.concatenate(
                    [
                        summed[:, c * low_dim : (c + 1) * low_dim],
                        summed[:, 3 * low_dim + c * HEAD_DIM : 3 * low_dim + (c + 1) * HEAD_DIM],
                    ],
                    axis=1,
                )
                for c in range(3)
            ],
            axis=1,
        )
        grad_out = jnp.concatenate([summed[:, 640:], summed[:, 576:640]], axis=1).T
        return (
            out_rows.reshape(rows, width),
            grad_tokens.reshape(rows, width),
            small[0],
            grad_qkv,
            grad_out,
            small[1],
            small[2:-1].T,
            grad_w_in[None],
            grad_w_back[None],
            root_squares,
        )

    return per_device


def solution(mesh):
    in_specs = (
        P(("dp", "mp"), None),
        P("dp", None),
        P("dp"),
        P("dp", None, "mp"),
        P("mp", "dp"),
        P("dp"),
        P("dp", None),
        P("dp", None, "mp"),
        P("dp", "mp", None),
        P(("dp", "mp"), None),
    )
    out_specs = (
        P(("dp", "mp"), None),
        P(("dp", "mp"), None),
        P("dp"),
        P("dp", None, "mp"),
        P("mp", "dp"),
        P("dp"),
        P("dp", None),
        P("dp", None, "mp"),
        P("dp", "mp", None),
        P(None, "dp"),
    )
    return jax.shard_map(
        make(mesh), mesh=mesh, in_specs=in_specs, out_specs=out_specs, check_vma=False
    )
```

time: 395 us -> 256 us (0.65)
  Pallas kernels: 0 us -> 77.4 us
  matrix products: 63.4 us -> 3.8 us
  local copies, waits for them, and re-layouts: 72.6 us -> 21.5 us
  blocking collectives: 66.9 us -> 21.4 us
  waiting for transfers between devices: 129 us -> 85.9 us
  other arithmetic: 37.7 us -> 11.3 us
  starting transfers between devices: 19.2 us -> 32.7 us
    pallas_call x0 -> x8, Pallas kernels: none -> 77.4 us  [the longest x6 67.7 us: call(): pl.pallas_call(functools.partial(kernel, **static), out_shape=[jax.ShapeD...]
    dot_general x27 -> x2, matrix products: 63.4 us -> 3.8 us  [mm_tn(): lax.dot_general(a, b, (((0,), (0,)), ((), ())), preferred_element_type=f32)]
    ppermute x17 -> x27, waiting for transfers between devices: 129 us -> 85.9 us  [swap(): lax.ppermute(array_in, axis_name, [(i, i ^ bit) for i in range(size)])]
    psum x1 -> x0, blocking collectives: 39.3 us -> none  [per_device(): small = lax.psum(small, ('dp', 'mp'))]
    reshape x4 -> x0, local copies, waits for them, and re-layouts: 18.3 us -> none  [the longest x1 11.4 us: per_device(): joined = joined.reshape(mp, images, seq_len, 3, heads, HEAD_DIM)]
    another operation x7 -> x5, local copies, waits for them, and re-layouts: 14.6 us -> 0.78 us  [the longest x1 0.66 us: per_device(): root_squares = small[-1, :3 * mp * images].reshape(3, mp * images)]
    ppermute x17 -> x27, starting transfers between devices: 19.2 us -> 32.7 us  [swap(): lax.ppermute(array_in, axis_name, [(i, i ^ bit) for i in range(size)])]
    convert_element_type x4 -> x2, local copies, waits for them, and re-layouts: 11.1 us -> 1.34 us  [per_device(): gain_a, gain_b = (extra[:1].astype(f32), extra[1:2].astype(f32))]
  transfers between devices with their start and end apart: 17 -> 27, of which waited for: 15 -> 21; matrix products, arithmetic and copies ran while one was open for 5% -> 9% of each run, Pallas kernels for 0% -> 2%
where the time goes in v2:
time: 256 us; the launch traced here: 255 us
  waiting for transfers between devices  85.9 us (34%)
  Pallas kernels  77.4 us (30%)
  starting transfers between devices  32.7 us (13%)
  local copies, waits for them, and re-layouts  21.5 us (8%)
  blocking collectives  21.4 us (8%)
  other arithmetic  11.3 us (4%)
  matrix products  3.8 us (1%)
    ppermute x27, waiting for transfers between devices, swap(): lax.ppermute(array_in, axis_name, [(i, i ^ bit) for i in range(size)])  85.9 us
    pallas_call x6, Pallas kernels, call(): pl.pallas_call(functools.partial(kernel, **static), out_shape=[jax.ShapeD...  67.7 us
    ppermute x27, starting transfers between devices, swap(): lax.ppermute(array_in, axis_name, [(i, i ^ bit) for i in range(size)])  32.7 us
    all_to_all x1, blocking collectives, per_device(): got = lax.all_to_all(got, 'dp', split_axis=0, concat_axis=0, tiled=True)  12.1 us
    all_to_all x1, blocking collectives, per_device(): back = lax.all_to_all(back, 'dp', split_axis=0, concat_axis=0, tiled=True)  9.34 us
  transfers between devices with their start and end apart: 27, of which 21 were waited for; matrix products, arithmetic and copies ran while one was open for 9% of the time, Pallas kernels for 2%

profile of v2, /device:TPU:0, one launch (start us, length us, event | category | flops | bytes accessed | tf_op | source)
XLA Modules:
  0.0 255.3 jit_solution(11211454882528691695)
XLA Ops:
  3.3 4.1 %collective-permute-start.3 = (bf16[48,768]{1,0:T(8,128)(2,1)S(1)}, bf16[48,768]{1,0:T(8,128)(2,1)S(1)}, u32[]{:S(2)}, u32[]{:S(2)}) collective-permute-start(bf16[48,768]{1,0:T(8,128)(2,1)S(1)} %get-tuple-element.153), channel_id=1, source_target_pairs={{0,16},{4,20},{8,24},{12,28},{16,0},{20,4},{24,8},{28,12},{1,17},{... | collective-permute-start | bytes 221192 | tf_op jit(solution)/shard_map/ppermute | solution.py:20
  7.5 4.9 %collective-permute-done.3 = bf16[48,768]{1,0:T(8,128)(2,1)S(1)} collective-permute-done((bf16[48,768]{1,0:T(8,128)(2,1)S(1)}, bf16[48,768]{1,0:T(8,128)(2,1)S(1)}, u32[]{:S(2)}, u32[]{:S(2)}) %collective-permute-start.3) | collective-permute-done | bytes 73760 | tf_op jit(solution)/shard_map/ppermute | solution.py:20
  15.2 3.1 %collective-permute-done.4 = bf16[2,48,768]{2,1,0:T(8,128)(2,1)S(1)} collective-permute-done((bf16[2,48,768]{2,1,0:T(8,128)(2,1)S(1)}, bf16[2,48,768]{2,1,0:T(8,128)(2,1)S(1)}, u32[]{:S(2)}, u32[]{:S(2)}) %collective-permute-start.4) | collective-permute-done | bytes 147488 | tf_op jit(solution)/shard_map/ppermute | solution.py:20
  18.4 2.2 collective-permute-start.5
  22.8 2.6 %collective-permute-done.5 = bf16[2,2,48,768]{3,2,1,0:T(8,128)(2,1)S(1)} collective-permute-done((bf16[2,2,48,768]{3,2,1,0:T(8,128)(2,1)S(1)}, bf16[2,2,48,768]{3,2,1,0:T(8,128)(2,1)S(1)}, u32[]{:S(2)}, u32[]{:S(2)}) %collective-permute-start.5) | collective-permute-done | bytes 294944 | tf_op jit(solution)/shard_map/ppermute | solution.py:20
  25.4 2.0 collective-permute-start.6
  27.4 3.4 %collective-permute-done.10 = bf16[2,2,48,768]{3,2,1,0:T(8,128)(2,1)S(1)} collective-permute-done((bf16[2,2,48,768]{3,2,1,0:T(8,128)(2,1)S(1)}, bf16[2,2,48,768]{3,2,1,0:T(8,128)(2,1)S(1)}, u32[]{:S(2)}, u32[]{:S(2)}) %collective-permute-start.10) | collective-permute-done | bytes 294944 | tf_op jit(solution)/shard_map/ppermute | solution.py:20
  30.9 1.9 collective-permute-start.11
  32.8 3.1 %collective-permute-start = (bf16[10,96]{1,0:T(8,128)(2,1)S(1)}, bf16[10,96]{1,0:T(8,128)(2,1)S(1)}, u32[]{:S(2)}, u32[]{:S(2)}) collective-permute-start(bf16[10,96]{1,0:T(8,128)(2,1)S(1)} %get-tuple-element.177), channel_id=1, source_target_pairs={{0,16},{4,20},{8,24},{12,28},{16,0},{20,4},{24,8},{28,12},{1,17},{... | collective-permute-start | bytes 5768 | tf_op jit(solution)/shard_map/ppermute | solution.py:20
  39.4 2.6 %collective-permute-done.6 = bf16[2,2,2,48,768]{4,3,2,1,0:T(8,128)(2,1)S(1)} collective-permute-done((bf16[2,2,2,48,768]{4,3,2,1,0:T(8,128)(2,1)S(1)}, bf16[2,2,2,48,768]{4,3,2,1,0:T(8,128)(2,1)S(1)}, u32[]{:S(2)}, u32[]{:S(2)}) %collective-permute-start.6) | collective-permute-done | bytes 589856 | tf_op jit(solution)/shard_map/ppermute | solution.py:20
  60.0 4.8 %assemble.1.w_ref = bf16[4,768,768]{2,1,0:T(8,128)(2,1)} custom-call(s32[1]{0:T(128)} %bitcast.16.me_ref, bf16[2,8,48,768]{3,2,1,0:T(8,128)(2,1)} %copy-done.3, bf16[2,8,48,768]{3,2,1,0:T(8,128)(2,1)} %collective-permute-done.7.a_other_ref, bf16[2,8,48,768]{3,2,1,0:T(8,128)(2,1)} %bitcast.214, bf16[2,8,48,768]{3,2,1,0:T(8,128)(2,1)} %copy-done.7), custom_call_target="tpu_custom_call" | custom-call | tf_op jit(solution)/shard_map/assemble/pallas_call | solution.py:385
  64.8 19.7 %front.1 = (bf16[624,768]{1,0:T(8,128)(2,1)}, bf16[4,624,640]{2,1,0:T(8,128)(2,1)}, bf16[4,3,3,208,208]{4,3,2,1,0:T(8,128)(2,1)}, bf16[4,624,256]{2,1,0:T(8,128)(2,1)}, f32[624,768]{1,0:T(8,128)}) custom-call(bf16[3,200,768]{2,1,0:T(8,128)(2,1)} %bitcast.219, f32[3,1,208]{2,1,0:T(1,128)} %copy.198.bias_ref, f32[1,768]{1,0:T(1,128)} %reshape.279.gain_ref, ...), custom_call_target="tpu_custom_call" | custom-call | flops 4000000000 | bytes 5645760 | tf_op jit(solution)/shard_map/front/pallas_call | solution.py:309
  84.5 4.2 %route.1 = (f32[624,768]{1,0:T(8,128)}, bf16[624,768]{1,0:T(8,128)(2,1)}, f32[2,3,8,208]{3,2,1,0:T(8,128)}, bf16[2,3,8,768]{3,2,1,0:T(8,128)(2,1)}, f32[3,1,128]{2,1,0:T(1,128)}) custom-call(bf16[3,200,768]{2,1,0:T(8,128)(2,1)} %bitcast.220, f32[624,768]{1,0:T(8,128)} %get-tuple-element.32.br_ref, bf16[3,200,768]{2,1,0:T(8,128)(2,1)} %bitcast.217, ...), custom_call_target="tpu_custom_call" | custom-call | flops 100000000 | bytes 3780480 | tf_op jit(solution)/shard_map/route/pallas_call | solution.py:309
  89.6 12.1 %all_to_all.10 = bf16[8,2,3,768]{3,1,2,0:T(2,128)(2,1)S(1)} all-to-all(bf16[8,2,3,768]{3,1,2,0:T(2,128)(2,1)S(1)} %copy.200), channel_id=1, replica_groups=mesh['dp'=8,'mp'=4] {'dp'}, dimensions={0} | all-to-all | bytes 147456 | tf_op jit(solution)/shard_map/all_to_all | solution.py:431
  103.3 2.9 %collective-permute-done.13 = bf16[1,8,2,3,768]{4,1,3,2,0:T(8,128)(2,1)S(1)} collective-permute-done((bf16[1,8,2,3,768]{4,1,3,2,0:T(8,128)(2,1)S(1)}, bf16[1,8,2,3,768]{4,1,3,2,0:T(8,128)(2,1)S(1)}, u32[]{:S(2)}, u32[]{:S(2)}) %collective-permute-start.13) | collective-permute-done | bytes 73760 | tf_op jit(solution)/shard_map/ppermute | solution.py:20
  109.4 3.8 %expert.1 = (bf16[96,768]{1,0:T(8,128)(2,1)}, bf16[96,768]{1,0:T(8,128)(2,1)}, bf16[2,96,768]{2,1,0:T(8,128)(2,1)}) custom-call(bf16[96,768]{1,0:T(8,128)(2,1)} %squeeze.72.slot_ref, bf16[96,768]{1,0:T(8,128)(2,1)} %squeeze.73.grad_ref, bf16[768,768]{1,0:T(8,128)(2,1)} %bitcast.228, bf16[768,768]{1,0:T(8,128)(2,1)} %bitcast.229), custom_call_target="tpu_custom_call" | custom-call | flops 500000000 | bytes 2654208 | tf_op jit(solution)/shard_map/expert/pallas_call | solution.py:309
  117.6 2.9 %collective-permute-done.16 = bf16[1,1,8,2,3,768]{5,2,4,3,1,0:T(8,128)(2,1)S(1)} collective-permute-done((bf16[1,1,8,2,3,768]{5,2,4,3,1,0:T(8,128)(2,1)S(1)}, bf16[1,1,8,2,3,768]{5,2,4,3,1,0:T(8,128)(2,1)S(1)}, u32[]{:S(2)}, u32[]{:S(2)}) %collective-permute-start.16) | collective-permute-done | bytes 73760 | tf_op jit(solution)/shard_map/ppermute | solution.py:20
  120.5 9.3 %all_to_all.11 = bf16[8,2,3,768]{3,1,2,0:T(2,128)(2,1)S(1)} all-to-all(bf16[8,2,3,768]{3,1,2,0:T(2,128)(2,1)S(1)} %copy.210), channel_id=1, replica_groups=mesh['dp'=8,'mp'=4] {'dp'}, dimensions={0} | all-to-all | bytes 147456 | tf_op jit(solution)/shard_map/all_to_all | solution.py:447
  130.5 6.6 %mix.1 = (bf16[3,200,768]{2,1,0:T(8,128)(2,1)}, f32[624,768]{1,0:T(8,128)}, f32[8,768]{1,0:T(8,128)}, f32[1,768]{1,0:T(1,128)}, f32[2,3,1,128]{3,2,1,0:T(1,128)}) custom-call(f32[624,768]{1,0:T(8,128)} %get-tuple-element.33.res_ref, bf16[624,768]{1,0:T(8,128)(2,1)} %get-tuple-element.34.h_ref, f32[2,3,8,208]{3,2,1,0:T(8,128)} %get-tuple-element.35.soft_ref, ...), custom_call_target="tpu_custom_call" | custom-call | flops 100000000 | bytes 3928512 | tf_op jit(solution)/shard_map/mix/pallas_call | solution.py:309
  137.1 28.6 %back.1 = (bf16[4,768,768]{2,1,0:T(8,128)(2,1)}, f32[624,768]{1,0:T(8,128)}) custom-call(f32[624,768]{1,0:T(8,128)} %get-tuple-element.39.gres_ref, bf16[624,768]{1,0:T(8,128)(2,1)} %get-tuple-element.40.h_ref, bf16[4,624,640]{2,1,0:T(8,128)(2,1)} %get-tuple-element.41.qkv_ref, bf16[4,3,3,208,208]{4,3,2,1,0:T(8,128)(2,1)} %get-tuple-element.42.p_ref, ...), custom_call_target="tpu_custom_call" | custom-call | flops 8000000000 | bytes 15181824 | tf_op jit(solution)/shard_map/back/pallas_call | solution.py:309
  165.7 4.8 %spread.1 = bf16[4,8,96,768]{3,2,1,0:T(8,128)(2,1)} custom-call(s32[1]{0:T(128)} %bitcast.16.me_ref, bf16[4,768,768]{2,1,0:T(8,128)(2,1)} %get-tuple-element.51.gw_ref), custom_call_target="tpu_custom_call" | custom-call | tf_op jit(solution)/shard_map/spread/pallas_call | solution.py:489
  170.6 2.0 slice_bitcast_fusion
  172.6 4.5 %collective-permute-done.22 = bf16[2,1,8,96,768]{4,3,2,0,1:T(8,128)(2,1)S(1)} collective-permute-done((bf16[2,1,8,96,768]{4,3,2,0,1:T(8,128)(2,1)S(1)}, bf16[2,1,8,96,768]{4,3,2,0,1:T(8,128)(2,1)S(1)}, u32[]{:S(2)}, u32[]{:S(2)}) %collective-permute-start.22) | collective-permute-done | bytes 2359328 | tf_op jit(solution)/shard_map/ppermute | solution.py:20
  180.0 4.9 %last.1 = (f32[3,200,768]{2,1,0:T(8,128)}, f32[1,768]{1,0:T(1,128)}) custom-call(bf16[3,200,768]{2,1,0:T(8,128)(2,1)} %bitcast.221, f32[624,768]{1,0:T(8,128)} %get-tuple-element.39.gres_ref, f32[624,768]{1,0:T(8,128)} %get-tuple-element.44.gh_ref, f32[1,768]{1,0:T(1,128)} %reshape.279.gain_ref), custom_call_target="tpu_custom_call" | custom-call | flops 10000000 | bytes 4758528 | tf_op jit(solution)/shard_map/last/pallas_call | solution.py:309
  185.7 20.5 %collective-permute-done.23 = bf16[1,1,8,96,768]{4,3,2,1,0:T(8,128)(2,1)} collective-permute-done((bf16[1,1,8,96,768]{4,3,2,1,0:T(8,128)(2,1)S(1)}, bf16[1,1,8,96,768]{4,3,2,1,0:T(8,128)(2,1)}, u32[]{:S(2)}, u32[]{:S(2)}) %collective-permute-start.23) | collective-permute-done | bytes 1179680 | tf_op jit(solution)/shard_map/ppermute | solution.py:20
  209.8 1.9 convolution_bitcast_fusion.1
  216.0 7.4 %collective-permute-done.19 = f32[11,768]{1,0:T(8,128)S(1)} collective-permute-done((f32[11,768]{1,0:T(8,128)S(1)}, f32[11,768]{1,0:T(8,128)S(1)}, u32[]{:S(2)}, u32[]{:S(2)}) %collective-permute-start.19) | collective-permute-done | bytes 33824 | tf_op jit(solution)/shard_map/ppermute | solution.py:20
  224.3 3.2 %collective-permute-done.20 = f32[11,768]{1,0:T(8,128)S(1)} collective-permute-done((f32[11,768]{1,0:T(8,128)S(1)}, f32[11,768]{1,0:T(8,128)S(1)}, u32[]{:S(2)}, u32[]{:S(2)}) %collective-permute-start.20) | collective-permute-done | bytes 33824 | tf_op jit(solution)/shard_map/ppermute | solution.py:20
  228.5 2.5 collective-permute-start.25
  231.0 8.2 %collective-permute-done.21 = f32[11,768]{1,0:T(8,128)S(1)} collective-permute-done((f32[11,768]{1,0:T(8,128)S(1)}, f32[11,768]{1,0:T(8,128)S(1)}, u32[]{:S(2)}, u32[]{:S(2)}) %collective-permute-start.21) | collective-permute-done | bytes 33824 | tf_op jit(solution)/shard_map/ppermute | solution.py:20
  240.1 6.9 %collective-permute-done.25 = bf16[1,2,96,768]{2,3,1,0:T(8,128)(2,1)S(1)} collective-permute-done((bf16[1,2,96,768]{2,3,1,0:T(8,128)(2,1)S(1)}, bf16[1,2,96,768]{2,3,1,0:T(8,128)(2,1)S(1)}, u32[]{:S(2)}, u32[]{:S(2)}) %collective-permute-start.25) | collective-permute-done | bytes 294944 | tf_op jit(solution)/shard_map/ppermute | solution.py:20
  247.8 5.8 %collective-permute-done.26 = bf16[1,1,96,768]{2,3,1,0:T(8,128)(2,1)S(1)} collective-permute-done((bf16[1,1,96,768]{2,3,1,0:T(8,128)(2,1)S(1)}, bf16[1,1,96,768]{2,3,1,0:T(8,128)(2,1)S(1)}, u32[]{:S(2)}, u32[]{:S(2)}) %collective-permute-start.26) | collective-permute-done | bytes 147488 | tf_op jit(solution)/shard_map/ppermute | solution.py:20
  (166 shorter events, 56.7 us)
Async XLA Ops:
  0.6 35.3 %copy-start = (s32[12,200]{1,0:T(8,128)S(1)}, s32[12,200]{1,0:T(8,128)}, u32[]{:S(2)}) copy-start(s32[12,200]{1,0:T(8,128)} %param.11) | copy-start | bytes 28804
  3.3 9.1 %collective-permute-start.3 = (bf16[48,768]{1,0:T(8,128)(2,1)S(1)}, bf16[48,768]{1,0:T(8,128)(2,1)S(1)}, u32[]{:S(2)}, u32[]{:S(2)}) collective-permute-start(bf16[48,768]{1,0:T(8,128)(2,1)S(1)} %get-tuple-element.153), channel_id=1, source_target_pairs={{0,16},{4,20},{8,24},{12,28},{16,0},{20,4},{24,8},{28,12},{1,17},{... | collective-permute-start | bytes 221192 | tf_op jit(solution)/shard_map/ppermute | solution.py:20
  7.4 7.1 %collective-permute-start.8 = (bf16[48,768]{1,0:T(8,128)(2,1)S(1)}, bf16[48,768]{1,0:T(8,128)(2,1)S(1)}, u32[]{:S(2)}, u32[]{:S(2)}) collective-permute-start(bf16[48,768]{1,0:T(8,128)(2,1)S(1)} %get-tuple-element.152), channel_id=1, source_target_pairs={{0,16},{4,20},{8,24},{12,28},{16,0},{20,4},{24,8},{28,12},{1,17},{... | collective-permute-start | bytes 221192 | tf_op jit(solution)/shard_map/ppermute | solution.py:20
  12.4 5.9 %collective-permute-start.4 = (bf16[2,48,768]{2,1,0:T(8,128)(2,1)S(1)}, bf16[2,48,768]{2,1,0:T(8,128)(2,1)S(1)}, u32[]{:S(2)}, u32[]{:S(2)}) collective-permute-start(bf16[2,48,768]{2,1,0:T(8,128)(2,1)S(1)} %get-tuple-element.155), channel_id=1, source_target_pairs={{0,8},{4,12},{8,0},{12,4},{16,24},{20,28},{24,16},{28,20},{1,9},{5... | collective-permute-start | bytes 442376 | tf_op jit(solution)/shard_map/ppermute | solution.py:20
  14.5 6.3 %collective-permute-start.9 = (bf16[2,48,768]{2,1,0:T(8,128)(2,1)S(1)}, bf16[2,48,768]{2,1,0:T(8,128)(2,1)S(1)}, u32[]{:S(2)}, u32[]{:S(2)}) collective-permute-start(bf16[2,48,768]{2,1,0:T(8,128)(2,1)S(1)} %get-tuple-element.149), channel_id=1, source_target_pairs={{0,8},{4,12},{8,0},{12,4},{16,24},{20,28},{24,16},{28,20},{1,9},{5... | collective-permute-start | bytes 442376 | tf_op jit(solution)/shard_map/ppermute | solution.py:20
  18.4 7.0 %collective-permute-start.5 = (bf16[2,2,48,768]{3,2,1,0:T(8,128)(2,1)S(1)}, bf16[2,2,48,768]{3,2,1,0:T(8,128)(2,1)S(1)}, u32[]{:S(2)}, u32[]{:S(2)}) collective-permute-start(bf16[2,2,48,768]{3,2,1,0:T(8,128)(2,1)S(1)} %get-tuple-element.145), channel_id=1, source_target_pairs={{0,4},{4,0},{8,12},{12,8},{16,20},{20,16},{24,28},{28,24},{1,5},{5... | collective-permute-start | bytes 884744 | tf_op jit(solution)/shard_map/ppermute | solution.py:20
  20.9 9.9 %collective-permute-start.10 = (bf16[2,2,48,768]{3,2,1,0:T(8,128)(2,1)S(1)}, bf16[2,2,48,768]{3,2,1,0:T(8,128)(2,1)S(1)}, u32[]{:S(2)}, u32[]{:S(2)}) collective-permute-start(bf16[2,2,48,768]{3,2,1,0:T(8,128)(2,1)S(1)} %get-tuple-element.143), channel_id=1, source_target_pairs={{0,2},{1,3},{2,0},{3,1},{4,6},{5,7},{6,4},{7,5},{8,10},{9,11},{10,... | collective-permute-start | bytes 884744 | tf_op jit(solution)/shard_map/ppermute | solution.py:20
  25.4 16.6 %collective-permute-start.6 = (bf16[2,2,2,48,768]{4,3,2,1,0:T(8,128)(2,1)S(1)}, bf16[2,2,2,48,768]{4,3,2,1,0:T(8,128)(2,1)S(1)}, u32[]{:S(2)}, u32[]{:S(2)}) collective-permute-start(bf16[2,2,2,48,768]{4,3,2,1,0:T(8,128)(2,1)S(1)} %pad_maximum_fusion.2), channel_id=1, source_target_pairs={{0,2},{1,3},{2,0},{3,1},{4,6},{5,7},{6,4},{7,5},{8,10},{9,11},{10,... | collective-permute-start | bytes 1769480 | tf_op jit(solution)/shard_map/ppermute | solution.py:20
  30.9 12.5 %collective-permute-start.11 = (bf16[2,2,2,48,768]{4,3,2,1,0:T(8,128)(2,1)S(1)}, bf16[2,2,2,48,768]{4,3,2,1,0:T(8,128)(2,1)}, u32[]{:S(2)}, u32[]{:S(2)}) collective-permute-start(bf16[2,2,2,48,768]{4,3,2,1,0:T(8,128)(2,1)S(1)} %get-tuple-element.129), channel_id=1, source_target_pairs={{0,4},{4,0},{8,12},{12,8},{16,20},{20,16},{24,28},{28,24},{1,5},{5... | collective-permute-start | bytes 1769480 | tf_op jit(solution)/shard_map/ppermute | solution.py:20
  32.8 4.7 %collective-permute-start = (bf16[10,96]{1,0:T(8,128)(2,1)S(1)}, bf16[10,96]{1,0:T(8,128)(2,1)S(1)}, u32[]{:S(2)}, u32[]{:S(2)}) collective-permute-start(bf16[10,96]{1,0:T(8,128)(2,1)S(1)} %get-tuple-element.177), channel_id=1, source_target_pairs={{0,16},{4,20},{8,24},{12,28},{16,0},{20,4},{24,8},{28,12},{1,17},{... | collective-permute-start | bytes 5768 | tf_op jit(solution)/shard_map/ppermute | solution.py:20
  37.6 7.2 %collective-permute-start.1 = (bf16[2,10,96]{2,1,0:T(8,128)(2,1)S(1)}, bf16[2,10,96]{2,1,0:T(8,128)(2,1)S(1)}, u32[]{:S(2)}, u32[]{:S(2)}) collective-permute-start(bf16[2,10,96]{2,1,0:T(8,128)(2,1)S(1)} %get-tuple-element.171), channel_id=1, source_target_pairs={{0,8},{4,12},{8,0},{12,4},{16,24},{20,28},{24,16},{28,20},{1,9},{5... | collective-permute-start | bytes 11528 | tf_op jit(solution)/shard_map/ppermute | solution.py:20
  42.1 16.9 %copy-start.3 = (bf16[2,8,48,768]{3,2,1,0:T(8,128)(2,1)}, bf16[2,8,48,768]{3,2,1,0:T(8,128)(2,1)S(1)}, u32[]{:S(2)}) copy-start(bf16[2,8,48,768]{3,2,1,0:T(8,128)(2,1)S(1)} %pad_maximum_fusion.a_ref) | copy-start | bytes 3538948
  42.1 16.9 %collective-permute-start.7 = (bf16[2,8,48,768]{3,2,1,0:T(8,128)(2,1)S(1)}, bf16[2,8,48,768]{3,2,1,0:T(8,128)(2,1)}, u32[]{:S(2)}, u32[]{:S(2)}) collective-permute-start(bf16[2,8,48,768]{3,2,1,0:T(8,128)(2,1)S(1)} %pad_maximum_fusion.a_ref), channel_id=1, source_target_pairs={{0,1},{1,0},{2,3},{3,2},{4,5},{5,4},{6,7},{7,6},{8,9},{9,8},{10,11... | collective-permute-start | bytes 3538952 | tf_op jit(solution)/shard_map/ppermute | solution.py:20
  44.6 14.4 %collective-permute-start.12 = (bf16[2,8,48,768]{3,2,1,0:T(8,128)(2,1)S(1)}, bf16[2,8,48,768]{3,2,1,0:T(8,128)(2,1)S(1)}, u32[]{:S(2)}, u32[]{:S(2)}) collective-permute-start(bf16[2,8,48,768]{3,2,1,0:T(8,128)(2,1)S(1)} %bitcast.213), channel_id=1, source_target_pairs={{0,1},{1,0},{2,3},{3,2},{4,5},{5,4},{6,7},{7,6},{8,9},{9,8},{10,11... | collective-permute-start | bytes 3538952 | tf_op jit(solution)/shard_map/ppermute | solution.py:20
  45.5 6.6 %collective-permute-start.2 = (bf16[2,2,10,96]{3,2,0,1:T(8,128)(2,1)}, bf16[2,2,10,96]{3,2,0,1:T(8,128)(2,1)}, u32[]{:S(2)}, u32[]{:S(2)}) collective-permute-start(bf16[2,2,10,96]{3,2,0,1:T(8,128)(2,1)} %get-tuple-element.167), channel_id=1, source_target_pairs={{0,4},{4,0},{8,12},{12,8},{16,20},{20,16},{24,28},{28,24},{1,5},{5... | collective-permute-start | bytes 23048 | tf_op jit(solution)/shard_map/ppermute | solution.py:20
  101.8 4.4 %collective-permute-start.13 = (bf16[1,8,2,3,768]{4,1,3,2,0:T(8,128)(2,1)S(1)}, bf16[1,8,2,3,768]{4,1,3,2,0:T(8,128)(2,1)S(1)}, u32[]{:S(2)}, u32[]{:S(2)}) collective-permute-start(bf16[1,8,2,3,768]{4,1,3,2,0:T(8,128)(2,1)S(1)} %bitcast.233), channel_id=1, source_target_pairs={{0,2},{1,3},{2,0},{3,1},{4,6},{5,7},{6,4},{7,5},{8,10},{9,11},{10,... | collective-permute-start | bytes 221192 | tf_op jit(solution)/shard_map/ppermute | solution.py:20
  106.2 1.4 collective-permute-start.14
  114.5 1.4 collective-permute-start.15
  116.0 4.4 %collective-permute-start.16 = (bf16[1,1,8,2,3,768]{5,2,4,3,1,0:T(8,128)(2,1)S(1)}, bf16[1,1,8,2,3,768]{5,2,4,3,1,0:T(8,128)(2,1)S(1)}, u32[]{:S(2)}, u32[]{:S(2)}) collective-permute-start(bf16[1,1,8,2,3,768]{5,2,4,3,1,0:T(8,128)(2,1)S(1)} %slice_bitcast_fusion.10), channel_id=1, source_target_pairs={{0,2},{1,3},{2,0},{3,1},{4,6},{5,7},{6,4},{7,5},{8,10},{9,11},{10,... | collective-permute-start | bytes 221192 | tf_op jit(solution)/shard_map/ppermute | solution.py:20
  172.5 4.6 %collective-permute-start.22 = (bf16[2,1,8,96,768]{4,3,2,0,1:T(8,128)(2,1)S(1)}, bf16[2,1,8,96,768]{4,3,2,0,1:T(8,128)(2,1)S(1)}, u32[]{:S(2)}, u32[]{:S(2)}) collective-permute-start(bf16[2,1,8,96,768]{4,3,2,0,1:T(8,128)(2,1)S(1)} %slice_bitcast_fusion), channel_id=1, source_target_pairs={{0,1},{1,0},{2,3},{3,2},{4,5},{5,4},{6,7},{7,6},{8,9},{9,8},{10,11... | collective-permute-start | bytes 7077896 | tf_op jit(solution)/shard_map/ppermute | solution.py:20
  178.0 28.2 %collective-permute-start.23 = (bf16[1,1,8,96,768]{4,3,2,1,0:T(8,128)(2,1)S(1)}, bf16[1,1,8,96,768]{4,3,2,1,0:T(8,128)(2,1)}, u32[]{:S(2)}, u32[]{:S(2)}) collective-permute-start(bf16[1,1,8,96,768]{4,3,2,1,0:T(8,128)(2,1)S(1)} %slice_bitcast_fusion.2), channel_id=1, source_target_pairs={{0,2},{1,3},{2,0},{3,1},{4,6},{5,7},{6,4},{7,5},{8,10},{9,11},{10,... | collective-permute-start | bytes 3538952 | tf_op jit(solution)/shard_map/ppermute | solution.py:20
  185.5 22.6 %copy-start.14 = (f32[1,768]{1,0:T(1,128)S(1)}, f32[1,768]{1,0:T(1,128)}, u32[]{:S(2)}) copy-start(f32[1,768]{1,0:T(1,128)} %get-tuple-element.46) | copy-start | bytes 9220
  185.6 24.2 %copy-start.6 = (bf16[96,768]{1,0:T(8,128)(2,1)S(1)}, bf16[96,768]{1,0:T(8,128)(2,1)}, u32[]{:S(2)}) copy-start(bf16[96,768]{1,0:T(8,128)(2,1)} %squeeze.72.slot_ref) | copy-start | bytes 442372
  185.6 24.2 %copy-start.9 = (bf16[96,768]{1,0:T(8,128)(2,1)S(1)}, bf16[96,768]{1,0:T(8,128)(2,1)}, u32[]{:S(2)}) copy-start(bf16[96,768]{1,0:T(8,128)(2,1)} %get-tuple-element.52) | copy-start | bytes 442372
  185.6 22.6 %collective-permute-start.17 = (f32[11,768]{1,0:T(8,128)S(1)}, f32[11,768]{1,0:T(8,128)S(1)}, u32[]{:S(2)}, u32[]{:S(2)}) collective-permute-start(f32[11,768]{1,0:T(8,128)S(1)} %select_maximum_fusion), channel_id=1, source_target_pairs={{0,1},{1,0},{2,3},{3,2},{4,5},{5,4},{6,7},{7,6},{8,9},{9,8},{10,11... | collective-permute-start | bytes 101384 | tf_op jit(solution)/shard_map/ppermute | solution.py:20
  207.8 20.3 %collective-permute-start.24 = (bf16[4,1,96,768]{3,2,1,0:T(8,128)(2,1)S(1)}, bf16[4,1,96,768]{3,2,1,0:T(8,128)(2,1)S(1)}, u32[]{:S(2)}, u32[]{:S(2)}) collective-permute-start(bf16[4,1,96,768]{3,2,1,0:T(8,128)(2,1)S(1)} %slice_bitcast_fusion.4), channel_id=1, source_target_pairs={{0,4},{4,0},{8,12},{12,8},{16,20},{20,16},{24,28},{28,24},{1,5},{5... | collective-permute-start | bytes 1769480 | tf_op jit(solution)/shard_map/ppermute | solution.py:20
  208.2 4.2 %collective-permute-start.18 = (f32[11,768]{1,0:T(8,128)S(1)}, f32[11,768]{1,0:T(8,128)S(1)}, u32[]{:S(2)}, u32[]{:S(2)}) collective-permute-start(f32[11,768]{1,0:T(8,128)S(1)} %fusion.22), channel_id=1, source_target_pairs={{0,2},{1,3},{2,0},{3,1},{4,6},{5,7},{6,4},{7,5},{8,10},{9,11},{10,... | collective-permute-start | bytes 101384 | tf_op jit(solution)/shard_map/ppermute | solution.py:20
  212.4 11.0 %collective-permute-start.19 = (f32[11,768]{1,0:T(8,128)S(1)}, f32[11,768]{1,0:T(8,128)S(1)}, u32[]{:S(2)}, u32[]{:S(2)}) collective-permute-start(f32[11,768]{1,0:T(8,128)S(1)} %add.50), channel_id=1, source_target_pairs={{0,4},{4,0},{8,12},{12,8},{16,20},{20,16},{24,28},{28,24},{1,5},{5... | collective-permute-start | bytes 101384 | tf_op jit(solution)/shard_map/ppermute | solution.py:20
  223.4 4.2 %collective-permute-start.20 = (f32[11,768]{1,0:T(8,128)S(1)}, f32[11,768]{1,0:T(8,128)S(1)}, u32[]{:S(2)}, u32[]{:S(2)}) collective-permute-start(f32[11,768]{1,0:T(8,128)S(1)} %add.51), channel_id=1, source_target_pairs={{0,8},{4,12},{8,0},{12,4},{16,24},{20,28},{24,16},{28,20},{1,9},{5... | collective-permute-start | bytes 101384 | tf_op jit(solution)/shard_map/ppermute | solution.py:20
  227.6 11.7 %collective-permute-start.21 = (f32[11,768]{1,0:T(8,128)S(1)}, f32[11,768]{1,0:T(8,128)S(1)}, u32[]{:S(2)}, u32[]{:S(2)}) collective-permute-start(f32[11,768]{1,0:T(8,128)S(1)} %add.52), channel_id=1, source_target_pairs={{0,16},{4,20},{8,24},{12,28},{16,0},{20,4},{24,8},{28,12},{1,17},{... | collective-permute-start | bytes 101384 | tf_op jit(solution)/shard_map/ppermute | solution.py:20
  228.5 18.6 %collective-permute-start.25 = (bf16[1,2,96,768]{2,3,1,0:T(8,128)(2,1)S(1)}, bf16[1,2,96,768]{2,3,1,0:T(8,128)(2,1)S(1)}, u32[]{:S(2)}, u32[]{:S(2)}) collective-permute-start(bf16[1,2,96,768]{2,3,1,0:T(8,128)(2,1)S(1)} %bitcast.231), channel_id=1, source_target_pairs={{0,16},{4,20},{8,24},{12,28},{16,0},{20,4},{24,8},{28,12},{1,17},{... | collective-permute-start | bytes 884744 | tf_op jit(solution)/shard_map/ppermute | solution.py:20
  247.2 6.4 %collective-permute-start.26 = (bf16[1,1,96,768]{2,3,1,0:T(8,128)(2,1)S(1)}, bf16[1,1,96,768]{2,3,1,0:T(8,128)(2,1)S(1)}, u32[]{:S(2)}, u32[]{:S(2)}) collective-permute-start(bf16[1,1,96,768]{2,3,1,0:T(8,128)(2,1)S(1)} %slice_bitcast_fusion.6), channel_id=1, source_target_pairs={{0,8},{4,12},{8,0},{12,4},{16,24},{20,28},{24,16},{28,20},{1,9},{5... | collective-permute-start | bytes 442376 | tf_op jit(solution)/shard_map/ppermute | solution.py:20
  (16 other events, 105.2 us)

commit v3 on v2

--- a/solution.py
+++ b/solution.py
@@ -303,6 +303,10 @@
     ggain_ref[...] = total
 
 
+def static_limit(name):
+    return {'front':26<<20,'route':14<<20,'expert':10<<20,'mix':16<<20,'back':34<<20,'last':14<<20}[name]
+
+
 def call(kernel, outs, args, scratch=(), flops=0, name=None, **static):
     spec = pl.BlockSpec(memory_space=pltpu.VMEM)
     moved = sum(math.prod(a.shape) * a.dtype.itemsize for a in args)
@@ -312,7 +316,7 @@
         in_specs=[spec] * len(args),
         out_specs=[spec] * len(outs),
         scratch_shapes=list(scratch),
-        compiler_params=pltpu.CompilerParams(vmem_limit_bytes=60 << 20),
+        compiler_params=pltpu.CompilerParams(vmem_limit_bytes=static_limit(name)),
         cost_estimate=pl.CostEstimate(flops=flops, bytes_accessed=moved, transcendentals=0),
         name=name,
     )(*args)

time: 256 us -> 250 us (0.977)
  Pallas kernels: 77.4 us -> 56.6 us
  local copies, waits for them, and re-layouts: 21.5 us -> 37.6 us
  other arithmetic: 11.3 us -> 7.79 us
    unnamed x46 -> x72, local copies, waits for them, and re-layouts: 3.9 us -> 25.8 us
    pallas_call x6, Pallas kernels: 67.7 us -> 46.9 us  [call(): pl.pallas_call(functools.partial(kernel, **static), out_shape=[jax.ShapeD...]
  transfers between devices with their start and end apart: 27 -> 27, of which waited for: 21 -> 21; matrix products, arithmetic and copies ran while one was open for 9% -> 5% of each run, Pallas kernels for 2% -> 1%
where the time goes in v3:
time: 250 us; the launch traced here: 249 us
  waiting for transfers between devices  86.7 us (35%)
  Pallas kernels  56.6 us (23%)
  local copies, waits for them, and re-layouts  37.6 us (15%)
  starting transfers between devices  33.1 us (13%)
  blocking collectives  22.5 us (9%)
  other arithmetic  7.79 us (3%)
  matrix products  3.8 us (2%)
    ppermute x27, waiting for transfers between devices, swap(): lax.ppermute(array_in, axis_name, [(i, i ^ bit) for i in range(size)])  86.7 us
    pallas_call x6, Pallas kernels, call(): pl.pallas_call(functools.partial(kernel, **static), out_shape=[jax.ShapeD...  46.9 us
    ppermute x27, starting transfers between devices, swap(): lax.ppermute(array_in, axis_name, [(i, i ^ bit) for i in range(size)])  33.1 us
    unnamed x72, local copies, waits for them, and re-layouts  25.8 us
    all_to_all x1, blocking collectives, per_device(): got = lax.all_to_all(got, 'dp', split_axis=0, concat_axis=0, tiled=True)  13.1 us
    all_to_all x1, blocking collectives, per_device(): back = lax.all_to_all(back, 'dp', split_axis=0, concat_axis=0, tiled=True)  9.34 us
  transfers between devices with their start and end apart: 27, of which 21 were waited for; matrix products, arithmetic and copies ran while one was open for 5% of the time, Pallas kernels for 1%

profile of v3, /device:TPU:0, one launch (start us, length us, event | category | flops | bytes accessed | tf_op | source)
XLA Modules:
  0.0 249.4 jit_solution(3318631230886852250)
XLA Ops:
  3.3 4.1 %collective-permute-start.3 = (bf16[48,768]{1,0:T(8,128)(2,1)S(1)}, bf16[48,768]{1,0:T(8,128)(2,1)S(1)}, u32[]{:S(2)}, u32[]{:S(2)}) collective-permute-start(bf16[48,768]{1,0:T(8,128)(2,1)S(1)} %get-tuple-element.153), channel_id=1, source_target_pairs={{0,16},{4,20},{8,24},{12,28},{16,0},{20,4},{24,8},{28,12},{1,17},{... | collective-permute-start | bytes 221192 | tf_op jit(solution)/shard_map/ppermute | solution.py:20
  7.5 4.9 %collective-permute-done.3 = bf16[48,768]{1,0:T(8,128)(2,1)S(1)} collective-permute-done((bf16[48,768]{1,0:T(8,128)(2,1)S(1)}, bf16[48,768]{1,0:T(8,128)(2,1)S(1)}, u32[]{:S(2)}, u32[]{:S(2)}) %collective-permute-start.3) | collective-permute-done | bytes 73760 | tf_op jit(solution)/shard_map/ppermute | solution.py:20
  15.2 3.1 %collective-permute-done.4 = bf16[2,48,768]{2,1,0:T(8,128)(2,1)S(1)} collective-permute-done((bf16[2,48,768]{2,1,0:T(8,128)(2,1)S(1)}, bf16[2,48,768]{2,1,0:T(8,128)(2,1)S(1)}, u32[]{:S(2)}, u32[]{:S(2)}) %collective-permute-start.4) | collective-permute-done | bytes 147488 | tf_op jit(solution)/shard_map/ppermute | solution.py:20
  18.4 2.2 collective-permute-start.5
  22.8 2.6 %collective-permute-done.5 = bf16[2,2,48,768]{3,2,1,0:T(8,128)(2,1)S(1)} collective-permute-done((bf16[2,2,48,768]{3,2,1,0:T(8,128)(2,1)S(1)}, bf16[2,2,48,768]{3,2,1,0:T(8,128)(2,1)S(1)}, u32[]{:S(2)}, u32[]{:S(2)}) %collective-permute-start.5) | collective-permute-done | bytes 294944 | tf_op jit(solution)/shard_map/ppermute | solution.py:20
  25.4 2.0 collective-permute-start.6
  27.4 3.4 %collective-permute-done.10 = bf16[2,2,48,768]{3,2,1,0:T(8,128)(2,1)S(1)} collective-permute-done((bf16[2,2,48,768]{3,2,1,0:T(8,128)(2,1)S(1)}, bf16[2,2,48,768]{3,2,1,0:T(8,128)(2,1)S(1)}, u32[]{:S(2)}, u32[]{:S(2)}) %collective-permute-start.10) | collective-permute-done | bytes 294944 | tf_op jit(solution)/shard_map/ppermute | solution.py:20
  32.8 3.1 %collective-permute-start = (bf16[10,96]{1,0:T(8,128)(2,1)S(1)}, bf16[10,96]{1,0:T(8,128)(2,1)S(1)}, u32[]{:S(2)}, u32[]{:S(2)}) collective-permute-start(bf16[10,96]{1,0:T(8,128)(2,1)S(1)} %get-tuple-element.177), channel_id=1, source_target_pairs={{0,16},{4,20},{8,24},{12,28},{16,0},{20,4},{24,8},{28,12},{1,17},{... | collective-permute-start | bytes 5768 | tf_op jit(solution)/shard_map/ppermute | solution.py:20
  39.4 2.6 %collective-permute-done.6 = bf16[2,2,2,48,768]{4,3,2,1,0:T(8,128)(2,1)S(1)} collective-permute-done((bf16[2,2,2,48,768]{4,3,2,1,0:T(8,128)(2,1)S(1)}, bf16[2,2,2,48,768]{4,3,2,1,0:T(8,128)(2,1)S(1)}, u32[]{:S(2)}, u32[]{:S(2)}) %collective-permute-start.6) | collective-permute-done | bytes 589856 | tf_op jit(solution)/shard_map/ppermute | solution.py:20
  44.1 2.5 %pad_maximum_fusion.1 = bf16[2,2,2,2,48,768]{5,4,3,2,1,0:T(8,128)(2,1)} fusion(bf16[2,2,2,1,48,768]{5,4,3,2,1,0:T(8,128)(2,1)} %bitcast.47, bf16[2,2,2,1,48,768]{5,4,3,2,1,0:T(8,128)(2,1)S(1)} %get-tuple-element.128), kind=kLoop, calls=%fused_computation.12 | loop fusion | flops 589824 | bytes 2359296 | tf_op jit(solution)/shard_map/stack | solution.py:36
  51.2 4.9 %assemble.1.w_ref = bf16[4,768,768]{2,1,0:T(8,128)(2,1)} custom-call(s32[1]{0:T(128)} %bitcast.16.me_ref, bf16[2,8,48,768]{3,2,1,0:T(8,128)(2,1)} %copy-done.29, bf16[2,8,48,768]{3,2,1,0:T(8,128)(2,1)} %collective-permute-done.7.a_other_ref, bf16[2,8,48,768]{3,2,1,0:T(8,128)(2,1)} %bitcast.48.b_ref, bf16[2,8,48,768]{3,2,1,0:T(8,128)(2,1)} %collective-permute-done.12.b_other_ref), custom_call_target="tpu_custom_call" | custom-call | tf_op jit(solution)/shard_map/assemble/pallas_call | solution.py:389
  56.1 2.3 copy-done.2
  58.4 14.4 %front.1 = (bf16[624,768]{1,0:T(8,128)(2,1)S(1)}, bf16[4,624,640]{2,1,0:T(8,128)(2,1)S(1)}, bf16[4,3,3,208,208]{4,3,2,1,0:T(8,128)(2,1)S(1)}, bf16[4,624,256]{2,1,0:T(8,128)(2,1)S(1)}, f32[624,768]{1,0:T(8,128)S(1)}) custom-call(bf16[3,200,768]{2,1,0:T(8,128)(2,1)S(1)} %bitcast.213, f32[3,1,208]{2,1,0:T(1,128)S(1)} %copy.198.bias_ref, ...), custom_call_target="tpu_custom_call" | custom-call | flops 4000000000 | bytes 5645760 | tf_op jit(solution)/shard_map/front/pallas_call | solution.py:313
  79.8 13.1 %all_to_all.10 = bf16[8,2,3,768]{3,1,2,0:T(2,128)(2,1)S(1)} all-to-all(bf16[8,2,3,768]{3,1,2,0:T(2,128)(2,1)S(1)} %copy.200), channel_id=1, replica_groups=mesh['dp'=8,'mp'=4] {'dp'}, dimensions={0} | all-to-all | bytes 147456 | tf_op jit(solution)/shard_map/all_to_all | solution.py:435
  94.5 2.9 %collective-permute-done.13 = bf16[1,8,2,3,768]{4,1,3,2,0:T(8,128)(2,1)S(1)} collective-permute-done((bf16[1,8,2,3,768]{4,1,3,2,0:T(8,128)(2,1)S(1)}, bf16[1,8,2,3,768]{4,1,3,2,0:T(8,128)(2,1)S(1)}, u32[]{:S(2)}, u32[]{:S(2)}) %collective-permute-start.13) | collective-permute-done | bytes 73760 | tf_op jit(solution)/shard_map/ppermute | solution.py:20
  111.0 2.9 %collective-permute-done.16 = bf16[1,1,8,2,3,768]{5,2,4,3,1,0:T(8,128)(2,1)S(1)} collective-permute-done((bf16[1,1,8,2,3,768]{5,2,4,3,1,0:T(8,128)(2,1)S(1)}, bf16[1,1,8,2,3,768]{5,2,4,3,1,0:T(8,128)(2,1)S(1)}, u32[]{:S(2)}, u32[]{:S(2)}) %collective-permute-start.16) | collective-permute-done | bytes 73760 | tf_op jit(solution)/shard_map/ppermute | solution.py:20
  114.0 9.3 %all_to_all.11 = bf16[8,2,3,768]{3,1,2,0:T(2,128)(2,1)S(1)} all-to-all(bf16[8,2,3,768]{3,1,2,0:T(2,128)(2,1)S(1)} %copy.210), channel_id=1, replica_groups=mesh['dp'=8,'mp'=4] {'dp'}, dimensions={0} | all-to-all | bytes 147456 | tf_op jit(solution)/shard_map/all_to_all | solution.py:451
  123.4 4.0 %mix.1 = (bf16[3,200,768]{2,1,0:T(8,128)(2,1)}, f32[624,768]{1,0:T(8,128)S(1)}, f32[8,768]{1,0:T(8,128)S(1)}, f32[1,768]{1,0:T(1,128)S(1)}, f32[2,3,1,128]{3,2,1,0:T(1,128)S(1)}) custom-call(f32[624,768]{1,0:T(8,128)S(1)} %copy-done.7, bf16[624,768]{1,0:T(8,128)(2,1)S(1)} %get-tuple-element.34.h_ref, f32[2,3,8,208]{3,2,1,0:T(8,128)S(1)} %get-tuple-element.35.soft_ref, ...), custom_call_target="tpu_custom_call" | custom-call | flops 100000000 | bytes 3928512 | tf_op jit(solution)/shard_map/mix/pallas_call | solution.py:313
  127.3 2.0 copy-done.23
  130.5 23.3 %back.1 = (bf16[4,768,768]{2,1,0:T(8,128)(2,1)S(1)}, f32[624,768]{1,0:T(8,128)S(1)}) custom-call(f32[624,768]{1,0:T(8,128)S(1)} %get-tuple-element.39.gres_ref, bf16[624,768]{1,0:T(8,128)(2,1)S(1)} %copy-done.25, bf16[4,624,640]{2,1,0:T(8,128)(2,1)S(1)} %copy-done.21, bf16[4,3,3,208,208]{4,3,2,1,0:T(8,128)(2,1)S(1)} %copy-done.19, ...), custom_call_target="tpu_custom_call" | custom-call | flops 8000000000 | bytes 15181824 | tf_op jit(solution)/shard_map/back/pallas_call | solution.py:313
  153.9 2.2 copy-done.3
  157.3 4.8 %spread.1 = bf16[4,8,96,768]{3,2,1,0:T(8,128)(2,1)} custom-call(s32[1]{0:T(128)} %bitcast.16.me_ref, bf16[4,768,768]{2,1,0:T(8,128)(2,1)} %copy-done.3), custom_call_target="tpu_custom_call" | custom-call | tf_op jit(solution)/shard_map/spread/pallas_call | solution.py:493
  162.1 2.0 slice_bitcast_fusion
  164.2 4.5 %collective-permute-done.22 = bf16[2,1,8,96,768]{4,3,2,0,1:T(8,128)(2,1)S(1)} collective-permute-done((bf16[2,1,8,96,768]{4,3,2,0,1:T(8,128)(2,1)S(1)}, bf16[2,1,8,96,768]{4,3,2,0,1:T(8,128)(2,1)S(1)}, u32[]{:S(2)}, u32[]{:S(2)}) %collective-permute-start.22) | collective-permute-done | bytes 2359328 | tf_op jit(solution)/shard_map/ppermute | solution.py:20
  176.9 2.6 %last.1 = (f32[3,200,768]{2,1,0:T(8,128)}, f32[1,768]{1,0:T(1,128)S(1)}) custom-call(bf16[3,200,768]{2,1,0:T(8,128)(2,1)S(1)} %bitcast.215, f32[624,768]{1,0:T(8,128)S(1)} %copy-done.9, f32[624,768]{1,0:T(8,128)S(1)} %copy-done.11, f32[1,768]{1,0:T(1,128)S(1)} %reshape.279.gain_ref), custom_call_target="tpu_custom_call" | custom-call | flops 10000000 | bytes 4758528 | tf_op jit(solution)/shard_map/last/pallas_call | solution.py:313
  179.6 20.6 %collective-permute-done.23 = bf16[1,1,8,96,768]{4,3,2,1,0:T(8,128)(2,1)} collective-permute-done((bf16[1,1,8,96,768]{4,3,2,1,0:T(8,128)(2,1)}, bf16[1,1,8,96,768]{4,3,2,1,0:T(8,128)(2,1)}, u32[]{:S(2)}, u32[]{:S(2)}) %collective-permute-start.23) | collective-permute-done | bytes 1179680 | tf_op jit(solution)/shard_map/ppermute | solution.py:20
  210.1 7.4 %collective-permute-done.19 = f32[11,768]{1,0:T(8,128)S(1)} collective-permute-done((f32[11,768]{1,0:T(8,128)S(1)}, f32[11,768]{1,0:T(8,128)S(1)}, u32[]{:S(2)}, u32[]{:S(2)}) %collective-permute-start.19) | collective-permute-done | bytes 33824 | tf_op jit(solution)/shard_map/ppermute | solution.py:20
  218.5 3.2 %collective-permute-done.20 = f32[11,768]{1,0:T(8,128)S(1)} collective-permute-done((f32[11,768]{1,0:T(8,128)S(1)}, f32[11,768]{1,0:T(8,128)S(1)}, u32[]{:S(2)}, u32[]{:S(2)}) %collective-permute-start.20) | collective-permute-done | bytes 33824 | tf_op jit(solution)/shard_map/ppermute | solution.py:20
  222.6 2.5 %collective-permute-start.25 = (bf16[1,2,96,768]{2,3,1,0:T(8,128)(2,1)S(1)}, bf16[1,2,96,768]{2,3,1,0:T(8,128)(2,1)S(1)}, u32[]{:S(2)}, u32[]{:S(2)}) collective-permute-start(bf16[1,2,96,768]{2,3,1,0:T(8,128)(2,1)S(1)} %bitcast.231), channel_id=1, source_target_pairs={{0,16},{4,20},{8,24},{12,28},{16,0},{20,4},{24,8},{28,12},{1,17},{... | collective-permute-start | bytes 884744 | tf_op jit(solution)/shard_map/ppermute | solution.py:20
  225.2 8.2 %collective-permute-done.21 = f32[11,768]{1,0:T(8,128)S(1)} collective-permute-done((f32[11,768]{1,0:T(8,128)S(1)}, f32[11,768]{1,0:T(8,128)S(1)}, u32[]{:S(2)}, u32[]{:S(2)}) %collective-permute-start.21) | collective-permute-done | bytes 33824 | tf_op jit(solution)/shard_map/ppermute | solution.py:20
  234.3 6.9 %collective-permute-done.25 = bf16[1,2,96,768]{2,3,1,0:T(8,128)(2,1)S(1)} collective-permute-done((bf16[1,2,96,768]{2,3,1,0:T(8,128)(2,1)S(1)}, bf16[1,2,96,768]{2,3,1,0:T(8,128)(2,1)S(1)}, u32[]{:S(2)}, u32[]{:S(2)}) %collective-permute-start.25) | collective-permute-done | bytes 294944 | tf_op jit(solution)/shard_map/ppermute | solution.py:20
  241.9 5.8 %collective-permute-done.26 = bf16[1,1,96,768]{2,3,1,0:T(8,128)(2,1)S(1)} collective-permute-done((bf16[1,1,96,768]{2,3,1,0:T(8,128)(2,1)S(1)}, bf16[1,1,96,768]{2,3,1,0:T(8,128)(2,1)S(1)}, u32[]{:S(2)}, u32[]{:S(2)}) %collective-permute-start.26) | collective-permute-done | bytes 147488 | tf_op jit(solution)/shard_map/ppermute | solution.py:20
  (192 shorter events, 67.7 us)
Async XLA Ops:
  0.6 35.3 %copy-start = (s32[12,200]{1,0:T(8,128)S(1)}, s32[12,200]{1,0:T(8,128)}, u32[]{:S(2)}) copy-start(s32[12,200]{1,0:T(8,128)} %param.11) | copy-start | bytes 28804
  3.3 9.1 %collective-permute-start.3 = (bf16[48,768]{1,0:T(8,128)(2,1)S(1)}, bf16[48,768]{1,0:T(8,128)(2,1)S(1)}, u32[]{:S(2)}, u32[]{:S(2)}) collective-permute-start(bf16[48,768]{1,0:T(8,128)(2,1)S(1)} %get-tuple-element.153), channel_id=1, source_target_pairs={{0,16},{4,20},{8,24},{12,28},{16,0},{20,4},{24,8},{28,12},{1,17},{... | collective-permute-start | bytes 221192 | tf_op jit(solution)/shard_map/ppermute | solution.py:20
  7.4 7.1 %collective-permute-start.8 = (bf16[48,768]{1,0:T(8,128)(2,1)S(1)}, bf16[48,768]{1,0:T(8,128)(2,1)S(1)}, u32[]{:S(2)}, u32[]{:S(2)}) collective-permute-start(bf16[48,768]{1,0:T(8,128)(2,1)S(1)} %get-tuple-element.152), channel_id=1, source_target_pairs={{0,16},{4,20},{8,24},{12,28},{16,0},{20,4},{24,8},{28,12},{1,17},{... | collective-permute-start | bytes 221192 | tf_op jit(solution)/shard_map/ppermute | solution.py:20
  12.4 5.9 %collective-permute-start.4 = (bf16[2,48,768]{2,1,0:T(8,128)(2,1)S(1)}, bf16[2,48,768]{2,1,0:T(8,128)(2,1)S(1)}, u32[]{:S(2)}, u32[]{:S(2)}) collective-permute-start(bf16[2,48,768]{2,1,0:T(8,128)(2,1)S(1)} %get-tuple-element.155), channel_id=1, source_target_pairs={{0,8},{4,12},{8,0},{12,4},{16,24},{20,28},{24,16},{28,20},{1,9},{5... | collective-permute-start | bytes 442376 | tf_op jit(solution)/shard_map/ppermute | solution.py:20
  14.5 6.3 %collective-permute-start.9 = (bf16[2,48,768]{2,1,0:T(8,128)(2,1)S(1)}, bf16[2,48,768]{2,1,0:T(8,128)(2,1)S(1)}, u32[]{:S(2)}, u32[]{:S(2)}) collective-permute-start(bf16[2,48,768]{2,1,0:T(8,128)(2,1)S(1)} %get-tuple-element.149), channel_id=1, source_target_pairs={{0,8},{4,12},{8,0},{12,4},{16,24},{20,28},{24,16},{28,20},{1,9},{5... | collective-permute-start | bytes 442376 | tf_op jit(solution)/shard_map/ppermute | solution.py:20
  18.4 7.0 %collective-permute-start.5 = (bf16[2,2,48,768]{3,2,1,0:T(8,128)(2,1)S(1)}, bf16[2,2,48,768]{3,2,1,0:T(8,128)(2,1)S(1)}, u32[]{:S(2)}, u32[]{:S(2)}) collective-permute-start(bf16[2,2,48,768]{3,2,1,0:T(8,128)(2,1)S(1)} %get-tuple-element.145), channel_id=1, source_target_pairs={{0,4},{4,0},{8,12},{12,8},{16,20},{20,16},{24,28},{28,24},{1,5},{5... | collective-permute-start | bytes 884744 | tf_op jit(solution)/shard_map/ppermute | solution.py:20
  20.9 9.9 %collective-permute-start.10 = (bf16[2,2,48,768]{3,2,1,0:T(8,128)(2,1)S(1)}, bf16[2,2,48,768]{3,2,1,0:T(8,128)(2,1)S(1)}, u32[]{:S(2)}, u32[]{:S(2)}) collective-permute-start(bf16[2,2,48,768]{3,2,1,0:T(8,128)(2,1)S(1)} %get-tuple-element.143), channel_id=1, source_target_pairs={{0,2},{1,3},{2,0},{3,1},{4,6},{5,7},{6,4},{7,5},{8,10},{9,11},{10,... | collective-permute-start | bytes 884744 | tf_op jit(solution)/shard_map/ppermute | solution.py:20
  25.4 16.6 %collective-permute-start.6 = (bf16[2,2,2,48,768]{4,3,2,1,0:T(8,128)(2,1)S(1)}, bf16[2,2,2,48,768]{4,3,2,1,0:T(8,128)(2,1)S(1)}, u32[]{:S(2)}, u32[]{:S(2)}) collective-permute-start(bf16[2,2,2,48,768]{4,3,2,1,0:T(8,128)(2,1)S(1)} %pad_maximum_fusion.2), channel_id=1, source_target_pairs={{0,2},{1,3},{2,0},{3,1},{4,6},{5,7},{6,4},{7,5},{8,10},{9,11},{10,... | collective-permute-start | bytes 1769480 | tf_op jit(solution)/shard_map/ppermute | solution.py:20
  30.9 13.2 %collective-permute-start.11 = (bf16[2,2,2,48,768]{4,3,2,1,0:T(8,128)(2,1)S(1)}, bf16[2,2,2,48,768]{4,3,2,1,0:T(8,128)(2,1)}, u32[]{:S(2)}, u32[]{:S(2)}) collective-permute-start(bf16[2,2,2,48,768]{4,3,2,1,0:T(8,128)(2,1)S(1)} %get-tuple-element.129), channel_id=1, source_target_pairs={{0,4},{4,0},{8,12},{12,8},{16,20},{20,16},{24,28},{28,24},{1,5},{5... | collective-permute-start | bytes 1769480 | tf_op jit(solution)/shard_map/ppermute | solution.py:20
  32.8 4.7 %collective-permute-start = (bf16[10,96]{1,0:T(8,128)(2,1)S(1)}, bf16[10,96]{1,0:T(8,128)(2,1)S(1)}, u32[]{:S(2)}, u32[]{:S(2)}) collective-permute-start(bf16[10,96]{1,0:T(8,128)(2,1)S(1)} %get-tuple-element.177), channel_id=1, source_target_pairs={{0,16},{4,20},{8,24},{12,28},{16,0},{20,4},{24,8},{28,12},{1,17},{... | collective-permute-start | bytes 5768 | tf_op jit(solution)/shard_map/ppermute | solution.py:20
  37.6 9.2 %collective-permute-start.1 = (bf16[2,10,96]{2,1,0:T(8,128)(2,1)S(1)}, bf16[2,10,96]{2,1,0:T(8,128)(2,1)S(1)}, u32[]{:S(2)}, u32[]{:S(2)}) collective-permute-start(bf16[2,10,96]{2,1,0:T(8,128)(2,1)S(1)} %get-tuple-element.171), channel_id=1, source_target_pairs={{0,8},{4,12},{8,0},{12,4},{16,24},{20,28},{24,16},{28,20},{1,9},{5... | collective-permute-start | bytes 11528 | tf_op jit(solution)/shard_map/ppermute | solution.py:20
  44.0 7.2 %collective-permute-start.7 = (bf16[2,8,48,768]{3,2,1,0:T(8,128)(2,1)S(1)}, bf16[2,8,48,768]{3,2,1,0:T(8,128)(2,1)}, u32[]{:S(2)}, u32[]{:S(2)}) collective-permute-start(bf16[2,8,48,768]{3,2,1,0:T(8,128)(2,1)S(1)} %pad_maximum_fusion.a_ref), channel_id=1, source_target_pairs={{0,1},{1,0},{2,3},{3,2},{4,5},{5,4},{6,7},{7,6},{8,9},{9,8},{10,11... | collective-permute-start | bytes 3538952 | tf_op jit(solution)/shard_map/ppermute | solution.py:20
  46.6 4.5 %collective-permute-start.12 = (bf16[2,8,48,768]{3,2,1,0:T(8,128)(2,1)}, bf16[2,8,48,768]{3,2,1,0:T(8,128)(2,1)}, u32[]{:S(2)}, u32[]{:S(2)}) collective-permute-start(bf16[2,8,48,768]{3,2,1,0:T(8,128)(2,1)} %bitcast.48.b_ref), channel_id=1, source_target_pairs={{0,1},{1,0},{2,3},{3,2},{4,5},{5,4},{6,7},{7,6},{8,9},{9,8},{10,11... | collective-permute-start | bytes 3538952 | tf_op jit(solution)/shard_map/ppermute | solution.py:20
  46.8 3.8 %collective-permute-start.2 = (bf16[2,2,10,96]{3,2,0,1:T(8,128)(2,1)S(1)}, bf16[2,2,10,96]{3,2,0,1:T(8,128)(2,1)S(1)}, u32[]{:S(2)}, u32[]{:S(2)}) collective-permute-start(bf16[2,2,10,96]{3,2,0,1:T(8,128)(2,1)S(1)} %get-tuple-element.167), channel_id=1, source_target_pairs={{0,4},{4,0},{8,12},{12,8},{16,20},{20,16},{24,28},{28,24},{1,5},{5... | collective-permute-start | bytes 23048 | tf_op jit(solution)/shard_map/ppermute | solution.py:20
  92.9 4.4 %collective-permute-start.13 = (bf16[1,8,2,3,768]{4,1,3,2,0:T(8,128)(2,1)S(1)}, bf16[1,8,2,3,768]{4,1,3,2,0:T(8,128)(2,1)S(1)}, u32[]{:S(2)}, u32[]{:S(2)}) collective-permute-start(bf16[1,8,2,3,768]{4,1,3,2,0:T(8,128)(2,1)S(1)} %bitcast.233), channel_id=1, source_target_pairs={{0,2},{1,3},{2,0},{3,1},{4,6},{5,7},{6,4},{7,5},{8,10},{9,11},{10,... | collective-permute-start | bytes 221192 | tf_op jit(solution)/shard_map/ppermute | solution.py:20
  97.4 1.4 collective-permute-start.14
  105.0 22.3 %copy-start.21 = (bf16[4,624,640]{2,1,0:T(8,128)(2,1)S(1)}, bf16[4,624,640]{2,1,0:T(8,128)(2,1)}, u32[]{:S(2)}) copy-start(bf16[4,624,640]{2,1,0:T(8,128)(2,1)} %copy-done.20) | copy-start | bytes 9584644
  108.0 1.4 collective-permute-start.15
  109.5 4.4 %collective-permute-start.16 = (bf16[1,1,8,2,3,768]{5,2,4,3,1,0:T(8,128)(2,1)S(1)}, bf16[1,1,8,2,3,768]{5,2,4,3,1,0:T(8,128)(2,1)S(1)}, u32[]{:S(2)}, u32[]{:S(2)}) collective-permute-start(bf16[1,1,8,2,3,768]{5,2,4,3,1,0:T(8,128)(2,1)S(1)} %slice_bitcast_fusion.10), channel_id=1, source_target_pairs={{0,2},{1,3},{2,0},{3,1},{4,6},{5,7},{6,4},{7,5},{8,10},{9,11},{10,... | collective-permute-start | bytes 221192 | tf_op jit(solution)/shard_map/ppermute | solution.py:20
  127.3 26.6 %copy-start.8 = (f32[624,768]{1,0:T(8,128)}, f32[624,768]{1,0:T(8,128)S(1)}, u32[]{:S(2)}) copy-start(f32[624,768]{1,0:T(8,128)S(1)} %get-tuple-element.39.gres_ref) | copy-start | bytes 5750788
  164.1 4.6 %collective-permute-start.22 = (bf16[2,1,8,96,768]{4,3,2,0,1:T(8,128)(2,1)S(1)}, bf16[2,1,8,96,768]{4,3,2,0,1:T(8,128)(2,1)S(1)}, u32[]{:S(2)}, u32[]{:S(2)}) collective-permute-start(bf16[2,1,8,96,768]{4,3,2,0,1:T(8,128)(2,1)S(1)} %slice_bitcast_fusion), channel_id=1, source_target_pairs={{0,1},{1,0},{2,3},{3,2},{4,5},{5,4},{6,7},{7,6},{8,9},{9,8},{10,11... | collective-permute-start | bytes 7077896 | tf_op jit(solution)/shard_map/ppermute | solution.py:20
  171.9 28.3 %collective-permute-start.23 = (bf16[1,1,8,96,768]{4,3,2,1,0:T(8,128)(2,1)}, bf16[1,1,8,96,768]{4,3,2,1,0:T(8,128)(2,1)}, u32[]{:S(2)}, u32[]{:S(2)}) collective-permute-start(bf16[1,1,8,96,768]{4,3,2,1,0:T(8,128)(2,1)} %slice_bitcast_fusion.2), channel_id=1, source_target_pairs={{0,2},{1,3},{2,0},{3,1},{4,6},{5,7},{6,4},{7,5},{8,10},{9,11},{10,... | collective-permute-start | bytes 3538952 | tf_op jit(solution)/shard_map/ppermute | solution.py:20
  176.9 23.4 %copy-start.28 = (bf16[1,2,1,8,96,768]{5,4,3,2,1,0:T(8,128)(2,1)S(1)}, bf16[1,2,1,8,96,768]{5,4,3,2,1,0:T(8,128)(2,1)}, u32[]{:S(2)}) copy-start(bf16[1,2,1,8,96,768]{5,4,3,2,1,0:T(8,128)(2,1)} %copy-done.27) | copy-start | bytes 7077892
  179.5 24.4 %copy-start.17 = (bf16[96,768]{1,0:T(8,128)(2,1)S(1)}, bf16[96,768]{1,0:T(8,128)(2,1)}, u32[]{:S(2)}) copy-start(bf16[96,768]{1,0:T(8,128)(2,1)} %copy-done.16) | copy-start | bytes 442372
  179.5 22.8 %collective-permute-start.17 = (f32[11,768]{1,0:T(8,128)S(1)}, f32[11,768]{1,0:T(8,128)S(1)}, u32[]{:S(2)}, u32[]{:S(2)}) collective-permute-start(f32[11,768]{1,0:T(8,128)S(1)} %select_maximum_fusion), channel_id=1, source_target_pairs={{0,1},{1,0},{2,3},{3,2},{4,5},{5,4},{6,7},{7,6},{8,9},{9,8},{10,11... | collective-permute-start | bytes 101384 | tf_op jit(solution)/shard_map/ppermute | solution.py:20
  201.9 20.3 %collective-permute-start.24 = (bf16[4,1,96,768]{3,2,1,0:T(8,128)(2,1)S(1)}, bf16[4,1,96,768]{3,2,1,0:T(8,128)(2,1)S(1)}, u32[]{:S(2)}, u32[]{:S(2)}) collective-permute-start(bf16[4,1,96,768]{3,2,1,0:T(8,128)(2,1)S(1)} %slice_bitcast_fusion.4), channel_id=1, source_target_pairs={{0,4},{4,0},{8,12},{12,8},{16,20},{20,16},{24,28},{28,24},{1,5},{5... | collective-permute-start | bytes 1769480 | tf_op jit(solution)/shard_map/ppermute | solution.py:20
  202.4 4.2 %collective-permute-start.18 = (f32[11,768]{1,0:T(8,128)S(1)}, f32[11,768]{1,0:T(8,128)S(1)}, u32[]{:S(2)}, u32[]{:S(2)}) collective-permute-start(f32[11,768]{1,0:T(8,128)S(1)} %fusion.22), channel_id=1, source_target_pairs={{0,2},{1,3},{2,0},{3,1},{4,6},{5,7},{6,4},{7,5},{8,10},{9,11},{10,... | collective-permute-start | bytes 101384 | tf_op jit(solution)/shard_map/ppermute | solution.py:20
  206.5 11.0 %collective-permute-start.19 = (f32[11,768]{1,0:T(8,128)S(1)}, f32[11,768]{1,0:T(8,128)S(1)}, u32[]{:S(2)}, u32[]{:S(2)}) collective-permute-start(f32[11,768]{1,0:T(8,128)S(1)} %add.50), channel_id=1, source_target_pairs={{0,4},{4,0},{8,12},{12,8},{16,20},{20,16},{24,28},{28,24},{1,5},{5... | collective-permute-start | bytes 101384 | tf_op jit(solution)/shard_map/ppermute | solution.py:20
  217.5 4.2 %collective-permute-start.20 = (f32[11,768]{1,0:T(8,128)S(1)}, f32[11,768]{1,0:T(8,128)S(1)}, u32[]{:S(2)}, u32[]{:S(2)}) collective-permute-start(f32[11,768]{1,0:T(8,128)S(1)} %add.51), channel_id=1, source_target_pairs={{0,8},{4,12},{8,0},{12,4},{16,24},{20,28},{24,16},{28,20},{1,9},{5... | collective-permute-start | bytes 101384 | tf_op jit(solution)/shard_map/ppermute | solution.py:20
  221.7 11.7 %collective-permute-start.21 = (f32[11,768]{1,0:T(8,128)S(1)}, f32[11,768]{1,0:T(8,128)S(1)}, u32[]{:S(2)}, u32[]{:S(2)}) collective-permute-start(f32[11,768]{1,0:T(8,128)S(1)} %add.52), channel_id=1, source_target_pairs={{0,16},{4,20},{8,24},{12,28},{16,0},{20,4},{24,8},{28,12},{1,17},{... | collective-permute-start | bytes 101384 | tf_op jit(solution)/shard_map/ppermute | solution.py:20
  222.6 18.6 %collective-permute-start.25 = (bf16[1,2,96,768]{2,3,1,0:T(8,128)(2,1)S(1)}, bf16[1,2,96,768]{2,3,1,0:T(8,128)(2,1)S(1)}, u32[]{:S(2)}, u32[]{:S(2)}) collective-permute-start(bf16[1,2,96,768]{2,3,1,0:T(8,128)(2,1)S(1)} %bitcast.231), channel_id=1, source_target_pairs={{0,16},{4,20},{8,24},{12,28},{16,0},{20,4},{24,8},{28,12},{1,17},{... | collective-permute-start | bytes 884744 | tf_op jit(solution)/shard_map/ppermute | solution.py:20
  241.3 6.4 %collective-permute-start.26 = (bf16[1,1,96,768]{2,3,1,0:T(8,128)(2,1)S(1)}, bf16[1,1,96,768]{2,3,1,0:T(8,128)(2,1)S(1)}, u32[]{:S(2)}, u32[]{:S(2)}) collective-permute-start(bf16[1,1,96,768]{2,3,1,0:T(8,128)(2,1)S(1)} %slice_bitcast_fusion.6), channel_id=1, source_target_pairs={{0,8},{4,12},{8,0},{12,4},{16,24},{20,28},{24,16},{28,20},{1,9},{5... | collective-permute-start | bytes 442376 | tf_op jit(solution)/shard_map/ppermute | solution.py:20
  (29 other events, 132.0 us)

commit v4 on v2

v4 whole, which is shorter than its diff:
```python
import functools
import math

import jax
import jax.numpy as jnp
from jax import lax
from jax.experimental import pallas as pl
from jax.experimental.pallas import tpu as pltpu
from jax.sharding import PartitionSpec as P

HEAD_DIM = 64


epsilon = 1e-06
bf16 = jnp.bfloat16
f32 = jnp.float32


def bits_of(size):
    return [1 << k for k in reversed(range(size.bit_length() - 1))]


def swap(array_in, axis_name, size, bit):
    return lax.ppermute(array_in, axis_name, [(i, i ^ bit) for i in range(size)])


def swap_both(array_in, dp, mp, even, odd):
    pairs = []
    for d in range(dp):
        for m in range(mp):
            flip = odd if m & 1 else even
            pairs.append((d * mp + m, (d ^ flip[0]) * mp + (m ^ flip[1])))
    return lax.ppermute(array_in, ("dp", "mp"), pairs)


def gather_mp(block, mp):
    held = block[None]
    for bit in bits_of(mp):
        other = swap(held, "mp", mp, bit)
        held = jnp.stack([held, other], 1).reshape((-1,) + block.shape)
    return held


def scatter(held, axis_name, size, bits, unit=1):
    left = sorted(bits)
    for bit in bits:
        inner = 1 << left.index(bit)
        left.remove(bit)
        pairs = held.reshape((held.shape[0] // (2 * inner), 2, inner) + held.shape[1:])
        other = swap(pairs[:, 1], axis_name, size, bit * unit)
        held = pairs[:, 0].astype(f32) + other.astype(f32)
        held = held.astype(bf16).reshape((-1,) + held.shape[2:])
    return held[0]


def scatter_open(held, axis_name, size, bits, unit):
    held = held.reshape((-1,) + held.shape[-2:])
    last = bits[-1]
    for bit in bits[:-1]:
        half = held.shape[0] // 2
        other = swap(held[half:], axis_name, size, bit * unit)
        held = plus(held[:half], other)
    return held[0], swap(held[1], axis_name, size, last * unit)


def plus(*terms):
    total = terms[0].astype(f32)
    for term in terms[1:]:
        total = total + term.astype(f32)
    return total.astype(bf16)


def reorder(blocks, me):
    size = blocks.shape[0]
    for bit in bits_of(size):
        pairs = blocks.reshape((size // (2 * bit), 2, bit) + blocks.shape[1:])
        blocks = jnp.where((me & bit) > 0, pairs[:, ::-1], pairs).reshape(blocks.shape)
    return blocks


def mm(a, b):
    return lax.dot_general(a, b, (((1,), (0,)), ((), ())), preferred_element_type=f32)


def mm_nt(a, b):
    return lax.dot_general(a, b, (((1,), (1,)), ((), ())), preferred_element_type=f32)


def mm_tn(a, b):
    return lax.dot_general(a, b, (((0,), (0,)), ((), ())), preferred_element_type=f32)


def unit_of(rows_f):
    mean_row = jnp.mean(rows_f, axis=-1, keepdims=True)
    centered = rows_f - mean_row
    variance = jnp.mean(centered * centered, axis=-1, keepdims=True)
    inverse = lax.rsqrt(variance + epsilon)
    return centered * inverse, inverse


def padded(value, pad):
    return jnp.concatenate([value, jnp.zeros((pad, value.shape[1]), value.dtype)], 0)


def low_lanes(rows):
    return lax.broadcasted_iota(jnp.int32, (rows, 128), 1) < HEAD_DIM


JOINED = 640


def pack_kernel(qkv_ref, out_ref, one_ref, two_ref, router_ref, packed_ref, extra_ref):
    low, mid = 2 * HEAD_DIM, qkv_ref.shape[2]
    out = out_ref[...].astype(f32).T.astype(bf16)
    packed_ref[...] = jnp.concatenate(
        [qkv_ref[c, :, :low] for c in range(3)]
        + [qkv_ref[c, :, low:mid] for c in range(3)]
        + [out[:, low:mid], out[:, :low]],
        axis=1,
    )
    rows = one_ref.shape[1]
    columns = [one_ref[...], two_ref[...], router_ref[...]]
    columns = [value.astype(f32) for value in columns]
    filled = sum(value.shape[0] for value in columns)
    columns.append(jnp.zeros((extra_ref.shape[1] - filled, rows), f32))
    extra_ref[...] = jnp.concatenate(columns, 0).T.astype(bf16)


def unpack_kernel(own_ref, other_ref, qkv_ref, out_ref):
    low, mid = 2 * HEAD_DIM, qkv_ref.shape[2]
    summed = own_ref[...].astype(f32) + other_ref[...].astype(f32)
    for c in range(3):
        qkv_ref[c, :, :low] = summed[:, c * low : (c + 1) * low]
        start = 3 * low + c * HEAD_DIM
        qkv_ref[c, :, low:mid] = summed[:, start : start + HEAD_DIM]
    out_ref[...] = jnp.concatenate([summed[:, 640:], summed[:, 576:640]], axis=1).T


def length_of(mask_ref, me_ref, b, images):
    row = mask_ref[pl.ds(me_ref[2] * images + b, 1), :]
    return jnp.sum(row.astype(f32), axis=1, keepdims=True)


def seen_row(length, tall):
    return lax.broadcasted_iota(jnp.int32, (1, tall), 1).astype(f32) < length


def seen_column(length, tall):
    return lax.broadcasted_iota(jnp.int32, (tall, 1), 0).astype(f32) < length


def prep_kernel(me_ref, x_ref, extra_ref, h_ref, ht_ref, small_ref, *, images, seq, tall):
    blocks, rows = extra_ref.shape[0], extra_ref.shape[1]
    me = me_ref[0]
    parts = [extra_ref[jnp.bitwise_xor(me, d) if blocks > 1 else 0] for d in range(blocks)]
    small_ref[...] = jnp.concatenate(parts, 0).astype(f32).T
    gain = small_ref[0:1, :]
    for b in range(images):
        unit, _ = unit_of(x_ref[b].astype(f32))
        h_ref[pl.ds(b * tall, tall), :] = padded((unit * gain).astype(bf16), tall - seq)
    ht_ref[...] = h_ref[...].T


def fetch_group(me_ref, w_ref, slot, x, core, near, far, other_near, other_far):
    me, at_core = me_ref[0], me_ref[1]
    rows = near.shape[2]
    blocks = 2 * near.shape[1]

    def block(d, carry):
        r = jnp.bitwise_xor(me, d)
        low, high = jnp.bitwise_and(r, 1), jnp.right_shift(r, 1)
        at = pl.ds(pl.multiple_of(d * rows, 16), rows)
        for mine, first, second in ((True, near, far), (False, other_near, other_far)):
            ours = at_core == core if mine else at_core != core
            if core == 0:

                @pl.when(ours)
                def _(first=first, second=second):
                    w_ref[slot, at, :] = (second if x else first)[low, high]

            else:

                @pl.when(jnp.logical_and(ours, low == 0))
                def _(first=first):
                    w_ref[slot, at, :] = first[x, high]

                @pl.when(jnp.logical_and(ours, low == 1))
                def _(second=second):
                    w_ref[slot, at, :] = second[x, high]

        return carry

    lax.fori_loop(0, blocks, block, 0)


def front_group(j, h_ref, mask_ref, me_ref, w_ref, qkv_ref, p_ref, ho_ref, br_ref, images, tall):
    scale = HEAD_DIM ** (-0.5)
    low = low_lanes(tall)
    qkv_ref[j] = mm(h_ref[...], w_ref[j, :, :JOINED]).astype(bf16)
    for b in range(images):
        at = pl.ds(b * tall, tall)
        joined = qkv_ref[j, at, :]
        q_pair, k_pair, v_pair = joined[:, :128], joined[:, 128:256], joined[:, 256:384]
        qk_last, v_last = joined[:, 384:512], joined[:, 512:640]
        k_last = pltpu.roll(qk_last.astype(f32), HEAD_DIM, 1).astype(bf16)
        none = jnp.zeros_like(q_pair)
        bias = jnp.where(seen_row(length_of(mask_ref, me_ref, b, images), tall), 0.0, -1e30)
        outs = []
        for head, (q, k, v) in enumerate(
            (
                (jnp.where(low, q_pair, none), k_pair, v_pair),
                (jnp.where(low, none, q_pair), k_pair, v_pair),
                (jnp.where(low, qk_last, none), k_last, v_last),
            )
        ):
            scores = mm_nt(q, k) * scale + bias
            terms = jnp.exp(scores - jnp.max(scores, axis=-1, keepdims=True))
            probs = (terms * (1.0 / jnp.sum(terms, axis=-1, keepdims=True))).astype(bf16)
            p_ref[j, b, head] = probs
            outs.append(mm(probs, v))
        last = jnp.where(low, 0.0, pltpu.roll(outs[2], HEAD_DIM, 1))
        pair = jnp.where(low, outs[0], outs[1])
        ho_ref[j, at, :] = jnp.concatenate([last, pair], 1).astype(bf16)
    br_ref[...] += mm_nt(ho_ref[j], w_ref[j, :, 512:])


def front_first_kernel(me_ref, h_ref, mask_ref, *refs, images, tall, ready):
    if ready:
        (source,), outs = refs[:1], refs[1:]
    else:
        (near, other_near), outs = refs[:2], refs[2:]
    w_ref, qkv_ref, p_ref, ho_ref, br_ref = outs
    if ready:
        w_ref[0] = source[...]
    else:
        fetch_group(me_ref, w_ref, 0, 0, 0, near, None, other_near, None)
    br_ref[...] = jnp.zeros_like(br_ref)
    front_group(0, h_ref, mask_ref, me_ref, w_ref, qkv_ref, p_ref, ho_ref, br_ref, images, tall)


def front_rest_kernel(me_ref, h_ref, mask_ref, first_ref, *refs, images, tall, ready):
    outs = refs[-5:]
    w_ref, qkv_ref, p_ref, ho_ref, br_ref = outs
    order = ((1, 0), (0, 1), (1, 1))
    for slot, (x, core) in enumerate(order):
        if ready:
            w_ref[slot] = refs[slot][...]
        else:
            fetch_group(me_ref, w_ref, slot, x, core, *refs[:4])
    br_ref[...] = first_ref[...]

    def group(j, carry):
        front_group(j, h_ref, mask_ref, me_ref, w_ref, qkv_ref, p_ref, ho_ref, br_ref, images, tall)
        return carry

    lax.fori_loop(0, len(order), group, 0)


def spot(rows, b, start, experts):
    each = rows // experts
    at_row = lax.broadcasted_iota(jnp.int32, (rows, experts), 0)
    at_column = lax.broadcasted_iota(jnp.int32, (rows, experts), 1)
    return jnp.where(at_row == at_column * each + (start + b), 1.0, 0.0).astype(bf16)


def route_kernel(
    me_ref, x_ref, br_ref, cot_ref, mask_ref, ex_ref,
    res_ref, h_ref, soft_ref, sent_ref, sq_ref, *, images, seq, tall, experts
):
    rows = sent_ref.shape[0]
    half = rows // experts // 2
    router = ex_ref[2 : 2 + experts, :].astype(bf16)
    gain = ex_ref[1:2, :]
    total = jnp.zeros(sent_ref.shape, f32)
    for b in range(images):
        at = pl.ds(b * tall, tall)
        length = length_of(mask_ref, me_ref, b, images)
        branch = br_ref[at, :]
        resid = padded(x_ref[b].astype(f32), tall - seq) + branch
        res_ref[at, :] = resid
        unit, _ = unit_of(resid)
        h_two = (unit * gain).astype(bf16)
        h_ref[at, :] = h_two
        logits = mm_nt(router, h_two)
        held = jnp.where(seen_row(length, tall), logits, -1e30)
        terms = jnp.exp(held - jnp.max(held, axis=1, keepdims=True))
        dispatch = terms / jnp.sum(terms, axis=1, keepdims=True)
        terms = jnp.exp(logits - jnp.max(logits, axis=0, keepdims=True))
        combine = terms / jnp.sum(terms, axis=0, keepdims=True)
        soft_ref[0, b] = dispatch
        soft_ref[1, b] = combine
        cot = padded(cot_ref[b], tall - seq)
        wide_d = mm(spot(rows, b, 0, experts), dispatch.astype(bf16)).astype(bf16)
        wide_c = mm(spot(rows, b, half, experts), combine.astype(bf16)).astype(bf16)
        total += mm(wide_d, h_two) + mm(wide_c, cot)
        squares = jnp.sum(branch * branch, axis=1, keepdims=True)
        squares = jnp.sum(jnp.where(seen_column(length, tall), squares, 0.0), axis=0, keepdims=True)
        sq_ref[b] = jnp.broadcast_to(squares, (1, 128))
    sent_ref[...] = total.astype(bf16)


def expert_kernel(got_ref, first_ref, second_ref, hid_ref, pre_ref, grad_ref, back_ref, *, each):
    rows = got_ref.shape[0]
    half = each // 2
    got = got_ref[...]
    own = jnp.bitwise_and(lax.broadcasted_iota(jnp.int32, (rows, 1), 0), each - 1) < half
    grads = jnp.where(own, pltpu.roll(got.astype(f32), rows - half, 0), 0.0).astype(bf16)
    grad_ref[...] = grads
    u = mm(got, first_ref[...])
    cubic = 0.7978845608028654 * (u + 0.044715 * u * u * u)
    t = jnp.tanh(cubic)
    hidden = jnp.where(own, 0.5 * u * (1.0 + t), 0.0).astype(bf16)
    hid_ref[...] = hidden
    slope = 0.5 * (1.0 + t) + 0.5 * u * (1.0 - t * t) * 0.7978845608028654 * (
        1.0 + 3.0 * 0.044715 * u * u
    )
    grad_pre = (mm_nt(grads, second_ref[...]) * slope).astype(bf16)
    pre_ref[...] = grad_pre
    out = mm(hidden, second_ref[...])
    grad_in = mm_nt(grad_pre, first_ref[...])
    back_ref[...] = jnp.where(own, out, pltpu.roll(grad_in, half, 0)).astype(bf16)


def mix_kernel(
    me_ref, res_ref, h_ref, soft_ref, cot_ref, mask_ref, ex_ref, back_ref, sq_ref,
    out_ref, gres_ref, small_ref, *, images, seq, tall, experts, groups
):
    small_ref[...] = jnp.zeros_like(small_ref)
    router = ex_ref[2 : 2 + experts, :].astype(bf16)
    gain = ex_ref[1:2, :]
    width = out_ref.shape[2]
    lanes = lax.broadcasted_iota(jnp.int32, (1, width), 1)
    roots = jnp.zeros((1, width), f32)
    for b in range(images):
        at = pl.ds(b * tall, tall)
        length = length_of(mask_ref, me_ref, b, images)
        resid, h_two = res_ref[at, :], h_ref[at, :]
        dispatch, combine = soft_ref[0, b], soft_ref[1, b]
        dispatch_low, combine_low = dispatch.astype(bf16), combine.astype(bf16)
        returned, grad_slots = back_ref[0, b], back_ref[1, b]
        cot = padded(cot_ref[b], tall - seq)
        mixed = mm_tn(combine_low, returned)
        stream = resid + mixed
        out_ref[b] = stream[:seq].astype(bf16)
        column = seen_column(length, tall)
        sums = []
        for value in (stream, mixed):
            squares = jnp.sum(value * value, axis=1, keepdims=True)
            sums.append(jnp.sum(jnp.where(column, squares, 0.0), axis=0, keepdims=True))
        sums.insert(1, sq_ref[b, :, 0:1])
        for k, value in enumerate(sums):
            root = jnp.sqrt(value / (length * width))
            mine = lanes == k * (groups * images) + me_ref[2] * images + b
            roots += jnp.where(mine, root, 0.0)
        grad_c = mm_nt(returned, cot)
        grad_c = combine * (grad_c - jnp.sum(grad_c * combine, axis=0, keepdims=True))
        grad_d = mm_nt(grad_slots, h_two)
        grad_d = dispatch * (grad_d - jnp.sum(grad_d * dispatch, axis=1, keepdims=True))
        grad_logits = (grad_d + grad_c).astype(bf16)
        grad_h = mm_tn(dispatch_low, grad_slots) + mm_tn(grad_logits, router)
        small_ref[0:experts, :] += mm(grad_logits, h_two)
        unit, inverse = unit_of(resid)
        small_ref[experts + 1 : experts + 2, :] += jnp.sum(grad_h * unit, axis=0, keepdims=True)
        scaled = grad_h * gain
        mean_grad = jnp.mean(scaled, axis=-1, keepdims=True)
        mean_proj = jnp.mean(scaled * unit, axis=-1, keepdims=True)
        gres_ref[at, :] = cot.astype(f32) + inverse * (scaled - mean_grad - unit * mean_proj)
    small_ref[experts + 2 : experts + 3, :] = roots


def back_group(
    core, source, me_ref, gb_ref, gbt_ref, ht_ref, gw_ref, gh_ref, gj_ref, dho_ref, images, tall
):
    qkv_ref, p_ref, ho_ref, w_ref, j = source
    scale = HEAD_DIM ** (-0.5)
    low = low_lanes(tall)
    dho_ref[...] = mm(gb_ref[...], w_ref[j, :, 512:])
    for b in range(images):
        at = pl.ds(b * tall, tall)
        joined = qkv_ref[j, at, :]
        q_pair, k_pair, v_pair = joined[:, :128], joined[:, 128:256], joined[:, 256:384]
        qk_last, v_last = joined[:, 384:512], joined[:, 512:640]
        heads = ho_ref[j, at, :].astype(f32)
        grad = dho_ref[at, :].astype(bf16).astype(f32)
        product = grad * heads
        pair = product[:, 128:]
        dots = (
            jnp.sum(jnp.where(low, pair, 0.0), axis=1, keepdims=True),
            jnp.sum(jnp.where(low, 0.0, pair), axis=1, keepdims=True),
            jnp.sum(product[:, :128], axis=1, keepdims=True),
        )
        grad_pair = grad[:, 128:]
        grad_last = jnp.where(low, pltpu.roll(grad[:, :128], HEAD_DIM, 1), 0.0).astype(bf16)
        gq, gk, gv = [], [], []
        for head, (g, v, q, k) in enumerate(
            (
                (jnp.where(low, grad_pair, 0.0).astype(bf16), v_pair, q_pair, k_pair),
                (jnp.where(low, 0.0, grad_pair).astype(bf16), v_pair, q_pair, k_pair),
                (grad_last, v_last, qk_last, qk_last),
            )
        ):
            probs = p_ref[j, b, head]
            grad_p = mm_nt(g, v)
            grad_s = (probs.astype(f32) * (grad_p - dots[head])).astype(bf16)
            gq.append(mm(grad_s, k))
            gk.append(mm_tn(grad_s, q))
            gv.append(mm_tn(probs, g))
        last = pltpu.roll(jnp.where(low, gk[2], gq[2]), HEAD_DIM, 1)
        gj_ref[at, :] = jnp.concatenate(
            [
                jnp.where(low, gq[0], gq[1]) * scale,
                jnp.where(low, gk[0], gk[1]) * scale,
                gv[0] + gv[1],
                last * scale,
                gv[2],
            ],
            1,
        ).astype(bf16)
    grad_out = mm(gbt_ref[...], ho_ref[j])
    grad_in = mm(ht_ref[...], gj_ref[...])
    slot = jnp.bitwise_xor(me_ref[1], core)
    halves, blocks, rows = gw_ref.shape[1:4]
    for d in range(halves * blocks):
        r = jnp.bitwise_xor(me_ref[0], d) if halves > 1 else 0
        entry = (slot, jnp.bitwise_and(r, 1), jnp.right_shift(r, 1)) if halves > 1 else (slot, 0, 0)
        at = slice(d * rows, (d + 1) * rows)
        gw_ref[entry + (slice(None), slice(0, 512))] = grad_in[at, :512].astype(bf16)
        gw_ref[entry + (slice(None), slice(512, 640))] = (
            grad_in[at, 512:] + grad_out[at, :128]
        ).astype(bf16)
        gw_ref[entry + (slice(None), slice(640, 768))] = grad_out[at, 128:].astype(bf16)
    gh_ref[...] += mm_nt(gj_ref[...], w_ref[j, :, :JOINED])


def back_far_kernel(
    me_ref, gres_ref, ht_ref, qkv_ref, p_ref, ho_ref, w_ref,
    gw_ref, gh_ref, gb_ref, gbt_ref, gj_ref, dho_ref, *, images, tall
):
    gb_ref[...] = gres_ref[...].astype(bf16)
    gbt_ref[...] = gres_ref[...].T.astype(bf16)
    gh_ref[...] = jnp.zeros_like(gh_ref)

    def group(core, carry):
        source = (qkv_ref, p_ref, ho_ref, w_ref, 2 * core)
        back_group(
            core, source, me_ref, gb_ref, gbt_ref, ht_ref, gw_ref, gh_ref, gj_ref, dho_ref, images, tall
        )
        return carry

    lax.fori_loop(0, 2, group, 0)


def back_near_kernel(
    me_ref, gb_ref, gbt_ref, ht_ref, far_ref, qkv_a, p_a, ho_a, w_a, qkv_b, p_b, ho_b, w_b,
    gw_ref, gh_ref, gj_ref, dho_ref, *, images, tall
):
    gh_ref[...] = far_ref[...]
    for core, source in enumerate(((qkv_a, p_a, ho_a, w_a, 0), (qkv_b, p_b, ho_b, w_b, 1))):
        back_group(
            core, source, me_ref, gb_ref, gbt_ref, ht_ref, gw_ref, gh_ref, gj_ref, dho_ref, images, tall
        )


def last_kernel(
    x_ref, gres_ref, gh_ref, ex_ref, part_ref, gt_ref, small_ref, *, images, seq, tall, experts
):
    total = jnp.zeros((1, x_ref.shape[2]), f32)
    gain = ex_ref[0:1, :]
    for b in range(images):
        at = pl.ds(b * tall, seq)
        unit, inverse = unit_of(x_ref[b].astype(f32))
        grad_h = gh_ref[at, :]
        total += jnp.sum(grad_h * unit, axis=0, keepdims=True)
        scaled = grad_h * gain
        mean_grad = jnp.mean(scaled, axis=-1, keepdims=True)
        mean_proj = jnp.mean(scaled * unit, axis=-1, keepdims=True)
        gt_ref[b] = gres_ref[at, :] + inverse * (scaled - mean_grad - unit * mean_proj)
    small_ref[...] = part_ref[...]
    small_ref[experts : experts + 1, :] = total


def cost(microseconds):
    return int(microseconds * 1.1e9)


def call(kernel, outs, args, scratch=(), flops=0, name=None, scalars=1, grant=16, **static):
    spec = pl.BlockSpec(memory_space=pltpu.VMEM)
    word = pl.BlockSpec(memory_space=pltpu.SMEM)
    moved = sum(math.prod(a.shape) * a.dtype.itemsize for a in args)
    return pl.pallas_call(
        functools.partial(kernel, **static),
        out_shape=[jax.ShapeDtypeStruct(s, d) for s, d in outs],
        in_specs=[word] * scalars + [spec] * (len(args) - scalars),
        out_specs=[spec] * len(outs),
        scratch_shapes=list(scratch),
        compiler_params=pltpu.CompilerParams(vmem_limit_bytes=grant << 20),
        cost_estimate=pl.CostEstimate(flops=flops, bytes_accessed=moved, transcendentals=0),
        name=name,
    )(*args)


def make(mesh):
    dp, mp = mesh.shape["dp"], mesh.shape["mp"]

    def per_device(
        tokens, token_mask, gain_one, w_qkv, w_out, gain_two, router, w_in, w_back, cotangent
    ):
        rows, width = tokens.shape
        seq = token_mask.shape[1]
        tall = -(-seq // 16) * 16
        images = rows // seq
        experts = router.shape[1]
        d_rows, _, part = w_qkv.shape
        count = images * tall
        high = dp // 2
        heads = part // HEAD_DIM
        ready = d_rows % 16 != 0
        each = 2 * (1 << (images - 1).bit_length())
        me = lax.axis_index("dp")
        at_mp = lax.axis_index("mp")
        core = at_mp & 1
        words = jnp.stack([me, core, at_mp]).astype(jnp.int32)
        static = {"images": images, "tall": tall}
        exact = {"images": images, "seq": seq, "tall": tall}

        columns = experts + 2
        packed, extra = call(
            pack_kernel,
            [((d_rows, 4 * part), bf16), ((d_rows, columns + -columns % 128), bf16)],
            (w_qkv.transpose(1, 0, 2), w_out, gain_one[None], gain_two[None], router.T),
            flops=cost(1),
            name="pack",
            scalars=0,
            grant=4,
        )

        held, held_extra = packed, extra
        for depth, bit in enumerate(bits_of(dp)[:-1]):
            other, other_extra = lax.optimization_barrier(
                (swap(held, "dp", dp, bit), swap(held_extra, "dp", dp, bit))
            )
            held = jnp.stack([held, other], depth)
            held_extra = jnp.stack([held_extra, other_extra], depth)
        held = held.reshape((high,) + packed.shape)
        other, other_extra = lax.optimization_barrier(
            (swap_both(held, dp, mp, (1, 0), (0, 2)), swap(held_extra, "dp", dp, 1))
        )
        near = jnp.stack([held, other])
        held_extra = jnp.stack([held_extra, other_extra], len(bits_of(dp)) - 1)
        held_extra = held_extra.reshape((dp,) + extra.shape)
        far = swap_both(near, dp, mp, (0, 2), (1, 0))
        other_near = swap(near, "mp", mp, 1)
        other_far = swap(far, "mp", mp, 1)
        if ready:
            held_extra = reorder(held_extra, me).reshape(1, width, -1)

            def whole(x, of_core):
                mine = core == of_core
                first = jnp.where(mine, near, other_near)
                second = jnp.where(mine, far, other_far)
                blocks = jnp.stack([first[x], second[x]]) if of_core else (second if x else first)
                blocks = blocks.transpose(1, 0, 2, 3).reshape((dp,) + packed.shape)
                return reorder(blocks, me).reshape(width, 4 * part)

            first_weights = (whole(0, 0),)
            rest_weights = (whole(1, 0), whole(0, 1), whole(1, 1))
        else:
            first_weights = (near, other_near)
            rest_weights = (near, far, other_near, other_far)

        x3 = tokens.reshape(images, seq, width)
        cot3 = cotangent.reshape(images, seq, width)
        h_one, h_turned, ex = call(
            prep_kernel,
            [((count, width), bf16), ((width, count), bf16), ((held_extra.shape[2], width), f32)],
            (words, x3, held_extra),
            flops=cost(2),
            name="prep",
            grant=4,
            **exact,
        )

        def saved(groups):
            return [
                ((groups, width, 4 * part), bf16),
                ((groups, count, JOINED), bf16),
                ((groups, images, heads, tall, tall), bf16),
                ((groups, count, 256), bf16),
                ((count, width), f32),
            ]

        w_a, qkv_a, p_a, ho_a, branch = call(
            front_first_kernel,
            saved(1),
            (words, h_one, token_mask) + first_weights,
            flops=cost(5),
            name="front_first",
            grant=6,
            ready=ready,
            **static,
        )
        w_b, qkv_b, p_b, ho_b, branch = call(
            front_rest_kernel,
            saved(3),
            (words, h_one, token_mask, branch) + rest_weights,
            flops=cost(12),
            name="front_rest",
            grant=10,
            ready=ready,
            **static,
        )
        resid, h_two, soft, sent, sq_branch = call(
            route_kernel,
            [
                ((count, width), f32),
                ((count, width), bf16),
                ((2, images, experts, tall), f32),
                ((experts * each, width), bf16),
                ((images, 1, 128), f32),
            ],
            (words, x3, branch, cot3, token_mask, ex),
            flops=cost(2),
            name="route",
            grant=6,
            experts=experts,
            **exact,
        )
        got = sent.reshape(dp, each, width)
        got = lax.all_to_all(got, "dp", split_axis=0, concat_axis=0, tiled=True)
        got = gather_mp(got, mp).reshape(-1, width)
        everyone = got.shape[0]
        hidden, grad_pre, grad_expert, back = call(
            expert_kernel,
            [
                ((everyone, w_in.shape[2]), bf16),
                ((everyone, w_in.shape[2]), bf16),
                ((everyone, width), bf16),
                ((everyone, width), bf16),
            ],
            (got, w_in[0], w_back[0]),
            flops=cost(2),
            name="expert",
            scalars=0,
            grant=12 if dp <= 8 else 56,
            each=each,
        )
        back = back.reshape(mp, dp, each, width)
        back = scatter(back, "mp", mp, [1, 2])
        back = lax.all_to_all(back, "dp", split_axis=0, concat_axis=0, tiled=True)
        back = back.reshape(dp, 2, each // 2, width)[:, :, :images].transpose(1, 2, 0, 3)
        grad_w_back = mm_tn(hidden, grad_expert)
        grad_w_in = mm_tn(got, grad_pre)

        out_rows, grad_resid, small = call(
            mix_kernel,
            [
                ((images, seq, width), bf16),
                ((count, width), f32),
                ((experts + 3, width), f32),
            ],
            (words, resid, h_two, soft, cot3, token_mask, ex, back, sq_branch),
            flops=cost(4),
            name="mix",
            grant=6,
            experts=experts,
            groups=mp,
            **exact,
        )
        shape = (2, 1, 1, width, 4 * part) if ready else (2, 2, high, d_rows, 4 * part)
        scratch = [pltpu.VMEM((count, JOINED), bf16), pltpu.VMEM((count, 256), f32)]
        far_grads, grad_h, grad_low, grad_turned = call(
            back_far_kernel,
            [
                (shape, bf16),
                ((count, width), f32),
                ((count, width), bf16),
                ((width, count), bf16),
            ],
            (words, grad_resid, h_turned, qkv_b, p_b, ho_b, w_b),
            scratch,
            flops=cost(12),
            name="back_far",
            grant=10,
            **static,
        )
        if ready:

            def spread(grads):
                grads = grads.reshape(2, dp, d_rows, 4 * part)
                grads = jnp.stack([reorder(grads[0], me), reorder(grads[1], me)])
                return grads.reshape(2, high, 2, d_rows, 4 * part).transpose(0, 2, 1, 3, 4)

        else:

            def spread(grads):
                return grads

        far_grads = spread(far_grads)
        far_sum = plus(far_grads[0], swap(far_grads[1], "mp", mp, 1))
        far_sum, grad_low = lax.optimization_barrier((far_sum, grad_low))
        early = swap_both(far_sum[1], dp, mp, (0, 2), (1, 0))
        near_grads, grad_h = call(
            back_near_kernel,
            [(shape, bf16), ((count, width), f32)],
            (words, grad_low, grad_turned, h_turned, grad_h)
            + (qkv_a, p_a, ho_a, w_a, qkv_b, p_b, ho_b, w_b),
            scratch,
            flops=cost(12),
            name="back_near",
            grant=10,
            **static,
        )
        grad_tokens, small = call(
            last_kernel,
            [((images, seq, width), f32), ((experts + 3, width), f32)],
            (x3, grad_resid, grad_h, ex, small),
            flops=cost(3),
            name="last",
            scalars=0,
            grant=6,
            experts=experts,
            **exact,
        )
        near_grads = spread(near_grads)
        near_sum = plus(near_grads[0], swap(near_grads[1], "mp", mp, 1))
        second = jnp.where(core == 0, far_sum[0], near_sum[1])
        third = plus(jnp.where(core == 0, near_sum[1], far_sum[0]), early)
        second = swap_both(second, dp, mp, (0, 2), (1, 0))
        third = swap_both(third, dp, mp, (1, 0), (0, 2))
        summed = plus(near_sum[0], second, third)
        own, other = scatter_open(summed, "dp", dp, bits_of(high), 2)
        grad_qkv, grad_out = call(
            unpack_kernel,
            [((3, d_rows, part), f32), ((part, d_rows), f32)],
            (own, other),
            flops=cost(1),
            name="unpack",
            scalars=0,
            grant=6,
        )

        for bit in bits_of(mp)[::-1]:
            small = small + swap(small, "mp", mp, bit)
        root_squares = small[-1, : 3 * mp * images].reshape(3, mp * images)
        for bit in bits_of(dp)[::-1]:
            small = small + swap(small, "dp", dp, bit)
        small = lax.dynamic_slice_in_dim(small, me * d_rows, d_rows, 1)
        return (
            out_rows.reshape(rows, width),
            grad_tokens.reshape(rows, width),
            small[experts],
            grad_qkv.transpose(1, 0, 2),
            grad_out,
            small[experts + 1],
            small[:experts].T,
            grad_w_in[None],
            grad_w_back[None],
            root_squares,
        )

    return per_device


def solution(mesh):
    in_specs = (
        P(("dp", "mp"), None),
        P("dp", None),
        P("dp"),
        P("dp", None, "mp"),
        P("mp", "dp"),
        P("dp"),
        P("dp", None),
        P("dp", None, "mp"),
        P("dp", "mp", None),
        P(("dp", "mp"), None),
    )
    out_specs = (
        P(("dp", "mp"), None),
        P(("dp", "mp"), None),
        P("dp"),
        P("dp", None, "mp"),
        P("mp", "dp"),
        P("dp"),
        P("dp", None),
        P("dp", None, "mp"),
        P("dp", "mp", None),
        P(None, "dp"),
    )
    return jax.shard_map(
        make(mesh), mesh=mesh, in_specs=in_specs, out_specs=out_specs, check_vma=False
    )
```

time: 256 us -> 211 us (0.82)
  Pallas kernels: 77.4 us -> 52.5 us
  starting transfers between devices: 32.7 us -> 17.5 us
  local copies, waits for them, and re-layouts: 21.5 us -> 9.99 us
  waiting for transfers between devices: 85.9 us -> 92.4 us
  blocking collectives: 21.4 us -> 24.3 us
  other arithmetic: 11.3 us -> 8.53 us
    ppermute x0 -> x5, waiting for transfers between devices: none -> 23 us  [swap_both(): return lax.ppermute(array_in, ('dp', 'mp'), pairs)]
    ppermute x27 -> x20, starting transfers between devices: 32.7 us -> 12.6 us  [swap(): lax.ppermute(array_in, axis_name, [(i, i ^ bit) for i in range(size)])]
    ppermute x27 -> x20, waiting for transfers between devices: 85.9 us -> 69.5 us  [swap(): lax.ppermute(array_in, axis_name, [(i, i ^ bit) for i in range(size)])]
    pallas_call x6 -> x11, Pallas kernels: 67.7 us -> 52.5 us  [call(): pl.pallas_call(functools.partial(kernel, **static), out_shape=[jax.ShapeD...]
    pallas_call x2 -> x0, Pallas kernels: 9.62 us -> none  [the longest x1 4.81 us: per_device(): pl.pallas_call(spread_kernel, out_shape=jax.ShapeDtypeStruct((mp, dp, d_r...]
    ppermute x0 -> x5, starting transfers between devices: none -> 4.87 us  [swap_both(): return lax.ppermute(array_in, ('dp', 'mp'), pairs)]
    squeeze x11 -> x6, local copies, waits for them, and re-layouts: 5.76 us -> 1.8 us  [the longest x1 1.16 us: per_device(): near_sum = plus(near_grads[0], swap(near_grads[1], 'mp', mp, 1))]
    broadcast_in_dim x3 -> x0, local copies, waits for them, and re-layouts: 3.43 us -> none  [the longest x1 1.59 us: per_device(): column = mask[:, :, None]]
  transfers between devices with their start and end apart: 27 -> 25, of which waited for: 21 -> 18; matrix products, arithmetic and copies ran while one was open for 9% -> 5% of each run, Pallas kernels for 2% -> 4%
where the time goes in v4:
time: 211 us; the launch traced here: 210 us
  waiting for transfers between devices  92.4 us (44%)
  Pallas kernels  52.5 us (25%)
  blocking collectives  24.3 us (12%)
  starting transfers between devices  17.5 us (8%)
  local copies, waits for them, and re-layouts  9.99 us (5%)
  other arithmetic  8.53 us (4%)
  matrix products  3.84 us (2%)
    ppermute x20, waiting for transfers between devices, swap(): lax.ppermute(array_in, axis_name, [(i, i ^ bit) for i in range(size)])  69.5 us
    pallas_call x11, Pallas kernels, call(): pl.pallas_call(functools.partial(kernel, **static), out_shape=[jax.ShapeD...  52.5 us
    ppermute x5, waiting for transfers between devices, swap_both(): return lax.ppermute(array_in, ('dp', 'mp'), pairs)  23 us
    all_to_all x1, blocking collectives, per_device(): got = lax.all_to_all(got, 'dp', split_axis=0, concat_axis=0, tiled=True)  14.8 us
    ppermute x20, starting transfers between devices, swap(): lax.ppermute(array_in, axis_name, [(i, i ^ bit) for i in range(size)])  12.6 us
    all_to_all x1, blocking collectives, per_device(): back = lax.all_to_all(back, 'dp', split_axis=0, concat_axis=0, tiled=True)  9.51 us
    unnamed x52, local copies, waits for them, and re-layouts  6.8 us
    convert_element_type x5, other arithmetic, plus(): return total.astype(bf16)  5.46 us
  transfers between devices with their start and end apart: 25, of which 18 were waited for; matrix products, arithmetic and copies ran while one was open for 5% of the time, Pallas kernels for 4%

profile of v4, /device:TPU:0, one launch (start us, length us, event | category | flops | bytes accessed | tf_op | source)
XLA Modules:
  0.0 210.2 jit_solution(15494725274576990684)
XLA Ops:
  4.5 4.1 %collective-permute-start = (bf16[96,768]{1,0:T(8,128)(2,1)S(1)}, bf16[96,768]{1,0:T(8,128)(2,1)S(1)}, u32[]{:S(2)}, u32[]{:S(2)}) collective-permute-start(bf16[96,768]{1,0:T(8,128)(2,1)S(1)} %get-tuple-element.56), channel_id=1, source_target_pairs={{0,16},{4,20},{8,24},{12,28},{16,0},{20,4},{24,8},{28,12},{1,17},{... | collective-permute-start | bytes 442376 | tf_op jit(solution)/shard_map/ppermute | solution.py:24
  8.8 8.0 %collective-permute-done.1 = bf16[96,128]{1,0:T(8,128)(2,1)S(1)} collective-permute-done((bf16[96,128]{1,0:T(8,128)(2,1)S(1)}, bf16[96,128]{1,0:T(8,128)(2,1)S(1)}, u32[]{:S(2)}, u32[]{:S(2)}) %collective-permute-start.1) | collective-permute-done | bytes 24608 | tf_op jit(solution)/shard_map/ppermute | solution.py:24
  19.0 7.1 %collective-permute-done.3 = bf16[2,96,128]{2,1,0:T(8,128)(2,1)S(1)} collective-permute-done((bf16[2,96,128]{2,1,0:T(8,128)(2,1)S(1)}, bf16[2,96,128]{2,1,0:T(8,128)(2,1)S(1)}, u32[]{:S(2)}, u32[]{:S(2)}) %collective-permute-start.3) | collective-permute-done | bytes 49184 | tf_op jit(solution)/shard_map/ppermute | solution.py:24
  28.9 9.2 %collective-permute-done.5 = bf16[2,2,96,128]{3,2,0,1:T(8,128)(2,1)S(1)} collective-permute-done((bf16[2,2,96,128]{3,2,0,1:T(8,128)(2,1)S(1)}, bf16[2,2,96,128]{3,2,0,1:T(8,128)(2,1)S(1)}, u32[]{:S(2)}, u32[]{:S(2)}) %collective-permute-start.5) | collective-permute-done | bytes 98336 | tf_op jit(solution)/shard_map/ppermute | solution.py:24
  40.1 15.1 %collective-permute-done.7.refs_1_ = bf16[2,4,96,768]{3,2,1,0:T(8,128)(2,1)S(1)} collective-permute-done((bf16[2,4,96,768]{3,2,1,0:T(8,128)(2,1)S(1)}, bf16[2,4,96,768]{3,2,1,0:T(8,128)(2,1)S(1)}, u32[]{:S(2)}, u32[]{:S(2)}) %collective-permute-start.7) | collective-permute-done | bytes 1179680 | tf_op jit(solution)/shard_map/ppermute | solution.py:33
  57.4 1.6 prep.1
  59.0 4.1 %front_first.1 = (bf16[1,768,768]{2,1,0:T(8,128)(2,1)S(1)}, bf16[1,624,640]{2,1,0:T(8,128)(2,1)S(1)}, bf16[1,3,3,208,208]{4,3,2,1,0:T(8,128)(2,1)S(1)}, bf16[1,624,256]{2,1,0:T(8,128)(2,1)S(1)}, f32[624,768]{1,0:T(8,128)S(1)}) custom-call(s32[3]{0:T(128)S(1)} %pad_add_fusion.me_ref, bf16[624,768]{1,0:T(8,128)(2,1)S(1)} %get-tuple-element.62.h_ref, ...), custom_call_target="tpu_custom_call" | custom-call | flops 5500000256 | bytes 3327372 | tf_op jit(solution)/shard_map/front_first/pallas_call | solution.py:490
  63.2 12.4 %front_rest.1 = (bf16[3,768,768]{2,1,0:T(8,128)(2,1)S(1)}, bf16[3,624,640]{2,1,0:T(8,128)(2,1)S(1)}, bf16[3,3,3,208,208]{4,3,2,1,0:T(8,128)(2,1)S(1)}, bf16[3,624,256]{2,1,0:T(8,128)(2,1)S(1)}, f32[624,768]{1,0:T(8,128)S(1)}) custom-call(s32[3]{0:T(128)S(1)} %pad_add_fusion.me_ref, bf16[624,768]{1,0:T(8,128)(2,1)S(1)} %get-tuple-element.62.h_ref, ...), custom_call_target="tpu_custom_call" | custom-call | flops 13200000000 | bytes 7603596 | tf_op jit(solution)/shard_map/front_rest/pallas_call | solution.py:490
  75.6 2.7 %route.1 = (f32[624,768]{1,0:T(8,128)S(1)}, bf16[624,768]{1,0:T(8,128)(2,1)S(1)}, f32[2,3,8,208]{3,2,1,0:T(8,128)S(1)}, bf16[64,768]{1,0:T(8,128)(2,1)S(1)}, f32[3,1,128]{2,1,0:T(1,128)S(1)}) custom-call(s32[3]{0:T(128)S(1)} %pad_add_fusion.me_ref, bf16[3,200,768]{2,1,0:T(8,128)(2,1)S(1)} %bitcast.122, f32[624,768]{1,0:T(8,128)S(1)} %get-tuple-element.65.br_ref, ...), custom_call_target="tpu_custom_call" | custom-call | flops 2200000000 | bytes 4162956 | tf_op jit(solution)/shard_map/route/pallas_call | solution.py:490
  78.3 14.8 %all_to_all.10 = bf16[8,8,768]{2,1,0:T(8,128)(2,1)S(1)} all-to-all(bf16[8,8,768]{2,1,0:T(8,128)(2,1)S(1)} %bitcast.115), channel_id=1, replica_groups=mesh['dp'=8,'mp'=4] {'dp'}, dimensions={0} | all-to-all | bytes 196608 | tf_op jit(solution)/shard_map/all_to_all | solution.py:629
  93.1 4.6 %collective-permute-done.9 = bf16[1,8,8,768]{3,2,1,0:T(8,128)(2,1)S(1)} collective-permute-done((bf16[1,8,8,768]{3,2,1,0:T(8,128)(2,1)S(1)}, bf16[1,8,8,768]{3,2,1,0:T(8,128)(2,1)S(1)}, u32[]{:S(2)}, u32[]{:S(2)}) %collective-permute-start.9) | collective-permute-done | bytes 98336 | tf_op jit(solution)/shard_map/ppermute | solution.py:24
  99.3 1.7 expert.1
  103.4 4.8 %collective-permute-done.12 = bf16[1,1,8,8,768]{4,3,2,1,0:T(8,128)(2,1)S(1)} collective-permute-done((bf16[1,1,8,8,768]{4,3,2,1,0:T(8,128)(2,1)S(1)}, bf16[1,1,8,8,768]{4,3,2,1,0:T(8,128)(2,1)S(1)}, u32[]{:S(2)}, u32[]{:S(2)}) %collective-permute-start.12) | collective-permute-done | bytes 98336 | tf_op jit(solution)/shard_map/ppermute | solution.py:24
  108.2 9.5 %all_to_all.11 = bf16[8,8,768]{2,1,0:T(8,128)(2,1)S(1)} all-to-all(bf16[8,8,768]{2,1,0:T(8,128)(2,1)S(1)} %fusion.10), channel_id=1, replica_groups=mesh['dp'=8,'mp'=4] {'dp'}, dimensions={0} | all-to-all | bytes 196608 | tf_op jit(solution)/shard_map/all_to_all | solution.py:649
  117.8 4.7 %mix.1 = (bf16[3,200,768]{2,1,0:T(8,128)(2,1)}, f32[624,768]{1,0:T(8,128)S(1)}, f32[11,768]{1,0:T(8,128)S(1)}) custom-call(s32[3]{0:T(128)S(1)} %pad_add_fusion.me_ref, f32[624,768]{1,0:T(8,128)S(1)} %get-tuple-element.67.res_ref, bf16[624,768]{1,0:T(8,128)(2,1)S(1)} %get-tuple-element.68.h_ref, f32[2,3,8,208]{3,2,1,0:T(8,128)S(1)} %get-tuple-element.69.soft_ref, ...), custom_call_target="tpu_custom_call" | custom-call | flops 4400000000 | bytes 4315020 | tf_op jit(solution)/shard_map/mix/pallas_call | solution.py:490
  122.5 11.3 %back_far.1 = (bf16[2,2,4,96,768]{4,3,2,1,0:T(8,128)(2,1)S(1)}, f32[624,768]{1,0:T(8,128)S(1)}, bf16[624,768]{1,0:T(8,128)(2,1)S(1)}, bf16[768,624]{1,0:T(8,128)(2,1)S(1)}) custom-call(s32[3]{0:T(128)S(1)} %pad_add_fusion.me_ref, f32[624,768]{1,0:T(8,128)S(1)} %get-tuple-element.74.gres_ref, bf16[768,624]{1,0:T(8,128)(2,1)S(1)} %get-tuple-element.75.ht_ref, ...), custom_call_target="tpu_custom_call" | custom-call | flops 13200000000 | bytes 12105228 | tf_op jit(solution)/shard_map/back_far/pallas_call | solution.py:490
  134.0 2.8 %collective-permute-done.13 = bf16[2,4,96,768]{3,2,1,0:T(8,128)(2,1)S(1)} collective-permute-done((bf16[2,4,96,768]{3,2,1,0:T(8,128)(2,1)S(1)}, bf16[2,4,96,768]{3,2,1,0:T(8,128)(2,1)S(1)}, u32[]{:S(2)}, u32[]{:S(2)}) %collective-permute-start.13) | collective-permute-done | bytes 1179680 | tf_op jit(solution)/shard_map/ppermute | solution.py:24
  138.2 10.4 %back_near.1 = (bf16[2,2,4,96,768]{4,3,2,1,0:T(8,128)(2,1)S(1)}, f32[624,768]{1,0:T(8,128)S(1)}) custom-call(s32[3]{0:T(128)S(1)} %pad_add_fusion.me_ref, bf16[624,768]{1,0:T(8,128)(2,1)S(1)} %get-tuple-element.82.gb_ref, bf16[768,624]{1,0:T(8,128)(2,1)S(1)} %get-tuple-element.83.gbt_ref, bf16[768,624]{1,0:T(8,128)(2,1)S(1)} %get-tuple-element.75.ht_ref, ...), custom_call_target="tpu_custom_call" | custom-call | flops 13200000000 | bytes 17098764 | tf_op jit(solution)/shard_map/back_near/pallas_call | solution.py:490
  150.4 3.1 %collective-permute-done.19 = bf16[2,4,96,768]{3,2,1,0:T(8,128)(2,1)} collective-permute-done((bf16[2,4,96,768]{3,2,1,0:T(8,128)(2,1)}, bf16[2,4,96,768]{3,2,1,0:T(8,128)(2,1)}, u32[]{:S(2)}, u32[]{:S(2)}) %collective-permute-start.19) | collective-permute-done | bytes 1179680 | tf_op jit(solution)/shard_map/ppermute | solution.py:24
  153.4 1.5 fusion
  156.3 1.7 collective-permute-start.20
  158.0 7.8 %collective-permute-done.21 = bf16[4,96,768]{2,1,0:T(8,128)(2,1)S(1)} collective-permute-done((bf16[4,96,768]{2,1,0:T(8,128)(2,1)S(1)}, bf16[4,96,768]{2,1,0:T(8,128)(2,1)S(1)}, u32[]{:S(2)}, u32[]{:S(2)}) %collective-permute-start.21) | collective-permute-done | bytes 589856 | tf_op jit(solution)/shard_map/ppermute | solution.py:33
  167.2 2.7 %last.1 = (f32[3,200,768]{2,1,0:T(8,128)}, f32[11,768]{1,0:T(8,128)S(1)}) custom-call(bf16[3,200,768]{2,1,0:T(8,128)(2,1)S(1)} %bitcast.123, f32[624,768]{1,0:T(8,128)S(1)} %copy-done.15, f32[624,768]{1,0:T(8,128)S(1)} %copy-done.17, f32[128,768]{1,0:T(8,128)S(1)} %copy-done.19, f32[11,768]{1,0:T(8,128)S(1)} %copy-done.21), custom_call_target="tpu_custom_call" | custom-call | flops 3300000000 | bytes 5182464 | tf_op jit(solution)/shard_map/last/pallas_call | solution.py:490
  171.5 1.9 convolution_bitcast_fusion.1
  173.4 3.0 %collective-permute-done.15 = f32[11,768]{1,0:T(8,128)S(1)} collective-permute-done((f32[11,768]{1,0:T(8,128)S(1)}, f32[11,768]{1,0:T(8,128)S(1)}, u32[]{:S(2)}, u32[]{:S(2)}) %collective-permute-start.15) | collective-permute-done | bytes 33824 | tf_op jit(solution)/shard_map/ppermute | solution.py:24
  177.6 1.9 convolution_bitcast_fusion
  181.6 3.1 %collective-permute-done.17 = f32[11,768]{1,0:T(8,128)S(1)} collective-permute-done((f32[11,768]{1,0:T(8,128)S(1)}, f32[11,768]{1,0:T(8,128)S(1)}, u32[]{:S(2)}, u32[]{:S(2)}) %collective-permute-start.17) | collective-permute-done | bytes 33824 | tf_op jit(solution)/shard_map/ppermute | solution.py:24
  185.3 1.5 fusion.4
  186.7 2.6 %collective-permute-start.23 = (bf16[2,96,768]{2,1,0:T(8,128)(2,1)S(1)}, bf16[2,96,768]{2,1,0:T(8,128)(2,1)S(1)}, u32[]{:S(2)}, u32[]{:S(2)}) collective-permute-start(bf16[2,96,768]{2,1,0:T(8,128)(2,1)S(1)} %slice.95), channel_id=1, source_target_pairs={{0,16},{4,20},{8,24},{12,28},{16,0},{20,4},{24,8},{28,12},{1,17},{... | collective-permute-start | bytes 884744 | tf_op jit(solution)/shard_map/ppermute | solution.py:24
  189.3 1.5 collective-permute-done.18
  191.5 11.9 %collective-permute-done.23 = bf16[2,96,768]{2,1,0:T(8,128)(2,1)S(1)} collective-permute-done((bf16[2,96,768]{2,1,0:T(8,128)(2,1)S(1)}, bf16[2,96,768]{2,1,0:T(8,128)(2,1)S(1)}, u32[]{:S(2)}, u32[]{:S(2)}) %collective-permute-start.23) | collective-permute-done | bytes 294944 | tf_op jit(solution)/shard_map/ppermute | solution.py:24
  204.1 5.2 %collective-permute-done.24.other_ref = bf16[96,768]{1,0:T(8,128)(2,1)S(1)} collective-permute-done((bf16[96,768]{1,0:T(8,128)(2,1)S(1)}, bf16[96,768]{1,0:T(8,128)(2,1)S(1)}, u32[]{:S(2)}, u32[]{:S(2)}) %collective-permute-start.24) | collective-permute-done | bytes 147488 | tf_op jit(solution)/shard_map/ppermute | solution.py:24
  (121 shorter events, 30.7 us)
Async XLA Ops:
  4.5 12.2 %collective-permute-start = (bf16[96,768]{1,0:T(8,128)(2,1)S(1)}, bf16[96,768]{1,0:T(8,128)(2,1)S(1)}, u32[]{:S(2)}, u32[]{:S(2)}) collective-permute-start(bf16[96,768]{1,0:T(8,128)(2,1)S(1)} %get-tuple-element.56), channel_id=1, source_target_pairs={{0,16},{4,20},{8,24},{12,28},{16,0},{20,4},{24,8},{28,12},{1,17},{... | collective-permute-start | bytes 442376 | tf_op jit(solution)/shard_map/ppermute | solution.py:24
  8.7 8.1 %collective-permute-start.1 = (bf16[96,128]{1,0:T(8,128)(2,1)S(1)}, bf16[96,128]{1,0:T(8,128)(2,1)S(1)}, u32[]{:S(2)}, u32[]{:S(2)}) collective-permute-start(bf16[96,128]{1,0:T(8,128)(2,1)S(1)} %get-tuple-element.55), channel_id=1, source_target_pairs={{0,16},{4,20},{8,24},{12,28},{16,0},{20,4},{24,8},{28,12},{1,17},{... | collective-permute-start | bytes 73736 | tf_op jit(solution)/shard_map/ppermute | solution.py:24
  16.8 9.3 %collective-permute-start.2 = (bf16[2,96,768]{2,1,0:T(8,128)(2,1)S(1)}, bf16[2,96,768]{2,1,0:T(8,128)(2,1)S(1)}, u32[]{:S(2)}, u32[]{:S(2)}) collective-permute-start(bf16[2,96,768]{2,1,0:T(8,128)(2,1)S(1)} %get-tuple-element.105), channel_id=1, source_target_pairs={{0,8},{4,12},{8,0},{12,4},{16,24},{20,28},{24,16},{28,20},{1,9},{5... | collective-permute-start | bytes 884744 | tf_op jit(solution)/shard_map/ppermute | solution.py:24
  17.6 8.5 %collective-permute-start.3 = (bf16[2,96,128]{2,1,0:T(8,128)(2,1)S(1)}, bf16[2,96,128]{2,1,0:T(8,128)(2,1)S(1)}, u32[]{:S(2)}, u32[]{:S(2)}) collective-permute-start(bf16[2,96,128]{2,1,0:T(8,128)(2,1)S(1)} %get-tuple-element.111), channel_id=1, source_target_pairs={{0,8},{4,12},{8,0},{12,4},{16,24},{20,28},{24,16},{28,20},{1,9},{5... | collective-permute-start | bytes 147464 | tf_op jit(solution)/shard_map/ppermute | solution.py:24
  26.2 11.9 %collective-permute-start.4 = (bf16[4,96,768]{2,1,0:T(8,128)(2,1)S(1)}, bf16[4,96,768]{2,1,0:T(8,128)(2,1)S(1)}, u32[]{:S(2)}, u32[]{:S(2)}) collective-permute-start(bf16[4,96,768]{2,1,0:T(8,128)(2,1)S(1)} %bitcast.128), channel_id=1, source_target_pairs={{0,4},{1,3},{2,6},{3,1},{4,0},{5,7},{6,2},{7,5},{8,12},{9,11},{10,... | collective-permute-start | bytes 1769480 | tf_op jit(solution)/shard_map/ppermute | solution.py:33
  28.2 9.9 %collective-permute-start.5 = (bf16[2,2,96,128]{3,2,0,1:T(8,128)(2,1)S(1)}, bf16[2,2,96,128]{3,2,0,1:T(8,128)(2,1)S(1)}, u32[]{:S(2)}, u32[]{:S(2)}) collective-permute-start(bf16[2,2,96,128]{3,2,0,1:T(8,128)(2,1)S(1)} %get-tuple-element.109), channel_id=1, source_target_pairs={{0,4},{4,0},{8,12},{12,8},{16,20},{20,16},{24,28},{28,24},{1,5},{5... | collective-permute-start | bytes 294920 | tf_op jit(solution)/shard_map/ppermute | solution.py:24
  38.9 16.3 %collective-permute-start.7 = (bf16[2,4,96,768]{3,2,1,0:T(8,128)(2,1)S(1)}, bf16[2,4,96,768]{3,2,1,0:T(8,128)(2,1)S(1)}, u32[]{:S(2)}, u32[]{:S(2)}) collective-permute-start(bf16[2,4,96,768]{3,2,1,0:T(8,128)(2,1)S(1)} %pad_maximum_fusion.refs_0_), channel_id=1, source_target_pairs={{0,2},{1,5},{2,0},{3,7},{4,6},{5,1},{6,4},{7,3},{8,10},{9,13},{10,... | collective-permute-start | bytes 3538952 | tf_op jit(solution)/shard_map/ppermute | solution.py:33
  40.1 18.9 %collective-permute-start.6 = (bf16[2,4,96,768]{3,2,1,0:T(8,128)(2,1)S(1)}, bf16[2,4,96,768]{3,2,1,0:T(8,128)(2,1)S(1)}, u32[]{:S(2)}, u32[]{:S(2)}) collective-permute-start(bf16[2,4,96,768]{3,2,1,0:T(8,128)(2,1)S(1)} %pad_maximum_fusion.refs_0_), channel_id=1, source_target_pairs={{0,1},{1,0},{2,3},{3,2},{4,5},{5,4},{6,7},{7,6},{8,9},{9,8},{10,11... | collective-permute-start | bytes 3538952 | tf_op jit(solution)/shard_map/ppermute | solution.py:24
  55.2 8.0 %collective-permute-start.8 = (bf16[2,4,96,768]{3,2,1,0:T(8,128)(2,1)S(1)}, bf16[2,4,96,768]{3,2,1,0:T(8,128)(2,1)}, u32[]{:S(2)}, u32[]{:S(2)}) collective-permute-start(bf16[2,4,96,768]{3,2,1,0:T(8,128)(2,1)S(1)} %collective-permute-done.7.refs_1_), channel_id=1, source_target_pairs={{0,1},{1,0},{2,3},{3,2},{4,5},{5,4},{6,7},{7,6},{8,9},{9,8},{10,11... | collective-permute-start | bytes 3538952 | tf_op jit(solution)/shard_map/ppermute | solution.py:24
  59.0 58.8 %copy-start.18 = (f32[128,768]{1,0:T(8,128)}, f32[128,768]{1,0:T(8,128)S(1)}, u32[]{:S(2)}) copy-start(f32[128,768]{1,0:T(8,128)S(1)} %get-tuple-element.66.ex_ref) | copy-start | bytes 1179652
  63.1 12.5 %copy-start.4 = (bf16[600,768]{1,0:T(8,128)(2,1)S(1)}, bf16[600,768]{1,0:T(8,128)(2,1)}, u32[]{:S(2)}) copy-start(bf16[600,768]{1,0:T(8,128)(2,1)} %param.19) | copy-start | bytes 2764804
  63.2 12.4 %copy-start.6 = (bf16[600,768]{1,0:T(8,128)(2,1)S(1)}, bf16[600,768]{1,0:T(8,128)(2,1)}, u32[]{:S(2)}) copy-start(bf16[600,768]{1,0:T(8,128)(2,1)} %param.10) | copy-start | bytes 2764804
  75.6 23.7 %copy-start.3 = (bf16[1,768,768]{2,1,0:T(8,128)(2,1)S(1)}, bf16[1,768,768]{2,1,0:T(8,128)(2,1)}, u32[]{:S(2)}) copy-start(bf16[1,768,768]{2,1,0:T(8,128)(2,1)} %param.18) | copy-start | bytes 3538948
  78.3 21.0 %copy-start.2 = (bf16[1,768,768]{2,1,0:T(8,128)(2,1)S(1)}, bf16[1,768,768]{2,1,0:T(8,128)(2,1)}, u32[]{:S(2)}) copy-start(bf16[1,768,768]{2,1,0:T(8,128)(2,1)} %param.17) | copy-start | bytes 3538948
  93.1 4.6 %collective-permute-start.9 = (bf16[1,8,8,768]{3,2,1,0:T(8,128)(2,1)S(1)}, bf16[1,8,8,768]{3,2,1,0:T(8,128)(2,1)S(1)}, u32[]{:S(2)}, u32[]{:S(2)}) collective-permute-start(bf16[1,8,8,768]{3,2,1,0:T(8,128)(2,1)S(1)} %bitcast.131), channel_id=1, source_target_pairs={{0,2},{1,3},{2,0},{3,1},{4,6},{5,7},{6,4},{7,5},{8,10},{9,11},{10,... | collective-permute-start | bytes 294920 | tf_op jit(solution)/shard_map/ppermute | solution.py:24
  97.7 1.5 collective-permute-start.10
  101.7 1.5 collective-permute-start.11
  103.3 4.9 %collective-permute-start.12 = (bf16[1,1,8,8,768]{4,3,2,1,0:T(8,128)(2,1)S(1)}, bf16[1,1,8,8,768]{4,3,2,1,0:T(8,128)(2,1)S(1)}, u32[]{:S(2)}, u32[]{:S(2)}) collective-permute-start(bf16[1,1,8,8,768]{4,3,2,1,0:T(8,128)(2,1)S(1)} %slice_bitcast_fusion.8), channel_id=1, source_target_pairs={{0,2},{1,3},{2,0},{3,1},{4,6},{5,7},{6,4},{7,5},{8,10},{9,11},{10,... | collective-permute-start | bytes 294920 | tf_op jit(solution)/shard_map/ppermute | solution.py:24
  133.9 2.9 %collective-permute-start.13 = (bf16[2,4,96,768]{3,2,1,0:T(8,128)(2,1)S(1)}, bf16[2,4,96,768]{3,2,1,0:T(8,128)(2,1)S(1)}, u32[]{:S(2)}, u32[]{:S(2)}) collective-permute-start(bf16[2,4,96,768]{3,2,1,0:T(8,128)(2,1)S(1)} %slice_bitcast_fusion.1), channel_id=1, source_target_pairs={{0,1},{1,0},{2,3},{3,2},{4,5},{5,4},{6,7},{7,6},{8,9},{9,8},{10,11... | collective-permute-start | bytes 3538952 | tf_op jit(solution)/shard_map/ppermute | solution.py:24
  150.3 3.2 %collective-permute-start.19 = (bf16[2,4,96,768]{3,2,1,0:T(8,128)(2,1)}, bf16[2,4,96,768]{3,2,1,0:T(8,128)(2,1)}, u32[]{:S(2)}, u32[]{:S(2)}) collective-permute-start(bf16[2,4,96,768]{3,2,1,0:T(8,128)(2,1)} %slice_bitcast_fusion), channel_id=1, source_target_pairs={{0,1},{1,0},{2,3},{3,2},{4,5},{5,4},{6,7},{7,6},{8,9},{9,8},{10,11... | collective-permute-start | bytes 3538952 | tf_op jit(solution)/shard_map/ppermute | solution.py:24
  155.0 12.1 %copy-start.15 = (f32[624,768]{1,0:T(8,128)S(1)}, f32[624,768]{1,0:T(8,128)}, u32[]{:S(2)}) copy-start(f32[624,768]{1,0:T(8,128)} %copy-done.14) | copy-start | bytes 5750788
  155.0 12.1 %copy-start.17 = (f32[624,768]{1,0:T(8,128)S(1)}, f32[624,768]{1,0:T(8,128)}, u32[]{:S(2)}) copy-start(f32[624,768]{1,0:T(8,128)} %copy-done.16) | copy-start | bytes 5750788
  156.0 9.9 %collective-permute-start.21 = (bf16[4,96,768]{2,1,0:T(8,128)(2,1)S(1)}, bf16[4,96,768]{2,1,0:T(8,128)(2,1)S(1)}, u32[]{:S(2)}, u32[]{:S(2)}) collective-permute-start(bf16[4,96,768]{2,1,0:T(8,128)(2,1)S(1)} %get-tuple-element.101), channel_id=1, source_target_pairs={{0,2},{1,5},{2,0},{3,7},{4,6},{5,1},{6,4},{7,3},{8,10},{9,13},{10,... | collective-permute-start | bytes 1769480 | tf_op jit(solution)/shard_map/ppermute | solution.py:33
  156.3 29.0 %collective-permute-start.20 = (bf16[4,96,768]{2,1,0:T(8,128)(2,1)}, bf16[4,96,768]{2,1,0:T(8,128)(2,1)}, u32[]{:S(2)}, u32[]{:S(2)}) collective-permute-start(bf16[4,96,768]{2,1,0:T(8,128)(2,1)} %get-tuple-element.100), channel_id=1, source_target_pairs={{0,2},{1,5},{2,0},{3,7},{4,6},{5,1},{6,4},{7,3},{8,10},{9,13},{10,... | collective-permute-start | bytes 1769480 | tf_op jit(solution)/shard_map/ppermute | solution.py:33
  166.9 18.4 %collective-permute-start.22 = (bf16[4,96,768]{2,1,0:T(8,128)(2,1)}, bf16[4,96,768]{2,1,0:T(8,128)(2,1)}, u32[]{:S(2)}, u32[]{:S(2)}) collective-permute-start(bf16[4,96,768]{2,1,0:T(8,128)(2,1)} %fusion.2), channel_id=1, source_target_pairs={{0,4},{1,3},{2,6},{3,1},{4,0},{5,7},{6,2},{7,5},{8,12},{9,11},{10,... | collective-permute-start | bytes 1769480 | tf_op jit(solution)/shard_map/ppermute | solution.py:33
  169.8 1.2 collective-permute-start.14
  171.1 5.3 %collective-permute-start.15 = (f32[11,768]{1,0:T(8,128)S(1)}, f32[11,768]{1,0:T(8,128)S(1)}, u32[]{:S(2)}, u32[]{:S(2)}) collective-permute-start(f32[11,768]{1,0:T(8,128)S(1)} %add.45), channel_id=1, source_target_pairs={{0,2},{1,3},{2,0},{3,1},{4,6},{5,7},{6,4},{7,5},{8,10},{9,11},{10,... | collective-permute-start | bytes 101384 | tf_op jit(solution)/shard_map/ppermute | solution.py:24
  176.4 4.2 %collective-permute-start.16 = (f32[11,768]{1,0:T(8,128)S(1)}, f32[11,768]{1,0:T(8,128)S(1)}, u32[]{:S(2)}, u32[]{:S(2)}) collective-permute-start(f32[11,768]{1,0:T(8,128)S(1)} %add.46), channel_id=1, source_target_pairs={{0,4},{4,0},{8,12},{12,8},{16,20},{20,16},{24,28},{28,24},{1,5},{5... | collective-permute-start | bytes 101384 | tf_op jit(solution)/shard_map/ppermute | solution.py:24
  180.6 4.2 %collective-permute-start.17 = (f32[11,768]{1,0:T(8,128)S(1)}, f32[11,768]{1,0:T(8,128)S(1)}, u32[]{:S(2)}, u32[]{:S(2)}) collective-permute-start(f32[11,768]{1,0:T(8,128)S(1)} %add.47), channel_id=1, source_target_pairs={{0,8},{4,12},{8,0},{12,4},{16,24},{20,28},{24,16},{28,20},{1,9},{5... | collective-permute-start | bytes 101384 | tf_op jit(solution)/shard_map/ppermute | solution.py:24
  184.8 6.0 %collective-permute-start.18 = (f32[11,768]{1,0:T(8,128)S(1)}, f32[11,768]{1,0:T(8,128)S(1)}, u32[]{:S(2)}, u32[]{:S(2)}) collective-permute-start(f32[11,768]{1,0:T(8,128)S(1)} %add.48), channel_id=1, source_target_pairs={{0,16},{4,20},{8,24},{12,28},{16,0},{20,4},{24,8},{28,12},{1,17},{... | collective-permute-start | bytes 101384 | tf_op jit(solution)/shard_map/ppermute | solution.py:24
  186.7 16.7 %collective-permute-start.23 = (bf16[2,96,768]{2,1,0:T(8,128)(2,1)S(1)}, bf16[2,96,768]{2,1,0:T(8,128)(2,1)S(1)}, u32[]{:S(2)}, u32[]{:S(2)}) collective-permute-start(bf16[2,96,768]{2,1,0:T(8,128)(2,1)S(1)} %slice.95), channel_id=1, source_target_pairs={{0,16},{4,20},{8,24},{12,28},{16,0},{20,4},{24,8},{28,12},{1,17},{... | collective-permute-start | bytes 884744 | tf_op jit(solution)/shard_map/ppermute | solution.py:24
  203.5 5.8 %collective-permute-start.24 = (bf16[96,768]{1,0:T(8,128)(2,1)S(1)}, bf16[96,768]{1,0:T(8,128)(2,1)S(1)}, u32[]{:S(2)}, u32[]{:S(2)}) collective-permute-start(bf16[96,768]{1,0:T(8,128)(2,1)S(1)} %get-tuple-element.102), channel_id=1, source_target_pairs={{0,8},{4,12},{8,0},{12,4},{16,24},{20,28},{24,16},{28,20},{1,9},{5... | collective-permute-start | bytes 442376 | tf_op jit(solution)/shard_map/ppermute | solution.py:24
  (19 other events, 92.3 us)

commit v5 on v4

--- a/solution.py
+++ b/solution.py
@@ -54,13 +54,12 @@
 
 
 def scatter_open(held, axis_name, size, bits, unit):
-    held = held.reshape((-1,) + held.shape[-2:])
-    last = bits[-1]
-    for bit in bits[:-1]:
-        half = held.shape[0] // 2
-        other = swap(held[half:], axis_name, size, bit * unit)
-        held = plus(held[:half], other)
-    return held[0], swap(held[1], axis_name, size, last * unit)
+    held = held.reshape((2,) * len(bits) + held.shape[-2:])
+    for bit in bits[:0:-1]:
+        depth = held.ndim - 3
+        kept, left = (lax.index_in_dim(held, k, depth, keepdims=False) for k in (0, 1))
+        held = plus(kept, swap(left, axis_name, size, bit * unit))
+    return held[0], swap(held[1], axis_name, size, bits[0] * unit)
 
 
 def plus(*terms):
@@ -193,67 +192,67 @@
     lax.fori_loop(0, blocks, block, 0)
 
 
-def front_group(j, h_ref, mask_ref, me_ref, w_ref, qkv_ref, p_ref, ho_ref, br_ref, images, tall):
-    scale = HEAD_DIM ** (-0.5)
-    low = low_lanes(tall)
-    qkv_ref[j] = mm(h_ref[...], w_ref[j, :, :JOINED]).astype(bf16)
-    for b in range(images):
-        at = pl.ds(b * tall, tall)
-        joined = qkv_ref[j, at, :]
-        q_pair, k_pair, v_pair = joined[:, :128], joined[:, 128:256], joined[:, 256:384]
-        qk_last, v_last = joined[:, 384:512], joined[:, 512:640]
-        k_last = pltpu.roll(qk_last.astype(f32), HEAD_DIM, 1).astype(bf16)
-        none = jnp.zeros_like(q_pair)
-        bias = jnp.where(seen_row(length_of(mask_ref, me_ref, b, images), tall), 0.0, -1e30)
-        outs = []
-        for head, (q, k, v) in enumerate(
-            (
-                (jnp.where(low, q_pair, none), k_pair, v_pair),
-                (jnp.where(low, none, q_pair), k_pair, v_pair),
-                (jnp.where(low, qk_last, none), k_last, v_last),
-            )
-        ):
-            scores = mm_nt(q, k) * scale + bias
-            terms = jnp.exp(scores - jnp.max(scores, axis=-1, keepdims=True))
-            probs = (terms * (1.0 / jnp.sum(terms, axis=-1, keepdims=True))).astype(bf16)
-            p_ref[j, b, head] = probs
-            outs.append(mm(probs, v))
-        last = jnp.where(low, 0.0, pltpu.roll(outs[2], HEAD_DIM, 1))
-        pair = jnp.where(low, outs[0], outs[1])
-        ho_ref[j, at, :] = jnp.concatenate([last, pair], 1).astype(bf16)
-    br_ref[...] += mm_nt(ho_ref[j], w_ref[j, :, 512:])
-
-
-def front_first_kernel(me_ref, h_ref, mask_ref, *refs, images, tall, ready):
-    if ready:
-        (source,), outs = refs[:1], refs[1:]
-    else:
-        (near, other_near), outs = refs[:2], refs[2:]
-    w_ref, qkv_ref, p_ref, ho_ref, br_ref = outs
-    if ready:
-        w_ref[0] = source[...]
-    else:
-        fetch_group(me_ref, w_ref, 0, 0, 0, near, None, other_near, None)
-    br_ref[...] = jnp.zeros_like(br_ref)
-    front_group(0, h_ref, mask_ref, me_ref, w_ref, qkv_ref, p_ref, ho_ref, br_ref, images, tall)
-
-
-def front_rest_kernel(me_ref, h_ref, mask_ref, first_ref, *refs, images, tall, ready):
-    outs = refs[-5:]
-    w_ref, qkv_ref, p_ref, ho_ref, br_ref = outs
-    order = ((1, 0), (0, 1), (1, 1))
-    for slot, (x, core) in enumerate(order):
+def attend(q, k, v, bias):
+    scores = mm_nt(q, k) * HEAD_DIM ** (-0.5) + bias
+    terms = jnp.exp(scores - jnp.max(scores, axis=-1, keepdims=True))
+    probs = (terms * (1.0 / jnp.sum(terms, axis=-1, keepdims=True))).astype(bf16)
+    return probs, mm(probs, v)
+
+
+def bias_of(mask_ref, me_ref, b, images, tall):
+    return jnp.where(seen_row(length_of(mask_ref, me_ref, b, images), tall), 0.0, -1e30)
+
+
+def fetch_all(me_ref, w_ref, refs, ready):
+    for slot in range(w_ref.shape[0]):
         if ready:
             w_ref[slot] = refs[slot][...]
         else:
-            fetch_group(me_ref, w_ref, slot, x, core, *refs[:4])
-    br_ref[...] = first_ref[...]
+            fetch_group(me_ref, w_ref, slot, slot & 1, slot >> 1, *refs)
+
+
+def front_pair_kernel(me_ref, h_ref, mask_ref, *refs, images, tall, ready):
+    w_ref, qkv_ref, p_ref, ho_ref = refs[4:]
+    fetch_all(me_ref, w_ref, refs[:4], ready)
+    low = low_lanes(tall)
 
     def group(j, carry):
-        front_group(j, h_ref, mask_ref, me_ref, w_ref, qkv_ref, p_ref, ho_ref, br_ref, images, tall)
+        qkv_ref[j] = mm(h_ref[...], w_ref[j]).astype(bf16)
+        for b in range(images):
+            at = pl.ds(b * tall, tall)
+            joined = qkv_ref[j, at, :]
+            q, k, v = joined[:, :128], joined[:, 128:256], joined[:, 256:384]
+            none = jnp.zeros_like(q)
+            bias = bias_of(mask_ref, me_ref, b, images, tall)
+            p_ref[j, b, 0], first = attend(jnp.where(low, q, none), k, v, bias)
+            p_ref[j, b, 1], second = attend(jnp.where(low, none, q), k, v, bias)
+            ho_ref[j, at, :] = jnp.where(low, first, second).astype(bf16)
         return carry
 
-    lax.fori_loop(0, len(order), group, 0)
+    lax.fori_loop(0, w_ref.shape[0], group, 0)
+
+
+def front_last_kernel(me_ref, h_ref, mask_ref, pair_ref, *refs, images, tall, ready):
+    w_ref, qkv_ref, p_ref, ho_ref, br_ref = refs[4:]
+    fetch_all(me_ref, w_ref, refs[:4], ready)
+    low = low_lanes(tall)
+    br_ref[...] = jnp.zeros_like(br_ref)
+
+    def group(j, carry):
+        qkv_ref[j] = mm(h_ref[...], w_ref[j, :, :256]).astype(bf16)
+        for b in range(images):
+            at = pl.ds(b * tall, tall)
+            joined = qkv_ref[j, at, :]
+            qk, v = joined[:, :128], joined[:, 128:256]
+            k = pltpu.roll(qk.astype(f32), HEAD_DIM, 1).astype(bf16)
+            bias = bias_of(mask_ref, me_ref, b, images, tall)
+            p_ref[j, b], out = attend(jnp.where(low, qk, jnp.zeros_like(qk)), k, v, bias)
+            ho_ref[j, at, :] = jnp.where(low, 0.0, pltpu.roll(out, HEAD_DIM, 1)).astype(bf16)
+        heads = jnp.concatenate([ho_ref[j], pair_ref[j]], 1)
+        br_ref[...] += mm_nt(heads, w_ref[j, :, 128:])
+        return carry
+
+    lax.fori_loop(0, w_ref.shape[0], group, 0)
 
 
 def spot(rows, b, start, experts):
@@ -323,7 +322,7 @@
 
 def mix_kernel(
     me_ref, res_ref, h_ref, soft_ref, cot_ref, mask_ref, ex_ref, back_ref, sq_ref,
-    out_ref, gres_ref, small_ref, *, images, seq, tall, experts, groups
+    out_ref, gres_ref, gb_ref, gbt_ref, small_ref, *, images, seq, tall, experts, groups
 ):
     small_ref[...] = jnp.zeros_like(small_ref)
     router = ex_ref[2 : 2 + experts, :].astype(bf16)
@@ -366,40 +365,42 @@
         mean_proj = jnp.mean(scaled * unit, axis=-1, keepdims=True)
         gres_ref[at, :] = cot.astype(f32) + inverse * (scaled - mean_grad - unit * mean_proj)
     small_ref[experts + 2 : experts + 3, :] = roots
-
-
-def back_group(
-    core, source, me_ref, gb_ref, gbt_ref, ht_ref, gw_ref, gh_ref, gj_ref, dho_ref, images, tall
+    gb_ref[...] = gres_ref[...].astype(bf16)
+    gbt_ref[...] = gres_ref[...].T.astype(bf16)
+
+
+def back_kernel(
+    me_ref, gb_ref, gbt_ref, ht_ref, qkv_a, p_a, ho_a, w_a, qkv_b, p_b, ho_b, w_b, *refs,
+    images, tall, x, flip
 ):
-    qkv_ref, p_ref, ho_ref, w_ref, j = source
+    gw_ref, gh_ref, gj_ref, dho_ref = refs[-4:]
+    j = x + 2 * jnp.bitwise_xor(me_ref[1], flip)
     scale = HEAD_DIM ** (-0.5)
     low = low_lanes(tall)
-    dho_ref[...] = mm(gb_ref[...], w_ref[j, :, 512:])
+    dho_ref[...] = mm(gb_ref[...], w_b[j, :, 128:])
     for b in range(images):
         at = pl.ds(b * tall, tall)
-        joined = qkv_ref[j, at, :]
+        joined, joined_last = qkv_a[j, at, :], qkv_b[j, at, :]
         q_pair, k_pair, v_pair = joined[:, :128], joined[:, 128:256], joined[:, 256:384]
-        qk_last, v_last = joined[:, 384:512], joined[:, 512:640]
-        heads = ho_ref[j, at, :].astype(f32)
+        qk_last, v_last = joined_last[:, :128], joined_last[:, 128:256]
         grad = dho_ref[at, :].astype(bf16).astype(f32)
-        product = grad * heads
-        pair = product[:, 128:]
+        pair = grad[:, 128:] * ho_a[j, at, :].astype(f32)
+        single = grad[:, :128] * ho_b[j, at, :].astype(f32)
         dots = (
             jnp.sum(jnp.where(low, pair, 0.0), axis=1, keepdims=True),
             jnp.sum(jnp.where(low, 0.0, pair), axis=1, keepdims=True),
-            jnp.sum(product[:, :128], axis=1, keepdims=True),
+            jnp.sum(single, axis=1, keepdims=True),
         )
         grad_pair = grad[:, 128:]
         grad_last = jnp.where(low, pltpu.roll(grad[:, :128], HEAD_DIM, 1), 0.0).astype(bf16)
         gq, gk, gv = [], [], []
-        for head, (g, v, q, k) in enumerate(
+        for head, (probs, g, v, q, k) in enumerate(
             (
-                (jnp.where(low, grad_pair, 0.0).astype(bf16), v_pair, q_pair, k_pair),
-                (jnp.where(low, 0.0, grad_pair).astype(bf16), v_pair, q_pair, k_pair),
-                (grad_last, v_last, qk_last, qk_last),
+                (p_a[j, b, 0], jnp.where(low, grad_pair, 0.0).astype(bf16), v_pair, q_pair, k_pair),
+                (p_a[j, b, 1], jnp.where(low, 0.0, grad_pair).astype(bf16), v_pair, q_pair, k_pair),
+                (p_b[j, b], grad_last, v_last, qk_last, qk_last),
             )
         ):
-            probs = p_ref[j, b, head]
             grad_p = mm_nt(g, v)
             grad_s = (probs.astype(f32) * (grad_p - dots[head])).astype(bf16)
             gq.append(mm(grad_s, k))
@@ -416,49 +417,20 @@
             ],
             1,
         ).astype(bf16)
-    grad_out = mm(gbt_ref[...], ho_ref[j])
+    grad_out = mm(gbt_ref[...], jnp.concatenate([ho_b[j], ho_a[j]], 1))
     grad_in = mm(ht_ref[...], gj_ref[...])
-    slot = jnp.bitwise_xor(me_ref[1], core)
-    halves, blocks, rows = gw_ref.shape[1:4]
+    halves, blocks, rows = gw_ref.shape[:3]
     for d in range(halves * blocks):
         r = jnp.bitwise_xor(me_ref[0], d) if halves > 1 else 0
-        entry = (slot, jnp.bitwise_and(r, 1), jnp.right_shift(r, 1)) if halves > 1 else (slot, 0, 0)
+        entry = (jnp.bitwise_and(r, 1), jnp.right_shift(r, 1)) if halves > 1 else (0, 0)
         at = slice(d * rows, (d + 1) * rows)
         gw_ref[entry + (slice(None), slice(0, 512))] = grad_in[at, :512].astype(bf16)
         gw_ref[entry + (slice(None), slice(512, 640))] = (
             grad_in[at, 512:] + grad_out[at, :128]
         ).astype(bf16)
         gw_ref[entry + (slice(None), slice(640, 768))] = grad_out[at, 128:].astype(bf16)
-    gh_ref[...] += mm_nt(gj_ref[...], w_ref[j, :, :JOINED])
-
-
-def back_far_kernel(
-    me_ref, gres_ref, ht_ref, qkv_ref, p_ref, ho_ref, w_ref,
-    gw_ref, gh_ref, gb_ref, gbt_ref, gj_ref, dho_ref, *, images, tall
-):
-    gb_ref[...] = gres_ref[...].astype(bf16)
-    gbt_ref[...] = gres_ref[...].T.astype(bf16)
-    gh_ref[...] = jnp.zeros_like(gh_ref)
-
-    def group(core, carry):
-        source = (qkv_ref, p_ref, ho_ref, w_ref, 2 * core)
-        back_group(
-            core, source, me_ref, gb_ref, gbt_ref, ht_ref, gw_ref, gh_ref, gj_ref, dho_ref, images, tall
-        )
-        return carry
-
-    lax.fori_loop(0, 2, group, 0)
-
-
-def back_near_kernel(
-    me_ref, gb_ref, gbt_ref, ht_ref, far_ref, qkv_a, p_a, ho_a, w_a, qkv_b, p_b, ho_b, w_b,
-    gw_ref, gh_ref, gj_ref, dho_ref, *, images, tall
-):
-    gh_ref[...] = far_ref[...]
-    for core, source in enumerate(((qkv_a, p_a, ho_a, w_a, 0), (qkv_b, p_b, ho_b, w_b, 1))):
-        back_group(
-            core, source, me_ref, gb_ref, gbt_ref, ht_ref, gw_ref, gh_ref, gj_ref, dho_ref, images, tall
-        )
+    into = mm_nt(gj_ref[:, :384], w_a[j]) + mm_nt(gj_ref[:, 384:], w_b[j, :, :256])
+    gh_ref[...] = into + refs[0][...] if len(refs) > 4 else into
 
 
 def last_kernel(
@@ -534,39 +506,44 @@
             grant=4,
         )
 
-        held, held_extra = packed, extra
+        half = 2 * part
+        first, second, held_extra = packed[:, :half], packed[:, half:], extra
         for depth, bit in enumerate(bits_of(dp)[:-1]):
             other, other_extra = lax.optimization_barrier(
-                (swap(held, "dp", dp, bit), swap(held_extra, "dp", dp, bit))
+                (swap(first, "dp", dp, bit), swap(held_extra, "dp", dp, bit))
             )
-            held = jnp.stack([held, other], depth)
+            first = jnp.stack([first, other], depth)
             held_extra = jnp.stack([held_extra, other_extra], depth)
-        held = held.reshape((high,) + packed.shape)
+            second = jnp.stack([second, swap(second, "dp", dp, bit)], depth)
+        first = first.reshape((high, d_rows, half))
+        second = second.reshape((high, d_rows, half))
         other, other_extra = lax.optimization_barrier(
-            (swap_both(held, dp, mp, (1, 0), (0, 2)), swap(held_extra, "dp", dp, 1))
-        )
-        near = jnp.stack([held, other])
+            (swap_both(first, dp, mp, (1, 0), (0, 2)), swap(held_extra, "dp", dp, 1))
+        )
         held_extra = jnp.stack([held_extra, other_extra], len(bits_of(dp)) - 1)
         held_extra = held_extra.reshape((dp,) + extra.shape)
+        near = jnp.stack([first, other])
         far = swap_both(near, dp, mp, (0, 2), (1, 0))
-        other_near = swap(near, "mp", mp, 1)
-        other_far = swap(far, "mp", mp, 1)
+        first = (near, far, swap(near, "mp", mp, 1), swap(far, "mp", mp, 1))
+        near = jnp.stack([second, swap_both(second, dp, mp, (1, 0), (0, 2))])
+        second_near, second_far = near, swap_both(near, dp, mp, (0, 2), (1, 0))
+        second_near_other = swap(second_near, "mp", mp, 1)
+
+        def whole(x, of_core, near, far, other_near, other_far):
+            mine = core == of_core
+            low = jnp.where(mine, near, other_near)
+            high_part = jnp.where(mine, far, other_far)
+            blocks = jnp.stack([low[x], high_part[x]]) if of_core else (high_part if x else low)
+            blocks = blocks.transpose(1, 0, 2, 3).reshape((dp, d_rows, half))
+            return reorder(blocks, me).reshape(width, half)
+
+        def weights_of(parts):
+            if ready:
+                return tuple(whole(j & 1, j >> 1, *parts) for j in range(4))
+            return parts
+
         if ready:
             held_extra = reorder(held_extra, me).reshape(1, width, -1)
-
-            def whole(x, of_core):
-                mine = core == of_core
-                first = jnp.where(mine, near, other_near)
-                second = jnp.where(mine, far, other_far)
-                blocks = jnp.stack([first[x], second[x]]) if of_core else (second if x else first)
-                blocks = blocks.transpose(1, 0, 2, 3).reshape((dp,) + packed.shape)
-                return reorder(blocks, me).reshape(width, 4 * part)
-
-            first_weights = (whole(0, 0),)
-            rest_weights = (whole(1, 0), whole(0, 1), whole(1, 1))
-        else:
-            first_weights = (near, other_near)
-            rest_weights = (near, far, other_near, other_far)
 
         x3 = tokens.reshape(images, seq, width)
         cot3 = cotangent.reshape(images, seq, width)
@@ -580,31 +557,33 @@
             **exact,
         )
 
-        def saved(groups):
+        def saved(columns, probs):
             return [
-                ((groups, width, 4 * part), bf16),
-                ((groups, count, JOINED), bf16),
-                ((groups, images, heads, tall, tall), bf16),
-                ((groups, count, 256), bf16),
-                ((count, width), f32),
+                ((mp, width, half), bf16),
+                ((mp, count, columns), bf16),
+                ((mp, images) + probs + (tall, tall), bf16),
+                ((mp, count, 128), bf16),
             ]
 
-        w_a, qkv_a, p_a, ho_a, branch = call(
-            front_first_kernel,
-            saved(1),
-            (words, h_one, token_mask) + first_weights,
-            flops=cost(5),
-            name="front_first",
-            grant=6,
+        pair = call(
+            front_pair_kernel,
+            saved(384, (2,)),
+            (words, h_one, token_mask) + weights_of(first),
+            flops=cost(10),
+            name="front_pair",
+            grant=10,
             ready=ready,
             **static,
         )
+        w_a, qkv_a, p_a, ho_a = pair
+        second_far, ho_a = lax.optimization_barrier((second_far, ho_a))
+        second = (second_near, second_far, second_near_other, swap(second_far, "mp", mp, 1))
         w_b, qkv_b, p_b, ho_b, branch = call(
-            front_rest_kernel,
-            saved(3),
-            (words, h_one, token_mask, branch) + rest_weights,
-            flops=cost(12),
-            name="front_rest",
+            front_last_kernel,
+            saved(256, ()) + [((count, width), f32)],
+            (words, h_one, token_mask, ho_a) + weights_of(second),
+            flops=cost(7),
+            name="front_last",
             grant=10,
             ready=ready,
             **static,
@@ -651,65 +630,56 @@
         grad_w_back = mm_tn(hidden, grad_expert)
         grad_w_in = mm_tn(got, grad_pre)
 
-        out_rows, grad_resid, small = call(
+        out_rows, grad_resid, grad_low, grad_turned, small = call(
             mix_kernel,
             [
                 ((images, seq, width), bf16),
                 ((count, width), f32),
+                ((count, width), bf16),
+                ((width, count), bf16),
                 ((experts + 3, width), f32),
             ],
             (words, resid, h_two, soft, cot3, token_mask, ex, back, sq_branch),
-            flops=cost(4),
+            flops=cost(5),
             name="mix",
-            grant=6,
+            grant=8,
             experts=experts,
             groups=mp,
             **exact,
         )
-        shape = (2, 1, 1, width, 4 * part) if ready else (2, 2, high, d_rows, 4 * part)
-        scratch = [pltpu.VMEM((count, JOINED), bf16), pltpu.VMEM((count, 256), f32)]
-        far_grads, grad_h, grad_low, grad_turned = call(
-            back_far_kernel,
-            [
-                (shape, bf16),
-                ((count, width), f32),
-                ((count, width), bf16),
-                ((width, count), bf16),
-            ],
-            (words, grad_resid, h_turned, qkv_b, p_b, ho_b, w_b),
-            scratch,
-            flops=cost(12),
-            name="back_far",
-            grant=10,
-            **static,
-        )
-        if ready:
-
-            def spread(grads):
-                grads = grads.reshape(2, dp, d_rows, 4 * part)
-                grads = jnp.stack([reorder(grads[0], me), reorder(grads[1], me)])
-                return grads.reshape(2, high, 2, d_rows, 4 * part).transpose(0, 2, 1, 3, 4)
-
-        else:
-
-            def spread(grads):
-                return grads
-
-        far_grads = spread(far_grads)
-        far_sum = plus(far_grads[0], swap(far_grads[1], "mp", mp, 1))
-        far_sum, grad_low = lax.optimization_barrier((far_sum, grad_low))
+        shape = (1, 1, width, 4 * part) if ready else (2, high, d_rows, 4 * part)
+
+        def back_of(x, flip, *so_far):
+            grads, total = call(
+                back_kernel,
+                [(shape, bf16), ((count, width), f32)],
+                (words, grad_low, grad_turned, h_turned)
+                + (qkv_a, p_a, ho_a, w_a, qkv_b, p_b, ho_b, w_b)
+                + so_far,
+                [pltpu.VMEM((count, JOINED), bf16), pltpu.VMEM((count, 256), f32)],
+                flops=cost(6),
+                name="back",
+                grant=10,
+                x=x,
+                flip=flip,
+                **static,
+            )
+            if ready:
+                grads = reorder(grads.reshape(dp, d_rows, 4 * part), me)
+                grads = grads.reshape(high, 2, d_rows, 4 * part).transpose(1, 0, 2, 3)
+            return grads, total
+
+        sent_grads, grad_h = back_of(1, 1)
+        other = swap(sent_grads, "mp", mp, 1)
+        kept_grads, grad_h = back_of(1, 0, grad_h)
+        far_sum = plus(kept_grads, other)
+        far_sum, grad_h = lax.optimization_barrier((far_sum, grad_h))
         early = swap_both(far_sum[1], dp, mp, (0, 2), (1, 0))
-        near_grads, grad_h = call(
-            back_near_kernel,
-            [(shape, bf16), ((count, width), f32)],
-            (words, grad_low, grad_turned, h_turned, grad_h)
-            + (qkv_a, p_a, ho_a, w_a, qkv_b, p_b, ho_b, w_b),
-            scratch,
-            flops=cost(12),
-            name="back_near",
-            grant=10,
-            **static,
-        )
+        sent_grads, grad_h = back_of(0, 1, grad_h)
+        early, grad_h = lax.optimization_barrier((early, grad_h))
+        other = swap(sent_grads, "mp", mp, 1)
+        kept_grads, grad_h = back_of(0, 0, grad_h)
+        near_sum = plus(kept_grads, other)
         grad_tokens, small = call(
             last_kernel,
             [((images, seq, width), f32), ((experts + 3, width), f32)],
@@ -721,8 +691,6 @@
             experts=experts,
             **exact,
         )
-        near_grads = spread(near_grads)
-        near_sum = plus(near_grads[0], swap(near_grads[1], "mp", mp, 1))
         second = jnp.where(core == 0, far_sum[0], near_sum[1])
         third = plus(jnp.where(core == 0, near_sum[1], far_sum[0]), early)
         second = swap_both(second, dp, mp, (0, 2), (1, 0))

time: 211 us -> 204 us (0.967)
  waiting for transfers between devices: 92.4 us -> 63.6 us
  local copies, waits for them, and re-layouts: 9.99 us -> 24.2 us
  starting transfers between devices: 17.5 us -> 24.9 us
  Pallas kernels: 52.5 us -> 54.7 us
    ppermute x5 -> x7, waiting for transfers between devices: 23 us -> 7.89 us  [swap_both(): return lax.ppermute(array_in, ('dp', 'mp'), pairs)]
    ppermute x20 -> x24, waiting for transfers between devices: 69.5 us -> 55.7 us  [swap(): lax.ppermute(array_in, axis_name, [(i, i ^ bit) for i in range(size)])]
    unnamed x52 -> x82, local copies, waits for them, and re-layouts: 6.8 us -> 20.5 us
    ppermute x20 -> x24, starting transfers between devices: 12.6 us -> 18.3 us  [swap(): lax.ppermute(array_in, axis_name, [(i, i ^ bit) for i in range(size)])]
    pallas_call x11 -> x13, Pallas kernels: 52.5 us -> 54.7 us  [call(): pl.pallas_call(functools.partial(kernel, **static), out_shape=[jax.ShapeD...]
    ppermute x5 -> x7, starting transfers between devices: 4.87 us -> 6.51 us  [swap_both(): return lax.ppermute(array_in, ('dp', 'mp'), pairs)]
  transfers between devices with their start and end apart: 25 -> 31, of which waited for: 18 -> 19; matrix products, arithmetic and copies ran while one was open for 5% -> 5% of each run, Pallas kernels for 4% -> 14%
where the time goes in v5:
time: 204 us; the launch traced here: 203 us
  waiting for transfers between devices  63.6 us (31%)
  Pallas kernels  54.7 us (27%)
  starting transfers between devices  24.9 us (12%)
  local copies, waits for them, and re-layouts  24.2 us (12%)
  blocking collectives  23.1 us (11%)
  other arithmetic  7.7 us (4%)
  matrix products  3.84 us (2%)
    ppermute x24, waiting for transfers between devices, swap(): lax.ppermute(array_in, axis_name, [(i, i ^ bit) for i in range(size)])  55.7 us
    pallas_call x13, Pallas kernels, call(): pl.pallas_call(functools.partial(kernel, **static), out_shape=[jax.ShapeD...  54.7 us
    unnamed x82, local copies, waits for them, and re-layouts  20.5 us
    ppermute x24, starting transfers between devices, swap(): lax.ppermute(array_in, axis_name, [(i, i ^ bit) for i in range(size)])  18.3 us
    all_to_all x1, blocking collectives, per_device(): got = lax.all_to_all(got, 'dp', split_axis=0, concat_axis=0, tiled=True)  13.6 us
    all_to_all x1, blocking collectives, per_device(): back = lax.all_to_all(back, 'dp', split_axis=0, concat_axis=0, tiled=True)  9.51 us
    ppermute x7, waiting for transfers between devices, swap_both(): return lax.ppermute(array_in, ('dp', 'mp'), pairs)  7.89 us
    ppermute x7, starting transfers between devices, swap_both(): return lax.ppermute(array_in, ('dp', 'mp'), pairs)  6.51 us
  transfers between devices with their start and end apart: 31, of which 19 were waited for; matrix products, arithmetic and copies ran while one was open for 5% of the time, Pallas kernels for 14%

profile of v5, /device:TPU:0, one launch (start us, length us, event | category | flops | bytes accessed | tf_op | source)
XLA Modules:
  0.0 203.2 jit_solution(10850557192966913170)
XLA Ops:
  4.6 4.1 %collective-permute-start = (bf16[96,384]{1,0:T(8,128)(2,1)S(1)}, bf16[96,384]{1,0:T(8,128)(2,1)S(1)}, u32[]{:S(2)}, u32[]{:S(2)}) collective-permute-start(bf16[96,384]{1,0:T(8,128)(2,1)S(1)} %get-tuple-element.123), channel_id=1, source_target_pairs={{0,16},{4,20},{8,24},{12,28},{16,0},{20,4},{24,8},{28,12},{1,17},{... | collective-permute-start | bytes 221192 | tf_op jit(solution)/shard_map/ppermute | solution.py:24
  8.8 4.6 %collective-permute-done.1 = bf16[96,128]{1,0:T(8,128)(2,1)S(1)} collective-permute-done((bf16[96,128]{1,0:T(8,128)(2,1)S(1)}, bf16[96,128]{1,0:T(8,128)(2,1)S(1)}, u32[]{:S(2)}, u32[]{:S(2)}) %collective-permute-start.1) | collective-permute-done | bytes 24608 | tf_op jit(solution)/shard_map/ppermute | solution.py:24
  15.6 4.5 %collective-permute-done.3 = bf16[2,96,128]{2,1,0:T(8,128)(2,1)S(1)} collective-permute-done((bf16[2,96,128]{2,1,0:T(8,128)(2,1)S(1)}, bf16[2,96,128]{2,1,0:T(8,128)(2,1)S(1)}, u32[]{:S(2)}, u32[]{:S(2)}) %collective-permute-start.3) | collective-permute-done | bytes 49184 | tf_op jit(solution)/shard_map/ppermute | solution.py:24
  22.4 2.8 %collective-permute-start.6 = (bf16[96,384]{1,0:T(8,128)(2,1)S(1)}, bf16[96,384]{1,0:T(8,128)(2,1)S(1)}, u32[]{:S(2)}, u32[]{:S(2)}) collective-permute-start(bf16[96,384]{1,0:T(8,128)(2,1)S(1)} %get-tuple-element.122), channel_id=1, source_target_pairs={{0,16},{4,20},{8,24},{12,28},{16,0},{20,4},{24,8},{28,12},{1,17},{... | collective-permute-start | bytes 221192 | tf_op jit(solution)/shard_map/ppermute | solution.py:24
  25.2 3.6 %collective-permute-done.5 = bf16[2,2,96,128]{3,2,0,1:T(8,128)(2,1)S(1)} collective-permute-done((bf16[2,2,96,128]{3,2,0,1:T(8,128)(2,1)S(1)}, bf16[2,2,96,128]{3,2,0,1:T(8,128)(2,1)S(1)}, u32[]{:S(2)}, u32[]{:S(2)}) %collective-permute-start.5) | collective-permute-done | bytes 98336 | tf_op jit(solution)/shard_map/ppermute | solution.py:24
  31.6 3.8 %collective-permute-done.7 = bf16[2,96,384]{2,1,0:T(8,128)(2,1)S(1)} collective-permute-done((bf16[2,96,384]{2,1,0:T(8,128)(2,1)S(1)}, bf16[2,96,384]{2,1,0:T(8,128)(2,1)S(1)}, u32[]{:S(2)}, u32[]{:S(2)}) %collective-permute-start.7) | collective-permute-done | bytes 147488 | tf_op jit(solution)/shard_map/ppermute | solution.py:24
  37.7 4.3 %collective-permute-done.10.refs_1_ = bf16[2,4,96,384]{3,2,1,0:T(8,128)(2,1)S(1)} collective-permute-done((bf16[2,4,96,384]{3,2,1,0:T(8,128)(2,1)S(1)}, bf16[2,4,96,384]{3,2,1,0:T(8,128)(2,1)S(1)}, u32[]{:S(2)}, u32[]{:S(2)}) %collective-permute-start.10) | collective-permute-done | bytes 589856 | tf_op jit(solution)/shard_map/ppermute | solution.py:33
  46.9 7.8 %front_pair.1 = (bf16[4,768,384]{2,1,0:T(8,128)(2,1)S(1)}, bf16[4,624,384]{2,1,0:T(8,128)(2,1)S(1)}, bf16[4,3,2,208,208]{4,3,2,1,0:T(8,128)(2,1)S(1)}, bf16[4,624,128]{2,1,0:T(8,128)(2,1)S(1)}) custom-call(s32[3]{0:T(128)S(1)} %pad_add_fusion.me_ref, bf16[624,768]{1,0:T(8,128)(2,1)S(1)} %get-tuple-element.69.h_ref, s32[12,200]{1,0:T(8,128)S(1)} %copy-done.7, ...), custom_call_target="tpu_custom_call" | custom-call | flops 11000000512 | bytes 3327372 | tf_op jit(solution)/shard_map/front_pair/pallas_call | solution.py:462
  57.0 10.9 %front_last.1 = (bf16[4,768,384]{2,1,0:T(8,128)(2,1)S(1)}, bf16[4,624,256]{2,1,0:T(8,128)(2,1)S(1)}, bf16[4,3,208,208]{3,2,1,0:T(8,128)(2,1)S(1)}, bf16[4,624,128]{2,1,0:T(8,128)(2,1)S(1)}, f32[624,768]{1,0:T(8,128)S(1)}) custom-call(s32[3]{0:T(128)S(1)} %pad_add_fusion.me_ref, bf16[624,768]{1,0:T(8,128)(2,1)S(1)} %get-tuple-element.69.h_ref, ...), custom_call_target="tpu_custom_call" | custom-call | flops 7699999744 | bytes 3966348 | tf_op jit(solution)/shard_map/front_last/pallas_call | solution.py:462
  67.9 2.7 %route.1 = (f32[624,768]{1,0:T(8,128)S(1)}, bf16[624,768]{1,0:T(8,128)(2,1)S(1)}, f32[2,3,8,208]{3,2,1,0:T(8,128)S(1)}, bf16[64,768]{1,0:T(8,128)(2,1)S(1)}, f32[3,1,128]{2,1,0:T(1,128)S(1)}) custom-call(s32[3]{0:T(128)S(1)} %pad_add_fusion.me_ref, bf16[3,200,768]{2,1,0:T(8,128)(2,1)S(1)} %bitcast.133, f32[624,768]{1,0:T(8,128)S(1)} %get-tuple-element.74.br_ref, ...), custom_call_target="tpu_custom_call" | custom-call | flops 2200000000 | bytes 4162956 | tf_op jit(solution)/shard_map/route/pallas_call | solution.py:462
  70.6 13.6 %all_to_all.10 = bf16[8,8,768]{2,1,0:T(8,128)(2,1)S(1)} all-to-all(bf16[8,8,768]{2,1,0:T(8,128)(2,1)S(1)} %bitcast.126), channel_id=1, replica_groups=mesh['dp'=8,'mp'=4] {'dp'}, dimensions={0} | all-to-all | bytes 196608 | tf_op jit(solution)/shard_map/all_to_all | solution.py:608
  84.6 4.2 %collective-permute-done.15 = bf16[1,8,8,768]{3,2,1,0:T(8,128)(2,1)S(1)} collective-permute-done((bf16[1,8,8,768]{3,2,1,0:T(8,128)(2,1)S(1)}, bf16[1,8,8,768]{3,2,1,0:T(8,128)(2,1)S(1)}, u32[]{:S(2)}, u32[]{:S(2)}) %collective-permute-start.15) | collective-permute-done | bytes 98336 | tf_op jit(solution)/shard_map/ppermute | solution.py:24
  90.4 1.7 expert.1
  94.2 4.4 %collective-permute-done.18 = bf16[1,1,8,8,768]{4,3,2,1,0:T(8,128)(2,1)S(1)} collective-permute-done((bf16[1,1,8,8,768]{4,3,2,1,0:T(8,128)(2,1)S(1)}, bf16[1,1,8,8,768]{4,3,2,1,0:T(8,128)(2,1)S(1)}, u32[]{:S(2)}, u32[]{:S(2)}) %collective-permute-start.18) | collective-permute-done | bytes 98336 | tf_op jit(solution)/shard_map/ppermute | solution.py:24
  98.7 9.5 %all_to_all.11 = bf16[8,8,768]{2,1,0:T(8,128)(2,1)S(1)} all-to-all(bf16[8,8,768]{2,1,0:T(8,128)(2,1)S(1)} %fusion.9), channel_id=1, replica_groups=mesh['dp'=8,'mp'=4] {'dp'}, dimensions={0} | all-to-all | bytes 196608 | tf_op jit(solution)/shard_map/all_to_all | solution.py:628
  108.2 3.9 %mix.1 = (bf16[3,200,768]{2,1,0:T(8,128)(2,1)}, f32[624,768]{1,0:T(8,128)S(1)}, bf16[624,768]{1,0:T(8,128)(2,1)S(1)}, bf16[768,624]{1,0:T(8,128)(2,1)S(1)}, f32[11,768]{1,0:T(8,128)S(1)}) custom-call(s32[3]{0:T(128)S(1)} %pad_add_fusion.me_ref, f32[624,768]{1,0:T(8,128)S(1)} %get-tuple-element.76.res_ref, bf16[624,768]{1,0:T(8,128)(2,1)S(1)} %get-tuple-element.77.h_ref, ...), custom_call_target="tpu_custom_call" | custom-call | flops 5500000256 | bytes 4315020 | tf_op jit(solution)/shard_map/mix/pallas_call | solution.py:462
  112.2 5.6 %back.4 = (bf16[2,4,96,768]{3,2,1,0:T(8,128)(2,1)S(1)}, f32[624,768]{1,0:T(8,128)S(1)}) custom-call(s32[3]{0:T(128)S(1)} %pad_add_fusion.me_ref, bf16[624,768]{1,0:T(8,128)(2,1)S(1)} %get-tuple-element.84.gb_ref, bf16[768,624]{1,0:T(8,128)(2,1)S(1)} %get-tuple-element.85.gbt_ref, bf16[768,624]{1,0:T(8,128)(2,1)S(1)} %get-tuple-element.86.ht_ref, ...), custom_call_target="tpu_custom_call" | custom-call | flops 6600000000 | bytes 15181836 | tf_op jit(solution)/shard_map/back/pallas_call | solution.py:462
  117.8 5.6 %back.5 = (bf16[2,4,96,768]{3,2,1,0:T(8,128)(2,1)S(1)}, f32[624,768]{1,0:T(8,128)S(1)}) custom-call(s32[3]{0:T(128)S(1)} %pad_add_fusion.me_ref, bf16[624,768]{1,0:T(8,128)(2,1)S(1)} %get-tuple-element.84.gb_ref, bf16[768,624]{1,0:T(8,128)(2,1)S(1)} %get-tuple-element.85.gbt_ref, bf16[768,624]{1,0:T(8,128)(2,1)S(1)} %get-tuple-element.86.ht_ref, ...), custom_call_target="tpu_custom_call" | custom-call | flops 6600000000 | bytes 17098764 | tf_op jit(solution)/shard_map/back/pallas_call | solution.py:462
  125.1 5.8 %back.6 = (bf16[2,4,96,768]{3,2,1,0:T(8,128)(2,1)S(1)}, f32[624,768]{1,0:T(8,128)S(1)}) custom-call(s32[3]{0:T(128)S(1)} %pad_add_fusion.me_ref, bf16[624,768]{1,0:T(8,128)(2,1)S(1)} %get-tuple-element.84.gb_ref, bf16[768,624]{1,0:T(8,128)(2,1)S(1)} %get-tuple-element.85.gbt_ref, bf16[768,624]{1,0:T(8,128)(2,1)S(1)} %get-tuple-element.86.ht_ref, ...), custom_call_target="tpu_custom_call" | custom-call | flops 6600000000 | bytes 17098764 | tf_op jit(solution)/shard_map/back/pallas_call | solution.py:462
  132.4 2.4 %collective-permute-done.20 = bf16[4,96,768]{2,1,0:T(8,128)(2,1)} collective-permute-done((bf16[4,96,768]{2,1,0:T(8,128)(2,1)}, bf16[4,96,768]{2,1,0:T(8,128)(2,1)}, u32[]{:S(2)}, u32[]{:S(2)}) %collective-permute-start.20) | collective-permute-done | bytes 589856 | tf_op jit(solution)/shard_map/ppermute | solution.py:33
  134.9 1.7 copy-done.12
  150.3 5.6 %back.7 = (bf16[2,4,96,768]{3,2,1,0:T(8,128)(2,1)S(1)}, f32[624,768]{1,0:T(8,128)S(1)}) custom-call(s32[3]{0:T(128)S(1)} %pad_add_fusion.me_ref, bf16[624,768]{1,0:T(8,128)(2,1)S(1)} %copy-done.34, bf16[768,624]{1,0:T(8,128)(2,1)S(1)} %copy-done.32, bf16[768,624]{1,0:T(8,128)(2,1)S(1)} %copy-done.30, bf16[4,624,384]{2,1,0:T(8,128)(2,1)S(1)} %copy-done.18, ...), custom_call_target="tpu_custom_call" | custom-call | flops 6600000000 | bytes 17098764 | tf_op jit(solution)/shard_map/back/pallas_call | solution.py:462
  160.9 2.7 %last.1 = (f32[3,200,768]{2,1,0:T(8,128)}, f32[11,768]{1,0:T(8,128)S(1)}) custom-call(bf16[3,200,768]{2,1,0:T(8,128)(2,1)S(1)} %bitcast.134, f32[624,768]{1,0:T(8,128)S(1)} %copy-done.22, f32[624,768]{1,0:T(8,128)S(1)} %get-tuple-element.102.gh_ref, f32[128,768]{1,0:T(8,128)S(1)} %copy-done.28, f32[11,768]{1,0:T(8,128)S(1)} %get-tuple-element.103.part_ref), custom_call_target="tpu_custom_call" | custom-call | flops 3300000000 | bytes 5182464 | tf_op jit(solution)/shard_map/last/pallas_call | solution.py:462
  166.4 1.9 convolution_bitcast_fusion.1
  168.4 7.7 %collective-permute-done.22 = f32[11,768]{1,0:T(8,128)S(1)} collective-permute-done((f32[11,768]{1,0:T(8,128)S(1)}, f32[11,768]{1,0:T(8,128)S(1)}, u32[]{:S(2)}, u32[]{:S(2)}) %collective-permute-start.22) | collective-permute-done | bytes 33824 | tf_op jit(solution)/shard_map/ppermute | solution.py:24
  176.5 1.9 convolution_bitcast_fusion
  178.4 1.9 collective-permute-done.23
  181.0 3.7 %collective-permute-done.24 = f32[11,768]{1,0:T(8,128)S(1)} collective-permute-done((f32[11,768]{1,0:T(8,128)S(1)}, f32[11,768]{1,0:T(8,128)S(1)}, u32[]{:S(2)}, u32[]{:S(2)}) %collective-permute-start.24) | collective-permute-done | bytes 33824 | tf_op jit(solution)/shard_map/ppermute | solution.py:24
  187.7 2.3 %collective-permute-done.25 = f32[11,768]{1,0:T(8,128)S(1)} collective-permute-done((f32[11,768]{1,0:T(8,128)S(1)}, f32[11,768]{1,0:T(8,128)S(1)}, u32[]{:S(2)}, u32[]{:S(2)}) %collective-permute-start.25) | collective-permute-done | bytes 33824 | tf_op jit(solution)/shard_map/ppermute | solution.py:24
  190.7 4.6 %collective-permute-done.29 = bf16[2,96,768]{2,1,0:T(8,128)(2,1)S(1)} collective-permute-done((bf16[2,96,768]{2,1,0:T(8,128)(2,1)S(1)}, bf16[2,96,768]{2,1,0:T(8,128)(2,1)S(1)}, u32[]{:S(2)}, u32[]{:S(2)}) %collective-permute-start.29) | collective-permute-done | bytes 294944 | tf_op jit(solution)/shard_map/ppermute | solution.py:24
  195.4 1.8 collective-permute-start.30
  197.7 4.7 %collective-permute-done.30.other_ref = bf16[96,768]{1,0:T(8,128)(2,1)S(1)} collective-permute-done((bf16[96,768]{1,0:T(8,128)(2,1)S(1)}, bf16[96,768]{1,0:T(8,128)(2,1)S(1)}, u32[]{:S(2)}, u32[]{:S(2)}) %collective-permute-start.30) | collective-permute-done | bytes 147488 | tf_op jit(solution)/shard_map/ppermute | solution.py:24
  (169 shorter events, 55.7 us)
Async XLA Ops:
  4.6 8.9 %collective-permute-start = (bf16[96,384]{1,0:T(8,128)(2,1)S(1)}, bf16[96,384]{1,0:T(8,128)(2,1)S(1)}, u32[]{:S(2)}, u32[]{:S(2)}) collective-permute-start(bf16[96,384]{1,0:T(8,128)(2,1)S(1)} %get-tuple-element.123), channel_id=1, source_target_pairs={{0,16},{4,20},{8,24},{12,28},{16,0},{20,4},{24,8},{28,12},{1,17},{... | collective-permute-start | bytes 221192 | tf_op jit(solution)/shard_map/ppermute | solution.py:24
  8.7 4.7 %collective-permute-start.1 = (bf16[96,128]{1,0:T(8,128)(2,1)S(1)}, bf16[96,128]{1,0:T(8,128)(2,1)S(1)}, u32[]{:S(2)}, u32[]{:S(2)}) collective-permute-start(bf16[96,128]{1,0:T(8,128)(2,1)S(1)} %get-tuple-element.62), channel_id=1, source_target_pairs={{0,16},{4,20},{8,24},{12,28},{16,0},{20,4},{24,8},{28,12},{1,17},{... | collective-permute-start | bytes 73736 | tf_op jit(solution)/shard_map/ppermute | solution.py:24
  13.5 6.7 %collective-permute-start.2 = (bf16[2,96,384]{2,1,0:T(8,128)(2,1)S(1)}, bf16[2,96,384]{2,1,0:T(8,128)(2,1)S(1)}, u32[]{:S(2)}, u32[]{:S(2)}) collective-permute-start(bf16[2,96,384]{2,1,0:T(8,128)(2,1)S(1)} %get-tuple-element.125), channel_id=1, source_target_pairs={{0,8},{4,12},{8,0},{12,4},{16,24},{20,28},{24,16},{28,20},{1,9},{5... | collective-permute-start | bytes 442376 | tf_op jit(solution)/shard_map/ppermute | solution.py:24
  15.1 5.0 %collective-permute-start.3 = (bf16[2,96,128]{2,1,0:T(8,128)(2,1)S(1)}, bf16[2,96,128]{2,1,0:T(8,128)(2,1)S(1)}, u32[]{:S(2)}, u32[]{:S(2)}) collective-permute-start(bf16[2,96,128]{2,1,0:T(8,128)(2,1)S(1)} %get-tuple-element.129), channel_id=1, source_target_pairs={{0,8},{4,12},{8,0},{12,4},{16,24},{20,28},{24,16},{28,20},{1,9},{5... | collective-permute-start | bytes 147464 | tf_op jit(solution)/shard_map/ppermute | solution.py:24
  20.2 8.5 %collective-permute-start.4 = (bf16[4,96,384]{2,1,0:T(8,128)(2,1)S(1)}, bf16[4,96,384]{2,1,0:T(8,128)(2,1)S(1)}, u32[]{:S(2)}, u32[]{:S(2)}) collective-permute-start(bf16[4,96,384]{2,1,0:T(8,128)(2,1)S(1)} %bitcast.141), channel_id=1, source_target_pairs={{0,4},{1,3},{2,6},{3,1},{4,0},{5,7},{6,2},{7,5},{8,12},{9,11},{10,... | collective-permute-start | bytes 884744 | tf_op jit(solution)/shard_map/ppermute | solution.py:33
  21.9 6.9 %collective-permute-start.5 = (bf16[2,2,96,128]{3,2,0,1:T(8,128)(2,1)S(1)}, bf16[2,2,96,128]{3,2,0,1:T(8,128)(2,1)S(1)}, u32[]{:S(2)}, u32[]{:S(2)}) collective-permute-start(bf16[2,2,96,128]{3,2,0,1:T(8,128)(2,1)S(1)} %get-tuple-element.127), channel_id=1, source_target_pairs={{0,4},{4,0},{8,12},{12,8},{16,20},{20,16},{24,28},{28,24},{1,5},{5... | collective-permute-start | bytes 294920 | tf_op jit(solution)/shard_map/ppermute | solution.py:24
  22.4 7.7 %collective-permute-start.6 = (bf16[96,384]{1,0:T(8,128)(2,1)S(1)}, bf16[96,384]{1,0:T(8,128)(2,1)S(1)}, u32[]{:S(2)}, u32[]{:S(2)}) collective-permute-start(bf16[96,384]{1,0:T(8,128)(2,1)S(1)} %get-tuple-element.122), channel_id=1, source_target_pairs={{0,16},{4,20},{8,24},{12,28},{16,0},{20,4},{24,8},{28,12},{1,17},{... | collective-permute-start | bytes 221192 | tf_op jit(solution)/shard_map/ppermute | solution.py:24
  28.9 13.1 %collective-permute-start.10 = (bf16[2,4,96,384]{3,2,1,0:T(8,128)(2,1)S(1)}, bf16[2,4,96,384]{3,2,1,0:T(8,128)(2,1)S(1)}, u32[]{:S(2)}, u32[]{:S(2)}) collective-permute-start(bf16[2,4,96,384]{3,2,1,0:T(8,128)(2,1)S(1)} %pad_maximum_fusion.1.refs_0_), channel_id=1, source_target_pairs={{0,2},{1,5},{2,0},{3,7},{4,6},{5,1},{6,4},{7,3},{8,10},{9,13},{10,... | collective-permute-start | bytes 1769480 | tf_op jit(solution)/shard_map/ppermute | solution.py:33
  30.2 5.2 %collective-permute-start.7 = (bf16[2,96,384]{2,1,0:T(8,128)(2,1)S(1)}, bf16[2,96,384]{2,1,0:T(8,128)(2,1)S(1)}, u32[]{:S(2)}, u32[]{:S(2)}) collective-permute-start(bf16[2,96,384]{2,1,0:T(8,128)(2,1)S(1)} %get-tuple-element.119), channel_id=1, source_target_pairs={{0,8},{4,12},{8,0},{12,4},{16,24},{20,28},{24,16},{28,20},{1,9},{5... | collective-permute-start | bytes 442376 | tf_op jit(solution)/shard_map/ppermute | solution.py:24
  36.2 7.0 %collective-permute-start.8 = (bf16[4,96,384]{2,1,0:T(8,128)(2,1)}, bf16[4,96,384]{2,1,0:T(8,128)(2,1)}, u32[]{:S(2)}, u32[]{:S(2)}) collective-permute-start(bf16[4,96,384]{2,1,0:T(8,128)(2,1)} %bitcast.25), channel_id=1, source_target_pairs={{0,4},{1,3},{2,6},{3,1},{4,0},{5,7},{6,2},{7,5},{8,12},{9,11},{10,... | collective-permute-start | bytes 884744 | tf_op jit(solution)/shard_map/ppermute | solution.py:33
  37.7 9.2 %collective-permute-start.11 = (bf16[2,4,96,384]{3,2,1,0:T(8,128)(2,1)S(1)}, bf16[2,4,96,384]{3,2,1,0:T(8,128)(2,1)S(1)}, u32[]{:S(2)}, u32[]{:S(2)}) collective-permute-start(bf16[2,4,96,384]{3,2,1,0:T(8,128)(2,1)S(1)} %pad_maximum_fusion.1.refs_0_), channel_id=1, source_target_pairs={{0,1},{1,0},{2,3},{3,2},{4,5},{5,4},{6,7},{7,6},{8,9},{9,8},{10,11... | collective-permute-start | bytes 1769480 | tf_op jit(solution)/shard_map/ppermute | solution.py:24
  42.0 4.9 %collective-permute-start.12 = (bf16[2,4,96,384]{3,2,1,0:T(8,128)(2,1)S(1)}, bf16[2,4,96,384]{3,2,1,0:T(8,128)(2,1)S(1)}, u32[]{:S(2)}, u32[]{:S(2)}) collective-permute-start(bf16[2,4,96,384]{3,2,1,0:T(8,128)(2,1)S(1)} %collective-permute-done.10.refs_1_), channel_id=1, source_target_pairs={{0,1},{1,0},{2,3},{3,2},{4,5},{5,4},{6,7},{7,6},{8,9},{9,8},{10,11... | collective-permute-start | bytes 1769480 | tf_op jit(solution)/shard_map/ppermute | solution.py:24
  44.3 10.4 %collective-permute-start.9 = (bf16[2,4,96,384]{3,2,1,0:T(8,128)(2,1)S(1)}, bf16[2,4,96,384]{3,2,1,0:T(8,128)(2,1)S(1)}, u32[]{:S(2)}, u32[]{:S(2)}) collective-permute-start(bf16[2,4,96,384]{3,2,1,0:T(8,128)(2,1)S(1)} %pad_maximum_fusion.refs_0_), channel_id=1, source_target_pairs={{0,2},{1,5},{2,0},{3,7},{4,6},{5,1},{6,4},{7,3},{8,10},{9,13},{10,... | collective-permute-start | bytes 1769480 | tf_op jit(solution)/shard_map/ppermute | solution.py:33
  45.2 10.1 %collective-permute-start.13 = (bf16[2,4,96,384]{3,2,1,0:T(8,128)(2,1)S(1)}, bf16[2,4,96,384]{3,2,1,0:T(8,128)(2,1)S(1)}, u32[]{:S(2)}, u32[]{:S(2)}) collective-permute-start(bf16[2,4,96,384]{3,2,1,0:T(8,128)(2,1)S(1)} %pad_maximum_fusion.refs_0_), channel_id=1, source_target_pairs={{0,1},{1,0},{2,3},{3,2},{4,5},{5,4},{6,7},{7,6},{8,9},{9,8},{10,11... | collective-permute-start | bytes 1769480 | tf_op jit(solution)/shard_map/ppermute | solution.py:24
  46.9 78.2 %copy-start.29 = (bf16[768,624]{1,0:T(8,128)(2,1)}, bf16[768,624]{1,0:T(8,128)(2,1)S(1)}, u32[]{:S(2)}) copy-start(bf16[768,624]{1,0:T(8,128)(2,1)S(1)} %get-tuple-element.86.ht_ref) | copy-start | bytes 2875396
  54.8 2.2 %collective-permute-start.14 = (bf16[2,4,96,384]{3,2,1,0:T(8,128)(2,1)S(1)}, bf16[2,4,96,384]{3,2,1,0:T(8,128)(2,1)S(1)}, u32[]{:S(2)}, u32[]{:S(2)}) collective-permute-start(bf16[2,4,96,384]{3,2,1,0:T(8,128)(2,1)S(1)} %collective-permute-done.9.refs_1_), channel_id=1, source_target_pairs={{0,1},{1,0},{2,3},{3,2},{4,5},{5,4},{6,7},{7,6},{8,9},{9,8},{10,11... | collective-permute-start | bytes 1769480 | tf_op jit(solution)/shard_map/ppermute | solution.py:24
  84.2 4.6 %collective-permute-start.15 = (bf16[1,8,8,768]{3,2,1,0:T(8,128)(2,1)S(1)}, bf16[1,8,8,768]{3,2,1,0:T(8,128)(2,1)S(1)}, u32[]{:S(2)}, u32[]{:S(2)}) collective-permute-start(bf16[1,8,8,768]{3,2,1,0:T(8,128)(2,1)S(1)} %bitcast.143), channel_id=1, source_target_pairs={{0,2},{1,3},{2,0},{3,1},{4,6},{5,7},{6,4},{7,5},{8,10},{9,11},{10,... | collective-permute-start | bytes 294920 | tf_op jit(solution)/shard_map/ppermute | solution.py:24
  88.8 1.5 collective-permute-start.16
  92.1 1.5 collective-permute-start.17
  93.7 4.9 %collective-permute-start.18 = (bf16[1,1,8,8,768]{4,3,2,1,0:T(8,128)(2,1)S(1)}, bf16[1,1,8,8,768]{4,3,2,1,0:T(8,128)(2,1)S(1)}, u32[]{:S(2)}, u32[]{:S(2)}) collective-permute-start(bf16[1,1,8,8,768]{4,3,2,1,0:T(8,128)(2,1)S(1)} %slice_bitcast_fusion.8), channel_id=1, source_target_pairs={{0,2},{1,3},{2,0},{3,1},{4,6},{5,7},{6,4},{7,5},{8,10},{9,11},{10,... | collective-permute-start | bytes 294920 | tf_op jit(solution)/shard_map/ppermute | solution.py:24
  117.7 5.7 %collective-permute-start.19 = (bf16[2,4,96,768]{3,2,1,0:T(8,128)(2,1)S(1)}, bf16[2,4,96,768]{3,2,1,0:T(8,128)(2,1)S(1)}, u32[]{:S(2)}, u32[]{:S(2)}) collective-permute-start(bf16[2,4,96,768]{3,2,1,0:T(8,128)(2,1)S(1)} %get-tuple-element.96), channel_id=1, source_target_pairs={{0,1},{1,0},{2,3},{3,2},{4,5},{5,4},{6,7},{7,6},{8,9},{9,8},{10,11... | collective-permute-start | bytes 3538952 | tf_op jit(solution)/shard_map/ppermute | solution.py:24
  124.7 10.2 %collective-permute-start.20 = (bf16[4,96,768]{2,1,0:T(8,128)(2,1)}, bf16[4,96,768]{2,1,0:T(8,128)(2,1)}, u32[]{:S(2)}, u32[]{:S(2)}) collective-permute-start(bf16[4,96,768]{2,1,0:T(8,128)(2,1)} %slice_bitcast_fusion.1), channel_id=1, source_target_pairs={{0,2},{1,5},{2,0},{3,7},{4,6},{5,1},{6,4},{7,3},{8,10},{9,13},{10,... | collective-permute-start | bytes 1769480 | tf_op jit(solution)/shard_map/ppermute | solution.py:33
  132.3 23.5 %collective-permute-start.26 = (bf16[2,4,96,768]{3,2,1,0:T(8,128)(2,1)S(1)}, bf16[2,4,96,768]{3,2,1,0:T(8,128)(2,1)}, u32[]{:S(2)}, u32[]{:S(2)}) collective-permute-start(bf16[2,4,96,768]{3,2,1,0:T(8,128)(2,1)S(1)} %get-tuple-element.107), channel_id=1, source_target_pairs={{0,1},{1,0},{2,3},{3,2},{4,5},{5,4},{6,7},{7,6},{8,9},{9,8},{10,11... | collective-permute-start | bytes 3538952 | tf_op jit(solution)/shard_map/ppermute | solution.py:24
  160.1 25.3 %collective-permute-start.28 = (bf16[4,96,768]{2,1,0:T(8,128)(2,1)S(1)}, bf16[4,96,768]{2,1,0:T(8,128)(2,1)}, u32[]{:S(2)}, u32[]{:S(2)}) collective-permute-start(bf16[4,96,768]{2,1,0:T(8,128)(2,1)S(1)} %fusion), channel_id=1, source_target_pairs={{0,4},{1,3},{2,6},{3,1},{4,0},{5,7},{6,2},{7,5},{8,12},{9,11},{10,... | collective-permute-start | bytes 1769480 | tf_op jit(solution)/shard_map/ppermute | solution.py:33
  160.5 25.0 %collective-permute-start.27 = (bf16[4,96,768]{2,1,0:T(8,128)(2,1)}, bf16[4,96,768]{2,1,0:T(8,128)(2,1)}, u32[]{:S(2)}, u32[]{:S(2)}) collective-permute-start(bf16[4,96,768]{2,1,0:T(8,128)(2,1)} %select_bitcast_fusion), channel_id=1, source_target_pairs={{0,2},{1,5},{2,0},{3,7},{4,6},{5,1},{6,4},{7,3},{8,10},{9,13},{10,... | collective-permute-start | bytes 1769480 | tf_op jit(solution)/shard_map/ppermute | solution.py:33
  163.5 1.2 collective-permute-start.21
  164.8 11.3 %collective-permute-start.22 = (f32[11,768]{1,0:T(8,128)S(1)}, f32[11,768]{1,0:T(8,128)S(1)}, u32[]{:S(2)}, u32[]{:S(2)}) collective-permute-start(f32[11,768]{1,0:T(8,128)S(1)} %add.45), channel_id=1, source_target_pairs={{0,2},{1,3},{2,0},{3,1},{4,6},{5,7},{6,4},{7,5},{8,10},{9,11},{10,... | collective-permute-start | bytes 101384 | tf_op jit(solution)/shard_map/ppermute | solution.py:24
  176.1 4.2 %collective-permute-start.23 = (f32[11,768]{1,0:T(8,128)S(1)}, f32[11,768]{1,0:T(8,128)S(1)}, u32[]{:S(2)}, u32[]{:S(2)}) collective-permute-start(f32[11,768]{1,0:T(8,128)S(1)} %add.46), channel_id=1, source_target_pairs={{0,4},{4,0},{8,12},{12,8},{16,20},{20,16},{24,28},{28,24},{1,5},{5... | collective-permute-start | bytes 101384 | tf_op jit(solution)/shard_map/ppermute | solution.py:24
  180.2 4.5 %collective-permute-start.24 = (f32[11,768]{1,0:T(8,128)S(1)}, f32[11,768]{1,0:T(8,128)S(1)}, u32[]{:S(2)}, u32[]{:S(2)}) collective-permute-start(f32[11,768]{1,0:T(8,128)S(1)} %add.47), channel_id=1, source_target_pairs={{0,8},{4,12},{8,0},{12,4},{16,24},{20,28},{24,16},{28,20},{1,9},{5... | collective-permute-start | bytes 101384 | tf_op jit(solution)/shard_map/ppermute | solution.py:24
  184.8 5.2 %collective-permute-start.25 = (f32[11,768]{1,0:T(8,128)S(1)}, f32[11,768]{1,0:T(8,128)S(1)}, u32[]{:S(2)}, u32[]{:S(2)}) collective-permute-start(f32[11,768]{1,0:T(8,128)S(1)} %add.48), channel_id=1, source_target_pairs={{0,16},{4,20},{8,24},{12,28},{16,0},{20,4},{24,8},{28,12},{1,17},{... | collective-permute-start | bytes 101384 | tf_op jit(solution)/shard_map/ppermute | solution.py:24
  186.9 8.4 %collective-permute-start.29 = (bf16[2,96,768]{2,1,0:T(8,128)(2,1)S(1)}, bf16[2,96,768]{2,1,0:T(8,128)(2,1)S(1)}, u32[]{:S(2)}, u32[]{:S(2)}) collective-permute-start(bf16[2,96,768]{2,1,0:T(8,128)(2,1)S(1)} %slice_bitcast_fusion.2), channel_id=1, source_target_pairs={{0,8},{4,12},{8,0},{12,4},{16,24},{20,28},{24,16},{28,20},{1,9},{5... | collective-permute-start | bytes 884744 | tf_op jit(solution)/shard_map/ppermute | solution.py:24
  195.4 7.0 %collective-permute-start.30 = (bf16[96,768]{1,0:T(8,128)(2,1)S(1)}, bf16[96,768]{1,0:T(8,128)(2,1)S(1)}, u32[]{:S(2)}, u32[]{:S(2)}) collective-permute-start(bf16[96,768]{1,0:T(8,128)(2,1)S(1)} %get-tuple-element.114), channel_id=1, source_target_pairs={{0,16},{4,20},{8,24},{12,28},{16,0},{20,4},{24,8},{28,12},{1,17},{... | collective-permute-start | bytes 442376 | tf_op jit(solution)/shard_map/ppermute | solution.py:24
  (40 other events, 662.1 us)

commit v6 on v5

--- a/solution.py
+++ b/solution.py
@@ -53,20 +53,17 @@
     return held[0]
 
 
-def scatter_open(held, axis_name, size, bits, unit):
-    held = held.reshape((2,) * len(bits) + held.shape[-2:])
-    for bit in bits[:0:-1]:
-        depth = held.ndim - 3
-        kept, left = (lax.index_in_dim(held, k, depth, keepdims=False) for k in (0, 1))
-        held = plus(kept, swap(left, axis_name, size, bit * unit))
-    return held[0], swap(held[1], axis_name, size, bits[0] * unit)
-
-
-def plus(*terms):
-    total = terms[0].astype(f32)
-    for term in terms[1:]:
-        total = total + term.astype(f32)
-    return total.astype(bf16)
+def mirrored(index, size):
+    bits = size.bit_length() - 1
+    return sum(((index >> k) & 1) << (bits - 1 - k) for k in range(bits)) if bits else index
+
+
+def unmirrored(blocks):
+    size = blocks.shape[0]
+    bits = size.bit_length() - 1
+    split = blocks.reshape((2,) * bits + blocks.shape[1:])
+    turn = tuple(range(bits))[::-1] + tuple(range(bits, split.ndim))
+    return split.transpose(turn).reshape(blocks.shape)
 
 
 def reorder(blocks, me):
@@ -108,14 +105,24 @@
 JOINED = 640
 
 
-def pack_kernel(qkv_ref, out_ref, one_ref, two_ref, router_ref, packed_ref, extra_ref):
+def pack_kernel(
+    me_ref, qkv_hbm, out_hbm, one_hbm, two_hbm, router_hbm, first_ref, second_ref, extra_ref,
+    qkv_ref, out_ref, one_ref, two_ref, router_ref, sems
+):
+    del me_ref
+    pairs = (
+        (qkv_hbm, qkv_ref), (out_hbm, out_ref), (one_hbm, one_ref), (two_hbm, two_ref), (router_hbm, router_ref),
+    )
+    copies = [pltpu.make_async_copy(a, b, sems.at[k]) for k, (a, b) in enumerate(pairs)]
+    for copy in copies:
+        copy.start()
+    for copy in copies:
+        copy.wait()
     low, mid = 2 * HEAD_DIM, qkv_ref.shape[2]
     out = out_ref[...].astype(f32).T.astype(bf16)
-    packed_ref[...] = jnp.concatenate(
-        [qkv_ref[c, :, :low] for c in range(3)]
-        + [qkv_ref[c, :, low:mid] for c in range(3)]
-        + [out[:, low:mid], out[:, :low]],
-        axis=1,
+    first_ref[...] = jnp.concatenate([qkv_ref[c, :, :low] for c in range(3)], axis=1)
+    second_ref[...] = jnp.concatenate(
+        [qkv_ref[c, :, low:mid] for c in range(3)] + [out[:, low:mid], out[:, :low]], axis=1
     )
     rows = one_ref.shape[1]
     columns = [one_ref[...], two_ref[...], router_ref[...]]
@@ -123,6 +130,46 @@
     filled = sum(value.shape[0] for value in columns)
     columns.append(jnp.zeros((extra_ref.shape[1] - filled, rows), f32))
     extra_ref[...] = jnp.concatenate(columns, 0).T.astype(bf16)
+
+
+def fold_kernel(*refs, halves):
+    terms, (kept_ref, left_ref) = refs[:-2], refs[-2:]
+    size = terms[0].shape[0]
+    for k in range(size):
+        total = terms[0][k].astype(f32)
+        for term in terms[1:]:
+            total = total + term[k].astype(f32)
+        at, odd = (k % (size // 2), k >= size // 2) if halves else (k // 2, k % 2 == 1)
+        (left_ref if odd else kept_ref)[at] = total.astype(bf16)
+
+
+def blend_kernel(me_ref, far_ref, kept_ref, other_ref, early_ref, near_ref, second_ref, third_ref):
+    near = [kept_ref[k].astype(f32) + other_ref[k].astype(f32) for k in (0, 1)]
+    near_ref[...] = near[0].astype(bf16)
+    first_core = me_ref[1] == 0
+
+    @pl.when(first_core)
+    def _():
+        second_ref[...] = far_ref[...]
+        third_ref[...] = (near[1] + early_ref[...].astype(f32)).astype(bf16)
+
+    @pl.when(jnp.logical_not(first_core))
+    def _():
+        second_ref[...] = near[1].astype(bf16)
+        third_ref[...] = (far_ref[...].astype(f32) + early_ref[...].astype(f32)).astype(bf16)
+
+
+def finish_kernel(me_ref, own_ref, other_ref, one_ref, two_ref, router_ref, root_ref):
+    experts, rows = router_ref.shape
+    total = own_ref[...] + other_ref[...]
+    width = total.shape[1]
+    mine = pltpu.roll(total, lax.rem(width - me_ref[0] * rows, width), 1)
+    one_ref[...] = mine[experts : experts + 1, :rows]
+    two_ref[...] = mine[experts + 1 : experts + 2, :rows]
+    router_ref[...] = mine[:experts, :rows]
+    images = root_ref.shape[1]
+    mine = pltpu.roll(total, lax.rem(width - me_ref[0] * images, width), 1)
+    root_ref[...] = mine[experts + 2 : experts + 5, :images]
 
 
 def unpack_kernel(own_ref, other_ref, qkv_ref, out_ref):
@@ -149,9 +196,9 @@
 
 
 def prep_kernel(me_ref, x_ref, extra_ref, h_ref, ht_ref, small_ref, *, images, seq, tall):
-    blocks, rows = extra_ref.shape[0], extra_ref.shape[1]
+    blocks = extra_ref.shape[0]
     me = me_ref[0]
-    parts = [extra_ref[jnp.bitwise_xor(me, d) if blocks > 1 else 0] for d in range(blocks)]
+    parts = [extra_ref[mirrored(me ^ d, blocks) if blocks > 1 else 0] for d in range(blocks)]
     small_ref[...] = jnp.concatenate(parts, 0).astype(f32).T
     gain = small_ref[0:1, :]
     for b in range(images):
@@ -167,7 +214,7 @@
 
     def block(d, carry):
         r = jnp.bitwise_xor(me, d)
-        low, high = jnp.bitwise_and(r, 1), jnp.right_shift(r, 1)
+        low, high = jnp.bitwise_and(r, 1), mirrored(jnp.right_shift(r, 1), near.shape[1])
         at = pl.ds(pl.multiple_of(d * rows, 16), rows)
         for mine, first, second in ((True, near, far), (False, other_near, other_far)):
             ours = at_core == core if mine else at_core != core
@@ -233,26 +280,31 @@
 
 
 def front_last_kernel(me_ref, h_ref, mask_ref, pair_ref, *refs, images, tall, ready):
-    w_ref, qkv_ref, p_ref, ho_ref, br_ref = refs[4:]
+    w_ref, qkv_ref, p_ref, ho_ref, wo_ref, br_ref = refs[4:]
     fetch_all(me_ref, w_ref, refs[:4], ready)
     low = low_lanes(tall)
-    br_ref[...] = jnp.zeros_like(br_ref)
-
-    def group(j, carry):
-        qkv_ref[j] = mm(h_ref[...], w_ref[j, :, :256]).astype(bf16)
-        for b in range(images):
-            at = pl.ds(b * tall, tall)
-            joined = qkv_ref[j, at, :]
-            qk, v = joined[:, :128], joined[:, 128:256]
-            k = pltpu.roll(qk.astype(f32), HEAD_DIM, 1).astype(bf16)
-            bias = bias_of(mask_ref, me_ref, b, images, tall)
-            p_ref[j, b], out = attend(jnp.where(low, qk, jnp.zeros_like(qk)), k, v, bias)
-            ho_ref[j, at, :] = jnp.where(low, 0.0, pltpu.roll(out, HEAD_DIM, 1)).astype(bf16)
-        heads = jnp.concatenate([ho_ref[j], pair_ref[j]], 1)
-        br_ref[...] += mm_nt(heads, w_ref[j, :, 128:])
+    groups = w_ref.shape[0]
+    for j in range(groups):
+        wo_ref[:, j * 256 : (j + 1) * 256] = w_ref[j, :, 128:]
+
+    def two(i, carry):
+        for j in (2 * i, 2 * i + 1):
+            qkv_ref[j] = mm(h_ref[...], w_ref[j, :, :256]).astype(bf16)
+            start = pl.multiple_of(j * 256, 256)
+            for b in range(images):
+                at = pl.ds(b * tall, tall)
+                joined = qkv_ref[j, at, :]
+                qk, v = joined[:, :128], joined[:, 128:256]
+                k = pltpu.roll(qk.astype(f32), HEAD_DIM, 1).astype(bf16)
+                bias = bias_of(mask_ref, me_ref, b, images, tall)
+                p_ref[j, b], out = attend(jnp.where(low, qk, jnp.zeros_like(qk)), k, v, bias)
+                out = jnp.where(low, 0.0, pltpu.roll(out, HEAD_DIM, 1)).astype(bf16)
+                ho_ref[at, pl.ds(start, 128)] = out
+                ho_ref[at, pl.ds(start + 128, 128)] = pair_ref[j, at, :]
         return carry
 
-    lax.fori_loop(0, w_ref.shape[0], group, 0)
+    lax.fori_loop(0, groups // 2, two, 0)
+    br_ref[...] = mm_nt(ho_ref[...], wo_ref[...])
 
 
 def spot(rows, b, start, experts):
@@ -329,7 +381,7 @@
     gain = ex_ref[1:2, :]
     width = out_ref.shape[2]
     lanes = lax.broadcasted_iota(jnp.int32, (1, width), 1)
-    roots = jnp.zeros((1, width), f32)
+    roots = [jnp.zeros((1, width), f32) for _ in range(3)]
     for b in range(images):
         at = pl.ds(b * tall, tall)
         length = length_of(mask_ref, me_ref, b, images)
@@ -349,8 +401,8 @@
         sums.insert(1, sq_ref[b, :, 0:1])
         for k, value in enumerate(sums):
             root = jnp.sqrt(value / (length * width))
-            mine = lanes == k * (groups * images) + me_ref[2] * images + b
-            roots += jnp.where(mine, root, 0.0)
+            mine = lanes == (me_ref[0] * groups + me_ref[2]) * images + b
+            roots[k] += jnp.where(mine, root, 0.0)
         grad_c = mm_nt(returned, cot)
         grad_c = combine * (grad_c - jnp.sum(grad_c * combine, axis=0, keepdims=True))
         grad_d = mm_nt(grad_slots, h_two)
@@ -364,28 +416,29 @@
         mean_grad = jnp.mean(scaled, axis=-1, keepdims=True)
         mean_proj = jnp.mean(scaled * unit, axis=-1, keepdims=True)
         gres_ref[at, :] = cot.astype(f32) + inverse * (scaled - mean_grad - unit * mean_proj)
-    small_ref[experts + 2 : experts + 3, :] = roots
+    for k in range(3):
+        small_ref[experts + 2 + k : experts + 3 + k, :] = roots[k]
     gb_ref[...] = gres_ref[...].astype(bf16)
     gbt_ref[...] = gres_ref[...].T.astype(bf16)
 
 
 def back_kernel(
-    me_ref, gb_ref, gbt_ref, ht_ref, qkv_a, p_a, ho_a, w_a, qkv_b, p_b, ho_b, w_b, *refs,
-    images, tall, x, flip
+    me_ref, gb_ref, gbt_ref, ht_ref, qkv_a, p_a, qkv_b, p_b, ho_ref, wo_ref,
+    gw_ref, gj_ref, dho_ref, *, images, tall, x, flip
 ):
-    gw_ref, gh_ref, gj_ref, dho_ref = refs[-4:]
     j = x + 2 * jnp.bitwise_xor(me_ref[1], flip)
+    own = pl.ds(pl.multiple_of(j * 256, 256), 256)
     scale = HEAD_DIM ** (-0.5)
     low = low_lanes(tall)
-    dho_ref[...] = mm(gb_ref[...], w_b[j, :, 128:])
+    dho_ref[...] = mm(gb_ref[...], wo_ref[:, own])
     for b in range(images):
         at = pl.ds(b * tall, tall)
         joined, joined_last = qkv_a[j, at, :], qkv_b[j, at, :]
         q_pair, k_pair, v_pair = joined[:, :128], joined[:, 128:256], joined[:, 256:384]
         qk_last, v_last = joined_last[:, :128], joined_last[:, 128:256]
         grad = dho_ref[at, :].astype(bf16).astype(f32)
-        pair = grad[:, 128:] * ho_a[j, at, :].astype(f32)
-        single = grad[:, :128] * ho_b[j, at, :].astype(f32)
+        product = grad * ho_ref[at, own].astype(f32)
+        single, pair = product[:, :128], product[:, 128:]
         dots = (
             jnp.sum(jnp.where(low, pair, 0.0), axis=1, keepdims=True),
             jnp.sum(jnp.where(low, 0.0, pair), axis=1, keepdims=True),
@@ -417,7 +470,7 @@
             ],
             1,
         ).astype(bf16)
-    grad_out = mm(gbt_ref[...], jnp.concatenate([ho_b[j], ho_a[j]], 1))
+    grad_out = mm(gbt_ref[...], ho_ref[:, own])
     grad_in = mm(ht_ref[...], gj_ref[...])
     halves, blocks, rows = gw_ref.shape[:3]
     for d in range(halves * blocks):
@@ -429,15 +482,21 @@
             grad_in[at, 512:] + grad_out[at, :128]
         ).astype(bf16)
         gw_ref[entry + (slice(None), slice(640, 768))] = grad_out[at, 128:].astype(bf16)
-    into = mm_nt(gj_ref[:, :384], w_a[j]) + mm_nt(gj_ref[:, 384:], w_b[j, :, :256])
-    gh_ref[...] = into + refs[0][...] if len(refs) > 4 else into
 
 
 def last_kernel(
-    x_ref, gres_ref, gh_ref, ex_ref, part_ref, gt_ref, small_ref, *, images, seq, tall, experts
+    me_ref, x_ref, gres_ref, ex_ref, part_ref, w_a, w_b, *refs, images, seq, tall, experts, order
 ):
+    grads, (gt_ref, small_ref, gh_ref) = refs[:-3], refs[-3:]
     total = jnp.zeros((1, x_ref.shape[2]), f32)
     gain = ex_ref[0:1, :]
+    for k, (ref, (x, flip)) in enumerate(zip(grads, order)):
+        j = x + 2 * jnp.bitwise_xor(me_ref[1], flip)
+        into = mm_nt(ref[:, :384], w_a[j]) + mm_nt(ref[:, 384:], w_b[j, :, :256])
+        if k == 0:
+            gh_ref[...] = into
+        else:
+            gh_ref[...] += into
     for b in range(images):
         at = pl.ds(b * tall, seq)
         unit, inverse = unit_of(x_ref[b].astype(f32))
@@ -496,32 +555,34 @@
         exact = {"images": images, "seq": seq, "tall": tall}
 
         columns = experts + 2
-        packed, extra = call(
+        half = 2 * part
+        hbm = pl.BlockSpec(memory_space=pltpu.HBM)
+        vmem = pl.BlockSpec(memory_space=pltpu.VMEM)
+        word = pl.BlockSpec(memory_space=pltpu.SMEM)
+        wide = columns + -columns % 128
+        shapes = [(3, d_rows, part), (part, d_rows), (1, d_rows), (1, d_rows), (experts, d_rows)]
+        first, second, extra = pl.pallas_call(
             pack_kernel,
-            [((d_rows, 4 * part), bf16), ((d_rows, columns + -columns % 128), bf16)],
-            (w_qkv.transpose(1, 0, 2), w_out, gain_one[None], gain_two[None], router.T),
-            flops=cost(1),
+            out_shape=[jax.ShapeDtypeStruct((d_rows, n), bf16) for n in (half, half, wide)],
+            in_specs=[word] + [hbm] * 5,
+            out_specs=[vmem] * 3,
+            scratch_shapes=[pltpu.VMEM(shape, bf16) for shape in shapes] + [pltpu.SemaphoreType.DMA((5,))],
+            compiler_params=pltpu.CompilerParams(vmem_limit_bytes=67_000_000),
             name="pack",
-            scalars=0,
-            grant=4,
-        )
-
-        half = 2 * part
-        first, second, held_extra = packed[:, :half], packed[:, half:], extra
-        for depth, bit in enumerate(bits_of(dp)[:-1]):
+        )(words, w_qkv.transpose(1, 0, 2), w_out, gain_one[None], gain_two[None], router.T)
+
+        first, second, held_extra = first[None], second[None], extra[None]
+        for bit in bits_of(dp)[:-1]:
             other, other_extra = lax.optimization_barrier(
                 (swap(first, "dp", dp, bit), swap(held_extra, "dp", dp, bit))
             )
-            first = jnp.stack([first, other], depth)
-            held_extra = jnp.stack([held_extra, other_extra], depth)
-            second = jnp.stack([second, swap(second, "dp", dp, bit)], depth)
-        first = first.reshape((high, d_rows, half))
-        second = second.reshape((high, d_rows, half))
+            first = jnp.concatenate([first, other])
+            held_extra = jnp.concatenate([held_extra, other_extra])
+            second = jnp.concatenate([second, swap(second, "dp", dp, bit)])
         other, other_extra = lax.optimization_barrier(
             (swap_both(first, dp, mp, (1, 0), (0, 2)), swap(held_extra, "dp", dp, 1))
         )
-        held_extra = jnp.stack([held_extra, other_extra], len(bits_of(dp)) - 1)
-        held_extra = held_extra.reshape((dp,) + extra.shape)
+        held_extra = jnp.concatenate([held_extra, other_extra])
         near = jnp.stack([first, other])
         far = swap_both(near, dp, mp, (0, 2), (1, 0))
         first = (near, far, swap(near, "mp", mp, 1), swap(far, "mp", mp, 1))
@@ -534,7 +595,8 @@
             low = jnp.where(mine, near, other_near)
             high_part = jnp.where(mine, far, other_far)
             blocks = jnp.stack([low[x], high_part[x]]) if of_core else (high_part if x else low)
-            blocks = blocks.transpose(1, 0, 2, 3).reshape((dp, d_rows, half))
+            blocks = blocks.reshape((dp, d_rows, half))
+            blocks = unmirrored(blocks)
             return reorder(blocks, me).reshape(width, half)
 
         def weights_of(parts):
@@ -543,7 +605,7 @@
             return parts
 
         if ready:
-            held_extra = reorder(held_extra, me).reshape(1, width, -1)
+            held_extra = reorder(unmirrored(held_extra), me).reshape(1, width, -1)
 
         x3 = tokens.reshape(images, seq, width)
         cot3 = cotangent.reshape(images, seq, width)
@@ -578,9 +640,14 @@
         w_a, qkv_a, p_a, ho_a = pair
         second_far, ho_a = lax.optimization_barrier((second_far, ho_a))
         second = (second_near, second_far, second_near_other, swap(second_far, "mp", mp, 1))
-        w_b, qkv_b, p_b, ho_b, branch = call(
+        w_b, qkv_b, p_b, heads_out, w_heads, branch = call(
             front_last_kernel,
-            saved(256, ()) + [((count, width), f32)],
+            saved(256, ())[:3]
+            + [
+                ((count, 256 * mp), bf16),
+                ((width, 256 * mp), bf16),
+                ((count, width), f32),
+            ],
             (words, h_one, token_mask, ho_a) + weights_of(second),
             flops=cost(7),
             name="front_last",
@@ -637,7 +704,7 @@
                 ((count, width), f32),
                 ((count, width), bf16),
                 ((width, count), bf16),
-                ((experts + 3, width), f32),
+                ((experts + 5, width), f32),
             ],
             (words, resid, h_two, soft, cot3, token_mask, ex, back, sq_branch),
             flops=cost(5),
@@ -649,15 +716,13 @@
         )
         shape = (1, 1, width, 4 * part) if ready else (2, high, d_rows, 4 * part)
 
-        def back_of(x, flip, *so_far):
-            grads, total = call(
+        def back_of(x, flip, grad_in):
+            grads, joined = call(
                 back_kernel,
-                [(shape, bf16), ((count, width), f32)],
-                (words, grad_low, grad_turned, h_turned)
-                + (qkv_a, p_a, ho_a, w_a, qkv_b, p_b, ho_b, w_b)
-                + so_far,
-                [pltpu.VMEM((count, JOINED), bf16), pltpu.VMEM((count, 256), f32)],
-                flops=cost(6),
+                [(shape, bf16), ((count, JOINED), bf16)],
+                (words, grad_in, grad_turned, h_turned, qkv_a, p_a, qkv_b, p_b, heads_out, w_heads),
+                [pltpu.VMEM((count, 256), f32)],
+                flops=cost(8),
                 name="back",
                 grant=10,
                 x=x,
@@ -667,36 +732,63 @@
             if ready:
                 grads = reorder(grads.reshape(dp, d_rows, 4 * part), me)
                 grads = grads.reshape(high, 2, d_rows, 4 * part).transpose(1, 0, 2, 3)
-            return grads, total
-
-        sent_grads, grad_h = back_of(1, 1)
+            return grads, joined
+
+        def fold(terms, halves):
+            size = terms[0].shape
+            kept = ((size[0] // 2,) + size[1:], bf16)
+            return call(
+                fold_kernel,
+                [kept, kept],
+                terms,
+                flops=cost(1),
+                name="fold",
+                scalars=0,
+                grant=6,
+                halves=halves,
+            )
+
+        order = ((1, 1), (1, 0), (0, 1), (0, 0))
+        sent_grads, joined_a = back_of(1, 1, grad_low)
         other = swap(sent_grads, "mp", mp, 1)
-        kept_grads, grad_h = back_of(1, 0, grad_h)
-        far_sum = plus(kept_grads, other)
-        far_sum, grad_h = lax.optimization_barrier((far_sum, grad_h))
-        early = swap_both(far_sum[1], dp, mp, (0, 2), (1, 0))
-        sent_grads, grad_h = back_of(0, 1, grad_h)
-        early, grad_h = lax.optimization_barrier((early, grad_h))
+        grad_low, joined_a = lax.optimization_barrier((grad_low, joined_a))
+        kept_grads, joined_b = back_of(1, 0, grad_low)
+        far_kept, far_left = fold((kept_grads, other), True)
+        far_left, grad_low, joined_b = lax.optimization_barrier((far_left, grad_low, joined_b))
+        early = swap_both(far_left[0], dp, mp, (0, 2), (1, 0))
+        sent_grads, joined_c = back_of(0, 1, grad_low)
+        early, grad_low, joined_c = lax.optimization_barrier((early, grad_low, joined_c))
         other = swap(sent_grads, "mp", mp, 1)
-        kept_grads, grad_h = back_of(0, 0, grad_h)
-        near_sum = plus(kept_grads, other)
-        grad_tokens, small = call(
-            last_kernel,
-            [((images, seq, width), f32), ((experts + 3, width), f32)],
-            (x3, grad_resid, grad_h, ex, small),
-            flops=cost(3),
-            name="last",
-            scalars=0,
-            grant=6,
-            experts=experts,
-            **exact,
-        )
-        second = jnp.where(core == 0, far_sum[0], near_sum[1])
-        third = plus(jnp.where(core == 0, near_sum[1], far_sum[0]), early)
+        kept_grads, joined_d = back_of(0, 0, grad_low)
+        part_shape = ((high, d_rows, 4 * part), bf16)
+        near_sum, second, third = call(
+            blend_kernel,
+            [part_shape] * 3,
+            (words, far_kept[0], kept_grads, other, early),
+            flops=cost(1),
+            name="blend",
+            grant=8,
+        )
         second = swap_both(second, dp, mp, (0, 2), (1, 0))
         third = swap_both(third, dp, mp, (1, 0), (0, 2))
-        summed = plus(near_sum[0], second, third)
-        own, other = scatter_open(summed, "dp", dp, bits_of(high), 2)
+        grad_tokens, small, _ = call(
+            last_kernel,
+            [((images, seq, width), f32), ((experts + 5, width), f32), ((count, width), f32)],
+            (words, x3, grad_resid, ex, small, w_a, w_b, joined_a, joined_b, joined_c, joined_d),
+            flops=cost(6),
+            name="last",
+            grant=8,
+            experts=experts,
+            order=order,
+            **exact,
+        )
+        for bit in bits_of(dp)[:-1]:
+            small = small + swap(small, "dp", dp, bit)
+        kept, left = fold((near_sum, second, third), False)
+        left, small = lax.optimization_barrier((left, small))
+        for bit in bits_of(high)[:0:-1]:
+            kept, left = fold((kept, swap(left, "dp", dp, 2 * bit)), False)
+        own, other = kept[0], swap(left[0], "dp", dp, 2 * bits_of(high)[0])
         grad_qkv, grad_out = call(
             unpack_kernel,
             [((3, d_rows, part), f32), ((part, d_rows), f32)],
@@ -706,21 +798,29 @@
             scalars=0,
             grant=6,
         )
-
-        for bit in bits_of(mp)[::-1]:
-            small = small + swap(small, "mp", mp, bit)
-        root_squares = small[-1, : 3 * mp * images].reshape(3, mp * images)
-        for bit in bits_of(dp)[::-1]:
-            small = small + swap(small, "dp", dp, bit)
-        small = lax.dynamic_slice_in_dim(small, me * d_rows, d_rows, 1)
+        small = small + swap(small, "dp", dp, 1)
+        small = small + swap(small, "mp", mp, 2)
+        grad_one, grad_two, grad_router, root_squares = call(
+            finish_kernel,
+            [
+                ((1, d_rows), f32),
+                ((1, d_rows), f32),
+                ((experts, d_rows), f32),
+                ((3, mp * images), f32),
+            ],
+            (words, small, swap(small, "mp", mp, 1)),
+            flops=cost(1),
+            name="finish",
+            grant=4,
+        )
         return (
             out_rows.reshape(rows, width),
             grad_tokens.reshape(rows, width),
-            small[experts],
+            grad_one[0],
             grad_qkv.transpose(1, 0, 2),
             grad_out,
-            small[experts + 1],
-            small[:experts].T,
+            grad_two[0],
+            grad_router.T,
             grad_w_in[None],
             grad_w_back[None],
             root_squares,

time: 204 us -> 175 us (0.86)
  local copies, waits for them, and re-layouts: 24.2 us -> 0.09 us
  waiting for transfers between devices: 63.6 us -> 57 us
  Pallas kernels: 54.7 us -> 60.2 us
  other arithmetic: 7.7 us -> 4.33 us
    unnamed x82 -> x16, local copies, waits for them, and re-layouts: 20.5 us -> 0.05 us
    ppermute x24, waiting for transfers between devices: 55.7 us -> 47.6 us  [swap(): lax.ppermute(array_in, axis_name, [(i, i ^ bit) for i in range(size)])]
    convert_element_type x5 -> x0, other arithmetic: 5.12 us -> none  [plus(): return total.astype(bf16)]
    pallas_call x13 -> x17, Pallas kernels: 54.7 us -> 57.8 us  [call(): pl.pallas_call(functools.partial(kernel, **static), out_shape=[jax.ShapeD...]
    concatenate x0 -> x5, other arithmetic: none -> 2.44 us  [the longest x3 1.51 us: per_device(): held_extra = jnp.concatenate([held_extra, other_extra])]
    pallas_call x0 -> x1, Pallas kernels: none -> 2.43 us  [per_device(): pl.pallas_call(pack_kernel, out_shape=[jax.ShapeDtypeStruct((d_rows, n),...]
  transfers between devices with their start and end apart: 31 -> 31, of which waited for: 19 -> 16; matrix products, arithmetic and copies ran while one was open for 5% -> 3% of each run, Pallas kernels for 14% -> 18%
where the time goes in v6:
time: 175 us; the launch traced here: 174 us
  Pallas kernels  60.2 us (34%)
  waiting for transfers between devices  57 us (33%)
  starting transfers between devices  26.2 us (15%)
  blocking collectives  21.8 us (12%)
  other arithmetic  4.33 us (2%)
  matrix products  3.84 us (2%)
    pallas_call x17, Pallas kernels, call(): pl.pallas_call(functools.partial(kernel, **static), out_shape=[jax.ShapeD...  57.8 us
    ppermute x24, waiting for transfers between devices, swap(): lax.ppermute(array_in, axis_name, [(i, i ^ bit) for i in range(size)])  47.6 us
    ppermute x24, starting transfers between devices, swap(): lax.ppermute(array_in, axis_name, [(i, i ^ bit) for i in range(size)])  18.8 us
    all_to_all x1, blocking collectives, per_device(): got = lax.all_to_all(got, 'dp', split_axis=0, concat_axis=0, tiled=True)  12.3 us
    all_to_all x1, blocking collectives, per_device(): back = lax.all_to_all(back, 'dp', split_axis=0, concat_axis=0, tiled=True)  9.51 us
    ppermute x7, waiting for transfers between devices, swap_both(): return lax.ppermute(array_in, ('dp', 'mp'), pairs)  9.4 us
    ppermute x7, starting transfers between devices, swap_both(): return lax.ppermute(array_in, ('dp', 'mp'), pairs)  7.38 us
    dot_general x2, matrix products, mm_tn(): lax.dot_general(a, b, (((0,), (0,)), ((), ())), preferred_element_type=f32)  3.84 us
  transfers between devices with their start and end apart: 31, of which 16 were waited for; matrix products, arithmetic and copies ran while one was open for 3% of the time, Pallas kernels for 18%

profile of v6, /device:TPU:0, one launch (start us, length us, event | category | flops | bytes accessed | tf_op | source)
XLA Modules:
  0.0 174.4 jit_solution(1460787988801647495)
XLA Ops:
  1.2 2.4 %pack.1 = (bf16[96,384]{1,0:T(8,128)(2,1)}, bf16[96,384]{1,0:T(8,128)(2,1)}, bf16[96,128]{1,0:T(8,128)(2,1)}) custom-call(s32[3]{0:T(128)} %pad_add_fusion.me_ref, bf16[3,96,192]{2,1,0:T(8,128)(2,1)} %bitcast.108, bf16[192,96]{1,0:T(8,128)(2,1)} %out_hbm.1, bf16[1,96]{1,0:T(2,128)(2,1)} %bitcast.111, bf16[1,96]{1,0:T(2,128)(2,1)} %bitcast.112, ...), custom_call_target="tpu_custom_call" | custom-call | tf_op jit(solution)/shard_map/pack/pallas_call | solution.py:564
  3.7 4.1 %collective-permute-start = (bf16[1,96,384]{2,1,0:T(8,128)(2,1)}, bf16[1,96,384]{2,1,0:T(8,128)(2,1)S(1)}, u32[]{:S(2)}, u32[]{:S(2)}) collective-permute-start(bf16[1,96,384]{2,1,0:T(8,128)(2,1)} %bitcast.98), channel_id=1, source_target_pairs={{0,16},{4,20},{8,24},{12,28},{16,0},{20,4},{24,8},{28,12},{1,17},{... | collective-permute-start | bytes 221192 | tf_op jit(solution)/shard_map/ppermute | solution.py:24
  7.9 4.9 %collective-permute-done.1 = bf16[1,96,128]{2,1,0:T(8,128)(2,1)S(1)} collective-permute-done((bf16[1,96,128]{2,1,0:T(8,128)(2,1)}, bf16[1,96,128]{2,1,0:T(8,128)(2,1)S(1)}, u32[]{:S(2)}, u32[]{:S(2)}) %collective-permute-start.1) | collective-permute-done | bytes 24608 | tf_op jit(solution)/shard_map/ppermute | solution.py:24
  13.7 1.6 collective-permute-start.2
  16.5 3.8 %collective-permute-done.3 = bf16[2,96,128]{2,1,0:T(8,128)(2,1)S(1)} collective-permute-done((bf16[2,96,128]{2,1,0:T(8,128)(2,1)S(1)}, bf16[2,96,128]{2,1,0:T(8,128)(2,1)S(1)}, u32[]{:S(2)}, u32[]{:S(2)}) %collective-permute-start.3) | collective-permute-done | bytes 49184 | tf_op jit(solution)/shard_map/ppermute | solution.py:24
  21.3 1.6 collective-permute-start.4
  24.2 2.8 %collective-permute-start.6 = (bf16[1,96,384]{2,1,0:T(8,128)(2,1)}, bf16[1,96,384]{2,1,0:T(8,128)(2,1)S(1)}, u32[]{:S(2)}, u32[]{:S(2)}) collective-permute-start(bf16[1,96,384]{2,1,0:T(8,128)(2,1)} %bitcast.95), channel_id=1, source_target_pairs={{0,16},{4,20},{8,24},{12,28},{16,0},{20,4},{24,8},{28,12},{1,17},{... | collective-permute-start | bytes 221192 | tf_op jit(solution)/shard_map/ppermute | solution.py:24
  27.0 3.5 %collective-permute-done.5 = bf16[4,96,128]{2,1,0:T(8,128)(2,1)S(1)} collective-permute-done((bf16[4,96,128]{2,1,0:T(8,128)(2,1)S(1)}, bf16[4,96,128]{2,1,0:T(8,128)(2,1)S(1)}, u32[]{:S(2)}, u32[]{:S(2)}) %collective-permute-start.5) | collective-permute-done | bytes 98336 | tf_op jit(solution)/shard_map/ppermute | solution.py:24
  32.4 4.1 %collective-permute-done.7 = bf16[2,96,384]{2,1,0:T(8,128)(2,1)S(1)} collective-permute-done((bf16[2,96,384]{2,1,0:T(8,128)(2,1)S(1)}, bf16[2,96,384]{2,1,0:T(8,128)(2,1)S(1)}, u32[]{:S(2)}, u32[]{:S(2)}) %collective-permute-start.7) | collective-permute-done | bytes 147488 | tf_op jit(solution)/shard_map/ppermute | solution.py:24
  38.1 5.6 %collective-permute-done.10.refs_1_ = bf16[2,4,96,384]{3,2,1,0:T(8,128)(2,1)S(1)} collective-permute-done((bf16[2,4,96,384]{3,2,1,0:T(8,128)(2,1)S(1)}, bf16[2,4,96,384]{3,2,1,0:T(8,128)(2,1)S(1)}, u32[]{:S(2)}, u32[]{:S(2)}) %collective-permute-start.10) | collective-permute-done | bytes 589856 | tf_op jit(solution)/shard_map/ppermute | solution.py:33
  47.3 7.8 %front_pair.1 = (bf16[4,768,384]{2,1,0:T(8,128)(2,1)S(1)}, bf16[4,624,384]{2,1,0:T(8,128)(2,1)S(1)}, bf16[4,3,2,208,208]{4,3,2,1,0:T(8,128)(2,1)S(1)}, bf16[4,624,128]{2,1,0:T(8,128)(2,1)S(1)}) custom-call(s32[3]{0:T(128)S(1)} %copy-done, bf16[624,768]{1,0:T(8,128)(2,1)S(1)} %get-tuple-element.90.h_ref, s32[12,200]{1,0:T(8,128)S(1)} %copy-done.5, ...), custom_call_target="tpu_custom_call" | custom-call | flops 11000000512 | bytes 3327372 | tf_op jit(solution)/shard_map/front_pair/pallas_call | solution.py:521
  55.3 2.0 %collective-permute-done.14.refs_3_ = bf16[2,4,96,384]{3,2,1,0:T(8,128)(2,1)S(1)} collective-permute-done((bf16[2,4,96,384]{3,2,1,0:T(8,128)(2,1)S(1)}, bf16[2,4,96,384]{3,2,1,0:T(8,128)(2,1)S(1)}, u32[]{:S(2)}, u32[]{:S(2)}) %collective-permute-start.14) | collective-permute-done | bytes 589856 | tf_op jit(solution)/shard_map/ppermute | solution.py:24
  57.2 10.4 %front_last.1 = (bf16[4,768,384]{2,1,0:T(8,128)(2,1)S(1)}, bf16[4,624,256]{2,1,0:T(8,128)(2,1)S(1)}, bf16[4,3,208,208]{3,2,1,0:T(8,128)(2,1)S(1)}, bf16[624,1024...) custom-call(s32[3]{0:T(128)S(1)} %copy-done, ...), custom_call_target="tpu_custom_call" | custom-call | flops 7699999744 | bytes 3966348 | tf_op jit(solution)/shard_map/front_last/pallas_call | solution.py:521
  67.7 2.7 %route.1 = (f32[624,768]{1,0:T(8,128)S(1)}, bf16[624,768]{1,0:T(8,128)(2,1)S(1)}, f32[2,3,8,208]{3,2,1,0:T(8,128)S(1)}, bf16[64,768]{1,0:T(8,128)(2,1)S(1)}, f32[3,1,128]{2,1,0:T(1,128)S(1)}) custom-call(s32[3]{0:T(128)S(1)} %copy-done, bf16[3,200,768]{2,1,0:T(8,128)(2,1)S(1)} %bitcast.86, f32[624,768]{1,0:T(8,128)S(1)} %get-tuple-element.96.br_ref, ...), custom_call_target="tpu_custom_call" | custom-call | flops 2200000000 | bytes 4162956 | tf_op jit(solution)/shard_map/route/pallas_call | solution.py:521
  70.4 12.3 %all_to_all.10 = bf16[8,8,768]{2,1,0:T(8,128)(2,1)S(1)} all-to-all(bf16[8,8,768]{2,1,0:T(8,128)(2,1)S(1)} %bitcast.80), channel_id=1, replica_groups=mesh['dp'=8,'mp'=4] {'dp'}, dimensions={0} | all-to-all | bytes 196608 | tf_op jit(solution)/shard_map/all_to_all | solution.py:675
  83.7 3.6 %collective-permute-done.15 = bf16[1,8,8,768]{3,2,1,0:T(8,128)(2,1)S(1)} collective-permute-done((bf16[1,8,8,768]{3,2,1,0:T(8,128)(2,1)S(1)}, bf16[1,8,8,768]{3,2,1,0:T(8,128)(2,1)S(1)}, u32[]{:S(2)}, u32[]{:S(2)}) %collective-permute-start.15) | collective-permute-done | bytes 98336 | tf_op jit(solution)/shard_map/ppermute | solution.py:24
  88.9 1.7 expert.1
  93.2 3.8 %collective-permute-done.18 = bf16[1,1,8,8,768]{4,3,2,1,0:T(8,128)(2,1)S(1)} collective-permute-done((bf16[1,1,8,8,768]{4,3,2,1,0:T(8,128)(2,1)S(1)}, bf16[1,1,8,8,768]{4,3,2,1,0:T(8,128)(2,1)S(1)}, u32[]{:S(2)}, u32[]{:S(2)}) %collective-permute-start.18) | collective-permute-done | bytes 98336 | tf_op jit(solution)/shard_map/ppermute | solution.py:24
  97.1 9.5 %all_to_all.11 = bf16[8,8,768]{2,1,0:T(8,128)(2,1)S(1)} all-to-all(bf16[8,8,768]{2,1,0:T(8,128)(2,1)S(1)} %fusion.5), channel_id=1, replica_groups=mesh['dp'=8,'mp'=4] {'dp'}, dimensions={0} | all-to-all | bytes 196608 | tf_op jit(solution)/shard_map/all_to_all | solution.py:695
  106.7 3.9 %mix.1 = (bf16[3,200,768]{2,1,0:T(8,128)(2,1)}, f32[624,768]{1,0:T(8,128)S(1)}, bf16[624,768]{1,0:T(8,128)(2,1)S(1)}, bf16[768,624]{1,0:T(8,128)(2,1)S(1)}, f32[13,768]{1,0:T(8,128)S(1)}) custom-call(s32[3]{0:T(128)S(1)} %copy-done, f32[624,768]{1,0:T(8,128)S(1)} %get-tuple-element.98.res_ref, bf16[624,768]{1,0:T(8,128)(2,1)S(1)} %get-tuple-element.99.h_ref, ...), custom_call_target="tpu_custom_call" | custom-call | flops 5500000256 | bytes 4315020 | tf_op jit(solution)/shard_map/mix/pallas_call | solution.py:521
  110.6 4.8 %back.4 = (bf16[2,4,96,768]{3,2,1,0:T(8,128)(2,1)S(1)}, bf16[624,640]{1,0:T(8,128)(2,1)S(1)}) custom-call(s32[3]{0:T(128)S(1)} %copy-done, bf16[624,768]{1,0:T(8,128)(2,1)S(1)} %get-tuple-element.130.gb_ref, bf16[768,624]{1,0:T(8,128)(2,1)S(1)} %get-tuple-element.110.gbt_ref, bf16[768,624]{1,0:T(8,128)(2,1)S(1)} %get-tuple-element.111.ht_ref, ...), custom_call_target="tpu_custom_call" | custom-call | flops 8800000000 | bytes 12036108 | tf_op jit(solution)/shard_map/back/pallas_call | solution.py:521
  115.5 4.8 %back.5 = (bf16[2,4,96,768]{3,2,1,0:T(8,128)(2,1)S(1)}, bf16[624,640]{1,0:T(8,128)(2,1)S(1)}) custom-call(s32[3]{0:T(128)S(1)} %copy-done, bf16[624,768]{1,0:T(8,128)(2,1)S(1)} %get-tuple-element.130.gb_ref, bf16[768,624]{1,0:T(8,128)(2,1)S(1)} %get-tuple-element.110.gbt_ref, bf16[768,624]{1,0:T(8,128)(2,1)S(1)} %get-tuple-element.111.ht_ref, ...), custom_call_target="tpu_custom_call" | custom-call | flops 8800000000 | bytes 12036108 | tf_op jit(solution)/shard_map/back/pallas_call | solution.py:521
  121.7 5.0 %back.6 = (bf16[2,4,96,768]{3,2,1,0:T(8,128)(2,1)S(1)}, bf16[624,640]{1,0:T(8,128)(2,1)S(1)}) custom-call(s32[3]{0:T(128)S(1)} %copy-done, bf16[624,768]{1,0:T(8,128)(2,1)S(1)} %get-tuple-element.130.gb_ref, bf16[768,624]{1,0:T(8,128)(2,1)S(1)} %get-tuple-element.110.gbt_ref, bf16[768,624]{1,0:T(8,128)(2,1)S(1)} %get-tuple-element.111.ht_ref, ...), custom_call_target="tpu_custom_call" | custom-call | flops 8800000000 | bytes 12036108 | tf_op jit(solution)/shard_map/back/pallas_call | solution.py:521
  126.8 3.8 %collective-permute-done.20.early_ref = bf16[4,96,768]{2,1,0:T(8,128)(2,1)S(1)} collective-permute-done((bf16[4,96,768]{2,1,0:T(8,128)(2,1)S(1)}, bf16[4,96,768]{2,1,0:T(8,128)(2,1)S(1)}, u32[]{:S(2)}, u32[]{:S(2)}) %collective-permute-start.20) | collective-permute-done | bytes 589856 | tf_op jit(solution)/shard_map/ppermute | solution.py:33
  130.5 4.8 %back.7 = (bf16[2,4,96,768]{3,2,1,0:T(8,128)(2,1)S(1)}, bf16[624,640]{1,0:T(8,128)(2,1)S(1)}) custom-call(s32[3]{0:T(128)S(1)} %copy-done, bf16[624,768]{1,0:T(8,128)(2,1)S(1)} %get-tuple-element.130.gb_ref, bf16[768,624]{1,0:T(8,128)(2,1)S(1)} %get-tuple-element.110.gbt_ref, bf16[768,624]{1,0:T(8,128)(2,1)S(1)} %get-tuple-element.111.ht_ref, ...), custom_call_target="tpu_custom_call" | custom-call | flops 8800000000 | bytes 12036108 | tf_op jit(solution)/shard_map/back/pallas_call | solution.py:521
  137.8 6.5 %last.1 = (f32[3,200,768]{2,1,0:T(8,128)}, f32[13,768]{1,0:T(8,128)S(1)}, f32[624,768]{1,0:T(8,128)}) custom-call(s32[3]{0:T(128)S(1)} %copy-done, bf16[3,200,768]{2,1,0:T(8,128)(2,1)S(1)} %bitcast.87, f32[624,768]{1,0:T(8,128)S(1)} %get-tuple-element.105.gres_ref, f32[128,768]{1,0:T(8,128)S(1)} %get-tuple-element.97.ex_ref, ...), custom_call_target="tpu_custom_call" | custom-call | flops 6600000000 | bytes 11185164 | tf_op jit(solution)/shard_map/last/pallas_call | solution.py:521
  144.7 5.1 %collective-permute-done.24 = f32[13,768]{1,0:T(8,128)S(1)} collective-permute-done((f32[13,768]{1,0:T(8,128)S(1)}, f32[13,768]{1,0:T(8,128)S(1)}, u32[]{:S(2)}, u32[]{:S(2)}) %collective-permute-start.24) | collective-permute-done | bytes 39968 | tf_op jit(solution)/shard_map/ppermute | solution.py:24
  150.4 3.6 %collective-permute-done.25 = f32[13,768]{1,0:T(8,128)S(1)} collective-permute-done((f32[13,768]{1,0:T(8,128)S(1)}, f32[13,768]{1,0:T(8,128)S(1)}, u32[]{:S(2)}, u32[]{:S(2)}) %collective-permute-start.25) | collective-permute-done | bytes 39968 | tf_op jit(solution)/shard_map/ppermute | solution.py:24
  155.6 3.3 %collective-permute-done.26 = f32[13,768]{1,0:T(8,128)S(1)} collective-permute-done((f32[13,768]{1,0:T(8,128)S(1)}, f32[13,768]{1,0:T(8,128)S(1)}, u32[]{:S(2)}, u32[]{:S(2)}) %collective-permute-start.26) | collective-permute-done | bytes 39968 | tf_op jit(solution)/shard_map/ppermute | solution.py:24
  160.0 1.9 %convolution_bitcast_fusion.1 = f32[1,768,768]{2,1,0:T(8,128)} fusion(bf16[256,768]{1,0:T(8,128)(2,1)S(1)} %bitcast.77, bf16[256,768]{1,0:T(8,128)(2,1)S(1)} %get-tuple-element.152), kind=kOutput, calls=%fused_computation.1 | convolution fusion | flops 301989888 | bytes 3145728 | tf_op jit(solution)/shard_map/dot_general | solution.py:86
  164.5 1.9 %convolution_bitcast_fusion = f32[1,768,768]{2,1,0:T(8,128)} fusion(bf16[256,768]{1,0:T(8,128)(2,1)S(1)} %get-tuple-element.153, bf16[256,768]{1,0:T(8,128)(2,1)S(1)} %get-tuple-element.154), kind=kOutput, calls=%fused_computation | convolution fusion | flops 301989888 | bytes 3145728 | tf_op jit(solution)/shard_map/dot_general | solution.py:86
  167.7 5.9 %collective-permute-done.30.other_ref = bf16[96,768]{1,0:T(8,128)(2,1)S(1)} collective-permute-done((bf16[96,768]{1,0:T(8,128)(2,1)S(1)}, bf16[96,768]{1,0:T(8,128)(2,1)S(1)}, u32[]{:S(2)}, u32[]{:S(2)}) %collective-permute-start.30) | collective-permute-done | bytes 147488 | tf_op jit(solution)/shard_map/ppermute | solution.py:24
  (90 shorter events, 29.6 us)
Async XLA Ops:
  3.7 27.6 %copy-start.6 = (bf16[96,384]{1,0:T(8,128)(2,1)S(1)}, bf16[96,384]{1,0:T(8,128)(2,1)}, u32[]{:S(2)}) copy-start(bf16[96,384]{1,0:T(8,128)(2,1)} %get-tuple-element.91) | copy-start | bytes 221188
  3.7 9.1 %collective-permute-start = (bf16[1,96,384]{2,1,0:T(8,128)(2,1)}, bf16[1,96,384]{2,1,0:T(8,128)(2,1)S(1)}, u32[]{:S(2)}, u32[]{:S(2)}) collective-permute-start(bf16[1,96,384]{2,1,0:T(8,128)(2,1)} %bitcast.98), channel_id=1, source_target_pairs={{0,16},{4,20},{8,24},{12,28},{16,0},{20,4},{24,8},{28,12},{1,17},{... | collective-permute-start | bytes 221192 | tf_op jit(solution)/shard_map/ppermute | solution.py:24
  7.8 4.9 %collective-permute-start.1 = (bf16[1,96,128]{2,1,0:T(8,128)(2,1)}, bf16[1,96,128]{2,1,0:T(8,128)(2,1)S(1)}, u32[]{:S(2)}, u32[]{:S(2)}) collective-permute-start(bf16[1,96,128]{2,1,0:T(8,128)(2,1)} %bitcast.103), channel_id=1, source_target_pairs={{0,16},{4,20},{8,24},{12,28},{16,0},{20,4},{24,8},{28,12},{1,17},{... | collective-permute-start | bytes 73736 | tf_op jit(solution)/shard_map/ppermute | solution.py:24
  13.7 6.7 %collective-permute-start.2 = (bf16[2,96,384]{2,1,0:T(8,128)(2,1)S(1)}, bf16[2,96,384]{2,1,0:T(8,128)(2,1)S(1)}, u32[]{:S(2)}, u32[]{:S(2)}) collective-permute-start(bf16[2,96,384]{2,1,0:T(8,128)(2,1)S(1)} %pad_maximum_fusion.7), channel_id=1, source_target_pairs={{0,8},{4,12},{8,0},{12,4},{16,24},{20,28},{24,16},{28,20},{1,9},{5... | collective-permute-start | bytes 442376 | tf_op jit(solution)/shard_map/ppermute | solution.py:24
  16.1 4.3 %collective-permute-start.3 = (bf16[2,96,128]{2,1,0:T(8,128)(2,1)S(1)}, bf16[2,96,128]{2,1,0:T(8,128)(2,1)S(1)}, u32[]{:S(2)}, u32[]{:S(2)}) collective-permute-start(bf16[2,96,128]{2,1,0:T(8,128)(2,1)S(1)} %pad_maximum_fusion.10), channel_id=1, source_target_pairs={{0,8},{4,12},{8,0},{12,4},{16,24},{20,28},{24,16},{28,20},{1,9},{5... | collective-permute-start | bytes 147464 | tf_op jit(solution)/shard_map/ppermute | solution.py:24
  21.3 9.2 %collective-permute-start.4 = (bf16[4,96,384]{2,1,0:T(8,128)(2,1)S(1)}, bf16[4,96,384]{2,1,0:T(8,128)(2,1)S(1)}, u32[]{:S(2)}, u32[]{:S(2)}) collective-permute-start(bf16[4,96,384]{2,1,0:T(8,128)(2,1)S(1)} %get-tuple-element.157), channel_id=1, source_target_pairs={{0,4},{1,3},{2,6},{3,1},{4,0},{5,7},{6,2},{7,5},{8,12},{9,11},{10,... | collective-permute-start | bytes 884744 | tf_op jit(solution)/shard_map/ppermute | solution.py:33
  23.7 6.8 %collective-permute-start.5 = (bf16[4,96,128]{2,1,0:T(8,128)(2,1)S(1)}, bf16[4,96,128]{2,1,0:T(8,128)(2,1)S(1)}, u32[]{:S(2)}, u32[]{:S(2)}) collective-permute-start(bf16[4,96,128]{2,1,0:T(8,128)(2,1)S(1)} %pad_maximum_fusion.9), channel_id=1, source_target_pairs={{0,4},{4,0},{8,12},{12,8},{16,20},{20,16},{24,28},{28,24},{1,5},{5... | collective-permute-start | bytes 294920 | tf_op jit(solution)/shard_map/ppermute | solution.py:24
  24.2 7.1 %collective-permute-start.6 = (bf16[1,96,384]{2,1,0:T(8,128)(2,1)}, bf16[1,96,384]{2,1,0:T(8,128)(2,1)S(1)}, u32[]{:S(2)}, u32[]{:S(2)}) collective-permute-start(bf16[1,96,384]{2,1,0:T(8,128)(2,1)} %bitcast.95), channel_id=1, source_target_pairs={{0,16},{4,20},{8,24},{12,28},{16,0},{20,4},{24,8},{28,12},{1,17},{... | collective-permute-start | bytes 221192 | tf_op jit(solution)/shard_map/ppermute | solution.py:24
  30.6 13.1 %collective-permute-start.10 = (bf16[2,4,96,384]{3,2,1,0:T(8,128)(2,1)S(1)}, bf16[2,4,96,384]{3,2,1,0:T(8,128)(2,1)S(1)}, u32[]{:S(2)}, u32[]{:S(2)}) collective-permute-start(bf16[2,4,96,384]{3,2,1,0:T(8,128)(2,1)S(1)} %pad_maximum_fusion.1.refs_0_), channel_id=1, source_target_pairs={{0,2},{1,5},{2,0},{3,7},{4,6},{5,1},{6,4},{7,3},{8,10},{9,13},{10,... | collective-permute-start | bytes 1769480 | tf_op jit(solution)/shard_map/ppermute | solution.py:33
  31.3 5.2 %collective-permute-start.7 = (bf16[2,96,384]{2,1,0:T(8,128)(2,1)S(1)}, bf16[2,96,384]{2,1,0:T(8,128)(2,1)S(1)}, u32[]{:S(2)}, u32[]{:S(2)}) collective-permute-start(bf16[2,96,384]{2,1,0:T(8,128)(2,1)S(1)} %pad_maximum_fusion.8), channel_id=1, source_target_pairs={{0,8},{4,12},{8,0},{12,4},{16,24},{20,28},{24,16},{28,20},{1,9},{5... | collective-permute-start | bytes 442376 | tf_op jit(solution)/shard_map/ppermute | solution.py:24
  36.6 7.1 %collective-permute-start.8 = (bf16[4,96,384]{2,1,0:T(8,128)(2,1)S(1)}, bf16[4,96,384]{2,1,0:T(8,128)(2,1)S(1)}, u32[]{:S(2)}, u32[]{:S(2)}) collective-permute-start(bf16[4,96,384]{2,1,0:T(8,128)(2,1)S(1)} %get-tuple-element.159), channel_id=1, source_target_pairs={{0,4},{1,3},{2,6},{3,1},{4,0},{5,7},{6,2},{7,5},{8,12},{9,11},{10,... | collective-permute-start | bytes 884744 | tf_op jit(solution)/shard_map/ppermute | solution.py:33
  38.1 9.2 %collective-permute-start.11 = (bf16[2,4,96,384]{3,2,1,0:T(8,128)(2,1)S(1)}, bf16[2,4,96,384]{3,2,1,0:T(8,128)(2,1)S(1)}, u32[]{:S(2)}, u32[]{:S(2)}) collective-permute-start(bf16[2,4,96,384]{3,2,1,0:T(8,128)(2,1)S(1)} %pad_maximum_fusion.1.refs_0_), channel_id=1, source_target_pairs={{0,1},{1,0},{2,3},{3,2},{4,5},{5,4},{6,7},{7,6},{8,9},{9,8},{10,11... | collective-permute-start | bytes 1769480 | tf_op jit(solution)/shard_map/ppermute | solution.py:24
  43.7 3.6 %collective-permute-start.12 = (bf16[2,4,96,384]{3,2,1,0:T(8,128)(2,1)S(1)}, bf16[2,4,96,384]{3,2,1,0:T(8,128)(2,1)S(1)}, u32[]{:S(2)}, u32[]{:S(2)}) collective-permute-start(bf16[2,4,96,384]{3,2,1,0:T(8,128)(2,1)S(1)} %collective-permute-done.10.refs_1_), channel_id=1, source_target_pairs={{0,1},{1,0},{2,3},{3,2},{4,5},{5,4},{6,7},{7,6},{8,9},{9,8},{10,11... | collective-permute-start | bytes 1769480 | tf_op jit(solution)/shard_map/ppermute | solution.py:24
  43.8 11.4 %collective-permute-start.9 = (bf16[2,4,96,384]{3,2,1,0:T(8,128)(2,1)S(1)}, bf16[2,4,96,384]{3,2,1,0:T(8,128)(2,1)S(1)}, u32[]{:S(2)}, u32[]{:S(2)}) collective-permute-start(bf16[2,4,96,384]{3,2,1,0:T(8,128)(2,1)S(1)} %pad_maximum_fusion.refs_0_), channel_id=1, source_target_pairs={{0,2},{1,5},{2,0},{3,7},{4,6},{5,1},{6,4},{7,3},{8,10},{9,13},{10,... | collective-permute-start | bytes 1769480 | tf_op jit(solution)/shard_map/ppermute | solution.py:33
  44.9 10.4 %collective-permute-start.13 = (bf16[2,4,96,384]{3,2,1,0:T(8,128)(2,1)S(1)}, bf16[2,4,96,384]{3,2,1,0:T(8,128)(2,1)S(1)}, u32[]{:S(2)}, u32[]{:S(2)}) collective-permute-start(bf16[2,4,96,384]{3,2,1,0:T(8,128)(2,1)S(1)} %pad_maximum_fusion.refs_0_), channel_id=1, source_target_pairs={{0,1},{1,0},{2,3},{3,2},{4,5},{5,4},{6,7},{7,6},{8,9},{9,8},{10,11... | collective-permute-start | bytes 1769480 | tf_op jit(solution)/shard_map/ppermute | solution.py:24
  55.2 2.1 %collective-permute-start.14 = (bf16[2,4,96,384]{3,2,1,0:T(8,128)(2,1)S(1)}, bf16[2,4,96,384]{3,2,1,0:T(8,128)(2,1)S(1)}, u32[]{:S(2)}, u32[]{:S(2)}) collective-permute-start(bf16[2,4,96,384]{3,2,1,0:T(8,128)(2,1)S(1)} %collective-permute-done.9.refs_1_), channel_id=1, source_target_pairs={{0,1},{1,0},{2,3},{3,2},{4,5},{5,4},{6,7},{7,6},{8,9},{9,8},{10,11... | collective-permute-start | bytes 1769480 | tf_op jit(solution)/shard_map/ppermute | solution.py:24
  82.7 4.6 %collective-permute-start.15 = (bf16[1,8,8,768]{3,2,1,0:T(8,128)(2,1)S(1)}, bf16[1,8,8,768]{3,2,1,0:T(8,128)(2,1)S(1)}, u32[]{:S(2)}, u32[]{:S(2)}) collective-permute-start(bf16[1,8,8,768]{3,2,1,0:T(8,128)(2,1)S(1)} %bitcast.92), channel_id=1, source_target_pairs={{0,2},{1,3},{2,0},{3,1},{4,6},{5,7},{6,4},{7,5},{8,10},{9,11},{10,... | collective-permute-start | bytes 294920 | tf_op jit(solution)/shard_map/ppermute | solution.py:24
  87.3 1.5 collective-permute-start.16
  90.6 1.5 collective-permute-start.17
  92.2 4.9 %collective-permute-start.18 = (bf16[1,1,8,8,768]{4,3,2,1,0:T(8,128)(2,1)S(1)}, bf16[1,1,8,8,768]{4,3,2,1,0:T(8,128)(2,1)S(1)}, u32[]{:S(2)}, u32[]{:S(2)}) collective-permute-start(bf16[1,1,8,8,768]{4,3,2,1,0:T(8,128)(2,1)S(1)} %slice_bitcast_fusion.2), channel_id=1, source_target_pairs={{0,2},{1,3},{2,0},{3,1},{4,6},{5,7},{6,4},{7,5},{8,10},{9,11},{10,... | collective-permute-start | bytes 294920 | tf_op jit(solution)/shard_map/ppermute | solution.py:24
  115.4 4.9 %collective-permute-start.19 = (bf16[2,4,96,768]{3,2,1,0:T(8,128)(2,1)S(1)}, bf16[2,4,96,768]{3,2,1,0:T(8,128)(2,1)S(1)}, u32[]{:S(2)}, u32[]{:S(2)}) collective-permute-start(bf16[2,4,96,768]{3,2,1,0:T(8,128)(2,1)S(1)} %get-tuple-element.122), channel_id=1, source_target_pairs={{0,1},{1,0},{2,3},{3,2},{4,5},{5,4},{6,7},{7,6},{8,9},{9,8},{10,11... | collective-permute-start | bytes 3538952 | tf_op jit(solution)/shard_map/ppermute | solution.py:24
  120.6 9.9 %collective-permute-start.20 = (bf16[4,96,768]{2,1,0:T(8,128)(2,1)S(1)}, bf16[4,96,768]{2,1,0:T(8,128)(2,1)S(1)}, u32[]{:S(2)}, u32[]{:S(2)}) collective-permute-start(bf16[4,96,768]{2,1,0:T(8,128)(2,1)S(1)} %bitcast.88), channel_id=1, source_target_pairs={{0,2},{1,5},{2,0},{3,7},{4,6},{5,1},{6,4},{7,3},{8,10},{9,13},{10,... | collective-permute-start | bytes 1769480 | tf_op jit(solution)/shard_map/ppermute | solution.py:33
  126.7 8.7 %collective-permute-start.21 = (bf16[2,4,96,768]{3,2,1,0:T(8,128)(2,1)S(1)}, bf16[2,4,96,768]{3,2,1,0:T(8,128)(2,1)S(1)}, u32[]{:S(2)}, u32[]{:S(2)}) collective-permute-start(bf16[2,4,96,768]{3,2,1,0:T(8,128)(2,1)S(1)} %get-tuple-element.135), channel_id=1, source_target_pairs={{0,1},{1,0},{2,3},{3,2},{4,5},{5,4},{6,7},{7,6},{8,9},{9,8},{10,11... | collective-permute-start | bytes 3538952 | tf_op jit(solution)/shard_map/ppermute | solution.py:24
  136.5 17.5 %collective-permute-start.22 = (bf16[4,96,768]{2,1,0:T(8,128)(2,1)S(1)}, bf16[4,96,768]{2,1,0:T(8,128)(2,1)S(1)}, u32[]{:S(2)}, u32[]{:S(2)}) collective-permute-start(bf16[4,96,768]{2,1,0:T(8,128)(2,1)S(1)} %get-tuple-element.138), channel_id=1, source_target_pairs={{0,2},{1,5},{2,0},{3,7},{4,6},{5,1},{6,4},{7,3},{8,10},{9,13},{10,... | collective-permute-start | bytes 1769480 | tf_op jit(solution)/shard_map/ppermute | solution.py:33
  137.5 16.5 %collective-permute-start.23 = (bf16[4,96,768]{2,1,0:T(8,128)(2,1)S(1)}, bf16[4,96,768]{2,1,0:T(8,128)(2,1)S(1)}, u32[]{:S(2)}, u32[]{:S(2)}) collective-permute-start(bf16[4,96,768]{2,1,0:T(8,128)(2,1)S(1)} %get-tuple-element.139), channel_id=1, source_target_pairs={{0,4},{1,3},{2,6},{3,1},{4,0},{5,7},{6,2},{7,5},{8,12},{9,11},{10,... | collective-permute-start | bytes 1769480 | tf_op jit(solution)/shard_map/ppermute | solution.py:33
  144.3 5.5 %collective-permute-start.24 = (f32[13,768]{1,0:T(8,128)S(1)}, f32[13,768]{1,0:T(8,128)S(1)}, u32[]{:S(2)}, u32[]{:S(2)}) collective-permute-start(f32[13,768]{1,0:T(8,128)S(1)} %get-tuple-element.141), channel_id=1, source_target_pairs={{0,16},{4,20},{8,24},{12,28},{16,0},{20,4},{24,8},{28,12},{1,17},{... | collective-permute-start | bytes 119816 | tf_op jit(solution)/shard_map/ppermute | solution.py:24
  149.8 4.2 %collective-permute-start.25 = (f32[13,768]{1,0:T(8,128)S(1)}, f32[13,768]{1,0:T(8,128)S(1)}, u32[]{:S(2)}, u32[]{:S(2)}) collective-permute-start(f32[13,768]{1,0:T(8,128)S(1)} %add.20), channel_id=1, source_target_pairs={{0,8},{4,12},{8,0},{12,4},{16,24},{20,28},{24,16},{28,20},{1,9},{5... | collective-permute-start | bytes 119816 | tf_op jit(solution)/shard_map/ppermute | solution.py:24
  154.2 8.9 %collective-permute-start.29 = (bf16[2,96,768]{2,1,0:T(8,128)(2,1)S(1)}, bf16[2,96,768]{2,1,0:T(8,128)(2,1)S(1)}, u32[]{:S(2)}, u32[]{:S(2)}) collective-permute-start(bf16[2,96,768]{2,1,0:T(8,128)(2,1)S(1)} %get-tuple-element.145), channel_id=1, source_target_pairs={{0,8},{4,12},{8,0},{12,4},{16,24},{20,28},{24,16},{28,20},{1,9},{5... | collective-permute-start | bytes 884744 | tf_op jit(solution)/shard_map/ppermute | solution.py:24
  154.8 4.1 %collective-permute-start.26 = (f32[13,768]{1,0:T(8,128)S(1)}, f32[13,768]{1,0:T(8,128)S(1)}, u32[]{:S(2)}, u32[]{:S(2)}) collective-permute-start(f32[13,768]{1,0:T(8,128)S(1)} %add.21), channel_id=1, source_target_pairs={{0,4},{4,0},{8,12},{12,8},{16,20},{20,16},{24,28},{28,24},{1,5},{5... | collective-permute-start | bytes 119816 | tf_op jit(solution)/shard_map/ppermute | solution.py:24
  158.9 4.2 %collective-permute-start.27 = (f32[13,768]{1,0:T(8,128)S(1)}, f32[13,768]{1,0:T(8,128)S(1)}, u32[]{:S(2)}, u32[]{:S(2)}) collective-permute-start(f32[13,768]{1,0:T(8,128)S(1)} %add.22), channel_id=1, source_target_pairs={{0,2},{1,3},{2,0},{3,1},{4,6},{5,7},{6,4},{7,5},{8,10},{9,11},{10,... | collective-permute-start | bytes 119816 | tf_op jit(solution)/shard_map/ppermute | solution.py:24
  163.1 3.4 %collective-permute-start.28 = (f32[13,768]{1,0:T(8,128)S(1)}, f32[13,768]{1,0:T(8,128)S(1)}, u32[]{:S(2)}, u32[]{:S(2)}) collective-permute-start(f32[13,768]{1,0:T(8,128)S(1)} %add.23.own_ref), channel_id=1, source_target_pairs={{0,1},{1,0},{2,3},{3,2},{4,5},{5,4},{6,7},{7,6},{8,9},{9,8},{10,11... | collective-permute-start | bytes 119816 | tf_op jit(solution)/shard_map/ppermute | solution.py:24
  163.2 10.4 %collective-permute-start.30 = (bf16[96,768]{1,0:T(8,128)(2,1)S(1)}, bf16[96,768]{1,0:T(8,128)(2,1)S(1)}, u32[]{:S(2)}, u32[]{:S(2)}) collective-permute-start(bf16[96,768]{1,0:T(8,128)(2,1)S(1)} %bitcast.89), channel_id=1, source_target_pairs={{0,16},{4,20},{8,24},{12,28},{16,0},{20,4},{24,8},{28,12},{1,17},{... | collective-permute-start | bytes 442376 | tf_op jit(solution)/shard_map/ppermute | solution.py:24
  (7 other events, 111.1 us)

commit v7 on v6

--- a/solution.py
+++ b/solution.py
@@ -207,73 +207,66 @@
     ht_ref[...] = h_ref[...].T
 
 
-def fetch_group(me_ref, w_ref, slot, x, core, near, far, other_near, other_far):
-    me, at_core = me_ref[0], me_ref[1]
-    rows = near.shape[2]
-    blocks = 2 * near.shape[1]
-
-    def block(d, carry):
-        r = jnp.bitwise_xor(me, d)
-        low, high = jnp.bitwise_and(r, 1), mirrored(jnp.right_shift(r, 1), near.shape[1])
-        at = pl.ds(pl.multiple_of(d * rows, 16), rows)
-        for mine, first, second in ((True, near, far), (False, other_near, other_far)):
-            ours = at_core == core if mine else at_core != core
-            if core == 0:
-
-                @pl.when(ours)
-                def _(first=first, second=second):
-                    w_ref[slot, at, :] = (second if x else first)[low, high]
-
-            else:
-
-                @pl.when(jnp.logical_and(ours, low == 0))
-                def _(first=first):
-                    w_ref[slot, at, :] = first[x, high]
-
-                @pl.when(jnp.logical_and(ours, low == 1))
-                def _(second=second):
-                    w_ref[slot, at, :] = second[x, high]
-
-        return carry
-
-    lax.fori_loop(0, blocks, block, 0)
-
-
-def attend(q, k, v, bias):
-    scores = mm_nt(q, k) * HEAD_DIM ** (-0.5) + bias
-    terms = jnp.exp(scores - jnp.max(scores, axis=-1, keepdims=True))
-    probs = (terms * (1.0 / jnp.sum(terms, axis=-1, keepdims=True))).astype(bf16)
-    return probs, mm(probs, v)
+def fetch_all(me_ref, refs, put):
+    rows, high_size = refs[0].shape[2], refs[0].shape[1]
+    for core in (0, 1):
+
+        @pl.when(me_ref[1] == core)
+        def _(core=core):
+            for slot in range(4):
+                x, of_core = slot & 1, slot >> 1
+                first, second = refs[:2] if of_core == core else refs[2:4]
+                for r in range(2 * high_size):
+                    low, high = r & 1, mirrored(r >> 1, high_size)
+                    if of_core == 0:
+                        block = (second if x else first)[low, high]
+                    else:
+                        block = (second if low else first)[x, high]
+                    d = jnp.bitwise_xor(me_ref[0], r)
+                    put(slot, pl.ds(pl.multiple_of(d * rows, 16), rows), block)
+
+
+def attend(triples):
+    scores = [mm_nt(q, k) * HEAD_DIM ** (-0.5) + bias for q, k, _, bias in triples]
+    terms = [jnp.exp(value - jnp.max(value, axis=-1, keepdims=True)) for value in scores]
+    probs = [
+        (value * (1.0 / jnp.sum(value, axis=-1, keepdims=True))).astype(bf16) for value in terms
+    ]
+    return probs, [mm(value, v) for value, (_, _, v, _) in zip(probs, triples)]
 
 
 def bias_of(mask_ref, me_ref, b, images, tall):
     return jnp.where(seen_row(length_of(mask_ref, me_ref, b, images), tall), 0.0, -1e30)
 
 
-def fetch_all(me_ref, w_ref, refs, ready):
-    for slot in range(w_ref.shape[0]):
-        if ready:
-            w_ref[slot] = refs[slot][...]
-        else:
-            fetch_group(me_ref, w_ref, slot, slot & 1, slot >> 1, *refs)
-
-
 def front_pair_kernel(me_ref, h_ref, mask_ref, *refs, images, tall, ready):
     w_ref, qkv_ref, p_ref, ho_ref = refs[4:]
-    fetch_all(me_ref, w_ref, refs[:4], ready)
+
+    def put(slot, at, block):
+        w_ref[slot, at, :] = block
+
+    if ready:
+        for slot in range(4):
+            put(slot, slice(None), refs[slot][...])
+    else:
+        fetch_all(me_ref, refs[:4], put)
     low = low_lanes(tall)
 
     def group(j, carry):
         qkv_ref[j] = mm(h_ref[...], w_ref[j]).astype(bf16)
+        triples = []
         for b in range(images):
-            at = pl.ds(b * tall, tall)
-            joined = qkv_ref[j, at, :]
+            joined = qkv_ref[j, pl.ds(b * tall, tall), :]
             q, k, v = joined[:, :128], joined[:, 128:256], joined[:, 256:384]
             none = jnp.zeros_like(q)
             bias = bias_of(mask_ref, me_ref, b, images, tall)
-            p_ref[j, b, 0], first = attend(jnp.where(low, q, none), k, v, bias)
-            p_ref[j, b, 1], second = attend(jnp.where(low, none, q), k, v, bias)
-            ho_ref[j, at, :] = jnp.where(low, first, second).astype(bf16)
+            triples.append((jnp.where(low, q, none), k, v, bias))
+            triples.append((jnp.where(low, none, q), k, v, bias))
+        probs, outs = attend(triples)
+        for b in range(images):
+            p_ref[j, b, 0], p_ref[j, b, 1] = probs[2 * b], probs[2 * b + 1]
+            pair = jnp.where(low, outs[2 * b], outs[2 * b + 1])
+            ho_ref[j, pl.ds(b * tall, tall), :] = pair.astype(bf16)
         return carry
 
     lax.fori_loop(0, w_ref.shape[0], group, 0)
@@ -281,29 +274,38 @@
 
 def front_last_kernel(me_ref, h_ref, mask_ref, pair_ref, *refs, images, tall, ready):
     w_ref, qkv_ref, p_ref, ho_ref, wo_ref, br_ref = refs[4:]
-    fetch_all(me_ref, w_ref, refs[:4], ready)
+
+    def put(slot, at, block):
+        w_ref[slot, at, :] = block[:, :256]
+        wo_ref[at, slot * 256 : (slot + 1) * 256] = block[:, 128:]
+
+    if ready:
+        for slot in range(4):
+            put(slot, slice(None), refs[slot][...])
+    else:
+        fetch_all(me_ref, refs[:4], put)
     low = low_lanes(tall)
-    groups = w_ref.shape[0]
-    for j in range(groups):
-        wo_ref[:, j * 256 : (j + 1) * 256] = w_ref[j, :, 128:]
 
     def two(i, carry):
+        places = [(2 * i + k, b) for k in (0, 1) for b in range(images)]
         for j in (2 * i, 2 * i + 1):
-            qkv_ref[j] = mm(h_ref[...], w_ref[j, :, :256]).astype(bf16)
-            start = pl.multiple_of(j * 256, 256)
-            for b in range(images):
-                at = pl.ds(b * tall, tall)
-                joined = qkv_ref[j, at, :]
-                qk, v = joined[:, :128], joined[:, 128:256]
-                k = pltpu.roll(qk.astype(f32), HEAD_DIM, 1).astype(bf16)
-                bias = bias_of(mask_ref, me_ref, b, images, tall)
-                p_ref[j, b], out = attend(jnp.where(low, qk, jnp.zeros_like(qk)), k, v, bias)
-                out = jnp.where(low, 0.0, pltpu.roll(out, HEAD_DIM, 1)).astype(bf16)
-                ho_ref[at, pl.ds(start, 128)] = out
-                ho_ref[at, pl.ds(start + 128, 128)] = pair_ref[j, at, :]
+            qkv_ref[j] = mm(h_ref[...], w_ref[j]).astype(bf16)
+        triples = []
+        for j, b in places:
+            joined = qkv_ref[j, pl.ds(b * tall, tall), :]
+            qk, v = joined[:, :128], joined[:, 128:256]
+            k = pltpu.roll(qk.astype(f32), HEAD_DIM, 1).astype(bf16)
+            bias = bias_of(mask_ref, me_ref, b, images, tall)
+            triples.append((jnp.where(low, qk, jnp.zeros_like(qk)), k, v, bias))
+        probs, outs = attend(triples)
+        for (j, b), prob, out in zip(places, probs, outs):
+            at, start = pl.ds(b * tall, tall), pl.multiple_of(j * 256, 256)
+            p_ref[j, b] = prob
+            ho_ref[at, pl.ds(start, 128)] = jnp.where(low, 0.0, pltpu.roll(out, HEAD_DIM, 1)).astype(bf16)
+            ho_ref[at, pl.ds(start + 128, 128)] = pair_ref[j, at, :]
         return carry
 
-    lax.fori_loop(0, groups // 2, two, 0)
+    lax.fori_loop(0, w_ref.shape[0] // 2, two, 0)
     br_ref[...] = mm_nt(ho_ref[...], wo_ref[...])
 
 
@@ -431,6 +433,7 @@
     scale = HEAD_DIM ** (-0.5)
     low = low_lanes(tall)
     dho_ref[...] = mm(gb_ref[...], wo_ref[:, own])
+    heads, dots = [], []
     for b in range(images):
         at = pl.ds(b * tall, tall)
         joined, joined_last = qkv_a[j, at, :], qkv_b[j, at, :]
@@ -439,26 +442,29 @@
         grad = dho_ref[at, :].astype(bf16).astype(f32)
         product = grad * ho_ref[at, own].astype(f32)
         single, pair = product[:, :128], product[:, 128:]
-        dots = (
+        dots += [
             jnp.sum(jnp.where(low, pair, 0.0), axis=1, keepdims=True),
             jnp.sum(jnp.where(low, 0.0, pair), axis=1, keepdims=True),
             jnp.sum(single, axis=1, keepdims=True),
-        )
+        ]
         grad_pair = grad[:, 128:]
         grad_last = jnp.where(low, pltpu.roll(grad[:, :128], HEAD_DIM, 1), 0.0).astype(bf16)
-        gq, gk, gv = [], [], []
-        for head, (probs, g, v, q, k) in enumerate(
-            (
-                (p_a[j, b, 0], jnp.where(low, grad_pair, 0.0).astype(bf16), v_pair, q_pair, k_pair),
-                (p_a[j, b, 1], jnp.where(low, 0.0, grad_pair).astype(bf16), v_pair, q_pair, k_pair),
-                (p_b[j, b], grad_last, v_last, qk_last, qk_last),
-            )
-        ):
-            grad_p = mm_nt(g, v)
-            grad_s = (probs.astype(f32) * (grad_p - dots[head])).astype(bf16)
-            gq.append(mm(grad_s, k))
-            gk.append(mm_tn(grad_s, q))
-            gv.append(mm_tn(probs, g))
+        heads += [
+            (p_a[j, b, 0], jnp.where(low, grad_pair, 0.0).astype(bf16), v_pair, q_pair, k_pair),
+            (p_a[j, b, 1], jnp.where(low, 0.0, grad_pair).astype(bf16), v_pair, q_pair, k_pair),
+            (p_b[j, b], grad_last, v_last, qk_last, qk_last),
+        ]
+    grad_p = [mm_nt(g, v) for _, g, v, _, _ in heads]
+    grad_s = [
+        (probs.astype(f32) * (value - dot)).astype(bf16)
+        for (probs, _, _, _, _), value, dot in zip(heads, grad_p, dots)
+    ]
+    gqs = [mm(value, k) for value, (_, _, _, _, k) in zip(grad_s, heads)]
+    gks = [mm_tn(value, q) for value, (_, _, _, q, _) in zip(grad_s, heads)]
+    gvs = [mm_tn(probs, g) for probs, g, _, _, _ in heads]
+    for b in range(images):
+        at = pl.ds(b * tall, tall)
+        gq, gk, gv = (value[3 * b : 3 * b + 3] for value in (gqs, gks, gvs))
         last = pltpu.roll(jnp.where(low, gk[2], gq[2]), HEAD_DIM, 1)
         gj_ref[at, :] = jnp.concatenate(
             [
@@ -492,7 +498,7 @@
     gain = ex_ref[0:1, :]
     for k, (ref, (x, flip)) in enumerate(zip(grads, order)):
         j = x + 2 * jnp.bitwise_xor(me_ref[1], flip)
-        into = mm_nt(ref[:, :384], w_a[j]) + mm_nt(ref[:, 384:], w_b[j, :, :256])
+        into = mm_nt(ref[:, :384], w_a[j]) + mm_nt(ref[:, 384:], w_b[j])
         if k == 0:
             gh_ref[...] = into
         else:
@@ -573,40 +579,16 @@
 
         first, second, held_extra = first[None], second[None], extra[None]
         for bit in bits_of(dp)[:-1]:
-            other, other_extra = lax.optimization_barrier(
-                (swap(first, "dp", dp, bit), swap(held_extra, "dp", dp, bit))
-            )
-            first = jnp.concatenate([first, other])
-            held_extra = jnp.concatenate([held_extra, other_extra])
+            first = jnp.concatenate([first, swap(first, "dp", dp, bit)])
+            held_extra = jnp.concatenate([held_extra, swap(held_extra, "dp", dp, bit)])
             second = jnp.concatenate([second, swap(second, "dp", dp, bit)])
-        other, other_extra = lax.optimization_barrier(
-            (swap_both(first, dp, mp, (1, 0), (0, 2)), swap(held_extra, "dp", dp, 1))
-        )
-        held_extra = jnp.concatenate([held_extra, other_extra])
-        near = jnp.stack([first, other])
-        far = swap_both(near, dp, mp, (0, 2), (1, 0))
-        first = (near, far, swap(near, "mp", mp, 1), swap(far, "mp", mp, 1))
-        near = jnp.stack([second, swap_both(second, dp, mp, (1, 0), (0, 2))])
-        second_near, second_far = near, swap_both(near, dp, mp, (0, 2), (1, 0))
-        second_near_other = swap(second_near, "mp", mp, 1)
-
-        def whole(x, of_core, near, far, other_near, other_far):
-            mine = core == of_core
-            low = jnp.where(mine, near, other_near)
-            high_part = jnp.where(mine, far, other_far)
-            blocks = jnp.stack([low[x], high_part[x]]) if of_core else (high_part if x else low)
-            blocks = blocks.reshape((dp, d_rows, half))
-            blocks = unmirrored(blocks)
-            return reorder(blocks, me).reshape(width, half)
-
-        def weights_of(parts):
-            if ready:
-                return tuple(whole(j & 1, j >> 1, *parts) for j in range(4))
-            return parts
-
+        other, held_extra = lax.optimization_barrier(
+            (swap_both(first, dp, mp, (1, 0), (0, 2)), held_extra)
+        )
+        held_extra = jnp.concatenate([held_extra, swap(held_extra, "dp", dp, 1)])
+        held_extra = held_extra.reshape((dp,) + extra.shape)
         if ready:
             held_extra = reorder(unmirrored(held_extra), me).reshape(1, width, -1)
-
         x3 = tokens.reshape(images, seq, width)
         cot3 = cotangent.reshape(images, seq, width)
         h_one, h_turned, ex = call(
@@ -618,10 +600,31 @@
             grant=4,
             **exact,
         )
-
-        def saved(columns, probs):
+        near = jnp.stack([first, other])
+        far = swap_both(near, dp, mp, (0, 2), (1, 0))
+        far, h_one = lax.optimization_barrier((far, h_one))
+        first = (near, far, swap(near, "mp", mp, 1), swap(far, "mp", mp, 1))
+        near = jnp.stack([second, swap_both(second, dp, mp, (1, 0), (0, 2))])
+        second_near, second_far = near, swap_both(near, dp, mp, (0, 2), (1, 0))
+        second_near_other = swap(second_near, "mp", mp, 1)
+
+        def whole(x, of_core, near, far, other_near, other_far):
+            mine = core == of_core
+            low = jnp.where(mine, near, other_near)
+            high_part = jnp.where(mine, far, other_far)
+            blocks = jnp.stack([low[x], high_part[x]]) if of_core else (high_part if x else low)
+            blocks = blocks.reshape((dp, d_rows, half))
+            blocks = unmirrored(blocks)
+            return reorder(blocks, me).reshape(width, half)
+
+        def weights_of(parts):
+            if ready:
+                return tuple(whole(j & 1, j >> 1, *parts) for j in range(4))
+            return parts
+
+        def saved(kept, columns, probs):
             return [
-                ((mp, width, half), bf16),
+                ((mp, width, kept), bf16),
                 ((mp, count, columns), bf16),
                 ((mp, images) + probs + (tall, tall), bf16),
                 ((mp, count, 128), bf16),
@@ -629,7 +632,7 @@
 
         pair = call(
             front_pair_kernel,
-            saved(384, (2,)),
+            saved(half, 384, (2,)),
             (words, h_one, token_mask) + weights_of(first),
             flops=cost(10),
             name="front_pair",
@@ -642,7 +645,7 @@
         second = (second_near, second_far, second_near_other, swap(second_far, "mp", mp, 1))
         w_b, qkv_b, p_b, heads_out, w_heads, branch = call(
             front_last_kernel,
-            saved(256, ())[:3]
+            saved(256, 256, ())[:3]
             + [
                 ((count, 256 * mp), bf16),
                 ((width, 256 * mp), bf16),
@@ -757,7 +760,7 @@
         far_left, grad_low, joined_b = lax.optimization_barrier((far_left, grad_low, joined_b))
         early = swap_both(far_left[0], dp, mp, (0, 2), (1, 0))
         sent_grads, joined_c = back_of(0, 1, grad_low)
-        early, grad_low, joined_c = lax.optimization_barrier((early, grad_low, joined_c))
+        grad_low, joined_c = lax.optimization_barrier((grad_low, joined_c))
         other = swap(sent_grads, "mp", mp, 1)
         kept_grads, joined_d = back_of(0, 0, grad_low)
         part_shape = ((high, d_rows, 4 * part), bf16)

time: 175 us -> 168 us (0.960)
  Pallas kernels: 60.2 us -> 48.6 us
  starting transfers between devices: 26.2 us -> 29 us
    pallas_call x17, Pallas kernels: 57.8 us -> 46.1 us  [call(): pl.pallas_call(functools.partial(kernel, **static), out_shape=[jax.ShapeD...]
    ppermute x7, waiting for transfers between devices: 9.4 us -> 14.5 us  [swap_both(): return lax.ppermute(array_in, ('dp', 'mp'), pairs)]
    ppermute x24, waiting for transfers between devices: 47.6 us -> 44 us  [swap(): lax.ppermute(array_in, axis_name, [(i, i ^ bit) for i in range(size)])]
    ppermute x24, starting transfers between devices: 18.8 us -> 21.8 us  [swap(): lax.ppermute(array_in, axis_name, [(i, i ^ bit) for i in range(size)])]
  transfers between devices with their start and end apart: 31 -> 31, of which waited for: 16 -> 19; matrix products, arithmetic and copies ran while one was open for 3% -> 4% of each run, Pallas kernels for 18% -> 14%
where the time goes in v7:
time: 168 us; the launch traced here: 167 us
  waiting for transfers between devices  58.5 us (35%)
  Pallas kernels  48.6 us (29%)
  starting transfers between devices  29 us (17%)
  blocking collectives  21.9 us (13%)
  other arithmetic  4.33 us (3%)
  matrix products  3.84 us (2%)
    pallas_call x17, Pallas kernels, call(): pl.pallas_call(functools.partial(kernel, **static), out_shape=[jax.ShapeD...  46.1 us
    ppermute x24, waiting for transfers between devices, swap(): lax.ppermute(array_in, axis_name, [(i, i ^ bit) for i in range(size)])  44 us
    ppermute x24, starting transfers between devices, swap(): lax.ppermute(array_in, axis_name, [(i, i ^ bit) for i in range(size)])  21.8 us
    ppermute x7, waiting for transfers between devices, swap_both(): return lax.ppermute(array_in, ('dp', 'mp'), pairs)  14.5 us
    all_to_all x1, blocking collectives, per_device(): got = lax.all_to_all(got, 'dp', split_axis=0, concat_axis=0, tiled=True)  12.4 us
    all_to_all x1, blocking collectives, per_device(): back = lax.all_to_all(back, 'dp', split_axis=0, concat_axis=0, tiled=True)  9.51 us
    ppermute x7, starting transfers between devices, swap_both(): return lax.ppermute(array_in, ('dp', 'mp'), pairs)  7.21 us
    dot_general x2, matrix products, mm_tn(): lax.dot_general(a, b, (((0,), (0,)), ((), ())), preferred_element_type=f32)  3.84 us
  transfers between devices with their start and end apart: 31, of which 19 were waited for; matrix products, arithmetic and copies ran while one was open for 4% of the time, Pallas kernels for 14%

profile of v7, /device:TPU:0, one launch (start us, length us, event | category | flops | bytes accessed | tf_op | source)
XLA Modules:
  0.0 167.3 jit_solution(12637913041194757797)
XLA Ops:
  1.2 2.4 %pack.1 = (bf16[96,384]{1,0:T(8,128)(2,1)}, bf16[96,384]{1,0:T(8,128)(2,1)}, bf16[96,128]{1,0:T(8,128)(2,1)}) custom-call(s32[3]{0:T(128)} %pad_add_fusion.me_ref, bf16[3,96,192]{2,1,0:T(8,128)(2,1)} %bitcast.104, bf16[192,96]{1,0:T(8,128)(2,1)} %out_hbm.1, bf16[1,96]{1,0:T(2,128)(2,1)} %bitcast.110, bf16[1,96]{1,0:T(2,128)(2,1)} %bitcast.111, ...), custom_call_target="tpu_custom_call" | custom-call | tf_op jit(solution)/shard_map/pack/pallas_call | solution.py:570
  3.7 4.1 %collective-permute-start = (bf16[1,96,384]{2,1,0:T(8,128)(2,1)}, bf16[1,96,384]{2,1,0:T(8,128)(2,1)S(1)}, u32[]{:S(2)}, u32[]{:S(2)}) collective-permute-start(bf16[1,96,384]{2,1,0:T(8,128)(2,1)} %bitcast.98), channel_id=1, source_target_pairs={{0,16},{4,20},{8,24},{12,28},{16,0},{20,4},{24,8},{28,12},{1,17},{... | collective-permute-start | bytes 221192 | tf_op jit(solution)/shard_map/ppermute | solution.py:24
  7.8 4.1 %collective-permute-done = bf16[1,96,384]{2,1,0:T(8,128)(2,1)S(1)} collective-permute-done((bf16[1,96,384]{2,1,0:T(8,128)(2,1)}, bf16[1,96,384]{2,1,0:T(8,128)(2,1)S(1)}, u32[]{:S(2)}, u32[]{:S(2)}) %collective-permute-start) | collective-permute-done | bytes 73760 | tf_op jit(solution)/shard_map/ppermute | solution.py:24
  13.7 3.3 %collective-permute-start.3 = (bf16[1,96,128]{2,1,0:T(8,128)(2,1)}, bf16[1,96,128]{2,1,0:T(8,128)(2,1)S(1)}, u32[]{:S(2)}, u32[]{:S(2)}) collective-permute-start(bf16[1,96,128]{2,1,0:T(8,128)(2,1)} %bitcast.106), channel_id=1, source_target_pairs={{0,16},{4,20},{8,24},{12,28},{16,0},{20,4},{24,8},{28,12},{1,17},{... | collective-permute-start | bytes 73736 | tf_op jit(solution)/shard_map/ppermute | solution.py:24
  22.5 3.4 %collective-permute-done.4 = bf16[2,96,128]{2,1,0:T(8,128)(2,1)S(1)} collective-permute-done((bf16[2,96,128]{2,1,0:T(8,128)(2,1)S(1)}, bf16[2,96,128]{2,1,0:T(8,128)(2,1)S(1)}, u32[]{:S(2)}, u32[]{:S(2)}) %collective-permute-start.4) | collective-permute-done | bytes 49184 | tf_op jit(solution)/shard_map/ppermute | solution.py:24
  28.6 2.2 %collective-permute-start.7 = (bf16[1,96,384]{2,1,0:T(8,128)(2,1)S(1)}, bf16[1,96,384]{2,1,0:T(8,128)(2,1)S(1)}, u32[]{:S(2)}, u32[]{:S(2)}) collective-permute-start(bf16[1,96,384]{2,1,0:T(8,128)(2,1)S(1)} %bitcast.95), channel_id=1, source_target_pairs={{0,16},{4,20},{8,24},{12,28},{16,0},{20,4},{24,8},{28,12},{1,17},{... | collective-permute-start | bytes 221192 | tf_op jit(solution)/shard_map/ppermute | solution.py:24
  31.9 2.0 %collective-permute-done.7 = bf16[1,96,384]{2,1,0:T(8,128)(2,1)S(1)} collective-permute-done((bf16[1,96,384]{2,1,0:T(8,128)(2,1)S(1)}, bf16[1,96,384]{2,1,0:T(8,128)(2,1)S(1)}, u32[]{:S(2)}, u32[]{:S(2)}) %collective-permute-start.7) | collective-permute-done | bytes 73760 | tf_op jit(solution)/shard_map/ppermute | solution.py:24
  39.2 2.3 %collective-permute-start.9 = (bf16[4,96,384]{2,1,0:T(8,128)(2,1)S(1)}, bf16[4,96,384]{2,1,0:T(8,128)(2,1)S(1)}, u32[]{:S(2)}, u32[]{:S(2)}) collective-permute-start(bf16[4,96,384]{2,1,0:T(8,128)(2,1)S(1)} %get-tuple-element.151), channel_id=1, source_target_pairs={{0,4},{1,3},{2,6},{3,1},{4,0},{5,7},{6,2},{7,5},{8,12},{9,11},{10,... | collective-permute-start | bytes 884744 | tf_op jit(solution)/shard_map/ppermute | solution.py:33
  41.5 5.2 %collective-permute-done.9 = bf16[4,96,384]{2,1,0:T(8,128)(2,1)S(1)} collective-permute-done((bf16[4,96,384]{2,1,0:T(8,128)(2,1)S(1)}, bf16[4,96,384]{2,1,0:T(8,128)(2,1)S(1)}, u32[]{:S(2)}, u32[]{:S(2)}) %collective-permute-start.9) | collective-permute-done | bytes 294944 | tf_op jit(solution)/shard_map/ppermute | solution.py:33
  47.0 6.0 %front_pair.1 = (bf16[4,768,384]{2,1,0:T(8,128)(2,1)S(1)}, bf16[4,624,384]{2,1,0:T(8,128)(2,1)S(1)}, bf16[4,3,2,208,208]{4,3,2,1,0:T(8,128)(2,1)S(1)}, bf16[4,624,128]{2,1,0:T(8,128)(2,1)S(1)}) custom-call(s32[3]{0:T(128)S(1)} %copy-done, bf16[624,768]{1,0:T(8,128)(2,1)S(1)} %get-tuple-element.85.h_ref, s32[12,200]{1,0:T(8,128)S(1)} %copy-done.5, ...), custom_call_target="tpu_custom_call" | custom-call | flops 11000000512 | bytes 3327372 | tf_op jit(solution)/shard_map/front_pair/pallas_call | solution.py:527
  52.9 3.8 %collective-permute-done.10.refs_1_ = bf16[2,4,96,384]{3,2,1,0:T(8,128)(2,1)S(1)} collective-permute-done((bf16[2,4,96,384]{3,2,1,0:T(8,128)(2,1)S(1)}, bf16[2,4,96,384]{3,2,1,0:T(8,128)(2,1)S(1)}, u32[]{:S(2)}, u32[]{:S(2)}) %collective-permute-start.10) | collective-permute-done | bytes 589856 | tf_op jit(solution)/shard_map/ppermute | solution.py:33
  56.7 2.0 %collective-permute-done.14.refs_3_ = bf16[2,4,96,384]{3,2,1,0:T(8,128)(2,1)S(1)} collective-permute-done((bf16[2,4,96,384]{3,2,1,0:T(8,128)(2,1)S(1)}, bf16[2,4,96,384]{3,2,1,0:T(8,128)(2,1)S(1)}, u32[]{:S(2)}, u32[]{:S(2)}) %collective-permute-start.14) | collective-permute-done | bytes 589856 | tf_op jit(solution)/shard_map/ppermute | solution.py:24
  58.7 5.2 %front_last.1 = (bf16[4,768,256]{2,1,0:T(8,128)(2,1)S(1)}, bf16[4,624,256]{2,1,0:T(8,128)(2,1)S(1)}, bf16[4,3,208,208]{3,2,1,0:T(8,128)(2,1)S(1)}, bf16[624,1024...) custom-call(s32[3]{0:T(128)S(1)} %copy-done, ...), custom_call_target="tpu_custom_call" | custom-call | flops 7699999744 | bytes 3966348 | tf_op jit(solution)/shard_map/front_last/pallas_call | solution.py:527
  63.9 2.7 %route.1 = (f32[624,768]{1,0:T(8,128)S(1)}, bf16[624,768]{1,0:T(8,128)(2,1)S(1)}, f32[2,3,8,208]{3,2,1,0:T(8,128)S(1)}, bf16[64,768]{1,0:T(8,128)(2,1)S(1)}, f32[3,1,128]{2,1,0:T(1,128)S(1)}) custom-call(s32[3]{0:T(128)S(1)} %copy-done, bf16[3,200,768]{2,1,0:T(8,128)(2,1)S(1)} %bitcast.86, f32[624,768]{1,0:T(8,128)S(1)} %get-tuple-element.91.br_ref, ...), custom_call_target="tpu_custom_call" | custom-call | flops 2200000000 | bytes 4162956 | tf_op jit(solution)/shard_map/route/pallas_call | solution.py:527
  66.6 12.4 %all_to_all.10 = bf16[8,8,768]{2,1,0:T(8,128)(2,1)S(1)} all-to-all(bf16[8,8,768]{2,1,0:T(8,128)(2,1)S(1)} %bitcast.80), channel_id=1, replica_groups=mesh['dp'=8,'mp'=4] {'dp'}, dimensions={0} | all-to-all | bytes 196608 | tf_op jit(solution)/shard_map/all_to_all | solution.py:678
  79.4 4.2 %collective-permute-done.15 = bf16[1,8,8,768]{3,2,1,0:T(8,128)(2,1)S(1)} collective-permute-done((bf16[1,8,8,768]{3,2,1,0:T(8,128)(2,1)S(1)}, bf16[1,8,8,768]{3,2,1,0:T(8,128)(2,1)S(1)}, u32[]{:S(2)}, u32[]{:S(2)}) %collective-permute-start.15) | collective-permute-done | bytes 98336 | tf_op jit(solution)/shard_map/ppermute | solution.py:24
  89.0 4.4 %collective-permute-done.18 = bf16[1,1,8,8,768]{4,3,2,1,0:T(8,128)(2,1)S(1)} collective-permute-done((bf16[1,1,8,8,768]{4,3,2,1,0:T(8,128)(2,1)S(1)}, bf16[1,1,8,8,768]{4,3,2,1,0:T(8,128)(2,1)S(1)}, u32[]{:S(2)}, u32[]{:S(2)}) %collective-permute-start.18) | collective-permute-done | bytes 98336 | tf_op jit(solution)/shard_map/ppermute | solution.py:24
  93.4 9.5 %all_to_all.11 = bf16[8,8,768]{2,1,0:T(8,128)(2,1)S(1)} all-to-all(bf16[8,8,768]{2,1,0:T(8,128)(2,1)S(1)} %fusion.5), channel_id=1, replica_groups=mesh['dp'=8,'mp'=4] {'dp'}, dimensions={0} | all-to-all | bytes 196608 | tf_op jit(solution)/shard_map/all_to_all | solution.py:698
  103.0 3.9 %mix.1 = (bf16[3,200,768]{2,1,0:T(8,128)(2,1)}, f32[624,768]{1,0:T(8,128)S(1)}, bf16[624,768]{1,0:T(8,128)(2,1)S(1)}, bf16[768,624]{1,0:T(8,128)(2,1)S(1)}, f32[13,768]{1,0:T(8,128)S(1)}) custom-call(s32[3]{0:T(128)S(1)} %copy-done, f32[624,768]{1,0:T(8,128)S(1)} %get-tuple-element.93.res_ref, bf16[624,768]{1,0:T(8,128)(2,1)S(1)} %get-tuple-element.94.h_ref, ...), custom_call_target="tpu_custom_call" | custom-call | flops 5500000256 | bytes 4315020 | tf_op jit(solution)/shard_map/mix/pallas_call | solution.py:527
  106.9 3.7 %back.4 = (bf16[2,4,96,768]{3,2,1,0:T(8,128)(2,1)S(1)}, bf16[624,640]{1,0:T(8,128)(2,1)S(1)}) custom-call(s32[3]{0:T(128)S(1)} %copy-done, bf16[624,768]{1,0:T(8,128)(2,1)S(1)} %get-tuple-element.124.gb_ref, bf16[768,624]{1,0:T(8,128)(2,1)S(1)} %get-tuple-element.105.gbt_ref, bf16[768,624]{1,0:T(8,128)(2,1)S(1)} %get-tuple-element.106.ht_ref, ...), custom_call_target="tpu_custom_call" | custom-call | flops 8800000000 | bytes 12036108 | tf_op jit(solution)/shard_map/back/pallas_call | solution.py:527
  110.7 3.7 %back.5 = (bf16[2,4,96,768]{3,2,1,0:T(8,128)(2,1)S(1)}, bf16[624,640]{1,0:T(8,128)(2,1)S(1)}) custom-call(s32[3]{0:T(128)S(1)} %copy-done, bf16[624,768]{1,0:T(8,128)(2,1)S(1)} %get-tuple-element.124.gb_ref, bf16[768,624]{1,0:T(8,128)(2,1)S(1)} %get-tuple-element.105.gbt_ref, bf16[768,624]{1,0:T(8,128)(2,1)S(1)} %get-tuple-element.106.ht_ref, ...), custom_call_target="tpu_custom_call" | custom-call | flops 8800000000 | bytes 12036108 | tf_op jit(solution)/shard_map/back/pallas_call | solution.py:527
  114.7 3.7 %back.6 = (bf16[2,4,96,768]{3,2,1,0:T(8,128)(2,1)S(1)}, bf16[624,640]{1,0:T(8,128)(2,1)S(1)}) custom-call(s32[3]{0:T(128)S(1)} %copy-done, bf16[624,768]{1,0:T(8,128)(2,1)S(1)} %get-tuple-element.124.gb_ref, bf16[768,624]{1,0:T(8,128)(2,1)S(1)} %get-tuple-element.105.gbt_ref, bf16[768,624]{1,0:T(8,128)(2,1)S(1)} %get-tuple-element.106.ht_ref, ...), custom_call_target="tpu_custom_call" | custom-call | flops 8800000000 | bytes 12036108 | tf_op jit(solution)/shard_map/back/pallas_call | solution.py:527
  119.3 3.9 %back.7 = (bf16[2,4,96,768]{3,2,1,0:T(8,128)(2,1)S(1)}, bf16[624,640]{1,0:T(8,128)(2,1)S(1)}) custom-call(s32[3]{0:T(128)S(1)} %copy-done, bf16[624,768]{1,0:T(8,128)(2,1)S(1)} %get-tuple-element.124.gb_ref, bf16[768,624]{1,0:T(8,128)(2,1)S(1)} %get-tuple-element.105.gbt_ref, bf16[768,624]{1,0:T(8,128)(2,1)S(1)} %get-tuple-element.106.ht_ref, ...), custom_call_target="tpu_custom_call" | custom-call | flops 8800000000 | bytes 12036108 | tf_op jit(solution)/shard_map/back/pallas_call | solution.py:527
  123.3 5.5 %collective-permute-done.21.early_ref = bf16[4,96,768]{2,1,0:T(8,128)(2,1)S(1)} collective-permute-done((bf16[4,96,768]{2,1,0:T(8,128)(2,1)S(1)}, bf16[4,96,768]{2,1,0:T(8,128)(2,1)S(1)}, u32[]{:S(2)}, u32[]{:S(2)}) %collective-permute-start.21) | collective-permute-done | bytes 589856 | tf_op jit(solution)/shard_map/ppermute | solution.py:33
  130.7 6.5 %last.1 = (f32[3,200,768]{2,1,0:T(8,128)}, f32[13,768]{1,0:T(8,128)S(1)}, f32[624,768]{1,0:T(8,128)}) custom-call(s32[3]{0:T(128)S(1)} %copy-done, bf16[3,200,768]{2,1,0:T(8,128)(2,1)S(1)} %bitcast.87, f32[624,768]{1,0:T(8,128)S(1)} %get-tuple-element.100.gres_ref, f32[128,768]{1,0:T(8,128)S(1)} %get-tuple-element.92.ex_ref, ...), custom_call_target="tpu_custom_call" | custom-call | flops 6600000000 | bytes 10398732 | tf_op jit(solution)/shard_map/last/pallas_call | solution.py:527
  137.6 5.1 %collective-permute-done.24 = f32[13,768]{1,0:T(8,128)S(1)} collective-permute-done((f32[13,768]{1,0:T(8,128)S(1)}, f32[13,768]{1,0:T(8,128)S(1)}, u32[]{:S(2)}, u32[]{:S(2)}) %collective-permute-start.24) | collective-permute-done | bytes 39968 | tf_op jit(solution)/shard_map/ppermute | solution.py:24
  143.3 3.9 %collective-permute-done.25 = f32[13,768]{1,0:T(8,128)S(1)} collective-permute-done((f32[13,768]{1,0:T(8,128)S(1)}, f32[13,768]{1,0:T(8,128)S(1)}, u32[]{:S(2)}, u32[]{:S(2)}) %collective-permute-start.25) | collective-permute-done | bytes 39968 | tf_op jit(solution)/shard_map/ppermute | solution.py:24
  148.4 3.4 %collective-permute-done.26 = f32[13,768]{1,0:T(8,128)S(1)} collective-permute-done((f32[13,768]{1,0:T(8,128)S(1)}, f32[13,768]{1,0:T(8,128)S(1)}, u32[]{:S(2)}, u32[]{:S(2)}) %collective-permute-start.26) | collective-permute-done | bytes 39968 | tf_op jit(solution)/shard_map/ppermute | solution.py:24
  151.8 2.0 %collective-permute-start.27 = (f32[13,768]{1,0:T(8,128)S(1)}, f32[13,768]{1,0:T(8,128)S(1)}, u32[]{:S(2)}, u32[]{:S(2)}) collective-permute-start(f32[13,768]{1,0:T(8,128)S(1)} %add.22), channel_id=1, source_target_pairs={{0,2},{1,3},{2,0},{3,1},{4,6},{5,7},{6,4},{7,5},{8,10},{9,11},{10,... | collective-permute-start | bytes 119816 | tf_op jit(solution)/shard_map/ppermute | solution.py:24
  153.8 1.9 %convolution_bitcast_fusion.1 = f32[1,768,768]{2,1,0:T(8,128)} fusion(bf16[256,768]{1,0:T(8,128)(2,1)S(1)} %bitcast.77, bf16[256,768]{1,0:T(8,128)(2,1)S(1)} %get-tuple-element.146), kind=kOutput, calls=%fused_computation.1 | convolution fusion | flops 301989888 | bytes 3145728 | tf_op jit(solution)/shard_map/dot_general | solution.py:86
  157.8 1.9 %convolution_bitcast_fusion = f32[1,768,768]{2,1,0:T(8,128)} fusion(bf16[256,768]{1,0:T(8,128)(2,1)S(1)} %get-tuple-element.147, bf16[256,768]{1,0:T(8,128)(2,1)S(1)} %get-tuple-element.148), kind=kOutput, calls=%fused_computation | convolution fusion | flops 301989888 | bytes 3145728 | tf_op jit(solution)/shard_map/dot_general | solution.py:86
  160.9 5.6 %collective-permute-done.30.other_ref = bf16[96,768]{1,0:T(8,128)(2,1)S(1)} collective-permute-done((bf16[96,768]{1,0:T(8,128)(2,1)S(1)}, bf16[96,768]{1,0:T(8,128)(2,1)S(1)}, u32[]{:S(2)}, u32[]{:S(2)}) %collective-permute-start.30) | collective-permute-done | bytes 147488 | tf_op jit(solution)/shard_map/ppermute | solution.py:24
  (88 shorter events, 32.5 us)
Async XLA Ops:
  3.7 24.9 %copy-start.6 = (bf16[96,384]{1,0:T(8,128)(2,1)S(1)}, bf16[96,384]{1,0:T(8,128)(2,1)}, u32[]{:S(2)}) copy-start(bf16[96,384]{1,0:T(8,128)(2,1)} %get-tuple-element.86) | copy-start | bytes 221188
  3.7 8.3 %collective-permute-start = (bf16[1,96,384]{2,1,0:T(8,128)(2,1)}, bf16[1,96,384]{2,1,0:T(8,128)(2,1)S(1)}, u32[]{:S(2)}, u32[]{:S(2)}) collective-permute-start(bf16[1,96,384]{2,1,0:T(8,128)(2,1)} %bitcast.98), channel_id=1, source_target_pairs={{0,16},{4,20},{8,24},{12,28},{16,0},{20,4},{24,8},{28,12},{1,17},{... | collective-permute-start | bytes 221192 | tf_op jit(solution)/shard_map/ppermute | solution.py:24
  12.9 5.5 %collective-permute-start.1 = (bf16[2,96,384]{2,1,0:T(8,128)(2,1)S(1)}, bf16[2,96,384]{2,1,0:T(8,128)(2,1)S(1)}, u32[]{:S(2)}, u32[]{:S(2)}) collective-permute-start(bf16[2,96,384]{2,1,0:T(8,128)(2,1)S(1)} %pad_maximum_fusion.7), channel_id=1, source_target_pairs={{0,8},{4,12},{8,0},{12,4},{16,24},{20,28},{24,16},{28,20},{1,9},{5... | collective-permute-start | bytes 442376 | tf_op jit(solution)/shard_map/ppermute | solution.py:24
  13.7 7.4 %collective-permute-start.3 = (bf16[1,96,128]{2,1,0:T(8,128)(2,1)}, bf16[1,96,128]{2,1,0:T(8,128)(2,1)S(1)}, u32[]{:S(2)}, u32[]{:S(2)}) collective-permute-start(bf16[1,96,128]{2,1,0:T(8,128)(2,1)} %bitcast.106), channel_id=1, source_target_pairs={{0,16},{4,20},{8,24},{12,28},{16,0},{20,4},{24,8},{28,12},{1,17},{... | collective-permute-start | bytes 73736 | tf_op jit(solution)/shard_map/ppermute | solution.py:24
  19.3 7.4 %collective-permute-start.2 = (bf16[4,96,384]{2,1,0:T(8,128)(2,1)S(1)}, bf16[4,96,384]{2,1,0:T(8,128)(2,1)S(1)}, u32[]{:S(2)}, u32[]{:S(2)}) collective-permute-start(bf16[4,96,384]{2,1,0:T(8,128)(2,1)S(1)} %get-tuple-element.153), channel_id=1, source_target_pairs={{0,4},{1,3},{2,6},{3,1},{4,0},{5,7},{6,2},{7,5},{8,12},{9,11},{10,... | collective-permute-start | bytes 884744 | tf_op jit(solution)/shard_map/ppermute | solution.py:33
  21.8 4.1 %collective-permute-start.4 = (bf16[2,96,128]{2,1,0:T(8,128)(2,1)S(1)}, bf16[2,96,128]{2,1,0:T(8,128)(2,1)S(1)}, u32[]{:S(2)}, u32[]{:S(2)}) collective-permute-start(bf16[2,96,128]{2,1,0:T(8,128)(2,1)S(1)} %pad_maximum_fusion.10), channel_id=1, source_target_pairs={{0,8},{4,12},{8,0},{12,4},{16,24},{20,28},{24,16},{28,20},{1,9},{5... | collective-permute-start | bytes 147464 | tf_op jit(solution)/shard_map/ppermute | solution.py:24
  26.8 10.3 %collective-permute-start.5 = (bf16[2,4,96,384]{3,2,1,0:T(8,128)(2,1)S(1)}, bf16[2,4,96,384]{3,2,1,0:T(8,128)(2,1)S(1)}, u32[]{:S(2)}, u32[]{:S(2)}) collective-permute-start(bf16[2,4,96,384]{3,2,1,0:T(8,128)(2,1)S(1)} %pad_maximum_fusion.refs_0_), channel_id=1, source_target_pairs={{0,2},{1,5},{2,0},{3,7},{4,6},{5,1},{6,4},{7,3},{8,10},{9,13},{10,... | collective-permute-start | bytes 1769480 | tf_op jit(solution)/shard_map/ppermute | solution.py:33
  28.6 5.4 %collective-permute-start.7 = (bf16[1,96,384]{2,1,0:T(8,128)(2,1)S(1)}, bf16[1,96,384]{2,1,0:T(8,128)(2,1)S(1)}, u32[]{:S(2)}, u32[]{:S(2)}) collective-permute-start(bf16[1,96,384]{2,1,0:T(8,128)(2,1)S(1)} %bitcast.95), channel_id=1, source_target_pairs={{0,16},{4,20},{8,24},{12,28},{16,0},{20,4},{24,8},{28,12},{1,17},{... | collective-permute-start | bytes 221192 | tf_op jit(solution)/shard_map/ppermute | solution.py:24
  30.8 4.6 %collective-permute-start.6 = (bf16[4,96,128]{2,1,0:T(8,128)(2,1)S(1)}, bf16[4,96,128]{2,1,0:T(8,128)(2,1)S(1)}, u32[]{:S(2)}, u32[]{:S(2)}) collective-permute-start(bf16[4,96,128]{2,1,0:T(8,128)(2,1)S(1)} %pad_maximum_fusion.9), channel_id=1, source_target_pairs={{0,4},{4,0},{8,12},{12,8},{16,20},{20,16},{24,28},{28,24},{1,5},{5... | collective-permute-start | bytes 294920 | tf_op jit(solution)/shard_map/ppermute | solution.py:24
  34.0 5.2 %collective-permute-start.8 = (bf16[2,96,384]{2,1,0:T(8,128)(2,1)S(1)}, bf16[2,96,384]{2,1,0:T(8,128)(2,1)S(1)}, u32[]{:S(2)}, u32[]{:S(2)}) collective-permute-start(bf16[2,96,384]{2,1,0:T(8,128)(2,1)S(1)} %pad_maximum_fusion.8), channel_id=1, source_target_pairs={{0,8},{4,12},{8,0},{12,4},{16,24},{20,28},{24,16},{28,20},{1,9},{5... | collective-permute-start | bytes 442376 | tf_op jit(solution)/shard_map/ppermute | solution.py:24
  35.3 11.6 %collective-permute-start.11 = (bf16[2,4,96,384]{3,2,1,0:T(8,128)(2,1)S(1)}, bf16[2,4,96,384]{3,2,1,0:T(8,128)(2,1)S(1)}, u32[]{:S(2)}, u32[]{:S(2)}) collective-permute-start(bf16[2,4,96,384]{3,2,1,0:T(8,128)(2,1)S(1)} %pad_maximum_fusion.refs_0_), channel_id=1, source_target_pairs={{0,1},{1,0},{2,3},{3,2},{4,5},{5,4},{6,7},{7,6},{8,9},{9,8},{10,11... | collective-permute-start | bytes 1769480 | tf_op jit(solution)/shard_map/ppermute | solution.py:24
  37.1 9.9 %collective-permute-start.12 = (bf16[2,4,96,384]{3,2,1,0:T(8,128)(2,1)S(1)}, bf16[2,4,96,384]{3,2,1,0:T(8,128)(2,1)S(1)}, u32[]{:S(2)}, u32[]{:S(2)}) collective-permute-start(bf16[2,4,96,384]{3,2,1,0:T(8,128)(2,1)S(1)} %collective-permute-done.5.refs_1_), channel_id=1, source_target_pairs={{0,1},{1,0},{2,3},{3,2},{4,5},{5,4},{6,7},{7,6},{8,9},{9,8},{10,11... | collective-permute-start | bytes 1769480 | tf_op jit(solution)/shard_map/ppermute | solution.py:24
  39.2 7.5 %collective-permute-start.9 = (bf16[4,96,384]{2,1,0:T(8,128)(2,1)S(1)}, bf16[4,96,384]{2,1,0:T(8,128)(2,1)S(1)}, u32[]{:S(2)}, u32[]{:S(2)}) collective-permute-start(bf16[4,96,384]{2,1,0:T(8,128)(2,1)S(1)} %get-tuple-element.151), channel_id=1, source_target_pairs={{0,4},{1,3},{2,6},{3,1},{4,0},{5,7},{6,2},{7,5},{8,12},{9,11},{10,... | collective-permute-start | bytes 884744 | tf_op jit(solution)/shard_map/ppermute | solution.py:33
  46.8 9.9 %collective-permute-start.10 = (bf16[2,4,96,384]{3,2,1,0:T(8,128)(2,1)S(1)}, bf16[2,4,96,384]{3,2,1,0:T(8,128)(2,1)S(1)}, u32[]{:S(2)}, u32[]{:S(2)}) collective-permute-start(bf16[2,4,96,384]{3,2,1,0:T(8,128)(2,1)S(1)} %pad_maximum_fusion.1.refs_0_), channel_id=1, source_target_pairs={{0,2},{1,5},{2,0},{3,7},{4,6},{5,1},{6,4},{7,3},{8,10},{9,13},{10,... | collective-permute-start | bytes 1769480 | tf_op jit(solution)/shard_map/ppermute | solution.py:33
  46.9 9.9 %collective-permute-start.13 = (bf16[2,4,96,384]{3,2,1,0:T(8,128)(2,1)S(1)}, bf16[2,4,96,384]{3,2,1,0:T(8,128)(2,1)S(1)}, u32[]{:S(2)}, u32[]{:S(2)}) collective-permute-start(bf16[2,4,96,384]{3,2,1,0:T(8,128)(2,1)S(1)} %pad_maximum_fusion.1.refs_0_), channel_id=1, source_target_pairs={{0,1},{1,0},{2,3},{3,2},{4,5},{5,4},{6,7},{7,6},{8,9},{9,8},{10,11... | collective-permute-start | bytes 1769480 | tf_op jit(solution)/shard_map/ppermute | solution.py:24
  56.7 2.0 %collective-permute-start.14 = (bf16[2,4,96,384]{3,2,1,0:T(8,128)(2,1)S(1)}, bf16[2,4,96,384]{3,2,1,0:T(8,128)(2,1)S(1)}, u32[]{:S(2)}, u32[]{:S(2)}) collective-permute-start(bf16[2,4,96,384]{3,2,1,0:T(8,128)(2,1)S(1)} %collective-permute-done.10.refs_1_), channel_id=1, source_target_pairs={{0,1},{1,0},{2,3},{3,2},{4,5},{5,4},{6,7},{7,6},{8,9},{9,8},{10,11... | collective-permute-start | bytes 1769480 | tf_op jit(solution)/shard_map/ppermute | solution.py:24
  79.0 4.6 %collective-permute-start.15 = (bf16[1,8,8,768]{3,2,1,0:T(8,128)(2,1)S(1)}, bf16[1,8,8,768]{3,2,1,0:T(8,128)(2,1)S(1)}, u32[]{:S(2)}, u32[]{:S(2)}) collective-permute-start(bf16[1,8,8,768]{3,2,1,0:T(8,128)(2,1)S(1)} %bitcast.92), channel_id=1, source_target_pairs={{0,2},{1,3},{2,0},{3,1},{4,6},{5,7},{6,4},{7,5},{8,10},{9,11},{10,... | collective-permute-start | bytes 294920 | tf_op jit(solution)/shard_map/ppermute | solution.py:24
  83.6 1.5 collective-permute-start.16
  86.9 1.5 collective-permute-start.17
  88.5 4.9 %collective-permute-start.18 = (bf16[1,1,8,8,768]{4,3,2,1,0:T(8,128)(2,1)S(1)}, bf16[1,1,8,8,768]{4,3,2,1,0:T(8,128)(2,1)S(1)}, u32[]{:S(2)}, u32[]{:S(2)}) collective-permute-start(bf16[1,1,8,8,768]{4,3,2,1,0:T(8,128)(2,1)S(1)} %slice_bitcast_fusion.2), channel_id=1, source_target_pairs={{0,2},{1,3},{2,0},{3,1},{4,6},{5,7},{6,4},{7,5},{8,10},{9,11},{10,... | collective-permute-start | bytes 294920 | tf_op jit(solution)/shard_map/ppermute | solution.py:24
  110.6 3.8 %collective-permute-start.19 = (bf16[2,4,96,768]{3,2,1,0:T(8,128)(2,1)S(1)}, bf16[2,4,96,768]{3,2,1,0:T(8,128)(2,1)S(1)}, u32[]{:S(2)}, u32[]{:S(2)}) collective-permute-start(bf16[2,4,96,768]{3,2,1,0:T(8,128)(2,1)S(1)} %get-tuple-element.117), channel_id=1, source_target_pairs={{0,1},{1,0},{2,3},{3,2},{4,5},{5,4},{6,7},{7,6},{8,9},{9,8},{10,11... | collective-permute-start | bytes 3538952 | tf_op jit(solution)/shard_map/ppermute | solution.py:24
  118.3 10.4 %collective-permute-start.20 = (bf16[2,4,96,768]{3,2,1,0:T(8,128)(2,1)S(1)}, bf16[2,4,96,768]{3,2,1,0:T(8,128)(2,1)S(1)}, u32[]{:S(2)}, u32[]{:S(2)}) collective-permute-start(bf16[2,4,96,768]{3,2,1,0:T(8,128)(2,1)S(1)} %get-tuple-element.129), channel_id=1, source_target_pairs={{0,1},{1,0},{2,3},{3,2},{4,5},{5,4},{6,7},{7,6},{8,9},{9,8},{10,11... | collective-permute-start | bytes 3538952 | tf_op jit(solution)/shard_map/ppermute | solution.py:24
  118.9 9.9 %collective-permute-start.21 = (bf16[4,96,768]{2,1,0:T(8,128)(2,1)S(1)}, bf16[4,96,768]{2,1,0:T(8,128)(2,1)S(1)}, u32[]{:S(2)}, u32[]{:S(2)}) collective-permute-start(bf16[4,96,768]{2,1,0:T(8,128)(2,1)S(1)} %bitcast.88), channel_id=1, source_target_pairs={{0,2},{1,5},{2,0},{3,7},{4,6},{5,1},{6,4},{7,3},{8,10},{9,13},{10,... | collective-permute-start | bytes 1769480 | tf_op jit(solution)/shard_map/ppermute | solution.py:33
  129.9 17.3 %collective-permute-start.22 = (bf16[4,96,768]{2,1,0:T(8,128)(2,1)S(1)}, bf16[4,96,768]{2,1,0:T(8,128)(2,1)S(1)}, u32[]{:S(2)}, u32[]{:S(2)}) collective-permute-start(bf16[4,96,768]{2,1,0:T(8,128)(2,1)S(1)} %get-tuple-element.132), channel_id=1, source_target_pairs={{0,2},{1,5},{2,0},{3,7},{4,6},{5,1},{6,4},{7,3},{8,10},{9,13},{10,... | collective-permute-start | bytes 1769480 | tf_op jit(solution)/shard_map/ppermute | solution.py:33
  130.4 16.8 %collective-permute-start.23 = (bf16[4,96,768]{2,1,0:T(8,128)(2,1)S(1)}, bf16[4,96,768]{2,1,0:T(8,128)(2,1)S(1)}, u32[]{:S(2)}, u32[]{:S(2)}) collective-permute-start(bf16[4,96,768]{2,1,0:T(8,128)(2,1)S(1)} %get-tuple-element.133), channel_id=1, source_target_pairs={{0,4},{1,3},{2,6},{3,1},{4,0},{5,7},{6,2},{7,5},{8,12},{9,11},{10,... | collective-permute-start | bytes 1769480 | tf_op jit(solution)/shard_map/ppermute | solution.py:33
  137.2 5.5 %collective-permute-start.24 = (f32[13,768]{1,0:T(8,128)S(1)}, f32[13,768]{1,0:T(8,128)S(1)}, u32[]{:S(2)}, u32[]{:S(2)}) collective-permute-start(f32[13,768]{1,0:T(8,128)S(1)} %get-tuple-element.135), channel_id=1, source_target_pairs={{0,16},{4,20},{8,24},{12,28},{16,0},{20,4},{24,8},{28,12},{1,17},{... | collective-permute-start | bytes 119816 | tf_op jit(solution)/shard_map/ppermute | solution.py:24
  142.7 4.5 %collective-permute-start.25 = (f32[13,768]{1,0:T(8,128)S(1)}, f32[13,768]{1,0:T(8,128)S(1)}, u32[]{:S(2)}, u32[]{:S(2)}) collective-permute-start(f32[13,768]{1,0:T(8,128)S(1)} %add.20), channel_id=1, source_target_pairs={{0,8},{4,12},{8,0},{12,4},{16,24},{20,28},{24,16},{28,20},{1,9},{5... | collective-permute-start | bytes 119816 | tf_op jit(solution)/shard_map/ppermute | solution.py:24
  147.4 8.6 %collective-permute-start.29 = (bf16[2,96,768]{2,1,0:T(8,128)(2,1)S(1)}, bf16[2,96,768]{2,1,0:T(8,128)(2,1)S(1)}, u32[]{:S(2)}, u32[]{:S(2)}) collective-permute-start(bf16[2,96,768]{2,1,0:T(8,128)(2,1)S(1)} %get-tuple-element.139), channel_id=1, source_target_pairs={{0,8},{4,12},{8,0},{12,4},{16,24},{20,28},{24,16},{28,20},{1,9},{5... | collective-permute-start | bytes 884744 | tf_op jit(solution)/shard_map/ppermute | solution.py:24
  147.7 4.1 %collective-permute-start.26 = (f32[13,768]{1,0:T(8,128)S(1)}, f32[13,768]{1,0:T(8,128)S(1)}, u32[]{:S(2)}, u32[]{:S(2)}) collective-permute-start(f32[13,768]{1,0:T(8,128)S(1)} %add.21), channel_id=1, source_target_pairs={{0,4},{4,0},{8,12},{12,8},{16,20},{20,16},{24,28},{28,24},{1,5},{5... | collective-permute-start | bytes 119816 | tf_op jit(solution)/shard_map/ppermute | solution.py:24
  151.8 4.1 %collective-permute-start.27 = (f32[13,768]{1,0:T(8,128)S(1)}, f32[13,768]{1,0:T(8,128)S(1)}, u32[]{:S(2)}, u32[]{:S(2)}) collective-permute-start(f32[13,768]{1,0:T(8,128)S(1)} %add.22), channel_id=1, source_target_pairs={{0,2},{1,3},{2,0},{3,1},{4,6},{5,7},{6,4},{7,5},{8,10},{9,11},{10,... | collective-permute-start | bytes 119816 | tf_op jit(solution)/shard_map/ppermute | solution.py:24
  156.0 3.7 %collective-permute-start.28 = (f32[13,768]{1,0:T(8,128)S(1)}, f32[13,768]{1,0:T(8,128)S(1)}, u32[]{:S(2)}, u32[]{:S(2)}) collective-permute-start(f32[13,768]{1,0:T(8,128)S(1)} %add.23.own_ref), channel_id=1, source_target_pairs={{0,1},{1,0},{2,3},{3,2},{4,5},{5,4},{6,7},{7,6},{8,9},{9,8},{10,11... | collective-permute-start | bytes 119816 | tf_op jit(solution)/shard_map/ppermute | solution.py:24
  156.1 10.4 %collective-permute-start.30 = (bf16[96,768]{1,0:T(8,128)(2,1)S(1)}, bf16[96,768]{1,0:T(8,128)(2,1)S(1)}, u32[]{:S(2)}, u32[]{:S(2)}) collective-permute-start(bf16[96,768]{1,0:T(8,128)(2,1)S(1)} %bitcast.89), channel_id=1, source_target_pairs={{0,16},{4,20},{8,24},{12,28},{16,0},{20,4},{24,8},{28,12},{1,17},{... | collective-permute-start | bytes 442376 | tf_op jit(solution)/shard_map/ppermute | solution.py:24
  (6 other events, 102.1 us)

commit v8 on v7

--- a/solution.py
+++ b/solution.py
@@ -132,31 +132,42 @@
     extra_ref[...] = jnp.concatenate(columns, 0).T.astype(bf16)
 
 
-def fold_kernel(*refs, halves):
+def fold_kernel(*refs, halves, starts):
     terms, (kept_ref, left_ref) = refs[:-2], refs[-2:]
-    size = terms[0].shape[0]
+    size, columns = terms[0].shape[0], kept_ref.shape[-1]
     for k in range(size):
-        total = terms[0][k].astype(f32)
-        for term in terms[1:]:
-            total = total + term[k].astype(f32)
+        total = None
+        for term, start in zip(terms, starts):
+            value = term[k][..., start : start + columns].astype(f32)
+            total = value if total is None else total + value
         at, odd = (k % (size // 2), k >= size // 2) if halves else (k // 2, k % 2 == 1)
         (left_ref if odd else kept_ref)[at] = total.astype(bf16)
 
 
-def blend_kernel(me_ref, far_ref, kept_ref, other_ref, early_ref, near_ref, second_ref, third_ref):
-    near = [kept_ref[k].astype(f32) + other_ref[k].astype(f32) for k in (0, 1)]
-    near_ref[...] = near[0].astype(bf16)
+def blend_kernel(me_ref, far_ref, kept_ref, other_ref, near_ref, own_ref, second_ref):
+    for k, ref in ((0, near_ref), (1, own_ref)):
+        ref[...] = (kept_ref[k].astype(f32) + other_ref[k].astype(f32)).astype(bf16)
     first_core = me_ref[1] == 0
 
     @pl.when(first_core)
     def _():
         second_ref[...] = far_ref[...]
-        third_ref[...] = (near[1] + early_ref[...].astype(f32)).astype(bf16)
 
     @pl.when(jnp.logical_not(first_core))
     def _():
-        second_ref[...] = near[1].astype(bf16)
-        third_ref[...] = (far_ref[...].astype(f32) + early_ref[...].astype(f32)).astype(bf16)
+        second_ref[...] = own_ref[...]
+
+
+def blend_late_kernel(me_ref, far_ref, own_ref, early_ref, *thirds):
+    columns = thirds[0].shape[-1]
+    for core, ref in ((0, own_ref), (1, far_ref)):
+
+        @pl.when(me_ref[1] == core)
+        def _(ref=ref):
+            for k, third in enumerate(thirds):
+                at = slice(k * columns, (k + 1) * columns)
+                total = ref[..., at].astype(f32) + early_ref[..., at].astype(f32)
+                third[...] = total.astype(bf16)
 
 
 def finish_kernel(me_ref, own_ref, other_ref, one_ref, two_ref, router_ref, root_ref):
@@ -172,14 +183,14 @@
     root_ref[...] = mine[experts + 2 : experts + 5, :images]
 
 
-def unpack_kernel(own_ref, other_ref, qkv_ref, out_ref):
+def unpack_kernel(own_a, other_a, own_b, other_b, qkv_ref, out_ref):
     low, mid = 2 * HEAD_DIM, qkv_ref.shape[2]
-    summed = own_ref[...].astype(f32) + other_ref[...].astype(f32)
+    pair = own_a[...].astype(f32) + other_a[...].astype(f32)
+    rest = own_b[...].astype(f32) + other_b[...].astype(f32)
     for c in range(3):
-        qkv_ref[c, :, :low] = summed[:, c * low : (c + 1) * low]
-        start = 3 * low + c * HEAD_DIM
-        qkv_ref[c, :, low:mid] = summed[:, start : start + HEAD_DIM]
-    out_ref[...] = jnp.concatenate([summed[:, 640:], summed[:, 576:640]], axis=1).T
+        qkv_ref[c, :, :low] = pair[:, c * low : (c + 1) * low]
+        qkv_ref[c, :, low:mid] = rest[:, c * HEAD_DIM : (c + 1) * HEAD_DIM]
+    out_ref[...] = jnp.concatenate([rest[:, 256:], rest[:, 192:256]], axis=1).T
 
 
 def length_of(mask_ref, me_ref, b, images):
@@ -581,10 +592,13 @@
         for bit in bits_of(dp)[:-1]:
             first = jnp.concatenate([first, swap(first, "dp", dp, bit)])
             held_extra = jnp.concatenate([held_extra, swap(held_extra, "dp", dp, bit)])
+        stages = bits_of(dp)[:-1]
+        second = jnp.concatenate([second, swap(second, "dp", dp, stages[0])])
+        other, held_extra, second = lax.optimization_barrier(
+            (swap_both(first, dp, mp, (1, 0), (0, 2)), held_extra, second)
+        )
+        for bit in stages[1:]:
             second = jnp.concatenate([second, swap(second, "dp", dp, bit)])
-        other, held_extra = lax.optimization_barrier(
-            (swap_both(first, dp, mp, (1, 0), (0, 2)), held_extra)
-        )
         held_extra = jnp.concatenate([held_extra, swap(held_extra, "dp", dp, 1)])
         held_extra = held_extra.reshape((dp,) + extra.shape)
         if ready:
@@ -602,9 +616,11 @@
         )
         near = jnp.stack([first, other])
         far = swap_both(near, dp, mp, (0, 2), (1, 0))
-        far, h_one = lax.optimization_barrier((far, h_one))
+        second = second.reshape((high, d_rows, half))
+        other = swap_both(second, dp, mp, (1, 0), (0, 2))
+        far, h_one, other = lax.optimization_barrier((far, h_one, other))
         first = (near, far, swap(near, "mp", mp, 1), swap(far, "mp", mp, 1))
-        near = jnp.stack([second, swap_both(second, dp, mp, (1, 0), (0, 2))])
+        near = jnp.stack([second, other])
         second_near, second_far = near, swap_both(near, dp, mp, (0, 2), (1, 0))
         second_near_other = swap(second_near, "mp", mp, 1)
 
@@ -737,9 +753,9 @@
                 grads = grads.reshape(high, 2, d_rows, 4 * part).transpose(1, 0, 2, 3)
             return grads, joined
 
-        def fold(terms, halves):
+        def fold(terms, halves, starts=None, kept_columns=4 * part):
             size = terms[0].shape
-            kept = ((size[0] // 2,) + size[1:], bf16)
+            kept = ((size[0] // 2,) + size[1:-1] + (kept_columns,), bf16)
             return call(
                 fold_kernel,
                 [kept, kept],
@@ -749,6 +765,7 @@
                 scalars=0,
                 grant=6,
                 halves=halves,
+                starts=starts or (0,) * len(terms),
             )
 
         order = ((1, 1), (1, 0), (0, 1), (0, 0))
@@ -764,16 +781,24 @@
         other = swap(sent_grads, "mp", mp, 1)
         kept_grads, joined_d = back_of(0, 0, grad_low)
         part_shape = ((high, d_rows, 4 * part), bf16)
-        near_sum, second, third = call(
+        near_sum, own_sum, second = call(
             blend_kernel,
             [part_shape] * 3,
-            (words, far_kept[0], kept_grads, other, early),
+            (words, far_kept[0], kept_grads, other),
             flops=cost(1),
             name="blend",
             grant=8,
         )
         second = swap_both(second, dp, mp, (0, 2), (1, 0))
-        third = swap_both(third, dp, mp, (1, 0), (0, 2))
+        thirds = call(
+            blend_late_kernel,
+            [((high, d_rows, half), bf16)] * 2,
+            (words, far_kept[0], own_sum, early),
+            flops=cost(1),
+            name="blend_late",
+            grant=8,
+        )
+        thirds = [swap_both(third, dp, mp, (1, 0), (0, 2)) for third in thirds]
         grad_tokens, small, _ = call(
             last_kernel,
             [((images, seq, width), f32), ((experts + 5, width), f32), ((count, width), f32)],
@@ -787,15 +812,19 @@
         )
         for bit in bits_of(dp)[:-1]:
             small = small + swap(small, "dp", dp, bit)
-        kept, left = fold((near_sum, second, third), False)
-        left, small = lax.optimization_barrier((left, small))
-        for bit in bits_of(high)[:0:-1]:
-            kept, left = fold((kept, swap(left, "dp", dp, 2 * bit)), False)
-        own, other = kept[0], swap(left[0], "dp", dp, 2 * bits_of(high)[0])
+        parts = []
+        for k, third in enumerate(thirds):
+            starts = (k * half, k * half, 0)
+            kept, left = fold((near_sum, second, third), False, starts, half)
+            if k == 0:
+                left, small = lax.optimization_barrier((left, small))
+            for bit in bits_of(high)[:0:-1]:
+                kept, left = fold((kept, swap(left, "dp", dp, 2 * bit)), False, None, half)
+            parts += [kept[0], swap(left[0], "dp", dp, 2 * bits_of(high)[0])]
         grad_qkv, grad_out = call(
             unpack_kernel,
             [((3, d_rows, part), f32), ((part, d_rows), f32)],
-            (own, other),
+            parts,
             flops=cost(1),
             name="unpack",
             scalars=0,

time: 168 us -> 162 us (0.964)
  waiting for transfers between devices: 58.5 us -> 47.8 us
  starting transfers between devices: 29 us -> 34.2 us
  blocking collectives: 21.9 us -> 20.1 us
    ppermute x24 -> x26, waiting for transfers between devices: 44 us -> 38.1 us  [swap(): lax.ppermute(array_in, axis_name, [(i, i ^ bit) for i in range(size)])]
    ppermute x7 -> x8, waiting for transfers between devices: 14.5 us -> 9.69 us  [swap_both(): return lax.ppermute(array_in, ('dp', 'mp'), pairs)]
    ppermute x24 -> x26, starting transfers between devices: 21.8 us -> 25 us  [swap(): lax.ppermute(array_in, axis_name, [(i, i ^ bit) for i in range(size)])]
    ppermute x7 -> x8, starting transfers between devices: 7.21 us -> 9.26 us  [swap_both(): return lax.ppermute(array_in, ('dp', 'mp'), pairs)]
    all_to_all x1, blocking collectives: 12.4 us -> 10.6 us  [per_device(): got = lax.all_to_all(got, 'dp', split_axis=0, concat_axis=0, tiled=True)]
    pallas_call x17 -> x20, Pallas kernels: 46.1 us -> 46.4 us  [call(): pl.pallas_call(functools.partial(kernel, **static), out_shape=[jax.ShapeD...]
  transfers between devices with their start and end apart: 31 -> 34, of which waited for: 19 -> 19; matrix products, arithmetic and copies ran while one was open for 4% -> 5% of each run, Pallas kernels for 14% -> 15%
where the time goes in v8:
time: 162 us; the launch traced here: 161 us
  Pallas kernels  48.9 us (30%)
  waiting for transfers between devices  47.8 us (30%)
  starting transfers between devices  34.2 us (21%)
  blocking collectives  20.1 us (12%)
  other arithmetic  5.15 us (3%)
  matrix products  3.84 us (2%)
    pallas_call x20, Pallas kernels, call(): pl.pallas_call(functools.partial(kernel, **static), out_shape=[jax.ShapeD...  46.4 us
    ppermute x26, waiting for transfers between devices, swap(): lax.ppermute(array_in, axis_name, [(i, i ^ bit) for i in range(size)])  38.1 us
    ppermute x26, starting transfers between devices, swap(): lax.ppermute(array_in, axis_name, [(i, i ^ bit) for i in range(size)])  25 us
    all_to_all x1, blocking collectives, per_device(): got = lax.all_to_all(got, 'dp', split_axis=0, concat_axis=0, tiled=True)  10.6 us
    ppermute x8, waiting for transfers between devices, swap_both(): return lax.ppermute(array_in, ('dp', 'mp'), pairs)  9.69 us
    all_to_all x1, blocking collectives, per_device(): back = lax.all_to_all(back, 'dp', split_axis=0, concat_axis=0, tiled=True)  9.51 us
    ppermute x8, starting transfers between devices, swap_both(): return lax.ppermute(array_in, ('dp', 'mp'), pairs)  9.26 us
    dot_general x2, matrix products, mm_tn(): lax.dot_general(a, b, (((0,), (0,)), ((), ())), preferred_element_type=f32)  3.84 us
  transfers between devices with their start and end apart: 34, of which 19 were waited for; matrix products, arithmetic and copies ran while one was open for 5% of the time, Pallas kernels for 15%

profile of v8, /device:TPU:0, one launch (start us, length us, event | category | flops | bytes accessed | tf_op | source)
XLA Modules:
  0.0 161.1 jit_solution(17728289694979694300)
XLA Ops:
  1.2 2.4 %pack.1 = (bf16[96,384]{1,0:T(8,128)(2,1)}, bf16[96,384]{1,0:T(8,128)(2,1)}, bf16[96,128]{1,0:T(8,128)(2,1)}) custom-call(s32[3]{0:T(128)} %pad_add_fusion.me_ref, bf16[3,96,192]{2,1,0:T(8,128)(2,1)} %bitcast.106, bf16[192,96]{1,0:T(8,128)(2,1)} %out_hbm.1, bf16[1,96]{1,0:T(2,128)(2,1)} %bitcast.114, bf16[1,96]{1,0:T(2,128)(2,1)} %bitcast.115, ...), custom_call_target="tpu_custom_call" | custom-call | tf_op jit(solution)/shard_map/pack/pallas_call | solution.py:581
  3.7 4.1 %collective-permute-start = (bf16[1,96,384]{2,1,0:T(8,128)(2,1)}, bf16[1,96,384]{2,1,0:T(8,128)(2,1)S(1)}, u32[]{:S(2)}, u32[]{:S(2)}) collective-permute-start(bf16[1,96,384]{2,1,0:T(8,128)(2,1)} %bitcast.100), channel_id=1, source_target_pairs={{0,16},{4,20},{8,24},{12,28},{16,0},{20,4},{24,8},{28,12},{1,17},{... | collective-permute-start | bytes 221192 | tf_op jit(solution)/shard_map/ppermute | solution.py:24
  7.8 4.1 %collective-permute-done = bf16[1,96,384]{2,1,0:T(8,128)(2,1)S(1)} collective-permute-done((bf16[1,96,384]{2,1,0:T(8,128)(2,1)}, bf16[1,96,384]{2,1,0:T(8,128)(2,1)S(1)}, u32[]{:S(2)}, u32[]{:S(2)}) %collective-permute-start) | collective-permute-done | bytes 73760 | tf_op jit(solution)/shard_map/ppermute | solution.py:24
  13.7 3.3 %collective-permute-start.3 = (bf16[1,96,128]{2,1,0:T(8,128)(2,1)}, bf16[1,96,128]{2,1,0:T(8,128)(2,1)S(1)}, u32[]{:S(2)}, u32[]{:S(2)}) collective-permute-start(bf16[1,96,128]{2,1,0:T(8,128)(2,1)} %bitcast.108), channel_id=1, source_target_pairs={{0,16},{4,20},{8,24},{12,28},{16,0},{20,4},{24,8},{28,12},{1,17},{... | collective-permute-start | bytes 73736 | tf_op jit(solution)/shard_map/ppermute | solution.py:24
  19.3 1.8 %collective-permute-start.2 = (bf16[4,96,384]{2,1,0:T(8,128)(2,1)S(1)}, bf16[4,96,384]{2,1,0:T(8,128)(2,1)S(1)}, u32[]{:S(2)}, u32[]{:S(2)}) collective-permute-start(bf16[4,96,384]{2,1,0:T(8,128)(2,1)S(1)} %get-tuple-element.167), channel_id=1, source_target_pairs={{0,4},{1,3},{2,6},{3,1},{4,0},{5,7},{6,2},{7,5},{8,12},{9,11},{10,... | collective-permute-start | bytes 884744 | tf_op jit(solution)/shard_map/ppermute | solution.py:33
  22.5 3.8 %collective-permute-start.5 = (bf16[1,96,384]{2,1,0:T(8,128)(2,1)}, bf16[1,96,384]{2,1,0:T(8,128)(2,1)S(1)}, u32[]{:S(2)}, u32[]{:S(2)}) collective-permute-start(bf16[1,96,384]{2,1,0:T(8,128)(2,1)} %bitcast.111), channel_id=1, source_target_pairs={{0,16},{4,20},{8,24},{12,28},{16,0},{20,4},{24,8},{28,12},{1,17},{... | collective-permute-start | bytes 221192 | tf_op jit(solution)/shard_map/ppermute | solution.py:24
  27.0 2.5 %collective-permute-done.5 = bf16[1,96,384]{2,1,0:T(8,128)(2,1)S(1)} collective-permute-done((bf16[1,96,384]{2,1,0:T(8,128)(2,1)}, bf16[1,96,384]{2,1,0:T(8,128)(2,1)S(1)}, u32[]{:S(2)}, u32[]{:S(2)}) %collective-permute-start.5) | collective-permute-done | bytes 73760 | tf_op jit(solution)/shard_map/ppermute | solution.py:24
  32.6 4.6 %collective-permute-done.8 = bf16[2,96,384]{2,1,0:T(8,128)(2,1)S(1)} collective-permute-done((bf16[2,96,384]{2,1,0:T(8,128)(2,1)S(1)}, bf16[2,96,384]{2,1,0:T(8,128)(2,1)S(1)}, u32[]{:S(2)}, u32[]{:S(2)}) %collective-permute-start.8) | collective-permute-done | bytes 147488 | tf_op jit(solution)/shard_map/ppermute | solution.py:24
  39.5 4.6 %collective-permute-done.9 = bf16[4,96,384]{2,1,0:T(8,128)(2,1)S(1)} collective-permute-done((bf16[4,96,384]{2,1,0:T(8,128)(2,1)S(1)}, bf16[4,96,384]{2,1,0:T(8,128)(2,1)S(1)}, u32[]{:S(2)}, u32[]{:S(2)}) %collective-permute-start.9) | collective-permute-done | bytes 294944 | tf_op jit(solution)/shard_map/ppermute | solution.py:33
  46.1 6.0 %front_pair.1 = (bf16[4,768,384]{2,1,0:T(8,128)(2,1)S(1)}, bf16[4,624,384]{2,1,0:T(8,128)(2,1)S(1)}, bf16[4,3,2,208,208]{4,3,2,1,0:T(8,128)(2,1)S(1)}, bf16[4,624,128]{2,1,0:T(8,128)(2,1)S(1)}) custom-call(s32[3]{0:T(128)S(1)} %copy-done, bf16[624,768]{1,0:T(8,128)(2,1)S(1)} %get-tuple-element.95.h_ref, s32[12,200]{1,0:T(8,128)S(1)} %copy-done.5, ...), custom_call_target="tpu_custom_call" | custom-call | flops 11000000512 | bytes 3327372 | tf_op jit(solution)/shard_map/front_pair/pallas_call | solution.py:538
  52.0 2.1 %collective-permute-done.10.refs_1_ = bf16[2,4,96,384]{3,2,1,0:T(8,128)(2,1)S(1)} collective-permute-done((bf16[2,4,96,384]{3,2,1,0:T(8,128)(2,1)S(1)}, bf16[2,4,96,384]{3,2,1,0:T(8,128)(2,1)S(1)}, u32[]{:S(2)}, u32[]{:S(2)}) %collective-permute-start.10) | collective-permute-done | bytes 589856 | tf_op jit(solution)/shard_map/ppermute | solution.py:33
  54.1 2.0 %collective-permute-done.14.refs_3_ = bf16[2,4,96,384]{3,2,1,0:T(8,128)(2,1)S(1)} collective-permute-done((bf16[2,4,96,384]{3,2,1,0:T(8,128)(2,1)S(1)}, bf16[2,4,96,384]{3,2,1,0:T(8,128)(2,1)S(1)}, u32[]{:S(2)}, u32[]{:S(2)}) %collective-permute-start.14) | collective-permute-done | bytes 589856 | tf_op jit(solution)/shard_map/ppermute | solution.py:24
  56.1 5.1 %front_last.1 = (bf16[4,768,256]{2,1,0:T(8,128)(2,1)S(1)}, bf16[4,624,256]{2,1,0:T(8,128)(2,1)S(1)}, bf16[4,3,208,208]{3,2,1,0:T(8,128)(2,1)S(1)}, bf16[624,1024...) custom-call(s32[3]{0:T(128)S(1)} %copy-done, ...), custom_call_target="tpu_custom_call" | custom-call | flops 7699999744 | bytes 3966348 | tf_op jit(solution)/shard_map/front_last/pallas_call | solution.py:538
  61.3 2.7 %route.1 = (f32[624,768]{1,0:T(8,128)S(1)}, bf16[624,768]{1,0:T(8,128)(2,1)S(1)}, f32[2,3,8,208]{3,2,1,0:T(8,128)S(1)}, bf16[64,768]{1,0:T(8,128)(2,1)S(1)}, f32[3,1,128]{2,1,0:T(1,128)S(1)}) custom-call(s32[3]{0:T(128)S(1)} %copy-done, bf16[3,200,768]{2,1,0:T(8,128)(2,1)S(1)} %bitcast.87, f32[624,768]{1,0:T(8,128)S(1)} %get-tuple-element.101.br_ref, ...), custom_call_target="tpu_custom_call" | custom-call | flops 2200000000 | bytes 4162956 | tf_op jit(solution)/shard_map/route/pallas_call | solution.py:538
  63.9 10.6 %all_to_all.10 = bf16[8,8,768]{2,1,0:T(8,128)(2,1)S(1)} all-to-all(bf16[8,8,768]{2,1,0:T(8,128)(2,1)S(1)} %bitcast.81), channel_id=1, replica_groups=mesh['dp'=8,'mp'=4] {'dp'}, dimensions={0} | all-to-all | bytes 196608 | tf_op jit(solution)/shard_map/all_to_all | solution.py:694
  75.6 3.5 %collective-permute-done.15 = bf16[1,8,8,768]{3,2,1,0:T(8,128)(2,1)S(1)} collective-permute-done((bf16[1,8,8,768]{3,2,1,0:T(8,128)(2,1)S(1)}, bf16[1,8,8,768]{3,2,1,0:T(8,128)(2,1)S(1)}, u32[]{:S(2)}, u32[]{:S(2)}) %collective-permute-start.15) | collective-permute-done | bytes 98336 | tf_op jit(solution)/shard_map/ppermute | solution.py:24
  85.2 3.8 %collective-permute-done.18 = bf16[1,1,8,8,768]{4,3,2,1,0:T(8,128)(2,1)S(1)} collective-permute-done((bf16[1,1,8,8,768]{4,3,2,1,0:T(8,128)(2,1)S(1)}, bf16[1,1,8,8,768]{4,3,2,1,0:T(8,128)(2,1)S(1)}, u32[]{:S(2)}, u32[]{:S(2)}) %collective-permute-start.18) | collective-permute-done | bytes 98336 | tf_op jit(solution)/shard_map/ppermute | solution.py:24
  89.0 9.5 %all_to_all.11 = bf16[8,8,768]{2,1,0:T(8,128)(2,1)S(1)} all-to-all(bf16[8,8,768]{2,1,0:T(8,128)(2,1)S(1)} %fusion.5), channel_id=1, replica_groups=mesh['dp'=8,'mp'=4] {'dp'}, dimensions={0} | all-to-all | bytes 196608 | tf_op jit(solution)/shard_map/all_to_all | solution.py:714
  98.5 3.9 %mix.1 = (bf16[3,200,768]{2,1,0:T(8,128)(2,1)}, f32[624,768]{1,0:T(8,128)S(1)}, bf16[624,768]{1,0:T(8,128)(2,1)S(1)}, bf16[768,624]{1,0:T(8,128)(2,1)S(1)}, f32[13,768]{1,0:T(8,128)S(1)}) custom-call(s32[3]{0:T(128)S(1)} %copy-done, f32[624,768]{1,0:T(8,128)S(1)} %get-tuple-element.103.res_ref, bf16[624,768]{1,0:T(8,128)(2,1)S(1)} %get-tuple-element.104.h_ref, ...), custom_call_target="tpu_custom_call" | custom-call | flops 5500000256 | bytes 4315020 | tf_op jit(solution)/shard_map/mix/pallas_call | solution.py:538
  102.4 3.6 %back.4 = (bf16[2,4,96,768]{3,2,1,0:T(8,128)(2,1)S(1)}, bf16[624,640]{1,0:T(8,128)(2,1)S(1)}) custom-call(s32[3]{0:T(128)S(1)} %copy-done, bf16[624,768]{1,0:T(8,128)(2,1)S(1)} %get-tuple-element.134.gb_ref, bf16[768,624]{1,0:T(8,128)(2,1)S(1)} %get-tuple-element.115.gbt_ref, bf16[768,624]{1,0:T(8,128)(2,1)S(1)} %get-tuple-element.116.ht_ref, ...), custom_call_target="tpu_custom_call" | custom-call | flops 8800000000 | bytes 12036108 | tf_op jit(solution)/shard_map/back/pallas_call | solution.py:538
  106.2 3.6 %back.5 = (bf16[2,4,96,768]{3,2,1,0:T(8,128)(2,1)S(1)}, bf16[624,640]{1,0:T(8,128)(2,1)S(1)}) custom-call(s32[3]{0:T(128)S(1)} %copy-done, bf16[624,768]{1,0:T(8,128)(2,1)S(1)} %get-tuple-element.134.gb_ref, bf16[768,624]{1,0:T(8,128)(2,1)S(1)} %get-tuple-element.115.gbt_ref, bf16[768,624]{1,0:T(8,128)(2,1)S(1)} %get-tuple-element.116.ht_ref, ...), custom_call_target="tpu_custom_call" | custom-call | flops 8800000000 | bytes 12036108 | tf_op jit(solution)/shard_map/back/pallas_call | solution.py:538
  110.1 3.6 %back.6 = (bf16[2,4,96,768]{3,2,1,0:T(8,128)(2,1)S(1)}, bf16[624,640]{1,0:T(8,128)(2,1)S(1)}) custom-call(s32[3]{0:T(128)S(1)} %copy-done, bf16[624,768]{1,0:T(8,128)(2,1)S(1)} %get-tuple-element.134.gb_ref, bf16[768,624]{1,0:T(8,128)(2,1)S(1)} %get-tuple-element.115.gbt_ref, bf16[768,624]{1,0:T(8,128)(2,1)S(1)} %get-tuple-element.116.ht_ref, ...), custom_call_target="tpu_custom_call" | custom-call | flops 8800000000 | bytes 12036108 | tf_op jit(solution)/shard_map/back/pallas_call | solution.py:538
  115.4 3.9 %back.7 = (bf16[2,4,96,768]{3,2,1,0:T(8,128)(2,1)S(1)}, bf16[624,640]{1,0:T(8,128)(2,1)S(1)}) custom-call(s32[3]{0:T(128)S(1)} %copy-done, bf16[624,768]{1,0:T(8,128)(2,1)S(1)} %get-tuple-element.134.gb_ref, bf16[768,624]{1,0:T(8,128)(2,1)S(1)} %get-tuple-element.115.gbt_ref, bf16[768,624]{1,0:T(8,128)(2,1)S(1)} %get-tuple-element.116.ht_ref, ...), custom_call_target="tpu_custom_call" | custom-call | flops 8800000000 | bytes 12036108 | tf_op jit(solution)/shard_map/back/pallas_call | solution.py:538
  121.1 3.1 %collective-permute-done.22.early_ref = bf16[4,96,768]{2,1,0:T(8,128)(2,1)S(1)} collective-permute-done((bf16[4,96,768]{2,1,0:T(8,128)(2,1)S(1)}, bf16[4,96,768]{2,1,0:T(8,128)(2,1)S(1)}, u32[]{:S(2)}, u32[]{:S(2)}) %collective-permute-start.22) | collective-permute-done | bytes 589856 | tf_op jit(solution)/shard_map/ppermute | solution.py:33
  125.2 6.4 %last.1 = (f32[3,200,768]{2,1,0:T(8,128)}, f32[13,768]{1,0:T(8,128)S(1)}, f32[624,768]{1,0:T(8,128)}) custom-call(s32[3]{0:T(128)S(1)} %copy-done, bf16[3,200,768]{2,1,0:T(8,128)(2,1)S(1)} %bitcast.88, f32[624,768]{1,0:T(8,128)S(1)} %get-tuple-element.110.gres_ref, f32[128,768]{1,0:T(8,128)S(1)} %get-tuple-element.102.ex_ref, ...), custom_call_target="tpu_custom_call" | custom-call | flops 6600000000 | bytes 10398732 | tf_op jit(solution)/shard_map/last/pallas_call | solution.py:538
  132.1 1.7 %collective-permute-start.31 = (bf16[4,96,384]{2,1,0:T(8,128)(2,1)S(1)}, bf16[4,96,384]{2,1,0:T(8,128)(2,1)S(1)}, u32[]{:S(2)}, u32[]{:S(2)}) collective-permute-start(bf16[4,96,384]{2,1,0:T(8,128)(2,1)S(1)} %get-tuple-element.153), channel_id=1, source_target_pairs={{0,4},{1,3},{2,6},{3,1},{4,0},{5,7},{6,2},{7,5},{8,12},{9,11},{10,... | collective-permute-start | bytes 884744 | tf_op jit(solution)/shard_map/ppermute | solution.py:33
  133.8 3.3 %collective-permute-done.24 = f32[13,768]{1,0:T(8,128)S(1)} collective-permute-done((f32[13,768]{1,0:T(8,128)S(1)}, f32[13,768]{1,0:T(8,128)S(1)}, u32[]{:S(2)}, u32[]{:S(2)}) %collective-permute-start.24) | collective-permute-done | bytes 39968 | tf_op jit(solution)/shard_map/ppermute | solution.py:24
  137.8 1.9 %convolution_bitcast_fusion.1 = f32[1,768,768]{2,1,0:T(8,128)} fusion(bf16[256,768]{1,0:T(8,128)(2,1)S(1)} %bitcast.78, bf16[256,768]{1,0:T(8,128)(2,1)S(1)} %get-tuple-element.162), kind=kOutput, calls=%fused_computation.1 | convolution fusion | flops 301989888 | bytes 3145728 | tf_op jit(solution)/shard_map/dot_general | solution.py:86
  142.9 2.1 %collective-permute-start.32 = (bf16[2,96,384]{2,1,0:T(8,128)(2,1)S(1)}, bf16[2,96,384]{2,1,0:T(8,128)(2,1)S(1)}, u32[]{:S(2)}, u32[]{:S(2)}) collective-permute-start(bf16[2,96,384]{2,1,0:T(8,128)(2,1)S(1)} %get-tuple-element.155), channel_id=1, source_target_pairs={{0,8},{4,12},{8,0},{12,4},{16,24},{20,28},{24,16},{28,20},{1,9},{5... | collective-permute-start | bytes 442376 | tf_op jit(solution)/shard_map/ppermute | solution.py:24
  146.8 1.9 %convolution_bitcast_fusion = f32[1,768,768]{2,1,0:T(8,128)} fusion(bf16[256,768]{1,0:T(8,128)(2,1)S(1)} %get-tuple-element.163, bf16[256,768]{1,0:T(8,128)(2,1)S(1)} %get-tuple-element.164), kind=kOutput, calls=%fused_computation | convolution fusion | flops 301989888 | bytes 3145728 | tf_op jit(solution)/shard_map/dot_general | solution.py:86
  150.1 3.0 %collective-permute-start.33 = (bf16[96,384]{1,0:T(8,128)(2,1)S(1)}, bf16[96,384]{1,0:T(8,128)(2,1)S(1)}, u32[]{:S(2)}, u32[]{:S(2)}) collective-permute-start(bf16[96,384]{1,0:T(8,128)(2,1)S(1)} %bitcast.91), channel_id=1, source_target_pairs={{0,16},{4,20},{8,24},{12,28},{16,0},{20,4},{24,8},{28,12},{1,17},{... | collective-permute-start | bytes 221192 | tf_op jit(solution)/shard_map/ppermute | solution.py:24
  154.3 4.5 %collective-permute-done.30.other_a = bf16[96,384]{1,0:T(8,128)(2,1)S(1)} collective-permute-done((bf16[96,384]{1,0:T(8,128)(2,1)S(1)}, bf16[96,384]{1,0:T(8,128)(2,1)S(1)}, u32[]{:S(2)}, u32[]{:S(2)}) %collective-permute-start.30) | collective-permute-done | bytes 73760 | tf_op jit(solution)/shard_map/ppermute | solution.py:24
  (96 shorter events, 37.1 us)
Async XLA Ops:
  3.7 8.3 %collective-permute-start = (bf16[1,96,384]{2,1,0:T(8,128)(2,1)}, bf16[1,96,384]{2,1,0:T(8,128)(2,1)S(1)}, u32[]{:S(2)}, u32[]{:S(2)}) collective-permute-start(bf16[1,96,384]{2,1,0:T(8,128)(2,1)} %bitcast.100), channel_id=1, source_target_pairs={{0,16},{4,20},{8,24},{12,28},{16,0},{20,4},{24,8},{28,12},{1,17},{... | collective-permute-start | bytes 221192 | tf_op jit(solution)/shard_map/ppermute | solution.py:24
  12.8 5.5 %collective-permute-start.1 = (bf16[2,96,384]{2,1,0:T(8,128)(2,1)S(1)}, bf16[2,96,384]{2,1,0:T(8,128)(2,1)S(1)}, u32[]{:S(2)}, u32[]{:S(2)}) collective-permute-start(bf16[2,96,384]{2,1,0:T(8,128)(2,1)S(1)} %pad_maximum_fusion.6), channel_id=1, source_target_pairs={{0,8},{4,12},{8,0},{12,4},{16,24},{20,28},{24,16},{28,20},{1,9},{5... | collective-permute-start | bytes 442376 | tf_op jit(solution)/shard_map/ppermute | solution.py:24
  13.7 7.4 %collective-permute-start.3 = (bf16[1,96,128]{2,1,0:T(8,128)(2,1)}, bf16[1,96,128]{2,1,0:T(8,128)(2,1)S(1)}, u32[]{:S(2)}, u32[]{:S(2)}) collective-permute-start(bf16[1,96,128]{2,1,0:T(8,128)(2,1)} %bitcast.108), channel_id=1, source_target_pairs={{0,16},{4,20},{8,24},{12,28},{16,0},{20,4},{24,8},{28,12},{1,17},{... | collective-permute-start | bytes 73736 | tf_op jit(solution)/shard_map/ppermute | solution.py:24
  19.3 11.2 %collective-permute-start.2 = (bf16[4,96,384]{2,1,0:T(8,128)(2,1)S(1)}, bf16[4,96,384]{2,1,0:T(8,128)(2,1)S(1)}, u32[]{:S(2)}, u32[]{:S(2)}) collective-permute-start(bf16[4,96,384]{2,1,0:T(8,128)(2,1)S(1)} %get-tuple-element.167), channel_id=1, source_target_pairs={{0,4},{1,3},{2,6},{3,1},{4,0},{5,7},{6,2},{7,5},{8,12},{9,11},{10,... | collective-permute-start | bytes 884744 | tf_op jit(solution)/shard_map/ppermute | solution.py:33
  21.8 4.5 %collective-permute-start.4 = (bf16[2,96,128]{2,1,0:T(8,128)(2,1)S(1)}, bf16[2,96,128]{2,1,0:T(8,128)(2,1)S(1)}, u32[]{:S(2)}, u32[]{:S(2)}) collective-permute-start(bf16[2,96,128]{2,1,0:T(8,128)(2,1)S(1)} %pad_maximum_fusion.9), channel_id=1, source_target_pairs={{0,8},{4,12},{8,0},{12,4},{16,24},{20,28},{24,16},{28,20},{1,9},{5... | collective-permute-start | bytes 147464 | tf_op jit(solution)/shard_map/ppermute | solution.py:24
  22.5 7.0 %collective-permute-start.5 = (bf16[1,96,384]{2,1,0:T(8,128)(2,1)}, bf16[1,96,384]{2,1,0:T(8,128)(2,1)S(1)}, u32[]{:S(2)}, u32[]{:S(2)}) collective-permute-start(bf16[1,96,384]{2,1,0:T(8,128)(2,1)} %bitcast.111), channel_id=1, source_target_pairs={{0,16},{4,20},{8,24},{12,28},{16,0},{20,4},{24,8},{28,12},{1,17},{... | collective-permute-start | bytes 221192 | tf_op jit(solution)/shard_map/ppermute | solution.py:24
  30.5 13.5 %collective-permute-start.6 = (bf16[2,4,96,384]{3,2,1,0:T(8,128)(2,1)S(1)}, bf16[2,4,96,384]{3,2,1,0:T(8,128)(2,1)S(1)}, u32[]{:S(2)}, u32[]{:S(2)}) collective-permute-start(bf16[2,4,96,384]{3,2,1,0:T(8,128)(2,1)S(1)} %pad_maximum_fusion.refs_0_), channel_id=1, source_target_pairs={{0,2},{1,5},{2,0},{3,7},{4,6},{5,1},{6,4},{7,3},{8,10},{9,13},{10,... | collective-permute-start | bytes 1769480 | tf_op jit(solution)/shard_map/ppermute | solution.py:33
  32.1 5.1 %collective-permute-start.8 = (bf16[2,96,384]{2,1,0:T(8,128)(2,1)S(1)}, bf16[2,96,384]{2,1,0:T(8,128)(2,1)S(1)}, u32[]{:S(2)}, u32[]{:S(2)}) collective-permute-start(bf16[2,96,384]{2,1,0:T(8,128)(2,1)S(1)} %pad_maximum_fusion.7), channel_id=1, source_target_pairs={{0,8},{4,12},{8,0},{12,4},{16,24},{20,28},{24,16},{28,20},{1,9},{5... | collective-permute-start | bytes 442376 | tf_op jit(solution)/shard_map/ppermute | solution.py:24
  32.1 13.2 %collective-permute-start.11 = (bf16[2,4,96,384]{3,2,1,0:T(8,128)(2,1)S(1)}, bf16[2,4,96,384]{3,2,1,0:T(8,128)(2,1)S(1)}, u32[]{:S(2)}, u32[]{:S(2)}) collective-permute-start(bf16[2,4,96,384]{3,2,1,0:T(8,128)(2,1)S(1)} %pad_maximum_fusion.refs_0_), channel_id=1, source_target_pairs={{0,1},{1,0},{2,3},{3,2},{4,5},{5,4},{6,7},{7,6},{8,9},{9,8},{10,11... | collective-permute-start | bytes 1769480 | tf_op jit(solution)/shard_map/ppermute | solution.py:24
  32.1 5.7 %collective-permute-start.7 = (bf16[4,96,128]{2,1,0:T(8,128)(2,1)S(1)}, bf16[4,96,128]{2,1,0:T(8,128)(2,1)S(1)}, u32[]{:S(2)}, u32[]{:S(2)}) collective-permute-start(bf16[4,96,128]{2,1,0:T(8,128)(2,1)S(1)} %pad_maximum_fusion.8), channel_id=1, source_target_pairs={{0,4},{4,0},{8,12},{12,8},{16,20},{20,16},{24,28},{28,24},{1,5},{5... | collective-permute-start | bytes 294920 | tf_op jit(solution)/shard_map/ppermute | solution.py:24
  37.3 6.8 %collective-permute-start.9 = (bf16[4,96,384]{2,1,0:T(8,128)(2,1)S(1)}, bf16[4,96,384]{2,1,0:T(8,128)(2,1)S(1)}, u32[]{:S(2)}, u32[]{:S(2)}) collective-permute-start(bf16[4,96,384]{2,1,0:T(8,128)(2,1)S(1)} %constant_dynamic-update-slice_fusion), channel_id=1, source_target_pairs={{0,4},{1,3},{2,6},{3,1},{4,0},{5,7},{6,2},{7,5},{8,12},{9,11},{10,... | collective-permute-start | bytes 884744 | tf_op jit(solution)/shard_map/ppermute | solution.py:33
  44.0 2.0 %collective-permute-start.12 = (bf16[2,4,96,384]{3,2,1,0:T(8,128)(2,1)S(1)}, bf16[2,4,96,384]{3,2,1,0:T(8,128)(2,1)S(1)}, u32[]{:S(2)}, u32[]{:S(2)}) collective-permute-start(bf16[2,4,96,384]{3,2,1,0:T(8,128)(2,1)S(1)} %collective-permute-done.6.refs_1_), channel_id=1, source_target_pairs={{0,1},{1,0},{2,3},{3,2},{4,5},{5,4},{6,7},{7,6},{8,9},{9,8},{10,11... | collective-permute-start | bytes 1769480 | tf_op jit(solution)/shard_map/ppermute | solution.py:24
  44.1 9.9 %collective-permute-start.10 = (bf16[2,4,96,384]{3,2,1,0:T(8,128)(2,1)S(1)}, bf16[2,4,96,384]{3,2,1,0:T(8,128)(2,1)S(1)}, u32[]{:S(2)}, u32[]{:S(2)}) collective-permute-start(bf16[2,4,96,384]{3,2,1,0:T(8,128)(2,1)S(1)} %pad_maximum_fusion.1.refs_0_), channel_id=1, source_target_pairs={{0,2},{1,5},{2,0},{3,7},{4,6},{5,1},{6,4},{7,3},{8,10},{9,13},{10,... | collective-permute-start | bytes 1769480 | tf_op jit(solution)/shard_map/ppermute | solution.py:33
  45.3 8.8 %collective-permute-start.13 = (bf16[2,4,96,384]{3,2,1,0:T(8,128)(2,1)S(1)}, bf16[2,4,96,384]{3,2,1,0:T(8,128)(2,1)S(1)}, u32[]{:S(2)}, u32[]{:S(2)}) collective-permute-start(bf16[2,4,96,384]{3,2,1,0:T(8,128)(2,1)S(1)} %pad_maximum_fusion.1.refs_0_), channel_id=1, source_target_pairs={{0,1},{1,0},{2,3},{3,2},{4,5},{5,4},{6,7},{7,6},{8,9},{9,8},{10,11... | collective-permute-start | bytes 1769480 | tf_op jit(solution)/shard_map/ppermute | solution.py:24
  54.1 2.0 %collective-permute-start.14 = (bf16[2,4,96,384]{3,2,1,0:T(8,128)(2,1)S(1)}, bf16[2,4,96,384]{3,2,1,0:T(8,128)(2,1)S(1)}, u32[]{:S(2)}, u32[]{:S(2)}) collective-permute-start(bf16[2,4,96,384]{3,2,1,0:T(8,128)(2,1)S(1)} %collective-permute-done.10.refs_1_), channel_id=1, source_target_pairs={{0,1},{1,0},{2,3},{3,2},{4,5},{5,4},{6,7},{7,6},{8,9},{9,8},{10,11... | collective-permute-start | bytes 1769480 | tf_op jit(solution)/shard_map/ppermute | solution.py:24
  74.5 4.6 %collective-permute-start.15 = (bf16[1,8,8,768]{3,2,1,0:T(8,128)(2,1)S(1)}, bf16[1,8,8,768]{3,2,1,0:T(8,128)(2,1)S(1)}, u32[]{:S(2)}, u32[]{:S(2)}) collective-permute-start(bf16[1,8,8,768]{3,2,1,0:T(8,128)(2,1)S(1)} %bitcast.97), channel_id=1, source_target_pairs={{0,2},{1,3},{2,0},{3,1},{4,6},{5,7},{6,4},{7,5},{8,10},{9,11},{10,... | collective-permute-start | bytes 294920 | tf_op jit(solution)/shard_map/ppermute | solution.py:24
  84.0 4.9 %collective-permute-start.18 = (bf16[1,1,8,8,768]{4,3,2,1,0:T(8,128)(2,1)S(1)}, bf16[1,1,8,8,768]{4,3,2,1,0:T(8,128)(2,1)S(1)}, u32[]{:S(2)}, u32[]{:S(2)}) collective-permute-start(bf16[1,1,8,8,768]{4,3,2,1,0:T(8,128)(2,1)S(1)} %slice_bitcast_fusion.2), channel_id=1, source_target_pairs={{0,2},{1,3},{2,0},{3,1},{4,6},{5,7},{6,4},{7,5},{8,10},{9,11},{10,... | collective-permute-start | bytes 294920 | tf_op jit(solution)/shard_map/ppermute | solution.py:24
  106.1 3.7 %collective-permute-start.19 = (bf16[2,4,96,768]{3,2,1,0:T(8,128)(2,1)S(1)}, bf16[2,4,96,768]{3,2,1,0:T(8,128)(2,1)S(1)}, u32[]{:S(2)}, u32[]{:S(2)}) collective-permute-start(bf16[2,4,96,768]{3,2,1,0:T(8,128)(2,1)S(1)} %get-tuple-element.127), channel_id=1, source_target_pairs={{0,1},{1,0},{2,3},{3,2},{4,5},{5,4},{6,7},{7,6},{8,9},{9,8},{10,11... | collective-permute-start | bytes 3538952 | tf_op jit(solution)/shard_map/ppermute | solution.py:24
  113.7 5.5 %collective-permute-start.20 = (bf16[2,4,96,768]{3,2,1,0:T(8,128)(2,1)S(1)}, bf16[2,4,96,768]{3,2,1,0:T(8,128)(2,1)S(1)}, u32[]{:S(2)}, u32[]{:S(2)}) collective-permute-start(bf16[2,4,96,768]{3,2,1,0:T(8,128)(2,1)S(1)} %get-tuple-element.139), channel_id=1, source_target_pairs={{0,1},{1,0},{2,3},{3,2},{4,5},{5,4},{6,7},{7,6},{8,9},{9,8},{10,11... | collective-permute-start | bytes 3538952 | tf_op jit(solution)/shard_map/ppermute | solution.py:24
  114.3 9.9 %collective-permute-start.22 = (bf16[4,96,768]{2,1,0:T(8,128)(2,1)S(1)}, bf16[4,96,768]{2,1,0:T(8,128)(2,1)S(1)}, u32[]{:S(2)}, u32[]{:S(2)}) collective-permute-start(bf16[4,96,768]{2,1,0:T(8,128)(2,1)S(1)} %bitcast.89), channel_id=1, source_target_pairs={{0,2},{1,5},{2,0},{3,7},{4,6},{5,1},{6,4},{7,3},{8,10},{9,13},{10,... | collective-permute-start | bytes 1769480 | tf_op jit(solution)/shard_map/ppermute | solution.py:33
  120.1 21.2 %collective-permute-start.21 = (bf16[4,96,768]{2,1,0:T(8,128)(2,1)S(1)}, bf16[4,96,768]{2,1,0:T(8,128)(2,1)S(1)}, u32[]{:S(2)}, u32[]{:S(2)}) collective-permute-start(bf16[4,96,768]{2,1,0:T(8,128)(2,1)S(1)} %get-tuple-element.141), channel_id=1, source_target_pairs={{0,2},{1,5},{2,0},{3,7},{4,6},{5,1},{6,4},{7,3},{8,10},{9,13},{10,... | collective-permute-start | bytes 1769480 | tf_op jit(solution)/shard_map/ppermute | solution.py:33
  124.9 16.5 %collective-permute-start.23 = (bf16[4,96,384]{2,1,0:T(8,128)(2,1)S(1)}, bf16[4,96,384]{2,1,0:T(8,128)(2,1)S(1)}, u32[]{:S(2)}, u32[]{:S(2)}) collective-permute-start(bf16[4,96,384]{2,1,0:T(8,128)(2,1)S(1)} %get-tuple-element.144), channel_id=1, source_target_pairs={{0,4},{1,3},{2,6},{3,1},{4,0},{5,7},{6,2},{7,5},{8,12},{9,11},{10,... | collective-permute-start | bytes 884744 | tf_op jit(solution)/shard_map/ppermute | solution.py:33
  131.7 5.5 %collective-permute-start.24 = (f32[13,768]{1,0:T(8,128)S(1)}, f32[13,768]{1,0:T(8,128)S(1)}, u32[]{:S(2)}, u32[]{:S(2)}) collective-permute-start(f32[13,768]{1,0:T(8,128)S(1)} %get-tuple-element.146), channel_id=1, source_target_pairs={{0,16},{4,20},{8,24},{12,28},{16,0},{20,4},{24,8},{28,12},{1,17},{... | collective-permute-start | bytes 119816 | tf_op jit(solution)/shard_map/ppermute | solution.py:24
  132.1 10.7 %collective-permute-start.31 = (bf16[4,96,384]{2,1,0:T(8,128)(2,1)S(1)}, bf16[4,96,384]{2,1,0:T(8,128)(2,1)S(1)}, u32[]{:S(2)}, u32[]{:S(2)}) collective-permute-start(bf16[4,96,384]{2,1,0:T(8,128)(2,1)S(1)} %get-tuple-element.153), channel_id=1, source_target_pairs={{0,4},{1,3},{2,6},{3,1},{4,0},{5,7},{6,2},{7,5},{8,12},{9,11},{10,... | collective-permute-start | bytes 884744 | tf_op jit(solution)/shard_map/ppermute | solution.py:33
  137.2 4.1 %collective-permute-start.25 = (f32[13,768]{1,0:T(8,128)S(1)}, f32[13,768]{1,0:T(8,128)S(1)}, u32[]{:S(2)}, u32[]{:S(2)}) collective-permute-start(f32[13,768]{1,0:T(8,128)S(1)} %add.20), channel_id=1, source_target_pairs={{0,8},{4,12},{8,0},{12,4},{16,24},{20,28},{24,16},{28,20},{1,9},{5... | collective-permute-start | bytes 119816 | tf_op jit(solution)/shard_map/ppermute | solution.py:24
  141.5 4.2 %collective-permute-start.26 = (f32[13,768]{1,0:T(8,128)S(1)}, f32[13,768]{1,0:T(8,128)S(1)}, u32[]{:S(2)}, u32[]{:S(2)}) collective-permute-start(f32[13,768]{1,0:T(8,128)S(1)} %add.21), channel_id=1, source_target_pairs={{0,4},{4,0},{8,12},{12,8},{16,20},{20,16},{24,28},{28,24},{1,5},{5... | collective-permute-start | bytes 119816 | tf_op jit(solution)/shard_map/ppermute | solution.py:24
  142.7 7.1 %collective-permute-start.29 = (bf16[2,96,384]{2,1,0:T(8,128)(2,1)S(1)}, bf16[2,96,384]{2,1,0:T(8,128)(2,1)S(1)}, u32[]{:S(2)}, u32[]{:S(2)}) collective-permute-start(bf16[2,96,384]{2,1,0:T(8,128)(2,1)S(1)} %get-tuple-element.150), channel_id=1, source_target_pairs={{0,8},{4,12},{8,0},{12,4},{16,24},{20,28},{24,16},{28,20},{1,9},{5... | collective-permute-start | bytes 442376 | tf_op jit(solution)/shard_map/ppermute | solution.py:24
  142.9 7.1 %collective-permute-start.32 = (bf16[2,96,384]{2,1,0:T(8,128)(2,1)S(1)}, bf16[2,96,384]{2,1,0:T(8,128)(2,1)S(1)}, u32[]{:S(2)}, u32[]{:S(2)}) collective-permute-start(bf16[2,96,384]{2,1,0:T(8,128)(2,1)S(1)} %get-tuple-element.155), channel_id=1, source_target_pairs={{0,8},{4,12},{8,0},{12,4},{16,24},{20,28},{24,16},{28,20},{1,9},{5... | collective-permute-start | bytes 442376 | tf_op jit(solution)/shard_map/ppermute | solution.py:24
  145.6 4.1 %collective-permute-start.27 = (f32[13,768]{1,0:T(8,128)S(1)}, f32[13,768]{1,0:T(8,128)S(1)}, u32[]{:S(2)}, u32[]{:S(2)}) collective-permute-start(f32[13,768]{1,0:T(8,128)S(1)} %add.22), channel_id=1, source_target_pairs={{0,2},{1,3},{2,0},{3,1},{4,6},{5,7},{6,4},{7,5},{8,10},{9,11},{10,... | collective-permute-start | bytes 119816 | tf_op jit(solution)/shard_map/ppermute | solution.py:24
  149.8 3.2 %collective-permute-start.28 = (f32[13,768]{1,0:T(8,128)S(1)}, f32[13,768]{1,0:T(8,128)S(1)}, u32[]{:S(2)}, u32[]{:S(2)}) collective-permute-start(f32[13,768]{1,0:T(8,128)S(1)} %add.23.own_ref), channel_id=1, source_target_pairs={{0,1},{1,0},{2,3},{3,2},{4,5},{5,4},{6,7},{7,6},{8,9},{9,8},{10,11... | collective-permute-start | bytes 119816 | tf_op jit(solution)/shard_map/ppermute | solution.py:24
  149.9 8.8 %collective-permute-start.30 = (bf16[96,384]{1,0:T(8,128)(2,1)S(1)}, bf16[96,384]{1,0:T(8,128)(2,1)S(1)}, u32[]{:S(2)}, u32[]{:S(2)}) collective-permute-start(bf16[96,384]{1,0:T(8,128)(2,1)S(1)} %bitcast.90), channel_id=1, source_target_pairs={{0,16},{4,20},{8,24},{12,28},{16,0},{20,4},{24,8},{28,12},{1,17},{... | collective-permute-start | bytes 221192 | tf_op jit(solution)/shard_map/ppermute | solution.py:24
  150.1 10.2 %collective-permute-start.33 = (bf16[96,384]{1,0:T(8,128)(2,1)S(1)}, bf16[96,384]{1,0:T(8,128)(2,1)S(1)}, u32[]{:S(2)}, u32[]{:S(2)}) collective-permute-start(bf16[96,384]{1,0:T(8,128)(2,1)S(1)} %bitcast.91), channel_id=1, source_target_pairs={{0,16},{4,20},{8,24},{12,28},{16,0},{20,4},{24,8},{28,12},{1,17},{... | collective-permute-start | bytes 221192 | tf_op jit(solution)/shard_map/ppermute | solution.py:24
  (8 other events, 91.8 us)

commit v9 on v8

--- a/solution.py
+++ b/solution.py
@@ -501,12 +501,8 @@
         gw_ref[entry + (slice(None), slice(640, 768))] = grad_out[at, 128:].astype(bf16)
 
 
-def last_kernel(
-    me_ref, x_ref, gres_ref, ex_ref, part_ref, w_a, w_b, *refs, images, seq, tall, experts, order
-):
-    grads, (gt_ref, small_ref, gh_ref) = refs[:-3], refs[-3:]
-    total = jnp.zeros((1, x_ref.shape[2]), f32)
-    gain = ex_ref[0:1, :]
+def input_kernel(me_ref, w_a, w_b, *refs, order):
+    grads, gh_ref = refs[:-1], refs[-1]
     for k, (ref, (x, flip)) in enumerate(zip(grads, order)):
         j = x + 2 * jnp.bitwise_xor(me_ref[1], flip)
         into = mm_nt(ref[:, :384], w_a[j]) + mm_nt(ref[:, 384:], w_b[j])
@@ -514,6 +510,11 @@
             gh_ref[...] = into
         else:
             gh_ref[...] += into
+
+
+def last_kernel(x_ref, gres_ref, gh_ref, ex_ref, part_ref, gt_ref, small_ref, *, images, seq, tall, experts):
+    total = jnp.zeros((1, x_ref.shape[2]), f32)
+    gain = ex_ref[0:1, :]
     for b in range(images):
         at = pl.ds(b * tall, seq)
         unit, inverse = unit_of(x_ref[b].astype(f32))
@@ -799,27 +800,40 @@
             grant=8,
         )
         thirds = [swap_both(third, dp, mp, (1, 0), (0, 2)) for third in thirds]
-        grad_tokens, small, _ = call(
+        grad_h = call(
+            input_kernel,
+            [((count, width), f32)],
+            (words, w_a, w_b, joined_a, joined_b, joined_c, joined_d),
+            flops=cost(4),
+            name="input",
+            grant=8,
+            order=order,
+        )[0]
+        pieces = [
+            list(fold((near_sum, second, third), False, (k * half, k * half, 0), half))
+            for k, third in enumerate(thirds)
+        ]
+        pieces[0][1], grad_h = lax.optimization_barrier((pieces[0][1], grad_h))
+        grad_tokens, small = call(
             last_kernel,
-            [((images, seq, width), f32), ((experts + 5, width), f32), ((count, width), f32)],
-            (words, x3, grad_resid, ex, small, w_a, w_b, joined_a, joined_b, joined_c, joined_d),
-            flops=cost(6),
+            [((images, seq, width), f32), ((experts + 5, width), f32)],
+            (x3, grad_resid, grad_h, ex, small),
+            flops=cost(0.1),
             name="last",
+            scalars=0,
             grant=8,
             experts=experts,
-            order=order,
             **exact,
         )
-        for bit in bits_of(dp)[:-1]:
-            small = small + swap(small, "dp", dp, bit)
+        for bit in bits_of(mp)[::-1]:
+            small = small + swap(small, "mp", mp, bit)
         parts = []
-        for k, third in enumerate(thirds):
-            starts = (k * half, k * half, 0)
-            kept, left = fold((near_sum, second, third), False, starts, half)
-            if k == 0:
-                left, small = lax.optimization_barrier((left, small))
+        for k, (kept, left) in enumerate(pieces):
             for bit in bits_of(high)[:0:-1]:
-                kept, left = fold((kept, swap(left, "dp", dp, 2 * bit)), False, None, half)
+                other = swap(left, "dp", dp, 2 * bit)
+                if k == 0:
+                    other, small = lax.optimization_barrier((other, small))
+                kept, left = fold((kept, other), False, None, half)
             parts += [kept[0], swap(left[0], "dp", dp, 2 * bits_of(high)[0])]
         grad_qkv, grad_out = call(
             unpack_kernel,
@@ -830,8 +844,8 @@
             scalars=0,
             grant=6,
         )
-        small = small + swap(small, "dp", dp, 1)
-        small = small + swap(small, "mp", mp, 2)
+        for bit in bits_of(dp)[:0:-1]:
+            small = small + swap(small, "dp", dp, bit)
         grad_one, grad_two, grad_router, root_squares = call(
             finish_kernel,
             [
@@ -840,7 +854,7 @@
                 ((experts, d_rows), f32),
                 ((3, mp * images), f32),
             ],
-            (words, small, swap(small, "mp", mp, 1)),
+            (words, small, swap(small, "dp", dp, bits_of(dp)[0])),
             flops=cost(1),
             name="finish",
             grant=4,

time: 162 us -> 161 us (level)
    ppermute x26, waiting for transfers between devices: 38.1 us -> 34.6 us  [swap(): lax.ppermute(array_in, axis_name, [(i, i ^ bit) for i in range(size)])]
    ppermute x8, waiting for transfers between devices: 9.69 us -> 13.1 us  [swap_both(): return lax.ppermute(array_in, ('dp', 'mp'), pairs)]
    pallas_call x20 -> x21, Pallas kernels: 46.4 us -> 46.7 us  [call(): pl.pallas_call(functools.partial(kernel, **static), out_shape=[jax.ShapeD...]
where the time goes in v9:
time: 161 us; the launch traced here: 160 us
  Pallas kernels  49.1 us (30%)
  waiting for transfers between devices  47.7 us (30%)
  starting transfers between devices  33.4 us (21%)
  blocking collectives  20.1 us (12%)
  other arithmetic  5.16 us (3%)
  matrix products  3.85 us (2%)
    pallas_call x21, Pallas kernels, call(): pl.pallas_call(functools.partial(kernel, **static), out_shape=[jax.ShapeD...  46.7 us
    ppermute x26, waiting for transfers between devices, swap(): lax.ppermute(array_in, axis_name, [(i, i ^ bit) for i in range(size)])  34.6 us
    ppermute x26, starting transfers between devices, swap(): lax.ppermute(array_in, axis_name, [(i, i ^ bit) for i in range(size)])  24.2 us
    ppermute x8, waiting for transfers between devices, swap_both(): return lax.ppermute(array_in, ('dp', 'mp'), pairs)  13.1 us
    all_to_all x1, blocking collectives, per_device(): got = lax.all_to_all(got, 'dp', split_axis=0, concat_axis=0, tiled=True)  10.6 us
    all_to_all x1, blocking collectives, per_device(): back = lax.all_to_all(back, 'dp', split_axis=0, concat_axis=0, tiled=True)  9.51 us
    ppermute x8, starting transfers between devices, swap_both(): return lax.ppermute(array_in, ('dp', 'mp'), pairs)  9.24 us
    dot_general x2, matrix products, mm_tn(): lax.dot_general(a, b, (((0,), (0,)), ((), ())), preferred_element_type=f32)  3.85 us
  transfers between devices with their start and end apart: 34, of which 19 were waited for; matrix products, arithmetic and copies ran while one was open for 5% of the time, Pallas kernels for 15%

profile of v9, /device:TPU:0, one launch (start us, length us, event | category | flops | bytes accessed | tf_op | source)
XLA Modules:
  0.0 160.5 jit_solution(9597376971978723477)
XLA Ops:
  1.2 2.4 %pack.1 = (bf16[96,384]{1,0:T(8,128)(2,1)}, bf16[96,384]{1,0:T(8,128)(2,1)}, bf16[96,128]{1,0:T(8,128)(2,1)}) custom-call(s32[3]{0:T(128)} %pad_add_fusion.me_ref, bf16[3,96,192]{2,1,0:T(8,128)(2,1)} %bitcast.106, bf16[192,96]{1,0:T(8,128)(2,1)} %out_hbm.1, bf16[1,96]{1,0:T(2,128)(2,1)} %bitcast.114, bf16[1,96]{1,0:T(2,128)(2,1)} %bitcast.115, ...), custom_call_target="tpu_custom_call" | custom-call | tf_op jit(solution)/shard_map/pack/pallas_call | solution.py:582
  3.7 4.1 %collective-permute-start = (bf16[1,96,384]{2,1,0:T(8,128)(2,1)}, bf16[1,96,384]{2,1,0:T(8,128)(2,1)S(1)}, u32[]{:S(2)}, u32[]{:S(2)}) collective-permute-start(bf16[1,96,384]{2,1,0:T(8,128)(2,1)} %bitcast.100), channel_id=1, source_target_pairs={{0,16},{4,20},{8,24},{12,28},{16,0},{20,4},{24,8},{28,12},{1,17},{... | collective-permute-start | bytes 221192 | tf_op jit(solution)/shard_map/ppermute | solution.py:24
  7.8 4.1 %collective-permute-done = bf16[1,96,384]{2,1,0:T(8,128)(2,1)S(1)} collective-permute-done((bf16[1,96,384]{2,1,0:T(8,128)(2,1)}, bf16[1,96,384]{2,1,0:T(8,128)(2,1)S(1)}, u32[]{:S(2)}, u32[]{:S(2)}) %collective-permute-start) | collective-permute-done | bytes 73760 | tf_op jit(solution)/shard_map/ppermute | solution.py:24
  13.7 3.3 %collective-permute-start.3 = (bf16[1,96,128]{2,1,0:T(8,128)(2,1)}, bf16[1,96,128]{2,1,0:T(8,128)(2,1)S(1)}, u32[]{:S(2)}, u32[]{:S(2)}) collective-permute-start(bf16[1,96,128]{2,1,0:T(8,128)(2,1)} %bitcast.108), channel_id=1, source_target_pairs={{0,16},{4,20},{8,24},{12,28},{16,0},{20,4},{24,8},{28,12},{1,17},{... | collective-permute-start | bytes 73736 | tf_op jit(solution)/shard_map/ppermute | solution.py:24
  22.5 3.8 %collective-permute-start.5 = (bf16[1,96,384]{2,1,0:T(8,128)(2,1)}, bf16[1,96,384]{2,1,0:T(8,128)(2,1)S(1)}, u32[]{:S(2)}, u32[]{:S(2)}) collective-permute-start(bf16[1,96,384]{2,1,0:T(8,128)(2,1)} %bitcast.111), channel_id=1, source_target_pairs={{0,16},{4,20},{8,24},{12,28},{16,0},{20,4},{24,8},{28,12},{1,17},{... | collective-permute-start | bytes 221192 | tf_op jit(solution)/shard_map/ppermute | solution.py:24
  27.0 2.5 %collective-permute-done.5 = bf16[1,96,384]{2,1,0:T(8,128)(2,1)S(1)} collective-permute-done((bf16[1,96,384]{2,1,0:T(8,128)(2,1)}, bf16[1,96,384]{2,1,0:T(8,128)(2,1)S(1)}, u32[]{:S(2)}, u32[]{:S(2)}) %collective-permute-start.5) | collective-permute-done | bytes 73760 | tf_op jit(solution)/shard_map/ppermute | solution.py:24
  32.6 4.6 %collective-permute-done.8 = bf16[2,96,384]{2,1,0:T(8,128)(2,1)S(1)} collective-permute-done((bf16[2,96,384]{2,1,0:T(8,128)(2,1)S(1)}, bf16[2,96,384]{2,1,0:T(8,128)(2,1)S(1)}, u32[]{:S(2)}, u32[]{:S(2)}) %collective-permute-start.8) | collective-permute-done | bytes 147488 | tf_op jit(solution)/shard_map/ppermute | solution.py:24
  39.5 4.6 %collective-permute-done.9 = bf16[4,96,384]{2,1,0:T(8,128)(2,1)S(1)} collective-permute-done((bf16[4,96,384]{2,1,0:T(8,128)(2,1)S(1)}, bf16[4,96,384]{2,1,0:T(8,128)(2,1)S(1)}, u32[]{:S(2)}, u32[]{:S(2)}) %collective-permute-start.9) | collective-permute-done | bytes 294944 | tf_op jit(solution)/shard_map/ppermute | solution.py:33
  46.1 6.0 %front_pair.1 = (bf16[4,768,384]{2,1,0:T(8,128)(2,1)S(1)}, bf16[4,624,384]{2,1,0:T(8,128)(2,1)S(1)}, bf16[4,3,2,208,208]{4,3,2,1,0:T(8,128)(2,1)S(1)}, bf16[4,624,128]{2,1,0:T(8,128)(2,1)S(1)}) custom-call(s32[3]{0:T(128)S(1)} %copy-done.1, bf16[624,768]{1,0:T(8,128)(2,1)S(1)} %get-tuple-element.97.h_ref, s32[12,200]{1,0:T(8,128)S(1)} %copy-done.5, ...), custom_call_target="tpu_custom_call" | custom-call | flops 11000000512 | bytes 3327372 | tf_op jit(solution)/shard_map/front_pair/pallas_call | solution.py:539
  52.0 2.0 %collective-permute-done.10.refs_1_ = bf16[2,4,96,384]{3,2,1,0:T(8,128)(2,1)S(1)} collective-permute-done((bf16[2,4,96,384]{3,2,1,0:T(8,128)(2,1)S(1)}, bf16[2,4,96,384]{3,2,1,0:T(8,128)(2,1)S(1)}, u32[]{:S(2)}, u32[]{:S(2)}) %collective-permute-start.10) | collective-permute-done | bytes 589856 | tf_op jit(solution)/shard_map/ppermute | solution.py:33
  54.1 2.0 %collective-permute-done.14.refs_3_ = bf16[2,4,96,384]{3,2,1,0:T(8,128)(2,1)S(1)} collective-permute-done((bf16[2,4,96,384]{3,2,1,0:T(8,128)(2,1)S(1)}, bf16[2,4,96,384]{3,2,1,0:T(8,128)(2,1)S(1)}, u32[]{:S(2)}, u32[]{:S(2)}) %collective-permute-start.14) | collective-permute-done | bytes 589856 | tf_op jit(solution)/shard_map/ppermute | solution.py:24
  56.1 5.2 %front_last.1 = (bf16[4,768,256]{2,1,0:T(8,128)(2,1)S(1)}, bf16[4,624,256]{2,1,0:T(8,128)(2,1)S(1)}, bf16[4,3,208,208]{3,2,1,0:T(8,128)(2,1)S(1)}, bf16[624,1024...) custom-call(s32[3]{0:T(128)S(1)} %copy-done.1, ...), custom_call_target="tpu_custom_call" | custom-call | flops 7699999744 | bytes 3966348 | tf_op jit(solution)/shard_map/front_last/pallas_call | solution.py:539
  61.3 2.7 %route.1 = (f32[624,768]{1,0:T(8,128)S(1)}, bf16[624,768]{1,0:T(8,128)(2,1)S(1)}, f32[2,3,8,208]{3,2,1,0:T(8,128)S(1)}, bf16[64,768]{1,0:T(8,128)(2,1)S(1)}, f32[3,1,128]{2,1,0:T(1,128)S(1)}) custom-call(s32[3]{0:T(128)S(1)} %copy-done.1, bf16[3,200,768]{2,1,0:T(8,128)(2,1)S(1)} %bitcast.80, f32[624,768]{1,0:T(8,128)S(1)} %get-tuple-element.103.br_ref, ...), custom_call_target="tpu_custom_call" | custom-call | flops 2200000000 | bytes 4162956 | tf_op jit(solution)/shard_map/route/pallas_call | solution.py:539
  64.0 10.6 %all_to_all.10 = bf16[8,8,768]{2,1,0:T(8,128)(2,1)S(1)} all-to-all(bf16[8,8,768]{2,1,0:T(8,128)(2,1)S(1)} %bitcast.84), channel_id=1, replica_groups=mesh['dp'=8,'mp'=4] {'dp'}, dimensions={0} | all-to-all | bytes 196608 | tf_op jit(solution)/shard_map/all_to_all | solution.py:695
  75.6 3.5 %collective-permute-done.15 = bf16[1,8,8,768]{3,2,1,0:T(8,128)(2,1)S(1)} collective-permute-done((bf16[1,8,8,768]{3,2,1,0:T(8,128)(2,1)S(1)}, bf16[1,8,8,768]{3,2,1,0:T(8,128)(2,1)S(1)}, u32[]{:S(2)}, u32[]{:S(2)}) %collective-permute-start.15) | collective-permute-done | bytes 98336 | tf_op jit(solution)/shard_map/ppermute | solution.py:24
  85.2 3.8 %collective-permute-done.18 = bf16[1,1,8,8,768]{4,3,2,1,0:T(8,128)(2,1)S(1)} collective-permute-done((bf16[1,1,8,8,768]{4,3,2,1,0:T(8,128)(2,1)S(1)}, bf16[1,1,8,8,768]{4,3,2,1,0:T(8,128)(2,1)S(1)}, u32[]{:S(2)}, u32[]{:S(2)}) %collective-permute-start.18) | collective-permute-done | bytes 98336 | tf_op jit(solution)/shard_map/ppermute | solution.py:24
  89.0 9.5 %all_to_all.11 = bf16[8,8,768]{2,1,0:T(8,128)(2,1)S(1)} all-to-all(bf16[8,8,768]{2,1,0:T(8,128)(2,1)S(1)} %fusion.5), channel_id=1, replica_groups=mesh['dp'=8,'mp'=4] {'dp'}, dimensions={0} | all-to-all | bytes 196608 | tf_op jit(solution)/shard_map/all_to_all | solution.py:715
  98.5 3.9 %mix.1 = (bf16[3,200,768]{2,1,0:T(8,128)(2,1)}, f32[624,768]{1,0:T(8,128)S(1)}, bf16[624,768]{1,0:T(8,128)(2,1)S(1)}, bf16[768,624]{1,0:T(8,128)(2,1)S(1)}, f32[13,768]{1,0:T(8,128)S(1)}) custom-call(s32[3]{0:T(128)S(1)} %copy-done.1, f32[624,768]{1,0:T(8,128)S(1)} %get-tuple-element.105.res_ref, bf16[624,768]{1,0:T(8,128)(2,1)S(1)} %get-tuple-element.106.h_ref, ...), custom_call_target="tpu_custom_call" | custom-call | flops 5500000256 | bytes 4315020 | tf_op jit(solution)/shard_map/mix/pallas_call | solution.py:539
  102.4 3.7 %back.4 = (bf16[2,4,96,768]{3,2,1,0:T(8,128)(2,1)S(1)}, bf16[624,640]{1,0:T(8,128)(2,1)S(1)}) custom-call(s32[3]{0:T(128)S(1)} %copy-done.1, bf16[624,768]{1,0:T(8,128)(2,1)S(1)} %get-tuple-element.131.gb_ref, bf16[768,624]{1,0:T(8,128)(2,1)S(1)} %get-tuple-element.114.gbt_ref, bf16[768,624]{1,0:T(8,128)(2,1)S(1)} %get-tuple-element.115.ht_ref, ...), custom_call_target="tpu_custom_call" | custom-call | flops 8800000000 | bytes 12036108 | tf_op jit(solution)/shard_map/back/pallas_call | solution.py:539
  106.2 3.7 %back.5 = (bf16[2,4,96,768]{3,2,1,0:T(8,128)(2,1)S(1)}, bf16[624,640]{1,0:T(8,128)(2,1)S(1)}) custom-call(s32[3]{0:T(128)S(1)} %copy-done.1, bf16[624,768]{1,0:T(8,128)(2,1)S(1)} %get-tuple-element.131.gb_ref, bf16[768,624]{1,0:T(8,128)(2,1)S(1)} %get-tuple-element.114.gbt_ref, bf16[768,624]{1,0:T(8,128)(2,1)S(1)} %get-tuple-element.115.ht_ref, ...), custom_call_target="tpu_custom_call" | custom-call | flops 8800000000 | bytes 12036108 | tf_op jit(solution)/shard_map/back/pallas_call | solution.py:539
  110.2 3.7 %back.6 = (bf16[2,4,96,768]{3,2,1,0:T(8,128)(2,1)S(1)}, bf16[624,640]{1,0:T(8,128)(2,1)S(1)}) custom-call(s32[3]{0:T(128)S(1)} %copy-done.1, bf16[624,768]{1,0:T(8,128)(2,1)S(1)} %get-tuple-element.131.gb_ref, bf16[768,624]{1,0:T(8,128)(2,1)S(1)} %get-tuple-element.114.gbt_ref, bf16[768,624]{1,0:T(8,128)(2,1)S(1)} %get-tuple-element.115.ht_ref, ...), custom_call_target="tpu_custom_call" | custom-call | flops 8800000000 | bytes 12036108 | tf_op jit(solution)/shard_map/back/pallas_call | solution.py:539
  115.6 3.9 %back.7 = (bf16[2,4,96,768]{3,2,1,0:T(8,128)(2,1)S(1)}, bf16[624,640]{1,0:T(8,128)(2,1)S(1)}) custom-call(s32[3]{0:T(128)S(1)} %copy-done.1, bf16[624,768]{1,0:T(8,128)(2,1)S(1)} %get-tuple-element.131.gb_ref, bf16[768,624]{1,0:T(8,128)(2,1)S(1)} %get-tuple-element.114.gbt_ref, bf16[768,624]{1,0:T(8,128)(2,1)S(1)} %get-tuple-element.115.ht_ref, ...), custom_call_target="tpu_custom_call" | custom-call | flops 8800000000 | bytes 12036108 | tf_op jit(solution)/shard_map/back/pallas_call | solution.py:539
  121.4 3.0 %collective-permute-done.22.early_ref = bf16[4,96,768]{2,1,0:T(8,128)(2,1)S(1)} collective-permute-done((bf16[4,96,768]{2,1,0:T(8,128)(2,1)S(1)}, bf16[4,96,768]{2,1,0:T(8,128)(2,1)S(1)}, u32[]{:S(2)}, u32[]{:S(2)}) %collective-permute-start.22) | collective-permute-done | bytes 589856 | tf_op jit(solution)/shard_map/ppermute | solution.py:33
  127.2 3.8 %input.1.gh_ref = f32[624,768]{1,0:T(8,128)S(1)} custom-call(s32[3]{0:T(128)S(1)} %copy-done.1, bf16[4,768,384]{2,1,0:T(8,128)(2,1)S(1)} %get-tuple-element.140.w_a, bf16[4,768,256]{2,1,0:T(8,128)(2,1)S(1)} %get-tuple-element.141.w_b, bf16[624,640]{1,0:T(8,128)(2,1)S(1)} %get-tuple-element.142.refs_0_, bf16[624,640]{1,0:T(8,128)(2,1)S(1)} %get-tuple-element.143.refs_1_, ...), custom_call_target="tpu_custom_call" | custom-call | flops 4400000000 | bytes 7127052 | tf_op jit(solution)/shard_map/input/pallas_call | solution.py:539
  130.9 2.0 %collective-permute-done.23.refs_2_ = bf16[4,96,384]{2,1,0:T(8,128)(2,1)S(1)} collective-permute-done((bf16[4,96,384]{2,1,0:T(8,128)(2,1)S(1)}, bf16[4,96,384]{2,1,0:T(8,128)(2,1)S(1)}, u32[]{:S(2)}, u32[]{:S(2)}) %collective-permute-start.23) | collective-permute-done | bytes 294944 | tf_op jit(solution)/shard_map/ppermute | solution.py:33
  134.7 2.7 %last.1 = (f32[3,200,768]{2,1,0:T(8,128)}, f32[13,768]{1,0:T(8,128)S(1)}) custom-call(bf16[3,200,768]{2,1,0:T(8,128)(2,1)S(1)} %bitcast.81, f32[624,768]{1,0:T(8,128)S(1)} %get-tuple-element.112.gres_ref, f32[624,768]{1,0:T(8,128)S(1)} %input.1.gh_ref, f32[128,768]{1,0:T(8,128)S(1)} %get-tuple-element.104.ex_ref, f32[13,768]{1,0:T(8,128)S(1)} %get-tuple-element.147.part_ref), custom_call_target="tpu_custom_call" | custom-call | flops 110000000 | bytes 5188608 | tf_op jit(solution)/shard_map/last/pallas_call | solution.py:539
  137.5 2.1 %collective-permute-start.32 = (bf16[2,96,384]{2,1,0:T(8,128)(2,1)S(1)}, bf16[2,96,384]{2,1,0:T(8,128)(2,1)S(1)}, u32[]{:S(2)}, u32[]{:S(2)}) collective-permute-start(bf16[2,96,384]{2,1,0:T(8,128)(2,1)S(1)} %get-tuple-element.159), channel_id=1, source_target_pairs={{0,8},{4,12},{8,0},{12,4},{16,24},{20,28},{24,16},{28,20},{1,9},{5... | collective-permute-start | bytes 442376 | tf_op jit(solution)/shard_map/ppermute | solution.py:24
  140.7 1.9 %convolution_bitcast_fusion.1 = f32[1,768,768]{2,1,0:T(8,128)} fusion(bf16[256,768]{1,0:T(8,128)(2,1)S(1)} %bitcast.78, bf16[256,768]{1,0:T(8,128)(2,1)S(1)} %get-tuple-element.166), kind=kOutput, calls=%fused_computation.1 | convolution fusion | flops 301989888 | bytes 3145728 | tf_op jit(solution)/shard_map/dot_general | solution.py:86
  145.0 2.3 %collective-permute-start.33 = (bf16[96,384]{1,0:T(8,128)(2,1)S(1)}, bf16[96,384]{1,0:T(8,128)(2,1)S(1)}, u32[]{:S(2)}, u32[]{:S(2)}) collective-permute-start(bf16[96,384]{1,0:T(8,128)(2,1)S(1)} %bitcast.91), channel_id=1, source_target_pairs={{0,16},{4,20},{8,24},{12,28},{16,0},{20,4},{24,8},{28,12},{1,17},{... | collective-permute-start | bytes 221192 | tf_op jit(solution)/shard_map/ppermute | solution.py:24
  148.9 1.9 %convolution_bitcast_fusion = f32[1,768,768]{2,1,0:T(8,128)} fusion(bf16[256,768]{1,0:T(8,128)(2,1)S(1)} %get-tuple-element.167, bf16[256,768]{1,0:T(8,128)(2,1)S(1)} %get-tuple-element.168), kind=kOutput, calls=%fused_computation | convolution fusion | flops 301989888 | bytes 3145728 | tf_op jit(solution)/shard_map/dot_general | solution.py:86
  150.8 3.3 %collective-permute-done.28 = f32[13,768]{1,0:T(8,128)S(1)} collective-permute-done((f32[13,768]{1,0:T(8,128)S(1)}, f32[13,768]{1,0:T(8,128)S(1)}, u32[]{:S(2)}, u32[]{:S(2)}) %collective-permute-start.28) | collective-permute-done | bytes 39968 | tf_op jit(solution)/shard_map/ppermute | solution.py:24
  155.1 4.1 %collective-permute-done.29.other_ref = f32[13,768]{1,0:T(8,128)S(1)} collective-permute-done((f32[13,768]{1,0:T(8,128)S(1)}, f32[13,768]{1,0:T(8,128)S(1)}, u32[]{:S(2)}, u32[]{:S(2)}) %collective-permute-start.29) | collective-permute-done | bytes 39968 | tf_op jit(solution)/shard_map/ppermute | solution.py:24
  (97 shorter events, 38.9 us)
Async XLA Ops:
  3.7 8.3 %collective-permute-start = (bf16[1,96,384]{2,1,0:T(8,128)(2,1)}, bf16[1,96,384]{2,1,0:T(8,128)(2,1)S(1)}, u32[]{:S(2)}, u32[]{:S(2)}) collective-permute-start(bf16[1,96,384]{2,1,0:T(8,128)(2,1)} %bitcast.100), channel_id=1, source_target_pairs={{0,16},{4,20},{8,24},{12,28},{16,0},{20,4},{24,8},{28,12},{1,17},{... | collective-permute-start | bytes 221192 | tf_op jit(solution)/shard_map/ppermute | solution.py:24
  12.8 5.5 %collective-permute-start.1 = (bf16[2,96,384]{2,1,0:T(8,128)(2,1)S(1)}, bf16[2,96,384]{2,1,0:T(8,128)(2,1)S(1)}, u32[]{:S(2)}, u32[]{:S(2)}) collective-permute-start(bf16[2,96,384]{2,1,0:T(8,128)(2,1)S(1)} %pad_maximum_fusion.6), channel_id=1, source_target_pairs={{0,8},{4,12},{8,0},{12,4},{16,24},{20,28},{24,16},{28,20},{1,9},{5... | collective-permute-start | bytes 442376 | tf_op jit(solution)/shard_map/ppermute | solution.py:24
  13.7 7.4 %collective-permute-start.3 = (bf16[1,96,128]{2,1,0:T(8,128)(2,1)}, bf16[1,96,128]{2,1,0:T(8,128)(2,1)S(1)}, u32[]{:S(2)}, u32[]{:S(2)}) collective-permute-start(bf16[1,96,128]{2,1,0:T(8,128)(2,1)} %bitcast.108), channel_id=1, source_target_pairs={{0,16},{4,20},{8,24},{12,28},{16,0},{20,4},{24,8},{28,12},{1,17},{... | collective-permute-start | bytes 73736 | tf_op jit(solution)/shard_map/ppermute | solution.py:24
  19.3 11.2 %collective-permute-start.2 = (bf16[4,96,384]{2,1,0:T(8,128)(2,1)S(1)}, bf16[4,96,384]{2,1,0:T(8,128)(2,1)S(1)}, u32[]{:S(2)}, u32[]{:S(2)}) collective-permute-start(bf16[4,96,384]{2,1,0:T(8,128)(2,1)S(1)} %get-tuple-element.171), channel_id=1, source_target_pairs={{0,4},{1,3},{2,6},{3,1},{4,0},{5,7},{6,2},{7,5},{8,12},{9,11},{10,... | collective-permute-start | bytes 884744 | tf_op jit(solution)/shard_map/ppermute | solution.py:33
  21.8 4.5 %collective-permute-start.4 = (bf16[2,96,128]{2,1,0:T(8,128)(2,1)S(1)}, bf16[2,96,128]{2,1,0:T(8,128)(2,1)S(1)}, u32[]{:S(2)}, u32[]{:S(2)}) collective-permute-start(bf16[2,96,128]{2,1,0:T(8,128)(2,1)S(1)} %pad_maximum_fusion.9), channel_id=1, source_target_pairs={{0,8},{4,12},{8,0},{12,4},{16,24},{20,28},{24,16},{28,20},{1,9},{5... | collective-permute-start | bytes 147464 | tf_op jit(solution)/shard_map/ppermute | solution.py:24
  22.5 7.0 %collective-permute-start.5 = (bf16[1,96,384]{2,1,0:T(8,128)(2,1)}, bf16[1,96,384]{2,1,0:T(8,128)(2,1)S(1)}, u32[]{:S(2)}, u32[]{:S(2)}) collective-permute-start(bf16[1,96,384]{2,1,0:T(8,128)(2,1)} %bitcast.111), channel_id=1, source_target_pairs={{0,16},{4,20},{8,24},{12,28},{16,0},{20,4},{24,8},{28,12},{1,17},{... | collective-permute-start | bytes 221192 | tf_op jit(solution)/shard_map/ppermute | solution.py:24
  30.5 13.5 %collective-permute-start.6 = (bf16[2,4,96,384]{3,2,1,0:T(8,128)(2,1)S(1)}, bf16[2,4,96,384]{3,2,1,0:T(8,128)(2,1)S(1)}, u32[]{:S(2)}, u32[]{:S(2)}) collective-permute-start(bf16[2,4,96,384]{3,2,1,0:T(8,128)(2,1)S(1)} %pad_maximum_fusion.refs_0_), channel_id=1, source_target_pairs={{0,2},{1,5},{2,0},{3,7},{4,6},{5,1},{6,4},{7,3},{8,10},{9,13},{10,... | collective-permute-start | bytes 1769480 | tf_op jit(solution)/shard_map/ppermute | solution.py:33
  32.1 5.1 %collective-permute-start.8 = (bf16[2,96,384]{2,1,0:T(8,128)(2,1)S(1)}, bf16[2,96,384]{2,1,0:T(8,128)(2,1)S(1)}, u32[]{:S(2)}, u32[]{:S(2)}) collective-permute-start(bf16[2,96,384]{2,1,0:T(8,128)(2,1)S(1)} %pad_maximum_fusion.7), channel_id=1, source_target_pairs={{0,8},{4,12},{8,0},{12,4},{16,24},{20,28},{24,16},{28,20},{1,9},{5... | collective-permute-start | bytes 442376 | tf_op jit(solution)/shard_map/ppermute | solution.py:24
  32.1 13.2 %collective-permute-start.11 = (bf16[2,4,96,384]{3,2,1,0:T(8,128)(2,1)S(1)}, bf16[2,4,96,384]{3,2,1,0:T(8,128)(2,1)S(1)}, u32[]{:S(2)}, u32[]{:S(2)}) collective-permute-start(bf16[2,4,96,384]{3,2,1,0:T(8,128)(2,1)S(1)} %pad_maximum_fusion.refs_0_), channel_id=1, source_target_pairs={{0,1},{1,0},{2,3},{3,2},{4,5},{5,4},{6,7},{7,6},{8,9},{9,8},{10,11... | collective-permute-start | bytes 1769480 | tf_op jit(solution)/shard_map/ppermute | solution.py:24
  32.1 5.7 %collective-permute-start.7 = (bf16[4,96,128]{2,1,0:T(8,128)(2,1)S(1)}, bf16[4,96,128]{2,1,0:T(8,128)(2,1)S(1)}, u32[]{:S(2)}, u32[]{:S(2)}) collective-permute-start(bf16[4,96,128]{2,1,0:T(8,128)(2,1)S(1)} %pad_maximum_fusion.8), channel_id=1, source_target_pairs={{0,4},{4,0},{8,12},{12,8},{16,20},{20,16},{24,28},{28,24},{1,5},{5... | collective-permute-start | bytes 294920 | tf_op jit(solution)/shard_map/ppermute | solution.py:24
  37.3 6.8 %collective-permute-start.9 = (bf16[4,96,384]{2,1,0:T(8,128)(2,1)S(1)}, bf16[4,96,384]{2,1,0:T(8,128)(2,1)S(1)}, u32[]{:S(2)}, u32[]{:S(2)}) collective-permute-start(bf16[4,96,384]{2,1,0:T(8,128)(2,1)S(1)} %constant_dynamic-update-slice_fusion), channel_id=1, source_target_pairs={{0,4},{1,3},{2,6},{3,1},{4,0},{5,7},{6,2},{7,5},{8,12},{9,11},{10,... | collective-permute-start | bytes 884744 | tf_op jit(solution)/shard_map/ppermute | solution.py:33
  44.0 2.0 %collective-permute-start.12 = (bf16[2,4,96,384]{3,2,1,0:T(8,128)(2,1)S(1)}, bf16[2,4,96,384]{3,2,1,0:T(8,128)(2,1)S(1)}, u32[]{:S(2)}, u32[]{:S(2)}) collective-permute-start(bf16[2,4,96,384]{3,2,1,0:T(8,128)(2,1)S(1)} %collective-permute-done.6.refs_1_), channel_id=1, source_target_pairs={{0,1},{1,0},{2,3},{3,2},{4,5},{5,4},{6,7},{7,6},{8,9},{9,8},{10,11... | collective-permute-start | bytes 1769480 | tf_op jit(solution)/shard_map/ppermute | solution.py:24
  44.1 9.9 %collective-permute-start.10 = (bf16[2,4,96,384]{3,2,1,0:T(8,128)(2,1)S(1)}, bf16[2,4,96,384]{3,2,1,0:T(8,128)(2,1)S(1)}, u32[]{:S(2)}, u32[]{:S(2)}) collective-permute-start(bf16[2,4,96,384]{3,2,1,0:T(8,128)(2,1)S(1)} %pad_maximum_fusion.1.refs_0_), channel_id=1, source_target_pairs={{0,2},{1,5},{2,0},{3,7},{4,6},{5,1},{6,4},{7,3},{8,10},{9,13},{10,... | collective-permute-start | bytes 1769480 | tf_op jit(solution)/shard_map/ppermute | solution.py:33
  45.3 8.8 %collective-permute-start.13 = (bf16[2,4,96,384]{3,2,1,0:T(8,128)(2,1)S(1)}, bf16[2,4,96,384]{3,2,1,0:T(8,128)(2,1)S(1)}, u32[]{:S(2)}, u32[]{:S(2)}) collective-permute-start(bf16[2,4,96,384]{3,2,1,0:T(8,128)(2,1)S(1)} %pad_maximum_fusion.1.refs_0_), channel_id=1, source_target_pairs={{0,1},{1,0},{2,3},{3,2},{4,5},{5,4},{6,7},{7,6},{8,9},{9,8},{10,11... | collective-permute-start | bytes 1769480 | tf_op jit(solution)/shard_map/ppermute | solution.py:24
  54.1 2.0 %collective-permute-start.14 = (bf16[2,4,96,384]{3,2,1,0:T(8,128)(2,1)S(1)}, bf16[2,4,96,384]{3,2,1,0:T(8,128)(2,1)S(1)}, u32[]{:S(2)}, u32[]{:S(2)}) collective-permute-start(bf16[2,4,96,384]{3,2,1,0:T(8,128)(2,1)S(1)} %collective-permute-done.10.refs_1_), channel_id=1, source_target_pairs={{0,1},{1,0},{2,3},{3,2},{4,5},{5,4},{6,7},{7,6},{8,9},{9,8},{10,11... | collective-permute-start | bytes 1769480 | tf_op jit(solution)/shard_map/ppermute | solution.py:24
  74.5 4.6 %collective-permute-start.15 = (bf16[1,8,8,768]{3,2,1,0:T(8,128)(2,1)S(1)}, bf16[1,8,8,768]{3,2,1,0:T(8,128)(2,1)S(1)}, u32[]{:S(2)}, u32[]{:S(2)}) collective-permute-start(bf16[1,8,8,768]{3,2,1,0:T(8,128)(2,1)S(1)} %bitcast.97), channel_id=1, source_target_pairs={{0,2},{1,3},{2,0},{3,1},{4,6},{5,7},{6,4},{7,5},{8,10},{9,11},{10,... | collective-permute-start | bytes 294920 | tf_op jit(solution)/shard_map/ppermute | solution.py:24
  84.1 4.9 %collective-permute-start.18 = (bf16[1,1,8,8,768]{4,3,2,1,0:T(8,128)(2,1)S(1)}, bf16[1,1,8,8,768]{4,3,2,1,0:T(8,128)(2,1)S(1)}, u32[]{:S(2)}, u32[]{:S(2)}) collective-permute-start(bf16[1,1,8,8,768]{4,3,2,1,0:T(8,128)(2,1)S(1)} %slice_bitcast_fusion.2), channel_id=1, source_target_pairs={{0,2},{1,3},{2,0},{3,1},{4,6},{5,7},{6,4},{7,5},{8,10},{9,11},{10,... | collective-permute-start | bytes 294920 | tf_op jit(solution)/shard_map/ppermute | solution.py:24
  106.1 3.8 %collective-permute-start.19 = (bf16[2,4,96,768]{3,2,1,0:T(8,128)(2,1)S(1)}, bf16[2,4,96,768]{3,2,1,0:T(8,128)(2,1)S(1)}, u32[]{:S(2)}, u32[]{:S(2)}) collective-permute-start(bf16[2,4,96,768]{3,2,1,0:T(8,128)(2,1)S(1)} %get-tuple-element.125), channel_id=1, source_target_pairs={{0,1},{1,0},{2,3},{3,2},{4,5},{5,4},{6,7},{7,6},{8,9},{9,8},{10,11... | collective-permute-start | bytes 3538952 | tf_op jit(solution)/shard_map/ppermute | solution.py:24
  113.9 5.6 %collective-permute-start.20 = (bf16[2,4,96,768]{3,2,1,0:T(8,128)(2,1)S(1)}, bf16[2,4,96,768]{3,2,1,0:T(8,128)(2,1)S(1)}, u32[]{:S(2)}, u32[]{:S(2)}) collective-permute-start(bf16[2,4,96,768]{3,2,1,0:T(8,128)(2,1)S(1)} %get-tuple-element.133), channel_id=1, source_target_pairs={{0,1},{1,0},{2,3},{3,2},{4,5},{5,4},{6,7},{7,6},{8,9},{9,8},{10,11... | collective-permute-start | bytes 3538952 | tf_op jit(solution)/shard_map/ppermute | solution.py:24
  114.5 9.9 %collective-permute-start.22 = (bf16[4,96,768]{2,1,0:T(8,128)(2,1)S(1)}, bf16[4,96,768]{2,1,0:T(8,128)(2,1)S(1)}, u32[]{:S(2)}, u32[]{:S(2)}) collective-permute-start(bf16[4,96,768]{2,1,0:T(8,128)(2,1)S(1)} %bitcast.89), channel_id=1, source_target_pairs={{0,2},{1,5},{2,0},{3,7},{4,6},{5,1},{6,4},{7,3},{8,10},{9,13},{10,... | collective-permute-start | bytes 1769480 | tf_op jit(solution)/shard_map/ppermute | solution.py:33
  120.4 14.0 %collective-permute-start.21 = (bf16[4,96,768]{2,1,0:T(8,128)(2,1)S(1)}, bf16[4,96,768]{2,1,0:T(8,128)(2,1)S(1)}, u32[]{:S(2)}, u32[]{:S(2)}) collective-permute-start(bf16[4,96,768]{2,1,0:T(8,128)(2,1)S(1)} %get-tuple-element.135), channel_id=1, source_target_pairs={{0,2},{1,5},{2,0},{3,7},{4,6},{5,1},{6,4},{7,3},{8,10},{9,13},{10,... | collective-permute-start | bytes 1769480 | tf_op jit(solution)/shard_map/ppermute | solution.py:33
  125.1 7.9 %collective-permute-start.23 = (bf16[4,96,384]{2,1,0:T(8,128)(2,1)S(1)}, bf16[4,96,384]{2,1,0:T(8,128)(2,1)S(1)}, u32[]{:S(2)}, u32[]{:S(2)}) collective-permute-start(bf16[4,96,384]{2,1,0:T(8,128)(2,1)S(1)} %get-tuple-element.138), channel_id=1, source_target_pairs={{0,4},{1,3},{2,6},{3,1},{4,0},{5,7},{6,2},{7,5},{8,12},{9,11},{10,... | collective-permute-start | bytes 884744 | tf_op jit(solution)/shard_map/ppermute | solution.py:33
  125.5 11.9 %collective-permute-start.31 = (bf16[4,96,384]{2,1,0:T(8,128)(2,1)S(1)}, bf16[4,96,384]{2,1,0:T(8,128)(2,1)S(1)}, u32[]{:S(2)}, u32[]{:S(2)}) collective-permute-start(bf16[4,96,384]{2,1,0:T(8,128)(2,1)S(1)} %get-tuple-element.157), channel_id=1, source_target_pairs={{0,4},{1,3},{2,6},{3,1},{4,0},{5,7},{6,2},{7,5},{8,12},{9,11},{10,... | collective-permute-start | bytes 884744 | tf_op jit(solution)/shard_map/ppermute | solution.py:33
  134.5 9.2 %collective-permute-start.24 = (bf16[2,96,384]{2,1,0:T(8,128)(2,1)S(1)}, bf16[2,96,384]{2,1,0:T(8,128)(2,1)S(1)}, u32[]{:S(2)}, u32[]{:S(2)}) collective-permute-start(bf16[2,96,384]{2,1,0:T(8,128)(2,1)S(1)} %get-tuple-element.149), channel_id=1, source_target_pairs={{0,8},{4,12},{8,0},{12,4},{16,24},{20,28},{24,16},{28,20},{1,9},{5... | collective-permute-start | bytes 442376 | tf_op jit(solution)/shard_map/ppermute | solution.py:24
  137.3 2.2 %collective-permute-start.25 = (f32[13,768]{1,0:T(8,128)S(1)}, f32[13,768]{1,0:T(8,128)S(1)}, u32[]{:S(2)}, u32[]{:S(2)}) collective-permute-start(f32[13,768]{1,0:T(8,128)S(1)} %get-tuple-element.150), channel_id=1, source_target_pairs={{0,1},{1,0},{2,3},{3,2},{4,5},{5,4},{6,7},{7,6},{8,9},{9,8},{10,11... | collective-permute-start | bytes 119816 | tf_op jit(solution)/shard_map/ppermute | solution.py:24
  137.5 7.4 %collective-permute-start.32 = (bf16[2,96,384]{2,1,0:T(8,128)(2,1)S(1)}, bf16[2,96,384]{2,1,0:T(8,128)(2,1)S(1)}, u32[]{:S(2)}, u32[]{:S(2)}) collective-permute-start(bf16[2,96,384]{2,1,0:T(8,128)(2,1)S(1)} %get-tuple-element.159), channel_id=1, source_target_pairs={{0,8},{4,12},{8,0},{12,4},{16,24},{20,28},{24,16},{28,20},{1,9},{5... | collective-permute-start | bytes 442376 | tf_op jit(solution)/shard_map/ppermute | solution.py:24
  139.5 4.2 %collective-permute-start.26 = (f32[13,768]{1,0:T(8,128)S(1)}, f32[13,768]{1,0:T(8,128)S(1)}, u32[]{:S(2)}, u32[]{:S(2)}) collective-permute-start(f32[13,768]{1,0:T(8,128)S(1)} %add.20), channel_id=1, source_target_pairs={{0,2},{1,3},{2,0},{3,1},{4,6},{5,7},{6,4},{7,5},{8,10},{9,11},{10,... | collective-permute-start | bytes 119816 | tf_op jit(solution)/shard_map/ppermute | solution.py:24
  143.7 4.2 %collective-permute-start.27 = (f32[13,768]{1,0:T(8,128)S(1)}, f32[13,768]{1,0:T(8,128)S(1)}, u32[]{:S(2)}, u32[]{:S(2)}) collective-permute-start(f32[13,768]{1,0:T(8,128)S(1)} %add.21), channel_id=1, source_target_pairs={{0,4},{4,0},{8,12},{12,8},{16,20},{20,16},{24,28},{28,24},{1,5},{5... | collective-permute-start | bytes 119816 | tf_op jit(solution)/shard_map/ppermute | solution.py:24
  144.1 10.1 %collective-permute-start.30 = (bf16[96,384]{1,0:T(8,128)(2,1)S(1)}, bf16[96,384]{1,0:T(8,128)(2,1)S(1)}, u32[]{:S(2)}, u32[]{:S(2)}) collective-permute-start(bf16[96,384]{1,0:T(8,128)(2,1)S(1)} %bitcast.90), channel_id=1, source_target_pairs={{0,16},{4,20},{8,24},{12,28},{16,0},{20,4},{24,8},{28,12},{1,17},{... | collective-permute-start | bytes 221192 | tf_op jit(solution)/shard_map/ppermute | solution.py:24
  145.0 9.3 %collective-permute-start.33 = (bf16[96,384]{1,0:T(8,128)(2,1)S(1)}, bf16[96,384]{1,0:T(8,128)(2,1)S(1)}, u32[]{:S(2)}, u32[]{:S(2)}) collective-permute-start(bf16[96,384]{1,0:T(8,128)(2,1)S(1)} %bitcast.91), channel_id=1, source_target_pairs={{0,16},{4,20},{8,24},{12,28},{16,0},{20,4},{24,8},{28,12},{1,17},{... | collective-permute-start | bytes 221192 | tf_op jit(solution)/shard_map/ppermute | solution.py:24
  147.9 6.3 %collective-permute-start.28 = (f32[13,768]{1,0:T(8,128)S(1)}, f32[13,768]{1,0:T(8,128)S(1)}, u32[]{:S(2)}, u32[]{:S(2)}) collective-permute-start(f32[13,768]{1,0:T(8,128)S(1)} %add.22), channel_id=1, source_target_pairs={{0,8},{4,12},{8,0},{12,4},{16,24},{20,28},{24,16},{28,20},{1,9},{5... | collective-permute-start | bytes 119816 | tf_op jit(solution)/shard_map/ppermute | solution.py:24
  154.2 5.0 %collective-permute-start.29 = (f32[13,768]{1,0:T(8,128)S(1)}, f32[13,768]{1,0:T(8,128)S(1)}, u32[]{:S(2)}, u32[]{:S(2)}) collective-permute-start(f32[13,768]{1,0:T(8,128)S(1)} %add.23.own_ref), channel_id=1, source_target_pairs={{0,16},{4,20},{8,24},{12,28},{16,0},{20,4},{24,8},{28,12},{1,17},{... | collective-permute-start | bytes 119816 | tf_op jit(solution)/shard_map/ppermute | solution.py:24
  (8 other events, 91.8 us)

commit v10 on v9

--- a/solution.py
+++ b/solution.py
@@ -791,15 +791,6 @@
             grant=8,
         )
         second = swap_both(second, dp, mp, (0, 2), (1, 0))
-        thirds = call(
-            blend_late_kernel,
-            [((high, d_rows, half), bf16)] * 2,
-            (words, far_kept[0], own_sum, early),
-            flops=cost(1),
-            name="blend_late",
-            grant=8,
-        )
-        thirds = [swap_both(third, dp, mp, (1, 0), (0, 2)) for third in thirds]
         grad_h = call(
             input_kernel,
             [((count, width), f32)],
@@ -809,11 +800,20 @@
             grant=8,
             order=order,
         )[0]
+        early, grad_h = lax.optimization_barrier((early, grad_h))
+        thirds = call(
+            blend_late_kernel,
+            [((high, d_rows, half), bf16)] * 2,
+            (words, far_kept[0], own_sum, early),
+            flops=cost(1),
+            name="blend_late",
+            grant=8,
+        )
+        thirds = [swap_both(third, dp, mp, (1, 0), (0, 2)) for third in thirds]
         pieces = [
             list(fold((near_sum, second, third), False, (k * half, k * half, 0), half))
             for k, third in enumerate(thirds)
         ]
-        pieces[0][1], grad_h = lax.optimization_barrier((pieces[0][1], grad_h))
         grad_tokens, small = call(
             last_kernel,
             [((images, seq, width), f32), ((experts + 5, width), f32)],
@@ -825,8 +825,8 @@
             experts=experts,
             **exact,
         )
-        for bit in bits_of(mp)[::-1]:
-            small = small + swap(small, "mp", mp, bit)
+        for bit in bits_of(dp)[:-1]:
+            small = small + swap(small, "dp", dp, bit)
         parts = []
         for k, (kept, left) in enumerate(pieces):
             for bit in bits_of(high)[:0:-1]:
@@ -844,8 +844,8 @@
             scalars=0,
             grant=6,
         )
-        for bit in bits_of(dp)[:0:-1]:
-            small = small + swap(small, "dp", dp, bit)
+        small = small + swap(small, "dp", dp, 1)
+        small = small + swap(small, "mp", mp, 2)
         grad_one, grad_two, grad_router, root_squares = call(
             finish_kernel,
             [
@@ -854,7 +854,7 @@
                 ((experts, d_rows), f32),
                 ((3, mp * images), f32),
             ],
-            (words, small, swap(small, "dp", dp, bits_of(dp)[0])),
+            (words, small, swap(small, "mp", mp, 1)),
             flops=cost(1),
             name="finish",
             grant=4,

time: 161 us -> 154 us (0.957)
  waiting for transfers between devices: 47.7 us -> 42.5 us
    ppermute x8, waiting for transfers between devices: 13.1 us -> 6.64 us  [swap_both(): return lax.ppermute(array_in, ('dp', 'mp'), pairs)]
  transfers between devices with their start and end apart: 34 -> 34, of which waited for: 19 -> 19; matrix products, arithmetic and copies ran while one was open for 5% -> 5% of each run, Pallas kernels for 15% -> 16%
where the time goes in v10:
time: 154 us
  Pallas kernels  49.1 us (32%)
  waiting for transfers between devices  42.5 us (28%)
  starting transfers between devices  31.9 us (21%)
  blocking collectives  20.1 us (13%)
  other arithmetic  5.16 us (3%)
  matrix products  3.85 us (2%)
    pallas_call x21, Pallas kernels, call(): pl.pallas_call(functools.partial(kernel, **static), out_shape=[jax.ShapeD...  46.7 us
    ppermute x26, waiting for transfers between devices, swap(): lax.ppermute(array_in, axis_name, [(i, i ^ bit) for i in range(size)])  35.8 us
    ppermute x26, starting transfers between devices, swap(): lax.ppermute(array_in, axis_name, [(i, i ^ bit) for i in range(size)])  22.7 us
    all_to_all x1, blocking collectives, per_device(): got = lax.all_to_all(got, 'dp', split_axis=0, concat_axis=0, tiled=True)  10.6 us
    all_to_all x1, blocking collectives, per_device(): back = lax.all_to_all(back, 'dp', split_axis=0, concat_axis=0, tiled=True)  9.51 us
    ppermute x8, starting transfers between devices, swap_both(): return lax.ppermute(array_in, ('dp', 'mp'), pairs)  9.24 us
    ppermute x8, waiting for transfers between devices, swap_both(): return lax.ppermute(array_in, ('dp', 'mp'), pairs)  6.64 us
    dot_general x2, matrix products, mm_tn(): lax.dot_general(a, b, (((0,), (0,)), ((), ())), preferred_element_type=f32)  3.85 us
  transfers between devices with their start and end apart: 34, of which 19 were waited for; matrix products, arithmetic and copies ran while one was open for 5% of the time, Pallas kernels for 16%

profile of v10, /device:TPU:0, one launch (start us, length us, event | category | flops | bytes accessed | tf_op | source)
XLA Modules:
  0.0 153.8 jit_solution(1037885643702145432)
XLA Ops:
  1.2 2.4 %pack.1 = (bf16[96,384]{1,0:T(8,128)(2,1)}, bf16[96,384]{1,0:T(8,128)(2,1)}, bf16[96,128]{1,0:T(8,128)(2,1)}) custom-call(s32[3]{0:T(128)} %pad_add_fusion.me_ref, bf16[3,96,192]{2,1,0:T(8,128)(2,1)} %bitcast.106, bf16[192,96]{1,0:T(8,128)(2,1)} %out_hbm.1, bf16[1,96]{1,0:T(2,128)(2,1)} %bitcast.114, bf16[1,96]{1,0:T(2,128)(2,1)} %bitcast.115, ...), custom_call_target="tpu_custom_call" | custom-call | tf_op jit(solution)/shard_map/pack/pallas_call | solution.py:582
  3.7 4.1 %collective-permute-start = (bf16[1,96,384]{2,1,0:T(8,128)(2,1)}, bf16[1,96,384]{2,1,0:T(8,128)(2,1)S(1)}, u32[]{:S(2)}, u32[]{:S(2)}) collective-permute-start(bf16[1,96,384]{2,1,0:T(8,128)(2,1)} %bitcast.100), channel_id=1, source_target_pairs={{0,16},{4,20},{8,24},{12,28},{16,0},{20,4},{24,8},{28,12},{1,17},{... | collective-permute-start | bytes 221192 | tf_op jit(solution)/shard_map/ppermute | solution.py:24
  7.8 4.1 %collective-permute-done = bf16[1,96,384]{2,1,0:T(8,128)(2,1)S(1)} collective-permute-done((bf16[1,96,384]{2,1,0:T(8,128)(2,1)}, bf16[1,96,384]{2,1,0:T(8,128)(2,1)S(1)}, u32[]{:S(2)}, u32[]{:S(2)}) %collective-permute-start) | collective-permute-done | bytes 73760 | tf_op jit(solution)/shard_map/ppermute | solution.py:24
  13.7 3.3 %collective-permute-start.3 = (bf16[1,96,128]{2,1,0:T(8,128)(2,1)}, bf16[1,96,128]{2,1,0:T(8,128)(2,1)S(1)}, u32[]{:S(2)}, u32[]{:S(2)}) collective-permute-start(bf16[1,96,128]{2,1,0:T(8,128)(2,1)} %bitcast.108), channel_id=1, source_target_pairs={{0,16},{4,20},{8,24},{12,28},{16,0},{20,4},{24,8},{28,12},{1,17},{... | collective-permute-start | bytes 73736 | tf_op jit(solution)/shard_map/ppermute | solution.py:24
  19.3 1.8 %collective-permute-start.2 = (bf16[4,96,384]{2,1,0:T(8,128)(2,1)S(1)}, bf16[4,96,384]{2,1,0:T(8,128)(2,1)S(1)}, u32[]{:S(2)}, u32[]{:S(2)}) collective-permute-start(bf16[4,96,384]{2,1,0:T(8,128)(2,1)S(1)} %get-tuple-element.171), channel_id=1, source_target_pairs={{0,4},{1,3},{2,6},{3,1},{4,0},{5,7},{6,2},{7,5},{8,12},{9,11},{10,... | collective-permute-start | bytes 884744 | tf_op jit(solution)/shard_map/ppermute | solution.py:33
  22.5 3.8 %collective-permute-start.5 = (bf16[1,96,384]{2,1,0:T(8,128)(2,1)}, bf16[1,96,384]{2,1,0:T(8,128)(2,1)S(1)}, u32[]{:S(2)}, u32[]{:S(2)}) collective-permute-start(bf16[1,96,384]{2,1,0:T(8,128)(2,1)} %bitcast.111), channel_id=1, source_target_pairs={{0,16},{4,20},{8,24},{12,28},{16,0},{20,4},{24,8},{28,12},{1,17},{... | collective-permute-start | bytes 221192 | tf_op jit(solution)/shard_map/ppermute | solution.py:24
  27.0 2.5 %collective-permute-done.5 = bf16[1,96,384]{2,1,0:T(8,128)(2,1)S(1)} collective-permute-done((bf16[1,96,384]{2,1,0:T(8,128)(2,1)}, bf16[1,96,384]{2,1,0:T(8,128)(2,1)S(1)}, u32[]{:S(2)}, u32[]{:S(2)}) %collective-permute-start.5) | collective-permute-done | bytes 73760 | tf_op jit(solution)/shard_map/ppermute | solution.py:24
  32.6 4.6 %collective-permute-done.8 = bf16[2,96,384]{2,1,0:T(8,128)(2,1)S(1)} collective-permute-done((bf16[2,96,384]{2,1,0:T(8,128)(2,1)S(1)}, bf16[2,96,384]{2,1,0:T(8,128)(2,1)S(1)}, u32[]{:S(2)}, u32[]{:S(2)}) %collective-permute-start.8) | collective-permute-done | bytes 147488 | tf_op jit(solution)/shard_map/ppermute | solution.py:24
  39.5 4.6 %collective-permute-done.9 = bf16[4,96,384]{2,1,0:T(8,128)(2,1)S(1)} collective-permute-done((bf16[4,96,384]{2,1,0:T(8,128)(2,1)S(1)}, bf16[4,96,384]{2,1,0:T(8,128)(2,1)S(1)}, u32[]{:S(2)}, u32[]{:S(2)}) %collective-permute-start.9) | collective-permute-done | bytes 294944 | tf_op jit(solution)/shard_map/ppermute | solution.py:33
  46.1 6.0 %front_pair.1 = (bf16[4,768,384]{2,1,0:T(8,128)(2,1)S(1)}, bf16[4,624,384]{2,1,0:T(8,128)(2,1)S(1)}, bf16[4,3,2,208,208]{4,3,2,1,0:T(8,128)(2,1)S(1)}, bf16[4,624,128]{2,1,0:T(8,128)(2,1)S(1)}) custom-call(s32[3]{0:T(128)S(1)} %copy-done.1, bf16[624,768]{1,0:T(8,128)(2,1)S(1)} %get-tuple-element.97.h_ref, s32[12,200]{1,0:T(8,128)S(1)} %copy-done.5, ...), custom_call_target="tpu_custom_call" | custom-call | flops 11000000512 | bytes 3327372 | tf_op jit(solution)/shard_map/front_pair/pallas_call | solution.py:539
  52.0 2.0 %collective-permute-done.10.refs_1_ = bf16[2,4,96,384]{3,2,1,0:T(8,128)(2,1)S(1)} collective-permute-done((bf16[2,4,96,384]{3,2,1,0:T(8,128)(2,1)S(1)}, bf16[2,4,96,384]{3,2,1,0:T(8,128)(2,1)S(1)}, u32[]{:S(2)}, u32[]{:S(2)}) %collective-permute-start.10) | collective-permute-done | bytes 589856 | tf_op jit(solution)/shard_map/ppermute | solution.py:33
  54.1 2.0 %collective-permute-done.14.refs_3_ = bf16[2,4,96,384]{3,2,1,0:T(8,128)(2,1)S(1)} collective-permute-done((bf16[2,4,96,384]{3,2,1,0:T(8,128)(2,1)S(1)}, bf16[2,4,96,384]{3,2,1,0:T(8,128)(2,1)S(1)}, u32[]{:S(2)}, u32[]{:S(2)}) %collective-permute-start.14) | collective-permute-done | bytes 589856 | tf_op jit(solution)/shard_map/ppermute | solution.py:24
  56.1 5.1 %front_last.1 = (bf16[4,768,256]{2,1,0:T(8,128)(2,1)S(1)}, bf16[4,624,256]{2,1,0:T(8,128)(2,1)S(1)}, bf16[4,3,208,208]{3,2,1,0:T(8,128)(2,1)S(1)}, bf16[624,1024...) custom-call(s32[3]{0:T(128)S(1)} %copy-done.1, ...), custom_call_target="tpu_custom_call" | custom-call | flops 7699999744 | bytes 3966348 | tf_op jit(solution)/shard_map/front_last/pallas_call | solution.py:539
  61.3 2.7 %route.1 = (f32[624,768]{1,0:T(8,128)S(1)}, bf16[624,768]{1,0:T(8,128)(2,1)S(1)}, f32[2,3,8,208]{3,2,1,0:T(8,128)S(1)}, bf16[64,768]{1,0:T(8,128)(2,1)S(1)}, f32[3,1,128]{2,1,0:T(1,128)S(1)}) custom-call(s32[3]{0:T(128)S(1)} %copy-done.1, bf16[3,200,768]{2,1,0:T(8,128)(2,1)S(1)} %bitcast.80, f32[624,768]{1,0:T(8,128)S(1)} %get-tuple-element.103.br_ref, ...), custom_call_target="tpu_custom_call" | custom-call | flops 2200000000 | bytes 4162956 | tf_op jit(solution)/shard_map/route/pallas_call | solution.py:539
  64.0 10.6 %all_to_all.10 = bf16[8,8,768]{2,1,0:T(8,128)(2,1)S(1)} all-to-all(bf16[8,8,768]{2,1,0:T(8,128)(2,1)S(1)} %bitcast.84), channel_id=1, replica_groups=mesh['dp'=8,'mp'=4] {'dp'}, dimensions={0} | all-to-all | bytes 196608 | tf_op jit(solution)/shard_map/all_to_all | solution.py:695
  75.6 3.5 %collective-permute-done.15 = bf16[1,8,8,768]{3,2,1,0:T(8,128)(2,1)S(1)} collective-permute-done((bf16[1,8,8,768]{3,2,1,0:T(8,128)(2,1)S(1)}, bf16[1,8,8,768]{3,2,1,0:T(8,128)(2,1)S(1)}, u32[]{:S(2)}, u32[]{:S(2)}) %collective-permute-start.15) | collective-permute-done | bytes 98336 | tf_op jit(solution)/shard_map/ppermute | solution.py:24
  80.7 1.7 %expert.1 = (bf16[256,768]{1,0:T(8,128)(2,1)S(1)}, bf16[256,768]{1,0:T(8,128)(2,1)S(1)}, bf16[256,768]{1,0:T(8,128)(2,1)S(1)}, bf16[256,768]{1,0:T(8,128)(2,1)S(1)}) custom-call(bf16[256,768]{1,0:T(8,128)(2,1)S(1)} %bitcast.77, bf16[768,768]{1,0:T(8,128)(2,1)S(1)} %bitcast.85, bf16[768,768]{1,0:T(8,128)(2,1)S(1)} %bitcast.86), custom_call_target="tpu_custom_call" | custom-call | flops 2200000000 | bytes 2752512 | tf_op jit(solution)/shard_map/expert/pallas_call | solution.py:539
  85.2 3.8 %collective-permute-done.18 = bf16[1,1,8,8,768]{4,3,2,1,0:T(8,128)(2,1)S(1)} collective-permute-done((bf16[1,1,8,8,768]{4,3,2,1,0:T(8,128)(2,1)S(1)}, bf16[1,1,8,8,768]{4,3,2,1,0:T(8,128)(2,1)S(1)}, u32[]{:S(2)}, u32[]{:S(2)}) %collective-permute-start.18) | collective-permute-done | bytes 98336 | tf_op jit(solution)/shard_map/ppermute | solution.py:24
  89.0 9.5 %all_to_all.11 = bf16[8,8,768]{2,1,0:T(8,128)(2,1)S(1)} all-to-all(bf16[8,8,768]{2,1,0:T(8,128)(2,1)S(1)} %fusion.5), channel_id=1, replica_groups=mesh['dp'=8,'mp'=4] {'dp'}, dimensions={0} | all-to-all | bytes 196608 | tf_op jit(solution)/shard_map/all_to_all | solution.py:715
  98.5 3.9 %mix.1 = (bf16[3,200,768]{2,1,0:T(8,128)(2,1)}, f32[624,768]{1,0:T(8,128)S(1)}, bf16[624,768]{1,0:T(8,128)(2,1)S(1)}, bf16[768,624]{1,0:T(8,128)(2,1)S(1)}, f32[13,768]{1,0:T(8,128)S(1)}) custom-call(s32[3]{0:T(128)S(1)} %copy-done.1, f32[624,768]{1,0:T(8,128)S(1)} %get-tuple-element.105.res_ref, bf16[624,768]{1,0:T(8,128)(2,1)S(1)} %get-tuple-element.106.h_ref, ...), custom_call_target="tpu_custom_call" | custom-call | flops 5500000256 | bytes 4315020 | tf_op jit(solution)/shard_map/mix/pallas_call | solution.py:539
  102.4 3.7 %back.4 = (bf16[2,4,96,768]{3,2,1,0:T(8,128)(2,1)S(1)}, bf16[624,640]{1,0:T(8,128)(2,1)S(1)}) custom-call(s32[3]{0:T(128)S(1)} %copy-done.1, bf16[624,768]{1,0:T(8,128)(2,1)S(1)} %get-tuple-element.136.gb_ref, bf16[768,624]{1,0:T(8,128)(2,1)S(1)} %get-tuple-element.114.gbt_ref, bf16[768,624]{1,0:T(8,128)(2,1)S(1)} %get-tuple-element.115.ht_ref, ...), custom_call_target="tpu_custom_call" | custom-call | flops 8800000000 | bytes 12036108 | tf_op jit(solution)/shard_map/back/pallas_call | solution.py:539
  106.2 3.7 %back.5 = (bf16[2,4,96,768]{3,2,1,0:T(8,128)(2,1)S(1)}, bf16[624,640]{1,0:T(8,128)(2,1)S(1)}) custom-call(s32[3]{0:T(128)S(1)} %copy-done.1, bf16[624,768]{1,0:T(8,128)(2,1)S(1)} %get-tuple-element.136.gb_ref, bf16[768,624]{1,0:T(8,128)(2,1)S(1)} %get-tuple-element.114.gbt_ref, bf16[768,624]{1,0:T(8,128)(2,1)S(1)} %get-tuple-element.115.ht_ref, ...), custom_call_target="tpu_custom_call" | custom-call | flops 8800000000 | bytes 12036108 | tf_op jit(solution)/shard_map/back/pallas_call | solution.py:539
  110.2 3.7 %back.6 = (bf16[2,4,96,768]{3,2,1,0:T(8,128)(2,1)S(1)}, bf16[624,640]{1,0:T(8,128)(2,1)S(1)}) custom-call(s32[3]{0:T(128)S(1)} %copy-done.1, bf16[624,768]{1,0:T(8,128)(2,1)S(1)} %get-tuple-element.136.gb_ref, bf16[768,624]{1,0:T(8,128)(2,1)S(1)} %get-tuple-element.114.gbt_ref, bf16[768,624]{1,0:T(8,128)(2,1)S(1)} %get-tuple-element.115.ht_ref, ...), custom_call_target="tpu_custom_call" | custom-call | flops 8800000000 | bytes 12036108 | tf_op jit(solution)/shard_map/back/pallas_call | solution.py:539
  115.6 3.9 %back.7 = (bf16[2,4,96,768]{3,2,1,0:T(8,128)(2,1)S(1)}, bf16[624,640]{1,0:T(8,128)(2,1)S(1)}) custom-call(s32[3]{0:T(128)S(1)} %copy-done.1, bf16[624,768]{1,0:T(8,128)(2,1)S(1)} %get-tuple-element.136.gb_ref, bf16[768,624]{1,0:T(8,128)(2,1)S(1)} %get-tuple-element.114.gbt_ref, bf16[768,624]{1,0:T(8,128)(2,1)S(1)} %get-tuple-element.115.ht_ref, ...), custom_call_target="tpu_custom_call" | custom-call | flops 8800000000 | bytes 12036108 | tf_op jit(solution)/shard_map/back/pallas_call | solution.py:539
  121.4 3.8 %input.1.gh_ref = f32[624,768]{1,0:T(8,128)S(1)} custom-call(s32[3]{0:T(128)S(1)} %copy-done.1, bf16[4,768,384]{2,1,0:T(8,128)(2,1)S(1)} %get-tuple-element.129.w_a, bf16[4,768,256]{2,1,0:T(8,128)(2,1)S(1)} %get-tuple-element.130.w_b, bf16[624,640]{1,0:T(8,128)(2,1)S(1)} %get-tuple-element.131.refs_0_, bf16[624,640]{1,0:T(8,128)(2,1)S(1)} %get-tuple-element.132.refs_1_, ...), custom_call_target="tpu_custom_call" | custom-call | flops 4400000000 | bytes 7127052 | tf_op jit(solution)/shard_map/input/pallas_call | solution.py:539
  126.3 1.7 %collective-permute-start.31 = (bf16[4,96,384]{2,1,0:T(8,128)(2,1)S(1)}, bf16[4,96,384]{2,1,0:T(8,128)(2,1)S(1)}, u32[]{:S(2)}, u32[]{:S(2)}) collective-permute-start(bf16[4,96,384]{2,1,0:T(8,128)(2,1)S(1)} %get-tuple-element.157), channel_id=1, source_target_pairs={{0,4},{1,3},{2,6},{3,1},{4,0},{5,7},{6,2},{7,5},{8,12},{9,11},{10,... | collective-permute-start | bytes 884744 | tf_op jit(solution)/shard_map/ppermute | solution.py:33
  128.0 2.7 %last.1 = (f32[3,200,768]{2,1,0:T(8,128)}, f32[13,768]{1,0:T(8,128)S(1)}) custom-call(bf16[3,200,768]{2,1,0:T(8,128)(2,1)S(1)} %bitcast.81, f32[624,768]{1,0:T(8,128)S(1)} %get-tuple-element.112.gres_ref, f32[624,768]{1,0:T(8,128)S(1)} %input.1.gh_ref, f32[128,768]{1,0:T(8,128)S(1)} %get-tuple-element.104.ex_ref, f32[13,768]{1,0:T(8,128)S(1)} %get-tuple-element.139.part_ref), custom_call_target="tpu_custom_call" | custom-call | flops 110000000 | bytes 5188608 | tf_op jit(solution)/shard_map/last/pallas_call | solution.py:539
  131.1 4.6 %collective-permute-done.25 = f32[13,768]{1,0:T(8,128)S(1)} collective-permute-done((f32[13,768]{1,0:T(8,128)S(1)}, f32[13,768]{1,0:T(8,128)S(1)}, u32[]{:S(2)}, u32[]{:S(2)}) %collective-permute-start.25) | collective-permute-done | bytes 39968 | tf_op jit(solution)/shard_map/ppermute | solution.py:24
  135.9 2.1 %collective-permute-start.24 = (bf16[2,96,384]{2,1,0:T(8,128)(2,1)S(1)}, bf16[2,96,384]{2,1,0:T(8,128)(2,1)S(1)}, u32[]{:S(2)}, u32[]{:S(2)}) collective-permute-start(bf16[2,96,384]{2,1,0:T(8,128)(2,1)S(1)} %get-tuple-element.149), channel_id=1, source_target_pairs={{0,8},{4,12},{8,0},{12,4},{16,24},{20,28},{24,16},{28,20},{1,9},{5... | collective-permute-start | bytes 442376 | tf_op jit(solution)/shard_map/ppermute | solution.py:24
  138.2 1.9 %convolution_bitcast_fusion.1 = f32[1,768,768]{2,1,0:T(8,128)} fusion(bf16[256,768]{1,0:T(8,128)(2,1)S(1)} %bitcast.78, bf16[256,768]{1,0:T(8,128)(2,1)S(1)} %get-tuple-element.166), kind=kOutput, calls=%fused_computation.1 | convolution fusion | flops 301989888 | bytes 3145728 | tf_op jit(solution)/shard_map/dot_general | solution.py:86
  140.1 2.8 %collective-permute-done.24.refs_1_ = bf16[2,96,384]{2,1,0:T(8,128)(2,1)S(1)} collective-permute-done((bf16[2,96,384]{2,1,0:T(8,128)(2,1)S(1)}, bf16[2,96,384]{2,1,0:T(8,128)(2,1)S(1)}, u32[]{:S(2)}, u32[]{:S(2)}) %collective-permute-start.24) | collective-permute-done | bytes 147488 | tf_op jit(solution)/shard_map/ppermute | solution.py:24
  148.2 1.9 %convolution_bitcast_fusion = f32[1,768,768]{2,1,0:T(8,128)} fusion(bf16[256,768]{1,0:T(8,128)(2,1)S(1)} %get-tuple-element.167, bf16[256,768]{1,0:T(8,128)(2,1)S(1)} %get-tuple-element.168), kind=kOutput, calls=%fused_computation | convolution fusion | flops 301989888 | bytes 3145728 | tf_op jit(solution)/shard_map/dot_general | solution.py:86
  (97 shorter events, 34.3 us)
Async XLA Ops:
  3.7 8.3 %collective-permute-start = (bf16[1,96,384]{2,1,0:T(8,128)(2,1)}, bf16[1,96,384]{2,1,0:T(8,128)(2,1)S(1)}, u32[]{:S(2)}, u32[]{:S(2)}) collective-permute-start(bf16[1,96,384]{2,1,0:T(8,128)(2,1)} %bitcast.100), channel_id=1, source_target_pairs={{0,16},{4,20},{8,24},{12,28},{16,0},{20,4},{24,8},{28,12},{1,17},{... | collective-permute-start | bytes 221192 | tf_op jit(solution)/shard_map/ppermute | solution.py:24
  12.8 5.5 %collective-permute-start.1 = (bf16[2,96,384]{2,1,0:T(8,128)(2,1)S(1)}, bf16[2,96,384]{2,1,0:T(8,128)(2,1)S(1)}, u32[]{:S(2)}, u32[]{:S(2)}) collective-permute-start(bf16[2,96,384]{2,1,0:T(8,128)(2,1)S(1)} %pad_maximum_fusion.6), channel_id=1, source_target_pairs={{0,8},{4,12},{8,0},{12,4},{16,24},{20,28},{24,16},{28,20},{1,9},{5... | collective-permute-start | bytes 442376 | tf_op jit(solution)/shard_map/ppermute | solution.py:24
  13.7 7.4 %collective-permute-start.3 = (bf16[1,96,128]{2,1,0:T(8,128)(2,1)}, bf16[1,96,128]{2,1,0:T(8,128)(2,1)S(1)}, u32[]{:S(2)}, u32[]{:S(2)}) collective-permute-start(bf16[1,96,128]{2,1,0:T(8,128)(2,1)} %bitcast.108), channel_id=1, source_target_pairs={{0,16},{4,20},{8,24},{12,28},{16,0},{20,4},{24,8},{28,12},{1,17},{... | collective-permute-start | bytes 73736 | tf_op jit(solution)/shard_map/ppermute | solution.py:24
  19.3 11.2 %collective-permute-start.2 = (bf16[4,96,384]{2,1,0:T(8,128)(2,1)S(1)}, bf16[4,96,384]{2,1,0:T(8,128)(2,1)S(1)}, u32[]{:S(2)}, u32[]{:S(2)}) collective-permute-start(bf16[4,96,384]{2,1,0:T(8,128)(2,1)S(1)} %get-tuple-element.171), channel_id=1, source_target_pairs={{0,4},{1,3},{2,6},{3,1},{4,0},{5,7},{6,2},{7,5},{8,12},{9,11},{10,... | collective-permute-start | bytes 884744 | tf_op jit(solution)/shard_map/ppermute | solution.py:33
  21.8 4.5 %collective-permute-start.4 = (bf16[2,96,128]{2,1,0:T(8,128)(2,1)S(1)}, bf16[2,96,128]{2,1,0:T(8,128)(2,1)S(1)}, u32[]{:S(2)}, u32[]{:S(2)}) collective-permute-start(bf16[2,96,128]{2,1,0:T(8,128)(2,1)S(1)} %pad_maximum_fusion.9), channel_id=1, source_target_pairs={{0,8},{4,12},{8,0},{12,4},{16,24},{20,28},{24,16},{28,20},{1,9},{5... | collective-permute-start | bytes 147464 | tf_op jit(solution)/shard_map/ppermute | solution.py:24
  22.5 7.0 %collective-permute-start.5 = (bf16[1,96,384]{2,1,0:T(8,128)(2,1)}, bf16[1,96,384]{2,1,0:T(8,128)(2,1)S(1)}, u32[]{:S(2)}, u32[]{:S(2)}) collective-permute-start(bf16[1,96,384]{2,1,0:T(8,128)(2,1)} %bitcast.111), channel_id=1, source_target_pairs={{0,16},{4,20},{8,24},{12,28},{16,0},{20,4},{24,8},{28,12},{1,17},{... | collective-permute-start | bytes 221192 | tf_op jit(solution)/shard_map/ppermute | solution.py:24
  30.5 13.5 %collective-permute-start.6 = (bf16[2,4,96,384]{3,2,1,0:T(8,128)(2,1)S(1)}, bf16[2,4,96,384]{3,2,1,0:T(8,128)(2,1)S(1)}, u32[]{:S(2)}, u32[]{:S(2)}) collective-permute-start(bf16[2,4,96,384]{3,2,1,0:T(8,128)(2,1)S(1)} %pad_maximum_fusion.refs_0_), channel_id=1, source_target_pairs={{0,2},{1,5},{2,0},{3,7},{4,6},{5,1},{6,4},{7,3},{8,10},{9,13},{10,... | collective-permute-start | bytes 1769480 | tf_op jit(solution)/shard_map/ppermute | solution.py:33
  32.1 5.1 %collective-permute-start.8 = (bf16[2,96,384]{2,1,0:T(8,128)(2,1)S(1)}, bf16[2,96,384]{2,1,0:T(8,128)(2,1)S(1)}, u32[]{:S(2)}, u32[]{:S(2)}) collective-permute-start(bf16[2,96,384]{2,1,0:T(8,128)(2,1)S(1)} %pad_maximum_fusion.7), channel_id=1, source_target_pairs={{0,8},{4,12},{8,0},{12,4},{16,24},{20,28},{24,16},{28,20},{1,9},{5... | collective-permute-start | bytes 442376 | tf_op jit(solution)/shard_map/ppermute | solution.py:24
  32.1 13.2 %collective-permute-start.11 = (bf16[2,4,96,384]{3,2,1,0:T(8,128)(2,1)S(1)}, bf16[2,4,96,384]{3,2,1,0:T(8,128)(2,1)S(1)}, u32[]{:S(2)}, u32[]{:S(2)}) collective-permute-start(bf16[2,4,96,384]{3,2,1,0:T(8,128)(2,1)S(1)} %pad_maximum_fusion.refs_0_), channel_id=1, source_target_pairs={{0,1},{1,0},{2,3},{3,2},{4,5},{5,4},{6,7},{7,6},{8,9},{9,8},{10,11... | collective-permute-start | bytes 1769480 | tf_op jit(solution)/shard_map/ppermute | solution.py:24
  32.1 5.7 %collective-permute-start.7 = (bf16[4,96,128]{2,1,0:T(8,128)(2,1)S(1)}, bf16[4,96,128]{2,1,0:T(8,128)(2,1)S(1)}, u32[]{:S(2)}, u32[]{:S(2)}) collective-permute-start(bf16[4,96,128]{2,1,0:T(8,128)(2,1)S(1)} %pad_maximum_fusion.8), channel_id=1, source_target_pairs={{0,4},{4,0},{8,12},{12,8},{16,20},{20,16},{24,28},{28,24},{1,5},{5... | collective-permute-start | bytes 294920 | tf_op jit(solution)/shard_map/ppermute | solution.py:24
  37.3 6.8 %collective-permute-start.9 = (bf16[4,96,384]{2,1,0:T(8,128)(2,1)S(1)}, bf16[4,96,384]{2,1,0:T(8,128)(2,1)S(1)}, u32[]{:S(2)}, u32[]{:S(2)}) collective-permute-start(bf16[4,96,384]{2,1,0:T(8,128)(2,1)S(1)} %constant_dynamic-update-slice_fusion), channel_id=1, source_target_pairs={{0,4},{1,3},{2,6},{3,1},{4,0},{5,7},{6,2},{7,5},{8,12},{9,11},{10,... | collective-permute-start | bytes 884744 | tf_op jit(solution)/shard_map/ppermute | solution.py:33
  44.0 2.0 %collective-permute-start.12 = (bf16[2,4,96,384]{3,2,1,0:T(8,128)(2,1)S(1)}, bf16[2,4,96,384]{3,2,1,0:T(8,128)(2,1)S(1)}, u32[]{:S(2)}, u32[]{:S(2)}) collective-permute-start(bf16[2,4,96,384]{3,2,1,0:T(8,128)(2,1)S(1)} %collective-permute-done.6.refs_1_), channel_id=1, source_target_pairs={{0,1},{1,0},{2,3},{3,2},{4,5},{5,4},{6,7},{7,6},{8,9},{9,8},{10,11... | collective-permute-start | bytes 1769480 | tf_op jit(solution)/shard_map/ppermute | solution.py:24
  44.1 9.9 %collective-permute-start.10 = (bf16[2,4,96,384]{3,2,1,0:T(8,128)(2,1)S(1)}, bf16[2,4,96,384]{3,2,1,0:T(8,128)(2,1)S(1)}, u32[]{:S(2)}, u32[]{:S(2)}) collective-permute-start(bf16[2,4,96,384]{3,2,1,0:T(8,128)(2,1)S(1)} %pad_maximum_fusion.1.refs_0_), channel_id=1, source_target_pairs={{0,2},{1,5},{2,0},{3,7},{4,6},{5,1},{6,4},{7,3},{8,10},{9,13},{10,... | collective-permute-start | bytes 1769480 | tf_op jit(solution)/shard_map/ppermute | solution.py:33
  45.3 8.8 %collective-permute-start.13 = (bf16[2,4,96,384]{3,2,1,0:T(8,128)(2,1)S(1)}, bf16[2,4,96,384]{3,2,1,0:T(8,128)(2,1)S(1)}, u32[]{:S(2)}, u32[]{:S(2)}) collective-permute-start(bf16[2,4,96,384]{3,2,1,0:T(8,128)(2,1)S(1)} %pad_maximum_fusion.1.refs_0_), channel_id=1, source_target_pairs={{0,1},{1,0},{2,3},{3,2},{4,5},{5,4},{6,7},{7,6},{8,9},{9,8},{10,11... | collective-permute-start | bytes 1769480 | tf_op jit(solution)/shard_map/ppermute | solution.py:24
  54.1 2.0 %collective-permute-start.14 = (bf16[2,4,96,384]{3,2,1,0:T(8,128)(2,1)S(1)}, bf16[2,4,96,384]{3,2,1,0:T(8,128)(2,1)S(1)}, u32[]{:S(2)}, u32[]{:S(2)}) collective-permute-start(bf16[2,4,96,384]{3,2,1,0:T(8,128)(2,1)S(1)} %collective-permute-done.10.refs_1_), channel_id=1, source_target_pairs={{0,1},{1,0},{2,3},{3,2},{4,5},{5,4},{6,7},{7,6},{8,9},{9,8},{10,11... | collective-permute-start | bytes 1769480 | tf_op jit(solution)/shard_map/ppermute | solution.py:24
  74.5 4.6 %collective-permute-start.15 = (bf16[1,8,8,768]{3,2,1,0:T(8,128)(2,1)S(1)}, bf16[1,8,8,768]{3,2,1,0:T(8,128)(2,1)S(1)}, u32[]{:S(2)}, u32[]{:S(2)}) collective-permute-start(bf16[1,8,8,768]{3,2,1,0:T(8,128)(2,1)S(1)} %bitcast.97), channel_id=1, source_target_pairs={{0,2},{1,3},{2,0},{3,1},{4,6},{5,7},{6,4},{7,5},{8,10},{9,11},{10,... | collective-permute-start | bytes 294920 | tf_op jit(solution)/shard_map/ppermute | solution.py:24
  79.2 1.5 collective-permute-start.16
  84.1 4.9 %collective-permute-start.18 = (bf16[1,1,8,8,768]{4,3,2,1,0:T(8,128)(2,1)S(1)}, bf16[1,1,8,8,768]{4,3,2,1,0:T(8,128)(2,1)S(1)}, u32[]{:S(2)}, u32[]{:S(2)}) collective-permute-start(bf16[1,1,8,8,768]{4,3,2,1,0:T(8,128)(2,1)S(1)} %slice_bitcast_fusion.2), channel_id=1, source_target_pairs={{0,2},{1,3},{2,0},{3,1},{4,6},{5,7},{6,4},{7,5},{8,10},{9,11},{10,... | collective-permute-start | bytes 294920 | tf_op jit(solution)/shard_map/ppermute | solution.py:24
  106.1 3.8 %collective-permute-start.19 = (bf16[2,4,96,768]{3,2,1,0:T(8,128)(2,1)S(1)}, bf16[2,4,96,768]{3,2,1,0:T(8,128)(2,1)S(1)}, u32[]{:S(2)}, u32[]{:S(2)}) collective-permute-start(bf16[2,4,96,768]{3,2,1,0:T(8,128)(2,1)S(1)} %get-tuple-element.125), channel_id=1, source_target_pairs={{0,1},{1,0},{2,3},{3,2},{4,5},{5,4},{6,7},{7,6},{8,9},{9,8},{10,11... | collective-permute-start | bytes 3538952 | tf_op jit(solution)/shard_map/ppermute | solution.py:24
  113.9 5.6 %collective-permute-start.21 = (bf16[2,4,96,768]{3,2,1,0:T(8,128)(2,1)S(1)}, bf16[2,4,96,768]{3,2,1,0:T(8,128)(2,1)S(1)}, u32[]{:S(2)}, u32[]{:S(2)}) collective-permute-start(bf16[2,4,96,768]{3,2,1,0:T(8,128)(2,1)S(1)} %get-tuple-element.143), channel_id=1, source_target_pairs={{0,1},{1,0},{2,3},{3,2},{4,5},{5,4},{6,7},{7,6},{8,9},{9,8},{10,11... | collective-permute-start | bytes 3538952 | tf_op jit(solution)/shard_map/ppermute | solution.py:24
  114.5 10.7 %collective-permute-start.20 = (bf16[4,96,768]{2,1,0:T(8,128)(2,1)S(1)}, bf16[4,96,768]{2,1,0:T(8,128)(2,1)S(1)}, u32[]{:S(2)}, u32[]{:S(2)}) collective-permute-start(bf16[4,96,768]{2,1,0:T(8,128)(2,1)S(1)} %bitcast.89), channel_id=1, source_target_pairs={{0,2},{1,5},{2,0},{3,7},{4,6},{5,1},{6,4},{7,3},{8,10},{9,13},{10,... | collective-permute-start | bytes 1769480 | tf_op jit(solution)/shard_map/ppermute | solution.py:33
  120.4 15.3 %collective-permute-start.22 = (bf16[4,96,768]{2,1,0:T(8,128)(2,1)S(1)}, bf16[4,96,768]{2,1,0:T(8,128)(2,1)S(1)}, u32[]{:S(2)}, u32[]{:S(2)}) collective-permute-start(bf16[4,96,768]{2,1,0:T(8,128)(2,1)S(1)} %get-tuple-element.145), channel_id=1, source_target_pairs={{0,2},{1,5},{2,0},{3,7},{4,6},{5,1},{6,4},{7,3},{8,10},{9,13},{10,... | collective-permute-start | bytes 1769480 | tf_op jit(solution)/shard_map/ppermute | solution.py:33
  125.9 9.9 %collective-permute-start.23 = (bf16[4,96,384]{2,1,0:T(8,128)(2,1)S(1)}, bf16[4,96,384]{2,1,0:T(8,128)(2,1)S(1)}, u32[]{:S(2)}, u32[]{:S(2)}) collective-permute-start(bf16[4,96,384]{2,1,0:T(8,128)(2,1)S(1)} %get-tuple-element.148), channel_id=1, source_target_pairs={{0,4},{1,3},{2,6},{3,1},{4,0},{5,7},{6,2},{7,5},{8,12},{9,11},{10,... | collective-permute-start | bytes 884744 | tf_op jit(solution)/shard_map/ppermute | solution.py:33
  126.3 11.7 %collective-permute-start.31 = (bf16[4,96,384]{2,1,0:T(8,128)(2,1)S(1)}, bf16[4,96,384]{2,1,0:T(8,128)(2,1)S(1)}, u32[]{:S(2)}, u32[]{:S(2)}) collective-permute-start(bf16[4,96,384]{2,1,0:T(8,128)(2,1)S(1)} %get-tuple-element.157), channel_id=1, source_target_pairs={{0,4},{1,3},{2,6},{3,1},{4,0},{5,7},{6,2},{7,5},{8,12},{9,11},{10,... | collective-permute-start | bytes 884744 | tf_op jit(solution)/shard_map/ppermute | solution.py:33
  130.6 5.0 %collective-permute-start.25 = (f32[13,768]{1,0:T(8,128)S(1)}, f32[13,768]{1,0:T(8,128)S(1)}, u32[]{:S(2)}, u32[]{:S(2)}) collective-permute-start(f32[13,768]{1,0:T(8,128)S(1)} %get-tuple-element.150), channel_id=1, source_target_pairs={{0,16},{4,20},{8,24},{12,28},{16,0},{20,4},{24,8},{28,12},{1,17},{... | collective-permute-start | bytes 119816 | tf_op jit(solution)/shard_map/ppermute | solution.py:24
  135.7 4.5 %collective-permute-start.26 = (f32[13,768]{1,0:T(8,128)S(1)}, f32[13,768]{1,0:T(8,128)S(1)}, u32[]{:S(2)}, u32[]{:S(2)}) collective-permute-start(f32[13,768]{1,0:T(8,128)S(1)} %add.20), channel_id=1, source_target_pairs={{0,8},{4,12},{8,0},{12,4},{16,24},{20,28},{24,16},{28,20},{1,9},{5... | collective-permute-start | bytes 119816 | tf_op jit(solution)/shard_map/ppermute | solution.py:24
  135.9 7.1 %collective-permute-start.24 = (bf16[2,96,384]{2,1,0:T(8,128)(2,1)S(1)}, bf16[2,96,384]{2,1,0:T(8,128)(2,1)S(1)}, u32[]{:S(2)}, u32[]{:S(2)}) collective-permute-start(bf16[2,96,384]{2,1,0:T(8,128)(2,1)S(1)} %get-tuple-element.149), channel_id=1, source_target_pairs={{0,8},{4,12},{8,0},{12,4},{16,24},{20,28},{24,16},{28,20},{1,9},{5... | collective-permute-start | bytes 442376 | tf_op jit(solution)/shard_map/ppermute | solution.py:24
  138.1 7.2 %collective-permute-start.32 = (bf16[2,96,384]{2,1,0:T(8,128)(2,1)S(1)}, bf16[2,96,384]{2,1,0:T(8,128)(2,1)S(1)}, u32[]{:S(2)}, u32[]{:S(2)}) collective-permute-start(bf16[2,96,384]{2,1,0:T(8,128)(2,1)S(1)} %get-tuple-element.159), channel_id=1, source_target_pairs={{0,8},{4,12},{8,0},{12,4},{16,24},{20,28},{24,16},{28,20},{1,9},{5... | collective-permute-start | bytes 442376 | tf_op jit(solution)/shard_map/ppermute | solution.py:24
  143.0 4.1 %collective-permute-start.27 = (f32[13,768]{1,0:T(8,128)S(1)}, f32[13,768]{1,0:T(8,128)S(1)}, u32[]{:S(2)}, u32[]{:S(2)}) collective-permute-start(f32[13,768]{1,0:T(8,128)S(1)} %add.21), channel_id=1, source_target_pairs={{0,4},{4,0},{8,12},{12,8},{16,20},{20,16},{24,28},{28,24},{1,5},{5... | collective-permute-start | bytes 119816 | tf_op jit(solution)/shard_map/ppermute | solution.py:24
  143.7 7.6 %collective-permute-start.30 = (bf16[96,384]{1,0:T(8,128)(2,1)S(1)}, bf16[96,384]{1,0:T(8,128)(2,1)S(1)}, u32[]{:S(2)}, u32[]{:S(2)}) collective-permute-start(bf16[96,384]{1,0:T(8,128)(2,1)S(1)} %bitcast.90), channel_id=1, source_target_pairs={{0,16},{4,20},{8,24},{12,28},{16,0},{20,4},{24,8},{28,12},{1,17},{... | collective-permute-start | bytes 221192 | tf_op jit(solution)/shard_map/ppermute | solution.py:24
  145.4 6.0 %collective-permute-start.33 = (bf16[96,384]{1,0:T(8,128)(2,1)S(1)}, bf16[96,384]{1,0:T(8,128)(2,1)S(1)}, u32[]{:S(2)}, u32[]{:S(2)}) collective-permute-start(bf16[96,384]{1,0:T(8,128)(2,1)S(1)} %bitcast.91), channel_id=1, source_target_pairs={{0,16},{4,20},{8,24},{12,28},{16,0},{20,4},{24,8},{28,12},{1,17},{... | collective-permute-start | bytes 221192 | tf_op jit(solution)/shard_map/ppermute | solution.py:24
  147.1 4.1 %collective-permute-start.28 = (f32[13,768]{1,0:T(8,128)S(1)}, f32[13,768]{1,0:T(8,128)S(1)}, u32[]{:S(2)}, u32[]{:S(2)}) collective-permute-start(f32[13,768]{1,0:T(8,128)S(1)} %add.22), channel_id=1, source_target_pairs={{0,2},{1,3},{2,0},{3,1},{4,6},{5,7},{6,4},{7,5},{8,10},{9,11},{10,... | collective-permute-start | bytes 119816 | tf_op jit(solution)/shard_map/ppermute | solution.py:24
  (8 other events, 91.6 us)

commit v11 on v10

--- a/solution.py
+++ b/solution.py
@@ -130,6 +130,17 @@
     filled = sum(value.shape[0] for value in columns)
     columns.append(jnp.zeros((extra_ref.shape[1] - filled, rows), f32))
     extra_ref[...] = jnp.concatenate(columns, 0).T.astype(bf16)
+
+
+def join_kernel(a_ref, b_ref, out_ref):
+    size = a_ref.shape[0]
+    out_ref[:size] = a_ref[...]
+    out_ref[size:] = b_ref[...]
+
+
+def join(a, b):
+    shape = (a.shape[0] + b.shape[0],) + a.shape[1:]
+    return call(join_kernel, [(shape, a.dtype)], (a, b), flops=1000, name="join", scalars=0, grant=4)[0]
 
 
 def fold_kernel(*refs, halves, starts):
@@ -590,17 +601,21 @@
         )(words, w_qkv.transpose(1, 0, 2), w_out, gain_one[None], gain_two[None], router.T)
 
         first, second, held_extra = first[None], second[None], extra[None]
-        for bit in bits_of(dp)[:-1]:
-            first = jnp.concatenate([first, swap(first, "dp", dp, bit)])
-            held_extra = jnp.concatenate([held_extra, swap(held_extra, "dp", dp, bit)])
         stages = bits_of(dp)[:-1]
-        second = jnp.concatenate([second, swap(second, "dp", dp, stages[0])])
-        other, held_extra, second = lax.optimization_barrier(
-            (swap_both(first, dp, mp, (1, 0), (0, 2)), held_extra, second)
-        )
-        for bit in stages[1:]:
-            second = jnp.concatenate([second, swap(second, "dp", dp, bit)])
-        held_extra = jnp.concatenate([held_extra, swap(held_extra, "dp", dp, 1)])
+        for bit in stages:
+            others = swap(first, "dp", dp, bit), swap(second, "dp", dp, bit)
+            if bit != stages[-1]:
+                others = lax.optimization_barrier(others)
+            put = jnp.concatenate if bit == stages[0] else lambda pair: join(*pair)
+            first = put([first, others[0]])
+            held_extra = put([held_extra, swap(held_extra, "dp", dp, bit)])
+            if bit != stages[-1]:
+                second = put([second, others[1]])
+        other, held_extra, late = lax.optimization_barrier(
+            (swap_both(first, dp, mp, (1, 0), (0, 2)), held_extra, others[1])
+        )
+        second = join(second, late)
+        held_extra = join(held_extra, swap(held_extra, "dp", dp, 1))
         held_extra = held_extra.reshape((dp,) + extra.shape)
         if ready:
             held_extra = reorder(unmirrored(held_extra), me).reshape(1, width, -1)
@@ -615,13 +630,13 @@
             grant=4,
             **exact,
         )
-        near = jnp.stack([first, other])
+        near = join(first, other).reshape((2, high, d_rows, half))
         far = swap_both(near, dp, mp, (0, 2), (1, 0))
         second = second.reshape((high, d_rows, half))
         other = swap_both(second, dp, mp, (1, 0), (0, 2))
         far, h_one, other = lax.optimization_barrier((far, h_one, other))
         first = (near, far, swap(near, "mp", mp, 1), swap(far, "mp", mp, 1))
-        near = jnp.stack([second, other])
+        near = join(second, other).reshape((2, high, d_rows, half))
         second_near, second_far = near, swap_both(near, dp, mp, (0, 2), (1, 0))
         second_near_other = swap(second_near, "mp", mp, 1)
 

time: 154 us -> 157 us (1.019)
  waiting for transfers between devices: 42.5 us -> 48 us
  other arithmetic: 5.16 us -> 3.3 us
    ppermute x26, waiting for transfers between devices: 35.8 us -> 43 us  [swap(): lax.ppermute(array_in, axis_name, [(i, i ^ bit) for i in range(size)])]
    ppermute x8, waiting for transfers between devices: 6.64 us -> 4.97 us  [swap_both(): return lax.ppermute(array_in, ('dp', 'mp'), pairs)]
    concatenate x5 -> x3, other arithmetic: 3.32 us -> 2.55 us  [the longest x1 0.9 us: per_device(): first = put([first, others[0]])]
    pallas_call x21 -> x27, Pallas kernels: 46.7 us -> 46.7 us  [call(): pl.pallas_call(functools.partial(kernel, **static), out_shape=[jax.ShapeD...]
  transfers between devices with their start and end apart: 34 -> 34, of which waited for: 19 -> 19; matrix products, arithmetic and copies ran while one was open for 5% -> 4% of each run, Pallas kernels for 16% -> 16%
where the time goes in v11:
time: 157 us
  Pallas kernels  49.1 us (31%)
  waiting for transfers between devices  48 us (31%)
  starting transfers between devices  30.4 us (19%)
  blocking collectives  20.8 us (13%)
  matrix products  3.84 us (2%)
  other arithmetic  3.3 us (2%)
    pallas_call x27, Pallas kernels, call(): pl.pallas_call(functools.partial(kernel, **static), out_shape=[jax.ShapeD...  46.7 us
    ppermute x26, waiting for transfers between devices, swap(): lax.ppermute(array_in, axis_name, [(i, i ^ bit) for i in range(size)])  43 us
    ppermute x26, starting transfers between devices, swap(): lax.ppermute(array_in, axis_name, [(i, i ^ bit) for i in range(size)])  21.5 us
    all_to_all x1, blocking collectives, per_device(): got = lax.all_to_all(got, 'dp', split_axis=0, concat_axis=0, tiled=True)  11.3 us
    all_to_all x1, blocking collectives, per_device(): back = lax.all_to_all(back, 'dp', split_axis=0, concat_axis=0, tiled=True)  9.51 us
    ppermute x8, starting transfers between devices, swap_both(): return lax.ppermute(array_in, ('dp', 'mp'), pairs)  8.98 us
    ppermute x8, waiting for transfers between devices, swap_both(): return lax.ppermute(array_in, ('dp', 'mp'), pairs)  4.97 us
    dot_general x2, matrix products, mm_tn(): lax.dot_general(a, b, (((0,), (0,)), ((), ())), preferred_element_type=f32)  3.84 us
  transfers between devices with their start and end apart: 34, of which 19 were waited for; matrix products, arithmetic and copies ran while one was open for 4% of the time, Pallas kernels for 16%

profile of v11, /device:TPU:0, one launch (start us, length us, event | category | flops | bytes accessed | tf_op | source)
XLA Modules:
  0.0 156.7 jit_solution(2042318308860016239)
XLA Ops:
  1.2 2.4 %pack.1 = (bf16[96,384]{1,0:T(8,128)(2,1)}, bf16[96,384]{1,0:T(8,128)(2,1)}, bf16[96,128]{1,0:T(8,128)(2,1)}) custom-call(s32[3]{0:T(128)} %pad_add_fusion.me_ref, bf16[3,96,192]{2,1,0:T(8,128)(2,1)} %bitcast.103, bf16[192,96]{1,0:T(8,128)(2,1)} %out_hbm.1, bf16[1,96]{1,0:T(2,128)(2,1)} %bitcast.112, bf16[1,96]{1,0:T(2,128)(2,1)} %bitcast.113, ...), custom_call_target="tpu_custom_call" | custom-call | tf_op jit(solution)/shard_map/pack/pallas_call | solution.py:593
  3.7 4.1 %collective-permute-start = (bf16[1,96,384]{2,1,0:T(8,128)(2,1)}, bf16[1,96,384]{2,1,0:T(8,128)(2,1)S(1)}, u32[]{:S(2)}, u32[]{:S(2)}) collective-permute-start(bf16[1,96,384]{2,1,0:T(8,128)(2,1)} %bitcast.107), channel_id=1, source_target_pairs={{0,16},{4,20},{8,24},{12,28},{16,0},{20,4},{24,8},{28,12},{1,17},{... | collective-permute-start | bytes 221192 | tf_op jit(solution)/shard_map/ppermute | solution.py:24
  7.9 5.1 %collective-permute-done = bf16[1,96,384]{2,1,0:T(8,128)(2,1)S(1)} collective-permute-done((bf16[1,96,384]{2,1,0:T(8,128)(2,1)}, bf16[1,96,384]{2,1,0:T(8,128)(2,1)S(1)}, u32[]{:S(2)}, u32[]{:S(2)}) %collective-permute-start) | collective-permute-done | bytes 73760 | tf_op jit(solution)/shard_map/ppermute | solution.py:24
  13.0 2.1 %collective-permute-done.1 = bf16[1,96,384]{2,1,0:T(8,128)(2,1)S(1)} collective-permute-done((bf16[1,96,384]{2,1,0:T(8,128)(2,1)}, bf16[1,96,384]{2,1,0:T(8,128)(2,1)S(1)}, u32[]{:S(2)}, u32[]{:S(2)}) %collective-permute-start.1) | collective-permute-done | bytes 73760 | tf_op jit(solution)/shard_map/ppermute | solution.py:24
  16.8 4.9 %collective-permute-done.2.b_ref = bf16[2,96,384]{2,1,0:T(8,128)(2,1)S(1)} collective-permute-done((bf16[2,96,384]{2,1,0:T(8,128)(2,1)S(1)}, bf16[2,96,384]{2,1,0:T(8,128)(2,1)S(1)}, u32[]{:S(2)}, u32[]{:S(2)}) %collective-permute-start.2) | collective-permute-done | bytes 147488 | tf_op jit(solution)/shard_map/ppermute | solution.py:24
  23.3 2.4 %collective-permute-start.4 = (bf16[1,96,128]{2,1,0:T(8,128)(2,1)}, bf16[1,96,128]{2,1,0:T(8,128)(2,1)S(1)}, u32[]{:S(2)}, u32[]{:S(2)}) collective-permute-start(bf16[1,96,128]{2,1,0:T(8,128)(2,1)} %bitcast.109), channel_id=1, source_target_pairs={{0,16},{4,20},{8,24},{12,28},{16,0},{20,4},{24,8},{28,12},{1,17},{... | collective-permute-start | bytes 73736 | tf_op jit(solution)/shard_map/ppermute | solution.py:24
  26.7 1.8 %collective-permute-start.6 = (bf16[2,96,384]{2,1,0:T(8,128)(2,1)S(1)}, bf16[2,96,384]{2,1,0:T(8,128)(2,1)S(1)}, u32[]{:S(2)}, u32[]{:S(2)}) collective-permute-start(bf16[2,96,384]{2,1,0:T(8,128)(2,1)S(1)} %pad_maximum_fusion.3.a_ref), channel_id=1, source_target_pairs={{0,8},{4,12},{8,0},{12,4},{16,24},{20,28},{24,16},{28,20},{1,9},{5... | collective-permute-start | bytes 442376 | tf_op jit(solution)/shard_map/ppermute | solution.py:24
  30.5 2.8 %collective-permute-done.5.b_ref = bf16[2,96,128]{2,1,0:T(8,128)(2,1)S(1)} collective-permute-done((bf16[2,96,128]{2,1,0:T(8,128)(2,1)S(1)}, bf16[2,96,128]{2,1,0:T(8,128)(2,1)S(1)}, u32[]{:S(2)}, u32[]{:S(2)}) %collective-permute-start.5) | collective-permute-done | bytes 49184 | tf_op jit(solution)/shard_map/ppermute | solution.py:24
  37.1 3.5 %collective-permute-done.8.b_ref = bf16[4,96,128]{2,1,0:T(8,128)(2,1)S(1)} collective-permute-done((bf16[4,96,128]{2,1,0:T(8,128)(2,1)S(1)}, bf16[4,96,128]{2,1,0:T(8,128)(2,1)S(1)}, u32[]{:S(2)}, u32[]{:S(2)}) %collective-permute-start.8) | collective-permute-done | bytes 98336 | tf_op jit(solution)/shard_map/ppermute | solution.py:24
  42.3 3.3 %collective-permute-done.9.b_ref = bf16[4,96,384]{2,1,0:T(8,128)(2,1)S(1)} collective-permute-done((bf16[4,96,384]{2,1,0:T(8,128)(2,1)S(1)}, bf16[4,96,384]{2,1,0:T(8,128)(2,1)S(1)}, u32[]{:S(2)}, u32[]{:S(2)}) %collective-permute-start.9) | collective-permute-done | bytes 294944 | tf_op jit(solution)/shard_map/ppermute | solution.py:33
  46.5 2.2 %collective-permute-start.13 = (bf16[2,4,96,384]{3,2,1,0:T(8,128)(2,1)S(1)}, bf16[2,4,96,384]{3,2,1,0:T(8,128)(2,1)S(1)}, u32[]{:S(2)}, u32[]{:S(2)}) collective-permute-start(bf16[2,4,96,384]{3,2,1,0:T(8,128)(2,1)S(1)} %bitcast.83), channel_id=1, source_target_pairs={{0,1},{1,0},{2,3},{3,2},{4,5},{5,4},{6,7},{7,6},{8,9},{9,8},{10,11... | collective-permute-start | bytes 1769480 | tf_op jit(solution)/shard_map/ppermute | solution.py:24
  48.8 5.9 %front_pair.1 = (bf16[4,768,384]{2,1,0:T(8,128)(2,1)S(1)}, bf16[4,624,384]{2,1,0:T(8,128)(2,1)S(1)}, bf16[4,3,2,208,208]{4,3,2,1,0:T(8,128)(2,1)S(1)}, bf16[4,624,128]{2,1,0:T(8,128)(2,1)S(1)}) custom-call(s32[3]{0:T(128)S(1)} %copy-done.1, bf16[624,768]{1,0:T(8,128)(2,1)S(1)} %get-tuple-element.101.h_ref, s32[12,200]{1,0:T(8,128)S(1)} %copy-done.5, ...), custom_call_target="tpu_custom_call" | custom-call | flops 11000000512 | bytes 3327372 | tf_op jit(solution)/shard_map/front_pair/pallas_call | solution.py:550
  56.4 2.0 %collective-permute-done.14.refs_3_ = bf16[2,4,96,384]{3,2,1,0:T(8,128)(2,1)S(1)} collective-permute-done((bf16[2,4,96,384]{3,2,1,0:T(8,128)(2,1)S(1)}, bf16[2,4,96,384]{3,2,1,0:T(8,128)(2,1)S(1)}, u32[]{:S(2)}, u32[]{:S(2)}) %collective-permute-start.14) | collective-permute-done | bytes 589856 | tf_op jit(solution)/shard_map/ppermute | solution.py:24
  58.4 5.2 %front_last.1 = (bf16[4,768,256]{2,1,0:T(8,128)(2,1)S(1)}, bf16[4,624,256]{2,1,0:T(8,128)(2,1)S(1)}, bf16[4,3,208,208]{3,2,1,0:T(8,128)(2,1)S(1)}, bf16[624,1024...) custom-call(s32[3]{0:T(128)S(1)} %copy-done.1, ...), custom_call_target="tpu_custom_call" | custom-call | flops 7699999744 | bytes 3966348 | tf_op jit(solution)/shard_map/front_last/pallas_call | solution.py:550
  63.6 2.7 %route.1 = (f32[624,768]{1,0:T(8,128)S(1)}, bf16[624,768]{1,0:T(8,128)(2,1)S(1)}, f32[2,3,8,208]{3,2,1,0:T(8,128)S(1)}, bf16[64,768]{1,0:T(8,128)(2,1)S(1)}, f32[3,1,128]{2,1,0:T(1,128)S(1)}) custom-call(s32[3]{0:T(128)S(1)} %copy-done.1, bf16[3,200,768]{2,1,0:T(8,128)(2,1)S(1)} %bitcast.77, f32[624,768]{1,0:T(8,128)S(1)} %get-tuple-element.107.br_ref, ...), custom_call_target="tpu_custom_call" | custom-call | flops 2200000000 | bytes 4162956 | tf_op jit(solution)/shard_map/route/pallas_call | solution.py:550
  66.3 11.3 %all_to_all.10 = bf16[8,8,768]{2,1,0:T(8,128)(2,1)S(1)} all-to-all(bf16[8,8,768]{2,1,0:T(8,128)(2,1)S(1)} %bitcast.87), channel_id=1, replica_groups=mesh['dp'=8,'mp'=4] {'dp'}, dimensions={0} | all-to-all | bytes 196608 | tf_op jit(solution)/shard_map/all_to_all | solution.py:710
  78.0 4.2 %collective-permute-done.15 = bf16[1,8,8,768]{3,2,1,0:T(8,128)(2,1)S(1)} collective-permute-done((bf16[1,8,8,768]{3,2,1,0:T(8,128)(2,1)S(1)}, bf16[1,8,8,768]{3,2,1,0:T(8,128)(2,1)S(1)}, u32[]{:S(2)}, u32[]{:S(2)}) %collective-permute-start.15) | collective-permute-done | bytes 98336 | tf_op jit(solution)/shard_map/ppermute | solution.py:24
  87.5 4.5 %collective-permute-done.18 = bf16[1,1,8,8,768]{4,3,2,1,0:T(8,128)(2,1)S(1)} collective-permute-done((bf16[1,1,8,8,768]{4,3,2,1,0:T(8,128)(2,1)S(1)}, bf16[1,1,8,8,768]{4,3,2,1,0:T(8,128)(2,1)S(1)}, u32[]{:S(2)}, u32[]{:S(2)}) %collective-permute-start.18) | collective-permute-done | bytes 98336 | tf_op jit(solution)/shard_map/ppermute | solution.py:24
  92.0 9.5 %all_to_all.11 = bf16[8,8,768]{2,1,0:T(8,128)(2,1)S(1)} all-to-all(bf16[8,8,768]{2,1,0:T(8,128)(2,1)S(1)} %fusion.5), channel_id=1, replica_groups=mesh['dp'=8,'mp'=4] {'dp'}, dimensions={0} | all-to-all | bytes 196608 | tf_op jit(solution)/shard_map/all_to_all | solution.py:730
  101.6 3.9 %mix.1 = (bf16[3,200,768]{2,1,0:T(8,128)(2,1)}, f32[624,768]{1,0:T(8,128)S(1)}, bf16[624,768]{1,0:T(8,128)(2,1)S(1)}, bf16[768,624]{1,0:T(8,128)(2,1)S(1)}, f32[13,768]{1,0:T(8,128)S(1)}) custom-call(s32[3]{0:T(128)S(1)} %copy-done.1, f32[624,768]{1,0:T(8,128)S(1)} %get-tuple-element.109.res_ref, bf16[624,768]{1,0:T(8,128)(2,1)S(1)} %get-tuple-element.110.h_ref, ...), custom_call_target="tpu_custom_call" | custom-call | flops 5500000256 | bytes 4315020 | tf_op jit(solution)/shard_map/mix/pallas_call | solution.py:550
  105.5 3.7 %back.4 = (bf16[2,4,96,768]{3,2,1,0:T(8,128)(2,1)S(1)}, bf16[624,640]{1,0:T(8,128)(2,1)S(1)}) custom-call(s32[3]{0:T(128)S(1)} %copy-done.1, bf16[624,768]{1,0:T(8,128)(2,1)S(1)} %get-tuple-element.140.gb_ref, bf16[768,624]{1,0:T(8,128)(2,1)S(1)} %get-tuple-element.118.gbt_ref, bf16[768,624]{1,0:T(8,128)(2,1)S(1)} %get-tuple-element.119.ht_ref, ...), custom_call_target="tpu_custom_call" | custom-call | flops 8800000000 | bytes 12036108 | tf_op jit(solution)/shard_map/back/pallas_call | solution.py:550
  109.3 3.7 %back.5 = (bf16[2,4,96,768]{3,2,1,0:T(8,128)(2,1)S(1)}, bf16[624,640]{1,0:T(8,128)(2,1)S(1)}) custom-call(s32[3]{0:T(128)S(1)} %copy-done.1, bf16[624,768]{1,0:T(8,128)(2,1)S(1)} %get-tuple-element.140.gb_ref, bf16[768,624]{1,0:T(8,128)(2,1)S(1)} %get-tuple-element.118.gbt_ref, bf16[768,624]{1,0:T(8,128)(2,1)S(1)} %get-tuple-element.119.ht_ref, ...), custom_call_target="tpu_custom_call" | custom-call | flops 8800000000 | bytes 12036108 | tf_op jit(solution)/shard_map/back/pallas_call | solution.py:550
  113.2 3.7 %back.6 = (bf16[2,4,96,768]{3,2,1,0:T(8,128)(2,1)S(1)}, bf16[624,640]{1,0:T(8,128)(2,1)S(1)}) custom-call(s32[3]{0:T(128)S(1)} %copy-done.1, bf16[624,768]{1,0:T(8,128)(2,1)S(1)} %get-tuple-element.140.gb_ref, bf16[768,624]{1,0:T(8,128)(2,1)S(1)} %get-tuple-element.118.gbt_ref, bf16[768,624]{1,0:T(8,128)(2,1)S(1)} %get-tuple-element.119.ht_ref, ...), custom_call_target="tpu_custom_call" | custom-call | flops 8800000000 | bytes 12036108 | tf_op jit(solution)/shard_map/back/pallas_call | solution.py:550
  117.8 3.9 %back.7 = (bf16[2,4,96,768]{3,2,1,0:T(8,128)(2,1)S(1)}, bf16[624,640]{1,0:T(8,128)(2,1)S(1)}) custom-call(s32[3]{0:T(128)S(1)} %copy-done.1, bf16[624,768]{1,0:T(8,128)(2,1)S(1)} %get-tuple-element.140.gb_ref, bf16[768,624]{1,0:T(8,128)(2,1)S(1)} %get-tuple-element.118.gbt_ref, bf16[768,624]{1,0:T(8,128)(2,1)S(1)} %get-tuple-element.119.ht_ref, ...), custom_call_target="tpu_custom_call" | custom-call | flops 8800000000 | bytes 12036108 | tf_op jit(solution)/shard_map/back/pallas_call | solution.py:550
  124.4 3.8 %input.1.gh_ref = f32[624,768]{1,0:T(8,128)S(1)} custom-call(s32[3]{0:T(128)S(1)} %copy-done.1, bf16[4,768,384]{2,1,0:T(8,128)(2,1)S(1)} %get-tuple-element.133.w_a, bf16[4,768,256]{2,1,0:T(8,128)(2,1)S(1)} %get-tuple-element.134.w_b, bf16[624,640]{1,0:T(8,128)(2,1)S(1)} %get-tuple-element.135.refs_0_, bf16[624,640]{1,0:T(8,128)(2,1)S(1)} %get-tuple-element.136.refs_1_, ...), custom_call_target="tpu_custom_call" | custom-call | flops 4400000000 | bytes 7127052 | tf_op jit(solution)/shard_map/input/pallas_call | solution.py:550
  130.9 2.7 %last.1 = (f32[3,200,768]{2,1,0:T(8,128)}, f32[13,768]{1,0:T(8,128)S(1)}) custom-call(bf16[3,200,768]{2,1,0:T(8,128)(2,1)S(1)} %bitcast.78, f32[624,768]{1,0:T(8,128)S(1)} %get-tuple-element.116.gres_ref, f32[624,768]{1,0:T(8,128)S(1)} %input.1.gh_ref, f32[128,768]{1,0:T(8,128)S(1)} %get-tuple-element.108.ex_ref, f32[13,768]{1,0:T(8,128)S(1)} %get-tuple-element.143.part_ref), custom_call_target="tpu_custom_call" | custom-call | flops 110000000 | bytes 5188608 | tf_op jit(solution)/shard_map/last/pallas_call | solution.py:550
  134.0 4.6 %collective-permute-done.25 = f32[13,768]{1,0:T(8,128)S(1)} collective-permute-done((f32[13,768]{1,0:T(8,128)S(1)}, f32[13,768]{1,0:T(8,128)S(1)}, u32[]{:S(2)}, u32[]{:S(2)}) %collective-permute-start.25) | collective-permute-done | bytes 39968 | tf_op jit(solution)/shard_map/ppermute | solution.py:24
  138.8 2.1 %collective-permute-start.24 = (bf16[2,96,384]{2,1,0:T(8,128)(2,1)S(1)}, bf16[2,96,384]{2,1,0:T(8,128)(2,1)S(1)}, u32[]{:S(2)}, u32[]{:S(2)}) collective-permute-start(bf16[2,96,384]{2,1,0:T(8,128)(2,1)S(1)} %get-tuple-element.153), channel_id=1, source_target_pairs={{0,8},{4,12},{8,0},{12,4},{16,24},{20,28},{24,16},{28,20},{1,9},{5... | collective-permute-start | bytes 442376 | tf_op jit(solution)/shard_map/ppermute | solution.py:24
  141.1 1.9 %convolution_bitcast_fusion.1 = f32[1,768,768]{2,1,0:T(8,128)} fusion(bf16[256,768]{1,0:T(8,128)(2,1)S(1)} %bitcast.75, bf16[256,768]{1,0:T(8,128)(2,1)S(1)} %get-tuple-element.170), kind=kOutput, calls=%fused_computation.1 | convolution fusion | flops 301989888 | bytes 3145728 | tf_op jit(solution)/shard_map/dot_general | solution.py:86
  143.0 2.8 %collective-permute-done.24.refs_1_ = bf16[2,96,384]{2,1,0:T(8,128)(2,1)S(1)} collective-permute-done((bf16[2,96,384]{2,1,0:T(8,128)(2,1)S(1)}, bf16[2,96,384]{2,1,0:T(8,128)(2,1)S(1)}, u32[]{:S(2)}, u32[]{:S(2)}) %collective-permute-start.24) | collective-permute-done | bytes 147488 | tf_op jit(solution)/shard_map/ppermute | solution.py:24
  150.3 1.9 %convolution_bitcast_fusion = f32[1,768,768]{2,1,0:T(8,128)} fusion(bf16[256,768]{1,0:T(8,128)(2,1)S(1)} %get-tuple-element.171, bf16[256,768]{1,0:T(8,128)(2,1)S(1)} %get-tuple-element.172), kind=kOutput, calls=%fused_computation | convolution fusion | flops 301989888 | bytes 3145728 | tf_op jit(solution)/shard_map/dot_general | solution.py:86
  152.3 1.9 %collective-permute-done.28 = f32[13,768]{1,0:T(8,128)S(1)} collective-permute-done((f32[13,768]{1,0:T(8,128)S(1)}, f32[13,768]{1,0:T(8,128)S(1)}, u32[]{:S(2)}, u32[]{:S(2)}) %collective-permute-start.28) | collective-permute-done | bytes 39968 | tf_op jit(solution)/shard_map/ppermute | solution.py:24
  (96 shorter events, 35.2 us)
Async XLA Ops:
  3.7 9.3 %collective-permute-start = (bf16[1,96,384]{2,1,0:T(8,128)(2,1)}, bf16[1,96,384]{2,1,0:T(8,128)(2,1)S(1)}, u32[]{:S(2)}, u32[]{:S(2)}) collective-permute-start(bf16[1,96,384]{2,1,0:T(8,128)(2,1)} %bitcast.107), channel_id=1, source_target_pairs={{0,16},{4,20},{8,24},{12,28},{16,0},{20,4},{24,8},{28,12},{1,17},{... | collective-permute-start | bytes 221192 | tf_op jit(solution)/shard_map/ppermute | solution.py:24
  7.8 7.3 %collective-permute-start.1 = (bf16[1,96,384]{2,1,0:T(8,128)(2,1)}, bf16[1,96,384]{2,1,0:T(8,128)(2,1)S(1)}, u32[]{:S(2)}, u32[]{:S(2)}) collective-permute-start(bf16[1,96,384]{2,1,0:T(8,128)(2,1)} %bitcast.105), channel_id=1, source_target_pairs={{0,16},{4,20},{8,24},{12,28},{16,0},{20,4},{24,8},{28,12},{1,17},{... | collective-permute-start | bytes 221192 | tf_op jit(solution)/shard_map/ppermute | solution.py:24
  16.0 5.7 %collective-permute-start.2 = (bf16[2,96,384]{2,1,0:T(8,128)(2,1)S(1)}, bf16[2,96,384]{2,1,0:T(8,128)(2,1)S(1)}, u32[]{:S(2)}, u32[]{:S(2)}) collective-permute-start(bf16[2,96,384]{2,1,0:T(8,128)(2,1)S(1)} %pad_maximum_fusion.2.a_ref), channel_id=1, source_target_pairs={{0,8},{4,12},{8,0},{12,4},{16,24},{20,28},{24,16},{28,20},{1,9},{5... | collective-permute-start | bytes 442376 | tf_op jit(solution)/shard_map/ppermute | solution.py:24
  21.7 11.6 %collective-permute-start.3 = (bf16[4,96,384]{2,1,0:T(8,128)(2,1)S(1)}, bf16[4,96,384]{2,1,0:T(8,128)(2,1)S(1)}, u32[]{:S(2)}, u32[]{:S(2)}) collective-permute-start(bf16[4,96,384]{2,1,0:T(8,128)(2,1)S(1)} %join.6.a_ref), channel_id=1, source_target_pairs={{0,4},{1,3},{2,6},{3,1},{4,0},{5,7},{6,2},{7,5},{8,12},{9,11},{10,... | collective-permute-start | bytes 884744 | tf_op jit(solution)/shard_map/ppermute | solution.py:33
  23.3 5.2 %collective-permute-start.4 = (bf16[1,96,128]{2,1,0:T(8,128)(2,1)}, bf16[1,96,128]{2,1,0:T(8,128)(2,1)S(1)}, u32[]{:S(2)}, u32[]{:S(2)}) collective-permute-start(bf16[1,96,128]{2,1,0:T(8,128)(2,1)} %bitcast.109), channel_id=1, source_target_pairs={{0,16},{4,20},{8,24},{12,28},{16,0},{20,4},{24,8},{28,12},{1,17},{... | collective-permute-start | bytes 73736 | tf_op jit(solution)/shard_map/ppermute | solution.py:24
  26.7 6.7 %collective-permute-start.6 = (bf16[2,96,384]{2,1,0:T(8,128)(2,1)S(1)}, bf16[2,96,384]{2,1,0:T(8,128)(2,1)S(1)}, u32[]{:S(2)}, u32[]{:S(2)}) collective-permute-start(bf16[2,96,384]{2,1,0:T(8,128)(2,1)S(1)} %pad_maximum_fusion.3.a_ref), channel_id=1, source_target_pairs={{0,8},{4,12},{8,0},{12,4},{16,24},{20,28},{24,16},{28,20},{1,9},{5... | collective-permute-start | bytes 442376 | tf_op jit(solution)/shard_map/ppermute | solution.py:24
  29.2 4.1 %collective-permute-start.5 = (bf16[2,96,128]{2,1,0:T(8,128)(2,1)S(1)}, bf16[2,96,128]{2,1,0:T(8,128)(2,1)S(1)}, u32[]{:S(2)}, u32[]{:S(2)}) collective-permute-start(bf16[2,96,128]{2,1,0:T(8,128)(2,1)S(1)} %pad_maximum_fusion.4.a_ref), channel_id=1, source_target_pairs={{0,8},{4,12},{8,0},{12,4},{16,24},{20,28},{24,16},{28,20},{1,9},{5... | collective-permute-start | bytes 147464 | tf_op jit(solution)/shard_map/ppermute | solution.py:24
  33.4 12.1 %collective-permute-start.7 = (bf16[2,4,96,384]{3,2,1,0:T(8,128)(2,1)S(1)}, bf16[2,4,96,384]{3,2,1,0:T(8,128)(2,1)S(1)}, u32[]{:S(2)}, u32[]{:S(2)}) collective-permute-start(bf16[2,4,96,384]{3,2,1,0:T(8,128)(2,1)S(1)} %bitcast.79), channel_id=1, source_target_pairs={{0,2},{1,5},{2,0},{3,7},{4,6},{5,1},{6,4},{7,3},{8,10},{9,13},{10,... | collective-permute-start | bytes 1769480 | tf_op jit(solution)/shard_map/ppermute | solution.py:33
  35.0 5.7 %collective-permute-start.8 = (bf16[4,96,128]{2,1,0:T(8,128)(2,1)S(1)}, bf16[4,96,128]{2,1,0:T(8,128)(2,1)S(1)}, u32[]{:S(2)}, u32[]{:S(2)}) collective-permute-start(bf16[4,96,128]{2,1,0:T(8,128)(2,1)S(1)} %join.7.a_ref), channel_id=1, source_target_pairs={{0,4},{4,0},{8,12},{12,8},{16,20},{20,16},{24,28},{28,24},{1,5},{5... | collective-permute-start | bytes 294920 | tf_op jit(solution)/shard_map/ppermute | solution.py:24
  35.5 10.0 %collective-permute-start.9 = (bf16[4,96,384]{2,1,0:T(8,128)(2,1)S(1)}, bf16[4,96,384]{2,1,0:T(8,128)(2,1)S(1)}, u32[]{:S(2)}, u32[]{:S(2)}) collective-permute-start(bf16[4,96,384]{2,1,0:T(8,128)(2,1)S(1)} %join.10.a_ref), channel_id=1, source_target_pairs={{0,4},{1,3},{2,6},{3,1},{4,0},{5,7},{6,2},{7,5},{8,12},{9,11},{10,... | collective-permute-start | bytes 884744 | tf_op jit(solution)/shard_map/ppermute | solution.py:33
  37.1 11.7 %collective-permute-start.11 = (bf16[2,4,96,384]{3,2,1,0:T(8,128)(2,1)S(1)}, bf16[2,4,96,384]{3,2,1,0:T(8,128)(2,1)S(1)}, u32[]{:S(2)}, u32[]{:S(2)}) collective-permute-start(bf16[2,4,96,384]{3,2,1,0:T(8,128)(2,1)S(1)} %bitcast.80), channel_id=1, source_target_pairs={{0,1},{1,0},{2,3},{3,2},{4,5},{5,4},{6,7},{7,6},{8,9},{9,8},{10,11... | collective-permute-start | bytes 1769480 | tf_op jit(solution)/shard_map/ppermute | solution.py:24
  45.5 3.2 %collective-permute-start.12 = (bf16[2,4,96,384]{3,2,1,0:T(8,128)(2,1)S(1)}, bf16[2,4,96,384]{3,2,1,0:T(8,128)(2,1)S(1)}, u32[]{:S(2)}, u32[]{:S(2)}) collective-permute-start(bf16[2,4,96,384]{3,2,1,0:T(8,128)(2,1)S(1)} %collective-permute-done.7.refs_1_), channel_id=1, source_target_pairs={{0,1},{1,0},{2,3},{3,2},{4,5},{5,4},{6,7},{7,6},{8,9},{9,8},{10,11... | collective-permute-start | bytes 1769480 | tf_op jit(solution)/shard_map/ppermute | solution.py:24
  46.5 9.9 %collective-permute-start.10 = (bf16[2,4,96,384]{3,2,1,0:T(8,128)(2,1)S(1)}, bf16[2,4,96,384]{3,2,1,0:T(8,128)(2,1)S(1)}, u32[]{:S(2)}, u32[]{:S(2)}) collective-permute-start(bf16[2,4,96,384]{3,2,1,0:T(8,128)(2,1)S(1)} %bitcast.82), channel_id=1, source_target_pairs={{0,2},{1,5},{2,0},{3,7},{4,6},{5,1},{6,4},{7,3},{8,10},{9,13},{10,... | collective-permute-start | bytes 1769480 | tf_op jit(solution)/shard_map/ppermute | solution.py:33
  46.5 9.9 %collective-permute-start.13 = (bf16[2,4,96,384]{3,2,1,0:T(8,128)(2,1)S(1)}, bf16[2,4,96,384]{3,2,1,0:T(8,128)(2,1)S(1)}, u32[]{:S(2)}, u32[]{:S(2)}) collective-permute-start(bf16[2,4,96,384]{3,2,1,0:T(8,128)(2,1)S(1)} %bitcast.83), channel_id=1, source_target_pairs={{0,1},{1,0},{2,3},{3,2},{4,5},{5,4},{6,7},{7,6},{8,9},{9,8},{10,11... | collective-permute-start | bytes 1769480 | tf_op jit(solution)/shard_map/ppermute | solution.py:24
  56.4 2.0 %collective-permute-start.14 = (bf16[2,4,96,384]{3,2,1,0:T(8,128)(2,1)S(1)}, bf16[2,4,96,384]{3,2,1,0:T(8,128)(2,1)S(1)}, u32[]{:S(2)}, u32[]{:S(2)}) collective-permute-start(bf16[2,4,96,384]{3,2,1,0:T(8,128)(2,1)S(1)} %collective-permute-done.10.refs_1_), channel_id=1, source_target_pairs={{0,1},{1,0},{2,3},{3,2},{4,5},{5,4},{6,7},{7,6},{8,9},{9,8},{10,11... | collective-permute-start | bytes 1769480 | tf_op jit(solution)/shard_map/ppermute | solution.py:24
  77.6 4.6 %collective-permute-start.15 = (bf16[1,8,8,768]{3,2,1,0:T(8,128)(2,1)S(1)}, bf16[1,8,8,768]{3,2,1,0:T(8,128)(2,1)S(1)}, u32[]{:S(2)}, u32[]{:S(2)}) collective-permute-start(bf16[1,8,8,768]{3,2,1,0:T(8,128)(2,1)S(1)} %bitcast.99), channel_id=1, source_target_pairs={{0,2},{1,3},{2,0},{3,1},{4,6},{5,7},{6,4},{7,5},{8,10},{9,11},{10,... | collective-permute-start | bytes 294920 | tf_op jit(solution)/shard_map/ppermute | solution.py:24
  82.3 1.5 collective-permute-start.16
  87.1 4.9 %collective-permute-start.18 = (bf16[1,1,8,8,768]{4,3,2,1,0:T(8,128)(2,1)S(1)}, bf16[1,1,8,8,768]{4,3,2,1,0:T(8,128)(2,1)S(1)}, u32[]{:S(2)}, u32[]{:S(2)}) collective-permute-start(bf16[1,1,8,8,768]{4,3,2,1,0:T(8,128)(2,1)S(1)} %slice_bitcast_fusion.2), channel_id=1, source_target_pairs={{0,2},{1,3},{2,0},{3,1},{4,6},{5,7},{6,4},{7,5},{8,10},{9,11},{10,... | collective-permute-start | bytes 294920 | tf_op jit(solution)/shard_map/ppermute | solution.py:24
  109.2 3.8 %collective-permute-start.19 = (bf16[2,4,96,768]{3,2,1,0:T(8,128)(2,1)S(1)}, bf16[2,4,96,768]{3,2,1,0:T(8,128)(2,1)S(1)}, u32[]{:S(2)}, u32[]{:S(2)}) collective-permute-start(bf16[2,4,96,768]{3,2,1,0:T(8,128)(2,1)S(1)} %get-tuple-element.129), channel_id=1, source_target_pairs={{0,1},{1,0},{2,3},{3,2},{4,5},{5,4},{6,7},{7,6},{8,9},{9,8},{10,11... | collective-permute-start | bytes 3538952 | tf_op jit(solution)/shard_map/ppermute | solution.py:24
  116.9 4.8 %collective-permute-start.21 = (bf16[2,4,96,768]{3,2,1,0:T(8,128)(2,1)S(1)}, bf16[2,4,96,768]{3,2,1,0:T(8,128)(2,1)S(1)}, u32[]{:S(2)}, u32[]{:S(2)}) collective-permute-start(bf16[2,4,96,768]{3,2,1,0:T(8,128)(2,1)S(1)} %get-tuple-element.147), channel_id=1, source_target_pairs={{0,1},{1,0},{2,3},{3,2},{4,5},{5,4},{6,7},{7,6},{8,9},{9,8},{10,11... | collective-permute-start | bytes 3538952 | tf_op jit(solution)/shard_map/ppermute | solution.py:24
  117.5 10.7 %collective-permute-start.20 = (bf16[4,96,768]{2,1,0:T(8,128)(2,1)S(1)}, bf16[4,96,768]{2,1,0:T(8,128)(2,1)S(1)}, u32[]{:S(2)}, u32[]{:S(2)}) collective-permute-start(bf16[4,96,768]{2,1,0:T(8,128)(2,1)S(1)} %bitcast.92), channel_id=1, source_target_pairs={{0,2},{1,5},{2,0},{3,7},{4,6},{5,1},{6,4},{7,3},{8,10},{9,13},{10,... | collective-permute-start | bytes 1769480 | tf_op jit(solution)/shard_map/ppermute | solution.py:33
  122.6 16.0 %collective-permute-start.22 = (bf16[4,96,768]{2,1,0:T(8,128)(2,1)S(1)}, bf16[4,96,768]{2,1,0:T(8,128)(2,1)S(1)}, u32[]{:S(2)}, u32[]{:S(2)}) collective-permute-start(bf16[4,96,768]{2,1,0:T(8,128)(2,1)S(1)} %get-tuple-element.149), channel_id=1, source_target_pairs={{0,2},{1,5},{2,0},{3,7},{4,6},{5,1},{6,4},{7,3},{8,10},{9,13},{10,... | collective-permute-start | bytes 1769480 | tf_op jit(solution)/shard_map/ppermute | solution.py:33
  128.8 9.8 %collective-permute-start.23 = (bf16[4,96,384]{2,1,0:T(8,128)(2,1)S(1)}, bf16[4,96,384]{2,1,0:T(8,128)(2,1)S(1)}, u32[]{:S(2)}, u32[]{:S(2)}) collective-permute-start(bf16[4,96,384]{2,1,0:T(8,128)(2,1)S(1)} %get-tuple-element.152), channel_id=1, source_target_pairs={{0,4},{1,3},{2,6},{3,1},{4,0},{5,7},{6,2},{7,5},{8,12},{9,11},{10,... | collective-permute-start | bytes 884744 | tf_op jit(solution)/shard_map/ppermute | solution.py:33
  129.2 11.7 %collective-permute-start.31 = (bf16[4,96,384]{2,1,0:T(8,128)(2,1)S(1)}, bf16[4,96,384]{2,1,0:T(8,128)(2,1)S(1)}, u32[]{:S(2)}, u32[]{:S(2)}) collective-permute-start(bf16[4,96,384]{2,1,0:T(8,128)(2,1)S(1)} %get-tuple-element.161), channel_id=1, source_target_pairs={{0,4},{1,3},{2,6},{3,1},{4,0},{5,7},{6,2},{7,5},{8,12},{9,11},{10,... | collective-permute-start | bytes 884744 | tf_op jit(solution)/shard_map/ppermute | solution.py:33
  133.6 5.0 %collective-permute-start.25 = (f32[13,768]{1,0:T(8,128)S(1)}, f32[13,768]{1,0:T(8,128)S(1)}, u32[]{:S(2)}, u32[]{:S(2)}) collective-permute-start(f32[13,768]{1,0:T(8,128)S(1)} %get-tuple-element.154), channel_id=1, source_target_pairs={{0,16},{4,20},{8,24},{12,28},{16,0},{20,4},{24,8},{28,12},{1,17},{... | collective-permute-start | bytes 119816 | tf_op jit(solution)/shard_map/ppermute | solution.py:24
  138.6 4.5 %collective-permute-start.26 = (f32[13,768]{1,0:T(8,128)S(1)}, f32[13,768]{1,0:T(8,128)S(1)}, u32[]{:S(2)}, u32[]{:S(2)}) collective-permute-start(f32[13,768]{1,0:T(8,128)S(1)} %add.20), channel_id=1, source_target_pairs={{0,8},{4,12},{8,0},{12,4},{16,24},{20,28},{24,16},{28,20},{1,9},{5... | collective-permute-start | bytes 119816 | tf_op jit(solution)/shard_map/ppermute | solution.py:24
  138.8 7.1 %collective-permute-start.24 = (bf16[2,96,384]{2,1,0:T(8,128)(2,1)S(1)}, bf16[2,96,384]{2,1,0:T(8,128)(2,1)S(1)}, u32[]{:S(2)}, u32[]{:S(2)}) collective-permute-start(bf16[2,96,384]{2,1,0:T(8,128)(2,1)S(1)} %get-tuple-element.153), channel_id=1, source_target_pairs={{0,8},{4,12},{8,0},{12,4},{16,24},{20,28},{24,16},{28,20},{1,9},{5... | collective-permute-start | bytes 442376 | tf_op jit(solution)/shard_map/ppermute | solution.py:24
  141.0 7.2 %collective-permute-start.32 = (bf16[2,96,384]{2,1,0:T(8,128)(2,1)S(1)}, bf16[2,96,384]{2,1,0:T(8,128)(2,1)S(1)}, u32[]{:S(2)}, u32[]{:S(2)}) collective-permute-start(bf16[2,96,384]{2,1,0:T(8,128)(2,1)S(1)} %get-tuple-element.163), channel_id=1, source_target_pairs={{0,8},{4,12},{8,0},{12,4},{16,24},{20,28},{24,16},{28,20},{1,9},{5... | collective-permute-start | bytes 442376 | tf_op jit(solution)/shard_map/ppermute | solution.py:24
  145.9 4.1 %collective-permute-start.27 = (f32[13,768]{1,0:T(8,128)S(1)}, f32[13,768]{1,0:T(8,128)S(1)}, u32[]{:S(2)}, u32[]{:S(2)}) collective-permute-start(f32[13,768]{1,0:T(8,128)S(1)} %add.21), channel_id=1, source_target_pairs={{0,4},{4,0},{8,12},{12,8},{16,20},{20,16},{24,28},{28,24},{1,5},{5... | collective-permute-start | bytes 119816 | tf_op jit(solution)/shard_map/ppermute | solution.py:24
  146.7 7.6 %collective-permute-start.30 = (bf16[96,384]{1,0:T(8,128)(2,1)S(1)}, bf16[96,384]{1,0:T(8,128)(2,1)S(1)}, u32[]{:S(2)}, u32[]{:S(2)}) collective-permute-start(bf16[96,384]{1,0:T(8,128)(2,1)S(1)} %bitcast.93), channel_id=1, source_target_pairs={{0,16},{4,20},{8,24},{12,28},{16,0},{20,4},{24,8},{28,12},{1,17},{... | collective-permute-start | bytes 221192 | tf_op jit(solution)/shard_map/ppermute | solution.py:24
  148.3 6.0 %collective-permute-start.33 = (bf16[96,384]{1,0:T(8,128)(2,1)S(1)}, bf16[96,384]{1,0:T(8,128)(2,1)S(1)}, u32[]{:S(2)}, u32[]{:S(2)}) collective-permute-start(bf16[96,384]{1,0:T(8,128)(2,1)S(1)} %bitcast.94), channel_id=1, source_target_pairs={{0,16},{4,20},{8,24},{12,28},{16,0},{20,4},{24,8},{28,12},{1,17},{... | collective-permute-start | bytes 221192 | tf_op jit(solution)/shard_map/ppermute | solution.py:24
  150.0 4.2 %collective-permute-start.28 = (f32[13,768]{1,0:T(8,128)S(1)}, f32[13,768]{1,0:T(8,128)S(1)}, u32[]{:S(2)}, u32[]{:S(2)}) collective-permute-start(f32[13,768]{1,0:T(8,128)S(1)} %add.22), channel_id=1, source_target_pairs={{0,2},{1,3},{2,0},{3,1},{4,6},{5,7},{6,4},{7,5},{8,10},{9,11},{10,... | collective-permute-start | bytes 119816 | tf_op jit(solution)/shard_map/ppermute | solution.py:24
  (8 other events, 105.1 us)

commit v12 on v11

--- a/solution.py
+++ b/solution.py
@@ -116,11 +116,12 @@
     copies = [pltpu.make_async_copy(a, b, sems.at[k]) for k, (a, b) in enumerate(pairs)]
     for copy in copies:
         copy.start()
-    for copy in copies:
+    low, mid = 2 * HEAD_DIM, qkv_ref.shape[2]
+    copies[0].wait()
+    first_ref[...] = jnp.concatenate([qkv_ref[c, :, :low] for c in range(3)], axis=1)
+    for copy in copies[1:]:
         copy.wait()
-    low, mid = 2 * HEAD_DIM, qkv_ref.shape[2]
     out = out_ref[...].astype(f32).T.astype(bf16)
-    first_ref[...] = jnp.concatenate([qkv_ref[c, :, :low] for c in range(3)], axis=1)
     second_ref[...] = jnp.concatenate(
         [qkv_ref[c, :, low:mid] for c in range(3)] + [out[:, low:mid], out[:, :low]], axis=1
     )
@@ -603,18 +604,16 @@
         first, second, held_extra = first[None], second[None], extra[None]
         stages = bits_of(dp)[:-1]
         for bit in stages:
-            others = swap(first, "dp", dp, bit), swap(second, "dp", dp, bit)
-            if bit != stages[-1]:
-                others = lax.optimization_barrier(others)
             put = jnp.concatenate if bit == stages[0] else lambda pair: join(*pair)
-            first = put([first, others[0]])
-            held_extra = put([held_extra, swap(held_extra, "dp", dp, bit)])
-            if bit != stages[-1]:
-                second = put([second, others[1]])
+            first = put([first, swap(first, "dp", dp, bit)])
+        held_extra = jnp.concatenate([held_extra, swap(held_extra, "dp", dp, stages[0])])
         other, held_extra, late = lax.optimization_barrier(
-            (swap_both(first, dp, mp, (1, 0), (0, 2)), held_extra, others[1])
-        )
-        second = join(second, late)
+            (swap_both(first, dp, mp, (1, 0), (0, 2)), held_extra, swap(second, "dp", dp, stages[0]))
+        )
+        second = jnp.concatenate([second, late])
+        for bit in stages[1:]:
+            second = join(second, swap(second, "dp", dp, bit))
+            held_extra = join(held_extra, swap(held_extra, "dp", dp, bit))
         held_extra = join(held_extra, swap(held_extra, "dp", dp, 1))
         held_extra = held_extra.reshape((dp,) + extra.shape)
         if ready:

time: 157 us -> 154 us (0.981)
  starting transfers between devices: 30.4 us -> 27.6 us
    ppermute x26, starting transfers between devices: 21.5 us -> 17.9 us  [swap(): lax.ppermute(array_in, axis_name, [(i, i ^ bit) for i in range(size)])]
    ppermute x26, waiting for transfers between devices: 43 us -> 45 us  [swap(): lax.ppermute(array_in, axis_name, [(i, i ^ bit) for i in range(size)])]
  transfers between devices with their start and end apart: 34 -> 34, of which waited for: 19 -> 21; matrix products, arithmetic and copies ran while one was open for 4% -> 3% of each run, Pallas kernels for 16% -> 16%
where the time goes in v12:
time: 154 us
  Pallas kernels  49.1 us (32%)
  waiting for transfers between devices  48.6 us (32%)
  starting transfers between devices  27.6 us (18%)
  blocking collectives  21.3 us (14%)
  matrix products  3.84 us (2%)
  other arithmetic  2.42 us (2%)
    pallas_call x27, Pallas kernels, call(): pl.pallas_call(functools.partial(kernel, **static), out_shape=[jax.ShapeD...  46.7 us
    ppermute x26, waiting for transfers between devices, swap(): lax.ppermute(array_in, axis_name, [(i, i ^ bit) for i in range(size)])  45 us
    ppermute x26, starting transfers between devices, swap(): lax.ppermute(array_in, axis_name, [(i, i ^ bit) for i in range(size)])  17.9 us
    all_to_all x1, blocking collectives, per_device(): got = lax.all_to_all(got, 'dp', split_axis=0, concat_axis=0, tiled=True)  11.8 us
    ppermute x8, starting transfers between devices, swap_both(): return lax.ppermute(array_in, ('dp', 'mp'), pairs)  9.72 us
    all_to_all x1, blocking collectives, per_device(): back = lax.all_to_all(back, 'dp', split_axis=0, concat_axis=0, tiled=True)  9.51 us
    dot_general x2, matrix products, mm_tn(): lax.dot_general(a, b, (((0,), (0,)), ((), ())), preferred_element_type=f32)  3.84 us
    ppermute x8, waiting for transfers between devices, swap_both(): return lax.ppermute(array_in, ('dp', 'mp'), pairs)  3.59 us
  transfers between devices with their start and end apart: 34, of which 21 were waited for; matrix products, arithmetic and copies ran while one was open for 3% of the time, Pallas kernels for 16%

profile of v12, /device:TPU:0, one launch (start us, length us, event | category | flops | bytes accessed | tf_op | source)
XLA Modules:
  0.0 154.0 jit_solution(13712404378477648809)
XLA Ops:
  1.2 2.4 %pack.1 = (bf16[96,384]{1,0:T(8,128)(2,1)}, bf16[96,384]{1,0:T(8,128)(2,1)}, bf16[96,128]{1,0:T(8,128)(2,1)}) custom-call(s32[3]{0:T(128)} %pad_add_fusion.me_ref, bf16[3,96,192]{2,1,0:T(8,128)(2,1)} %bitcast.103, bf16[192,96]{1,0:T(8,128)(2,1)} %out_hbm.1, bf16[1,96]{1,0:T(2,128)(2,1)} %bitcast.112, bf16[1,96]{1,0:T(2,128)(2,1)} %bitcast.113, ...), custom_call_target="tpu_custom_call" | custom-call | tf_op jit(solution)/shard_map/pack/pallas_call | solution.py:594
  3.7 4.1 %collective-permute-start = (bf16[1,96,384]{2,1,0:T(8,128)(2,1)}, bf16[1,96,384]{2,1,0:T(8,128)(2,1)S(1)}, u32[]{:S(2)}, u32[]{:S(2)}) collective-permute-start(bf16[1,96,384]{2,1,0:T(8,128)(2,1)} %bitcast.107), channel_id=1, source_target_pairs={{0,16},{4,20},{8,24},{12,28},{16,0},{20,4},{24,8},{28,12},{1,17},{... | collective-permute-start | bytes 221192 | tf_op jit(solution)/shard_map/ppermute | solution.py:24
  7.8 4.1 %collective-permute-done = bf16[1,96,384]{2,1,0:T(8,128)(2,1)S(1)} collective-permute-done((bf16[1,96,384]{2,1,0:T(8,128)(2,1)}, bf16[1,96,384]{2,1,0:T(8,128)(2,1)S(1)}, u32[]{:S(2)}, u32[]{:S(2)}) %collective-permute-start) | collective-permute-done | bytes 73760 | tf_op jit(solution)/shard_map/ppermute | solution.py:24
  13.7 4.4 %collective-permute-done.1.b_ref = bf16[2,96,384]{2,1,0:T(8,128)(2,1)S(1)} collective-permute-done((bf16[2,96,384]{2,1,0:T(8,128)(2,1)S(1)}, bf16[2,96,384]{2,1,0:T(8,128)(2,1)S(1)}, u32[]{:S(2)}, u32[]{:S(2)}) %collective-permute-start.1) | collective-permute-done | bytes 147488 | tf_op jit(solution)/shard_map/ppermute | solution.py:24
  19.9 2.5 %collective-permute-start.3 = (bf16[1,96,128]{2,1,0:T(8,128)(2,1)}, bf16[1,96,128]{2,1,0:T(8,128)(2,1)S(1)}, u32[]{:S(2)}, u32[]{:S(2)}) collective-permute-start(bf16[1,96,128]{2,1,0:T(8,128)(2,1)} %bitcast.109), channel_id=1, source_target_pairs={{0,16},{4,20},{8,24},{12,28},{16,0},{20,4},{24,8},{28,12},{1,17},{... | collective-permute-start | bytes 73736 | tf_op jit(solution)/shard_map/ppermute | solution.py:24
  22.8 2.2 %collective-permute-done.3 = bf16[1,96,128]{2,1,0:T(8,128)(2,1)S(1)} collective-permute-done((bf16[1,96,128]{2,1,0:T(8,128)(2,1)}, bf16[1,96,128]{2,1,0:T(8,128)(2,1)S(1)}, u32[]{:S(2)}, u32[]{:S(2)}) %collective-permute-start.3) | collective-permute-done | bytes 24608 | tf_op jit(solution)/shard_map/ppermute | solution.py:24
  25.7 2.1 %collective-permute-done.4 = bf16[1,96,384]{2,1,0:T(8,128)(2,1)S(1)} collective-permute-done((bf16[1,96,384]{2,1,0:T(8,128)(2,1)}, bf16[1,96,384]{2,1,0:T(8,128)(2,1)S(1)}, u32[]{:S(2)}, u32[]{:S(2)}) %collective-permute-start.4) | collective-permute-done | bytes 73760 | tf_op jit(solution)/shard_map/ppermute | solution.py:24
  31.6 3.8 %collective-permute-done.6.b_ref = bf16[2,96,128]{2,1,0:T(8,128)(2,1)S(1)} collective-permute-done((bf16[2,96,128]{2,1,0:T(8,128)(2,1)S(1)}, bf16[2,96,128]{2,1,0:T(8,128)(2,1)S(1)}, u32[]{:S(2)}, u32[]{:S(2)}) %collective-permute-start.6) | collective-permute-done | bytes 49184 | tf_op jit(solution)/shard_map/ppermute | solution.py:24
  37.6 2.5 %collective-permute-done.7.b_ref = bf16[4,96,128]{2,1,0:T(8,128)(2,1)S(1)} collective-permute-done((bf16[4,96,128]{2,1,0:T(8,128)(2,1)S(1)}, bf16[4,96,128]{2,1,0:T(8,128)(2,1)S(1)}, u32[]{:S(2)}, u32[]{:S(2)}) %collective-permute-start.7) | collective-permute-done | bytes 98336 | tf_op jit(solution)/shard_map/ppermute | solution.py:24
  45.3 5.9 %front_pair.1 = (bf16[4,768,384]{2,1,0:T(8,128)(2,1)S(1)}, bf16[4,624,384]{2,1,0:T(8,128)(2,1)S(1)}, bf16[4,3,2,208,208]{4,3,2,1,0:T(8,128)(2,1)S(1)}, bf16[4,624,128]{2,1,0:T(8,128)(2,1)S(1)}) custom-call(s32[3]{0:T(128)S(1)} %copy-done.1, bf16[624,768]{1,0:T(8,128)(2,1)S(1)} %get-tuple-element.97.h_ref, s32[12,200]{1,0:T(8,128)S(1)} %copy-done.5, ...), custom_call_target="tpu_custom_call" | custom-call | flops 11000000512 | bytes 3327372 | tf_op jit(solution)/shard_map/front_pair/pallas_call | solution.py:551
  51.2 2.0 %collective-permute-done.10.refs_1_ = bf16[2,4,96,384]{3,2,1,0:T(8,128)(2,1)S(1)} collective-permute-done((bf16[2,4,96,384]{3,2,1,0:T(8,128)(2,1)S(1)}, bf16[2,4,96,384]{3,2,1,0:T(8,128)(2,1)S(1)}, u32[]{:S(2)}, u32[]{:S(2)}) %collective-permute-start.10) | collective-permute-done | bytes 589856 | tf_op jit(solution)/shard_map/ppermute | solution.py:33
  53.3 2.0 %collective-permute-done.14.refs_3_ = bf16[2,4,96,384]{3,2,1,0:T(8,128)(2,1)S(1)} collective-permute-done((bf16[2,4,96,384]{3,2,1,0:T(8,128)(2,1)S(1)}, bf16[2,4,96,384]{3,2,1,0:T(8,128)(2,1)S(1)}, u32[]{:S(2)}, u32[]{:S(2)}) %collective-permute-start.14) | collective-permute-done | bytes 589856 | tf_op jit(solution)/shard_map/ppermute | solution.py:24
  55.3 5.2 %front_last.1 = (bf16[4,768,256]{2,1,0:T(8,128)(2,1)S(1)}, bf16[4,624,256]{2,1,0:T(8,128)(2,1)S(1)}, bf16[4,3,208,208]{3,2,1,0:T(8,128)(2,1)S(1)}, bf16[624,1024...) custom-call(s32[3]{0:T(128)S(1)} %copy-done.1, ...), custom_call_target="tpu_custom_call" | custom-call | flops 7699999744 | bytes 3966348 | tf_op jit(solution)/shard_map/front_last/pallas_call | solution.py:551
  60.4 2.7 %route.1 = (f32[624,768]{1,0:T(8,128)S(1)}, bf16[624,768]{1,0:T(8,128)(2,1)S(1)}, f32[2,3,8,208]{3,2,1,0:T(8,128)S(1)}, bf16[64,768]{1,0:T(8,128)(2,1)S(1)}, f32[3,1,128]{2,1,0:T(1,128)S(1)}) custom-call(s32[3]{0:T(128)S(1)} %copy-done.1, bf16[3,200,768]{2,1,0:T(8,128)(2,1)S(1)} %bitcast.77, f32[624,768]{1,0:T(8,128)S(1)} %get-tuple-element.103.br_ref, ...), custom_call_target="tpu_custom_call" | custom-call | flops 2200000000 | bytes 4162956 | tf_op jit(solution)/shard_map/route/pallas_call | solution.py:551
  63.1 11.8 %all_to_all.10 = bf16[8,8,768]{2,1,0:T(8,128)(2,1)S(1)} all-to-all(bf16[8,8,768]{2,1,0:T(8,128)(2,1)S(1)} %bitcast.87), channel_id=1, replica_groups=mesh['dp'=8,'mp'=4] {'dp'}, dimensions={0} | all-to-all | bytes 196608 | tf_op jit(solution)/shard_map/all_to_all | solution.py:709
  75.0 4.5 %collective-permute-done.15 = bf16[1,8,8,768]{3,2,1,0:T(8,128)(2,1)S(1)} collective-permute-done((bf16[1,8,8,768]{3,2,1,0:T(8,128)(2,1)S(1)}, bf16[1,8,8,768]{3,2,1,0:T(8,128)(2,1)S(1)}, u32[]{:S(2)}, u32[]{:S(2)}) %collective-permute-start.15) | collective-permute-done | bytes 98336 | tf_op jit(solution)/shard_map/ppermute | solution.py:24
  84.5 4.7 %collective-permute-done.18 = bf16[1,1,8,8,768]{4,3,2,1,0:T(8,128)(2,1)S(1)} collective-permute-done((bf16[1,1,8,8,768]{4,3,2,1,0:T(8,128)(2,1)S(1)}, bf16[1,1,8,8,768]{4,3,2,1,0:T(8,128)(2,1)S(1)}, u32[]{:S(2)}, u32[]{:S(2)}) %collective-permute-start.18) | collective-permute-done | bytes 98336 | tf_op jit(solution)/shard_map/ppermute | solution.py:24
  89.3 9.5 %all_to_all.11 = bf16[8,8,768]{2,1,0:T(8,128)(2,1)S(1)} all-to-all(bf16[8,8,768]{2,1,0:T(8,128)(2,1)S(1)} %fusion.5), channel_id=1, replica_groups=mesh['dp'=8,'mp'=4] {'dp'}, dimensions={0} | all-to-all | bytes 196608 | tf_op jit(solution)/shard_map/all_to_all | solution.py:729
  98.9 3.9 %mix.1 = (bf16[3,200,768]{2,1,0:T(8,128)(2,1)}, f32[624,768]{1,0:T(8,128)S(1)}, bf16[624,768]{1,0:T(8,128)(2,1)S(1)}, bf16[768,624]{1,0:T(8,128)(2,1)S(1)}, f32[13,768]{1,0:T(8,128)S(1)}) custom-call(s32[3]{0:T(128)S(1)} %copy-done.1, f32[624,768]{1,0:T(8,128)S(1)} %get-tuple-element.105.res_ref, bf16[624,768]{1,0:T(8,128)(2,1)S(1)} %get-tuple-element.106.h_ref, ...), custom_call_target="tpu_custom_call" | custom-call | flops 5500000256 | bytes 4315020 | tf_op jit(solution)/shard_map/mix/pallas_call | solution.py:551
  102.8 3.7 %back.4 = (bf16[2,4,96,768]{3,2,1,0:T(8,128)(2,1)S(1)}, bf16[624,640]{1,0:T(8,128)(2,1)S(1)}) custom-call(s32[3]{0:T(128)S(1)} %copy-done.1, bf16[624,768]{1,0:T(8,128)(2,1)S(1)} %get-tuple-element.136.gb_ref, bf16[768,624]{1,0:T(8,128)(2,1)S(1)} %get-tuple-element.114.gbt_ref, bf16[768,624]{1,0:T(8,128)(2,1)S(1)} %get-tuple-element.115.ht_ref, ...), custom_call_target="tpu_custom_call" | custom-call | flops 8800000000 | bytes 12036108 | tf_op jit(solution)/shard_map/back/pallas_call | solution.py:551
  106.6 3.7 %back.5 = (bf16[2,4,96,768]{3,2,1,0:T(8,128)(2,1)S(1)}, bf16[624,640]{1,0:T(8,128)(2,1)S(1)}) custom-call(s32[3]{0:T(128)S(1)} %copy-done.1, bf16[624,768]{1,0:T(8,128)(2,1)S(1)} %get-tuple-element.136.gb_ref, bf16[768,624]{1,0:T(8,128)(2,1)S(1)} %get-tuple-element.114.gbt_ref, bf16[768,624]{1,0:T(8,128)(2,1)S(1)} %get-tuple-element.115.ht_ref, ...), custom_call_target="tpu_custom_call" | custom-call | flops 8800000000 | bytes 12036108 | tf_op jit(solution)/shard_map/back/pallas_call | solution.py:551
  110.5 3.7 %back.6 = (bf16[2,4,96,768]{3,2,1,0:T(8,128)(2,1)S(1)}, bf16[624,640]{1,0:T(8,128)(2,1)S(1)}) custom-call(s32[3]{0:T(128)S(1)} %copy-done.1, bf16[624,768]{1,0:T(8,128)(2,1)S(1)} %get-tuple-element.136.gb_ref, bf16[768,624]{1,0:T(8,128)(2,1)S(1)} %get-tuple-element.114.gbt_ref, bf16[768,624]{1,0:T(8,128)(2,1)S(1)} %get-tuple-element.115.ht_ref, ...), custom_call_target="tpu_custom_call" | custom-call | flops 8800000000 | bytes 12036108 | tf_op jit(solution)/shard_map/back/pallas_call | solution.py:551
  115.1 3.9 %back.7 = (bf16[2,4,96,768]{3,2,1,0:T(8,128)(2,1)S(1)}, bf16[624,640]{1,0:T(8,128)(2,1)S(1)}) custom-call(s32[3]{0:T(128)S(1)} %copy-done.1, bf16[624,768]{1,0:T(8,128)(2,1)S(1)} %get-tuple-element.136.gb_ref, bf16[768,624]{1,0:T(8,128)(2,1)S(1)} %get-tuple-element.114.gbt_ref, bf16[768,624]{1,0:T(8,128)(2,1)S(1)} %get-tuple-element.115.ht_ref, ...), custom_call_target="tpu_custom_call" | custom-call | flops 8800000000 | bytes 12036108 | tf_op jit(solution)/shard_map/back/pallas_call | solution.py:551
  119.9 1.8 %collective-permute-start.22 = (bf16[4,96,768]{2,1,0:T(8,128)(2,1)S(1)}, bf16[4,96,768]{2,1,0:T(8,128)(2,1)S(1)}, u32[]{:S(2)}, u32[]{:S(2)}) collective-permute-start(bf16[4,96,768]{2,1,0:T(8,128)(2,1)S(1)} %get-tuple-element.145), channel_id=1, source_target_pairs={{0,2},{1,5},{2,0},{3,7},{4,6},{5,1},{6,4},{7,3},{8,10},{9,13},{10,... | collective-permute-start | bytes 1769480 | tf_op jit(solution)/shard_map/ppermute | solution.py:33
  121.7 3.8 %input.1.gh_ref = f32[624,768]{1,0:T(8,128)S(1)} custom-call(s32[3]{0:T(128)S(1)} %copy-done.1, bf16[4,768,384]{2,1,0:T(8,128)(2,1)S(1)} %get-tuple-element.129.w_a, bf16[4,768,256]{2,1,0:T(8,128)(2,1)S(1)} %get-tuple-element.130.w_b, bf16[624,640]{1,0:T(8,128)(2,1)S(1)} %get-tuple-element.131.refs_0_, bf16[624,640]{1,0:T(8,128)(2,1)S(1)} %get-tuple-element.132.refs_1_, ...), custom_call_target="tpu_custom_call" | custom-call | flops 4400000000 | bytes 7127052 | tf_op jit(solution)/shard_map/input/pallas_call | solution.py:551
  128.2 2.7 %last.1 = (f32[3,200,768]{2,1,0:T(8,128)}, f32[13,768]{1,0:T(8,128)S(1)}) custom-call(bf16[3,200,768]{2,1,0:T(8,128)(2,1)S(1)} %bitcast.78, f32[624,768]{1,0:T(8,128)S(1)} %get-tuple-element.112.gres_ref, f32[624,768]{1,0:T(8,128)S(1)} %input.1.gh_ref, f32[128,768]{1,0:T(8,128)S(1)} %get-tuple-element.104.ex_ref, f32[13,768]{1,0:T(8,128)S(1)} %get-tuple-element.139.part_ref), custom_call_target="tpu_custom_call" | custom-call | flops 110000000 | bytes 5188608 | tf_op jit(solution)/shard_map/last/pallas_call | solution.py:551
  131.3 4.6 %collective-permute-done.25 = f32[13,768]{1,0:T(8,128)S(1)} collective-permute-done((f32[13,768]{1,0:T(8,128)S(1)}, f32[13,768]{1,0:T(8,128)S(1)}, u32[]{:S(2)}, u32[]{:S(2)}) %collective-permute-start.25) | collective-permute-done | bytes 39968 | tf_op jit(solution)/shard_map/ppermute | solution.py:24
  136.1 2.1 %collective-permute-start.24 = (bf16[2,96,384]{2,1,0:T(8,128)(2,1)S(1)}, bf16[2,96,384]{2,1,0:T(8,128)(2,1)S(1)}, u32[]{:S(2)}, u32[]{:S(2)}) collective-permute-start(bf16[2,96,384]{2,1,0:T(8,128)(2,1)S(1)} %get-tuple-element.149), channel_id=1, source_target_pairs={{0,8},{4,12},{8,0},{12,4},{16,24},{20,28},{24,16},{28,20},{1,9},{5... | collective-permute-start | bytes 442376 | tf_op jit(solution)/shard_map/ppermute | solution.py:24
  138.4 1.9 %convolution_bitcast_fusion.1 = f32[1,768,768]{2,1,0:T(8,128)} fusion(bf16[256,768]{1,0:T(8,128)(2,1)S(1)} %bitcast.75, bf16[256,768]{1,0:T(8,128)(2,1)S(1)} %get-tuple-element.166), kind=kOutput, calls=%fused_computation.1 | convolution fusion | flops 301989888 | bytes 3145728 | tf_op jit(solution)/shard_map/dot_general | solution.py:86
  140.4 2.8 %collective-permute-done.24.refs_1_ = bf16[2,96,384]{2,1,0:T(8,128)(2,1)S(1)} collective-permute-done((bf16[2,96,384]{2,1,0:T(8,128)(2,1)S(1)}, bf16[2,96,384]{2,1,0:T(8,128)(2,1)S(1)}, u32[]{:S(2)}, u32[]{:S(2)}) %collective-permute-start.24) | collective-permute-done | bytes 147488 | tf_op jit(solution)/shard_map/ppermute | solution.py:24
  147.5 1.9 %convolution_bitcast_fusion = f32[1,768,768]{2,1,0:T(8,128)} fusion(bf16[256,768]{1,0:T(8,128)(2,1)S(1)} %get-tuple-element.167, bf16[256,768]{1,0:T(8,128)(2,1)S(1)} %get-tuple-element.168), kind=kOutput, calls=%fused_computation | convolution fusion | flops 301989888 | bytes 3145728 | tf_op jit(solution)/shard_map/dot_general | solution.py:86
  149.5 2.0 %collective-permute-done.28 = f32[13,768]{1,0:T(8,128)S(1)} collective-permute-done((f32[13,768]{1,0:T(8,128)S(1)}, f32[13,768]{1,0:T(8,128)S(1)}, u32[]{:S(2)}, u32[]{:S(2)}) %collective-permute-start.28) | collective-permute-done | bytes 39968 | tf_op jit(solution)/shard_map/ppermute | solution.py:24
  (98 shorter events, 34.1 us)
Async XLA Ops:
  3.7 8.3 %collective-permute-start = (bf16[1,96,384]{2,1,0:T(8,128)(2,1)}, bf16[1,96,384]{2,1,0:T(8,128)(2,1)S(1)}, u32[]{:S(2)}, u32[]{:S(2)}) collective-permute-start(bf16[1,96,384]{2,1,0:T(8,128)(2,1)} %bitcast.107), channel_id=1, source_target_pairs={{0,16},{4,20},{8,24},{12,28},{16,0},{20,4},{24,8},{28,12},{1,17},{... | collective-permute-start | bytes 221192 | tf_op jit(solution)/shard_map/ppermute | solution.py:24
  12.9 5.2 %collective-permute-start.1 = (bf16[2,96,384]{2,1,0:T(8,128)(2,1)S(1)}, bf16[2,96,384]{2,1,0:T(8,128)(2,1)S(1)}, u32[]{:S(2)}, u32[]{:S(2)}) collective-permute-start(bf16[2,96,384]{2,1,0:T(8,128)(2,1)S(1)} %pad_maximum_fusion.2.a_ref), channel_id=1, source_target_pairs={{0,8},{4,12},{8,0},{12,4},{16,24},{20,28},{24,16},{28,20},{1,9},{5... | collective-permute-start | bytes 442376 | tf_op jit(solution)/shard_map/ppermute | solution.py:24
  18.1 9.7 %collective-permute-start.2 = (bf16[4,96,384]{2,1,0:T(8,128)(2,1)S(1)}, bf16[4,96,384]{2,1,0:T(8,128)(2,1)S(1)}, u32[]{:S(2)}, u32[]{:S(2)}) collective-permute-start(bf16[4,96,384]{2,1,0:T(8,128)(2,1)S(1)} %join.6.a_ref), channel_id=1, source_target_pairs={{0,4},{1,3},{2,6},{3,1},{4,0},{5,7},{6,2},{7,5},{8,12},{9,11},{10,... | collective-permute-start | bytes 884744 | tf_op jit(solution)/shard_map/ppermute | solution.py:33
  19.9 5.1 %collective-permute-start.3 = (bf16[1,96,128]{2,1,0:T(8,128)(2,1)}, bf16[1,96,128]{2,1,0:T(8,128)(2,1)S(1)}, u32[]{:S(2)}, u32[]{:S(2)}) collective-permute-start(bf16[1,96,128]{2,1,0:T(8,128)(2,1)} %bitcast.109), channel_id=1, source_target_pairs={{0,16},{4,20},{8,24},{12,28},{16,0},{20,4},{24,8},{28,12},{1,17},{... | collective-permute-start | bytes 73736 | tf_op jit(solution)/shard_map/ppermute | solution.py:24
  22.4 5.5 %collective-permute-start.4 = (bf16[1,96,384]{2,1,0:T(8,128)(2,1)}, bf16[1,96,384]{2,1,0:T(8,128)(2,1)S(1)}, u32[]{:S(2)}, u32[]{:S(2)}) collective-permute-start(bf16[1,96,384]{2,1,0:T(8,128)(2,1)} %bitcast.105), channel_id=1, source_target_pairs={{0,16},{4,20},{8,24},{12,28},{16,0},{20,4},{24,8},{28,12},{1,17},{... | collective-permute-start | bytes 221192 | tf_op jit(solution)/shard_map/ppermute | solution.py:24
  27.9 15.3 %collective-permute-start.5 = (bf16[2,4,96,384]{3,2,1,0:T(8,128)(2,1)S(1)}, bf16[2,4,96,384]{3,2,1,0:T(8,128)(2,1)S(1)}, u32[]{:S(2)}, u32[]{:S(2)}) collective-permute-start(bf16[2,4,96,384]{3,2,1,0:T(8,128)(2,1)S(1)} %bitcast.79), channel_id=1, source_target_pairs={{0,2},{1,5},{2,0},{3,7},{4,6},{5,1},{6,4},{7,3},{8,10},{9,13},{10,... | collective-permute-start | bytes 1769480 | tf_op jit(solution)/shard_map/ppermute | solution.py:33
  29.5 6.5 %collective-permute-start.8 = (bf16[2,96,384]{2,1,0:T(8,128)(2,1)S(1)}, bf16[2,96,384]{2,1,0:T(8,128)(2,1)S(1)}, u32[]{:S(2)}, u32[]{:S(2)}) collective-permute-start(bf16[2,96,384]{2,1,0:T(8,128)(2,1)S(1)} %pad_maximum_fusion.3.a_ref), channel_id=1, source_target_pairs={{0,8},{4,12},{8,0},{12,4},{16,24},{20,28},{24,16},{28,20},{1,9},{5... | collective-permute-start | bytes 442376 | tf_op jit(solution)/shard_map/ppermute | solution.py:24
  31.3 4.1 %collective-permute-start.6 = (bf16[2,96,128]{2,1,0:T(8,128)(2,1)S(1)}, bf16[2,96,128]{2,1,0:T(8,128)(2,1)S(1)}, u32[]{:S(2)}, u32[]{:S(2)}) collective-permute-start(bf16[2,96,128]{2,1,0:T(8,128)(2,1)S(1)} %pad_maximum_fusion.4.a_ref), channel_id=1, source_target_pairs={{0,8},{4,12},{8,0},{12,4},{16,24},{20,28},{24,16},{28,20},{1,9},{5... | collective-permute-start | bytes 147464 | tf_op jit(solution)/shard_map/ppermute | solution.py:24
  35.4 4.7 %collective-permute-start.7 = (bf16[4,96,128]{2,1,0:T(8,128)(2,1)S(1)}, bf16[4,96,128]{2,1,0:T(8,128)(2,1)S(1)}, u32[]{:S(2)}, u32[]{:S(2)}) collective-permute-start(bf16[4,96,128]{2,1,0:T(8,128)(2,1)S(1)} %join.8.a_ref), channel_id=1, source_target_pairs={{0,4},{4,0},{8,12},{12,8},{16,20},{20,16},{24,28},{28,24},{1,5},{5... | collective-permute-start | bytes 294920 | tf_op jit(solution)/shard_map/ppermute | solution.py:24
  36.0 7.2 %collective-permute-start.9 = (bf16[4,96,384]{2,1,0:T(8,128)(2,1)S(1)}, bf16[4,96,384]{2,1,0:T(8,128)(2,1)S(1)}, u32[]{:S(2)}, u32[]{:S(2)}) collective-permute-start(bf16[4,96,384]{2,1,0:T(8,128)(2,1)S(1)} %join.10.a_ref), channel_id=1, source_target_pairs={{0,4},{1,3},{2,6},{3,1},{4,0},{5,7},{6,2},{7,5},{8,12},{9,11},{10,... | collective-permute-start | bytes 884744 | tf_op jit(solution)/shard_map/ppermute | solution.py:33
  37.6 7.1 %collective-permute-start.11 = (bf16[2,4,96,384]{3,2,1,0:T(8,128)(2,1)S(1)}, bf16[2,4,96,384]{3,2,1,0:T(8,128)(2,1)S(1)}, u32[]{:S(2)}, u32[]{:S(2)}) collective-permute-start(bf16[2,4,96,384]{3,2,1,0:T(8,128)(2,1)S(1)} %bitcast.80), channel_id=1, source_target_pairs={{0,1},{1,0},{2,3},{3,2},{4,5},{5,4},{6,7},{7,6},{8,9},{9,8},{10,11... | collective-permute-start | bytes 1769480 | tf_op jit(solution)/shard_map/ppermute | solution.py:24
  43.2 2.0 %collective-permute-start.12 = (bf16[2,4,96,384]{3,2,1,0:T(8,128)(2,1)S(1)}, bf16[2,4,96,384]{3,2,1,0:T(8,128)(2,1)S(1)}, u32[]{:S(2)}, u32[]{:S(2)}) collective-permute-start(bf16[2,4,96,384]{3,2,1,0:T(8,128)(2,1)S(1)} %collective-permute-done.5.refs_1_), channel_id=1, source_target_pairs={{0,1},{1,0},{2,3},{3,2},{4,5},{5,4},{6,7},{7,6},{8,9},{9,8},{10,11... | collective-permute-start | bytes 1769480 | tf_op jit(solution)/shard_map/ppermute | solution.py:24
  43.3 9.9 %collective-permute-start.10 = (bf16[2,4,96,384]{3,2,1,0:T(8,128)(2,1)S(1)}, bf16[2,4,96,384]{3,2,1,0:T(8,128)(2,1)S(1)}, u32[]{:S(2)}, u32[]{:S(2)}) collective-permute-start(bf16[2,4,96,384]{3,2,1,0:T(8,128)(2,1)S(1)} %bitcast.82), channel_id=1, source_target_pairs={{0,2},{1,5},{2,0},{3,7},{4,6},{5,1},{6,4},{7,3},{8,10},{9,13},{10,... | collective-permute-start | bytes 1769480 | tf_op jit(solution)/shard_map/ppermute | solution.py:33
  43.9 9.4 %collective-permute-start.13 = (bf16[2,4,96,384]{3,2,1,0:T(8,128)(2,1)S(1)}, bf16[2,4,96,384]{3,2,1,0:T(8,128)(2,1)S(1)}, u32[]{:S(2)}, u32[]{:S(2)}) collective-permute-start(bf16[2,4,96,384]{3,2,1,0:T(8,128)(2,1)S(1)} %bitcast.83), channel_id=1, source_target_pairs={{0,1},{1,0},{2,3},{3,2},{4,5},{5,4},{6,7},{7,6},{8,9},{9,8},{10,11... | collective-permute-start | bytes 1769480 | tf_op jit(solution)/shard_map/ppermute | solution.py:24
  53.3 2.0 %collective-permute-start.14 = (bf16[2,4,96,384]{3,2,1,0:T(8,128)(2,1)S(1)}, bf16[2,4,96,384]{3,2,1,0:T(8,128)(2,1)S(1)}, u32[]{:S(2)}, u32[]{:S(2)}) collective-permute-start(bf16[2,4,96,384]{3,2,1,0:T(8,128)(2,1)S(1)} %collective-permute-done.10.refs_1_), channel_id=1, source_target_pairs={{0,1},{1,0},{2,3},{3,2},{4,5},{5,4},{6,7},{7,6},{8,9},{9,8},{10,11... | collective-permute-start | bytes 1769480 | tf_op jit(solution)/shard_map/ppermute | solution.py:24
  74.9 4.6 %collective-permute-start.15 = (bf16[1,8,8,768]{3,2,1,0:T(8,128)(2,1)S(1)}, bf16[1,8,8,768]{3,2,1,0:T(8,128)(2,1)S(1)}, u32[]{:S(2)}, u32[]{:S(2)}) collective-permute-start(bf16[1,8,8,768]{3,2,1,0:T(8,128)(2,1)S(1)} %bitcast.99), channel_id=1, source_target_pairs={{0,2},{1,3},{2,0},{3,1},{4,6},{5,7},{6,4},{7,5},{8,10},{9,11},{10,... | collective-permute-start | bytes 294920 | tf_op jit(solution)/shard_map/ppermute | solution.py:24
  79.6 1.5 collective-permute-start.16
  84.4 4.9 %collective-permute-start.18 = (bf16[1,1,8,8,768]{4,3,2,1,0:T(8,128)(2,1)S(1)}, bf16[1,1,8,8,768]{4,3,2,1,0:T(8,128)(2,1)S(1)}, u32[]{:S(2)}, u32[]{:S(2)}) collective-permute-start(bf16[1,1,8,8,768]{4,3,2,1,0:T(8,128)(2,1)S(1)} %slice_bitcast_fusion.2), channel_id=1, source_target_pairs={{0,2},{1,3},{2,0},{3,1},{4,6},{5,7},{6,4},{7,5},{8,10},{9,11},{10,... | collective-permute-start | bytes 294920 | tf_op jit(solution)/shard_map/ppermute | solution.py:24
  106.5 3.8 %collective-permute-start.19 = (bf16[2,4,96,768]{3,2,1,0:T(8,128)(2,1)S(1)}, bf16[2,4,96,768]{3,2,1,0:T(8,128)(2,1)S(1)}, u32[]{:S(2)}, u32[]{:S(2)}) collective-permute-start(bf16[2,4,96,768]{3,2,1,0:T(8,128)(2,1)S(1)} %get-tuple-element.125), channel_id=1, source_target_pairs={{0,1},{1,0},{2,3},{3,2},{4,5},{5,4},{6,7},{7,6},{8,9},{9,8},{10,11... | collective-permute-start | bytes 3538952 | tf_op jit(solution)/shard_map/ppermute | solution.py:24
  114.2 4.8 %collective-permute-start.21 = (bf16[2,4,96,768]{3,2,1,0:T(8,128)(2,1)S(1)}, bf16[2,4,96,768]{3,2,1,0:T(8,128)(2,1)S(1)}, u32[]{:S(2)}, u32[]{:S(2)}) collective-permute-start(bf16[2,4,96,768]{3,2,1,0:T(8,128)(2,1)S(1)} %get-tuple-element.143), channel_id=1, source_target_pairs={{0,1},{1,0},{2,3},{3,2},{4,5},{5,4},{6,7},{7,6},{8,9},{9,8},{10,11... | collective-permute-start | bytes 3538952 | tf_op jit(solution)/shard_map/ppermute | solution.py:24
  114.8 10.7 %collective-permute-start.20 = (bf16[4,96,768]{2,1,0:T(8,128)(2,1)S(1)}, bf16[4,96,768]{2,1,0:T(8,128)(2,1)S(1)}, u32[]{:S(2)}, u32[]{:S(2)}) collective-permute-start(bf16[4,96,768]{2,1,0:T(8,128)(2,1)S(1)} %bitcast.92), channel_id=1, source_target_pairs={{0,2},{1,5},{2,0},{3,7},{4,6},{5,1},{6,4},{7,3},{8,10},{9,13},{10,... | collective-permute-start | bytes 1769480 | tf_op jit(solution)/shard_map/ppermute | solution.py:33
  119.9 16.1 %collective-permute-start.22 = (bf16[4,96,768]{2,1,0:T(8,128)(2,1)S(1)}, bf16[4,96,768]{2,1,0:T(8,128)(2,1)S(1)}, u32[]{:S(2)}, u32[]{:S(2)}) collective-permute-start(bf16[4,96,768]{2,1,0:T(8,128)(2,1)S(1)} %get-tuple-element.145), channel_id=1, source_target_pairs={{0,2},{1,5},{2,0},{3,7},{4,6},{5,1},{6,4},{7,3},{8,10},{9,13},{10,... | collective-permute-start | bytes 1769480 | tf_op jit(solution)/shard_map/ppermute | solution.py:33
  126.1 9.8 %collective-permute-start.23 = (bf16[4,96,384]{2,1,0:T(8,128)(2,1)S(1)}, bf16[4,96,384]{2,1,0:T(8,128)(2,1)S(1)}, u32[]{:S(2)}, u32[]{:S(2)}) collective-permute-start(bf16[4,96,384]{2,1,0:T(8,128)(2,1)S(1)} %get-tuple-element.148), channel_id=1, source_target_pairs={{0,4},{1,3},{2,6},{3,1},{4,0},{5,7},{6,2},{7,5},{8,12},{9,11},{10,... | collective-permute-start | bytes 884744 | tf_op jit(solution)/shard_map/ppermute | solution.py:33
  126.5 11.7 %collective-permute-start.31 = (bf16[4,96,384]{2,1,0:T(8,128)(2,1)S(1)}, bf16[4,96,384]{2,1,0:T(8,128)(2,1)S(1)}, u32[]{:S(2)}, u32[]{:S(2)}) collective-permute-start(bf16[4,96,384]{2,1,0:T(8,128)(2,1)S(1)} %get-tuple-element.157), channel_id=1, source_target_pairs={{0,4},{1,3},{2,6},{3,1},{4,0},{5,7},{6,2},{7,5},{8,12},{9,11},{10,... | collective-permute-start | bytes 884744 | tf_op jit(solution)/shard_map/ppermute | solution.py:33
  130.9 5.0 %collective-permute-start.25 = (f32[13,768]{1,0:T(8,128)S(1)}, f32[13,768]{1,0:T(8,128)S(1)}, u32[]{:S(2)}, u32[]{:S(2)}) collective-permute-start(f32[13,768]{1,0:T(8,128)S(1)} %get-tuple-element.150), channel_id=1, source_target_pairs={{0,16},{4,20},{8,24},{12,28},{16,0},{20,4},{24,8},{28,12},{1,17},{... | collective-permute-start | bytes 119816 | tf_op jit(solution)/shard_map/ppermute | solution.py:24
  135.9 4.5 %collective-permute-start.26 = (f32[13,768]{1,0:T(8,128)S(1)}, f32[13,768]{1,0:T(8,128)S(1)}, u32[]{:S(2)}, u32[]{:S(2)}) collective-permute-start(f32[13,768]{1,0:T(8,128)S(1)} %add.20), channel_id=1, source_target_pairs={{0,8},{4,12},{8,0},{12,4},{16,24},{20,28},{24,16},{28,20},{1,9},{5... | collective-permute-start | bytes 119816 | tf_op jit(solution)/shard_map/ppermute | solution.py:24
  136.1 7.1 %collective-permute-start.24 = (bf16[2,96,384]{2,1,0:T(8,128)(2,1)S(1)}, bf16[2,96,384]{2,1,0:T(8,128)(2,1)S(1)}, u32[]{:S(2)}, u32[]{:S(2)}) collective-permute-start(bf16[2,96,384]{2,1,0:T(8,128)(2,1)S(1)} %get-tuple-element.149), channel_id=1, source_target_pairs={{0,8},{4,12},{8,0},{12,4},{16,24},{20,28},{24,16},{28,20},{1,9},{5... | collective-permute-start | bytes 442376 | tf_op jit(solution)/shard_map/ppermute | solution.py:24
  138.3 7.2 %collective-permute-start.32 = (bf16[2,96,384]{2,1,0:T(8,128)(2,1)S(1)}, bf16[2,96,384]{2,1,0:T(8,128)(2,1)S(1)}, u32[]{:S(2)}, u32[]{:S(2)}) collective-permute-start(bf16[2,96,384]{2,1,0:T(8,128)(2,1)S(1)} %get-tuple-element.159), channel_id=1, source_target_pairs={{0,8},{4,12},{8,0},{12,4},{16,24},{20,28},{24,16},{28,20},{1,9},{5... | collective-permute-start | bytes 442376 | tf_op jit(solution)/shard_map/ppermute | solution.py:24
  143.2 4.1 %collective-permute-start.27 = (f32[13,768]{1,0:T(8,128)S(1)}, f32[13,768]{1,0:T(8,128)S(1)}, u32[]{:S(2)}, u32[]{:S(2)}) collective-permute-start(f32[13,768]{1,0:T(8,128)S(1)} %add.21), channel_id=1, source_target_pairs={{0,4},{4,0},{8,12},{12,8},{16,20},{20,16},{24,28},{28,24},{1,5},{5... | collective-permute-start | bytes 119816 | tf_op jit(solution)/shard_map/ppermute | solution.py:24
  144.0 7.6 %collective-permute-start.30 = (bf16[96,384]{1,0:T(8,128)(2,1)S(1)}, bf16[96,384]{1,0:T(8,128)(2,1)S(1)}, u32[]{:S(2)}, u32[]{:S(2)}) collective-permute-start(bf16[96,384]{1,0:T(8,128)(2,1)S(1)} %bitcast.93), channel_id=1, source_target_pairs={{0,16},{4,20},{8,24},{12,28},{16,0},{20,4},{24,8},{28,12},{1,17},{... | collective-permute-start | bytes 221192 | tf_op jit(solution)/shard_map/ppermute | solution.py:24
  145.6 6.0 %collective-permute-start.33 = (bf16[96,384]{1,0:T(8,128)(2,1)S(1)}, bf16[96,384]{1,0:T(8,128)(2,1)S(1)}, u32[]{:S(2)}, u32[]{:S(2)}) collective-permute-start(bf16[96,384]{1,0:T(8,128)(2,1)S(1)} %bitcast.94), channel_id=1, source_target_pairs={{0,16},{4,20},{8,24},{12,28},{16,0},{20,4},{24,8},{28,12},{1,17},{... | collective-permute-start | bytes 221192 | tf_op jit(solution)/shard_map/ppermute | solution.py:24
  147.3 4.2 %collective-permute-start.28 = (f32[13,768]{1,0:T(8,128)S(1)}, f32[13,768]{1,0:T(8,128)S(1)}, u32[]{:S(2)}, u32[]{:S(2)}) collective-permute-start(f32[13,768]{1,0:T(8,128)S(1)} %add.22), channel_id=1, source_target_pairs={{0,2},{1,3},{2,0},{3,1},{4,6},{5,7},{6,4},{7,5},{8,10},{9,11},{10,... | collective-permute-start | bytes 119816 | tf_op jit(solution)/shard_map/ppermute | solution.py:24
  (9 other events, 134.1 us)

commit v13 on v12

--- a/solution.py
+++ b/solution.py
@@ -106,7 +106,7 @@
 
 
 def pack_kernel(
-    me_ref, qkv_hbm, out_hbm, one_hbm, two_hbm, router_hbm, first_ref, second_ref, extra_ref,
+    me_ref, qkv_hbm, out_hbm, one_hbm, two_hbm, router_hbm, second_ref, extra_ref,
     qkv_ref, out_ref, one_ref, two_ref, router_ref, sems
 ):
     del me_ref
@@ -117,9 +117,7 @@
     for copy in copies:
         copy.start()
     low, mid = 2 * HEAD_DIM, qkv_ref.shape[2]
-    copies[0].wait()
-    first_ref[...] = jnp.concatenate([qkv_ref[c, :, :low] for c in range(3)], axis=1)
-    for copy in copies[1:]:
+    for copy in copies:
         copy.wait()
     out = out_ref[...].astype(f32).T.astype(bf16)
     second_ref[...] = jnp.concatenate(
@@ -231,7 +229,7 @@
 
 
 def fetch_all(me_ref, refs, put):
-    rows, high_size = refs[0].shape[2], refs[0].shape[1]
+    rows, high_size = refs[0].shape[-2], refs[0].shape[1]
     for core in (0, 1):
 
         @pl.when(me_ref[1] == core)
@@ -266,11 +264,12 @@
     w_ref, qkv_ref, p_ref, ho_ref = refs[4:]
 
     def put(slot, at, block):
-        w_ref[slot, at, :] = block
+        for c in range(3):
+            w_ref[slot, at, c * 128 : (c + 1) * 128] = block[c]
 
     if ready:
         for slot in range(4):
-            put(slot, slice(None), refs[slot][...])
+            w_ref[slot] = refs[slot][...]
     else:
         fetch_all(me_ref, refs[:4], put)
     low = low_lanes(tall)
@@ -591,26 +590,32 @@
         word = pl.BlockSpec(memory_space=pltpu.SMEM)
         wide = columns + -columns % 128
         shapes = [(3, d_rows, part), (part, d_rows), (1, d_rows), (1, d_rows), (experts, d_rows)]
-        first, second, extra = pl.pallas_call(
+        qkv = w_qkv.transpose(1, 0, 2)
+        qkv, words = lax.optimization_barrier((qkv, words))
+        first = qkv[:, :, : 2 * HEAD_DIM]
+        second, extra = pl.pallas_call(
             pack_kernel,
-            out_shape=[jax.ShapeDtypeStruct((d_rows, n), bf16) for n in (half, half, wide)],
+            out_shape=[jax.ShapeDtypeStruct((d_rows, n), bf16) for n in (half, wide)],
             in_specs=[word] + [hbm] * 5,
-            out_specs=[vmem] * 3,
+            out_specs=[vmem] * 2,
             scratch_shapes=[pltpu.VMEM(shape, bf16) for shape in shapes] + [pltpu.SemaphoreType.DMA((5,))],
-            compiler_params=pltpu.CompilerParams(vmem_limit_bytes=67_000_000),
+            compiler_params=pltpu.CompilerParams(vmem_limit_bytes=4 << 20),
+            cost_estimate=pl.CostEstimate(flops=cost(2), bytes_accessed=300_000, transcendentals=0),
             name="pack",
-        )(words, w_qkv.transpose(1, 0, 2), w_out, gain_one[None], gain_two[None], router.T)
+        )(words, qkv, w_out, gain_one[None], gain_two[None], router.T)
 
         first, second, held_extra = first[None], second[None], extra[None]
         stages = bits_of(dp)[:-1]
         for bit in stages:
-            put = jnp.concatenate if bit == stages[0] else lambda pair: join(*pair)
-            first = put([first, swap(first, "dp", dp, bit)])
-        held_extra = jnp.concatenate([held_extra, swap(held_extra, "dp", dp, stages[0])])
+            other = swap(first, "dp", dp, bit)
+            if bit == stages[0]:
+                other, second, held_extra = lax.optimization_barrier((other, second, held_extra))
+            first = join(first, other)
+        held_extra = join(held_extra, swap(held_extra, "dp", dp, stages[0]))
         other, held_extra, late = lax.optimization_barrier(
             (swap_both(first, dp, mp, (1, 0), (0, 2)), held_extra, swap(second, "dp", dp, stages[0]))
         )
-        second = jnp.concatenate([second, late])
+        second = join(second, late)
         for bit in stages[1:]:
             second = join(second, swap(second, "dp", dp, bit))
             held_extra = join(held_extra, swap(held_extra, "dp", dp, bit))
@@ -629,7 +634,7 @@
             grant=4,
             **exact,
         )
-        near = join(first, other).reshape((2, high, d_rows, half))
+        near = join(first, other).reshape((2,) + first.shape)
         far = swap_both(near, dp, mp, (0, 2), (1, 0))
         second = second.reshape((high, d_rows, half))
         other = swap_both(second, dp, mp, (1, 0), (0, 2))
@@ -644,9 +649,11 @@
             low = jnp.where(mine, near, other_near)
             high_part = jnp.where(mine, far, other_far)
             blocks = jnp.stack([low[x], high_part[x]]) if of_core else (high_part if x else low)
-            blocks = blocks.reshape((dp, d_rows, half))
-            blocks = unmirrored(blocks)
-            return reorder(blocks, me).reshape(width, half)
+            blocks = blocks.reshape((dp,) + near.shape[2:])
+            blocks = reorder(unmirrored(blocks), me)
+            if blocks.ndim == 4:
+                blocks = blocks.transpose(0, 2, 1, 3)
+            return blocks.reshape(width, half)
 
         def weights_of(parts):
             if ready:

time: 154 us -> 151 us (0.981)
  waiting for transfers between devices: 48.6 us -> 42.8 us
  local copies, waits for them, and re-layouts: 0.09 us -> 4.67 us
  other arithmetic: 2.42 us -> 0.25 us
    ppermute x26, waiting for transfers between devices: 45 us -> 39.4 us  [swap(): lax.ppermute(array_in, axis_name, [(i, i ^ bit) for i in range(size)])]
    unnamed x14 -> x20, local copies, waits for them, and re-layouts: 0.04 us -> 3.73 us
    concatenate x3 -> x0, other arithmetic: 1.67 us -> none  [the longest x1 0.9 us: per_device(): first = put([first, swap(first, 'dp', dp, bit)])]
    pallas_call x27 -> x30, Pallas kernels: 46.7 us -> 47.1 us  [call(): pl.pallas_call(functools.partial(kernel, **static), out_shape=[jax.ShapeD...]
  transfers between devices with their start and end apart: 34 -> 34, of which waited for: 21 -> 19; matrix products, arithmetic and copies ran while one was open for 3% -> 3% of each run, Pallas kernels for 16% -> 17%
where the time goes in v13:
time: 151 us
  Pallas kernels  48.2 us (32%)
  waiting for transfers between devices  42.8 us (28%)
  starting transfers between devices  28.1 us (19%)
  blocking collectives  21.8 us (14%)
  local copies, waits for them, and re-layouts  4.67 us (3%)
  matrix products  3.85 us (3%)
    pallas_call x30, Pallas kernels, call(): pl.pallas_call(functools.partial(kernel, **static), out_shape=[jax.ShapeD...  47.1 us
    ppermute x26, waiting for transfers between devices, swap(): lax.ppermute(array_in, axis_name, [(i, i ^ bit) for i in range(size)])  39.4 us
    ppermute x26, starting transfers between devices, swap(): lax.ppermute(array_in, axis_name, [(i, i ^ bit) for i in range(size)])  18.6 us
    all_to_all x1, blocking collectives, per_device(): got = lax.all_to_all(got, 'dp', split_axis=0, concat_axis=0, tiled=True)  12.3 us
    ppermute x8, starting transfers between devices, swap_both(): return lax.ppermute(array_in, ('dp', 'mp'), pairs)  9.52 us
    all_to_all x1, blocking collectives, per_device(): back = lax.all_to_all(back, 'dp', split_axis=0, concat_axis=0, tiled=True)  9.51 us
    dot_general x2, matrix products, mm_tn(): lax.dot_general(a, b, (((0,), (0,)), ((), ())), preferred_element_type=f32)  3.85 us
    unnamed x20, local copies, waits for them, and re-layouts  3.73 us
  transfers between devices with their start and end apart: 34, of which 19 were waited for; matrix products, arithmetic and copies ran while one was open for 3% of the time, Pallas kernels for 17%

profile of v13, /device:TPU:0, one launch (start us, length us, event | category | flops | bytes accessed | tf_op | source)
XLA Modules:
  0.0 150.7 jit_solution(16846688248406252677)
XLA Ops:
  1.6 4.1 %collective-permute-start = (bf16[1,3,96,128]{3,2,1,0:T(8,128)(2,1)S(1)}, bf16[1,3,96,128]{3,2,1,0:T(8,128)(2,1)S(1)}, u32[]{:S(2)}, u32[]{:S(2)}) collective-permute-start(bf16[1,3,96,128]{3,2,1,0:T(8,128)(2,1)S(1)} %slice_bitcast_fusion.5.a_ref), channel_id=1, source_target_pairs={{0,16},{4,20},{8,24},{12,28},{16,0},{20,4},{24,8},{28,12},{1,17},{... | collective-permute-start | bytes 221192 | tf_op jit(solution)/shard_map/ppermute | solution.py:24
  12.1 3.7 %collective-permute-done.1.b_ref = bf16[2,3,96,128]{3,2,1,0:T(8,128)(2,1)S(1)} collective-permute-done((bf16[2,3,96,128]{3,2,1,0:T(8,128)(2,1)S(1)}, bf16[2,3,96,128]{3,2,1,0:T(8,128)(2,1)S(1)}, u32[]{:S(2)}, u32[]{:S(2)}) %collective-permute-start.1) | collective-permute-done | bytes 147488 | tf_op jit(solution)/shard_map/ppermute | solution.py:24
  17.5 1.6 %collective-permute-start.4 = (bf16[1,96,384]{2,1,0:T(8,128)(2,1)S(1)}, bf16[1,96,384]{2,1,0:T(8,128)(2,1)S(1)}, u32[]{:S(2)}, u32[]{:S(2)}) collective-permute-start(bf16[1,96,384]{2,1,0:T(8,128)(2,1)S(1)} %bitcast.89), channel_id=1, source_target_pairs={{0,16},{4,20},{8,24},{12,28},{16,0},{20,4},{24,8},{28,12},{1,17},{... | collective-permute-start | bytes 221192 | tf_op jit(solution)/shard_map/ppermute | solution.py:24
  20.4 3.6 %collective-permute-done.3.b_ref = bf16[1,96,128]{2,1,0:T(8,128)(2,1)S(1)} collective-permute-done((bf16[1,96,128]{2,1,0:T(8,128)(2,1)S(1)}, bf16[1,96,128]{2,1,0:T(8,128)(2,1)S(1)}, u32[]{:S(2)}, u32[]{:S(2)}) %collective-permute-start.3) | collective-permute-done | bytes 24608 | tf_op jit(solution)/shard_map/ppermute | solution.py:24
  25.6 1.7 %collective-permute-start.8 = (bf16[2,96,384]{2,1,0:T(8,128)(2,1)S(1)}, bf16[2,96,384]{2,1,0:T(8,128)(2,1)S(1)}, u32[]{:S(2)}, u32[]{:S(2)}) collective-permute-start(bf16[2,96,384]{2,1,0:T(8,128)(2,1)S(1)} %join.15.a_ref), channel_id=1, source_target_pairs={{0,8},{4,12},{8,0},{12,4},{16,24},{20,28},{24,16},{28,20},{1,9},{5... | collective-permute-start | bytes 442376 | tf_op jit(solution)/shard_map/ppermute | solution.py:24
  27.7 3.6 %collective-permute-done.6.b_ref = bf16[2,96,128]{2,1,0:T(8,128)(2,1)S(1)} collective-permute-done((bf16[2,96,128]{2,1,0:T(8,128)(2,1)S(1)}, bf16[2,96,128]{2,1,0:T(8,128)(2,1)S(1)}, u32[]{:S(2)}, u32[]{:S(2)}) %collective-permute-start.6) | collective-permute-done | bytes 49184 | tf_op jit(solution)/shard_map/ppermute | solution.py:24
  33.6 2.5 %collective-permute-done.7.b_ref = bf16[4,96,128]{2,1,0:T(8,128)(2,1)S(1)} collective-permute-done((bf16[4,96,128]{2,1,0:T(8,128)(2,1)S(1)}, bf16[4,96,128]{2,1,0:T(8,128)(2,1)S(1)}, u32[]{:S(2)}, u32[]{:S(2)}) %collective-permute-start.7) | collective-permute-done | bytes 98336 | tf_op jit(solution)/shard_map/ppermute | solution.py:24
  41.2 6.2 %front_pair.1 = (bf16[4,768,384]{2,1,0:T(8,128)(2,1)S(1)}, bf16[4,624,384]{2,1,0:T(8,128)(2,1)S(1)}, bf16[4,3,2,208,208]{4,3,2,1,0:T(8,128)(2,1)S(1)}, bf16[4,624,128]{2,1,0:T(8,128)(2,1)S(1)}) custom-call(s32[3]{0:T(128)S(1)} %pad_add_fusion.me_ref, bf16[624,768]{1,0:T(8,128)(2,1)S(1)} %get-tuple-element.105.h_ref, s32[12,200]{1,0:T(8,128)S(1)} %copy-done.6, ...), custom_call_target="tpu_custom_call" | custom-call | flops 11000000512 | bytes 3327372 | tf_op jit(solution)/shard_map/front_pair/pallas_call | solution.py:550
  47.4 1.8 %collective-permute-done.10.refs_1_ = bf16[2,4,96,384]{3,2,1,0:T(8,128)(2,1)S(1)} collective-permute-done((bf16[2,4,96,384]{3,2,1,0:T(8,128)(2,1)S(1)}, bf16[2,4,96,384]{3,2,1,0:T(8,128)(2,1)S(1)}, u32[]{:S(2)}, u32[]{:S(2)}) %collective-permute-start.10) | collective-permute-done | bytes 589856 | tf_op jit(solution)/shard_map/ppermute | solution.py:33
  49.3 2.0 %collective-permute-done.14.refs_3_ = bf16[2,4,96,384]{3,2,1,0:T(8,128)(2,1)S(1)} collective-permute-done((bf16[2,4,96,384]{3,2,1,0:T(8,128)(2,1)S(1)}, bf16[2,4,96,384]{3,2,1,0:T(8,128)(2,1)S(1)}, u32[]{:S(2)}, u32[]{:S(2)}) %collective-permute-start.14) | collective-permute-done | bytes 589856 | tf_op jit(solution)/shard_map/ppermute | solution.py:24
  51.3 5.1 %front_last.1 = (bf16[4,768,256]{2,1,0:T(8,128)(2,1)S(1)}, bf16[4,624,256]{2,1,0:T(8,128)(2,1)S(1)}, bf16[4,3,208,208]{3,2,1,0:T(8,128)(2,1)S(1)}, bf16[624,1024...) custom-call(s32[3]{0:T(128)S(1)} %pad_add_fusion.me_ref, ...), custom_call_target="tpu_custom_call" | custom-call | flops 7699999744 | bytes 3966348 | tf_op jit(solution)/shard_map/front_last/pallas_call | solution.py:550
  56.4 2.7 %route.1 = (f32[624,768]{1,0:T(8,128)S(1)}, bf16[624,768]{1,0:T(8,128)(2,1)S(1)}, f32[2,3,8,208]{3,2,1,0:T(8,128)S(1)}, bf16[64,768]{1,0:T(8,128)(2,1)S(1)}, f32[3,1,128]{2,1,0:T(1,128)S(1)}) custom-call(s32[3]{0:T(128)S(1)} %pad_add_fusion.me_ref, bf16[3,200,768]{2,1,0:T(8,128)(2,1)S(1)} %bitcast.78, f32[624,768]{1,0:T(8,128)S(1)} %get-tuple-element.111.br_ref, ...), custom_call_target="tpu_custom_call" | custom-call | flops 2200000000 | bytes 4162956 | tf_op jit(solution)/shard_map/route/pallas_call | solution.py:550
  59.1 12.3 %all_to_all.10 = bf16[8,8,768]{2,1,0:T(8,128)(2,1)S(1)} all-to-all(bf16[8,8,768]{2,1,0:T(8,128)(2,1)S(1)} %bitcast.88), channel_id=1, replica_groups=mesh['dp'=8,'mp'=4] {'dp'}, dimensions={0} | all-to-all | bytes 196608 | tf_op jit(solution)/shard_map/all_to_all | solution.py:716
  71.6 4.5 %collective-permute-done.15 = bf16[1,8,8,768]{3,2,1,0:T(8,128)(2,1)S(1)} collective-permute-done((bf16[1,8,8,768]{3,2,1,0:T(8,128)(2,1)S(1)}, bf16[1,8,8,768]{3,2,1,0:T(8,128)(2,1)S(1)}, u32[]{:S(2)}, u32[]{:S(2)}) %collective-permute-start.15) | collective-permute-done | bytes 98336 | tf_op jit(solution)/shard_map/ppermute | solution.py:24
  77.7 1.7 %expert.1 = (bf16[256,768]{1,0:T(8,128)(2,1)S(1)}, bf16[256,768]{1,0:T(8,128)(2,1)S(1)}, bf16[256,768]{1,0:T(8,128)(2,1)S(1)}, bf16[256,768]{1,0:T(8,128)(2,1)S(1)}) custom-call(bf16[256,768]{1,0:T(8,128)(2,1)S(1)} %bitcast.75, bf16[768,768]{1,0:T(8,128)(2,1)S(1)} %bitcast.95, bf16[768,768]{1,0:T(8,128)(2,1)S(1)} %bitcast.96), custom_call_target="tpu_custom_call" | custom-call | flops 2200000000 | bytes 2752512 | tf_op jit(solution)/shard_map/expert/pallas_call | solution.py:550
  81.2 4.8 %collective-permute-done.18 = bf16[1,1,8,8,768]{4,3,2,1,0:T(8,128)(2,1)S(1)} collective-permute-done((bf16[1,1,8,8,768]{4,3,2,1,0:T(8,128)(2,1)S(1)}, bf16[1,1,8,8,768]{4,3,2,1,0:T(8,128)(2,1)S(1)}, u32[]{:S(2)}, u32[]{:S(2)}) %collective-permute-start.18) | collective-permute-done | bytes 98336 | tf_op jit(solution)/shard_map/ppermute | solution.py:24
  86.0 9.5 %all_to_all.11 = bf16[8,8,768]{2,1,0:T(8,128)(2,1)S(1)} all-to-all(bf16[8,8,768]{2,1,0:T(8,128)(2,1)S(1)} %fusion.5), channel_id=1, replica_groups=mesh['dp'=8,'mp'=4] {'dp'}, dimensions={0} | all-to-all | bytes 196608 | tf_op jit(solution)/shard_map/all_to_all | solution.py:736
  95.5 3.9 %mix.1 = (bf16[3,200,768]{2,1,0:T(8,128)(2,1)}, f32[624,768]{1,0:T(8,128)S(1)}, bf16[624,768]{1,0:T(8,128)(2,1)S(1)}, bf16[768,624]{1,0:T(8,128)(2,1)S(1)}, f32[13,768]{1,0:T(8,128)S(1)}) custom-call(s32[3]{0:T(128)S(1)} %pad_add_fusion.me_ref, f32[624,768]{1,0:T(8,128)S(1)} %get-tuple-element.113.res_ref, bf16[624,768]{1,0:T(8,128)(2,1)S(1)} %get-tuple-element.114.h_ref, ...), custom_call_target="tpu_custom_call" | custom-call | flops 5500000256 | bytes 4315020 | tf_op jit(solution)/shard_map/mix/pallas_call | solution.py:550
  99.4 3.7 %back.4 = (bf16[2,4,96,768]{3,2,1,0:T(8,128)(2,1)S(1)}, bf16[624,640]{1,0:T(8,128)(2,1)S(1)}) custom-call(s32[3]{0:T(128)S(1)} %pad_add_fusion.me_ref, bf16[624,768]{1,0:T(8,128)(2,1)S(1)} %get-tuple-element.144.gb_ref, bf16[768,624]{1,0:T(8,128)(2,1)S(1)} %get-tuple-element.122.gbt_ref, bf16[768,624]{1,0:T(8,128)(2,1)S(1)} %get-tuple-element.123.ht_ref, ...), custom_call_target="tpu_custom_call" | custom-call | flops 8800000000 | bytes 12036108 | tf_op jit(solution)/shard_map/back/pallas_call | solution.py:550
  103.2 3.7 %back.5 = (bf16[2,4,96,768]{3,2,1,0:T(8,128)(2,1)S(1)}, bf16[624,640]{1,0:T(8,128)(2,1)S(1)}) custom-call(s32[3]{0:T(128)S(1)} %pad_add_fusion.me_ref, bf16[624,768]{1,0:T(8,128)(2,1)S(1)} %get-tuple-element.144.gb_ref, bf16[768,624]{1,0:T(8,128)(2,1)S(1)} %get-tuple-element.122.gbt_ref, bf16[768,624]{1,0:T(8,128)(2,1)S(1)} %get-tuple-element.123.ht_ref, ...), custom_call_target="tpu_custom_call" | custom-call | flops 8800000000 | bytes 12036108 | tf_op jit(solution)/shard_map/back/pallas_call | solution.py:550
  107.2 3.7 %back.6 = (bf16[2,4,96,768]{3,2,1,0:T(8,128)(2,1)S(1)}, bf16[624,640]{1,0:T(8,128)(2,1)S(1)}) custom-call(s32[3]{0:T(128)S(1)} %pad_add_fusion.me_ref, bf16[624,768]{1,0:T(8,128)(2,1)S(1)} %get-tuple-element.144.gb_ref, bf16[768,624]{1,0:T(8,128)(2,1)S(1)} %get-tuple-element.122.gbt_ref, bf16[768,624]{1,0:T(8,128)(2,1)S(1)} %get-tuple-element.123.ht_ref, ...), custom_call_target="tpu_custom_call" | custom-call | flops 8800000000 | bytes 12036108 | tf_op jit(solution)/shard_map/back/pallas_call | solution.py:550
  111.7 3.9 %back.7 = (bf16[2,4,96,768]{3,2,1,0:T(8,128)(2,1)S(1)}, bf16[624,640]{1,0:T(8,128)(2,1)S(1)}) custom-call(s32[3]{0:T(128)S(1)} %pad_add_fusion.me_ref, bf16[624,768]{1,0:T(8,128)(2,1)S(1)} %get-tuple-element.144.gb_ref, bf16[768,624]{1,0:T(8,128)(2,1)S(1)} %get-tuple-element.122.gbt_ref, bf16[768,624]{1,0:T(8,128)(2,1)S(1)} %get-tuple-element.123.ht_ref, ...), custom_call_target="tpu_custom_call" | custom-call | flops 8800000000 | bytes 12036108 | tf_op jit(solution)/shard_map/back/pallas_call | solution.py:550
  116.6 1.8 %collective-permute-start.22 = (bf16[4,96,768]{2,1,0:T(8,128)(2,1)S(1)}, bf16[4,96,768]{2,1,0:T(8,128)(2,1)S(1)}, u32[]{:S(2)}, u32[]{:S(2)}) collective-permute-start(bf16[4,96,768]{2,1,0:T(8,128)(2,1)S(1)} %get-tuple-element.153), channel_id=1, source_target_pairs={{0,2},{1,5},{2,0},{3,7},{4,6},{5,1},{6,4},{7,3},{8,10},{9,13},{10,... | collective-permute-start | bytes 1769480 | tf_op jit(solution)/shard_map/ppermute | solution.py:33
  118.4 3.8 %input.1.gh_ref = f32[624,768]{1,0:T(8,128)S(1)} custom-call(s32[3]{0:T(128)S(1)} %pad_add_fusion.me_ref, bf16[4,768,384]{2,1,0:T(8,128)(2,1)S(1)} %get-tuple-element.137.w_a, bf16[4,768,256]{2,1,0:T(8,128)(2,1)S(1)} %get-tuple-element.138.w_b, bf16[624,640]{1,0:T(8,128)(2,1)S(1)} %get-tuple-element.139.refs_0_, ...), custom_call_target="tpu_custom_call" | custom-call | flops 4400000000 | bytes 7127052 | tf_op jit(solution)/shard_map/input/pallas_call | solution.py:550
  123.2 1.7 %collective-permute-start.31 = (bf16[4,96,384]{2,1,0:T(8,128)(2,1)S(1)}, bf16[4,96,384]{2,1,0:T(8,128)(2,1)S(1)}, u32[]{:S(2)}, u32[]{:S(2)}) collective-permute-start(bf16[4,96,384]{2,1,0:T(8,128)(2,1)S(1)} %get-tuple-element.165), channel_id=1, source_target_pairs={{0,4},{1,3},{2,6},{3,1},{4,0},{5,7},{6,2},{7,5},{8,12},{9,11},{10,... | collective-permute-start | bytes 884744 | tf_op jit(solution)/shard_map/ppermute | solution.py:33
  125.0 2.7 %last.1 = (f32[3,200,768]{2,1,0:T(8,128)}, f32[13,768]{1,0:T(8,128)S(1)}) custom-call(bf16[3,200,768]{2,1,0:T(8,128)(2,1)S(1)} %bitcast.79, f32[624,768]{1,0:T(8,128)S(1)} %get-tuple-element.120.gres_ref, f32[624,768]{1,0:T(8,128)S(1)} %input.1.gh_ref, f32[128,768]{1,0:T(8,128)S(1)} %get-tuple-element.112.ex_ref, f32[13,768]{1,0:T(8,128)S(1)} %get-tuple-element.147.part_ref), custom_call_target="tpu_custom_call" | custom-call | flops 110000000 | bytes 5188608 | tf_op jit(solution)/shard_map/last/pallas_call | solution.py:550
  128.1 4.6 %collective-permute-done.25 = f32[13,768]{1,0:T(8,128)S(1)} collective-permute-done((f32[13,768]{1,0:T(8,128)S(1)}, f32[13,768]{1,0:T(8,128)S(1)}, u32[]{:S(2)}, u32[]{:S(2)}) %collective-permute-start.25) | collective-permute-done | bytes 39968 | tf_op jit(solution)/shard_map/ppermute | solution.py:24
  132.9 2.1 %collective-permute-start.24 = (bf16[2,96,384]{2,1,0:T(8,128)(2,1)S(1)}, bf16[2,96,384]{2,1,0:T(8,128)(2,1)S(1)}, u32[]{:S(2)}, u32[]{:S(2)}) collective-permute-start(bf16[2,96,384]{2,1,0:T(8,128)(2,1)S(1)} %get-tuple-element.157), channel_id=1, source_target_pairs={{0,8},{4,12},{8,0},{12,4},{16,24},{20,28},{24,16},{28,20},{1,9},{5... | collective-permute-start | bytes 442376 | tf_op jit(solution)/shard_map/ppermute | solution.py:24
  135.2 1.9 %convolution_bitcast_fusion.1 = f32[1,768,768]{2,1,0:T(8,128)} fusion(bf16[256,768]{1,0:T(8,128)(2,1)S(1)} %bitcast.76, bf16[256,768]{1,0:T(8,128)(2,1)S(1)} %get-tuple-element.174), kind=kOutput, calls=%fused_computation.1 | convolution fusion | flops 301989888 | bytes 3145728 | tf_op jit(solution)/shard_map/dot_general | solution.py:86
  137.1 2.8 %collective-permute-done.24.refs_1_ = bf16[2,96,384]{2,1,0:T(8,128)(2,1)S(1)} collective-permute-done((bf16[2,96,384]{2,1,0:T(8,128)(2,1)S(1)}, bf16[2,96,384]{2,1,0:T(8,128)(2,1)S(1)}, u32[]{:S(2)}, u32[]{:S(2)}) %collective-permute-start.24) | collective-permute-done | bytes 147488 | tf_op jit(solution)/shard_map/ppermute | solution.py:24
  144.3 1.9 %convolution_bitcast_fusion = f32[1,768,768]{2,1,0:T(8,128)} fusion(bf16[256,768]{1,0:T(8,128)(2,1)S(1)} %get-tuple-element.175, bf16[256,768]{1,0:T(8,128)(2,1)S(1)} %get-tuple-element.176), kind=kOutput, calls=%fused_computation | convolution fusion | flops 301989888 | bytes 3145728 | tf_op jit(solution)/shard_map/dot_general | solution.py:86
  146.2 2.0 %collective-permute-done.28 = f32[13,768]{1,0:T(8,128)S(1)} collective-permute-done((f32[13,768]{1,0:T(8,128)S(1)}, f32[13,768]{1,0:T(8,128)S(1)}, u32[]{:S(2)}, u32[]{:S(2)}) %collective-permute-start.28) | collective-permute-done | bytes 39968 | tf_op jit(solution)/shard_map/ppermute | solution.py:24
  (105 shorter events, 34.1 us)
Async XLA Ops:
  1.6 8.8 %collective-permute-start = (bf16[1,3,96,128]{3,2,1,0:T(8,128)(2,1)S(1)}, bf16[1,3,96,128]{3,2,1,0:T(8,128)(2,1)S(1)}, u32[]{:S(2)}, u32[]{:S(2)}) collective-permute-start(bf16[1,3,96,128]{3,2,1,0:T(8,128)(2,1)S(1)} %slice_bitcast_fusion.5.a_ref), channel_id=1, source_target_pairs={{0,16},{4,20},{8,24},{12,28},{16,0},{20,4},{24,8},{28,12},{1,17},{... | collective-permute-start | bytes 221192 | tf_op jit(solution)/shard_map/ppermute | solution.py:24
  10.5 5.4 %collective-permute-start.1 = (bf16[2,3,96,128]{3,2,1,0:T(8,128)(2,1)S(1)}, bf16[2,3,96,128]{3,2,1,0:T(8,128)(2,1)S(1)}, u32[]{:S(2)}, u32[]{:S(2)}) collective-permute-start(bf16[2,3,96,128]{3,2,1,0:T(8,128)(2,1)S(1)} %join.9.a_ref), channel_id=1, source_target_pairs={{0,8},{4,12},{8,0},{12,4},{16,24},{20,28},{24,16},{28,20},{1,9},{5... | collective-permute-start | bytes 442376 | tf_op jit(solution)/shard_map/ppermute | solution.py:24
  15.9 8.2 %collective-permute-start.2 = (bf16[4,3,96,128]{3,2,1,0:T(8,128)(2,1)S(1)}, bf16[4,3,96,128]{3,2,1,0:T(8,128)(2,1)S(1)}, u32[]{:S(2)}, u32[]{:S(2)}) collective-permute-start(bf16[4,3,96,128]{3,2,1,0:T(8,128)(2,1)S(1)} %join.10.a_ref), channel_id=1, source_target_pairs={{0,4},{1,3},{2,6},{3,1},{4,0},{5,7},{6,2},{7,5},{8,12},{9,11},{10,... | collective-permute-start | bytes 884744 | tf_op jit(solution)/shard_map/ppermute | solution.py:33
  17.5 6.6 %collective-permute-start.4 = (bf16[1,96,384]{2,1,0:T(8,128)(2,1)S(1)}, bf16[1,96,384]{2,1,0:T(8,128)(2,1)S(1)}, u32[]{:S(2)}, u32[]{:S(2)}) collective-permute-start(bf16[1,96,384]{2,1,0:T(8,128)(2,1)S(1)} %bitcast.89), channel_id=1, source_target_pairs={{0,16},{4,20},{8,24},{12,28},{16,0},{20,4},{24,8},{28,12},{1,17},{... | collective-permute-start | bytes 221192 | tf_op jit(solution)/shard_map/ppermute | solution.py:24
  19.1 4.9 %collective-permute-start.3 = (bf16[1,96,128]{2,1,0:T(8,128)(2,1)S(1)}, bf16[1,96,128]{2,1,0:T(8,128)(2,1)S(1)}, u32[]{:S(2)}, u32[]{:S(2)}) collective-permute-start(bf16[1,96,128]{2,1,0:T(8,128)(2,1)S(1)} %bitcast.93), channel_id=1, source_target_pairs={{0,16},{4,20},{8,24},{12,28},{16,0},{20,4},{24,8},{28,12},{1,17},{... | collective-permute-start | bytes 73736 | tf_op jit(solution)/shard_map/ppermute | solution.py:24
  24.1 15.1 %collective-permute-start.5 = (bf16[2,4,3,96,128]{4,3,2,1,0:T(8,128)(2,1)S(1)}, bf16[2,4,3,96,128]{4,3,2,1,0:T(8,128)(2,1)S(1)}, u32[]{:S(2)}, u32[]{:S(2)}) collective-permute-start(bf16[2,4,3,96,128]{4,3,2,1,0:T(8,128)(2,1)S(1)} %bitcast.80), channel_id=1, source_target_pairs={{0,2},{1,5},{2,0},{3,7},{4,6},{5,1},{6,4},{7,3},{8,10},{9,13},{10,... | collective-permute-start | bytes 1769480 | tf_op jit(solution)/shard_map/ppermute | solution.py:33
  25.6 6.4 %collective-permute-start.8 = (bf16[2,96,384]{2,1,0:T(8,128)(2,1)S(1)}, bf16[2,96,384]{2,1,0:T(8,128)(2,1)S(1)}, u32[]{:S(2)}, u32[]{:S(2)}) collective-permute-start(bf16[2,96,384]{2,1,0:T(8,128)(2,1)S(1)} %join.15.a_ref), channel_id=1, source_target_pairs={{0,8},{4,12},{8,0},{12,4},{16,24},{20,28},{24,16},{28,20},{1,9},{5... | collective-permute-start | bytes 442376 | tf_op jit(solution)/shard_map/ppermute | solution.py:24
  27.3 4.1 %collective-permute-start.6 = (bf16[2,96,128]{2,1,0:T(8,128)(2,1)S(1)}, bf16[2,96,128]{2,1,0:T(8,128)(2,1)S(1)}, u32[]{:S(2)}, u32[]{:S(2)}) collective-permute-start(bf16[2,96,128]{2,1,0:T(8,128)(2,1)S(1)} %join.11.a_ref), channel_id=1, source_target_pairs={{0,8},{4,12},{8,0},{12,4},{16,24},{20,28},{24,16},{28,20},{1,9},{5... | collective-permute-start | bytes 147464 | tf_op jit(solution)/shard_map/ppermute | solution.py:24
  31.4 4.7 %collective-permute-start.7 = (bf16[4,96,128]{2,1,0:T(8,128)(2,1)S(1)}, bf16[4,96,128]{2,1,0:T(8,128)(2,1)S(1)}, u32[]{:S(2)}, u32[]{:S(2)}) collective-permute-start(bf16[4,96,128]{2,1,0:T(8,128)(2,1)S(1)} %join.13.a_ref), channel_id=1, source_target_pairs={{0,4},{4,0},{8,12},{12,8},{16,20},{20,16},{24,28},{28,24},{1,5},{5... | collective-permute-start | bytes 294920 | tf_op jit(solution)/shard_map/ppermute | solution.py:24
  32.0 7.2 %collective-permute-start.9 = (bf16[4,96,384]{2,1,0:T(8,128)(2,1)S(1)}, bf16[4,96,384]{2,1,0:T(8,128)(2,1)S(1)}, u32[]{:S(2)}, u32[]{:S(2)}) collective-permute-start(bf16[4,96,384]{2,1,0:T(8,128)(2,1)S(1)} %join.16.a_ref), channel_id=1, source_target_pairs={{0,4},{1,3},{2,6},{3,1},{4,0},{5,7},{6,2},{7,5},{8,12},{9,11},{10,... | collective-permute-start | bytes 884744 | tf_op jit(solution)/shard_map/ppermute | solution.py:33
  33.6 7.1 %collective-permute-start.11 = (bf16[2,4,3,96,128]{4,3,2,1,0:T(8,128)(2,1)S(1)}, bf16[2,4,3,96,128]{4,3,2,1,0:T(8,128)(2,1)S(1)}, u32[]{:S(2)}, u32[]{:S(2)}) collective-permute-start(bf16[2,4,3,96,128]{4,3,2,1,0:T(8,128)(2,1)S(1)} %bitcast.81), channel_id=1, source_target_pairs={{0,1},{1,0},{2,3},{3,2},{4,5},{5,4},{6,7},{7,6},{8,9},{9,8},{10,11... | collective-permute-start | bytes 1769480 | tf_op jit(solution)/shard_map/ppermute | solution.py:24
  39.2 2.0 %collective-permute-start.12 = (bf16[2,4,3,96,128]{4,3,2,1,0:T(8,128)(2,1)S(1)}, bf16[2,4,3,96,128]{4,3,2,1,0:T(8,128)(2,1)S(1)}, u32[]{:S(2)}, u32[]{:S(2)}) collective-permute-start(bf16[2,4,3,96,128]{4,3,2,1,0:T(8,128)(2,1)S(1)} %collective-permute-done.5.refs_1_), channel_id=1, source_target_pairs={{0,1},{1,0},{2,3},{3,2},{4,5},{5,4},{6,7},{7,6},{8,9},{9,8},{10,11... | collective-permute-start | bytes 1769480 | tf_op jit(solution)/shard_map/ppermute | solution.py:24
  39.3 9.9 %collective-permute-start.10 = (bf16[2,4,96,384]{3,2,1,0:T(8,128)(2,1)S(1)}, bf16[2,4,96,384]{3,2,1,0:T(8,128)(2,1)S(1)}, u32[]{:S(2)}, u32[]{:S(2)}) collective-permute-start(bf16[2,4,96,384]{3,2,1,0:T(8,128)(2,1)S(1)} %bitcast.83), channel_id=1, source_target_pairs={{0,2},{1,5},{2,0},{3,7},{4,6},{5,1},{6,4},{7,3},{8,10},{9,13},{10,... | collective-permute-start | bytes 1769480 | tf_op jit(solution)/shard_map/ppermute | solution.py:33
  40.0 9.3 %collective-permute-start.13 = (bf16[2,4,96,384]{3,2,1,0:T(8,128)(2,1)S(1)}, bf16[2,4,96,384]{3,2,1,0:T(8,128)(2,1)S(1)}, u32[]{:S(2)}, u32[]{:S(2)}) collective-permute-start(bf16[2,4,96,384]{3,2,1,0:T(8,128)(2,1)S(1)} %bitcast.84), channel_id=1, source_target_pairs={{0,1},{1,0},{2,3},{3,2},{4,5},{5,4},{6,7},{7,6},{8,9},{9,8},{10,11... | collective-permute-start | bytes 1769480 | tf_op jit(solution)/shard_map/ppermute | solution.py:24
  49.3 2.0 %collective-permute-start.14 = (bf16[2,4,96,384]{3,2,1,0:T(8,128)(2,1)S(1)}, bf16[2,4,96,384]{3,2,1,0:T(8,128)(2,1)S(1)}, u32[]{:S(2)}, u32[]{:S(2)}) collective-permute-start(bf16[2,4,96,384]{3,2,1,0:T(8,128)(2,1)S(1)} %collective-permute-done.10.refs_1_), channel_id=1, source_target_pairs={{0,1},{1,0},{2,3},{3,2},{4,5},{5,4},{6,7},{7,6},{8,9},{9,8},{10,11... | collective-permute-start | bytes 1769480 | tf_op jit(solution)/shard_map/ppermute | solution.py:24
  71.5 4.6 %collective-permute-start.15 = (bf16[1,8,8,768]{3,2,1,0:T(8,128)(2,1)S(1)}, bf16[1,8,8,768]{3,2,1,0:T(8,128)(2,1)S(1)}, u32[]{:S(2)}, u32[]{:S(2)}) collective-permute-start(bf16[1,8,8,768]{3,2,1,0:T(8,128)(2,1)S(1)} %bitcast.109), channel_id=1, source_target_pairs={{0,2},{1,3},{2,0},{3,1},{4,6},{5,7},{6,4},{7,5},{8,10},{9,11},{10,... | collective-permute-start | bytes 294920 | tf_op jit(solution)/shard_map/ppermute | solution.py:24
  76.1 1.5 %collective-permute-start.16 = (bf16[2,8,8,768]{3,2,1,0:T(8,128)(2,1)S(1)}, bf16[2,8,8,768]{3,2,1,0:T(8,128)(2,1)S(1)}, u32[]{:S(2)}, u32[]{:S(2)}) collective-permute-start(bf16[2,8,8,768]{3,2,1,0:T(8,128)(2,1)S(1)} %get-tuple-element.179), channel_id=1, source_target_pairs={{0,1},{1,0},{2,3},{3,2},{4,5},{5,4},{6,7},{7,6},{8,9},{9,8},{10,11... | collective-permute-start | bytes 589832 | tf_op jit(solution)/shard_map/ppermute | solution.py:24
  81.0 4.9 %collective-permute-start.18 = (bf16[1,1,8,8,768]{4,3,2,1,0:T(8,128)(2,1)S(1)}, bf16[1,1,8,8,768]{4,3,2,1,0:T(8,128)(2,1)S(1)}, u32[]{:S(2)}, u32[]{:S(2)}) collective-permute-start(bf16[1,1,8,8,768]{4,3,2,1,0:T(8,128)(2,1)S(1)} %slice_bitcast_fusion.2), channel_id=1, source_target_pairs={{0,2},{1,3},{2,0},{3,1},{4,6},{5,7},{6,4},{7,5},{8,10},{9,11},{10,... | collective-permute-start | bytes 294920 | tf_op jit(solution)/shard_map/ppermute | solution.py:24
  103.1 3.8 %collective-permute-start.19 = (bf16[2,4,96,768]{3,2,1,0:T(8,128)(2,1)S(1)}, bf16[2,4,96,768]{3,2,1,0:T(8,128)(2,1)S(1)}, u32[]{:S(2)}, u32[]{:S(2)}) collective-permute-start(bf16[2,4,96,768]{3,2,1,0:T(8,128)(2,1)S(1)} %get-tuple-element.133), channel_id=1, source_target_pairs={{0,1},{1,0},{2,3},{3,2},{4,5},{5,4},{6,7},{7,6},{8,9},{9,8},{10,11... | collective-permute-start | bytes 3538952 | tf_op jit(solution)/shard_map/ppermute | solution.py:24
  110.9 4.8 %collective-permute-start.21 = (bf16[2,4,96,768]{3,2,1,0:T(8,128)(2,1)S(1)}, bf16[2,4,96,768]{3,2,1,0:T(8,128)(2,1)S(1)}, u32[]{:S(2)}, u32[]{:S(2)}) collective-permute-start(bf16[2,4,96,768]{3,2,1,0:T(8,128)(2,1)S(1)} %get-tuple-element.151), channel_id=1, source_target_pairs={{0,1},{1,0},{2,3},{3,2},{4,5},{5,4},{6,7},{7,6},{8,9},{9,8},{10,11... | collective-permute-start | bytes 3538952 | tf_op jit(solution)/shard_map/ppermute | solution.py:24
  111.5 10.7 %collective-permute-start.20 = (bf16[4,96,768]{2,1,0:T(8,128)(2,1)S(1)}, bf16[4,96,768]{2,1,0:T(8,128)(2,1)S(1)}, u32[]{:S(2)}, u32[]{:S(2)}) collective-permute-start(bf16[4,96,768]{2,1,0:T(8,128)(2,1)S(1)} %bitcast.99), channel_id=1, source_target_pairs={{0,2},{1,5},{2,0},{3,7},{4,6},{5,1},{6,4},{7,3},{8,10},{9,13},{10,... | collective-permute-start | bytes 1769480 | tf_op jit(solution)/shard_map/ppermute | solution.py:33
  116.6 16.1 %collective-permute-start.22 = (bf16[4,96,768]{2,1,0:T(8,128)(2,1)S(1)}, bf16[4,96,768]{2,1,0:T(8,128)(2,1)S(1)}, u32[]{:S(2)}, u32[]{:S(2)}) collective-permute-start(bf16[4,96,768]{2,1,0:T(8,128)(2,1)S(1)} %get-tuple-element.153), channel_id=1, source_target_pairs={{0,2},{1,5},{2,0},{3,7},{4,6},{5,1},{6,4},{7,3},{8,10},{9,13},{10,... | collective-permute-start | bytes 1769480 | tf_op jit(solution)/shard_map/ppermute | solution.py:33
  122.9 9.9 %collective-permute-start.23 = (bf16[4,96,384]{2,1,0:T(8,128)(2,1)S(1)}, bf16[4,96,384]{2,1,0:T(8,128)(2,1)S(1)}, u32[]{:S(2)}, u32[]{:S(2)}) collective-permute-start(bf16[4,96,384]{2,1,0:T(8,128)(2,1)S(1)} %get-tuple-element.156), channel_id=1, source_target_pairs={{0,4},{1,3},{2,6},{3,1},{4,0},{5,7},{6,2},{7,5},{8,12},{9,11},{10,... | collective-permute-start | bytes 884744 | tf_op jit(solution)/shard_map/ppermute | solution.py:33
  123.2 11.7 %collective-permute-start.31 = (bf16[4,96,384]{2,1,0:T(8,128)(2,1)S(1)}, bf16[4,96,384]{2,1,0:T(8,128)(2,1)S(1)}, u32[]{:S(2)}, u32[]{:S(2)}) collective-permute-start(bf16[4,96,384]{2,1,0:T(8,128)(2,1)S(1)} %get-tuple-element.165), channel_id=1, source_target_pairs={{0,4},{1,3},{2,6},{3,1},{4,0},{5,7},{6,2},{7,5},{8,12},{9,11},{10,... | collective-permute-start | bytes 884744 | tf_op jit(solution)/shard_map/ppermute | solution.py:33
  127.6 5.0 %collective-permute-start.25 = (f32[13,768]{1,0:T(8,128)S(1)}, f32[13,768]{1,0:T(8,128)S(1)}, u32[]{:S(2)}, u32[]{:S(2)}) collective-permute-start(f32[13,768]{1,0:T(8,128)S(1)} %get-tuple-element.158), channel_id=1, source_target_pairs={{0,16},{4,20},{8,24},{12,28},{16,0},{20,4},{24,8},{28,12},{1,17},{... | collective-permute-start | bytes 119816 | tf_op jit(solution)/shard_map/ppermute | solution.py:24
  132.6 4.5 %collective-permute-start.26 = (f32[13,768]{1,0:T(8,128)S(1)}, f32[13,768]{1,0:T(8,128)S(1)}, u32[]{:S(2)}, u32[]{:S(2)}) collective-permute-start(f32[13,768]{1,0:T(8,128)S(1)} %add.20), channel_id=1, source_target_pairs={{0,8},{4,12},{8,0},{12,4},{16,24},{20,28},{24,16},{28,20},{1,9},{5... | collective-permute-start | bytes 119816 | tf_op jit(solution)/shard_map/ppermute | solution.py:24
  132.9 7.1 %collective-permute-start.24 = (bf16[2,96,384]{2,1,0:T(8,128)(2,1)S(1)}, bf16[2,96,384]{2,1,0:T(8,128)(2,1)S(1)}, u32[]{:S(2)}, u32[]{:S(2)}) collective-permute-start(bf16[2,96,384]{2,1,0:T(8,128)(2,1)S(1)} %get-tuple-element.157), channel_id=1, source_target_pairs={{0,8},{4,12},{8,0},{12,4},{16,24},{20,28},{24,16},{28,20},{1,9},{5... | collective-permute-start | bytes 442376 | tf_op jit(solution)/shard_map/ppermute | solution.py:24
  135.1 7.2 %collective-permute-start.32 = (bf16[2,96,384]{2,1,0:T(8,128)(2,1)S(1)}, bf16[2,96,384]{2,1,0:T(8,128)(2,1)S(1)}, u32[]{:S(2)}, u32[]{:S(2)}) collective-permute-start(bf16[2,96,384]{2,1,0:T(8,128)(2,1)S(1)} %get-tuple-element.167), channel_id=1, source_target_pairs={{0,8},{4,12},{8,0},{12,4},{16,24},{20,28},{24,16},{28,20},{1,9},{5... | collective-permute-start | bytes 442376 | tf_op jit(solution)/shard_map/ppermute | solution.py:24
  139.9 4.1 %collective-permute-start.27 = (f32[13,768]{1,0:T(8,128)S(1)}, f32[13,768]{1,0:T(8,128)S(1)}, u32[]{:S(2)}, u32[]{:S(2)}) collective-permute-start(f32[13,768]{1,0:T(8,128)S(1)} %add.21), channel_id=1, source_target_pairs={{0,4},{4,0},{8,12},{12,8},{16,20},{20,16},{24,28},{28,24},{1,5},{5... | collective-permute-start | bytes 119816 | tf_op jit(solution)/shard_map/ppermute | solution.py:24
  140.7 7.6 %collective-permute-start.30 = (bf16[96,384]{1,0:T(8,128)(2,1)S(1)}, bf16[96,384]{1,0:T(8,128)(2,1)S(1)}, u32[]{:S(2)}, u32[]{:S(2)}) collective-permute-start(bf16[96,384]{1,0:T(8,128)(2,1)S(1)} %bitcast.100), channel_id=1, source_target_pairs={{0,16},{4,20},{8,24},{12,28},{16,0},{20,4},{24,8},{28,12},{1,17},{... | collective-permute-start | bytes 221192 | tf_op jit(solution)/shard_map/ppermute | solution.py:24
  142.3 6.0 %collective-permute-start.33 = (bf16[96,384]{1,0:T(8,128)(2,1)S(1)}, bf16[96,384]{1,0:T(8,128)(2,1)S(1)}, u32[]{:S(2)}, u32[]{:S(2)}) collective-permute-start(bf16[96,384]{1,0:T(8,128)(2,1)S(1)} %bitcast.101), channel_id=1, source_target_pairs={{0,16},{4,20},{8,24},{12,28},{16,0},{20,4},{24,8},{28,12},{1,17},{... | collective-permute-start | bytes 221192 | tf_op jit(solution)/shard_map/ppermute | solution.py:24
  144.0 4.1 %collective-permute-start.28 = (f32[13,768]{1,0:T(8,128)S(1)}, f32[13,768]{1,0:T(8,128)S(1)}, u32[]{:S(2)}, u32[]{:S(2)}) collective-permute-start(f32[13,768]{1,0:T(8,128)S(1)} %add.22), channel_id=1, source_target_pairs={{0,2},{1,3},{2,0},{3,1},{4,6},{5,7},{6,4},{7,5},{8,10},{9,11},{10,... | collective-permute-start | bytes 119816 | tf_op jit(solution)/shard_map/ppermute | solution.py:24
  (12 other events, 84.2 us)

commit v14 on v13

--- a/solution.py
+++ b/solution.py
@@ -294,41 +294,53 @@
     lax.fori_loop(0, w_ref.shape[0], group, 0)
 
 
-def front_last_kernel(me_ref, h_ref, mask_ref, pair_ref, *refs, images, tall, ready):
-    w_ref, qkv_ref, p_ref, ho_ref, wo_ref, br_ref = refs[4:]
+def front_last_kernel(me_ref, h_ref, mask_ref, pair_ref, *refs, images, tall, ready, flip):
+    w_ref, qkv_ref, p_ref, ho_ref, wo_ref, br_ref = refs[-6:]
 
     def put(slot, at, block):
         w_ref[slot, at, :] = block[:, :256]
         wo_ref[at, slot * 256 : (slot + 1) * 256] = block[:, 128:]
 
     if ready:
-        for slot in range(4):
+        for slot in range(2):
             put(slot, slice(None), refs[slot][...])
     else:
-        fetch_all(me_ref, refs[:4], put)
+        near, far = refs[:2]
+        rows, high_size = near.shape[-2], near.shape[1]
+        for core in (0, 1):
+
+            @pl.when(me_ref[1] == core)
+            def _(core=core):
+                for x in (0, 1):
+                    for r in range(2 * high_size):
+                        low, high = r & 1, mirrored(r >> 1, high_size)
+                        if core == flip:
+                            block = (far if x else near)[low, high]
+                        else:
+                            block = (far if low else near)[x, high]
+                        d = jnp.bitwise_xor(me_ref[0], r)
+                        put(x, pl.ds(pl.multiple_of(d * rows, 16), rows), block)
+
     low = low_lanes(tall)
-
-    def two(i, carry):
-        places = [(2 * i + k, b) for k in (0, 1) for b in range(images)]
-        for j in (2 * i, 2 * i + 1):
-            qkv_ref[j] = mm(h_ref[...], w_ref[j]).astype(bf16)
-        triples = []
-        for j, b in places:
-            joined = qkv_ref[j, pl.ds(b * tall, tall), :]
-            qk, v = joined[:, :128], joined[:, 128:256]
-            k = pltpu.roll(qk.astype(f32), HEAD_DIM, 1).astype(bf16)
-            bias = bias_of(mask_ref, me_ref, b, images, tall)
-            triples.append((jnp.where(low, qk, jnp.zeros_like(qk)), k, v, bias))
-        probs, outs = attend(triples)
-        for (j, b), prob, out in zip(places, probs, outs):
-            at, start = pl.ds(b * tall, tall), pl.multiple_of(j * 256, 256)
-            p_ref[j, b] = prob
-            ho_ref[at, pl.ds(start, 128)] = jnp.where(low, 0.0, pltpu.roll(out, HEAD_DIM, 1)).astype(bf16)
-            ho_ref[at, pl.ds(start + 128, 128)] = pair_ref[j, at, :]
-        return carry
-
-    lax.fori_loop(0, w_ref.shape[0] // 2, two, 0)
-    br_ref[...] = mm_nt(ho_ref[...], wo_ref[...])
+    places = [(x, b) for x in (0, 1) for b in range(images)]
+    for x in (0, 1):
+        qkv_ref[x] = mm(h_ref[...], w_ref[x]).astype(bf16)
+    triples = []
+    for x, b in places:
+        joined = qkv_ref[x, pl.ds(b * tall, tall), :]
+        qk, v = joined[:, :128], joined[:, 128:256]
+        k = pltpu.roll(qk.astype(f32), HEAD_DIM, 1).astype(bf16)
+        bias = bias_of(mask_ref, me_ref, b, images, tall)
+        triples.append((jnp.where(low, qk, jnp.zeros_like(qk)), k, v, bias))
+    probs, outs = attend(triples)
+    of_core = jnp.bitwise_xor(me_ref[1], flip)
+    for (x, b), prob, out in zip(places, probs, outs):
+        at, start = pl.ds(b * tall, tall), x * 256
+        p_ref[x, b] = prob
+        ho_ref[at, start : start + 128] = jnp.where(low, 0.0, pltpu.roll(out, HEAD_DIM, 1)).astype(bf16)
+        ho_ref[at, start + 128 : start + 256] = pair_ref[x + 2 * of_core, at, :]
+    branch = mm_nt(ho_ref[...], wo_ref[...])
+    br_ref[...] = branch + refs[2][...] if flip else branch
 
 
 def spot(rows, b, start, experts):
@@ -451,14 +463,14 @@
     gw_ref, gj_ref, dho_ref, *, images, tall, x, flip
 ):
     j = x + 2 * jnp.bitwise_xor(me_ref[1], flip)
-    own = pl.ds(pl.multiple_of(j * 256, 256), 256)
+    own = slice(x * 256, (x + 1) * 256)
     scale = HEAD_DIM ** (-0.5)
     low = low_lanes(tall)
     dho_ref[...] = mm(gb_ref[...], wo_ref[:, own])
     heads, dots = [], []
     for b in range(images):
         at = pl.ds(b * tall, tall)
-        joined, joined_last = qkv_a[j, at, :], qkv_b[j, at, :]
+        joined, joined_last = qkv_a[j, at, :], qkv_b[x, at, :]
         q_pair, k_pair, v_pair = joined[:, :128], joined[:, 128:256], joined[:, 256:384]
         qk_last, v_last = joined_last[:, :128], joined_last[:, 128:256]
         grad = dho_ref[at, :].astype(bf16).astype(f32)
@@ -474,7 +486,7 @@
         heads += [
             (p_a[j, b, 0], jnp.where(low, grad_pair, 0.0).astype(bf16), v_pair, q_pair, k_pair),
             (p_a[j, b, 1], jnp.where(low, 0.0, grad_pair).astype(bf16), v_pair, q_pair, k_pair),
-            (p_b[j, b], grad_last, v_last, qk_last, qk_last),
+            (p_b[x, b], grad_last, v_last, qk_last, qk_last),
         ]
     grad_p = [mm_nt(g, v) for _, g, v, _, _ in heads]
     grad_s = [
@@ -512,11 +524,11 @@
         gw_ref[entry + (slice(None), slice(640, 768))] = grad_out[at, 128:].astype(bf16)
 
 
-def input_kernel(me_ref, w_a, w_b, *refs, order):
+def input_kernel(me_ref, w_a, w_own, w_other, *refs, order):
     grads, gh_ref = refs[:-1], refs[-1]
     for k, (ref, (x, flip)) in enumerate(zip(grads, order)):
         j = x + 2 * jnp.bitwise_xor(me_ref[1], flip)
-        into = mm_nt(ref[:, :384], w_a[j]) + mm_nt(ref[:, 384:], w_b[j])
+        into = mm_nt(ref[:, :384], w_a[j]) + mm_nt(ref[:, 384:], (w_own, w_other)[flip][x])
         if k == 0:
             gh_ref[...] = into
         else:
@@ -681,21 +693,35 @@
         w_a, qkv_a, p_a, ho_a = pair
         second_far, ho_a = lax.optimization_barrier((second_far, ho_a))
         second = (second_near, second_far, second_near_other, swap(second_far, "mp", mp, 1))
-        w_b, qkv_b, p_b, heads_out, w_heads, branch = call(
-            front_last_kernel,
-            saved(256, 256, ())[:3]
-            + [
-                ((count, 256 * mp), bf16),
-                ((width, 256 * mp), bf16),
-                ((count, width), f32),
-            ],
-            (words, h_one, token_mask, ho_a) + weights_of(second),
-            flops=cost(7),
-            name="front_last",
-            grant=10,
-            ready=ready,
-            **static,
-        )
+        last_parts, branch = [], ()
+        for flip in (0, 1):
+            if ready:
+                sources = tuple(
+                    jnp.where(core == flip, whole(x, 0, *second), whole(x, 1, *second)) for x in (0, 1)
+                )
+            else:
+                sources = second[2:] if flip else second[:2]
+            outs = call(
+                front_last_kernel,
+                [
+                    ((2, width, 256), bf16),
+                    ((2, count, 256), bf16),
+                    ((2, images, tall, tall), bf16),
+                    ((count, 512), bf16),
+                    ((width, 512), bf16),
+                    ((count, width), f32),
+                ],
+                (words, h_one, token_mask, ho_a) + sources + branch,
+                flops=cost(3),
+                name="front_last",
+                grant=10,
+                ready=ready,
+                flip=flip,
+                **static,
+            )
+            last_parts.append(outs[:5])
+            branch = (outs[5],)
+        branch = branch[0]
         resid, h_two, soft, sent, sq_branch = call(
             route_kernel,
             [
@@ -761,7 +787,7 @@
             grads, joined = call(
                 back_kernel,
                 [(shape, bf16), ((count, JOINED), bf16)],
-                (words, grad_in, grad_turned, h_turned, qkv_a, p_a, qkv_b, p_b, heads_out, w_heads),
+                (words, grad_in, grad_turned, h_turned, qkv_a, p_a) + tuple(last_parts[flip][1:5]),
                 [pltpu.VMEM((count, 256), f32)],
                 flops=cost(8),
                 name="back",
@@ -815,7 +841,7 @@
         grad_h = call(
             input_kernel,
             [((count, width), f32)],
-            (words, w_a, w_b, joined_a, joined_b, joined_c, joined_d),
+            (words, w_a, last_parts[0][0], last_parts[1][0], joined_a, joined_b, joined_c, joined_d),
             flops=cost(4),
             name="input",
             grant=8,

time: 151 us -> 151 us (level)
  waiting for transfers between devices: 42.8 us -> 40.7 us
    ppermute x26, waiting for transfers between devices: 39.4 us -> 37.3 us  [swap(): lax.ppermute(array_in, axis_name, [(i, i ^ bit) for i in range(size)])]
    pallas_call x30 -> x31, Pallas kernels: 47.1 us -> 48.6 us  [call(): pl.pallas_call(functools.partial(kernel, **static), out_shape=[jax.ShapeD...]
  transfers between devices with their start and end apart: 34 -> 34, of which waited for: 19 -> 18; matrix products, arithmetic and copies ran while one was open for 3% -> 3% of each run, Pallas kernels for 17% -> 19%
where the time goes in v14:
time: 151 us; the launch traced here: 150 us
  Pallas kernels  49.7 us (33%)
  waiting for transfers between devices  40.7 us (27%)
  starting transfers between devices  28.2 us (19%)
  blocking collectives  21.8 us (14%)
  local copies, waits for them, and re-layouts  4.67 us (3%)
  matrix products  3.85 us (3%)
    pallas_call x31, Pallas kernels, call(): pl.pallas_call(functools.partial(kernel, **static), out_shape=[jax.ShapeD...  48.6 us
    ppermute x26, waiting for transfers between devices, swap(): lax.ppermute(array_in, axis_name, [(i, i ^ bit) for i in range(size)])  37.3 us
    ppermute x26, starting transfers between devices, swap(): lax.ppermute(array_in, axis_name, [(i, i ^ bit) for i in range(size)])  18.7 us
    all_to_all x1, blocking collectives, per_device(): got = lax.all_to_all(got, 'dp', split_axis=0, concat_axis=0, tiled=True)  12.2 us
    ppermute x8, starting transfers between devices, swap_both(): return lax.ppermute(array_in, ('dp', 'mp'), pairs)  9.52 us
    all_to_all x1, blocking collectives, per_device(): back = lax.all_to_all(back, 'dp', split_axis=0, concat_axis=0, tiled=True)  9.51 us
    dot_general x2, matrix products, mm_tn(): lax.dot_general(a, b, (((0,), (0,)), ((), ())), preferred_element_type=f32)  3.85 us
    unnamed x20, local copies, waits for them, and re-layouts  3.73 us
  transfers between devices with their start and end apart: 34, of which 18 were waited for; matrix products, arithmetic and copies ran while one was open for 3% of the time, Pallas kernels for 19%

profile of v14, /device:TPU:0, one launch (start us, length us, event | category | flops | bytes accessed | tf_op | source)
XLA Modules:
  0.0 150.2 jit_solution(7943461658107983416)
XLA Ops:
  1.6 4.1 %collective-permute-start = (bf16[1,3,96,128]{3,2,1,0:T(8,128)(2,1)S(1)}, bf16[1,3,96,128]{3,2,1,0:T(8,128)(2,1)S(1)}, u32[]{:S(2)}, u32[]{:S(2)}) collective-permute-start(bf16[1,3,96,128]{3,2,1,0:T(8,128)(2,1)S(1)} %slice_bitcast_fusion.5.a_ref), channel_id=1, source_target_pairs={{0,16},{4,20},{8,24},{12,28},{16,0},{20,4},{24,8},{28,12},{1,17},{... | collective-permute-start | bytes 221192 | tf_op jit(solution)/shard_map/ppermute | solution.py:24
  10.5 1.6 %collective-permute-start.1 = (bf16[2,3,96,128]{3,2,1,0:T(8,128)(2,1)S(1)}, bf16[2,3,96,128]{3,2,1,0:T(8,128)(2,1)S(1)}, u32[]{:S(2)}, u32[]{:S(2)}) collective-permute-start(bf16[2,3,96,128]{3,2,1,0:T(8,128)(2,1)S(1)} %join.9.a_ref), channel_id=1, source_target_pairs={{0,8},{4,12},{8,0},{12,4},{16,24},{20,28},{24,16},{28,20},{1,9},{5... | collective-permute-start | bytes 442376 | tf_op jit(solution)/shard_map/ppermute | solution.py:24
  12.1 3.7 %collective-permute-done.1.b_ref = bf16[2,3,96,128]{3,2,1,0:T(8,128)(2,1)S(1)} collective-permute-done((bf16[2,3,96,128]{3,2,1,0:T(8,128)(2,1)S(1)}, bf16[2,3,96,128]{3,2,1,0:T(8,128)(2,1)S(1)}, u32[]{:S(2)}, u32[]{:S(2)}) %collective-permute-start.1) | collective-permute-done | bytes 147488 | tf_op jit(solution)/shard_map/ppermute | solution.py:24
  20.4 3.6 %collective-permute-done.3.b_ref = bf16[1,96,128]{2,1,0:T(8,128)(2,1)S(1)} collective-permute-done((bf16[1,96,128]{2,1,0:T(8,128)(2,1)S(1)}, bf16[1,96,128]{2,1,0:T(8,128)(2,1)S(1)}, u32[]{:S(2)}, u32[]{:S(2)}) %collective-permute-start.3) | collective-permute-done | bytes 24608 | tf_op jit(solution)/shard_map/ppermute | solution.py:24
  25.6 1.6 %collective-permute-start.8 = (bf16[2,96,384]{2,1,0:T(8,128)(2,1)S(1)}, bf16[2,96,384]{2,1,0:T(8,128)(2,1)S(1)}, u32[]{:S(2)}, u32[]{:S(2)}) collective-permute-start(bf16[2,96,384]{2,1,0:T(8,128)(2,1)S(1)} %join.15.a_ref), channel_id=1, source_target_pairs={{0,8},{4,12},{8,0},{12,4},{16,24},{20,28},{24,16},{28,20},{1,9},{5... | collective-permute-start | bytes 442376 | tf_op jit(solution)/shard_map/ppermute | solution.py:24
  27.7 3.6 %collective-permute-done.6.b_ref = bf16[2,96,128]{2,1,0:T(8,128)(2,1)S(1)} collective-permute-done((bf16[2,96,128]{2,1,0:T(8,128)(2,1)S(1)}, bf16[2,96,128]{2,1,0:T(8,128)(2,1)S(1)}, u32[]{:S(2)}, u32[]{:S(2)}) %collective-permute-start.6) | collective-permute-done | bytes 49184 | tf_op jit(solution)/shard_map/ppermute | solution.py:24
  33.6 2.5 %collective-permute-done.7.b_ref = bf16[4,96,128]{2,1,0:T(8,128)(2,1)S(1)} collective-permute-done((bf16[4,96,128]{2,1,0:T(8,128)(2,1)S(1)}, bf16[4,96,128]{2,1,0:T(8,128)(2,1)S(1)}, u32[]{:S(2)}, u32[]{:S(2)}) %collective-permute-start.7) | collective-permute-done | bytes 98336 | tf_op jit(solution)/shard_map/ppermute | solution.py:24
  41.2 6.2 %front_pair.1 = (bf16[4,768,384]{2,1,0:T(8,128)(2,1)S(1)}, bf16[4,624,384]{2,1,0:T(8,128)(2,1)S(1)}, bf16[4,3,2,208,208]{4,3,2,1,0:T(8,128)(2,1)S(1)}, bf16[4,624,128]{2,1,0:T(8,128)(2,1)S(1)}) custom-call(s32[3]{0:T(128)S(1)} %pad_add_fusion.me_ref, bf16[624,768]{1,0:T(8,128)(2,1)S(1)} %get-tuple-element.111.h_ref, s32[12,200]{1,0:T(8,128)S(1)} %copy-done.6, ...), custom_call_target="tpu_custom_call" | custom-call | flops 11000000512 | bytes 3327372 | tf_op jit(solution)/shard_map/front_pair/pallas_call | solution.py:562
  47.4 1.8 %collective-permute-done.10.refs_1_ = bf16[2,4,96,384]{3,2,1,0:T(8,128)(2,1)S(1)} collective-permute-done((bf16[2,4,96,384]{3,2,1,0:T(8,128)(2,1)S(1)}, bf16[2,4,96,384]{3,2,1,0:T(8,128)(2,1)S(1)}, u32[]{:S(2)}, u32[]{:S(2)}) %collective-permute-start.10) | collective-permute-done | bytes 589856 | tf_op jit(solution)/shard_map/ppermute | solution.py:33
  49.2 3.5 %front_last.2 = (bf16[2,768,256]{2,1,0:T(8,128)(2,1)S(1)}, bf16[2,624,256]{2,1,0:T(8,128)(2,1)S(1)}, bf16[2,3,208,208]{3,2,1,0:T(8,128)(2,1)S(1)}, bf16[624,512]...) custom-call(s32[3]{0:T(128)S(1)} %pad_add_fusion.me_ref, ...), custom_call_target="tpu_custom_call" | custom-call | flops 3300000000 | bytes 2786700 | tf_op jit(solution)/shard_map/front_last/pallas_call | solution.py:562
  52.8 3.5 %front_last.3 = (bf16[2,768,256]{2,1,0:T(8,128)(2,1)S(1)}, bf16[2,624,256]{2,1,0:T(8,128)(2,1)S(1)}, bf16[2,3,208,208]{3,2,1,0:T(8,128)(2,1)S(1)}, bf16[624,512]...) custom-call(s32[3]{0:T(128)S(1)} %pad_add_fusion.me_ref, ...), custom_call_target="tpu_custom_call" | custom-call | flops 3300000000 | bytes 4703628 | tf_op jit(solution)/shard_map/front_last/pallas_call | solution.py:562
  56.3 2.7 %route.1 = (f32[624,768]{1,0:T(8,128)S(1)}, bf16[624,768]{1,0:T(8,128)(2,1)S(1)}, f32[2,3,8,208]{3,2,1,0:T(8,128)S(1)}, bf16[64,768]{1,0:T(8,128)(2,1)S(1)}, f32[3,1,128]{2,1,0:T(1,128)S(1)}) custom-call(s32[3]{0:T(128)S(1)} %pad_add_fusion.me_ref, bf16[3,200,768]{2,1,0:T(8,128)(2,1)S(1)} %bitcast.78, f32[624,768]{1,0:T(8,128)S(1)} %get-tuple-element.118.br_ref, ...), custom_call_target="tpu_custom_call" | custom-call | flops 2200000000 | bytes 4162956 | tf_op jit(solution)/shard_map/route/pallas_call | solution.py:562
  59.0 12.2 %all_to_all.10 = bf16[8,8,768]{2,1,0:T(8,128)(2,1)S(1)} all-to-all(bf16[8,8,768]{2,1,0:T(8,128)(2,1)S(1)} %bitcast.88), channel_id=1, replica_groups=mesh['dp'=8,'mp'=4] {'dp'}, dimensions={0} | all-to-all | bytes 196608 | tf_op jit(solution)/shard_map/all_to_all | solution.py:742
  71.3 4.5 %collective-permute-done.15 = bf16[1,8,8,768]{3,2,1,0:T(8,128)(2,1)S(1)} collective-permute-done((bf16[1,8,8,768]{3,2,1,0:T(8,128)(2,1)S(1)}, bf16[1,8,8,768]{3,2,1,0:T(8,128)(2,1)S(1)}, u32[]{:S(2)}, u32[]{:S(2)}) %collective-permute-start.15) | collective-permute-done | bytes 98336 | tf_op jit(solution)/shard_map/ppermute | solution.py:24
  77.5 1.7 %expert.1 = (bf16[256,768]{1,0:T(8,128)(2,1)S(1)}, bf16[256,768]{1,0:T(8,128)(2,1)S(1)}, bf16[256,768]{1,0:T(8,128)(2,1)S(1)}, bf16[256,768]{1,0:T(8,128)(2,1)S(1)}) custom-call(bf16[256,768]{1,0:T(8,128)(2,1)S(1)} %bitcast.75, bf16[768,768]{1,0:T(8,128)(2,1)S(1)} %bitcast.95, bf16[768,768]{1,0:T(8,128)(2,1)S(1)} %bitcast.96), custom_call_target="tpu_custom_call" | custom-call | flops 2200000000 | bytes 2752512 | tf_op jit(solution)/shard_map/expert/pallas_call | solution.py:562
  81.0 4.7 %collective-permute-done.18 = bf16[1,1,8,8,768]{4,3,2,1,0:T(8,128)(2,1)S(1)} collective-permute-done((bf16[1,1,8,8,768]{4,3,2,1,0:T(8,128)(2,1)S(1)}, bf16[1,1,8,8,768]{4,3,2,1,0:T(8,128)(2,1)S(1)}, u32[]{:S(2)}, u32[]{:S(2)}) %collective-permute-start.18) | collective-permute-done | bytes 98336 | tf_op jit(solution)/shard_map/ppermute | solution.py:24
  85.7 9.5 %all_to_all.11 = bf16[8,8,768]{2,1,0:T(8,128)(2,1)S(1)} all-to-all(bf16[8,8,768]{2,1,0:T(8,128)(2,1)S(1)} %fusion.5), channel_id=1, replica_groups=mesh['dp'=8,'mp'=4] {'dp'}, dimensions={0} | all-to-all | bytes 196608 | tf_op jit(solution)/shard_map/all_to_all | solution.py:762
  95.3 3.9 %mix.1 = (bf16[3,200,768]{2,1,0:T(8,128)(2,1)}, f32[624,768]{1,0:T(8,128)S(1)}, bf16[624,768]{1,0:T(8,128)(2,1)S(1)}, bf16[768,624]{1,0:T(8,128)(2,1)S(1)}, f32[13,768]{1,0:T(8,128)S(1)}) custom-call(s32[3]{0:T(128)S(1)} %pad_add_fusion.me_ref, f32[624,768]{1,0:T(8,128)S(1)} %get-tuple-element.120.res_ref, bf16[624,768]{1,0:T(8,128)(2,1)S(1)} %get-tuple-element.121.h_ref, ...), custom_call_target="tpu_custom_call" | custom-call | flops 5500000256 | bytes 4315020 | tf_op jit(solution)/shard_map/mix/pallas_call | solution.py:562
  99.2 3.6 %back.4 = (bf16[2,4,96,768]{3,2,1,0:T(8,128)(2,1)S(1)}, bf16[624,640]{1,0:T(8,128)(2,1)S(1)}) custom-call(s32[3]{0:T(128)S(1)} %pad_add_fusion.me_ref, bf16[624,768]{1,0:T(8,128)(2,1)S(1)} %get-tuple-element.156.gb_ref, bf16[768,624]{1,0:T(8,128)(2,1)S(1)} %get-tuple-element.129.gbt_ref, bf16[768,624]{1,0:T(8,128)(2,1)S(1)} %get-tuple-element.130.ht_ref, ...), custom_call_target="tpu_custom_call" | custom-call | flops 8800000000 | bytes 9452556 | tf_op jit(solution)/shard_map/back/pallas_call | solution.py:562
  102.9 3.6 %back.5 = (bf16[2,4,96,768]{3,2,1,0:T(8,128)(2,1)S(1)}, bf16[624,640]{1,0:T(8,128)(2,1)S(1)}) custom-call(s32[3]{0:T(128)S(1)} %pad_add_fusion.me_ref, bf16[624,768]{1,0:T(8,128)(2,1)S(1)} %get-tuple-element.156.gb_ref, bf16[768,624]{1,0:T(8,128)(2,1)S(1)} %get-tuple-element.129.gbt_ref, bf16[768,624]{1,0:T(8,128)(2,1)S(1)} %get-tuple-element.130.ht_ref, ...), custom_call_target="tpu_custom_call" | custom-call | flops 8800000000 | bytes 9452556 | tf_op jit(solution)/shard_map/back/pallas_call | solution.py:562
  106.8 3.6 %back.6 = (bf16[2,4,96,768]{3,2,1,0:T(8,128)(2,1)S(1)}, bf16[624,640]{1,0:T(8,128)(2,1)S(1)}) custom-call(s32[3]{0:T(128)S(1)} %pad_add_fusion.me_ref, bf16[624,768]{1,0:T(8,128)(2,1)S(1)} %get-tuple-element.156.gb_ref, bf16[768,624]{1,0:T(8,128)(2,1)S(1)} %get-tuple-element.129.gbt_ref, bf16[768,624]{1,0:T(8,128)(2,1)S(1)} %get-tuple-element.130.ht_ref, ...), custom_call_target="tpu_custom_call" | custom-call | flops 8800000000 | bytes 9452556 | tf_op jit(solution)/shard_map/back/pallas_call | solution.py:562
  111.3 3.9 %back.7 = (bf16[2,4,96,768]{3,2,1,0:T(8,128)(2,1)S(1)}, bf16[624,640]{1,0:T(8,128)(2,1)S(1)}) custom-call(s32[3]{0:T(128)S(1)} %pad_add_fusion.me_ref, bf16[624,768]{1,0:T(8,128)(2,1)S(1)} %get-tuple-element.156.gb_ref, bf16[768,624]{1,0:T(8,128)(2,1)S(1)} %get-tuple-element.129.gbt_ref, bf16[768,624]{1,0:T(8,128)(2,1)S(1)} %get-tuple-element.130.ht_ref, ...), custom_call_target="tpu_custom_call" | custom-call | flops 8800000000 | bytes 9452556 | tf_op jit(solution)/shard_map/back/pallas_call | solution.py:562
  116.0 1.8 %collective-permute-start.22 = (bf16[4,96,768]{2,1,0:T(8,128)(2,1)S(1)}, bf16[4,96,768]{2,1,0:T(8,128)(2,1)S(1)}, u32[]{:S(2)}, u32[]{:S(2)}) collective-permute-start(bf16[4,96,768]{2,1,0:T(8,128)(2,1)S(1)} %get-tuple-element.165), channel_id=1, source_target_pairs={{0,2},{1,5},{2,0},{3,7},{4,6},{5,1},{6,4},{7,3},{8,10},{9,13},{10,... | collective-permute-start | bytes 1769480 | tf_op jit(solution)/shard_map/ppermute | solution.py:33
  117.8 3.7 %input.1.gh_ref = f32[624,768]{1,0:T(8,128)S(1)} custom-call(s32[3]{0:T(128)S(1)} %pad_add_fusion.me_ref, bf16[4,768,384]{2,1,0:T(8,128)(2,1)S(1)} %get-tuple-element.148.w_a, bf16[2,768,256]{2,1,0:T(8,128)(2,1)S(1)} %get-tuple-element.149.w_own, bf16[2,768,256]{2,1,0:T(8,128)(2,1)S(1)} %get-tuple-element.150.w_other, ...), custom_call_target="tpu_custom_call" | custom-call | flops 4400000000 | bytes 7127052 | tf_op jit(solution)/shard_map/input/pallas_call | solution.py:562
  122.7 1.7 %collective-permute-start.31 = (bf16[4,96,384]{2,1,0:T(8,128)(2,1)S(1)}, bf16[4,96,384]{2,1,0:T(8,128)(2,1)S(1)}, u32[]{:S(2)}, u32[]{:S(2)}) collective-permute-start(bf16[4,96,384]{2,1,0:T(8,128)(2,1)S(1)} %get-tuple-element.177), channel_id=1, source_target_pairs={{0,4},{1,3},{2,6},{3,1},{4,0},{5,7},{6,2},{7,5},{8,12},{9,11},{10,... | collective-permute-start | bytes 884744 | tf_op jit(solution)/shard_map/ppermute | solution.py:33
  124.4 2.7 %last.1 = (f32[3,200,768]{2,1,0:T(8,128)}, f32[13,768]{1,0:T(8,128)S(1)}) custom-call(bf16[3,200,768]{2,1,0:T(8,128)(2,1)S(1)} %bitcast.79, f32[624,768]{1,0:T(8,128)S(1)} %get-tuple-element.127.gres_ref, f32[624,768]{1,0:T(8,128)S(1)} %input.1.gh_ref, f32[128,768]{1,0:T(8,128)S(1)} %get-tuple-element.119.ex_ref, f32[13,768]{1,0:T(8,128)S(1)} %get-tuple-element.159.part_ref), custom_call_target="tpu_custom_call" | custom-call | flops 110000000 | bytes 5188608 | tf_op jit(solution)/shard_map/last/pallas_call | solution.py:562
  127.5 4.5 %collective-permute-done.25 = f32[13,768]{1,0:T(8,128)S(1)} collective-permute-done((f32[13,768]{1,0:T(8,128)S(1)}, f32[13,768]{1,0:T(8,128)S(1)}, u32[]{:S(2)}, u32[]{:S(2)}) %collective-permute-start.25) | collective-permute-done | bytes 39968 | tf_op jit(solution)/shard_map/ppermute | solution.py:24
  132.3 2.1 %collective-permute-start.24 = (bf16[2,96,384]{2,1,0:T(8,128)(2,1)S(1)}, bf16[2,96,384]{2,1,0:T(8,128)(2,1)S(1)}, u32[]{:S(2)}, u32[]{:S(2)}) collective-permute-start(bf16[2,96,384]{2,1,0:T(8,128)(2,1)S(1)} %get-tuple-element.169), channel_id=1, source_target_pairs={{0,8},{4,12},{8,0},{12,4},{16,24},{20,28},{24,16},{28,20},{1,9},{5... | collective-permute-start | bytes 442376 | tf_op jit(solution)/shard_map/ppermute | solution.py:24
  134.6 1.9 %convolution_bitcast_fusion.1 = f32[1,768,768]{2,1,0:T(8,128)} fusion(bf16[256,768]{1,0:T(8,128)(2,1)S(1)} %bitcast.76, bf16[256,768]{1,0:T(8,128)(2,1)S(1)} %get-tuple-element.186), kind=kOutput, calls=%fused_computation.1 | convolution fusion | flops 301989888 | bytes 3145728 | tf_op jit(solution)/shard_map/dot_general | solution.py:86
  136.6 2.8 %collective-permute-done.24.refs_1_ = bf16[2,96,384]{2,1,0:T(8,128)(2,1)S(1)} collective-permute-done((bf16[2,96,384]{2,1,0:T(8,128)(2,1)S(1)}, bf16[2,96,384]{2,1,0:T(8,128)(2,1)S(1)}, u32[]{:S(2)}, u32[]{:S(2)}) %collective-permute-start.24) | collective-permute-done | bytes 147488 | tf_op jit(solution)/shard_map/ppermute | solution.py:24
  143.7 1.9 %convolution_bitcast_fusion = f32[1,768,768]{2,1,0:T(8,128)} fusion(bf16[256,768]{1,0:T(8,128)(2,1)S(1)} %get-tuple-element.187, bf16[256,768]{1,0:T(8,128)(2,1)S(1)} %get-tuple-element.188), kind=kOutput, calls=%fused_computation | convolution fusion | flops 301989888 | bytes 3145728 | tf_op jit(solution)/shard_map/dot_general | solution.py:86
  145.6 2.0 %collective-permute-done.28 = f32[13,768]{1,0:T(8,128)S(1)} collective-permute-done((f32[13,768]{1,0:T(8,128)S(1)}, f32[13,768]{1,0:T(8,128)S(1)}, u32[]{:S(2)}, u32[]{:S(2)}) %collective-permute-start.28) | collective-permute-done | bytes 39968 | tf_op jit(solution)/shard_map/ppermute | solution.py:24
  (106 shorter events, 34.1 us)
Async XLA Ops:
  1.6 8.8 %collective-permute-start = (bf16[1,3,96,128]{3,2,1,0:T(8,128)(2,1)S(1)}, bf16[1,3,96,128]{3,2,1,0:T(8,128)(2,1)S(1)}, u32[]{:S(2)}, u32[]{:S(2)}) collective-permute-start(bf16[1,3,96,128]{3,2,1,0:T(8,128)(2,1)S(1)} %slice_bitcast_fusion.5.a_ref), channel_id=1, source_target_pairs={{0,16},{4,20},{8,24},{12,28},{16,0},{20,4},{24,8},{28,12},{1,17},{... | collective-permute-start | bytes 221192 | tf_op jit(solution)/shard_map/ppermute | solution.py:24
  10.5 5.4 %collective-permute-start.1 = (bf16[2,3,96,128]{3,2,1,0:T(8,128)(2,1)S(1)}, bf16[2,3,96,128]{3,2,1,0:T(8,128)(2,1)S(1)}, u32[]{:S(2)}, u32[]{:S(2)}) collective-permute-start(bf16[2,3,96,128]{3,2,1,0:T(8,128)(2,1)S(1)} %join.9.a_ref), channel_id=1, source_target_pairs={{0,8},{4,12},{8,0},{12,4},{16,24},{20,28},{24,16},{28,20},{1,9},{5... | collective-permute-start | bytes 442376 | tf_op jit(solution)/shard_map/ppermute | solution.py:24
  15.9 8.2 %collective-permute-start.2 = (bf16[4,3,96,128]{3,2,1,0:T(8,128)(2,1)S(1)}, bf16[4,3,96,128]{3,2,1,0:T(8,128)(2,1)S(1)}, u32[]{:S(2)}, u32[]{:S(2)}) collective-permute-start(bf16[4,3,96,128]{3,2,1,0:T(8,128)(2,1)S(1)} %join.10.a_ref), channel_id=1, source_target_pairs={{0,4},{1,3},{2,6},{3,1},{4,0},{5,7},{6,2},{7,5},{8,12},{9,11},{10,... | collective-permute-start | bytes 884744 | tf_op jit(solution)/shard_map/ppermute | solution.py:33
  17.5 6.6 %collective-permute-start.4 = (bf16[1,96,384]{2,1,0:T(8,128)(2,1)S(1)}, bf16[1,96,384]{2,1,0:T(8,128)(2,1)S(1)}, u32[]{:S(2)}, u32[]{:S(2)}) collective-permute-start(bf16[1,96,384]{2,1,0:T(8,128)(2,1)S(1)} %bitcast.89), channel_id=1, source_target_pairs={{0,16},{4,20},{8,24},{12,28},{16,0},{20,4},{24,8},{28,12},{1,17},{... | collective-permute-start | bytes 221192 | tf_op jit(solution)/shard_map/ppermute | solution.py:24
  19.1 4.9 %collective-permute-start.3 = (bf16[1,96,128]{2,1,0:T(8,128)(2,1)S(1)}, bf16[1,96,128]{2,1,0:T(8,128)(2,1)S(1)}, u32[]{:S(2)}, u32[]{:S(2)}) collective-permute-start(bf16[1,96,128]{2,1,0:T(8,128)(2,1)S(1)} %bitcast.93), channel_id=1, source_target_pairs={{0,16},{4,20},{8,24},{12,28},{16,0},{20,4},{24,8},{28,12},{1,17},{... | collective-permute-start | bytes 73736 | tf_op jit(solution)/shard_map/ppermute | solution.py:24
  24.1 15.1 %collective-permute-start.5 = (bf16[2,4,3,96,128]{4,3,2,1,0:T(8,128)(2,1)S(1)}, bf16[2,4,3,96,128]{4,3,2,1,0:T(8,128)(2,1)S(1)}, u32[]{:S(2)}, u32[]{:S(2)}) collective-permute-start(bf16[2,4,3,96,128]{4,3,2,1,0:T(8,128)(2,1)S(1)} %bitcast.80), channel_id=1, source_target_pairs={{0,2},{1,5},{2,0},{3,7},{4,6},{5,1},{6,4},{7,3},{8,10},{9,13},{10,... | collective-permute-start | bytes 1769480 | tf_op jit(solution)/shard_map/ppermute | solution.py:33
  25.6 6.4 %collective-permute-start.8 = (bf16[2,96,384]{2,1,0:T(8,128)(2,1)S(1)}, bf16[2,96,384]{2,1,0:T(8,128)(2,1)S(1)}, u32[]{:S(2)}, u32[]{:S(2)}) collective-permute-start(bf16[2,96,384]{2,1,0:T(8,128)(2,1)S(1)} %join.15.a_ref), channel_id=1, source_target_pairs={{0,8},{4,12},{8,0},{12,4},{16,24},{20,28},{24,16},{28,20},{1,9},{5... | collective-permute-start | bytes 442376 | tf_op jit(solution)/shard_map/ppermute | solution.py:24
  27.3 4.1 %collective-permute-start.6 = (bf16[2,96,128]{2,1,0:T(8,128)(2,1)S(1)}, bf16[2,96,128]{2,1,0:T(8,128)(2,1)S(1)}, u32[]{:S(2)}, u32[]{:S(2)}) collective-permute-start(bf16[2,96,128]{2,1,0:T(8,128)(2,1)S(1)} %join.11.a_ref), channel_id=1, source_target_pairs={{0,8},{4,12},{8,0},{12,4},{16,24},{20,28},{24,16},{28,20},{1,9},{5... | collective-permute-start | bytes 147464 | tf_op jit(solution)/shard_map/ppermute | solution.py:24
  31.4 4.7 %collective-permute-start.7 = (bf16[4,96,128]{2,1,0:T(8,128)(2,1)S(1)}, bf16[4,96,128]{2,1,0:T(8,128)(2,1)S(1)}, u32[]{:S(2)}, u32[]{:S(2)}) collective-permute-start(bf16[4,96,128]{2,1,0:T(8,128)(2,1)S(1)} %join.13.a_ref), channel_id=1, source_target_pairs={{0,4},{4,0},{8,12},{12,8},{16,20},{20,16},{24,28},{28,24},{1,5},{5... | collective-permute-start | bytes 294920 | tf_op jit(solution)/shard_map/ppermute | solution.py:24
  32.0 7.2 %collective-permute-start.9 = (bf16[4,96,384]{2,1,0:T(8,128)(2,1)S(1)}, bf16[4,96,384]{2,1,0:T(8,128)(2,1)S(1)}, u32[]{:S(2)}, u32[]{:S(2)}) collective-permute-start(bf16[4,96,384]{2,1,0:T(8,128)(2,1)S(1)} %join.16.a_ref), channel_id=1, source_target_pairs={{0,4},{1,3},{2,6},{3,1},{4,0},{5,7},{6,2},{7,5},{8,12},{9,11},{10,... | collective-permute-start | bytes 884744 | tf_op jit(solution)/shard_map/ppermute | solution.py:33
  33.6 7.1 %collective-permute-start.11 = (bf16[2,4,3,96,128]{4,3,2,1,0:T(8,128)(2,1)S(1)}, bf16[2,4,3,96,128]{4,3,2,1,0:T(8,128)(2,1)S(1)}, u32[]{:S(2)}, u32[]{:S(2)}) collective-permute-start(bf16[2,4,3,96,128]{4,3,2,1,0:T(8,128)(2,1)S(1)} %bitcast.81), channel_id=1, source_target_pairs={{0,1},{1,0},{2,3},{3,2},{4,5},{5,4},{6,7},{7,6},{8,9},{9,8},{10,11... | collective-permute-start | bytes 1769480 | tf_op jit(solution)/shard_map/ppermute | solution.py:24
  39.2 2.0 %collective-permute-start.12 = (bf16[2,4,3,96,128]{4,3,2,1,0:T(8,128)(2,1)S(1)}, bf16[2,4,3,96,128]{4,3,2,1,0:T(8,128)(2,1)S(1)}, u32[]{:S(2)}, u32[]{:S(2)}) collective-permute-start(bf16[2,4,3,96,128]{4,3,2,1,0:T(8,128)(2,1)S(1)} %collective-permute-done.5.refs_1_), channel_id=1, source_target_pairs={{0,1},{1,0},{2,3},{3,2},{4,5},{5,4},{6,7},{7,6},{8,9},{9,8},{10,11... | collective-permute-start | bytes 1769480 | tf_op jit(solution)/shard_map/ppermute | solution.py:24
  39.3 9.9 %collective-permute-start.10 = (bf16[2,4,96,384]{3,2,1,0:T(8,128)(2,1)S(1)}, bf16[2,4,96,384]{3,2,1,0:T(8,128)(2,1)S(1)}, u32[]{:S(2)}, u32[]{:S(2)}) collective-permute-start(bf16[2,4,96,384]{3,2,1,0:T(8,128)(2,1)S(1)} %bitcast.83), channel_id=1, source_target_pairs={{0,2},{1,5},{2,0},{3,7},{4,6},{5,1},{6,4},{7,3},{8,10},{9,13},{10,... | collective-permute-start | bytes 1769480 | tf_op jit(solution)/shard_map/ppermute | solution.py:33
  40.0 12.8 %collective-permute-start.13 = (bf16[2,4,96,384]{3,2,1,0:T(8,128)(2,1)S(1)}, bf16[2,4,96,384]{3,2,1,0:T(8,128)(2,1)S(1)}, u32[]{:S(2)}, u32[]{:S(2)}) collective-permute-start(bf16[2,4,96,384]{3,2,1,0:T(8,128)(2,1)S(1)} %bitcast.84), channel_id=1, source_target_pairs={{0,1},{1,0},{2,3},{3,2},{4,5},{5,4},{6,7},{7,6},{8,9},{9,8},{10,11... | collective-permute-start | bytes 1769480 | tf_op jit(solution)/shard_map/ppermute | solution.py:24
  49.2 3.5 %collective-permute-start.14 = (bf16[2,4,96,384]{3,2,1,0:T(8,128)(2,1)S(1)}, bf16[2,4,96,384]{3,2,1,0:T(8,128)(2,1)S(1)}, u32[]{:S(2)}, u32[]{:S(2)}) collective-permute-start(bf16[2,4,96,384]{3,2,1,0:T(8,128)(2,1)S(1)} %collective-permute-done.10.refs_1_), channel_id=1, source_target_pairs={{0,1},{1,0},{2,3},{3,2},{4,5},{5,4},{6,7},{7,6},{8,9},{9,8},{10,11... | collective-permute-start | bytes 1769480 | tf_op jit(solution)/shard_map/ppermute | solution.py:24
  71.2 4.6 %collective-permute-start.15 = (bf16[1,8,8,768]{3,2,1,0:T(8,128)(2,1)S(1)}, bf16[1,8,8,768]{3,2,1,0:T(8,128)(2,1)S(1)}, u32[]{:S(2)}, u32[]{:S(2)}) collective-permute-start(bf16[1,8,8,768]{3,2,1,0:T(8,128)(2,1)S(1)} %bitcast.109), channel_id=1, source_target_pairs={{0,2},{1,3},{2,0},{3,1},{4,6},{5,7},{6,4},{7,5},{8,10},{9,11},{10,... | collective-permute-start | bytes 294920 | tf_op jit(solution)/shard_map/ppermute | solution.py:24
  75.9 1.5 %collective-permute-start.16 = (bf16[2,8,8,768]{3,2,1,0:T(8,128)(2,1)S(1)}, bf16[2,8,8,768]{3,2,1,0:T(8,128)(2,1)S(1)}, u32[]{:S(2)}, u32[]{:S(2)}) collective-permute-start(bf16[2,8,8,768]{3,2,1,0:T(8,128)(2,1)S(1)} %get-tuple-element.191), channel_id=1, source_target_pairs={{0,1},{1,0},{2,3},{3,2},{4,5},{5,4},{6,7},{7,6},{8,9},{9,8},{10,11... | collective-permute-start | bytes 589832 | tf_op jit(solution)/shard_map/ppermute | solution.py:24
  80.8 4.9 %collective-permute-start.18 = (bf16[1,1,8,8,768]{4,3,2,1,0:T(8,128)(2,1)S(1)}, bf16[1,1,8,8,768]{4,3,2,1,0:T(8,128)(2,1)S(1)}, u32[]{:S(2)}, u32[]{:S(2)}) collective-permute-start(bf16[1,1,8,8,768]{4,3,2,1,0:T(8,128)(2,1)S(1)} %slice_bitcast_fusion.2), channel_id=1, source_target_pairs={{0,2},{1,3},{2,0},{3,1},{4,6},{5,7},{6,4},{7,5},{8,10},{9,11},{10,... | collective-permute-start | bytes 294920 | tf_op jit(solution)/shard_map/ppermute | solution.py:24
  102.8 3.7 %collective-permute-start.19 = (bf16[2,4,96,768]{3,2,1,0:T(8,128)(2,1)S(1)}, bf16[2,4,96,768]{3,2,1,0:T(8,128)(2,1)S(1)}, u32[]{:S(2)}, u32[]{:S(2)}) collective-permute-start(bf16[2,4,96,768]{3,2,1,0:T(8,128)(2,1)S(1)} %get-tuple-element.144), channel_id=1, source_target_pairs={{0,1},{1,0},{2,3},{3,2},{4,5},{5,4},{6,7},{7,6},{8,9},{9,8},{10,11... | collective-permute-start | bytes 3538952 | tf_op jit(solution)/shard_map/ppermute | solution.py:24
  110.4 4.7 %collective-permute-start.21 = (bf16[2,4,96,768]{3,2,1,0:T(8,128)(2,1)S(1)}, bf16[2,4,96,768]{3,2,1,0:T(8,128)(2,1)S(1)}, u32[]{:S(2)}, u32[]{:S(2)}) collective-permute-start(bf16[2,4,96,768]{3,2,1,0:T(8,128)(2,1)S(1)} %get-tuple-element.163), channel_id=1, source_target_pairs={{0,1},{1,0},{2,3},{3,2},{4,5},{5,4},{6,7},{7,6},{8,9},{9,8},{10,11... | collective-permute-start | bytes 3538952 | tf_op jit(solution)/shard_map/ppermute | solution.py:24
  111.0 10.6 %collective-permute-start.20 = (bf16[4,96,768]{2,1,0:T(8,128)(2,1)S(1)}, bf16[4,96,768]{2,1,0:T(8,128)(2,1)S(1)}, u32[]{:S(2)}, u32[]{:S(2)}) collective-permute-start(bf16[4,96,768]{2,1,0:T(8,128)(2,1)S(1)} %bitcast.99), channel_id=1, source_target_pairs={{0,2},{1,5},{2,0},{3,7},{4,6},{5,1},{6,4},{7,3},{8,10},{9,13},{10,... | collective-permute-start | bytes 1769480 | tf_op jit(solution)/shard_map/ppermute | solution.py:33
  116.0 16.1 %collective-permute-start.22 = (bf16[4,96,768]{2,1,0:T(8,128)(2,1)S(1)}, bf16[4,96,768]{2,1,0:T(8,128)(2,1)S(1)}, u32[]{:S(2)}, u32[]{:S(2)}) collective-permute-start(bf16[4,96,768]{2,1,0:T(8,128)(2,1)S(1)} %get-tuple-element.165), channel_id=1, source_target_pairs={{0,2},{1,5},{2,0},{3,7},{4,6},{5,1},{6,4},{7,3},{8,10},{9,13},{10,... | collective-permute-start | bytes 1769480 | tf_op jit(solution)/shard_map/ppermute | solution.py:33
  122.3 9.9 %collective-permute-start.23 = (bf16[4,96,384]{2,1,0:T(8,128)(2,1)S(1)}, bf16[4,96,384]{2,1,0:T(8,128)(2,1)S(1)}, u32[]{:S(2)}, u32[]{:S(2)}) collective-permute-start(bf16[4,96,384]{2,1,0:T(8,128)(2,1)S(1)} %get-tuple-element.168), channel_id=1, source_target_pairs={{0,4},{1,3},{2,6},{3,1},{4,0},{5,7},{6,2},{7,5},{8,12},{9,11},{10,... | collective-permute-start | bytes 884744 | tf_op jit(solution)/shard_map/ppermute | solution.py:33
  122.7 11.7 %collective-permute-start.31 = (bf16[4,96,384]{2,1,0:T(8,128)(2,1)S(1)}, bf16[4,96,384]{2,1,0:T(8,128)(2,1)S(1)}, u32[]{:S(2)}, u32[]{:S(2)}) collective-permute-start(bf16[4,96,384]{2,1,0:T(8,128)(2,1)S(1)} %get-tuple-element.177), channel_id=1, source_target_pairs={{0,4},{1,3},{2,6},{3,1},{4,0},{5,7},{6,2},{7,5},{8,12},{9,11},{10,... | collective-permute-start | bytes 884744 | tf_op jit(solution)/shard_map/ppermute | solution.py:33
  127.1 5.0 %collective-permute-start.25 = (f32[13,768]{1,0:T(8,128)S(1)}, f32[13,768]{1,0:T(8,128)S(1)}, u32[]{:S(2)}, u32[]{:S(2)}) collective-permute-start(f32[13,768]{1,0:T(8,128)S(1)} %get-tuple-element.170), channel_id=1, source_target_pairs={{0,16},{4,20},{8,24},{12,28},{16,0},{20,4},{24,8},{28,12},{1,17},{... | collective-permute-start | bytes 119816 | tf_op jit(solution)/shard_map/ppermute | solution.py:24
  132.1 4.5 %collective-permute-start.26 = (f32[13,768]{1,0:T(8,128)S(1)}, f32[13,768]{1,0:T(8,128)S(1)}, u32[]{:S(2)}, u32[]{:S(2)}) collective-permute-start(f32[13,768]{1,0:T(8,128)S(1)} %add.20), channel_id=1, source_target_pairs={{0,8},{4,12},{8,0},{12,4},{16,24},{20,28},{24,16},{28,20},{1,9},{5... | collective-permute-start | bytes 119816 | tf_op jit(solution)/shard_map/ppermute | solution.py:24
  132.3 7.1 %collective-permute-start.24 = (bf16[2,96,384]{2,1,0:T(8,128)(2,1)S(1)}, bf16[2,96,384]{2,1,0:T(8,128)(2,1)S(1)}, u32[]{:S(2)}, u32[]{:S(2)}) collective-permute-start(bf16[2,96,384]{2,1,0:T(8,128)(2,1)S(1)} %get-tuple-element.169), channel_id=1, source_target_pairs={{0,8},{4,12},{8,0},{12,4},{16,24},{20,28},{24,16},{28,20},{1,9},{5... | collective-permute-start | bytes 442376 | tf_op jit(solution)/shard_map/ppermute | solution.py:24
  134.5 7.2 %collective-permute-start.32 = (bf16[2,96,384]{2,1,0:T(8,128)(2,1)S(1)}, bf16[2,96,384]{2,1,0:T(8,128)(2,1)S(1)}, u32[]{:S(2)}, u32[]{:S(2)}) collective-permute-start(bf16[2,96,384]{2,1,0:T(8,128)(2,1)S(1)} %get-tuple-element.179), channel_id=1, source_target_pairs={{0,8},{4,12},{8,0},{12,4},{16,24},{20,28},{24,16},{28,20},{1,9},{5... | collective-permute-start | bytes 442376 | tf_op jit(solution)/shard_map/ppermute | solution.py:24
  139.4 4.1 %collective-permute-start.27 = (f32[13,768]{1,0:T(8,128)S(1)}, f32[13,768]{1,0:T(8,128)S(1)}, u32[]{:S(2)}, u32[]{:S(2)}) collective-permute-start(f32[13,768]{1,0:T(8,128)S(1)} %add.21), channel_id=1, source_target_pairs={{0,4},{4,0},{8,12},{12,8},{16,20},{20,16},{24,28},{28,24},{1,5},{5... | collective-permute-start | bytes 119816 | tf_op jit(solution)/shard_map/ppermute | solution.py:24
  140.2 7.5 %collective-permute-start.30 = (bf16[96,384]{1,0:T(8,128)(2,1)S(1)}, bf16[96,384]{1,0:T(8,128)(2,1)S(1)}, u32[]{:S(2)}, u32[]{:S(2)}) collective-permute-start(bf16[96,384]{1,0:T(8,128)(2,1)S(1)} %bitcast.100), channel_id=1, source_target_pairs={{0,16},{4,20},{8,24},{12,28},{16,0},{20,4},{24,8},{28,12},{1,17},{... | collective-permute-start | bytes 221192 | tf_op jit(solution)/shard_map/ppermute | solution.py:24
  141.8 6.1 %collective-permute-start.33 = (bf16[96,384]{1,0:T(8,128)(2,1)S(1)}, bf16[96,384]{1,0:T(8,128)(2,1)S(1)}, u32[]{:S(2)}, u32[]{:S(2)}) collective-permute-start(bf16[96,384]{1,0:T(8,128)(2,1)S(1)} %bitcast.101), channel_id=1, source_target_pairs={{0,16},{4,20},{8,24},{12,28},{16,0},{20,4},{24,8},{28,12},{1,17},{... | collective-permute-start | bytes 221192 | tf_op jit(solution)/shard_map/ppermute | solution.py:24
  143.5 4.1 %collective-permute-start.28 = (f32[13,768]{1,0:T(8,128)S(1)}, f32[13,768]{1,0:T(8,128)S(1)}, u32[]{:S(2)}, u32[]{:S(2)}) collective-permute-start(f32[13,768]{1,0:T(8,128)S(1)} %add.22), channel_id=1, source_target_pairs={{0,2},{1,3},{2,0},{3,1},{4,6},{5,7},{6,4},{7,5},{8,10},{9,11},{10,... | collective-permute-start | bytes 119816 | tf_op jit(solution)/shard_map/ppermute | solution.py:24
  (12 other events, 83.1 us)

commit v15 on v14

--- a/solution.py
+++ b/solution.py
@@ -622,15 +622,18 @@
             other = swap(first, "dp", dp, bit)
             if bit == stages[0]:
                 other, second, held_extra = lax.optimization_barrier((other, second, held_extra))
+            else:
+                at = stages[stages.index(bit) - 1]
+                other, more = lax.optimization_barrier((other, swap(held_extra, "dp", dp, at)))
+                held_extra = join(held_extra, more)
             first = join(first, other)
-        held_extra = join(held_extra, swap(held_extra, "dp", dp, stages[0]))
+        held_extra = join(held_extra, swap(held_extra, "dp", dp, stages[-1]))
         other, held_extra, late = lax.optimization_barrier(
             (swap_both(first, dp, mp, (1, 0), (0, 2)), held_extra, swap(second, "dp", dp, stages[0]))
         )
         second = join(second, late)
         for bit in stages[1:]:
             second = join(second, swap(second, "dp", dp, bit))
-            held_extra = join(held_extra, swap(held_extra, "dp", dp, bit))
         held_extra = join(held_extra, swap(held_extra, "dp", dp, 1))
         held_extra = held_extra.reshape((dp,) + extra.shape)
         if ready:

time: 151 us -> 148 us (0.980)
  waiting for transfers between devices: 40.7 us -> 37.8 us
  starting transfers between devices: 28.2 us -> 30.2 us
  blocking collectives: 21.8 us -> 20 us
    ppermute x26, waiting for transfers between devices: 37.3 us -> 32 us  [swap(): lax.ppermute(array_in, axis_name, [(i, i ^ bit) for i in range(size)])]
    ppermute x26, starting transfers between devices: 18.7 us -> 21.2 us  [swap(): lax.ppermute(array_in, axis_name, [(i, i ^ bit) for i in range(size)])]
    ppermute x8, waiting for transfers between devices: 3.38 us -> 5.85 us  [swap_both(): return lax.ppermute(array_in, ('dp', 'mp'), pairs)]
    all_to_all x1, blocking collectives: 12.2 us -> 10.5 us  [per_device(): got = lax.all_to_all(got, 'dp', split_axis=0, concat_axis=0, tiled=True)]
  transfers between devices with their start and end apart: 34 -> 34, of which waited for: 18 -> 18; matrix products, arithmetic and copies ran while one was open for 3% -> 3% of each run, Pallas kernels for 19% -> 20%
where the time goes in v15:
time: 148 us
  Pallas kernels  49.7 us (34%)
  waiting for transfers between devices  37.8 us (26%)
  starting transfers between devices  30.2 us (20%)
  blocking collectives  20 us (14%)
  local copies, waits for them, and re-layouts  4.67 us (3%)
  matrix products  3.85 us (3%)
    pallas_call x31, Pallas kernels, call(): pl.pallas_call(functools.partial(kernel, **static), out_shape=[jax.ShapeD...  48.6 us
    ppermute x26, waiting for transfers between devices, swap(): lax.ppermute(array_in, axis_name, [(i, i ^ bit) for i in range(size)])  32 us
    ppermute x26, starting transfers between devices, swap(): lax.ppermute(array_in, axis_name, [(i, i ^ bit) for i in range(size)])  21.2 us
    all_to_all x1, blocking collectives, per_device(): got = lax.all_to_all(got, 'dp', split_axis=0, concat_axis=0, tiled=True)  10.5 us
    all_to_all x1, blocking collectives, per_device(): back = lax.all_to_all(back, 'dp', split_axis=0, concat_axis=0, tiled=True)  9.51 us
    ppermute x8, starting transfers between devices, swap_both(): return lax.ppermute(array_in, ('dp', 'mp'), pairs)  8.95 us
    ppermute x8, waiting for transfers between devices, swap_both(): return lax.ppermute(array_in, ('dp', 'mp'), pairs)  5.85 us
    dot_general x2, matrix products, mm_tn(): lax.dot_general(a, b, (((0,), (0,)), ((), ())), preferred_element_type=f32)  3.85 us
  transfers between devices with their start and end apart: 34, of which 18 were waited for; matrix products, arithmetic and copies ran while one was open for 3% of the time, Pallas kernels for 20%

profile of v15, /device:TPU:0, one launch (start us, length us, event | category | flops | bytes accessed | tf_op | source)
XLA Modules:
  0.0 147.5 jit_solution(7973946288630373714)
XLA Ops:
  1.6 4.1 %collective-permute-start = (bf16[1,3,96,128]{3,2,1,0:T(8,128)(2,1)S(1)}, bf16[1,3,96,128]{3,2,1,0:T(8,128)(2,1)S(1)}, u32[]{:S(2)}, u32[]{:S(2)}) collective-permute-start(bf16[1,3,96,128]{3,2,1,0:T(8,128)(2,1)S(1)} %slice_bitcast_fusion.5.a_ref), channel_id=1, source_target_pairs={{0,16},{4,20},{8,24},{12,28},{16,0},{20,4},{24,8},{28,12},{1,17},{... | collective-permute-start | bytes 221192 | tf_op jit(solution)/shard_map/ppermute | solution.py:24
  10.5 1.6 %collective-permute-start.1 = (bf16[2,3,96,128]{3,2,1,0:T(8,128)(2,1)S(1)}, bf16[2,3,96,128]{3,2,1,0:T(8,128)(2,1)S(1)}, u32[]{:S(2)}, u32[]{:S(2)}) collective-permute-start(bf16[2,3,96,128]{3,2,1,0:T(8,128)(2,1)S(1)} %join.9.a_ref), channel_id=1, source_target_pairs={{0,8},{4,12},{8,0},{12,4},{16,24},{20,28},{24,16},{28,20},{1,9},{5... | collective-permute-start | bytes 442376 | tf_op jit(solution)/shard_map/ppermute | solution.py:24
  12.1 1.6 %collective-permute-start.2 = (bf16[1,96,128]{2,1,0:T(8,128)(2,1)S(1)}, bf16[1,96,128]{2,1,0:T(8,128)(2,1)S(1)}, u32[]{:S(2)}, u32[]{:S(2)}) collective-permute-start(bf16[1,96,128]{2,1,0:T(8,128)(2,1)S(1)} %bitcast.93), channel_id=1, source_target_pairs={{0,16},{4,20},{8,24},{12,28},{16,0},{20,4},{24,8},{28,12},{1,17},{... | collective-permute-start | bytes 73736 | tf_op jit(solution)/shard_map/ppermute | solution.py:24
  13.7 3.1 %collective-permute-done.2.b_ref = bf16[1,96,128]{2,1,0:T(8,128)(2,1)S(1)} collective-permute-done((bf16[1,96,128]{2,1,0:T(8,128)(2,1)S(1)}, bf16[1,96,128]{2,1,0:T(8,128)(2,1)S(1)}, u32[]{:S(2)}, u32[]{:S(2)}) %collective-permute-start.2) | collective-permute-done | bytes 24608 | tf_op jit(solution)/shard_map/ppermute | solution.py:24
  16.9 1.6 %collective-permute-start.3 = (bf16[4,3,96,128]{3,2,1,0:T(8,128)(2,1)S(1)}, bf16[4,3,96,128]{3,2,1,0:T(8,128)(2,1)S(1)}, u32[]{:S(2)}, u32[]{:S(2)}) collective-permute-start(bf16[4,3,96,128]{3,2,1,0:T(8,128)(2,1)S(1)} %join.10.a_ref), channel_id=1, source_target_pairs={{0,4},{1,3},{2,6},{3,1},{4,0},{5,7},{6,2},{7,5},{8,12},{9,11},{10,... | collective-permute-start | bytes 884744 | tf_op jit(solution)/shard_map/ppermute | solution.py:33
  18.5 2.0 %collective-permute-start.5 = (bf16[1,96,384]{2,1,0:T(8,128)(2,1)S(1)}, bf16[1,96,384]{2,1,0:T(8,128)(2,1)S(1)}, u32[]{:S(2)}, u32[]{:S(2)}) collective-permute-start(bf16[1,96,384]{2,1,0:T(8,128)(2,1)S(1)} %bitcast.89), channel_id=1, source_target_pairs={{0,16},{4,20},{8,24},{12,28},{16,0},{20,4},{24,8},{28,12},{1,17},{... | collective-permute-start | bytes 221192 | tf_op jit(solution)/shard_map/ppermute | solution.py:24
  21.4 3.3 %collective-permute-done.4.b_ref = bf16[2,96,128]{2,1,0:T(8,128)(2,1)S(1)} collective-permute-done((bf16[2,96,128]{2,1,0:T(8,128)(2,1)S(1)}, bf16[2,96,128]{2,1,0:T(8,128)(2,1)S(1)}, u32[]{:S(2)}, u32[]{:S(2)}) %collective-permute-start.4) | collective-permute-done | bytes 49184 | tf_op jit(solution)/shard_map/ppermute | solution.py:24
  28.0 3.5 %collective-permute-done.8.b_ref = bf16[2,96,384]{2,1,0:T(8,128)(2,1)S(1)} collective-permute-done((bf16[2,96,384]{2,1,0:T(8,128)(2,1)S(1)}, bf16[2,96,384]{2,1,0:T(8,128)(2,1)S(1)}, u32[]{:S(2)}, u32[]{:S(2)}) %collective-permute-start.8) | collective-permute-done | bytes 147488 | tf_op jit(solution)/shard_map/ppermute | solution.py:24
  34.3 4.0 %collective-permute-done.9.b_ref = bf16[4,96,384]{2,1,0:T(8,128)(2,1)S(1)} collective-permute-done((bf16[4,96,384]{2,1,0:T(8,128)(2,1)S(1)}, bf16[4,96,384]{2,1,0:T(8,128)(2,1)S(1)}, u32[]{:S(2)}, u32[]{:S(2)}) %collective-permute-start.9) | collective-permute-done | bytes 294944 | tf_op jit(solution)/shard_map/ppermute | solution.py:33
  40.3 6.2 %front_pair.1 = (bf16[4,768,384]{2,1,0:T(8,128)(2,1)S(1)}, bf16[4,624,384]{2,1,0:T(8,128)(2,1)S(1)}, bf16[4,3,2,208,208]{4,3,2,1,0:T(8,128)(2,1)S(1)}, bf16[4,624,128]{2,1,0:T(8,128)(2,1)S(1)}) custom-call(s32[3]{0:T(128)S(1)} %pad_add_fusion.me_ref, bf16[624,768]{1,0:T(8,128)(2,1)S(1)} %get-tuple-element.115.h_ref, s32[12,200]{1,0:T(8,128)S(1)} %copy-done.6, ...), custom_call_target="tpu_custom_call" | custom-call | flops 11000000512 | bytes 3327372 | tf_op jit(solution)/shard_map/front_pair/pallas_call | solution.py:562
  46.5 1.8 %collective-permute-done.10.refs_1_ = bf16[2,4,96,384]{3,2,1,0:T(8,128)(2,1)S(1)} collective-permute-done((bf16[2,4,96,384]{3,2,1,0:T(8,128)(2,1)S(1)}, bf16[2,4,96,384]{3,2,1,0:T(8,128)(2,1)S(1)}, u32[]{:S(2)}, u32[]{:S(2)}) %collective-permute-start.10) | collective-permute-done | bytes 589856 | tf_op jit(solution)/shard_map/ppermute | solution.py:33
  48.4 3.5 %front_last.2 = (bf16[2,768,256]{2,1,0:T(8,128)(2,1)S(1)}, bf16[2,624,256]{2,1,0:T(8,128)(2,1)S(1)}, bf16[2,3,208,208]{3,2,1,0:T(8,128)(2,1)S(1)}, bf16[624,512]...) custom-call(s32[3]{0:T(128)S(1)} %pad_add_fusion.me_ref, ...), custom_call_target="tpu_custom_call" | custom-call | flops 3300000000 | bytes 2786700 | tf_op jit(solution)/shard_map/front_last/pallas_call | solution.py:562
  51.9 3.5 %front_last.3 = (bf16[2,768,256]{2,1,0:T(8,128)(2,1)S(1)}, bf16[2,624,256]{2,1,0:T(8,128)(2,1)S(1)}, bf16[2,3,208,208]{3,2,1,0:T(8,128)(2,1)S(1)}, bf16[624,512]...) custom-call(s32[3]{0:T(128)S(1)} %pad_add_fusion.me_ref, ...), custom_call_target="tpu_custom_call" | custom-call | flops 3300000000 | bytes 4703628 | tf_op jit(solution)/shard_map/front_last/pallas_call | solution.py:562
  55.4 2.7 %route.1 = (f32[624,768]{1,0:T(8,128)S(1)}, bf16[624,768]{1,0:T(8,128)(2,1)S(1)}, f32[2,3,8,208]{3,2,1,0:T(8,128)S(1)}, bf16[64,768]{1,0:T(8,128)(2,1)S(1)}, f32[3,1,128]{2,1,0:T(1,128)S(1)}) custom-call(s32[3]{0:T(128)S(1)} %pad_add_fusion.me_ref, bf16[3,200,768]{2,1,0:T(8,128)(2,1)S(1)} %bitcast.78, f32[624,768]{1,0:T(8,128)S(1)} %get-tuple-element.122.br_ref, ...), custom_call_target="tpu_custom_call" | custom-call | flops 2200000000 | bytes 4162956 | tf_op jit(solution)/shard_map/route/pallas_call | solution.py:562
  58.1 10.5 %all_to_all.10 = bf16[8,8,768]{2,1,0:T(8,128)(2,1)S(1)} all-to-all(bf16[8,8,768]{2,1,0:T(8,128)(2,1)S(1)} %bitcast.88), channel_id=1, replica_groups=mesh['dp'=8,'mp'=4] {'dp'}, dimensions={0} | all-to-all | bytes 196608 | tf_op jit(solution)/shard_map/all_to_all | solution.py:745
  69.6 3.6 %collective-permute-done.15 = bf16[1,8,8,768]{3,2,1,0:T(8,128)(2,1)S(1)} collective-permute-done((bf16[1,8,8,768]{3,2,1,0:T(8,128)(2,1)S(1)}, bf16[1,8,8,768]{3,2,1,0:T(8,128)(2,1)S(1)}, u32[]{:S(2)}, u32[]{:S(2)}) %collective-permute-start.15) | collective-permute-done | bytes 98336 | tf_op jit(solution)/shard_map/ppermute | solution.py:24
  74.8 1.7 %expert.1 = (bf16[256,768]{1,0:T(8,128)(2,1)S(1)}, bf16[256,768]{1,0:T(8,128)(2,1)S(1)}, bf16[256,768]{1,0:T(8,128)(2,1)S(1)}, bf16[256,768]{1,0:T(8,128)(2,1)S(1)}) custom-call(bf16[256,768]{1,0:T(8,128)(2,1)S(1)} %bitcast.75, bf16[768,768]{1,0:T(8,128)(2,1)S(1)} %bitcast.95, bf16[768,768]{1,0:T(8,128)(2,1)S(1)} %bitcast.96), custom_call_target="tpu_custom_call" | custom-call | flops 2200000000 | bytes 2752512 | tf_op jit(solution)/shard_map/expert/pallas_call | solution.py:562
  79.2 3.8 %collective-permute-done.18 = bf16[1,1,8,8,768]{4,3,2,1,0:T(8,128)(2,1)S(1)} collective-permute-done((bf16[1,1,8,8,768]{4,3,2,1,0:T(8,128)(2,1)S(1)}, bf16[1,1,8,8,768]{4,3,2,1,0:T(8,128)(2,1)S(1)}, u32[]{:S(2)}, u32[]{:S(2)}) %collective-permute-start.18) | collective-permute-done | bytes 98336 | tf_op jit(solution)/shard_map/ppermute | solution.py:24
  83.1 9.5 %all_to_all.11 = bf16[8,8,768]{2,1,0:T(8,128)(2,1)S(1)} all-to-all(bf16[8,8,768]{2,1,0:T(8,128)(2,1)S(1)} %fusion.5), channel_id=1, replica_groups=mesh['dp'=8,'mp'=4] {'dp'}, dimensions={0} | all-to-all | bytes 196608 | tf_op jit(solution)/shard_map/all_to_all | solution.py:765
  92.7 3.9 %mix.1 = (bf16[3,200,768]{2,1,0:T(8,128)(2,1)}, f32[624,768]{1,0:T(8,128)S(1)}, bf16[624,768]{1,0:T(8,128)(2,1)S(1)}, bf16[768,624]{1,0:T(8,128)(2,1)S(1)}, f32[13,768]{1,0:T(8,128)S(1)}) custom-call(s32[3]{0:T(128)S(1)} %pad_add_fusion.me_ref, f32[624,768]{1,0:T(8,128)S(1)} %get-tuple-element.124.res_ref, bf16[624,768]{1,0:T(8,128)(2,1)S(1)} %get-tuple-element.125.h_ref, ...), custom_call_target="tpu_custom_call" | custom-call | flops 5500000256 | bytes 4315020 | tf_op jit(solution)/shard_map/mix/pallas_call | solution.py:562
  96.6 3.6 %back.4 = (bf16[2,4,96,768]{3,2,1,0:T(8,128)(2,1)S(1)}, bf16[624,640]{1,0:T(8,128)(2,1)S(1)}) custom-call(s32[3]{0:T(128)S(1)} %pad_add_fusion.me_ref, bf16[624,768]{1,0:T(8,128)(2,1)S(1)} %get-tuple-element.160.gb_ref, bf16[768,624]{1,0:T(8,128)(2,1)S(1)} %get-tuple-element.133.gbt_ref, bf16[768,624]{1,0:T(8,128)(2,1)S(1)} %get-tuple-element.134.ht_ref, ...), custom_call_target="tpu_custom_call" | custom-call | flops 8800000000 | bytes 9452556 | tf_op jit(solution)/shard_map/back/pallas_call | solution.py:562
  100.3 3.6 %back.5 = (bf16[2,4,96,768]{3,2,1,0:T(8,128)(2,1)S(1)}, bf16[624,640]{1,0:T(8,128)(2,1)S(1)}) custom-call(s32[3]{0:T(128)S(1)} %pad_add_fusion.me_ref, bf16[624,768]{1,0:T(8,128)(2,1)S(1)} %get-tuple-element.160.gb_ref, bf16[768,624]{1,0:T(8,128)(2,1)S(1)} %get-tuple-element.133.gbt_ref, bf16[768,624]{1,0:T(8,128)(2,1)S(1)} %get-tuple-element.134.ht_ref, ...), custom_call_target="tpu_custom_call" | custom-call | flops 8800000000 | bytes 9452556 | tf_op jit(solution)/shard_map/back/pallas_call | solution.py:562
  104.2 3.6 %back.6 = (bf16[2,4,96,768]{3,2,1,0:T(8,128)(2,1)S(1)}, bf16[624,640]{1,0:T(8,128)(2,1)S(1)}) custom-call(s32[3]{0:T(128)S(1)} %pad_add_fusion.me_ref, bf16[624,768]{1,0:T(8,128)(2,1)S(1)} %get-tuple-element.160.gb_ref, bf16[768,624]{1,0:T(8,128)(2,1)S(1)} %get-tuple-element.133.gbt_ref, bf16[768,624]{1,0:T(8,128)(2,1)S(1)} %get-tuple-element.134.ht_ref, ...), custom_call_target="tpu_custom_call" | custom-call | flops 8800000000 | bytes 9452556 | tf_op jit(solution)/shard_map/back/pallas_call | solution.py:562
  109.4 3.9 %back.7 = (bf16[2,4,96,768]{3,2,1,0:T(8,128)(2,1)S(1)}, bf16[624,640]{1,0:T(8,128)(2,1)S(1)}) custom-call(s32[3]{0:T(128)S(1)} %pad_add_fusion.me_ref, bf16[624,768]{1,0:T(8,128)(2,1)S(1)} %get-tuple-element.160.gb_ref, bf16[768,624]{1,0:T(8,128)(2,1)S(1)} %get-tuple-element.133.gbt_ref, bf16[768,624]{1,0:T(8,128)(2,1)S(1)} %get-tuple-element.134.ht_ref, ...), custom_call_target="tpu_custom_call" | custom-call | flops 8800000000 | bytes 9452556 | tf_op jit(solution)/shard_map/back/pallas_call | solution.py:562
  115.2 3.7 %input.1.gh_ref = f32[624,768]{1,0:T(8,128)S(1)} custom-call(s32[3]{0:T(128)S(1)} %pad_add_fusion.me_ref, bf16[4,768,384]{2,1,0:T(8,128)(2,1)S(1)} %get-tuple-element.152.w_a, bf16[2,768,256]{2,1,0:T(8,128)(2,1)S(1)} %get-tuple-element.153.w_own, bf16[2,768,256]{2,1,0:T(8,128)(2,1)S(1)} %get-tuple-element.154.w_other, ...), custom_call_target="tpu_custom_call" | custom-call | flops 4400000000 | bytes 7127052 | tf_op jit(solution)/shard_map/input/pallas_call | solution.py:562
  120.1 1.7 %collective-permute-start.31 = (bf16[4,96,384]{2,1,0:T(8,128)(2,1)S(1)}, bf16[4,96,384]{2,1,0:T(8,128)(2,1)S(1)}, u32[]{:S(2)}, u32[]{:S(2)}) collective-permute-start(bf16[4,96,384]{2,1,0:T(8,128)(2,1)S(1)} %get-tuple-element.181), channel_id=1, source_target_pairs={{0,4},{1,3},{2,6},{3,1},{4,0},{5,7},{6,2},{7,5},{8,12},{9,11},{10,... | collective-permute-start | bytes 884744 | tf_op jit(solution)/shard_map/ppermute | solution.py:33
  121.8 2.7 %last.1 = (f32[3,200,768]{2,1,0:T(8,128)}, f32[13,768]{1,0:T(8,128)S(1)}) custom-call(bf16[3,200,768]{2,1,0:T(8,128)(2,1)S(1)} %bitcast.79, f32[624,768]{1,0:T(8,128)S(1)} %get-tuple-element.131.gres_ref, f32[624,768]{1,0:T(8,128)S(1)} %input.1.gh_ref, f32[128,768]{1,0:T(8,128)S(1)} %get-tuple-element.123.ex_ref, f32[13,768]{1,0:T(8,128)S(1)} %get-tuple-element.163.part_ref), custom_call_target="tpu_custom_call" | custom-call | flops 110000000 | bytes 5188608 | tf_op jit(solution)/shard_map/last/pallas_call | solution.py:562
  124.9 4.5 %collective-permute-done.25 = f32[13,768]{1,0:T(8,128)S(1)} collective-permute-done((f32[13,768]{1,0:T(8,128)S(1)}, f32[13,768]{1,0:T(8,128)S(1)}, u32[]{:S(2)}, u32[]{:S(2)}) %collective-permute-start.25) | collective-permute-done | bytes 39968 | tf_op jit(solution)/shard_map/ppermute | solution.py:24
  129.7 2.1 %collective-permute-start.24 = (bf16[2,96,384]{2,1,0:T(8,128)(2,1)S(1)}, bf16[2,96,384]{2,1,0:T(8,128)(2,1)S(1)}, u32[]{:S(2)}, u32[]{:S(2)}) collective-permute-start(bf16[2,96,384]{2,1,0:T(8,128)(2,1)S(1)} %get-tuple-element.173), channel_id=1, source_target_pairs={{0,8},{4,12},{8,0},{12,4},{16,24},{20,28},{24,16},{28,20},{1,9},{5... | collective-permute-start | bytes 442376 | tf_op jit(solution)/shard_map/ppermute | solution.py:24
  132.0 1.9 %convolution_bitcast_fusion.1 = f32[1,768,768]{2,1,0:T(8,128)} fusion(bf16[256,768]{1,0:T(8,128)(2,1)S(1)} %bitcast.76, bf16[256,768]{1,0:T(8,128)(2,1)S(1)} %get-tuple-element.190), kind=kOutput, calls=%fused_computation.1 | convolution fusion | flops 301989888 | bytes 3145728 | tf_op jit(solution)/shard_map/dot_general | solution.py:86
  133.9 2.8 %collective-permute-done.24.refs_1_ = bf16[2,96,384]{2,1,0:T(8,128)(2,1)S(1)} collective-permute-done((bf16[2,96,384]{2,1,0:T(8,128)(2,1)S(1)}, bf16[2,96,384]{2,1,0:T(8,128)(2,1)S(1)}, u32[]{:S(2)}, u32[]{:S(2)}) %collective-permute-start.24) | collective-permute-done | bytes 147488 | tf_op jit(solution)/shard_map/ppermute | solution.py:24
  141.9 1.9 %convolution_bitcast_fusion = f32[1,768,768]{2,1,0:T(8,128)} fusion(bf16[256,768]{1,0:T(8,128)(2,1)S(1)} %get-tuple-element.191, bf16[256,768]{1,0:T(8,128)(2,1)S(1)} %get-tuple-element.192), kind=kOutput, calls=%fused_computation | convolution fusion | flops 301989888 | bytes 3145728 | tf_op jit(solution)/shard_map/dot_general | solution.py:86
  (106 shorter events, 34.9 us)
Async XLA Ops:
  1.6 8.8 %collective-permute-start = (bf16[1,3,96,128]{3,2,1,0:T(8,128)(2,1)S(1)}, bf16[1,3,96,128]{3,2,1,0:T(8,128)(2,1)S(1)}, u32[]{:S(2)}, u32[]{:S(2)}) collective-permute-start(bf16[1,3,96,128]{3,2,1,0:T(8,128)(2,1)S(1)} %slice_bitcast_fusion.5.a_ref), channel_id=1, source_target_pairs={{0,16},{4,20},{8,24},{12,28},{16,0},{20,4},{24,8},{28,12},{1,17},{... | collective-permute-start | bytes 221192 | tf_op jit(solution)/shard_map/ppermute | solution.py:24
  10.5 6.4 %collective-permute-start.1 = (bf16[2,3,96,128]{3,2,1,0:T(8,128)(2,1)S(1)}, bf16[2,3,96,128]{3,2,1,0:T(8,128)(2,1)S(1)}, u32[]{:S(2)}, u32[]{:S(2)}) collective-permute-start(bf16[2,3,96,128]{3,2,1,0:T(8,128)(2,1)S(1)} %join.9.a_ref), channel_id=1, source_target_pairs={{0,8},{4,12},{8,0},{12,4},{16,24},{20,28},{24,16},{28,20},{1,9},{5... | collective-permute-start | bytes 442376 | tf_op jit(solution)/shard_map/ppermute | solution.py:24
  12.1 4.7 %collective-permute-start.2 = (bf16[1,96,128]{2,1,0:T(8,128)(2,1)S(1)}, bf16[1,96,128]{2,1,0:T(8,128)(2,1)S(1)}, u32[]{:S(2)}, u32[]{:S(2)}) collective-permute-start(bf16[1,96,128]{2,1,0:T(8,128)(2,1)S(1)} %bitcast.93), channel_id=1, source_target_pairs={{0,16},{4,20},{8,24},{12,28},{16,0},{20,4},{24,8},{28,12},{1,17},{... | collective-permute-start | bytes 73736 | tf_op jit(solution)/shard_map/ppermute | solution.py:24
  16.9 7.8 %collective-permute-start.3 = (bf16[4,3,96,128]{3,2,1,0:T(8,128)(2,1)S(1)}, bf16[4,3,96,128]{3,2,1,0:T(8,128)(2,1)S(1)}, u32[]{:S(2)}, u32[]{:S(2)}) collective-permute-start(bf16[4,3,96,128]{3,2,1,0:T(8,128)(2,1)S(1)} %join.10.a_ref), channel_id=1, source_target_pairs={{0,4},{1,3},{2,6},{3,1},{4,0},{5,7},{6,2},{7,5},{8,12},{9,11},{10,... | collective-permute-start | bytes 884744 | tf_op jit(solution)/shard_map/ppermute | solution.py:33
  18.5 6.2 %collective-permute-start.5 = (bf16[1,96,384]{2,1,0:T(8,128)(2,1)S(1)}, bf16[1,96,384]{2,1,0:T(8,128)(2,1)S(1)}, u32[]{:S(2)}, u32[]{:S(2)}) collective-permute-start(bf16[1,96,384]{2,1,0:T(8,128)(2,1)S(1)} %bitcast.89), channel_id=1, source_target_pairs={{0,16},{4,20},{8,24},{12,28},{16,0},{20,4},{24,8},{28,12},{1,17},{... | collective-permute-start | bytes 221192 | tf_op jit(solution)/shard_map/ppermute | solution.py:24
  20.5 4.2 %collective-permute-start.4 = (bf16[2,96,128]{2,1,0:T(8,128)(2,1)S(1)}, bf16[2,96,128]{2,1,0:T(8,128)(2,1)S(1)}, u32[]{:S(2)}, u32[]{:S(2)}) collective-permute-start(bf16[2,96,128]{2,1,0:T(8,128)(2,1)S(1)} %join.11.a_ref), channel_id=1, source_target_pairs={{0,8},{4,12},{8,0},{12,4},{16,24},{20,28},{24,16},{28,20},{1,9},{5... | collective-permute-start | bytes 147464 | tf_op jit(solution)/shard_map/ppermute | solution.py:24
  24.7 13.6 %collective-permute-start.6 = (bf16[2,4,3,96,128]{4,3,2,1,0:T(8,128)(2,1)S(1)}, bf16[2,4,3,96,128]{4,3,2,1,0:T(8,128)(2,1)S(1)}, u32[]{:S(2)}, u32[]{:S(2)}) collective-permute-start(bf16[2,4,3,96,128]{4,3,2,1,0:T(8,128)(2,1)S(1)} %bitcast.80), channel_id=1, source_target_pairs={{0,2},{1,5},{2,0},{3,7},{4,6},{5,1},{6,4},{7,3},{8,10},{9,13},{10,... | collective-permute-start | bytes 1769480 | tf_op jit(solution)/shard_map/ppermute | solution.py:33
  26.3 5.2 %collective-permute-start.8 = (bf16[2,96,384]{2,1,0:T(8,128)(2,1)S(1)}, bf16[2,96,384]{2,1,0:T(8,128)(2,1)S(1)}, u32[]{:S(2)}, u32[]{:S(2)}) collective-permute-start(bf16[2,96,384]{2,1,0:T(8,128)(2,1)S(1)} %join.15.a_ref), channel_id=1, source_target_pairs={{0,8},{4,12},{8,0},{12,4},{16,24},{20,28},{24,16},{28,20},{1,9},{5... | collective-permute-start | bytes 442376 | tf_op jit(solution)/shard_map/ppermute | solution.py:24
  27.2 5.5 %collective-permute-start.7 = (bf16[4,96,128]{2,1,0:T(8,128)(2,1)S(1)}, bf16[4,96,128]{2,1,0:T(8,128)(2,1)S(1)}, u32[]{:S(2)}, u32[]{:S(2)}) collective-permute-start(bf16[4,96,128]{2,1,0:T(8,128)(2,1)S(1)} %join.12.a_ref), channel_id=1, source_target_pairs={{0,4},{4,0},{8,12},{12,8},{16,20},{20,16},{24,28},{28,24},{1,5},{5... | collective-permute-start | bytes 294920 | tf_op jit(solution)/shard_map/ppermute | solution.py:24
  31.5 6.8 %collective-permute-start.9 = (bf16[4,96,384]{2,1,0:T(8,128)(2,1)S(1)}, bf16[4,96,384]{2,1,0:T(8,128)(2,1)S(1)}, u32[]{:S(2)}, u32[]{:S(2)}) collective-permute-start(bf16[4,96,384]{2,1,0:T(8,128)(2,1)S(1)} %join.16.a_ref), channel_id=1, source_target_pairs={{0,4},{1,3},{2,6},{3,1},{4,0},{5,7},{6,2},{7,5},{8,12},{9,11},{10,... | collective-permute-start | bytes 884744 | tf_op jit(solution)/shard_map/ppermute | solution.py:33
  32.1 7.3 %collective-permute-start.11 = (bf16[2,4,3,96,128]{4,3,2,1,0:T(8,128)(2,1)S(1)}, bf16[2,4,3,96,128]{4,3,2,1,0:T(8,128)(2,1)S(1)}, u32[]{:S(2)}, u32[]{:S(2)}) collective-permute-start(bf16[2,4,3,96,128]{4,3,2,1,0:T(8,128)(2,1)S(1)} %bitcast.81), channel_id=1, source_target_pairs={{0,1},{1,0},{2,3},{3,2},{4,5},{5,4},{6,7},{7,6},{8,9},{9,8},{10,11... | collective-permute-start | bytes 1769480 | tf_op jit(solution)/shard_map/ppermute | solution.py:24
  38.3 2.0 %collective-permute-start.12 = (bf16[2,4,3,96,128]{4,3,2,1,0:T(8,128)(2,1)S(1)}, bf16[2,4,3,96,128]{4,3,2,1,0:T(8,128)(2,1)S(1)}, u32[]{:S(2)}, u32[]{:S(2)}) collective-permute-start(bf16[2,4,3,96,128]{4,3,2,1,0:T(8,128)(2,1)S(1)} %collective-permute-done.6.refs_1_), channel_id=1, source_target_pairs={{0,1},{1,0},{2,3},{3,2},{4,5},{5,4},{6,7},{7,6},{8,9},{9,8},{10,11... | collective-permute-start | bytes 1769480 | tf_op jit(solution)/shard_map/ppermute | solution.py:24
  38.4 9.9 %collective-permute-start.10 = (bf16[2,4,96,384]{3,2,1,0:T(8,128)(2,1)S(1)}, bf16[2,4,96,384]{3,2,1,0:T(8,128)(2,1)S(1)}, u32[]{:S(2)}, u32[]{:S(2)}) collective-permute-start(bf16[2,4,96,384]{3,2,1,0:T(8,128)(2,1)S(1)} %bitcast.83), channel_id=1, source_target_pairs={{0,2},{1,5},{2,0},{3,7},{4,6},{5,1},{6,4},{7,3},{8,10},{9,13},{10,... | collective-permute-start | bytes 1769480 | tf_op jit(solution)/shard_map/ppermute | solution.py:33
  39.5 12.4 %collective-permute-start.13 = (bf16[2,4,96,384]{3,2,1,0:T(8,128)(2,1)S(1)}, bf16[2,4,96,384]{3,2,1,0:T(8,128)(2,1)S(1)}, u32[]{:S(2)}, u32[]{:S(2)}) collective-permute-start(bf16[2,4,96,384]{3,2,1,0:T(8,128)(2,1)S(1)} %bitcast.84), channel_id=1, source_target_pairs={{0,1},{1,0},{2,3},{3,2},{4,5},{5,4},{6,7},{7,6},{8,9},{9,8},{10,11... | collective-permute-start | bytes 1769480 | tf_op jit(solution)/shard_map/ppermute | solution.py:24
  48.3 3.5 %collective-permute-start.14 = (bf16[2,4,96,384]{3,2,1,0:T(8,128)(2,1)S(1)}, bf16[2,4,96,384]{3,2,1,0:T(8,128)(2,1)S(1)}, u32[]{:S(2)}, u32[]{:S(2)}) collective-permute-start(bf16[2,4,96,384]{3,2,1,0:T(8,128)(2,1)S(1)} %collective-permute-done.10.refs_1_), channel_id=1, source_target_pairs={{0,1},{1,0},{2,3},{3,2},{4,5},{5,4},{6,7},{7,6},{8,9},{9,8},{10,11... | collective-permute-start | bytes 1769480 | tf_op jit(solution)/shard_map/ppermute | solution.py:24
  68.6 4.6 %collective-permute-start.15 = (bf16[1,8,8,768]{3,2,1,0:T(8,128)(2,1)S(1)}, bf16[1,8,8,768]{3,2,1,0:T(8,128)(2,1)S(1)}, u32[]{:S(2)}, u32[]{:S(2)}) collective-permute-start(bf16[1,8,8,768]{3,2,1,0:T(8,128)(2,1)S(1)} %bitcast.109), channel_id=1, source_target_pairs={{0,2},{1,3},{2,0},{3,1},{4,6},{5,7},{6,4},{7,5},{8,10},{9,11},{10,... | collective-permute-start | bytes 294920 | tf_op jit(solution)/shard_map/ppermute | solution.py:24
  73.3 1.5 %collective-permute-start.16 = (bf16[2,8,8,768]{3,2,1,0:T(8,128)(2,1)S(1)}, bf16[2,8,8,768]{3,2,1,0:T(8,128)(2,1)S(1)}, u32[]{:S(2)}, u32[]{:S(2)}) collective-permute-start(bf16[2,8,8,768]{3,2,1,0:T(8,128)(2,1)S(1)} %get-tuple-element.195), channel_id=1, source_target_pairs={{0,1},{1,0},{2,3},{3,2},{4,5},{5,4},{6,7},{7,6},{8,9},{9,8},{10,11... | collective-permute-start | bytes 589832 | tf_op jit(solution)/shard_map/ppermute | solution.py:24
  78.2 4.9 %collective-permute-start.18 = (bf16[1,1,8,8,768]{4,3,2,1,0:T(8,128)(2,1)S(1)}, bf16[1,1,8,8,768]{4,3,2,1,0:T(8,128)(2,1)S(1)}, u32[]{:S(2)}, u32[]{:S(2)}) collective-permute-start(bf16[1,1,8,8,768]{4,3,2,1,0:T(8,128)(2,1)S(1)} %slice_bitcast_fusion.2), channel_id=1, source_target_pairs={{0,2},{1,3},{2,0},{3,1},{4,6},{5,7},{6,4},{7,5},{8,10},{9,11},{10,... | collective-permute-start | bytes 294920 | tf_op jit(solution)/shard_map/ppermute | solution.py:24
  100.2 3.7 %collective-permute-start.19 = (bf16[2,4,96,768]{3,2,1,0:T(8,128)(2,1)S(1)}, bf16[2,4,96,768]{3,2,1,0:T(8,128)(2,1)S(1)}, u32[]{:S(2)}, u32[]{:S(2)}) collective-permute-start(bf16[2,4,96,768]{3,2,1,0:T(8,128)(2,1)S(1)} %get-tuple-element.148), channel_id=1, source_target_pairs={{0,1},{1,0},{2,3},{3,2},{4,5},{5,4},{6,7},{7,6},{8,9},{9,8},{10,11... | collective-permute-start | bytes 3538952 | tf_op jit(solution)/shard_map/ppermute | solution.py:24
  107.8 5.4 %collective-permute-start.21 = (bf16[2,4,96,768]{3,2,1,0:T(8,128)(2,1)S(1)}, bf16[2,4,96,768]{3,2,1,0:T(8,128)(2,1)S(1)}, u32[]{:S(2)}, u32[]{:S(2)}) collective-permute-start(bf16[2,4,96,768]{3,2,1,0:T(8,128)(2,1)S(1)} %get-tuple-element.167), channel_id=1, source_target_pairs={{0,1},{1,0},{2,3},{3,2},{4,5},{5,4},{6,7},{7,6},{8,9},{9,8},{10,11... | collective-permute-start | bytes 3538952 | tf_op jit(solution)/shard_map/ppermute | solution.py:24
  108.4 10.6 %collective-permute-start.20 = (bf16[4,96,768]{2,1,0:T(8,128)(2,1)S(1)}, bf16[4,96,768]{2,1,0:T(8,128)(2,1)S(1)}, u32[]{:S(2)}, u32[]{:S(2)}) collective-permute-start(bf16[4,96,768]{2,1,0:T(8,128)(2,1)S(1)} %bitcast.99), channel_id=1, source_target_pairs={{0,2},{1,5},{2,0},{3,7},{4,6},{5,1},{6,4},{7,3},{8,10},{9,13},{10,... | collective-permute-start | bytes 1769480 | tf_op jit(solution)/shard_map/ppermute | solution.py:33
  114.1 15.4 %collective-permute-start.22 = (bf16[4,96,768]{2,1,0:T(8,128)(2,1)S(1)}, bf16[4,96,768]{2,1,0:T(8,128)(2,1)S(1)}, u32[]{:S(2)}, u32[]{:S(2)}) collective-permute-start(bf16[4,96,768]{2,1,0:T(8,128)(2,1)S(1)} %get-tuple-element.169), channel_id=1, source_target_pairs={{0,2},{1,5},{2,0},{3,7},{4,6},{5,1},{6,4},{7,3},{8,10},{9,13},{10,... | collective-permute-start | bytes 1769480 | tf_op jit(solution)/shard_map/ppermute | solution.py:33
  119.7 9.9 %collective-permute-start.23 = (bf16[4,96,384]{2,1,0:T(8,128)(2,1)S(1)}, bf16[4,96,384]{2,1,0:T(8,128)(2,1)S(1)}, u32[]{:S(2)}, u32[]{:S(2)}) collective-permute-start(bf16[4,96,384]{2,1,0:T(8,128)(2,1)S(1)} %get-tuple-element.172), channel_id=1, source_target_pairs={{0,4},{1,3},{2,6},{3,1},{4,0},{5,7},{6,2},{7,5},{8,12},{9,11},{10,... | collective-permute-start | bytes 884744 | tf_op jit(solution)/shard_map/ppermute | solution.py:33
  120.1 11.7 %collective-permute-start.31 = (bf16[4,96,384]{2,1,0:T(8,128)(2,1)S(1)}, bf16[4,96,384]{2,1,0:T(8,128)(2,1)S(1)}, u32[]{:S(2)}, u32[]{:S(2)}) collective-permute-start(bf16[4,96,384]{2,1,0:T(8,128)(2,1)S(1)} %get-tuple-element.181), channel_id=1, source_target_pairs={{0,4},{1,3},{2,6},{3,1},{4,0},{5,7},{6,2},{7,5},{8,12},{9,11},{10,... | collective-permute-start | bytes 884744 | tf_op jit(solution)/shard_map/ppermute | solution.py:33
  124.4 5.0 %collective-permute-start.25 = (f32[13,768]{1,0:T(8,128)S(1)}, f32[13,768]{1,0:T(8,128)S(1)}, u32[]{:S(2)}, u32[]{:S(2)}) collective-permute-start(f32[13,768]{1,0:T(8,128)S(1)} %get-tuple-element.174), channel_id=1, source_target_pairs={{0,16},{4,20},{8,24},{12,28},{16,0},{20,4},{24,8},{28,12},{1,17},{... | collective-permute-start | bytes 119816 | tf_op jit(solution)/shard_map/ppermute | solution.py:24
  129.5 4.5 %collective-permute-start.26 = (f32[13,768]{1,0:T(8,128)S(1)}, f32[13,768]{1,0:T(8,128)S(1)}, u32[]{:S(2)}, u32[]{:S(2)}) collective-permute-start(f32[13,768]{1,0:T(8,128)S(1)} %add.20), channel_id=1, source_target_pairs={{0,8},{4,12},{8,0},{12,4},{16,24},{20,28},{24,16},{28,20},{1,9},{5... | collective-permute-start | bytes 119816 | tf_op jit(solution)/shard_map/ppermute | solution.py:24
  129.7 7.1 %collective-permute-start.24 = (bf16[2,96,384]{2,1,0:T(8,128)(2,1)S(1)}, bf16[2,96,384]{2,1,0:T(8,128)(2,1)S(1)}, u32[]{:S(2)}, u32[]{:S(2)}) collective-permute-start(bf16[2,96,384]{2,1,0:T(8,128)(2,1)S(1)} %get-tuple-element.173), channel_id=1, source_target_pairs={{0,8},{4,12},{8,0},{12,4},{16,24},{20,28},{24,16},{28,20},{1,9},{5... | collective-permute-start | bytes 442376 | tf_op jit(solution)/shard_map/ppermute | solution.py:24
  131.9 7.2 %collective-permute-start.32 = (bf16[2,96,384]{2,1,0:T(8,128)(2,1)S(1)}, bf16[2,96,384]{2,1,0:T(8,128)(2,1)S(1)}, u32[]{:S(2)}, u32[]{:S(2)}) collective-permute-start(bf16[2,96,384]{2,1,0:T(8,128)(2,1)S(1)} %get-tuple-element.183), channel_id=1, source_target_pairs={{0,8},{4,12},{8,0},{12,4},{16,24},{20,28},{24,16},{28,20},{1,9},{5... | collective-permute-start | bytes 442376 | tf_op jit(solution)/shard_map/ppermute | solution.py:24
  136.8 4.1 %collective-permute-start.27 = (f32[13,768]{1,0:T(8,128)S(1)}, f32[13,768]{1,0:T(8,128)S(1)}, u32[]{:S(2)}, u32[]{:S(2)}) collective-permute-start(f32[13,768]{1,0:T(8,128)S(1)} %add.21), channel_id=1, source_target_pairs={{0,4},{4,0},{8,12},{12,8},{16,20},{20,16},{24,28},{28,24},{1,5},{5... | collective-permute-start | bytes 119816 | tf_op jit(solution)/shard_map/ppermute | solution.py:24
  137.6 7.5 %collective-permute-start.30 = (bf16[96,384]{1,0:T(8,128)(2,1)S(1)}, bf16[96,384]{1,0:T(8,128)(2,1)S(1)}, u32[]{:S(2)}, u32[]{:S(2)}) collective-permute-start(bf16[96,384]{1,0:T(8,128)(2,1)S(1)} %bitcast.100), channel_id=1, source_target_pairs={{0,16},{4,20},{8,24},{12,28},{16,0},{20,4},{24,8},{28,12},{1,17},{... | collective-permute-start | bytes 221192 | tf_op jit(solution)/shard_map/ppermute | solution.py:24
  139.2 6.1 %collective-permute-start.33 = (bf16[96,384]{1,0:T(8,128)(2,1)S(1)}, bf16[96,384]{1,0:T(8,128)(2,1)S(1)}, u32[]{:S(2)}, u32[]{:S(2)}) collective-permute-start(bf16[96,384]{1,0:T(8,128)(2,1)S(1)} %bitcast.101), channel_id=1, source_target_pairs={{0,16},{4,20},{8,24},{12,28},{16,0},{20,4},{24,8},{28,12},{1,17},{... | collective-permute-start | bytes 221192 | tf_op jit(solution)/shard_map/ppermute | solution.py:24
  140.9 4.1 %collective-permute-start.28 = (f32[13,768]{1,0:T(8,128)S(1)}, f32[13,768]{1,0:T(8,128)S(1)}, u32[]{:S(2)}, u32[]{:S(2)}) collective-permute-start(f32[13,768]{1,0:T(8,128)S(1)} %add.22), channel_id=1, source_target_pairs={{0,2},{1,3},{2,0},{3,1},{4,6},{5,7},{6,4},{7,5},{8,10},{9,11},{10,... | collective-permute-start | bytes 119816 | tf_op jit(solution)/shard_map/ppermute | solution.py:24
  (12 other events, 78.8 us)
